TPU v7x, 256 devices: a whole 4x4x8 slice. The times are simulated.
256 devices in a mesh: occ: 16 (over z, x_lo), aux: 16 (over x_hi, y, core).
Axes of the slice: x: 4 (x_hi: 2, x_lo: 2; x = x_hi * 2 + x_lo), y: 4, z: 8, core: 2. Of those that a mesh axis runs over, the one named last changes fastest.
Arguments:
- three_index: bfloat16 [16, 448, 6144], P('occ', None, 'aux'), may hold values from -0.75 to 0.75
- occ_energy: float32 [16], P('occ'), may hold values from -2 to -0.3
- vir_energy: float32 [448], replicated, may hold values from 0.3 to 3
Outputs:
- gamma: float32 [16, 448, 6144], P('occ', None, 'aux')
All inputs are finite; a program needn't handle non-finite values.
Results may differ from a plain program's by a relative error of at most 0.0019.
Values may be sent and summed in bfloat16 or wider, within the bound.
No kernel may reach another device: no remote copies, remote signals or barrier semaphores. Data moves between devices by JAX's collectives and lax.ppermute only.
A program may use at most 64 MiB of HBM per device.

v0:
```python
import jax
import jax.numpy as jnp
from jax import lax
from jax.sharding import PartitionSpec as P


def in_blocks(array, dim, size):
    shape = array.shape
    parts = array.reshape(*shape[:dim], size, shape[dim] // size, *shape[dim + 1 :])
    return jnp.moveaxis(parts, dim, 0)


def sent_and_summed(array, axis, dim):
    size = lax.axis_size(axis)
    parts = lax.all_to_all(in_blocks(array, dim, size), axis, 0, 0, tiled=True)
    return jnp.sum(parts, axis=0)


def joined_along(parts, dim):
    parts = jnp.moveaxis(parts, 0, dim)
    shape = parts.shape
    return parts.reshape(*shape[:dim], shape[dim] * shape[dim + 1], *shape[dim + 2 :])


def copy_for_each(array, axis):
    copies = jnp.broadcast_to(array, (lax.axis_size(axis), *array.shape))
    return lax.all_to_all(copies, axis, split_axis=0, concat_axis=0, tiled=True)


def collect(array, axis, dim):
    return joined_along(copy_for_each(array, axis), dim)


def from_behind(array, axis, by):
    size = lax.axis_size(axis)
    return lax.ppermute(array, axis, [(i, (i + by) % size) for i in range(size)])


def pair_amps(rows_i, eps_i, rows_j, eps_j, vir_energy):
    partial_value = lax.dot_general(
        rows_i, rows_j, (((1,), (1,)), ((), ())), preferred_element_type=jnp.float32
    )
    occ_count = eps_i.shape[0]
    vir_count = vir_energy.shape[0]
    width = occ_count * vir_count
    four = partial_value.reshape(occ_count, vir_count, occ_count, vir_count)
    numer = (2.0 * four - jnp.transpose(four, (0, 3, 2, 1))).reshape(width, width)
    denom = (
        vir_energy[None, :, None, None]
        + vir_energy[None, None, None, :]
        - eps_i[:, None, None, None]
        - eps_j[None, None, :, None]
    ).reshape(width, width)
    share = width // lax.axis_size("aux")
    mine = sent_and_summed(numer, "aux", 0)
    lower = lax.axis_index("aux") * share
    denom_rows = lax.dynamic_slice_in_dim(denom, lower, share, 0)
    amps_rows = (mine / denom_rows).astype(jnp.bfloat16)
    amps = collect(amps_rows, "aux", 0)
    return amps


def apply_other(amps, rows_i):
    return lax.dot_general(
        amps, rows_i, (((0,), (0,)), ((), ())), preferred_element_type=jnp.float32
    )


def local(three_index, occ_energy, vir_energy):
    occ_count, vir_count, aux_count = three_index.shape
    cycle_size = lax.axis_size("occ")
    my_index = lax.axis_index("occ")
    all_energy = collect(occ_energy, "occ", 0)
    own_rows = three_index.reshape(occ_count * vir_count, aux_count)

    def energy_of(step):
        block = (my_index - step + cycle_size) % cycle_size
        return lax.dynamic_slice_in_dim(all_energy, block * occ_count, occ_count)

    amps = pair_amps(own_rows, occ_energy, own_rows, occ_energy, vir_energy)
    gamma = jnp.dot(amps, own_rows, preferred_element_type=jnp.float32)
    half = cycle_size // 2
    carried = jnp.zeros_like(gamma)

    def cycle_step(step, state):
        rows_j, carried, gamma = state
        rows_j = from_behind(rows_j, "occ", 1)
        carried = from_behind(carried, "occ", 1)
        amps = pair_amps(own_rows, occ_energy, rows_j, energy_of(step), vir_energy)
        gamma = gamma + jnp.dot(amps, rows_j, preferred_element_type=jnp.float32)
        carried = carried + apply_other(amps, own_rows)
        return (rows_j, carried, gamma)

    rows_j, carried, gamma = lax.fori_loop(1, half, cycle_step, (own_rows, carried, gamma))
    rows_j = from_behind(rows_j, "occ", 1)
    amps = pair_amps(own_rows, occ_energy, rows_j, energy_of(half), vir_energy)
    gamma = gamma + jnp.dot(amps, rows_j, preferred_element_type=jnp.float32)
    returned = from_behind(carried, "occ", 1 - half)
    gamma = gamma + returned
    return gamma.reshape(occ_count, vir_count, aux_count)


def solution(mesh):
    return jax.shard_map(
        local,
        mesh=mesh,
        in_specs=(P("occ", None, "aux"), P("occ"), P()),
        out_specs=P("occ", None, "aux"),
        check_vma=False,
    )
```

profile of v0, /device:TPU:1, one launch (start us, length us, event | category | flops | bytes accessed | tf_op | source)
XLA Modules:
  0.0 619.7 jit_solution(3148662663515596447)
XLA Ops:
  0.0 1.5 fusion.9
  3.5 8.4 %all-to-all-start.2 = ((f32[16,28,448]{2,1,0:T(8,128)}), f32[16,28,448]{2,1,0:T(8,128)S(1)}, u32[]{:S(2)}, u32[]{:S(2)}) async-start(f32[16,28,448]{2,1,0:T(8,128)} %reshape_reshape.6), calls=%async_computation.2 | async-start | bytes 2097152 | tf_op jit(solution)/shard_map/all_to_all | solution.py:15
  13.4 15.7 %all-to-all-done.2 = f32[16,28,448]{2,1,0:T(8,128)S(1)} async-done(((f32[16,28,448]{2,1,0:T(8,128)}), f32[16,28,448]{2,1,0:T(8,128)S(1)}, u32[]{:S(2)}, u32[]{:S(2)}) %all-to-all-start.2) | async-done | bytes 802848 | tf_op jit(solution)/shard_map/all_to_all | solution.py:15
  29.8 8.4 %all-to-all-start.4 = ((f32[16,1,1]{2,1,0:T(1,128)}), f32[16,1,1]{2,1,0:T(1,128)S(1)}, u32[]{:S(2)}, u32[]{:S(2)}) async-start(f32[16,1,1]{2,1,0:T(1,128)} %broadcast_in_dim.44), calls=%async_computation.4 | async-start | bytes 16384 | tf_op jit(solution)/shard_map/all_to_all | solution.py:27
  38.2 7.2 %all-to-all-done.4 = f32[16,1,1]{2,1,0:T(1,128)S(1)} async-done(((f32[16,1,1]{2,1,0:T(1,128)}), f32[16,1,1]{2,1,0:T(1,128)S(1)}, u32[]{:S(2)}, u32[]{:S(2)}) %all-to-all-start.4) | async-done | bytes 96 | tf_op jit(solution)/shard_map/all_to_all | solution.py:27
  46.3 5.8 all-to-all-start.3
  53.1 10.4 %all-to-all-done.3 = bf16[16,28,448]{2,1,0:T(8,128)(2,1)S(1)} async-done(((bf16[16,28,448]{2,1,0:T(8,128)(2,1)}), bf16[16,28,448]{2,1,0:T(8,128)(2,1)S(1)}, u32[]{:S(2)}, u32[]{:S(2)}) %all-to-all-start.3) | async-done | bytes 401440 | tf_op jit(solution)/shard_map/all_to_all | solution.py:27
  65.0 476.7 %while.20 = (s32[]{:T(128)}, bf16[448,384]{1,0:T(8,128)(2,1)}, f32[448,384]{1,0:T(8,128)}, f32[448,384]{1,0:T(8,128)}, bf16[448,384]{1,0:T(8,128)(2,1)S(1)}, /*i...) while((s32[]{:T(128)}, bf16[448,384]{1,0:T(8,128)(2,1)}, ...), condition=%wide.region_3.4_spmd.clone, body=%wide.region_1.3_spmd.clone.sunk | while | flops 463590400 | bytes 33920728 | solution.py:94
  65.3 10.4 %collective-permute-done = bf16[448,384]{1,0:T(8,128)(2,1)S(1)} collective-permute-done((bf16[448,384]{1,0:T(8,128)(2,1)}, bf16[448,384]{1,0:T(8,128)(2,1)S(1)}, u32[]{:S(2)}, u32[]{:S(2)}) %collective-permute-start) | collective-permute-done | bytes 344096 | tf_op jit(solution)/shard_map/while/body/eval_jaxpr/ppermute | solution.py:36
  78.0 5.7 all-to-all-start
  84.5 16.4 %all-to-all-done = f32[16,28,448]{2,1,0:T(8,128)S(1)} async-done(((f32[16,28,448]{2,1,0:T(8,128)}), f32[16,28,448]{2,1,0:T(8,128)S(1)}, u32[]{:S(2)}, u32[]{:S(2)}) %all-to-all-start) | async-done | bytes 802848 | tf_op jit(solution)/shard_map/while/body/eval_jaxpr/all_to_all | solution.py:15
  103.3 4.7 all-to-all-start.1
  108.7 12.3 %all-to-all-done.1 = bf16[16,28,448]{2,1,0:T(8,128)(2,1)S(1)} async-done(((bf16[16,28,448]{2,1,0:T(8,128)(2,1)}), bf16[16,28,448]{2,1,0:T(8,128)(2,1)S(1)}, u32[]{:S(2)}, u32[]{:S(2)}) %all-to-all-start.1) | async-done | bytes 401440 | tf_op jit(solution)/shard_map/while/body/eval_jaxpr/all_to_all | solution.py:27
  121.7 2.6 convolution_add_fusion.5
  124.3 10.8 %collective-permute-start = (bf16[448,384]{1,0:T(8,128)(2,1)}, bf16[448,384]{1,0:T(8,128)(2,1)S(1)}, u32[]{:S(2)}, u32[]{:S(2)}) collective-permute-start(bf16[448,384]{1,0:T(8,128)(2,1)} %get-tuple-element.352), channel_id=1, source_target_pairs={{0,16},{16,32},{32,48},{48,64},{64,80},{80,96},{96,112},{112,128},... | collective-permute-start | bytes 1032200 | tf_op jit(solution)/shard_map/while/body/eval_jaxpr/ppermute | solution.py:36
  135.1 8.6 %collective-permute-done = bf16[448,384]{1,0:T(8,128)(2,1)S(1)} collective-permute-done((bf16[448,384]{1,0:T(8,128)(2,1)}, bf16[448,384]{1,0:T(8,128)(2,1)S(1)}, u32[]{:S(2)}, u32[]{:S(2)}) %collective-permute-start) | collective-permute-done | bytes 344096 | tf_op jit(solution)/shard_map/while/body/eval_jaxpr/ppermute | solution.py:36
  146.0 5.9 all-to-all-start
  152.8 16.4 %all-to-all-done = f32[16,28,448]{2,1,0:T(8,128)S(1)} async-done(((f32[16,28,448]{2,1,0:T(8,128)}), f32[16,28,448]{2,1,0:T(8,128)S(1)}, u32[]{:S(2)}, u32[]{:S(2)}) %all-to-all-start) | async-done | bytes 802848 | tf_op jit(solution)/shard_map/while/body/eval_jaxpr/all_to_all | solution.py:15
  171.5 4.7 all-to-all-start.1
  176.9 12.3 %all-to-all-done.1 = bf16[16,28,448]{2,1,0:T(8,128)(2,1)S(1)} async-done(((bf16[16,28,448]{2,1,0:T(8,128)(2,1)}), bf16[16,28,448]{2,1,0:T(8,128)(2,1)S(1)}, u32[]{:S(2)}, u32[]{:S(2)}) %all-to-all-start.1) | async-done | bytes 401440 | tf_op jit(solution)/shard_map/while/body/eval_jaxpr/all_to_all | solution.py:27
  189.9 2.6 convolution_add_fusion.5
  192.5 12.4 %collective-permute-start = (bf16[448,384]{1,0:T(8,128)(2,1)}, bf16[448,384]{1,0:T(8,128)(2,1)S(1)}, u32[]{:S(2)}, u32[]{:S(2)}) collective-permute-start(bf16[448,384]{1,0:T(8,128)(2,1)} %get-tuple-element.352), channel_id=1, source_target_pairs={{0,16},{16,32},{32,48},{48,64},{64,80},{80,96},{96,112},{112,128},... | collective-permute-start | bytes 1032200 | tf_op jit(solution)/shard_map/while/body/eval_jaxpr/ppermute | solution.py:36
  204.9 8.6 %collective-permute-done = bf16[448,384]{1,0:T(8,128)(2,1)S(1)} collective-permute-done((bf16[448,384]{1,0:T(8,128)(2,1)}, bf16[448,384]{1,0:T(8,128)(2,1)S(1)}, u32[]{:S(2)}, u32[]{:S(2)}) %collective-permute-start) | collective-permute-done | bytes 344096 | tf_op jit(solution)/shard_map/while/body/eval_jaxpr/ppermute | solution.py:36
  215.9 5.9 all-to-all-start
  222.7 16.4 %all-to-all-done = f32[16,28,448]{2,1,0:T(8,128)S(1)} async-done(((f32[16,28,448]{2,1,0:T(8,128)}), f32[16,28,448]{2,1,0:T(8,128)S(1)}, u32[]{:S(2)}, u32[]{:S(2)}) %all-to-all-start) | async-done | bytes 802848 | tf_op jit(solution)/shard_map/while/body/eval_jaxpr/all_to_all | solution.py:15
  241.3 4.7 all-to-all-start.1
  246.8 12.3 %all-to-all-done.1 = bf16[16,28,448]{2,1,0:T(8,128)(2,1)S(1)} async-done(((bf16[16,28,448]{2,1,0:T(8,128)(2,1)}), bf16[16,28,448]{2,1,0:T(8,128)(2,1)S(1)}, u32[]{:S(2)}, u32[]{:S(2)}) %all-to-all-start.1) | async-done | bytes 401440 | tf_op jit(solution)/shard_map/while/body/eval_jaxpr/all_to_all | solution.py:27
  259.7 2.6 convolution_add_fusion.5
  262.3 12.4 %collective-permute-start = (bf16[448,384]{1,0:T(8,128)(2,1)}, bf16[448,384]{1,0:T(8,128)(2,1)S(1)}, u32[]{:S(2)}, u32[]{:S(2)}) collective-permute-start(bf16[448,384]{1,0:T(8,128)(2,1)} %get-tuple-element.352), channel_id=1, source_target_pairs={{0,16},{16,32},{32,48},{48,64},{64,80},{80,96},{96,112},{112,128},... | collective-permute-start | bytes 1032200 | tf_op jit(solution)/shard_map/while/body/eval_jaxpr/ppermute | solution.py:36
  274.7 8.6 %collective-permute-done = bf16[448,384]{1,0:T(8,128)(2,1)S(1)} collective-permute-done((bf16[448,384]{1,0:T(8,128)(2,1)}, bf16[448,384]{1,0:T(8,128)(2,1)S(1)}, u32[]{:S(2)}, u32[]{:S(2)}) %collective-permute-start) | collective-permute-done | bytes 344096 | tf_op jit(solution)/shard_map/while/body/eval_jaxpr/ppermute | solution.py:36
  285.7 5.9 all-to-all-start
  292.5 16.4 %all-to-all-done = f32[16,28,448]{2,1,0:T(8,128)S(1)} async-done(((f32[16,28,448]{2,1,0:T(8,128)}), f32[16,28,448]{2,1,0:T(8,128)S(1)}, u32[]{:S(2)}, u32[]{:S(2)}) %all-to-all-start) | async-done | bytes 802848 | tf_op jit(solution)/shard_map/while/body/eval_jaxpr/all_to_all | solution.py:15
  311.1 4.7 all-to-all-start.1
  316.6 12.3 %all-to-all-done.1 = bf16[16,28,448]{2,1,0:T(8,128)(2,1)S(1)} async-done(((bf16[16,28,448]{2,1,0:T(8,128)(2,1)}), bf16[16,28,448]{2,1,0:T(8,128)(2,1)S(1)}, u32[]{:S(2)}, u32[]{:S(2)}) %all-to-all-start.1) | async-done | bytes 401440 | tf_op jit(solution)/shard_map/while/body/eval_jaxpr/all_to_all | solution.py:27
  329.5 2.6 convolution_add_fusion.5
  332.2 12.4 %collective-permute-start = (bf16[448,384]{1,0:T(8,128)(2,1)}, bf16[448,384]{1,0:T(8,128)(2,1)S(1)}, u32[]{:S(2)}, u32[]{:S(2)}) collective-permute-start(bf16[448,384]{1,0:T(8,128)(2,1)} %get-tuple-element.352), channel_id=1, source_target_pairs={{0,16},{16,32},{32,48},{48,64},{64,80},{80,96},{96,112},{112,128},... | collective-permute-start | bytes 1032200 | tf_op jit(solution)/shard_map/while/body/eval_jaxpr/ppermute | solution.py:36
  344.6 8.6 %collective-permute-done = bf16[448,384]{1,0:T(8,128)(2,1)S(1)} collective-permute-done((bf16[448,384]{1,0:T(8,128)(2,1)}, bf16[448,384]{1,0:T(8,128)(2,1)S(1)}, u32[]{:S(2)}, u32[]{:S(2)}) %collective-permute-start) | collective-permute-done | bytes 344096 | tf_op jit(solution)/shard_map/while/body/eval_jaxpr/ppermute | solution.py:36
  355.5 5.9 all-to-all-start
  362.3 16.4 %all-to-all-done = f32[16,28,448]{2,1,0:T(8,128)S(1)} async-done(((f32[16,28,448]{2,1,0:T(8,128)}), f32[16,28,448]{2,1,0:T(8,128)S(1)}, u32[]{:S(2)}, u32[]{:S(2)}) %all-to-all-start) | async-done | bytes 802848 | tf_op jit(solution)/shard_map/while/body/eval_jaxpr/all_to_all | solution.py:15
  381.0 4.7 all-to-all-start.1
  386.4 12.3 %all-to-all-done.1 = bf16[16,28,448]{2,1,0:T(8,128)(2,1)S(1)} async-done(((bf16[16,28,448]{2,1,0:T(8,128)(2,1)}), bf16[16,28,448]{2,1,0:T(8,128)(2,1)S(1)}, u32[]{:S(2)}, u32[]{:S(2)}) %all-to-all-start.1) | async-done | bytes 401440 | tf_op jit(solution)/shard_map/while/body/eval_jaxpr/all_to_all | solution.py:27
  399.4 2.6 convolution_add_fusion.5
  402.0 12.4 %collective-permute-start = (bf16[448,384]{1,0:T(8,128)(2,1)}, bf16[448,384]{1,0:T(8,128)(2,1)S(1)}, u32[]{:S(2)}, u32[]{:S(2)}) collective-permute-start(bf16[448,384]{1,0:T(8,128)(2,1)} %get-tuple-element.352), channel_id=1, source_target_pairs={{0,16},{16,32},{32,48},{48,64},{64,80},{80,96},{96,112},{112,128},... | collective-permute-start | bytes 1032200 | tf_op jit(solution)/shard_map/while/body/eval_jaxpr/ppermute | solution.py:36
  414.4 8.6 %collective-permute-done = bf16[448,384]{1,0:T(8,128)(2,1)S(1)} collective-permute-done((bf16[448,384]{1,0:T(8,128)(2,1)}, bf16[448,384]{1,0:T(8,128)(2,1)S(1)}, u32[]{:S(2)}, u32[]{:S(2)}) %collective-permute-start) | collective-permute-done | bytes 344096 | tf_op jit(solution)/shard_map/while/body/eval_jaxpr/ppermute | solution.py:36
  425.3 5.9 all-to-all-start
  432.1 16.4 %all-to-all-done = f32[16,28,448]{2,1,0:T(8,128)S(1)} async-done(((f32[16,28,448]{2,1,0:T(8,128)}), f32[16,28,448]{2,1,0:T(8,128)S(1)}, u32[]{:S(2)}, u32[]{:S(2)}) %all-to-all-start) | async-done | bytes 802848 | tf_op jit(solution)/shard_map/while/body/eval_jaxpr/all_to_all | solution.py:15
  450.8 4.7 all-to-all-start.1
  456.2 12.3 %all-to-all-done.1 = bf16[16,28,448]{2,1,0:T(8,128)(2,1)S(1)} async-done(((bf16[16,28,448]{2,1,0:T(8,128)(2,1)}), bf16[16,28,448]{2,1,0:T(8,128)(2,1)S(1)}, u32[]{:S(2)}, u32[]{:S(2)}) %all-to-all-start.1) | async-done | bytes 401440 | tf_op jit(solution)/shard_map/while/body/eval_jaxpr/all_to_all | solution.py:27
  469.2 2.6 convolution_add_fusion.5
  471.8 12.4 %collective-permute-start = (bf16[448,384]{1,0:T(8,128)(2,1)}, bf16[448,384]{1,0:T(8,128)(2,1)S(1)}, u32[]{:S(2)}, u32[]{:S(2)}) collective-permute-start(bf16[448,384]{1,0:T(8,128)(2,1)} %get-tuple-element.352), channel_id=1, source_target_pairs={{0,16},{16,32},{32,48},{48,64},{64,80},{80,96},{96,112},{112,128},... | collective-permute-start | bytes 1032200 | tf_op jit(solution)/shard_map/while/body/eval_jaxpr/ppermute | solution.py:36
  484.2 8.6 %collective-permute-done = bf16[448,384]{1,0:T(8,128)(2,1)S(1)} collective-permute-done((bf16[448,384]{1,0:T(8,128)(2,1)}, bf16[448,384]{1,0:T(8,128)(2,1)S(1)}, u32[]{:S(2)}, u32[]{:S(2)}) %collective-permute-start) | collective-permute-done | bytes 344096 | tf_op jit(solution)/shard_map/while/body/eval_jaxpr/ppermute | solution.py:36
  495.2 5.9 all-to-all-start
  501.9 16.4 %all-to-all-done = f32[16,28,448]{2,1,0:T(8,128)S(1)} async-done(((f32[16,28,448]{2,1,0:T(8,128)}), f32[16,28,448]{2,1,0:T(8,128)S(1)}, u32[]{:S(2)}, u32[]{:S(2)}) %all-to-all-start) | async-done | bytes 802848 | tf_op jit(solution)/shard_map/while/body/eval_jaxpr/all_to_all | solution.py:15
  520.6 4.7 all-to-all-start.1
  526.1 12.3 %all-to-all-done.1 = bf16[16,28,448]{2,1,0:T(8,128)(2,1)S(1)} async-done(((bf16[16,28,448]{2,1,0:T(8,128)(2,1)}), bf16[16,28,448]{2,1,0:T(8,128)(2,1)S(1)}, u32[]{:S(2)}, u32[]{:S(2)}) %all-to-all-start.1) | async-done | bytes 401440 | tf_op jit(solution)/shard_map/while/body/eval_jaxpr/all_to_all | solution.py:27
  539.0 2.6 convolution_add_fusion.5
  541.6 12.4 %collective-permute-start.2 = (bf16[448,384]{1,0:T(8,128)(2,1)}, bf16[448,384]{1,0:T(8,128)(2,1)S(1)}, u32[]{:S(2)}, u32[]{:S(2)}) collective-permute-start(bf16[448,384]{1,0:T(8,128)(2,1)} %get-tuple-element.229), channel_id=1, source_target_pairs={{0,16},{16,32},{32,48},{48,64},{64,80},{80,96},{96,112},{112,128},... | collective-permute-start | bytes 1032200 | tf_op jit(solution)/shard_map/ppermute | solution.py:36
  554.0 8.6 %collective-permute-done.2 = bf16[448,384]{1,0:T(8,128)(2,1)S(1)} collective-permute-done((bf16[448,384]{1,0:T(8,128)(2,1)}, bf16[448,384]{1,0:T(8,128)(2,1)S(1)}, u32[]{:S(2)}, u32[]{:S(2)}) %collective-permute-start.2) | collective-permute-done | bytes 344096 | tf_op jit(solution)/shard_map/ppermute | solution.py:36
  565.0 5.9 all-to-all-start.5
  571.5 26.0 %all-to-all-done.5 = f32[16,28,448]{2,1,0:T(8,128)S(1)} async-done(((f32[16,28,448]{2,1,0:T(8,128)}), f32[16,28,448]{2,1,0:T(8,128)S(1)}, u32[]{:S(2)}, u32[]{:S(2)}) %all-to-all-start.5) | async-done | bytes 802848 | tf_op jit(solution)/shard_map/all_to_all | solution.py:15
  597.6 1.6 fusion.3
  599.2 16.1 %all_to_all.54 = bf16[16,28,448]{2,1,0:T(8,128)(2,1)S(1)} all-to-all(bf16[16,28,448]{2,1,0:T(8,128)(2,1)S(1)} %broadcast_in_dim.45), channel_id=1, replica_groups=mesh['occ'=16,'aux'=16] {'aux'}, dimensions={0} | all-to-all | bytes 802816 | tf_op jit(solution)/shard_map/all_to_all | solution.py:27
  615.4 1.9 collective-permute-done.3
  617.3 2.3 fusion.2
  (189 shorter events, 57.2 us)
Async XLA Ops:
  3.5 25.7 %all-to-all-start.2 = ((f32[16,28,448]{2,1,0:T(8,128)}), f32[16,28,448]{2,1,0:T(8,128)S(1)}, u32[]{:S(2)}, u32[]{:S(2)}) async-start(f32[16,28,448]{2,1,0:T(8,128)} %reshape_reshape.6), calls=%async_computation.2 | async-start | bytes 2097152 | tf_op jit(solution)/shard_map/all_to_all | solution.py:15
  12.6 0.7 copy-start.7
  13.4 32.9 %copy-start.6 = (f32[1,448,1,448]{3,1,2,0:T(8,128)}, f32[1,448,1,448]{3,1,2,0:T(8,128)S(1)}, u32[]{:S(2)}) copy-start(f32[1,448,1,448]{3,1,2,0:T(8,128)S(1)} %add_subtract_fusion) | copy-start | bytes 2408452
  29.8 15.6 %all-to-all-start.4 = ((f32[16,1,1]{2,1,0:T(1,128)}), f32[16,1,1]{2,1,0:T(1,128)S(1)}, u32[]{:S(2)}, u32[]{:S(2)}) async-start(f32[16,1,1]{2,1,0:T(1,128)} %broadcast_in_dim.44), calls=%async_computation.4 | async-start | bytes 16384 | tf_op jit(solution)/shard_map/all_to_all | solution.py:27
  46.3 5.9 copy-start
  46.3 17.2 %all-to-all-start.3 = ((bf16[16,28,448]{2,1,0:T(8,128)(2,1)}), bf16[16,28,448]{2,1,0:T(8,128)(2,1)S(1)}, u32[]{:S(2)}, u32[]{:S(2)}) async-start(bf16[16,28,448]{2,1,0:T(8,128)(2,1)} %broadcast_in_dim.43), calls=%async_computation.3 | async-start | bytes 1048576 | tf_op jit(solution)/shard_map/all_to_all | solution.py:27
  65.0 10.7 %collective-permute-start = (bf16[448,384]{1,0:T(8,128)(2,1)}, bf16[448,384]{1,0:T(8,128)(2,1)S(1)}, u32[]{:S(2)}, u32[]{:S(2)}) collective-permute-start(bf16[448,384]{1,0:T(8,128)(2,1)} %get-tuple-element.352), channel_id=1, source_target_pairs={{0,16},{16,32},{32,48},{48,64},{64,80},{80,96},{96,112},{112,128},... | collective-permute-start | bytes 1032200 | tf_op jit(solution)/shard_map/while/body/eval_jaxpr/ppermute | solution.py:36
  78.0 5.7 copy-start.4
  78.0 23.0 %all-to-all-start = ((f32[16,28,448]{2,1,0:T(8,128)}), f32[16,28,448]{2,1,0:T(8,128)S(1)}, u32[]{:S(2)}, u32[]{:S(2)}) async-start(f32[16,28,448]{2,1,0:T(8,128)} %reshape.267), calls=%async_computation | async-start | bytes 2097152 | tf_op jit(solution)/shard_map/while/body/eval_jaxpr/all_to_all | solution.py:15
  83.7 37.9 %collective-permute-start.1 = (f32[448,384]{1,0:T(8,128)S(1)}, f32[448,384]{1,0:T(8,128)}, u32[]{:S(2)}, u32[]{:S(2)}) collective-permute-start(f32[448,384]{1,0:T(8,128)S(1)} %broadcast_select_fusion.2), channel_id=1, source_target_pairs={{0,16},{16,32},{32,48},{48,64},{64,80},{80,96},{96,112},{112,128},... | collective-permute-start | bytes 2064392 | tf_op jit(solution)/shard_map/while/body/eval_jaxpr/ppermute | solution.py:36
  103.3 17.8 %all-to-all-start.1 = ((bf16[16,28,448]{2,1,0:T(8,128)(2,1)}), bf16[16,28,448]{2,1,0:T(8,128)(2,1)S(1)}, u32[]{:S(2)}, u32[]{:S(2)}) async-start(bf16[16,28,448]{2,1,0:T(8,128)(2,1)} %broadcast_in_dim.48), calls=%async_computation.1 | async-start | bytes 1048576 | tf_op jit(solution)/shard_map/while/body/eval_jaxpr/all_to_all | solution.py:27
  108.0 13.2 %copy-start.1 = (f32[448,384]{1,0:T(8,128)S(1)}, f32[448,384]{1,0:T(8,128)}, u32[]{:S(2)}) copy-start(f32[448,384]{1,0:T(8,128)} %get-tuple-element.354) | copy-start | bytes 2064388 | tf_op jit(solution)/shard_map/while
  121.6 2.7 copy-start.2
  124.3 19.4 %collective-permute-start = (bf16[448,384]{1,0:T(8,128)(2,1)}, bf16[448,384]{1,0:T(8,128)(2,1)S(1)}, u32[]{:S(2)}, u32[]{:S(2)}) collective-permute-start(bf16[448,384]{1,0:T(8,128)(2,1)} %get-tuple-element.352), channel_id=1, source_target_pairs={{0,16},{16,32},{32,48},{48,64},{64,80},{80,96},{96,112},{112,128},... | collective-permute-start | bytes 1032200 | tf_op jit(solution)/shard_map/while/body/eval_jaxpr/ppermute | solution.py:36
  146.0 5.9 copy-start.4
  146.0 23.1 %all-to-all-start = ((f32[16,28,448]{2,1,0:T(8,128)}), f32[16,28,448]{2,1,0:T(8,128)S(1)}, u32[]{:S(2)}, u32[]{:S(2)}) async-start(f32[16,28,448]{2,1,0:T(8,128)} %reshape.267), calls=%async_computation | async-start | bytes 2097152 | tf_op jit(solution)/shard_map/while/body/eval_jaxpr/all_to_all | solution.py:15
  152.0 37.8 %collective-permute-start.1 = (f32[448,384]{1,0:T(8,128)S(1)}, f32[448,384]{1,0:T(8,128)}, u32[]{:S(2)}, u32[]{:S(2)}) collective-permute-start(f32[448,384]{1,0:T(8,128)S(1)} %broadcast_select_fusion.2), channel_id=1, source_target_pairs={{0,16},{16,32},{32,48},{48,64},{64,80},{80,96},{96,112},{112,128},... | collective-permute-start | bytes 2064392 | tf_op jit(solution)/shard_map/while/body/eval_jaxpr/ppermute | solution.py:36
  171.5 17.8 %all-to-all-start.1 = ((bf16[16,28,448]{2,1,0:T(8,128)(2,1)}), bf16[16,28,448]{2,1,0:T(8,128)(2,1)S(1)}, u32[]{:S(2)}, u32[]{:S(2)}) async-start(bf16[16,28,448]{2,1,0:T(8,128)(2,1)} %broadcast_in_dim.48), calls=%async_computation.1 | async-start | bytes 1048576 | tf_op jit(solution)/shard_map/while/body/eval_jaxpr/all_to_all | solution.py:27
  176.2 13.2 %copy-start.1 = (f32[448,384]{1,0:T(8,128)S(1)}, f32[448,384]{1,0:T(8,128)}, u32[]{:S(2)}) copy-start(f32[448,384]{1,0:T(8,128)} %get-tuple-element.354) | copy-start | bytes 2064388 | tf_op jit(solution)/shard_map/while
  189.9 2.7 copy-start.2
  192.5 21.0 %collective-permute-start = (bf16[448,384]{1,0:T(8,128)(2,1)}, bf16[448,384]{1,0:T(8,128)(2,1)S(1)}, u32[]{:S(2)}, u32[]{:S(2)}) collective-permute-start(bf16[448,384]{1,0:T(8,128)(2,1)} %get-tuple-element.352), channel_id=1, source_target_pairs={{0,16},{16,32},{32,48},{48,64},{64,80},{80,96},{96,112},{112,128},... | collective-permute-start | bytes 1032200 | tf_op jit(solution)/shard_map/while/body/eval_jaxpr/ppermute | solution.py:36
  215.9 5.9 copy-start.4
  215.9 23.2 %all-to-all-start = ((f32[16,28,448]{2,1,0:T(8,128)}), f32[16,28,448]{2,1,0:T(8,128)S(1)}, u32[]{:S(2)}, u32[]{:S(2)}) async-start(f32[16,28,448]{2,1,0:T(8,128)} %reshape.267), calls=%async_computation | async-start | bytes 2097152 | tf_op jit(solution)/shard_map/while/body/eval_jaxpr/all_to_all | solution.py:15
  221.9 37.8 %collective-permute-start.1 = (f32[448,384]{1,0:T(8,128)S(1)}, f32[448,384]{1,0:T(8,128)}, u32[]{:S(2)}, u32[]{:S(2)}) collective-permute-start(f32[448,384]{1,0:T(8,128)S(1)} %broadcast_select_fusion.2), channel_id=1, source_target_pairs={{0,16},{16,32},{32,48},{48,64},{64,80},{80,96},{96,112},{112,128},... | collective-permute-start | bytes 2064392 | tf_op jit(solution)/shard_map/while/body/eval_jaxpr/ppermute | solution.py:36
  241.3 17.8 %all-to-all-start.1 = ((bf16[16,28,448]{2,1,0:T(8,128)(2,1)}), bf16[16,28,448]{2,1,0:T(8,128)(2,1)S(1)}, u32[]{:S(2)}, u32[]{:S(2)}) async-start(bf16[16,28,448]{2,1,0:T(8,128)(2,1)} %broadcast_in_dim.48), calls=%async_computation.1 | async-start | bytes 1048576 | tf_op jit(solution)/shard_map/while/body/eval_jaxpr/all_to_all | solution.py:27
  246.0 13.2 %copy-start.1 = (f32[448,384]{1,0:T(8,128)S(1)}, f32[448,384]{1,0:T(8,128)}, u32[]{:S(2)}) copy-start(f32[448,384]{1,0:T(8,128)} %get-tuple-element.354) | copy-start | bytes 2064388 | tf_op jit(solution)/shard_map/while
  259.7 2.7 copy-start.2
  262.3 21.0 %collective-permute-start = (bf16[448,384]{1,0:T(8,128)(2,1)}, bf16[448,384]{1,0:T(8,128)(2,1)S(1)}, u32[]{:S(2)}, u32[]{:S(2)}) collective-permute-start(bf16[448,384]{1,0:T(8,128)(2,1)} %get-tuple-element.352), channel_id=1, source_target_pairs={{0,16},{16,32},{32,48},{48,64},{64,80},{80,96},{96,112},{112,128},... | collective-permute-start | bytes 1032200 | tf_op jit(solution)/shard_map/while/body/eval_jaxpr/ppermute | solution.py:36
  285.7 5.9 copy-start.4
  285.7 23.1 %all-to-all-start = ((f32[16,28,448]{2,1,0:T(8,128)}), f32[16,28,448]{2,1,0:T(8,128)S(1)}, u32[]{:S(2)}, u32[]{:S(2)}) async-start(f32[16,28,448]{2,1,0:T(8,128)} %reshape.267), calls=%async_computation | async-start | bytes 2097152 | tf_op jit(solution)/shard_map/while/body/eval_jaxpr/all_to_all | solution.py:15
  291.7 37.8 %collective-permute-start.1 = (f32[448,384]{1,0:T(8,128)S(1)}, f32[448,384]{1,0:T(8,128)}, u32[]{:S(2)}, u32[]{:S(2)}) collective-permute-start(f32[448,384]{1,0:T(8,128)S(1)} %broadcast_select_fusion.2), channel_id=1, source_target_pairs={{0,16},{16,32},{32,48},{48,64},{64,80},{80,96},{96,112},{112,128},... | collective-permute-start | bytes 2064392 | tf_op jit(solution)/shard_map/while/body/eval_jaxpr/ppermute | solution.py:36
  311.1 17.8 %all-to-all-start.1 = ((bf16[16,28,448]{2,1,0:T(8,128)(2,1)}), bf16[16,28,448]{2,1,0:T(8,128)(2,1)S(1)}, u32[]{:S(2)}, u32[]{:S(2)}) async-start(bf16[16,28,448]{2,1,0:T(8,128)(2,1)} %broadcast_in_dim.48), calls=%async_computation.1 | async-start | bytes 1048576 | tf_op jit(solution)/shard_map/while/body/eval_jaxpr/all_to_all | solution.py:27
  315.9 13.2 %copy-start.1 = (f32[448,384]{1,0:T(8,128)S(1)}, f32[448,384]{1,0:T(8,128)}, u32[]{:S(2)}) copy-start(f32[448,384]{1,0:T(8,128)} %get-tuple-element.354) | copy-start | bytes 2064388 | tf_op jit(solution)/shard_map/while
  329.5 2.7 copy-start.2
  332.2 21.0 %collective-permute-start = (bf16[448,384]{1,0:T(8,128)(2,1)}, bf16[448,384]{1,0:T(8,128)(2,1)S(1)}, u32[]{:S(2)}, u32[]{:S(2)}) collective-permute-start(bf16[448,384]{1,0:T(8,128)(2,1)} %get-tuple-element.352), channel_id=1, source_target_pairs={{0,16},{16,32},{32,48},{48,64},{64,80},{80,96},{96,112},{112,128},... | collective-permute-start | bytes 1032200 | tf_op jit(solution)/shard_map/while/body/eval_jaxpr/ppermute | solution.py:36
  355.5 5.9 copy-start.4
  355.5 23.2 %all-to-all-start = ((f32[16,28,448]{2,1,0:T(8,128)}), f32[16,28,448]{2,1,0:T(8,128)S(1)}, u32[]{:S(2)}, u32[]{:S(2)}) async-start(f32[16,28,448]{2,1,0:T(8,128)} %reshape.267), calls=%async_computation | async-start | bytes 2097152 | tf_op jit(solution)/shard_map/while/body/eval_jaxpr/all_to_all | solution.py:15
  361.5 37.8 %collective-permute-start.1 = (f32[448,384]{1,0:T(8,128)S(1)}, f32[448,384]{1,0:T(8,128)}, u32[]{:S(2)}, u32[]{:S(2)}) collective-permute-start(f32[448,384]{1,0:T(8,128)S(1)} %broadcast_select_fusion.2), channel_id=1, source_target_pairs={{0,16},{16,32},{32,48},{48,64},{64,80},{80,96},{96,112},{112,128},... | collective-permute-start | bytes 2064392 | tf_op jit(solution)/shard_map/while/body/eval_jaxpr/ppermute | solution.py:36
  381.0 17.8 %all-to-all-start.1 = ((bf16[16,28,448]{2,1,0:T(8,128)(2,1)}), bf16[16,28,448]{2,1,0:T(8,128)(2,1)S(1)}, u32[]{:S(2)}, u32[]{:S(2)}) async-start(bf16[16,28,448]{2,1,0:T(8,128)(2,1)} %broadcast_in_dim.48), calls=%async_computation.1 | async-start | bytes 1048576 | tf_op jit(solution)/shard_map/while/body/eval_jaxpr/all_to_all | solution.py:27
  385.7 13.2 %copy-start.1 = (f32[448,384]{1,0:T(8,128)S(1)}, f32[448,384]{1,0:T(8,128)}, u32[]{:S(2)}) copy-start(f32[448,384]{1,0:T(8,128)} %get-tuple-element.354) | copy-start | bytes 2064388 | tf_op jit(solution)/shard_map/while
  399.3 2.7 copy-start.2
  402.0 21.0 %collective-permute-start = (bf16[448,384]{1,0:T(8,128)(2,1)}, bf16[448,384]{1,0:T(8,128)(2,1)S(1)}, u32[]{:S(2)}, u32[]{:S(2)}) collective-permute-start(bf16[448,384]{1,0:T(8,128)(2,1)} %get-tuple-element.352), channel_id=1, source_target_pairs={{0,16},{16,32},{32,48},{48,64},{64,80},{80,96},{96,112},{112,128},... | collective-permute-start | bytes 1032200 | tf_op jit(solution)/shard_map/while/body/eval_jaxpr/ppermute | solution.py:36
  425.3 5.9 copy-start.4
  425.3 23.1 %all-to-all-start = ((f32[16,28,448]{2,1,0:T(8,128)}), f32[16,28,448]{2,1,0:T(8,128)S(1)}, u32[]{:S(2)}, u32[]{:S(2)}) async-start(f32[16,28,448]{2,1,0:T(8,128)} %reshape.267), calls=%async_computation | async-start | bytes 2097152 | tf_op jit(solution)/shard_map/while/body/eval_jaxpr/all_to_all | solution.py:15
  431.3 37.8 %collective-permute-start.1 = (f32[448,384]{1,0:T(8,128)S(1)}, f32[448,384]{1,0:T(8,128)}, u32[]{:S(2)}, u32[]{:S(2)}) collective-permute-start(f32[448,384]{1,0:T(8,128)S(1)} %broadcast_select_fusion.2), channel_id=1, source_target_pairs={{0,16},{16,32},{32,48},{48,64},{64,80},{80,96},{96,112},{112,128},... | collective-permute-start | bytes 2064392 | tf_op jit(solution)/shard_map/while/body/eval_jaxpr/ppermute | solution.py:36
  450.8 17.8 %all-to-all-start.1 = ((bf16[16,28,448]{2,1,0:T(8,128)(2,1)}), bf16[16,28,448]{2,1,0:T(8,128)(2,1)S(1)}, u32[]{:S(2)}, u32[]{:S(2)}) async-start(bf16[16,28,448]{2,1,0:T(8,128)(2,1)} %broadcast_in_dim.48), calls=%async_computation.1 | async-start | bytes 1048576 | tf_op jit(solution)/shard_map/while/body/eval_jaxpr/all_to_all | solution.py:27
  455.5 13.2 %copy-start.1 = (f32[448,384]{1,0:T(8,128)S(1)}, f32[448,384]{1,0:T(8,128)}, u32[]{:S(2)}) copy-start(f32[448,384]{1,0:T(8,128)} %get-tuple-element.354) | copy-start | bytes 2064388 | tf_op jit(solution)/shard_map/while
  469.1 2.7 copy-start.2
  471.8 21.0 %collective-permute-start = (bf16[448,384]{1,0:T(8,128)(2,1)}, bf16[448,384]{1,0:T(8,128)(2,1)S(1)}, u32[]{:S(2)}, u32[]{:S(2)}) collective-permute-start(bf16[448,384]{1,0:T(8,128)(2,1)} %get-tuple-element.352), channel_id=1, source_target_pairs={{0,16},{16,32},{32,48},{48,64},{64,80},{80,96},{96,112},{112,128},... | collective-permute-start | bytes 1032200 | tf_op jit(solution)/shard_map/while/body/eval_jaxpr/ppermute | solution.py:36
  495.2 5.9 copy-start.4
  495.2 23.2 %all-to-all-start = ((f32[16,28,448]{2,1,0:T(8,128)}), f32[16,28,448]{2,1,0:T(8,128)S(1)}, u32[]{:S(2)}, u32[]{:S(2)}) async-start(f32[16,28,448]{2,1,0:T(8,128)} %reshape.267), calls=%async_computation | async-start | bytes 2097152 | tf_op jit(solution)/shard_map/while/body/eval_jaxpr/all_to_all | solution.py:15
  501.2 37.8 %collective-permute-start.1 = (f32[448,384]{1,0:T(8,128)S(1)}, f32[448,384]{1,0:T(8,128)}, u32[]{:S(2)}, u32[]{:S(2)}) collective-permute-start(f32[448,384]{1,0:T(8,128)S(1)} %broadcast_select_fusion.2), channel_id=1, source_target_pairs={{0,16},{16,32},{32,48},{48,64},{64,80},{80,96},{96,112},{112,128},... | collective-permute-start | bytes 2064392 | tf_op jit(solution)/shard_map/while/body/eval_jaxpr/ppermute | solution.py:36
  520.6 17.8 %all-to-all-start.1 = ((bf16[16,28,448]{2,1,0:T(8,128)(2,1)}), bf16[16,28,448]{2,1,0:T(8,128)(2,1)S(1)}, u32[]{:S(2)}, u32[]{:S(2)}) async-start(bf16[16,28,448]{2,1,0:T(8,128)(2,1)} %broadcast_in_dim.48), calls=%async_computation.1 | async-start | bytes 1048576 | tf_op jit(solution)/shard_map/while/body/eval_jaxpr/all_to_all | solution.py:27
  525.3 13.2 %copy-start.1 = (f32[448,384]{1,0:T(8,128)S(1)}, f32[448,384]{1,0:T(8,128)}, u32[]{:S(2)}) copy-start(f32[448,384]{1,0:T(8,128)} %get-tuple-element.354) | copy-start | bytes 2064388 | tf_op jit(solution)/shard_map/while
  539.0 2.7 copy-start.2
  541.6 21.0 %collective-permute-start.2 = (bf16[448,384]{1,0:T(8,128)(2,1)}, bf16[448,384]{1,0:T(8,128)(2,1)S(1)}, u32[]{:S(2)}, u32[]{:S(2)}) collective-permute-start(bf16[448,384]{1,0:T(8,128)(2,1)} %get-tuple-element.229), channel_id=1, source_target_pairs={{0,16},{16,32},{32,48},{48,64},{64,80},{80,96},{96,112},{112,128},... | collective-permute-start | bytes 1032200 | tf_op jit(solution)/shard_map/ppermute | solution.py:36
  565.0 5.9 copy-start.5
  565.0 32.5 %all-to-all-start.5 = ((f32[16,28,448]{2,1,0:T(8,128)}), f32[16,28,448]{2,1,0:T(8,128)S(1)}, u32[]{:S(2)}, u32[]{:S(2)}) async-start(f32[16,28,448]{2,1,0:T(8,128)} %reshape_reshape.7), calls=%async_computation.5 | async-start | bytes 2097152 | tf_op jit(solution)/shard_map/all_to_all | solution.py:15
  570.9 46.4 %collective-permute-start.3 = (f32[448,384]{1,0:T(8,128)S(1)}, f32[448,384]{1,0:T(8,128)}, u32[]{:S(2)}, u32[]{:S(2)}) collective-permute-start(f32[448,384]{1,0:T(8,128)S(1)} %copy-done.5), channel_id=1, source_target_pairs={{0,144},{16,160},{32,176},{48,192},{64,208},{80,224},{96,240},{112... | collective-permute-start | bytes 2064392 | tf_op jit(solution)/shard_map/ppermute | solution.py:36
  615.3 2.1 copy-start.3
where the time goes:
time: 624 us; the launch traced here: 620 us
  waiting for transfers between devices  333 us (53%)
  starting transfers between devices  189 us (30%)
  local copies, waits for them, and re-layouts  36 us (6%)
  matrix products  29.8 us (5%)
  blocking collectives  16.1 us (3%)
  other arithmetic  14.4 us (2%)
    all_to_all x9, waiting for transfers between devices, sent_and_summed(): parts = lax.all_to_all(in_blocks(array, dim, size), axis, 0, 0, tiled=True)  156 us
    all_to_all x9, waiting for transfers between devices, copy_for_each(): return lax.all_to_all(copies, axis, split_axis=0, concat_axis=0, tiled=True)  104 us
    ppermute x16, starting transfers between devices, from_behind(): lax.ppermute(array, axis, [(i, (i + by) % size) for i in range(size)])  86.2 us
    ppermute x16, waiting for transfers between devices, from_behind(): lax.ppermute(array, axis, [(i, (i + by) % size) for i in range(size)])  72.6 us
    all_to_all x9, starting transfers between devices, sent_and_summed(): parts = lax.all_to_all(in_blocks(array, dim, size), axis, 0, 0, tiled=True)  55.7 us
    all_to_all x9, starting transfers between devices, copy_for_each(): return lax.all_to_all(copies, axis, split_axis=0, concat_axis=0, tiled=True)  47.1 us
    dot_general x7, matrix products, apply_other(): lax.dot_general(amps, rows_i, (((0,), (0,)), ((), ())), preferred_element...  18.4 us
    all_to_all x1, blocking collectives, copy_for_each(): return lax.all_to_all(copies, axis, split_axis=0, concat_axis=0, tiled=True)  16.1 us
  transfers between devices with their start and end apart: 34, of which 27 were waited for; matrix products, arithmetic and copies ran while one was open for 5% of the time, Pallas kernels for 0%

commit v1 on v0

v1 whole, which is shorter than its diff:
```python
import jax
import jax.numpy as jnp
from jax import lax
from jax.sharding import Mesh, PartitionSpec as P

NZ, NXL, NXH, NY, NC = 8, 2, 2, 4, 2
ALL = ("z", "xl", "xh", "y", "c")


def flat(z, xl, xh, y, c):
    return (((z % NZ * NXL + xl % NXL) * NXH + xh % NXH) * NY + y % NY) * NC + c % NC


def moved(array, where):
    pairs = [
        (flat(z, xl, xh, y, c), flat(*where(z, xl, xh, y, c)))
        for z in range(NZ)
        for xl in range(NXL)
        for xh in range(NXH)
        for y in range(NY)
        for c in range(NC)
    ]
    return lax.ppermute(array, ALL, pairs)


def dot_nt(a, b):
    return lax.dot_general(a, b, (((1,), (1,)), ((), ())), preferred_element_type=jnp.float32)


def dot_tn(a, b):
    return lax.dot_general(a, b, (((0,), (0,)), ((), ())), preferred_element_type=jnp.float32)


def local(three_index, occ_energy, vir_energy):
    own = three_index[0]
    nvir, depth = own.shape
    group = NXH * NY
    share = nvir // group
    z, xl, c = lax.axis_index("z"), lax.axis_index("xl"), lax.axis_index("c")
    member = lax.axis_index("xh") * NY + lax.axis_index("y")

    energies = lax.all_gather(occ_energy, ("z", "xl"), axis=0, tiled=True)
    other = moved(own, lambda z, xl, xh, y, c: (z, xl, xh, y, 1 - c))
    mine = jnp.concatenate([own, other], axis=1)
    start = moved(mine, lambda z, xl, xh, y, c: (z, xl if c == 0 else 1 - xl, xh, y, c))

    ahead = [start]
    for _ in range(4):
        ahead.append(moved(ahead[-1], lambda z, xl, xh, y, c: (z - 1 if c == 0 else z + 1, xl, xh, y, c)))
    behind = [start]
    for _ in range(3):
        behind.append(moved(behind[-1], lambda z, xl, xh, y, c: (z + 1 if c == 0 else z - 1, xl, xh, y, c)))

    double = mine * jnp.bfloat16(2)
    numer = jnp.stack([dot_nt(double, block) - dot_nt(block, mine) for block in ahead])
    parts = numer.reshape(5, group, share, nvir).transpose(1, 0, 2, 3)
    parts = lax.all_to_all(parts, ("xh", "y"), 0, 0, tiled=True)
    numer = jnp.sum(parts, axis=0)

    vir_rows = lax.dynamic_slice_in_dim(vir_energy, member * share, share)
    amps = []
    for d in range(5):
        zj = jnp.where(c == 0, z + d, z - d + NZ) % NZ
        xj = jnp.where(c == 0, xl, 1 - xl)
        eps_j = lax.dynamic_slice_in_dim(energies, zj * NXL + xj, 1)
        denom = vir_rows[:, None] + vir_energy[None, :] - occ_energy[0] - eps_j[0]
        amps.append((numer[d] / denom).astype(jnp.bfloat16))
    for d in range(1, 4):
        amps.append(
            moved(
                amps[d],
                lambda z, xl, xh, y, c: (z + d, xl, xh, y, c) if c == 0 else (z - d, 1 - xl, xh, y, c),
            )
        )
    rows = jnp.stack(amps)
    copies = jnp.broadcast_to(rows, (group, *rows.shape))
    gathered = lax.all_to_all(copies, ("xh", "y"), 0, 0, tiled=True)
    gathered = gathered.transpose(1, 0, 2, 3).reshape(8, nvir, nvir)

    total = jnp.zeros((nvir, 2 * depth), jnp.float32)
    for d in range(5):
        total = total + jnp.dot(gathered[d], ahead[d], preferred_element_type=jnp.float32)
    for d in range(1, 4):
        total = total + dot_tn(gathered[4 + d], behind[d])
    back = moved(total[:, depth:], lambda z, xl, xh, y, c: (z, xl, xh, y, 1 - c))
    return (total[:, :depth] + back)[None]


def solution(mesh):
    grid = Mesh(mesh.devices.reshape(NZ, NXL, NXH, NY, NC), ALL)
    return jax.shard_map(
        local,
        mesh=grid,
        in_specs=(P(("z", "xl"), None, ("xh", "y", "c")), P(("z", "xl")), P()),
        out_specs=P(("z", "xl"), None, ("xh", "y", "c")),
        check_vma=False,
    )
```

time: 624 us -> 219 us (0.35)
  waiting for transfers between devices: 333 us -> 80.8 us
  starting transfers between devices: 189 us -> 37.2 us
  blocking collectives: 16.1 us -> 65.4 us
  local copies, waits for them, and re-layouts: 36 us -> 11.2 us
  matrix products: 29.8 us -> 11.9 us
    all_to_all x18 -> x2, waiting for transfers between devices: 260 us -> 11.1 us  [the longest x1 11.1 us: local(): gathered = lax.all_to_all(copies, ('xh', 'y'), 0, 0, tiled=True)]
    all_to_all x18 -> x2, starting transfers between devices: 103 us -> 13.2 us  [the longest x1 6.78 us: local(): parts = lax.all_to_all(parts, ('xh', 'y'), 0, 0, tiled=True)]
    unnamed x0 -> x1, blocking collectives: none -> 65.4 us
    ppermute x16 -> x13, starting transfers between devices: 86.2 us -> 24 us  [moved(): return lax.ppermute(array, ALL, pairs)]
    dot_general x25 -> x18, matrix products: 29.8 us -> 11.9 us  [the longest x10 5.43 us: dot_nt(): lax.dot_general(a, b, (((1,), (1,)), ((), ())), preferred_element_type=jn...]
    all_to_all x1 -> x0, blocking collectives: 16.1 us -> none  [copy_for_each(): return lax.all_to_all(copies, axis, split_axis=0, concat_axis=0, tiled=True)]
    convert_element_type x9 -> x1, other arithmetic: 11.3 us -> 1.99 us  [local(): amps.append((numer[d] / denom).astype(jnp.bfloat16))]
    reshape x16 -> x0, local copies, waits for them, and re-layouts: 9.02 us -> none  [the longest x7 7.53 us: in_blocks(): array.reshape(*shape[:dim], size, shape[dim] // size, *shape[dim + 1:])]
  transfers between devices with their start and end apart: 34 -> 15, of which waited for: 27 -> 11; matrix products, arithmetic and copies ran while one was open for 5% -> 8% of each run, Pallas kernels for 0% -> 0%
where the time goes in v1:
time: 219 us; the launch traced here: 218 us
  waiting for transfers between devices  80.8 us (37%)
  blocking collectives  65.4 us (30%)
  starting transfers between devices  37.2 us (17%)
  matrix products  11.9 us (5%)
  local copies, waits for them, and re-layouts  11.2 us (5%)
  other arithmetic  10.4 us (5%)
    ppermute x13, waiting for transfers between devices, moved(): return lax.ppermute(array, ALL, pairs)  69.8 us
    unnamed x1, blocking collectives  65.4 us
    ppermute x13, starting transfers between devices, moved(): return lax.ppermute(array, ALL, pairs)  24 us
    all_to_all x1, waiting for transfers between devices, local(): gathered = lax.all_to_all(copies, ('xh', 'y'), 0, 0, tiled=True)  11.1 us
    all_to_all x1, starting transfers between devices, local(): parts = lax.all_to_all(parts, ('xh', 'y'), 0, 0, tiled=True)  6.78 us
    all_to_all x1, starting transfers between devices, local(): gathered = lax.all_to_all(copies, ('xh', 'y'), 0, 0, tiled=True)  6.44 us
    unnamed x25, local copies, waits for them, and re-layouts  5.96 us
    dot_general x10, matrix products, dot_nt(): lax.dot_general(a, b, (((1,), (1,)), ((), ())), preferred_element_type=jn...  5.43 us
  transfers between devices with their start and end apart: 15, of which 11 were waited for; matrix products, arithmetic and copies ran while one was open for 8% of the time, Pallas kernels for 0%

profile of v1, /device:TPU:1, one launch (start us, length us, event | category | flops | bytes accessed | tf_op | source)
XLA Modules:
  0.0 218.0 jit_solution(3097354254422162319)
XLA Ops:
  0.0 3.2 %collective-permute-start = (bf16[448,384]{1,0:T(8,128)(2,1)}, bf16[448,384]{1,0:T(8,128)(2,1)S(1)}, u32[]{:S(2)}, u32[]{:S(2)}) collective-permute-start(bf16[448,384]{1,0:T(8,128)(2,1)} %bitcast.85), channel_id=1, source_target_pairs={{0,1},{1,0},{2,3},{3,2},{4,5},{5,4},{6,7},{7,6},{8,9},{9,8},{10,11... | collective-permute-start | bytes 1032200 | tf_op jit(solution)/shard_map/ppermute | solution.py:23
  3.2 1.5 collective-permute-done
  4.7 1.0 pad_maximum_fusion
  5.8 1.9 collective-permute-start.1
  7.7 9.8 %collective-permute-done.1 = bf16[448,768]{1,0:T(8,128)(2,1)S(1)} collective-permute-done((bf16[448,768]{1,0:T(8,128)(2,1)S(1)}, bf16[448,768]{1,0:T(8,128)(2,1)S(1)}, u32[]{:S(2)}, u32[]{:S(2)}) %collective-permute-start.1) | collective-permute-done | bytes 688160 | tf_op jit(solution)/shard_map/ppermute | solution.py:23
  17.5 12.4 %collective-permute-done.2 = bf16[448,768]{1,0:T(8,128)(2,1)S(1)} collective-permute-done((bf16[448,768]{1,0:T(8,128)(2,1)S(1)}, bf16[448,768]{1,0:T(8,128)(2,1)S(1)}, u32[]{:S(2)}, u32[]{:S(2)}) %collective-permute-start.2) | collective-permute-done | bytes 688160 | tf_op jit(solution)/shard_map/ppermute | solution.py:23
  29.9 0.5 fusion.31
  30.5 0.5 convolution_subtract_fusion.4
  31.1 0.5 fusion.30
  31.6 9.3 %collective-permute-done.3 = bf16[448,768]{1,0:T(8,128)(2,1)S(1)} collective-permute-done((bf16[448,768]{1,0:T(8,128)(2,1)S(1)}, bf16[448,768]{1,0:T(8,128)(2,1)S(1)}, u32[]{:S(2)}, u32[]{:S(2)}) %collective-permute-start.3) | collective-permute-done | bytes 688160 | tf_op jit(solution)/shard_map/ppermute | solution.py:23
  40.9 0.5 convolution_subtract_fusion.3
  41.5 0.1 constant_dynamic-update-slice_fusion.3
  41.5 0.5 fusion.29
  42.1 0.5 convolution_subtract_fusion.2
  42.6 9.3 %collective-permute-done.4 = bf16[448,768]{1,0:T(8,128)(2,1)S(1)} collective-permute-done((bf16[448,768]{1,0:T(8,128)(2,1)S(1)}, bf16[448,768]{1,0:T(8,128)(2,1)S(1)}, u32[]{:S(2)}, u32[]{:S(2)}) %collective-permute-start.4) | collective-permute-done | bytes 688160 | tf_op jit(solution)/shard_map/ppermute | solution.py:23
  52.0 0.5 fusion.28
  52.5 0.2 copy-done.2
  52.8 0.5 convolution_subtract_fusion.1
  53.3 0.1 constant_dynamic-update-slice_fusion.1
  53.4 9.5 %collective-permute-done.5 = bf16[448,768]{1,0:T(8,128)(2,1)S(1)} collective-permute-done((bf16[448,768]{1,0:T(8,128)(2,1)S(1)}, bf16[448,768]{1,0:T(8,128)(2,1)S(1)}, u32[]{:S(2)}, u32[]{:S(2)}) %collective-permute-start.5) | collective-permute-done | bytes 688160 | tf_op jit(solution)/shard_map/ppermute | solution.py:23
  62.9 0.5 fusion.27
  63.5 0.5 convolution_subtract_fusion
  64.0 0.1 constant_dynamic-update-slice_fusion
  64.1 2.1 copy-done.1
  66.2 6.8 %all-to-all-start = ((f32[8,5,56,448]{3,2,1,0:T(8,128)}), f32[8,5,56,448]{3,2,1,0:T(8,128)}, u32[]{:S(2)}, u32[]{:S(2)}) async-start(f32[8,5,56,448]{3,2,1,0:T(8,128)} %bitcast.97), calls=%async_computation | async-start | bytes 9175040 | tf_op jit(solution)/shard_map/all_to_all | solution.py:57
  73.7 0.6 dynamic-slice
  74.3 0.1 dynamic_slice.18
  74.4 0.7 dynamic-update-slice
  75.1 65.4 %all-reduce = f32[16]{0:T(128)S(1)} all-reduce(f32[16]{0:T(128)S(1)} %dynamic-update-slice), channel_id=1, replica_groups=mesh['z'=8,'xl'=2,'xh'=2,'y'=4,'c'=2] {'z','xl'}, use_global_device_ids=true, to_apply=%add | all-reduce | flops 16 | bytes 128
  140.5 0.7 fusion.33
  141.2 2.9 %reduce_sum.9 = f32[5,56,448]{2,1,0:T(8,128)S(1)} reduce(f32[8,5,56,448]{3,2,1,0:T(8,128)} %all-to-all-done, f32[]{:T(128)} %constant.60.clone.1), dimensions={0}, to_apply=%region_0.0 | reduce | flops 878080 | bytes 4515844 | tf_op jit(solution)/shard_map/reduce_sum | solution.py:58
  144.1 2.0 fusion.14
  146.1 0.1 collective-permute-start.6
  146.2 0.1 collective-permute-start.7
  146.3 1.9 collective-permute-start.8
  148.2 0.7 fusion.20
  148.9 0.6 fusion.17
  149.6 0.8 fusion.18
  150.3 0.7 fusion.19
  151.1 0.7 fusion.21
  151.8 0.4 collective-permute-done.8
  152.3 2.2 broadcast_in_dim.4
  154.5 6.4 %all-to-all-start.1 = ((bf16[8,8,56,448]{3,2,1,0:T(8,128)(2,1)}), bf16[8,8,56,448]{3,2,1,0:T(8,128)(2,1)}, u32[]{:S(2)}, u32[]{:S(2)}) async-start(bf16[8,8,56,448]{3,2,1,0:T(8,128)(2,1)} %broadcast_in_dim.4), calls=%async_computation.1 | async-start | bytes 7340032 | tf_op jit(solution)/shard_map/all_to_all | solution.py:77
  160.9 3.5 %collective-permute-start.9 = (bf16[448,768]{1,0:T(8,128)(2,1)S(1)}, bf16[448,768]{1,0:T(8,128)(2,1)S(1)}, u32[]{:S(2)}, u32[]{:S(2)}) collective-permute-start(bf16[448,768]{1,0:T(8,128)(2,1)S(1)} %collective-permute-done.1), channel_id=1, source_target_pairs={{0,32},{1,225},{2,34},{3,227},{4,36},{5,229},{6,38},{7,231},{8,40}... | collective-permute-start | bytes 2064392 | tf_op jit(solution)/shard_map/ppermute | solution.py:23
  164.4 7.9 %collective-permute-done.9 = bf16[448,768]{1,0:T(8,128)(2,1)S(1)} collective-permute-done((bf16[448,768]{1,0:T(8,128)(2,1)S(1)}, bf16[448,768]{1,0:T(8,128)(2,1)S(1)}, u32[]{:S(2)}, u32[]{:S(2)}) %collective-permute-start.9) | collective-permute-done | bytes 688160 | tf_op jit(solution)/shard_map/ppermute | solution.py:23
  172.3 0.8 copy-done.4
  173.2 3.5 %collective-permute-start.10 = (bf16[448,768]{1,0:T(8,128)(2,1)S(1)}, bf16[448,768]{1,0:T(8,128)(2,1)}, u32[]{:S(2)}, u32[]{:S(2)}) collective-permute-start(bf16[448,768]{1,0:T(8,128)(2,1)S(1)} %collective-permute-done.9), channel_id=1, source_target_pairs={{0,32},{1,225},{2,34},{3,227},{4,36},{5,229},{6,38},{7,231},{8,40}... | collective-permute-start | bytes 2064392 | tf_op jit(solution)/shard_map/ppermute | solution.py:23
  176.7 7.9 %collective-permute-done.10 = bf16[448,768]{1,0:T(8,128)(2,1)} collective-permute-done((bf16[448,768]{1,0:T(8,128)(2,1)S(1)}, bf16[448,768]{1,0:T(8,128)(2,1)}, u32[]{:S(2)}, u32[]{:S(2)}) %collective-permute-start.10) | collective-permute-done | bytes 688160 | tf_op jit(solution)/shard_map/ppermute | solution.py:23
  184.5 3.5 %collective-permute-start.11 = (bf16[448,768]{1,0:T(8,128)(2,1)}, bf16[448,768]{1,0:T(8,128)(2,1)}, u32[]{:S(2)}, u32[]{:S(2)}) collective-permute-start(bf16[448,768]{1,0:T(8,128)(2,1)} %collective-permute-done.10), channel_id=1, source_target_pairs={{0,32},{1,225},{2,34},{3,227},{4,36},{5,229},{6,38},{7,231},{8,40}... | collective-permute-start | bytes 2064392 | tf_op jit(solution)/shard_map/ppermute | solution.py:23
  188.1 11.1 %all-to-all-done.1 = bf16[8,8,56,448]{3,2,1,0:T(8,128)(2,1)} async-done(((bf16[8,8,56,448]{3,2,1,0:T(8,128)(2,1)}), bf16[8,8,56,448]{3,2,1,0:T(8,128)(2,1)}, u32[]{:S(2)}, u32[]{:S(2)}) %all-to-all-start.1) | async-done | bytes 3211296 | tf_op jit(solution)/shard_map/all_to_all | solution.py:77
  199.1 2.2 %fusion.32 = (bf16[1,8,56,448]{3,2,0,1:T(8,128)(2,1)S(1)}, bf16[1,8,56,448]{3,2,0,1:T(8,128)(2,1)S(1)}, bf16[1,8,56,448]{3,2,0,1:T(8,128)(2,1)S(1)}, bf16[1,8,56...) fusion(bf16[8,8,56,448]{3,2,0,1:T(8,128)(2,1)} %bitcast.25), kind=kLoop, calls=%fused_computation.63 | loop fusion | bytes 6422528 | tf_op jit(solution)/shard_map/slice | solution.py:84
  201.4 0.5 fusion.34
  201.9 0.5 convolution_add_fusion.5
  202.4 0.5 convolution_add_fusion.4
  203.0 0.6 copy-done.3
  203.5 0.5 convolution_add_fusion.3
  204.1 0.6 copy-done.5
  204.6 0.5 fusion.35
  205.2 0.5 fusion
  205.7 1.7 convolution_add_fusion.1
  207.4 1.7 convolution_add_fusion
  209.1 6.2 %collective-permute-start.12 = (f32[448,384]{1,0:T(8,128)S(1)}, f32[448,384]{1,0:T(8,128)S(1)}, u32[]{:S(2)}, u32[]{:S(2)}) collective-permute-start(f32[448,384]{1,0:T(8,128)S(1)} %slice.82), channel_id=1, source_target_pairs={{0,1},{1,0},{2,3},{3,2},{4,5},{5,4},{6,7},{7,6},{8,9},{9,8},{10,11... | collective-permute-start | bytes 2064392 | tf_op jit(solution)/shard_map/ppermute | solution.py:23
  215.3 1.8 collective-permute-done.12
  217.1 0.9 fusion.1
  (26 shorter events, 0.2 us)
Async XLA Ops:
  0.0 29.9 %copy-start = (bf16[1,448,384]{2,1,0:T(8,128)(2,1)S(1)}, bf16[1,448,384]{2,1,0:T(8,128)(2,1)}, u32[]{:S(2)}) copy-start(bf16[1,448,384]{2,1,0:T(8,128)(2,1)} %param.3) | copy-start | bytes 1032196
  0.0 4.7 %collective-permute-start = (bf16[448,384]{1,0:T(8,128)(2,1)}, bf16[448,384]{1,0:T(8,128)(2,1)S(1)}, u32[]{:S(2)}, u32[]{:S(2)}) collective-permute-start(bf16[448,384]{1,0:T(8,128)(2,1)} %bitcast.85), channel_id=1, source_target_pairs={{0,1},{1,0},{2,3},{3,2},{4,5},{5,4},{6,7},{7,6},{8,9},{9,8},{10,11... | collective-permute-start | bytes 1032200 | tf_op jit(solution)/shard_map/ppermute | solution.py:23
  5.8 11.7 %collective-permute-start.1 = (bf16[448,768]{1,0:T(8,128)(2,1)S(1)}, bf16[448,768]{1,0:T(8,128)(2,1)S(1)}, u32[]{:S(2)}, u32[]{:S(2)}) collective-permute-start(bf16[448,768]{1,0:T(8,128)(2,1)S(1)} %pad_maximum_fusion), channel_id=1, source_target_pairs={{0,0},{1,17},{2,2},{3,19},{4,4},{5,21},{6,6},{7,23},{8,8},{9,25},{... | collective-permute-start | bytes 2064392 | tf_op jit(solution)/shard_map/ppermute | solution.py:23
  17.5 12.4 %collective-permute-start.2 = (bf16[448,768]{1,0:T(8,128)(2,1)S(1)}, bf16[448,768]{1,0:T(8,128)(2,1)S(1)}, u32[]{:S(2)}, u32[]{:S(2)}) collective-permute-start(bf16[448,768]{1,0:T(8,128)(2,1)S(1)} %collective-permute-done.1), channel_id=1, source_target_pairs={{0,224},{1,33},{2,226},{3,35},{4,228},{5,37},{6,230},{7,39},{8,232... | collective-permute-start | bytes 2064392 | tf_op jit(solution)/shard_map/ppermute | solution.py:23
  29.9 11.0 %collective-permute-start.3 = (bf16[448,768]{1,0:T(8,128)(2,1)S(1)}, bf16[448,768]{1,0:T(8,128)(2,1)S(1)}, u32[]{:S(2)}, u32[]{:S(2)}) collective-permute-start(bf16[448,768]{1,0:T(8,128)(2,1)S(1)} %collective-permute-done.2), channel_id=1, source_target_pairs={{0,224},{1,33},{2,226},{3,35},{4,228},{5,37},{6,230},{7,39},{8,232... | collective-permute-start | bytes 2064392 | tf_op jit(solution)/shard_map/ppermute | solution.py:23
  40.9 11.0 %collective-permute-start.4 = (bf16[448,768]{1,0:T(8,128)(2,1)S(1)}, bf16[448,768]{1,0:T(8,128)(2,1)S(1)}, u32[]{:S(2)}, u32[]{:S(2)}) collective-permute-start(bf16[448,768]{1,0:T(8,128)(2,1)S(1)} %collective-permute-done.3), channel_id=1, source_target_pairs={{0,224},{1,33},{2,226},{3,35},{4,228},{5,37},{6,230},{7,39},{8,232... | collective-permute-start | bytes 2064392 | tf_op jit(solution)/shard_map/ppermute | solution.py:23
  51.9 0.9 copy-start.2
  51.9 11.0 %collective-permute-start.5 = (bf16[448,768]{1,0:T(8,128)(2,1)S(1)}, bf16[448,768]{1,0:T(8,128)(2,1)S(1)}, u32[]{:S(2)}, u32[]{:S(2)}) collective-permute-start(bf16[448,768]{1,0:T(8,128)(2,1)S(1)} %collective-permute-done.4), channel_id=1, source_target_pairs={{0,224},{1,33},{2,226},{3,35},{4,228},{5,37},{6,230},{7,39},{8,232... | collective-permute-start | bytes 2064392 | tf_op jit(solution)/shard_map/ppermute | solution.py:23
  64.1 2.1 copy-start.1
  66.2 7.5 %copy-start.7 = (u32[256]{0:T(256)S(1)}, u32[256]{0:T(256)}, u32[]{:S(2)}) copy-start(u32[256]{0:T(256)} %constant.82) | copy-start | bytes 3076
  66.2 8.1 %copy-start.6 = (f32[448]{0:T(512)S(1)}, f32[448]{0:T(512)}, u32[]{:S(2)}) copy-start(f32[448]{0:T(512)} %param.5) | copy-start | bytes 5380
  66.2 75.0 %all-to-all-start = ((f32[8,5,56,448]{3,2,1,0:T(8,128)}), f32[8,5,56,448]{3,2,1,0:T(8,128)}, u32[]{:S(2)}, u32[]{:S(2)}) async-start(f32[8,5,56,448]{3,2,1,0:T(8,128)} %bitcast.97), calls=%async_computation | async-start | bytes 9175040 | tf_op jit(solution)/shard_map/all_to_all | solution.py:57
  146.1 5.7 %collective-permute-start.6 = (bf16[56,448]{1,0:T(8,128)(2,1)S(1)}, bf16[56,448]{1,0:T(8,128)(2,1)S(1)}, u32[]{:S(2)}, u32[]{:S(2)}) collective-permute-start(bf16[56,448]{1,0:T(8,128)(2,1)S(1)} %get-tuple-element.14), channel_id=1, source_target_pairs={{0,32},{1,241},{2,34},{3,243},{4,36},{5,245},{6,38},{7,247},{8,40}... | collective-permute-start | bytes 150536 | tf_op jit(solution)/shard_map/ppermute | solution.py:23
  146.2 5.6 %collective-permute-start.7 = (bf16[56,448]{1,0:T(8,128)(2,1)S(1)}, bf16[56,448]{1,0:T(8,128)(2,1)S(1)}, u32[]{:S(2)}, u32[]{:S(2)}) collective-permute-start(bf16[56,448]{1,0:T(8,128)(2,1)S(1)} %get-tuple-element.15), channel_id=1, source_target_pairs={{0,64},{1,209},{2,66},{3,211},{4,68},{5,213},{6,70},{7,215},{8,72}... | collective-permute-start | bytes 150536 | tf_op jit(solution)/shard_map/ppermute | solution.py:23
  146.3 6.0 %collective-permute-start.8 = (bf16[56,448]{1,0:T(8,128)(2,1)S(1)}, bf16[56,448]{1,0:T(8,128)(2,1)S(1)}, u32[]{:S(2)}, u32[]{:S(2)}) collective-permute-start(bf16[56,448]{1,0:T(8,128)(2,1)S(1)} %get-tuple-element.13), channel_id=1, source_target_pairs={{0,96},{1,177},{2,98},{3,179},{4,100},{5,181},{6,102},{7,183},{8,1... | collective-permute-start | bytes 150536 | tf_op jit(solution)/shard_map/ppermute | solution.py:23
  154.5 44.7 %all-to-all-start.1 = ((bf16[8,8,56,448]{3,2,1,0:T(8,128)(2,1)}), bf16[8,8,56,448]{3,2,1,0:T(8,128)(2,1)}, u32[]{:S(2)}, u32[]{:S(2)}) async-start(bf16[8,8,56,448]{3,2,1,0:T(8,128)(2,1)} %broadcast_in_dim.4), calls=%async_computation.1 | async-start | bytes 7340032 | tf_op jit(solution)/shard_map/all_to_all | solution.py:77
  160.9 11.4 %collective-permute-start.9 = (bf16[448,768]{1,0:T(8,128)(2,1)S(1)}, bf16[448,768]{1,0:T(8,128)(2,1)S(1)}, u32[]{:S(2)}, u32[]{:S(2)}) collective-permute-start(bf16[448,768]{1,0:T(8,128)(2,1)S(1)} %collective-permute-done.1), channel_id=1, source_target_pairs={{0,32},{1,225},{2,34},{3,227},{4,36},{5,229},{6,38},{7,231},{8,40}... | collective-permute-start | bytes 2064392 | tf_op jit(solution)/shard_map/ppermute | solution.py:23
  172.3 0.8 copy-start.4
  173.2 11.4 %collective-permute-start.10 = (bf16[448,768]{1,0:T(8,128)(2,1)S(1)}, bf16[448,768]{1,0:T(8,128)(2,1)}, u32[]{:S(2)}, u32[]{:S(2)}) collective-permute-start(bf16[448,768]{1,0:T(8,128)(2,1)S(1)} %collective-permute-done.9), channel_id=1, source_target_pairs={{0,32},{1,225},{2,34},{3,227},{4,36},{5,229},{6,38},{7,231},{8,40}... | collective-permute-start | bytes 2064392 | tf_op jit(solution)/shard_map/ppermute | solution.py:23
  184.5 22.8 %collective-permute-start.11 = (bf16[448,768]{1,0:T(8,128)(2,1)}, bf16[448,768]{1,0:T(8,128)(2,1)}, u32[]{:S(2)}, u32[]{:S(2)}) collective-permute-start(bf16[448,768]{1,0:T(8,128)(2,1)} %collective-permute-done.10), channel_id=1, source_target_pairs={{0,32},{1,225},{2,34},{3,227},{4,36},{5,229},{6,38},{7,231},{8,40}... | collective-permute-start | bytes 2064392 | tf_op jit(solution)/shard_map/ppermute | solution.py:23
  202.4 1.1 copy-start.3
  203.5 1.1 copy-start.5
  209.1 8.0 %collective-permute-start.12 = (f32[448,384]{1,0:T(8,128)S(1)}, f32[448,384]{1,0:T(8,128)S(1)}, u32[]{:S(2)}, u32[]{:S(2)}) collective-permute-start(f32[448,384]{1,0:T(8,128)S(1)} %slice.82), channel_id=1, source_target_pairs={{0,1},{1,0},{2,3},{3,2},{4,5},{5,4},{6,7},{7,6},{8,9},{9,8},{10,11... | collective-permute-start | bytes 2064392 | tf_op jit(solution)/shard_map/ppermute | solution.py:23

commit v2 on v1

--- a/solution.py
+++ b/solution.py
@@ -5,6 +5,7 @@
 
 NZ, NXL, NXH, NY, NC = 8, 2, 2, 4, 2
 ALL = ("z", "xl", "xh", "y", "c")
+CHUNKS = ((0, 1), (2, 3), (4,))
 
 
 def flat(z, xl, xh, y, c):
@@ -39,7 +40,8 @@
     z, xl, c = lax.axis_index("z"), lax.axis_index("xl"), lax.axis_index("c")
     member = lax.axis_index("xh") * NY + lax.axis_index("y")
 
-    energies = lax.all_gather(occ_energy, ("z", "xl"), axis=0, tiled=True)
+    copies = jnp.broadcast_to(occ_energy, (NZ * NXL, 1))
+    energies = lax.all_to_all(copies, ("z", "xl"), 0, 0, tiled=True)[:, 0]
     other = moved(own, lambda z, xl, xh, y, c: (z, xl, xh, y, 1 - c))
     mine = jnp.concatenate([own, other], axis=1)
     start = moved(mine, lambda z, xl, xh, y, c: (z, xl if c == 0 else 1 - xl, xh, y, c))
@@ -51,37 +53,45 @@
     for _ in range(3):
         behind.append(moved(behind[-1], lambda z, xl, xh, y, c: (z + 1 if c == 0 else z - 1, xl, xh, y, c)))
 
+    ahead[1], energies = lax.optimization_barrier((ahead[1], energies))
+
     double = mine * jnp.bfloat16(2)
-    numer = jnp.stack([dot_nt(double, block) - dot_nt(block, mine) for block in ahead])
-    parts = numer.reshape(5, group, share, nvir).transpose(1, 0, 2, 3)
-    parts = lax.all_to_all(parts, ("xh", "y"), 0, 0, tiled=True)
-    numer = jnp.sum(parts, axis=0)
+    vir_rows = lax.dynamic_slice_in_dim(vir_energy, member * share, share)
 
-    vir_rows = lax.dynamic_slice_in_dim(vir_energy, member * share, share)
-    amps = []
-    for d in range(5):
+    def summed(steps):
+        numer = [dot_nt(double, ahead[d]) - dot_nt(ahead[d], mine) for d in steps]
+        parts = jnp.stack([part.reshape(group, share, nvir) for part in numer], axis=1)
+        return jnp.sum(lax.all_to_all(parts, ("xh", "y"), 0, 0, tiled=True), axis=0)
+
+    def amps_of(d, numer):
         zj = jnp.where(c == 0, z + d, z - d + NZ) % NZ
         xj = jnp.where(c == 0, xl, 1 - xl)
         eps_j = lax.dynamic_slice_in_dim(energies, zj * NXL + xj, 1)
         denom = vir_rows[:, None] + vir_energy[None, :] - occ_energy[0] - eps_j[0]
-        amps.append((numer[d] / denom).astype(jnp.bfloat16))
-    for d in range(1, 4):
-        amps.append(
-            moved(
-                amps[d],
-                lambda z, xl, xh, y, c: (z + d, xl, xh, y, c) if c == 0 else (z - d, 1 - xl, xh, y, c),
-            )
+        return (numer / denom).astype(jnp.bfloat16)
+
+    def mirrored(d, amps):
+        return moved(
+            amps,
+            lambda z, xl, xh, y, c: (z + d, xl, xh, y, c) if c == 0 else (z - d, 1 - xl, xh, y, c),
         )
-    rows = jnp.stack(amps)
-    copies = jnp.broadcast_to(rows, (group, *rows.shape))
-    gathered = lax.all_to_all(copies, ("xh", "y"), 0, 0, tiled=True)
-    gathered = gathered.transpose(1, 0, 2, 3).reshape(8, nvir, nvir)
+
+    def gathered(parts):
+        rows = jnp.stack(parts)
+        copies = jnp.broadcast_to(rows, (group, *rows.shape))
+        whole = lax.all_to_all(copies, ("xh", "y"), 0, 0, tiled=True)
+        return [whole[:, n].reshape(nvir, nvir) for n in range(len(parts))]
 
     total = jnp.zeros((nvir, 2 * depth), jnp.float32)
-    for d in range(5):
-        total = total + jnp.dot(gathered[d], ahead[d], preferred_element_type=jnp.float32)
-    for d in range(1, 4):
-        total = total + dot_tn(gathered[4 + d], behind[d])
+    for steps in CHUNKS:
+        numer = summed(steps)
+        amps = [amps_of(d, numer[n]) for n, d in enumerate(steps)]
+        turned = [d for d in steps if 0 < d < 4]
+        blocks = gathered(amps + [mirrored(d, amps[steps.index(d)]) for d in turned])
+        for n, d in enumerate(steps):
+            total = total + jnp.dot(blocks[n], ahead[d], preferred_element_type=jnp.float32)
+        for n, d in enumerate(turned):
+            total = total + dot_tn(blocks[len(steps) + n], behind[d])
     back = moved(total[:, depth:], lambda z, xl, xh, y, c: (z, xl, xh, y, 1 - c))
     return (total[:, :depth] + back)[None]
 

time: 219 us -> 209 us (0.954)
  blocking collectives: 65.4 us -> 14 us
  waiting for transfers between devices: 80.8 us -> 99.8 us
  matrix products: 11.9 us -> 25.3 us
  starting transfers between devices: 37.2 us -> 49.9 us
  local copies, waits for them, and re-layouts: 11.2 us -> 5.49 us
    unnamed x1 -> x0, blocking collectives: 65.4 us -> none
    all_to_all x2 -> x6, waiting for transfers between devices: 11.1 us -> 58.4 us  [the longest x3 34 us: summed(): return jnp.sum(lax.all_to_all(parts, ('xh', 'y'), 0, 0, tiled=True), axis=0)]
    ppermute x13, waiting for transfers between devices: 69.8 us -> 41.4 us  [moved(): return lax.ppermute(array, ALL, pairs)]
    all_to_all x2 -> x6, starting transfers between devices: 13.2 us -> 31.8 us  [the longest x3 16.4 us: gathered(): whole = lax.all_to_all(copies, ('xh', 'y'), 0, 0, tiled=True)]
    all_to_all x0 -> x1, blocking collectives: none -> 14 us  [local(): energies = lax.all_to_all(copies, ('z', 'xl'), 0, 0, tiled=True)[:, 0]]
    dot_general x10, matrix products: 5.43 us -> 14.2 us  [dot_nt(): lax.dot_general(a, b, (((1,), (1,)), ((), ())), preferred_element_type=jn...]
    ppermute x13, starting transfers between devices: 24 us -> 18 us  [moved(): return lax.ppermute(array, ALL, pairs)]
    unnamed x25 -> x18, local copies, waits for them, and re-layouts: 5.96 us -> 0.97 us
  transfers between devices with their start and end apart: 15 -> 19, of which waited for: 11 -> 15; matrix products, arithmetic and copies ran while one was open for 8% -> 18% of each run, Pallas kernels for 0% -> 0%
where the time goes in v2:
time: 209 us; the launch traced here: 208 us
  waiting for transfers between devices  99.8 us (48%)
  starting transfers between devices  49.9 us (24%)
  matrix products  25.3 us (12%)
  blocking collectives  14 us (7%)
  other arithmetic  12.3 us (6%)
  local copies, waits for them, and re-layouts  5.49 us (3%)
    ppermute x13, waiting for transfers between devices, moved(): return lax.ppermute(array, ALL, pairs)  41.4 us
    all_to_all x3, waiting for transfers between devices, summed(): return jnp.sum(lax.all_to_all(parts, ('xh', 'y'), 0, 0, tiled=True), axis=0)  34 us
    all_to_all x3, waiting for transfers between devices, gathered(): whole = lax.all_to_all(copies, ('xh', 'y'), 0, 0, tiled=True)  24.5 us
    ppermute x13, starting transfers between devices, moved(): return lax.ppermute(array, ALL, pairs)  18 us
    all_to_all x3, starting transfers between devices, gathered(): whole = lax.all_to_all(copies, ('xh', 'y'), 0, 0, tiled=True)  16.4 us
    all_to_all x3, starting transfers between devices, summed(): return jnp.sum(lax.all_to_all(parts, ('xh', 'y'), 0, 0, tiled=True), axis=0)  15.4 us
    dot_general x10, matrix products, dot_nt(): lax.dot_general(a, b, (((1,), (1,)), ((), ())), preferred_element_type=jn...  14.2 us
    all_to_all x1, blocking collectives, local(): energies = lax.all_to_all(copies, ('z', 'xl'), 0, 0, tiled=True)[:, 0]  14 us
  transfers between devices with their start and end apart: 19, of which 15 were waited for; matrix products, arithmetic and copies ran while one was open for 18% of the time, Pallas kernels for 0%

profile of v2, /device:TPU:1, one launch (start us, length us, event | category | flops | bytes accessed | tf_op | source)
XLA Modules:
  0.0 207.7 jit_solution(7495488237592939516)
XLA Ops:
  0.0 3.2 %collective-permute-start = (bf16[448,384]{1,0:T(8,128)(2,1)}, bf16[448,384]{1,0:T(8,128)(2,1)S(1)}, u32[]{:S(2)}, u32[]{:S(2)}) collective-permute-start(bf16[448,384]{1,0:T(8,128)(2,1)} %bitcast.76), channel_id=1, source_target_pairs={{0,1},{1,0},{2,3},{3,2},{4,5},{5,4},{6,7},{7,6},{8,9},{9,8},{10,11... | collective-permute-start | bytes 1032200 | tf_op jit(solution)/shard_map/ppermute | solution.py:24
  3.2 1.5 collective-permute-done
  4.7 1.0 pad_maximum_fusion.2
  5.8 1.9 collective-permute-start.1
  7.7 10.0 %collective-permute-done.1 = bf16[448,768]{1,0:T(8,128)(2,1)} collective-permute-done((bf16[448,768]{1,0:T(8,128)(2,1)S(1)}, bf16[448,768]{1,0:T(8,128)(2,1)}, u32[]{:S(2)}, u32[]{:S(2)}) %collective-permute-start.1) | collective-permute-done | bytes 688160 | tf_op jit(solution)/shard_map/ppermute | solution.py:24
  17.8 12.4 %collective-permute-done.2 = bf16[448,768]{1,0:T(8,128)(2,1)S(1)} collective-permute-done((bf16[448,768]{1,0:T(8,128)(2,1)}, bf16[448,768]{1,0:T(8,128)(2,1)S(1)}, u32[]{:S(2)}, u32[]{:S(2)}) %collective-permute-start.2) | collective-permute-done | bytes 688160 | tf_op jit(solution)/shard_map/ppermute | solution.py:24
  30.8 14.0 %all_to_all.36 = f32[16,1,1]{2,1,0:T(1,128)S(1)} all-to-all(f32[16,1,1]{2,1,0:T(1,128)S(1)} %broadcast_in_dim.10), channel_id=1, replica_groups=mesh['z'=8,'xl'=2,'xh'=2,'y'=4,'c'=2] {'z','xl'}, dimensions={0} | all-to-all | bytes 128 | tf_op jit(solution)/shard_map/all_to_all | solution.py:44
  44.8 0.2 reduce.1
  45.0 1.6 fusion.25
  46.7 1.6 convolution_subtract_fusion.4
  48.3 0.5 collective-permute-start.6
  48.9 0.5 fusion.24
  49.4 1.6 convolution_subtract_fusion.3
  51.1 1.5 pad_maximum_fusion
  52.5 6.3 %all-to-all-start.1 = ((f32[8,2,56,448]{3,2,1,0:T(8,128)}), f32[8,2,56,448]{3,2,1,0:T(8,128)S(1)}, u32[]{:S(2)}, u32[]{:S(2)}) async-start(f32[8,2,56,448]{3,2,1,0:T(8,128)} %pad_maximum_fusion), calls=%async_computation.1 | async-start | bytes 3670016 | tf_op jit(solution)/shard_map/all_to_all | solution.py:64
  58.8 1.1 collective-permute-done.6
  59.9 1.9 fusion.23
  61.8 2.6 %convolution_subtract_fusion.2 = f32[448,448]{1,0:T(8,128)} fusion(f32[448,448]{1,0:T(8,128)S(1)} %fusion.23, bf16[448,768]{1,0:T(8,128)(2,1)} %collective-permute-done.5, bf16[448,384]{1,0:T(8,128)(2,1)S(1)} %collective-permute-done, bf16[448,384]{1,0:T(8,128)(2,1)S(1)} %bitcast.83), kind=kOutput, calls=%fused_computation.11 | convolution fusion | flops 310546432 | bytes 2981888 | tf_op jit(solution)/shard_map/dot_general | solution.py:28
  64.4 6.5 %collective-permute-done.11 = bf16[448,768]{1,0:T(8,128)(2,1)S(1)} collective-permute-done((bf16[448,768]{1,0:T(8,128)(2,1)S(1)}, bf16[448,768]{1,0:T(8,128)(2,1)S(1)}, u32[]{:S(2)}, u32[]{:S(2)}) %collective-permute-start.11) | collective-permute-done | bytes 688160 | tf_op jit(solution)/shard_map/ppermute | solution.py:24
  70.9 0.5 fusion.21
  71.5 0.3 copy-done.5
  71.8 1.5 convolution_subtract_fusion
  73.3 2.5 %all-to-all-done.1 = f32[8,2,56,448]{3,2,1,0:T(8,128)S(1)} async-done(((f32[8,2,56,448]{3,2,1,0:T(8,128)}), f32[8,2,56,448]{3,2,1,0:T(8,128)S(1)}, u32[]{:S(2)}, u32[]{:S(2)}) %all-to-all-start.1) | async-done | bytes 1605664 | tf_op jit(solution)/shard_map/all_to_all | solution.py:64
  75.7 4.5 %all-to-all-start.5 = ((f32[8,1,56,448]{3,2,1,0:T(8,128)}), f32[8,1,56,448]{3,2,1,0:T(8,128)S(1)}, u32[]{:S(2)}, u32[]{:S(2)}) async-start(f32[8,1,56,448]{3,2,1,0:T(8,128)} %bitcast.92), calls=%async_computation.5 | async-start | bytes 1835008 | tf_op jit(solution)/shard_map/all_to_all | solution.py:64
  80.2 1.7 fusion.22
  82.0 0.5 convolution_subtract_fusion.1
  82.5 0.6 copy-done.1
  83.1 1.4 pad_maximum_fusion.1
  84.6 9.8 %all-to-all-done.5 = f32[8,1,56,448]{3,2,1,0:T(8,128)S(1)} async-done(((f32[8,1,56,448]{3,2,1,0:T(8,128)}), f32[8,1,56,448]{3,2,1,0:T(8,128)S(1)}, u32[]{:S(2)}, u32[]{:S(2)}) %all-to-all-start.5) | async-done | bytes 802848 | tf_op jit(solution)/shard_map/all_to_all | solution.py:64
  94.4 4.7 %all-to-all-start.3 = ((f32[8,2,56,448]{3,2,1,0:T(8,128)}), f32[8,2,56,448]{3,2,1,0:T(8,128)}, u32[]{:S(2)}, u32[]{:S(2)}) async-start(f32[8,2,56,448]{3,2,1,0:T(8,128)} %pad_maximum_fusion.1), calls=%async_computation.3 | async-start | bytes 3670016 | tf_op jit(solution)/shard_map/all_to_all | solution.py:64
  99.1 0.8 collective-permute-start.4
  99.9 0.7 fusion.28
  100.6 0.2 reduce_sum.27
  100.8 21.7 %all-to-all-done.3 = f32[8,2,56,448]{3,2,1,0:T(8,128)} async-done(((f32[8,2,56,448]{3,2,1,0:T(8,128)}), f32[8,2,56,448]{3,2,1,0:T(8,128)}, u32[]{:S(2)}, u32[]{:S(2)}) %all-to-all-start.3) | async-done | bytes 1605664 | tf_op jit(solution)/shard_map/all_to_all | solution.py:64
  122.5 1.7 reduce_sum.28
  124.2 2.6 %fusion.14 = (bf16[56,448]{1,0:T(8,128)(2,1)S(1)}, bf16[56,448]{1,0:T(8,128)(2,1)S(1)}, bf16[56,448]{1,0:T(8,128)(2,1)S(1)}, bf16[56,448]{1,0:T(8,128)(2,1)S(1)}) fusion(f32[2,56,448]{2,1,0:T(8,128)S(1)} %reduce_sum.28, f32[]{:T(128)} %bitcast.17, f32[]{:T(128)} %bitcast.75, f32[448]{0:T(512)S(1)} %copy-done.8, f32[56]{0:T(128)S(1)} %dynamic_slice.18, ...), kind=kLoop, calls=%fused_computation.34 | loop fusion | flops 351232 | bytes 604148 | tf_op jit(solution)/shard_map/convert_element_type | solution.py:71
  126.8 0.7 collective-permute-start.3
  127.5 2.6 %fusion.12 = (bf16[1,56,448]{2,1,0:T(8,128)(2,1)S(1)}, bf16[1,56,448]{2,1,0:T(8,128)(2,1)S(1)}, bf16[1,56,448]{2,1,0:T(8,128)(2,1)S(1)}, bf16[1,56,448]{2,1,0:T(8,128)(2,1)S(1)}) fusion(f32[2,56,448]{2,1,0:T(8,128)S(1)} %reduce_sum.27, f32[]{:T(128)} %bitcast.6, f32[]{:T(128)} %bitcast.74, f32[448]{0:T(512)S(1)} %copy-done.8, f32[56]{0:T(128)S(1)} %dynamic_slice.18, ...), kind=kLoop, calls=%fused_computation.30 | loop fusion | flops 351232 | bytes 604148 | tf_op jit(solution)/shard_map/convert_element_type | solution.py:71
  130.1 0.7 collective-permute-done.3
  130.9 1.2 broadcast_in_dim.11
  132.0 5.2 %all-to-all-start.2 = ((bf16[8,3,56,448]{3,2,1,0:T(8,128)(2,1)}), bf16[8,3,56,448]{3,2,1,0:T(8,128)(2,1)S(1)}, u32[]{:S(2)}, u32[]{:S(2)}) async-start(bf16[8,3,56,448]{3,2,1,0:T(8,128)(2,1)} %broadcast_in_dim.11), calls=%async_computation.2 | async-start | bytes 2752512 | tf_op jit(solution)/shard_map/all_to_all | solution.py:82
  137.2 2.2 %collective-permute-start.9 = (bf16[448,768]{1,0:T(8,128)(2,1)}, bf16[448,768]{1,0:T(8,128)(2,1)}, u32[]{:S(2)}, u32[]{:S(2)}) collective-permute-start(bf16[448,768]{1,0:T(8,128)(2,1)} %collective-permute-done.4), channel_id=1, source_target_pairs={{0,32},{1,225},{2,34},{3,227},{4,36},{5,229},{6,38},{7,231},{8,40}... | collective-permute-start | bytes 2064392 | tf_op jit(solution)/shard_map/ppermute | solution.py:24
  139.5 3.8 %collective-permute-start.8 = (bf16[56,448]{1,0:T(8,128)(2,1)S(1)}, bf16[56,448]{1,0:T(8,128)(2,1)S(1)}, u32[]{:S(2)}, u32[]{:S(2)}) collective-permute-start(bf16[56,448]{1,0:T(8,128)(2,1)S(1)} %get-tuple-element.21), channel_id=1, source_target_pairs={{0,96},{1,177},{2,98},{3,179},{4,100},{5,181},{6,102},{7,183},{8,1... | collective-permute-start | bytes 150536 | tf_op jit(solution)/shard_map/ppermute | solution.py:24
  143.2 6.1 %collective-permute-done.7 = bf16[56,448]{1,0:T(8,128)(2,1)S(1)} collective-permute-done((bf16[56,448]{1,0:T(8,128)(2,1)S(1)}, bf16[56,448]{1,0:T(8,128)(2,1)S(1)}, u32[]{:S(2)}, u32[]{:S(2)}) %collective-permute-start.7) | collective-permute-done | bytes 50208 | tf_op jit(solution)/shard_map/ppermute | solution.py:24
  149.4 1.2 collective-permute-done.8
  150.7 4.2 %all-to-all-done.2 = bf16[8,3,56,448]{3,2,1,0:T(8,128)(2,1)S(1)} async-done(((bf16[8,3,56,448]{3,2,1,0:T(8,128)(2,1)}), bf16[8,3,56,448]{3,2,1,0:T(8,128)(2,1)S(1)}, u32[]{:S(2)}, u32[]{:S(2)}) %all-to-all-start.2) | async-done | bytes 1204256 | tf_op jit(solution)/shard_map/all_to_all | solution.py:82
  154.8 1.4 broadcast_in_dim.12
  156.3 6.0 %all-to-all-start.4 = ((bf16[8,4,56,448]{3,2,1,0:T(8,128)(2,1)}), bf16[8,4,56,448]{3,2,1,0:T(8,128)(2,1)S(1)}, u32[]{:S(2)}, u32[]{:S(2)}) async-start(bf16[8,4,56,448]{3,2,1,0:T(8,128)(2,1)} %broadcast_in_dim.12), calls=%async_computation.4 | async-start | bytes 3670016 | tf_op jit(solution)/shard_map/all_to_all | solution.py:82
  162.3 2.1 collective-permute-start.10
  164.5 1.7 fusion.29
  166.2 0.5 convolution_add_fusion.5
  166.7 1.7 convolution_add_fusion.4
  168.4 17.2 %all-to-all-done.4 = bf16[8,4,56,448]{3,2,1,0:T(8,128)(2,1)S(1)} async-done(((bf16[8,4,56,448]{3,2,1,0:T(8,128)(2,1)}), bf16[8,4,56,448]{3,2,1,0:T(8,128)(2,1)S(1)}, u32[]{:S(2)}, u32[]{:S(2)}) %all-to-all-start.4) | async-done | bytes 1605664 | tf_op jit(solution)/shard_map/all_to_all | solution.py:82
  185.6 0.8 broadcast_in_dim.13
  186.4 5.2 %all-to-all-start.6 = ((bf16[8,1,56,448]{3,2,1,0:T(8,128)(2,1)}), bf16[8,1,56,448]{3,2,1,0:T(8,128)(2,1)}, u32[]{:S(2)}, u32[]{:S(2)}) async-start(bf16[8,1,56,448]{3,2,1,0:T(8,128)(2,1)} %broadcast_in_dim.13), calls=%async_computation.6 | async-start | bytes 917504 | tf_op jit(solution)/shard_map/all_to_all | solution.py:82
  191.8 1.6 fusion.30
  193.5 1.7 convolution_add_fusion.3
  195.2 0.5 fusion
  195.7 1.7 convolution_add_fusion.1
  197.4 3.0 %all-to-all-done.6 = bf16[8,1,56,448]{3,2,1,0:T(8,128)(2,1)} async-done(((bf16[8,1,56,448]{3,2,1,0:T(8,128)(2,1)}), bf16[8,1,56,448]{3,2,1,0:T(8,128)(2,1)}, u32[]{:S(2)}, u32[]{:S(2)}) %all-to-all-start.6) | async-done | bytes 401440 | tf_op jit(solution)/shard_map/all_to_all | solution.py:82
  200.4 1.8 convolution_add_fusion
  202.2 2.8 %collective-permute-start.12 = (f32[448,384]{1,0:T(8,128)S(1)}, f32[448,384]{1,0:T(8,128)S(1)}, u32[]{:S(2)}, u32[]{:S(2)}) collective-permute-start(f32[448,384]{1,0:T(8,128)S(1)} %slice.64), channel_id=1, source_target_pairs={{0,1},{1,0},{2,3},{3,2},{4,5},{5,4},{6,7},{7,6},{8,9},{9,8},{10,11... | collective-permute-start | bytes 2064392 | tf_op jit(solution)/shard_map/ppermute | solution.py:24
  205.0 1.8 collective-permute-done.12
  206.8 0.9 fusion.1
  (32 shorter events, 0.6 us)
Async XLA Ops:
  0.0 45.0 %copy-start = (bf16[1,448,384]{2,1,0:T(8,128)(2,1)S(1)}, bf16[1,448,384]{2,1,0:T(8,128)(2,1)}, u32[]{:S(2)}) copy-start(bf16[1,448,384]{2,1,0:T(8,128)(2,1)} %param.3) | copy-start | bytes 1032196
  0.0 4.7 %collective-permute-start = (bf16[448,384]{1,0:T(8,128)(2,1)}, bf16[448,384]{1,0:T(8,128)(2,1)S(1)}, u32[]{:S(2)}, u32[]{:S(2)}) collective-permute-start(bf16[448,384]{1,0:T(8,128)(2,1)} %bitcast.76), channel_id=1, source_target_pairs={{0,1},{1,0},{2,3},{3,2},{4,5},{5,4},{6,7},{7,6},{8,9},{9,8},{10,11... | collective-permute-start | bytes 1032200 | tf_op jit(solution)/shard_map/ppermute | solution.py:24
  5.8 12.0 %collective-permute-start.1 = (bf16[448,768]{1,0:T(8,128)(2,1)S(1)}, bf16[448,768]{1,0:T(8,128)(2,1)}, u32[]{:S(2)}, u32[]{:S(2)}) collective-permute-start(bf16[448,768]{1,0:T(8,128)(2,1)S(1)} %pad_maximum_fusion.2), channel_id=1, source_target_pairs={{0,0},{1,17},{2,2},{3,19},{4,4},{5,21},{6,6},{7,23},{8,8},{9,25},{... | collective-permute-start | bytes 2064392 | tf_op jit(solution)/shard_map/ppermute | solution.py:24
  17.7 12.4 %collective-permute-start.2 = (bf16[448,768]{1,0:T(8,128)(2,1)}, bf16[448,768]{1,0:T(8,128)(2,1)S(1)}, u32[]{:S(2)}, u32[]{:S(2)}) collective-permute-start(bf16[448,768]{1,0:T(8,128)(2,1)} %collective-permute-done.1), channel_id=1, source_target_pairs={{0,224},{1,33},{2,226},{3,35},{4,228},{5,37},{6,230},{7,39},{8,232... | collective-permute-start | bytes 2064392 | tf_op jit(solution)/shard_map/ppermute | solution.py:24
  30.1 18.8 %copy-start.6 = (bf16[448,768]{1,0:T(8,128)(2,1)}, bf16[448,768]{1,0:T(8,128)(2,1)S(1)}, u32[]{:S(2)}) copy-start(bf16[448,768]{1,0:T(8,128)(2,1)S(1)} %collective-permute-done.2) | copy-start | bytes 2064388
  30.1 18.2 %collective-permute-start.5 = (bf16[448,768]{1,0:T(8,128)(2,1)S(1)}, bf16[448,768]{1,0:T(8,128)(2,1)}, u32[]{:S(2)}, u32[]{:S(2)}) collective-permute-start(bf16[448,768]{1,0:T(8,128)(2,1)S(1)} %collective-permute-done.2), channel_id=1, source_target_pairs={{0,224},{1,33},{2,226},{3,35},{4,228},{5,37},{6,230},{7,39},{8,232... | collective-permute-start | bytes 2064392 | tf_op jit(solution)/shard_map/ppermute | solution.py:24
  48.3 11.6 %collective-permute-start.6 = (bf16[448,768]{1,0:T(8,128)(2,1)}, bf16[448,768]{1,0:T(8,128)(2,1)S(1)}, u32[]{:S(2)}, u32[]{:S(2)}) collective-permute-start(bf16[448,768]{1,0:T(8,128)(2,1)} %collective-permute-done.5), channel_id=1, source_target_pairs={{0,224},{1,33},{2,226},{3,35},{4,228},{5,37},{6,230},{7,39},{8,232... | collective-permute-start | bytes 2064392 | tf_op jit(solution)/shard_map/ppermute | solution.py:24
  52.5 23.2 %all-to-all-start.1 = ((f32[8,2,56,448]{3,2,1,0:T(8,128)}), f32[8,2,56,448]{3,2,1,0:T(8,128)S(1)}, u32[]{:S(2)}, u32[]{:S(2)}) async-start(f32[8,2,56,448]{3,2,1,0:T(8,128)} %pad_maximum_fusion), calls=%async_computation.1 | async-start | bytes 3670016 | tf_op jit(solution)/shard_map/all_to_all | solution.py:64
  59.9 4.5 %copy-start.2 = (bf16[448,768]{1,0:T(8,128)(2,1)}, bf16[448,768]{1,0:T(8,128)(2,1)S(1)}, u32[]{:S(2)}) copy-start(bf16[448,768]{1,0:T(8,128)(2,1)S(1)} %collective-permute-done.6) | copy-start | bytes 2064388
  59.9 11.0 %collective-permute-start.11 = (bf16[448,768]{1,0:T(8,128)(2,1)S(1)}, bf16[448,768]{1,0:T(8,128)(2,1)S(1)}, u32[]{:S(2)}, u32[]{:S(2)}) collective-permute-start(bf16[448,768]{1,0:T(8,128)(2,1)S(1)} %collective-permute-done.6), channel_id=1, source_target_pairs={{0,224},{1,33},{2,226},{3,35},{4,228},{5,37},{6,230},{7,39},{8,232... | collective-permute-start | bytes 2064392 | tf_op jit(solution)/shard_map/ppermute | solution.py:24
  70.9 0.9 copy-start.5
  75.7 18.6 %all-to-all-start.5 = ((f32[8,1,56,448]{3,2,1,0:T(8,128)}), f32[8,1,56,448]{3,2,1,0:T(8,128)S(1)}, u32[]{:S(2)}, u32[]{:S(2)}) async-start(f32[8,1,56,448]{3,2,1,0:T(8,128)} %bitcast.92), calls=%async_computation.5 | async-start | bytes 1835008 | tf_op jit(solution)/shard_map/all_to_all | solution.py:64
  80.2 1.7 copy-start.3
  81.9 1.2 copy-start.1
  84.6 14.5 %copy-start.8 = (f32[448]{0:T(512)S(1)}, f32[448]{0:T(512)}, u32[]{:S(2)}) copy-start(f32[448]{0:T(512)} %param.5) | copy-start | bytes 5380
  94.4 28.2 %all-to-all-start.3 = ((f32[8,2,56,448]{3,2,1,0:T(8,128)}), f32[8,2,56,448]{3,2,1,0:T(8,128)}, u32[]{:S(2)}, u32[]{:S(2)}) async-start(f32[8,2,56,448]{3,2,1,0:T(8,128)} %pad_maximum_fusion.1), calls=%async_computation.3 | async-start | bytes 3670016 | tf_op jit(solution)/shard_map/all_to_all | solution.py:64
  99.1 38.1 %collective-permute-start.4 = (bf16[448,768]{1,0:T(8,128)(2,1)}, bf16[448,768]{1,0:T(8,128)(2,1)}, u32[]{:S(2)}, u32[]{:S(2)}) collective-permute-start(bf16[448,768]{1,0:T(8,128)(2,1)} %collective-permute-done.1), channel_id=1, source_target_pairs={{0,32},{1,225},{2,34},{3,227},{4,36},{5,229},{6,38},{7,231},{8,40}... | collective-permute-start | bytes 2064392 | tf_op jit(solution)/shard_map/ppermute | solution.py:24
  126.8 4.0 %collective-permute-start.3 = (bf16[56,448]{1,0:T(8,128)(2,1)S(1)}, bf16[56,448]{1,0:T(8,128)(2,1)S(1)}, u32[]{:S(2)}, u32[]{:S(2)}) collective-permute-start(bf16[56,448]{1,0:T(8,128)(2,1)S(1)} %get-tuple-element.25), channel_id=1, source_target_pairs={{0,32},{1,241},{2,34},{3,243},{4,36},{5,245},{6,38},{7,247},{8,40}... | collective-permute-start | bytes 150536 | tf_op jit(solution)/shard_map/ppermute | solution.py:24
  132.0 22.8 %all-to-all-start.2 = ((bf16[8,3,56,448]{3,2,1,0:T(8,128)(2,1)}), bf16[8,3,56,448]{3,2,1,0:T(8,128)(2,1)S(1)}, u32[]{:S(2)}, u32[]{:S(2)}) async-start(bf16[8,3,56,448]{3,2,1,0:T(8,128)(2,1)} %broadcast_in_dim.11), calls=%async_computation.2 | async-start | bytes 2752512 | tf_op jit(solution)/shard_map/all_to_all | solution.py:82
  137.2 25.1 %collective-permute-start.9 = (bf16[448,768]{1,0:T(8,128)(2,1)}, bf16[448,768]{1,0:T(8,128)(2,1)}, u32[]{:S(2)}, u32[]{:S(2)}) collective-permute-start(bf16[448,768]{1,0:T(8,128)(2,1)} %collective-permute-done.4), channel_id=1, source_target_pairs={{0,32},{1,225},{2,34},{3,227},{4,36},{5,229},{6,38},{7,231},{8,40}... | collective-permute-start | bytes 2064392 | tf_op jit(solution)/shard_map/ppermute | solution.py:24
  139.4 9.9 %collective-permute-start.7 = (bf16[56,448]{1,0:T(8,128)(2,1)S(1)}, bf16[56,448]{1,0:T(8,128)(2,1)S(1)}, u32[]{:S(2)}, u32[]{:S(2)}) collective-permute-start(bf16[56,448]{1,0:T(8,128)(2,1)S(1)} %get-tuple-element.20), channel_id=1, source_target_pairs={{0,64},{1,209},{2,66},{3,211},{4,68},{5,213},{6,70},{7,215},{8,72}... | collective-permute-start | bytes 150536 | tf_op jit(solution)/shard_map/ppermute | solution.py:24
  139.5 11.2 %collective-permute-start.8 = (bf16[56,448]{1,0:T(8,128)(2,1)S(1)}, bf16[56,448]{1,0:T(8,128)(2,1)S(1)}, u32[]{:S(2)}, u32[]{:S(2)}) collective-permute-start(bf16[56,448]{1,0:T(8,128)(2,1)S(1)} %get-tuple-element.21), channel_id=1, source_target_pairs={{0,96},{1,177},{2,98},{3,179},{4,100},{5,181},{6,102},{7,183},{8,1... | collective-permute-start | bytes 150536 | tf_op jit(solution)/shard_map/ppermute | solution.py:24
  156.3 29.3 %all-to-all-start.4 = ((bf16[8,4,56,448]{3,2,1,0:T(8,128)(2,1)}), bf16[8,4,56,448]{3,2,1,0:T(8,128)(2,1)S(1)}, u32[]{:S(2)}, u32[]{:S(2)}) async-start(bf16[8,4,56,448]{3,2,1,0:T(8,128)(2,1)} %broadcast_in_dim.12), calls=%async_computation.4 | async-start | bytes 3670016 | tf_op jit(solution)/shard_map/all_to_all | solution.py:82
  162.3 33.4 %collective-permute-start.10 = (bf16[448,768]{1,0:T(8,128)(2,1)}, bf16[448,768]{1,0:T(8,128)(2,1)}, u32[]{:S(2)}, u32[]{:S(2)}) collective-permute-start(bf16[448,768]{1,0:T(8,128)(2,1)} %collective-permute-done.9), channel_id=1, source_target_pairs={{0,32},{1,225},{2,34},{3,227},{4,36},{5,229},{6,38},{7,231},{8,40}... | collective-permute-start | bytes 2064392 | tf_op jit(solution)/shard_map/ppermute | solution.py:24
  164.5 1.7 copy-start.7
  186.4 14.0 %all-to-all-start.6 = ((bf16[8,1,56,448]{3,2,1,0:T(8,128)(2,1)}), bf16[8,1,56,448]{3,2,1,0:T(8,128)(2,1)}, u32[]{:S(2)}, u32[]{:S(2)}) async-start(bf16[8,1,56,448]{3,2,1,0:T(8,128)(2,1)} %broadcast_in_dim.13), calls=%async_computation.6 | async-start | bytes 917504 | tf_op jit(solution)/shard_map/all_to_all | solution.py:82
  193.5 1.7 copy-start.4
  202.2 4.6 %collective-permute-start.12 = (f32[448,384]{1,0:T(8,128)S(1)}, f32[448,384]{1,0:T(8,128)S(1)}, u32[]{:S(2)}, u32[]{:S(2)}) collective-permute-start(f32[448,384]{1,0:T(8,128)S(1)} %slice.64), channel_id=1, source_target_pairs={{0,1},{1,0},{2,3},{3,2},{4,5},{5,4},{6,7},{7,6},{8,9},{9,8},{10,11... | collective-permute-start | bytes 2064392 | tf_op jit(solution)/shard_map/ppermute | solution.py:24

commit v3 on v1

v3 whole, which is shorter than its diff:
```python
import jax
import jax.numpy as jnp
from jax import lax
from jax.sharding import Mesh, PartitionSpec as P

NZ, NXL, NXH, NY, NC = 8, 2, 2, 4, 2
ALL = ("z", "xl", "xh", "y", "c")


def flat(z, xl, xh, y, c):
    return (((z % NZ * NXL + xl % NXL) * NXH + xh % NXH) * NY + y % NY) * NC + c % NC


def moved(array, where):
    pairs = [
        (flat(z, xl, xh, y, c), flat(*where(z, xl, xh, y, c)))
        for z in range(NZ)
        for xl in range(NXL)
        for xh in range(NXH)
        for y in range(NY)
        for c in range(NC)
    ]
    return lax.ppermute(array, ALL, pairs)


def across(array):
    return moved(array, lambda z, xl, xh, y, c: (z, xl, 1 - xh, y, c))


def dot_nt(a, b):
    return lax.dot_general(a, b, (((1,), (1,)), ((), ())), preferred_element_type=jnp.float32)


def dot_tn(a, b):
    return lax.dot_general(a, b, (((0,), (0,)), ((), ())), preferred_element_type=jnp.float32)


def half_of(array, which, dim):
    return lax.dynamic_index_in_dim(array, which, dim, keepdims=False)


def local(three_index, occ_energy, vir_energy):
    own = three_index[0]
    nvir, depth = own.shape
    share = nvir // (NXH * NY)
    z, xl, c = lax.axis_index("z"), lax.axis_index("xl"), lax.axis_index("c")
    xh, y = lax.axis_index("xh"), lax.axis_index("y")

    other = moved(own, lambda z, xl, xh, y, c: (z, xl, xh, y, 1 - c))
    mine = jnp.concatenate([own, other], axis=1)

    ahead = [moved(mine, lambda z, xl, xh, y, c: (z, xl if c == 0 else 1 - xl, xh, y, c))]
    ahead.append(moved(mine, lambda z, xl, xh, y, c: (z - 1, xl if c == 0 else 1 - xl, xh, y, c)))
    behind = [mine, moved(mine, lambda z, xl, xh, y, c: (z + 1, xl, xh, y, c))]
    copies = jnp.broadcast_to(occ_energy, (NZ * NXL, 1))
    energies = lax.all_to_all(copies, ("z", "xl"), 0, 0, tiled=True)[:, 0]
    ahead.append(moved(ahead[1], lambda z, xl, xh, y, c: (z - 1, xl, xh, y, c)))
    behind.append(moved(behind[1], lambda z, xl, xh, y, c: (z + 1, xl, xh, y, c)))
    ahead[2], behind[2], energies = lax.optimization_barrier((ahead[2], behind[2], energies))

    def numer(i, j):
        a, b = behind[i], ahead[j]
        return dot_nt(a * jnp.bfloat16(2), b) - dot_nt(b, a)

    early = jnp.stack([numer(0, 0), numer(0, 1)]).reshape(2, NXH, NY, share, nvir)
    got = across(half_of(early, 1 - xh, 1))
    early = half_of(early, xh, 1) + got
    early = early.transpose(1, 0, 2, 3).reshape(NY, 2 * share, nvir)
    late = jnp.stack([numer(0, 2), numer(1, 2), numer(2, 2)]).reshape(3, NXH, NY, share, nvir)
    late = late.transpose(2, 0, 1, 3, 4).reshape(NY, 3 * NXH * share, nvir)
    parts = jnp.concatenate([early, late], axis=1)
    sums = jnp.sum(lax.all_to_all(parts, "y", 0, 0, tiled=True), axis=0)
    early = sums[: 2 * share].reshape(2, share, nvir)
    late = sums[2 * share :].reshape(3, NXH, share, nvir)
    late = half_of(late, xh, 1) + across(half_of(late, 1 - xh, 1))

    for _ in range(2):
        ahead.append(moved(ahead[-1], lambda z, xl, xh, y, c: (z - 1, xl, xh, y, c)))
    turned = [ahead[0]]
    for _ in range(3):
        turned.append(moved(turned[-1], lambda z, xl, xh, y, c: (z + 1, xl, xh, y, c)))

    vir_rows = lax.dynamic_slice_in_dim(vir_energy, (xh * NY + y) * share, share)
    virs = vir_rows[:, None] + vir_energy[None, :]
    xc = jnp.where(c == 0, xl, 1 - xl)

    def amps(value, i, j):
        eps_i = lax.dynamic_slice_in_dim(energies, (z - i + NZ) % NZ * NXL + xl, 1)
        eps_j = lax.dynamic_slice_in_dim(energies, (z + j) % NZ * NXL + xc, 1)
        return (value / (virs - eps_i[0] - eps_j[0])).astype(jnp.bfloat16)

    p0, p1 = amps(early[0], 0, 0), amps(early[1], 0, 1)
    p2, p3, p4 = amps(late[0], 0, 2), amps(late[1], 1, 2), amps(late[2], 2, 2)

    t1 = moved(p1, lambda z, xl, xh, y, c: (z + 1, xl if c == 0 else 1 - xl, xh, y, c))
    t23 = moved(jnp.stack([p2, p3]), lambda z, xl, xh, y, c: (z + 2, xl if c == 0 else 1 - xl, xh, y, c))
    d3 = moved(p3, lambda z, xl, xh, y, c: (z - 1, xl, xh, y, c))
    d4 = moved(p4, lambda z, xl, xh, y, c: (z - 2, xl, xh, y, c))

    rows = jnp.stack([p0, p1, p2])
    rows = lax.all_to_all(jnp.broadcast_to(rows, (NY, *rows.shape)), "y", 0, 0, tiled=True)
    rows_other = across(rows)
    more = jnp.stack([d3, d4, t1, t23[0], t23[1]])
    more_other = across(more)

    def in_order(here, there):
        return jnp.where(xh == 0, jnp.stack([here, there]), jnp.stack([there, here]))

    rows = in_order(rows, rows_other).transpose(2, 0, 1, 3, 4).reshape(3, nvir, nvir)
    more = in_order(more, more_other)
    more = lax.all_to_all(jnp.broadcast_to(more, (NY, *more.shape)), "y", 0, 0, tiled=True)
    more = more.transpose(2, 1, 0, 3, 4).reshape(5, nvir, nvir)

    total = jnp.dot(rows[0], ahead[0], preferred_element_type=jnp.float32)
    for n, block in enumerate((ahead[1], ahead[2])):
        total = total + jnp.dot(rows[n + 1], block, preferred_element_type=jnp.float32)
    for n, block in enumerate((ahead[3], ahead[4])):
        total = total + jnp.dot(more[n], block, preferred_element_type=jnp.float32)
    for n in range(3):
        total = total + dot_tn(more[2 + n], turned[n + 1])
    back = moved(total[:, depth:], lambda z, xl, xh, y, c: (z, xl, xh, y, 1 - c))
    return (total[:, :depth] + back)[None]


def solution(mesh):
    grid = Mesh(mesh.devices.reshape(NZ, NXL, NXH, NY, NC), ALL)
    return jax.shard_map(
        local,
        mesh=grid,
        in_specs=(P(("z", "xl"), None, ("xh", "y", "c")), P(("z", "xl")), P()),
        out_specs=P(("z", "xl"), None, ("xh", "y", "c")),
        check_vma=False,
    )
```

time: 219 us -> 193 us (0.88)
  waiting for transfers between devices: 80.8 us -> 52.1 us
  blocking collectives: 65.4 us -> 44.9 us
  starting transfers between devices: 37.2 us -> 55.5 us
  other arithmetic: 10.4 us -> 16 us
  local copies, waits for them, and re-layouts: 11.2 us -> 5.82 us
  matrix products: 11.9 us -> 16.4 us
    unnamed x1 -> x0, blocking collectives: 65.4 us -> none
    all_to_all x0 -> x1, blocking collectives: none -> 44.9 us  [local(): sums = jnp.sum(lax.all_to_all(parts, 'y', 0, 0, tiled=True), axis=0)]
    ppermute x13 -> x20, waiting for transfers between devices: 69.8 us -> 35.6 us  [moved(): return lax.ppermute(array, ALL, pairs)]
    ppermute x13 -> x20, starting transfers between devices: 24 us -> 42.1 us  [moved(): return lax.ppermute(array, ALL, pairs)]
    all_to_all x2 -> x3, waiting for transfers between devices: 11.1 us -> 16.5 us  [the longest x1 13.1 us: local(): energies = lax.all_to_all(copies, ('z', 'xl'), 0, 0, tiled=True)[:, 0]]
    unnamed x25 -> x14, local copies, waits for them, and re-layouts: 5.96 us -> 1.01 us
    convert_element_type x1 -> x2, other arithmetic: 1.99 us -> 6.05 us  [amps(): return (value / (virs - eps_i[0] - eps_j[0])).astype(jnp.bfloat16)]
    unnamed x5 -> x0, other arithmetic: 3.58 us -> none
  transfers between devices with their start and end apart: 15 -> 23, of which waited for: 11 -> 13; matrix products, arithmetic and copies ran while one was open for 8% -> 15% of each run, Pallas kernels for 0% -> 0%
where the time goes in v3:
time: 193 us; the launch traced here: 192 us
  starting transfers between devices  55.5 us (29%)
  waiting for transfers between devices  52.1 us (27%)
  blocking collectives  44.9 us (23%)
  matrix products  16.4 us (8%)
  other arithmetic  16 us (8%)
  local copies, waits for them, and re-layouts  5.82 us (3%)
    all_to_all x1, blocking collectives, local(): sums = jnp.sum(lax.all_to_all(parts, 'y', 0, 0, tiled=True), axis=0)  44.9 us
    ppermute x20, starting transfers between devices, moved(): return lax.ppermute(array, ALL, pairs)  42.1 us
    ppermute x20, waiting for transfers between devices, moved(): return lax.ppermute(array, ALL, pairs)  35.6 us
    all_to_all x1, waiting for transfers between devices, local(): energies = lax.all_to_all(copies, ('z', 'xl'), 0, 0, tiled=True)[:, 0]  13.1 us
    convert_element_type x2, other arithmetic, amps(): return (value / (virs - eps_i[0] - eps_j[0])).astype(jnp.bfloat16)  6.05 us
    dot_general x10, matrix products, dot_nt(): lax.dot_general(a, b, (((1,), (1,)), ((), ())), preferred_element_type=jn...  5.42 us
    all_to_all x1, starting transfers between devices, local(): energies = lax.all_to_all(copies, ('z', 'xl'), 0, 0, tiled=True)[:, 0]  5.1 us
    dot_general x3, matrix products, dot_tn(): lax.dot_general(a, b, (((0,), (0,)), ((), ())), preferred_element_type=jn...  4.95 us
  transfers between devices with their start and end apart: 23, of which 13 were waited for; matrix products, arithmetic and copies ran while one was open for 15% of the time, Pallas kernels for 0%

profile of v3, /device:TPU:1, one launch (start us, length us, event | category | flops | bytes accessed | tf_op | source)
XLA Modules:
  0.0 191.7 jit_solution(17295796216694547110)
XLA Ops:
  0.0 3.2 %collective-permute-start = (bf16[448,384]{1,0:T(8,128)(2,1)}, bf16[448,384]{1,0:T(8,128)(2,1)S(1)}, u32[]{:S(2)}, u32[]{:S(2)}) collective-permute-start(bf16[448,384]{1,0:T(8,128)(2,1)} %bitcast.96), channel_id=1, source_target_pairs={{0,1},{1,0},{2,3},{3,2},{4,5},{5,4},{6,7},{7,6},{8,9},{9,8},{10,11... | collective-permute-start | bytes 1032200 | tf_op jit(solution)/shard_map/ppermute | solution.py:23
  3.2 1.5 collective-permute-done
  4.7 1.9 pad_maximum_fusion.2
  6.6 4.8 %collective-permute-start.2 = (bf16[448,768]{1,0:T(8,128)(2,1)}, bf16[448,768]{1,0:T(8,128)(2,1)S(1)}, u32[]{:S(2)}, u32[]{:S(2)}) collective-permute-start(bf16[448,768]{1,0:T(8,128)(2,1)} %pad_maximum_fusion.2), channel_id=1, source_target_pairs={{0,224},{1,241},{2,226},{3,243},{4,228},{5,245},{6,230},{7,247},{8... | collective-permute-start | bytes 2064392 | tf_op jit(solution)/shard_map/ppermute | solution.py:23
  11.4 2.2 %collective-permute-start.1 = (bf16[448,768]{1,0:T(8,128)(2,1)}, bf16[448,768]{1,0:T(8,128)(2,1)S(1)}, u32[]{:S(2)}, u32[]{:S(2)}) collective-permute-start(bf16[448,768]{1,0:T(8,128)(2,1)} %pad_maximum_fusion.2), channel_id=1, source_target_pairs={{0,0},{1,17},{2,2},{3,19},{4,4},{5,21},{6,6},{7,23},{8,8},{9,25},{... | collective-permute-start | bytes 2064392 | tf_op jit(solution)/shard_map/ppermute | solution.py:23
  14.3 0.6 broadcast_in_dim.14
  14.9 5.1 %all-to-all-start = ((f32[16,1,1]{2,1,0:T(1,128)}), f32[16,1,1]{2,1,0:T(1,128)S(1)}, u32[]{:S(2)}, u32[]{:S(2)}) async-start(f32[16,1,1]{2,1,0:T(1,128)} %broadcast_in_dim.14), calls=%async_computation | async-start | bytes 16384 | tf_op jit(solution)/shard_map/all_to_all | solution.py:56
  20.0 13.1 %all-to-all-done = f32[16,1,1]{2,1,0:T(1,128)S(1)} async-done(((f32[16,1,1]{2,1,0:T(1,128)}), f32[16,1,1]{2,1,0:T(1,128)S(1)}, u32[]{:S(2)}, u32[]{:S(2)}) %all-to-all-start) | async-done | bytes 96 | tf_op jit(solution)/shard_map/all_to_all | solution.py:56
  33.3 0.4 collective-permute-start.4
  33.6 0.5 fusion.43
  34.2 0.6 convolution_subtract_fusion.4
  34.7 1.3 collective-permute-start.6
  36.0 0.5 fusion.42
  36.5 0.5 convolution_subtract_fusion.3
  37.4 2.5 %collective-permute-start.3 = (f32[2,4,56,448]{3,2,0,1:T(8,128)S(1)}, f32[2,4,56,448]{3,2,0,1:T(8,128)S(1)}, u32[]{:S(2)}, u32[]{:S(2)}) collective-permute-start(f32[2,4,56,448]{3,2,0,1:T(8,128)S(1)} %bitcast.120), channel_id=1, source_target_pairs={{0,8},{1,9},{2,10},{3,11},{4,12},{5,13},{6,14},{7,15},{8,0},{9,1},... | collective-permute-start | bytes 2408456 | tf_op jit(solution)/shard_map/ppermute | solution.py:23
  39.9 10.0 %collective-permute-done.4 = bf16[448,768]{1,0:T(8,128)(2,1)S(1)} collective-permute-done((bf16[448,768]{1,0:T(8,128)(2,1)S(1)}, bf16[448,768]{1,0:T(8,128)(2,1)S(1)}, u32[]{:S(2)}, u32[]{:S(2)}) %collective-permute-start.4) | collective-permute-done | bytes 688160 | tf_op jit(solution)/shard_map/ppermute | solution.py:23
  50.0 2.4 %collective-permute-done.6 = bf16[448,768]{1,0:T(8,128)(2,1)S(1)} collective-permute-done((bf16[448,768]{1,0:T(8,128)(2,1)S(1)}, bf16[448,768]{1,0:T(8,128)(2,1)S(1)}, u32[]{:S(2)}, u32[]{:S(2)}) %collective-permute-start.6) | collective-permute-done | bytes 688160 | tf_op jit(solution)/shard_map/ppermute | solution.py:23
  52.3 0.5 fusion.48
  52.9 0.5 fusion.41
  53.4 0.5 convolution_subtract_fusion.2
  54.0 0.5 fusion.47
  54.5 0.5 convolution_subtract_fusion
  55.1 0.5 convolution_subtract_fusion.1
  56.3 3.6 %collective-permute-done.3 = f32[2,4,56,448]{3,2,0,1:T(8,128)S(1)} collective-permute-done((f32[2,4,56,448]{3,2,0,1:T(8,128)S(1)}, f32[2,4,56,448]{3,2,0,1:T(8,128)S(1)}, u32[]{:S(2)}, u32[]{:S(2)}) %collective-permute-start.3) | collective-permute-done | bytes 802848 | tf_op jit(solution)/shard_map/ppermute | solution.py:23
  60.1 0.4 pad_maximum_fusion
  60.5 44.9 %all_to_all.21 = f32[4,448,448]{2,1,0:T(8,128)} all-to-all(f32[4,448,448]{2,1,0:T(8,128)S(1)} %pad_maximum_fusion), channel_id=1, replica_groups=mesh['z'=8,'xl'=2,'xh'=2,'y'=4,'c'=2] {'y'}, dimensions={0} | all-to-all | bytes 6422528 | tf_op jit(solution)/shard_map/all_to_all | solution.py:72
  105.3 2.6 %reduce_sum.9 = f32[448,448]{1,0:T(8,128)S(1)} reduce(f32[4,448,448]{2,1,0:T(8,128)} %all_to_all.21, f32[]{:T(128)} %constant.86.clone.1), dimensions={0}, to_apply=%region_0.1 | reduce | flops 602112 | bytes 4014084 | tf_op jit(solution)/shard_map/reduce_sum | solution.py:72
  108.0 2.5 %collective-permute-start.7 = (f32[3,56,448]{2,1,0:T(8,128)S(1)}, f32[3,56,448]{2,1,0:T(8,128)}, u32[]{:S(2)}, u32[]{:S(2)}) collective-permute-start(f32[3,56,448]{2,1,0:T(8,128)S(1)} %dynamic-slice_bitcast_fusion), channel_id=1, source_target_pairs={{0,8},{1,9},{2,10},{3,11},{4,12},{5,13},{6,14},{7,15},{8,0},{9,1},... | collective-permute-start | bytes 903176 | tf_op jit(solution)/shard_map/ppermute | solution.py:23
  110.7 1.3 collective-permute-start.16
  112.0 0.7 fusion.46
  112.7 3.2 %collective-permute-done.7 = f32[3,56,448]{2,1,0:T(8,128)} collective-permute-done((f32[3,56,448]{2,1,0:T(8,128)S(1)}, f32[3,56,448]{2,1,0:T(8,128)}, u32[]{:S(2)}, u32[]{:S(2)}) %collective-permute-start.7) | collective-permute-done | bytes 301088 | tf_op jit(solution)/shard_map/ppermute | solution.py:23
  115.8 1.0 bitcast_add_fusion.1
  116.8 2.1 %fusion.31 = (bf16[1,56,448]{2,1,0:T(8,128)(2,1)S(1)}, bf16[1,56,448]{2,1,0:T(8,128)(2,1)S(1)}) fusion(f32[3,56,448]{2,1,0:T(8,128)S(1)} %bitcast_add_fusion.1, f32[]{:T(128)} %bitcast.21, f32[]{:T(128)} %bitcast.13, f32[448]{0:T(512)S(1)} %copy-done.6, f32[56]{0:T(128)S(1)} %dynamic_slice.41, f32[]{:T(128)} %bitcast.29), kind=kLoop, calls=%fused_computation.65 | loop fusion | flops 225792 | bytes 303084 | tf_op jit(solution)/shard_map/convert_element_type | solution.py:90
  119.0 2.1 %collective-permute-start.12 = (bf16[2,56,448]{2,1,0:T(8,128)(2,1)S(1)}, bf16[2,56,448]{2,1,0:T(8,128)(2,1)S(1)}, u32[]{:S(2)}, u32[]{:S(2)}) collective-permute-start(bf16[2,56,448]{2,1,0:T(8,128)(2,1)S(1)} %pad_maximum_fusion.5), channel_id=1, source_target_pairs={{0,64},{1,81},{2,66},{3,83},{4,68},{5,85},{6,70},{7,87},{8,72},{9,... | collective-permute-start | bytes 301064 | tf_op jit(solution)/shard_map/ppermute | solution.py:23
  121.1 4.0 %fusion.34 = (bf16[1,56,448]{2,1,0:T(8,128)(2,1)S(1)}, bf16[56,448]{1,0:T(8,128)(2,1)S(1)}, bf16[56,448]{1,0:T(8,128)(2,1)S(1)}, bf16[56,448]{1,0:T(8,128)(2,1)S(1)}) fusion(f32[]{:T(128)} %bitcast.14, f32[]{:T(128)} %bitcast.13, f32[448]{0:T(512)S(1)} %copy-done.6, f32[56]{0:T(128)S(1)} %dynamic_slice.41, f32[448,448]{1,0:T(8,128)S(1)} %reduce_sum.9, ...), kind=kLoop, calls=%fused_computation.68 | loop fusion | flops 401408 | bytes 604152 | tf_op jit(solution)/shard_map/convert_element_type | solution.py:90
  125.1 0.9 broadcast_in_dim.15
  126.0 4.2 %all-to-all-start.2 = ((bf16[4,3,56,448]{3,2,1,0:T(8,128)(2,1)}), bf16[4,3,56,448]{3,2,1,0:T(8,128)(2,1)}, u32[]{:S(2)}, u32[]{:S(2)}) async-start(bf16[4,3,56,448]{3,2,1,0:T(8,128)(2,1)} %broadcast_in_dim.15), calls=%async_computation.2 | async-start | bytes 1376256 | tf_op jit(solution)/shard_map/all_to_all | solution.py:101
  130.2 1.6 collective-permute-start.9
  132.1 2.1 %collective-permute-start.11 = (bf16[56,448]{1,0:T(8,128)(2,1)S(1)}, bf16[56,448]{1,0:T(8,128)(2,1)S(1)}, u32[]{:S(2)}, u32[]{:S(2)}) collective-permute-start(bf16[56,448]{1,0:T(8,128)(2,1)S(1)} %get-tuple-element.22), channel_id=1, source_target_pairs={{0,32},{1,49},{2,34},{3,51},{4,36},{5,53},{6,38},{7,55},{8,40},{9,... | collective-permute-start | bytes 150536 | tf_op jit(solution)/shard_map/ppermute | solution.py:23
  134.2 2.1 %collective-permute-done.10 = bf16[56,448]{1,0:T(8,128)(2,1)S(1)} collective-permute-done((bf16[56,448]{1,0:T(8,128)(2,1)S(1)}, bf16[56,448]{1,0:T(8,128)(2,1)S(1)}, u32[]{:S(2)}, u32[]{:S(2)}) %collective-permute-start.10) | collective-permute-done | bytes 50208 | tf_op jit(solution)/shard_map/ppermute | solution.py:23
  136.3 0.9 collective-permute-done.11
  137.3 2.9 %collective-permute-start.13 = (bf16[5,56,448]{2,1,0:T(8,128)(2,1)S(1)}, bf16[5,56,448]{2,1,0:T(8,128)(2,1)S(1)}, u32[]{:S(2)}, u32[]{:S(2)}) collective-permute-start(bf16[5,56,448]{2,1,0:T(8,128)(2,1)S(1)} %get-tuple-element.28), channel_id=1, source_target_pairs={{0,8},{1,9},{2,10},{3,11},{4,12},{5,13},{6,14},{7,15},{8,0},{9,1},... | collective-permute-start | bytes 752648 | tf_op jit(solution)/shard_map/ppermute | solution.py:23
  140.1 1.5 collective-permute-start.17
  141.8 2.5 %collective-permute-done.13 = bf16[5,56,448]{2,1,0:T(8,128)(2,1)S(1)} collective-permute-done((bf16[5,56,448]{2,1,0:T(8,128)(2,1)S(1)}, bf16[5,56,448]{2,1,0:T(8,128)(2,1)S(1)}, u32[]{:S(2)}, u32[]{:S(2)}) %collective-permute-start.13) | collective-permute-done | bytes 250912 | tf_op jit(solution)/shard_map/ppermute | solution.py:23
  144.4 1.7 broadcast_in_dim.16
  146.1 4.1 %all-to-all-start.3 = ((bf16[4,2,5,56,448]{4,3,1,2,0:T(8,128)(2,1)}), bf16[4,2,5,56,448]{4,3,1,2,0:T(8,128)(2,1)S(1)}, u32[]{:S(2)}, u32[]{:S(2)}) async-start(bf16[4,2,5,56,448]{4,3,1,2,0:T(8,128)(2,1)} %broadcast_in_dim.16), calls=%async_computation.3 | async-start | bytes 4587520 | tf_op jit(solution)/shard_map/all_to_all | solution.py:111
  150.2 1.0 collective-permute-done.14
  151.2 0.8 collective-permute-start.15
  152.1 0.6 collective-permute-start.18
  152.7 6.5 %collective-permute-done.8 = bf16[4,3,56,448]{3,2,1,0:T(8,128)(2,1)} collective-permute-done((bf16[4,3,56,448]{3,2,1,0:T(8,128)(2,1)}, bf16[4,3,56,448]{3,2,1,0:T(8,128)(2,1)}, u32[]{:S(2)}, u32[]{:S(2)}) %collective-permute-start.8) | collective-permute-done | bytes 602144 | tf_op jit(solution)/shard_map/ppermute | solution.py:23
  159.2 2.1 %fusion.2 = bf16[3,2,4,56,448]{4,3,0,2,1:T(8,128)(2,1)S(1)} fusion(bf16[1,4,3,56,448]{4,3,2,1,0:T(8,128)(2,1)} %bitcast.23, bf16[1,4,3,56,448]{4,3,2,1,0:T(8,128)(2,1)} %bitcast.22, pred[]{:T(512)S(6)} %eq.18), kind=kLoop, calls=%fused_computation.15 | loop fusion | flops 1806336 | bytes 2408449 | tf_op jit(solution)/shard_map/transpose | solution.py:109
  161.4 1.0 copy-done.3
  162.4 0.5 fusion.49
  162.9 1.6 convolution_add_fusion.4
  164.5 3.4 %all-to-all-done.3 = bf16[4,2,5,56,448]{4,3,1,2,0:T(8,128)(2,1)S(1)} async-done(((bf16[4,2,5,56,448]{4,3,1,2,0:T(8,128)(2,1)}), bf16[4,2,5,56,448]{4,3,1,2,0:T(8,128)(2,1)S(1)}, u32[]{:S(2)}, u32[]{:S(2)}) %all-to-all-start.3) | async-done | bytes 2007072 | tf_op jit(solution)/shard_map/all_to_all | solution.py:111
  168.4 1.7 fusion.50
  170.1 0.5 fusion.1
  170.6 1.6 fusion.51
  172.3 1.6 fusion
  173.9 1.7 convolution_add_fusion.1
  175.6 1.6 convolution_add_fusion
  177.3 11.7 %collective-permute-start.19 = (f32[448,384]{1,0:T(8,128)S(1)}, f32[448,384]{1,0:T(8,128)S(1)}, u32[]{:S(2)}, u32[]{:S(2)}) collective-permute-start(f32[448,384]{1,0:T(8,128)S(1)} %slice.95), channel_id=1, source_target_pairs={{0,1},{1,0},{2,3},{3,2},{4,5},{5,4},{6,7},{7,6},{8,9},{9,8},{10,11... | collective-permute-start | bytes 2064392 | tf_op jit(solution)/shard_map/ppermute | solution.py:23
  189.0 1.8 collective-permute-done.19
  190.8 0.9 fusion.5
  (44 shorter events, 2.8 us)
Async XLA Ops:
  0.0 33.6 %copy-start = (bf16[1,448,384]{2,1,0:T(8,128)(2,1)S(1)}, bf16[1,448,384]{2,1,0:T(8,128)(2,1)}, u32[]{:S(2)}) copy-start(bf16[1,448,384]{2,1,0:T(8,128)(2,1)} %param.3) | copy-start | bytes 1032196
  0.0 4.7 %collective-permute-start = (bf16[448,384]{1,0:T(8,128)(2,1)}, bf16[448,384]{1,0:T(8,128)(2,1)S(1)}, u32[]{:S(2)}, u32[]{:S(2)}) collective-permute-start(bf16[448,384]{1,0:T(8,128)(2,1)} %bitcast.96), channel_id=1, source_target_pairs={{0,1},{1,0},{2,3},{3,2},{4,5},{5,4},{6,7},{7,6},{8,9},{9,8},{10,11... | collective-permute-start | bytes 1032200 | tf_op jit(solution)/shard_map/ppermute | solution.py:23
  6.6 26.6 %collective-permute-start.2 = (bf16[448,768]{1,0:T(8,128)(2,1)}, bf16[448,768]{1,0:T(8,128)(2,1)S(1)}, u32[]{:S(2)}, u32[]{:S(2)}) collective-permute-start(bf16[448,768]{1,0:T(8,128)(2,1)} %pad_maximum_fusion.2), channel_id=1, source_target_pairs={{0,224},{1,241},{2,226},{3,243},{4,228},{5,245},{6,230},{7,247},{8... | collective-permute-start | bytes 2064392 | tf_op jit(solution)/shard_map/ppermute | solution.py:23
  11.4 22.2 %collective-permute-start.1 = (bf16[448,768]{1,0:T(8,128)(2,1)}, bf16[448,768]{1,0:T(8,128)(2,1)S(1)}, u32[]{:S(2)}, u32[]{:S(2)}) collective-permute-start(bf16[448,768]{1,0:T(8,128)(2,1)} %pad_maximum_fusion.2), channel_id=1, source_target_pairs={{0,0},{1,17},{2,2},{3,19},{4,4},{5,21},{6,6},{7,23},{8,8},{9,25},{... | collective-permute-start | bytes 2064392 | tf_op jit(solution)/shard_map/ppermute | solution.py:23
  13.5 21.2 %collective-permute-start.5 = (bf16[448,768]{1,0:T(8,128)(2,1)}, bf16[448,768]{1,0:T(8,128)(2,1)S(1)}, u32[]{:S(2)}, u32[]{:S(2)}) collective-permute-start(bf16[448,768]{1,0:T(8,128)(2,1)} %pad_maximum_fusion.2), channel_id=1, source_target_pairs={{0,32},{1,33},{2,34},{3,35},{4,36},{5,37},{6,38},{7,39},{8,40},{9,... | collective-permute-start | bytes 2064392 | tf_op jit(solution)/shard_map/ppermute | solution.py:23
  14.9 18.2 %all-to-all-start = ((f32[16,1,1]{2,1,0:T(1,128)}), f32[16,1,1]{2,1,0:T(1,128)S(1)}, u32[]{:S(2)}, u32[]{:S(2)}) async-start(f32[16,1,1]{2,1,0:T(1,128)} %broadcast_in_dim.14), calls=%async_computation | async-start | bytes 16384 | tf_op jit(solution)/shard_map/all_to_all | solution.py:56
  33.3 3.3 %copy-start.2 = (bf16[448,768]{1,0:T(8,128)(2,1)}, bf16[448,768]{1,0:T(8,128)(2,1)S(1)}, u32[]{:S(2)}) copy-start(bf16[448,768]{1,0:T(8,128)(2,1)S(1)} %collective-permute-done.2) | copy-start | bytes 2064388
  33.3 16.7 %collective-permute-start.4 = (bf16[448,768]{1,0:T(8,128)(2,1)S(1)}, bf16[448,768]{1,0:T(8,128)(2,1)S(1)}, u32[]{:S(2)}, u32[]{:S(2)}) collective-permute-start(bf16[448,768]{1,0:T(8,128)(2,1)S(1)} %collective-permute-done.2), channel_id=1, source_target_pairs={{0,224},{1,225},{2,226},{3,227},{4,228},{5,229},{6,230},{7,231},{8... | collective-permute-start | bytes 2064392 | tf_op jit(solution)/shard_map/ppermute | solution.py:23
  33.6 77.0 %copy-start.4 = (bf16[448,768]{1,0:T(8,128)(2,1)}, bf16[448,768]{1,0:T(8,128)(2,1)S(1)}, u32[]{:S(2)}) copy-start(bf16[448,768]{1,0:T(8,128)(2,1)S(1)} %collective-permute-done.1) | copy-start | bytes 2064388
  34.7 17.6 %collective-permute-start.6 = (bf16[448,768]{1,0:T(8,128)(2,1)S(1)}, bf16[448,768]{1,0:T(8,128)(2,1)S(1)}, u32[]{:S(2)}, u32[]{:S(2)}) collective-permute-start(bf16[448,768]{1,0:T(8,128)(2,1)S(1)} %collective-permute-done.5), channel_id=1, source_target_pairs={{0,32},{1,33},{2,34},{3,35},{4,36},{5,37},{6,38},{7,39},{8,40},{9,... | collective-permute-start | bytes 2064392 | tf_op jit(solution)/shard_map/ppermute | solution.py:23
  37.4 22.5 %collective-permute-start.3 = (f32[2,4,56,448]{3,2,0,1:T(8,128)S(1)}, f32[2,4,56,448]{3,2,0,1:T(8,128)S(1)}, u32[]{:S(2)}, u32[]{:S(2)}) collective-permute-start(f32[2,4,56,448]{3,2,0,1:T(8,128)S(1)} %bitcast.120), channel_id=1, source_target_pairs={{0,8},{1,9},{2,10},{3,11},{4,12},{5,13},{6,14},{7,15},{8,0},{9,1},... | collective-permute-start | bytes 2408456 | tf_op jit(solution)/shard_map/ppermute | solution.py:23
  107.9 2.7 %copy-start.6 = (f32[448]{0:T(512)S(1)}, f32[448]{0:T(512)}, u32[]{:S(2)}) copy-start(f32[448]{0:T(512)} %param.5) | copy-start | bytes 5380
  108.0 7.8 %collective-permute-start.7 = (f32[3,56,448]{2,1,0:T(8,128)S(1)}, f32[3,56,448]{2,1,0:T(8,128)}, u32[]{:S(2)}, u32[]{:S(2)}) collective-permute-start(f32[3,56,448]{2,1,0:T(8,128)S(1)} %dynamic-slice_bitcast_fusion), channel_id=1, source_target_pairs={{0,8},{1,9},{2,10},{3,11},{4,12},{5,13},{6,14},{7,15},{8,0},{9,1},... | collective-permute-start | bytes 903176 | tf_op jit(solution)/shard_map/ppermute | solution.py:23
  110.7 29.5 %collective-permute-start.16 = (bf16[448,768]{1,0:T(8,128)(2,1)S(1)}, bf16[448,768]{1,0:T(8,128)(2,1)}, u32[]{:S(2)}, u32[]{:S(2)}) collective-permute-start(bf16[448,768]{1,0:T(8,128)(2,1)S(1)} %collective-permute-done.1), channel_id=1, source_target_pairs={{0,32},{1,33},{2,34},{3,35},{4,36},{5,37},{6,38},{7,39},{8,40},{9,... | collective-permute-start | bytes 2064392 | tf_op jit(solution)/shard_map/ppermute | solution.py:23
  119.0 18.3 %collective-permute-start.12 = (bf16[2,56,448]{2,1,0:T(8,128)(2,1)S(1)}, bf16[2,56,448]{2,1,0:T(8,128)(2,1)S(1)}, u32[]{:S(2)}, u32[]{:S(2)}) collective-permute-start(bf16[2,56,448]{2,1,0:T(8,128)(2,1)S(1)} %pad_maximum_fusion.5), channel_id=1, source_target_pairs={{0,64},{1,81},{2,66},{3,83},{4,68},{5,85},{6,70},{7,87},{8,72},{9,... | collective-permute-start | bytes 301064 | tf_op jit(solution)/shard_map/ppermute | solution.py:23
  126.0 15.6 %all-to-all-start.2 = ((bf16[4,3,56,448]{3,2,1,0:T(8,128)(2,1)}), bf16[4,3,56,448]{3,2,1,0:T(8,128)(2,1)}, u32[]{:S(2)}, u32[]{:S(2)}) async-start(bf16[4,3,56,448]{3,2,1,0:T(8,128)(2,1)} %broadcast_in_dim.15), calls=%async_computation.2 | async-start | bytes 1376256 | tf_op jit(solution)/shard_map/all_to_all | solution.py:101
  130.2 4.0 %collective-permute-start.9 = (bf16[56,448]{1,0:T(8,128)(2,1)S(1)}, bf16[56,448]{1,0:T(8,128)(2,1)S(1)}, u32[]{:S(2)}, u32[]{:S(2)}) collective-permute-start(bf16[56,448]{1,0:T(8,128)(2,1)S(1)} %get-tuple-element.30), channel_id=1, source_target_pairs={{0,224},{1,225},{2,226},{3,227},{4,228},{5,229},{6,230},{7,231},{8... | collective-permute-start | bytes 150536 | tf_op jit(solution)/shard_map/ppermute | solution.py:23
  131.8 4.5 %collective-permute-start.10 = (bf16[56,448]{1,0:T(8,128)(2,1)S(1)}, bf16[56,448]{1,0:T(8,128)(2,1)S(1)}, u32[]{:S(2)}, u32[]{:S(2)}) collective-permute-start(bf16[56,448]{1,0:T(8,128)(2,1)S(1)} %get-tuple-element.29), channel_id=1, source_target_pairs={{0,192},{1,193},{2,194},{3,195},{4,196},{5,197},{6,198},{7,199},{8... | collective-permute-start | bytes 150536 | tf_op jit(solution)/shard_map/ppermute | solution.py:23
  132.1 5.1 %collective-permute-start.11 = (bf16[56,448]{1,0:T(8,128)(2,1)S(1)}, bf16[56,448]{1,0:T(8,128)(2,1)S(1)}, u32[]{:S(2)}, u32[]{:S(2)}) collective-permute-start(bf16[56,448]{1,0:T(8,128)(2,1)S(1)} %get-tuple-element.22), channel_id=1, source_target_pairs={{0,32},{1,49},{2,34},{3,51},{4,36},{5,53},{6,38},{7,55},{8,40},{9,... | collective-permute-start | bytes 150536 | tf_op jit(solution)/shard_map/ppermute | solution.py:23
  137.3 7.1 %collective-permute-start.13 = (bf16[5,56,448]{2,1,0:T(8,128)(2,1)S(1)}, bf16[5,56,448]{2,1,0:T(8,128)(2,1)S(1)}, u32[]{:S(2)}, u32[]{:S(2)}) collective-permute-start(bf16[5,56,448]{2,1,0:T(8,128)(2,1)S(1)} %get-tuple-element.28), channel_id=1, source_target_pairs={{0,8},{1,9},{2,10},{3,11},{4,12},{5,13},{6,14},{7,15},{8,0},{9,1},... | collective-permute-start | bytes 752648 | tf_op jit(solution)/shard_map/ppermute | solution.py:23
  140.1 11.1 %collective-permute-start.14 = (bf16[448,768]{1,0:T(8,128)(2,1)S(1)}, bf16[448,768]{1,0:T(8,128)(2,1)}, u32[]{:S(2)}, u32[]{:S(2)}) collective-permute-start(bf16[448,768]{1,0:T(8,128)(2,1)S(1)} %collective-permute-done.4), channel_id=1, source_target_pairs={{0,224},{1,225},{2,226},{3,227},{4,228},{5,229},{6,230},{7,231},{8... | collective-permute-start | bytes 2064392 | tf_op jit(solution)/shard_map/ppermute | solution.py:23
  140.1 11.9 %collective-permute-start.17 = (bf16[448,768]{1,0:T(8,128)(2,1)}, bf16[448,768]{1,0:T(8,128)(2,1)}, u32[]{:S(2)}, u32[]{:S(2)}) collective-permute-start(bf16[448,768]{1,0:T(8,128)(2,1)} %collective-permute-done.16), channel_id=1, source_target_pairs={{0,32},{1,33},{2,34},{3,35},{4,36},{5,37},{6,38},{7,39},{8,40},{9,... | collective-permute-start | bytes 2064392 | tf_op jit(solution)/shard_map/ppermute | solution.py:23
  141.6 17.6 %collective-permute-start.8 = (bf16[4,3,56,448]{3,2,1,0:T(8,128)(2,1)}, bf16[4,3,56,448]{3,2,1,0:T(8,128)(2,1)}, u32[]{:S(2)}, u32[]{:S(2)}) collective-permute-start(bf16[4,3,56,448]{3,2,1,0:T(8,128)(2,1)} %all-to-all-done.2), channel_id=1, source_target_pairs={{0,8},{1,9},{2,10},{3,11},{4,12},{5,13},{6,14},{7,15},{8,0},{9,1},... | collective-permute-start | bytes 1806344 | tf_op jit(solution)/shard_map/ppermute | solution.py:23
  146.1 21.8 %all-to-all-start.3 = ((bf16[4,2,5,56,448]{4,3,1,2,0:T(8,128)(2,1)}), bf16[4,2,5,56,448]{4,3,1,2,0:T(8,128)(2,1)S(1)}, u32[]{:S(2)}, u32[]{:S(2)}) async-start(bf16[4,2,5,56,448]{4,3,1,2,0:T(8,128)(2,1)} %broadcast_in_dim.16), calls=%async_computation.3 | async-start | bytes 4587520 | tf_op jit(solution)/shard_map/all_to_all | solution.py:111
  151.2 21.1 %collective-permute-start.15 = (bf16[448,768]{1,0:T(8,128)(2,1)}, bf16[448,768]{1,0:T(8,128)(2,1)}, u32[]{:S(2)}, u32[]{:S(2)}) collective-permute-start(bf16[448,768]{1,0:T(8,128)(2,1)} %collective-permute-done.14), channel_id=1, source_target_pairs={{0,224},{1,225},{2,226},{3,227},{4,228},{5,229},{6,230},{7,231},{8... | collective-permute-start | bytes 2064392 | tf_op jit(solution)/shard_map/ppermute | solution.py:23
  152.1 23.5 %collective-permute-start.18 = (bf16[448,768]{1,0:T(8,128)(2,1)}, bf16[448,768]{1,0:T(8,128)(2,1)}, u32[]{:S(2)}, u32[]{:S(2)}) collective-permute-start(bf16[448,768]{1,0:T(8,128)(2,1)} %collective-permute-done.17), channel_id=1, source_target_pairs={{0,32},{1,33},{2,34},{3,35},{4,36},{5,37},{6,38},{7,39},{8,40},{9,... | collective-permute-start | bytes 2064392 | tf_op jit(solution)/shard_map/ppermute | solution.py:23
  161.3 1.1 copy-start.3
  161.4 1.5 copy-start.5
  168.3 1.7 copy-start.1
  177.3 13.5 %collective-permute-start.19 = (f32[448,384]{1,0:T(8,128)S(1)}, f32[448,384]{1,0:T(8,128)S(1)}, u32[]{:S(2)}, u32[]{:S(2)}) collective-permute-start(f32[448,384]{1,0:T(8,128)S(1)} %slice.95), channel_id=1, source_target_pairs={{0,1},{1,0},{2,3},{3,2},{4,5},{5,4},{6,7},{7,6},{8,9},{9,8},{10,11... | collective-permute-start | bytes 2064392 | tf_op jit(solution)/shard_map/ppermute | solution.py:23

commit v4 on v3

v4 whole, which is shorter than its diff:
```python
import jax
import jax.numpy as jnp
from jax import lax
from jax.sharding import Mesh, PartitionSpec as P

NZ, NXL, NXH, NY, NC = 8, 2, 2, 4, 2
ALL = ("z", "xl", "xh", "y", "c")


def flat(z, xl, xh, y, c):
    return (((z % NZ * NXL + xl % NXL) * NXH + xh % NXH) * NY + y % NY) * NC + c % NC


def moved(array, where):
    pairs = [
        (flat(z, xl, xh, y, c), flat(*where(z, xl, xh, y, c)))
        for z in range(NZ)
        for xl in range(NXL)
        for xh in range(NXH)
        for y in range(NY)
        for c in range(NC)
    ]
    return lax.ppermute(array, ALL, pairs)


def across(array):
    return moved(array, lambda z, xl, xh, y, c: (z, xl, 1 - xh, y, c))


def dot_nt(a, b):
    return lax.dot_general(a, b, (((1,), (1,)), ((), ())), preferred_element_type=jnp.float32)


def dot_tn(a, b):
    return lax.dot_general(a, b, (((0,), (0,)), ((), ())), preferred_element_type=jnp.float32)


def half_of(array, which, dim):
    return lax.dynamic_index_in_dim(array, which, dim, keepdims=False)


def local(three_index, occ_energy, vir_energy):
    own = three_index[0]
    nvir, depth = own.shape
    share = nvir // (NXH * NY)
    z, xl, c = lax.axis_index("z"), lax.axis_index("xl"), lax.axis_index("c")
    xh, y = lax.axis_index("xh"), lax.axis_index("y")

    other = moved(own, lambda z, xl, xh, y, c: (z, xl, xh, y, 1 - c))
    high = lax.reduce_precision(occ_energy[0], 8, 7)
    rest = occ_energy[0] - high
    middle = lax.reduce_precision(rest, 8, 7)
    column = lax.broadcasted_iota(jnp.int32, (8, 2 * depth), 1)
    tail = jnp.where(column == 0, high, jnp.where(column == 1, middle, jnp.where(column == 2, rest - middle, 0.0)))
    mine = jnp.concatenate([jnp.concatenate([own, other], axis=1), tail.astype(jnp.bfloat16)], axis=0)

    ahead = [moved(mine, lambda z, xl, xh, y, c: (z, xl if c == 0 else 1 - xl, xh, y, c))]
    ahead.append(moved(mine, lambda z, xl, xh, y, c: (z - 1, xl if c == 0 else 1 - xl, xh, y, c)))
    behind = [mine, moved(mine, lambda z, xl, xh, y, c: (z + 1, xl, xh, y, c))]
    ahead.append(moved(ahead[1], lambda z, xl, xh, y, c: (z - 1, xl, xh, y, c)))
    behind.append(moved(behind[1], lambda z, xl, xh, y, c: (z + 1, xl, xh, y, c)))

    def numer(i, j):
        a, b = behind[i][:nvir], ahead[j][:nvir]
        return dot_nt(a * jnp.bfloat16(2), b) - dot_nt(b, a)

    def halves(*values):
        value = jnp.stack(values).reshape(len(values), NXH, NY, share, nvir)
        got = across(half_of(value, 1 - xh, 1))
        value = half_of(value, xh, 1) + got
        return value.transpose(1, 0, 2, 3).reshape(NY, len(values) * share, nvir)

    def over_y(parts):
        return jnp.sum(lax.all_to_all(parts, "y", 0, 0, tiled=True), axis=0)

    def energy(block):
        terms = block[nvir, :3].astype(jnp.float32)
        return terms[0] + terms[1] + terms[2]

    vir_rows = lax.dynamic_slice_in_dim(vir_energy, (xh * NY + y) * share, share)
    virs = vir_rows[:, None] + vir_energy[None, :]

    def amps(value, i, j):
        return (value / (virs - energy(behind[i]) - energy(ahead[j]))).astype(jnp.bfloat16)

    early = halves(numer(0, 0), numer(0, 1))
    late = numer(0, 2).reshape(NXH, NY, share, nvir).transpose(1, 0, 2, 3).reshape(NY, NXH * share, nvir)
    last = halves(numer(1, 2), numer(2, 2))
    sums = over_y(jnp.concatenate([early, late], axis=1))

    for _ in range(2):
        ahead.append(moved(ahead[-1], lambda z, xl, xh, y, c: (z - 1, xl, xh, y, c)))
    turned = [ahead[0]]
    for _ in range(3):
        turned.append(moved(turned[-1], lambda z, xl, xh, y, c: (z + 1, xl, xh, y, c)))
    sums, ahead[3], turned[1] = lax.optimization_barrier((sums, ahead[3], turned[1]))

    p0, p1 = amps(sums[:share], 0, 0), amps(sums[share : 2 * share], 0, 1)
    late = sums[2 * share :].reshape(NXH, share, nvir)
    p2 = amps(half_of(late, xh, 0) + across(half_of(late, 1 - xh, 0)), 0, 2)
    t1 = moved(p1, lambda z, xl, xh, y, c: (z + 1, xl if c == 0 else 1 - xl, xh, y, c))
    t2 = moved(p2, lambda z, xl, xh, y, c: (z + 2, xl if c == 0 else 1 - xl, xh, y, c))

    last = over_y(last)
    p3, p4 = amps(last[:share], 1, 2), amps(last[share:], 2, 2)
    t3 = moved(p3, lambda z, xl, xh, y, c: (z + 2, xl if c == 0 else 1 - xl, xh, y, c))
    d3 = moved(p3, lambda z, xl, xh, y, c: (z - 1, xl, xh, y, c))
    d4 = moved(p4, lambda z, xl, xh, y, c: (z - 2, xl, xh, y, c))

    def to_all(parts):
        return lax.all_to_all(jnp.broadcast_to(parts, (NY, *parts.shape)), "y", 0, 0, tiled=True)

    def in_order(here, there):
        return jnp.where(xh == 0, jnp.stack([here, there]), jnp.stack([there, here]))

    rows = to_all(jnp.stack([p0, p1, t1]))
    rows = in_order(rows, across(rows)).transpose(2, 0, 1, 3, 4).reshape(3, nvir, nvir)
    more = jnp.stack([p2, t2, d3, d4, t3])
    more = to_all(in_order(more, across(more))).transpose(2, 1, 0, 3, 4).reshape(5, nvir, nvir)

    total = jnp.dot(rows[0], ahead[0][:nvir], preferred_element_type=jnp.float32)
    total = total + jnp.dot(rows[1], ahead[1][:nvir], preferred_element_type=jnp.float32)
    total = total + dot_tn(rows[2], turned[1][:nvir])
    for n, k in ((0, 2), (2, 3), (3, 4)):
        total = total + jnp.dot(more[n], ahead[k][:nvir], preferred_element_type=jnp.float32)
    for n, k in ((1, 2), (4, 3)):
        total = total + dot_tn(more[n], turned[k][:nvir])
    back = moved(total[:, depth:], lambda z, xl, xh, y, c: (z, xl, xh, y, 1 - c))
    return (total[:, :depth] + back)[None]


def solution(mesh):
    grid = Mesh(mesh.devices.reshape(NZ, NXL, NXH, NY, NC), ALL)
    return jax.shard_map(
        local,
        mesh=grid,
        in_specs=(P(("z", "xl"), None, ("xh", "y", "c")), P(("z", "xl")), P()),
        out_specs=P(("z", "xl"), None, ("xh", "y", "c")),
        check_vma=False,
    )
```

time: 193 us -> 194 us (level)
  blocking collectives: 44.9 us -> 0 us
  waiting for transfers between devices: 52.1 us -> 74.2 us
  between operations: 1.03 us -> 14.6 us
  starting transfers between devices: 55.5 us -> 61 us
  local copies, waits for them, and re-layouts: 5.82 us -> 10.5 us
    all_to_all x1 -> x0, blocking collectives: 44.9 us -> none  [local(): sums = jnp.sum(lax.all_to_all(parts, 'y', 0, 0, tiled=True), axis=0)]
    ppermute x20 -> x22, waiting for transfers between devices: 35.6 us -> 50.3 us  [moved(): return lax.ppermute(array, ALL, pairs)]
    all_to_all x3 -> x4, waiting for transfers between devices: 16.5 us -> 23.9 us  [the longest x2 17.7 us: to_all(): lax.all_to_all(jnp.broadcast_to(parts, (NY, *parts.shape)), 'y', 0, 0, ti...]
    slice x3 -> x9, local copies, waits for them, and re-layouts: 0.29 us -> 4.18 us  [the longest x6 3.85 us: energy(): return terms[0] + terms[1] + terms[2]]
    all_to_all x3 -> x4, starting transfers between devices: 13.4 us -> 16.2 us  [the longest x2 8.41 us: over_y(): return jnp.sum(lax.all_to_all(parts, 'y', 0, 0, tiled=True), axis=0)]
    ppermute x20 -> x22, starting transfers between devices: 42.1 us -> 44.7 us  [moved(): return lax.ppermute(array, ALL, pairs)]
    convert_element_type x2 -> x7, other arithmetic: 6.05 us -> 3.92 us  [the longest x6 2.72 us: energy(): terms = block[nvir, :3].astype(jnp.float32)]
  transfers between devices with their start and end apart: 23 -> 26, of which waited for: 13 -> 14; matrix products, arithmetic and copies ran while one was open for 15% -> 19% of each run, Pallas kernels for 0% -> 0%
where the time goes in v4:
time: 194 us; the launch traced here: 193 us
  waiting for transfers between devices  74.2 us (38%)
  starting transfers between devices  61 us (31%)
  matrix products  17.9 us (9%)
  between operations  14.6 us (8%)
  other arithmetic  14.5 us (7%)
  local copies, waits for them, and re-layouts  10.5 us (5%)
    ppermute x22, waiting for transfers between devices, moved(): return lax.ppermute(array, ALL, pairs)  50.3 us
    ppermute x22, starting transfers between devices, moved(): return lax.ppermute(array, ALL, pairs)  44.7 us
    all_to_all x2, waiting for transfers between devices, to_all(): lax.all_to_all(jnp.broadcast_to(parts, (NY, *parts.shape)), 'y', 0, 0, ti...  17.7 us
    all_to_all x2, starting transfers between devices, over_y(): return jnp.sum(lax.all_to_all(parts, 'y', 0, 0, tiled=True), axis=0)  8.41 us
    all_to_all x2, starting transfers between devices, to_all(): lax.all_to_all(jnp.broadcast_to(parts, (NY, *parts.shape)), 'y', 0, 0, ti...  7.81 us
    dot_general x10, matrix products, dot_nt(): lax.dot_general(a, b, (((1,), (1,)), ((), ())), preferred_element_type=jn...  7.02 us
    all_to_all x2, waiting for transfers between devices, over_y(): return jnp.sum(lax.all_to_all(parts, 'y', 0, 0, tiled=True), axis=0)  6.28 us
    dot_general x3, matrix products, dot_tn(): lax.dot_general(a, b, (((0,), (0,)), ((), ())), preferred_element_type=jn...  6.09 us
  transfers between devices with their start and end apart: 26, of which 14 were waited for; matrix products, arithmetic and copies ran while one was open for 19% of the time, Pallas kernels for 0%

profile of v4, /device:TPU:1, one launch (start us, length us, event | category | flops | bytes accessed | tf_op | source)
XLA Modules:
  0.0 192.7 jit_solution(10007510178457478316)
XLA Ops:
  0.0 3.2 %collective-permute-start = (bf16[448,384]{1,0:T(8,128)(2,1)}, bf16[448,384]{1,0:T(8,128)(2,1)S(1)}, u32[]{:S(2)}, u32[]{:S(2)}) collective-permute-start(bf16[448,384]{1,0:T(8,128)(2,1)} %bitcast.105), channel_id=1, source_target_pairs={{0,1},{1,0},{2,3},{3,2},{4,5},{5,4},{6,7},{7,6},{8,9},{9,8},{10,11... | collective-permute-start | bytes 1032200 | tf_op jit(solution)/shard_map/ppermute | solution.py:23
  6.1 1.2 select_convert_fusion
  7.3 1.2 pad_maximum_fusion.1
  8.5 4.8 %collective-permute-start.2 = (bf16[456,768]{1,0:T(8,128)(2,1)S(1)}, bf16[456,768]{1,0:T(8,128)(2,1)S(1)}, u32[]{:S(2)}, u32[]{:S(2)}) collective-permute-start(bf16[456,768]{1,0:T(8,128)(2,1)S(1)} %pad_maximum_fusion.1), channel_id=1, source_target_pairs={{0,224},{1,241},{2,226},{3,243},{4,228},{5,245},{6,230},{7,247},{8... | collective-permute-start | bytes 2101256 | tf_op jit(solution)/shard_map/ppermute | solution.py:23
  13.4 2.2 %collective-permute-start.1 = (bf16[456,768]{1,0:T(8,128)(2,1)S(1)}, bf16[456,768]{1,0:T(8,128)(2,1)S(1)}, u32[]{:S(2)}, u32[]{:S(2)}) collective-permute-start(bf16[456,768]{1,0:T(8,128)(2,1)S(1)} %pad_maximum_fusion.1), channel_id=1, source_target_pairs={{0,0},{1,17},{2,2},{3,19},{4,4},{5,21},{6,6},{7,23},{8,8},{9,25},{... | collective-permute-start | bytes 2101256 | tf_op jit(solution)/shard_map/ppermute | solution.py:23
  15.5 0.7 fusion.75
  18.1 10.3 %collective-permute-done.2 = bf16[456,768]{1,0:T(8,128)(2,1)S(1)} collective-permute-done((bf16[456,768]{1,0:T(8,128)(2,1)S(1)}, bf16[456,768]{1,0:T(8,128)(2,1)S(1)}, u32[]{:S(2)}, u32[]{:S(2)}) %collective-permute-start.2) | collective-permute-done | bytes 700448 | tf_op jit(solution)/shard_map/ppermute | solution.py:23
  28.4 3.1 %collective-permute-start.4 = (bf16[456,768]{1,0:T(8,128)(2,1)S(1)}, bf16[456,768]{1,0:T(8,128)(2,1)S(1)}, u32[]{:S(2)}, u32[]{:S(2)}) collective-permute-start(bf16[456,768]{1,0:T(8,128)(2,1)S(1)} %collective-permute-done.2), channel_id=1, source_target_pairs={{0,224},{1,225},{2,226},{3,227},{4,228},{5,229},{6,230},{7,231},{8... | collective-permute-start | bytes 2101256 | tf_op jit(solution)/shard_map/ppermute | solution.py:23
  31.9 2.1 %fusion.27 = f32[448,448]{1,0:T(8,128)S(1)} fusion(bf16[456,768]{1,0:T(8,128)(2,1)S(1)} %collective-permute-done.1, bf16[448,384]{1,0:T(8,128)(2,1)} %copy-done.8, bf16[448,384]{1,0:T(8,128)(2,1)} %bitcast.107), kind=kOutput, calls=%fused_computation.57 | convolution fusion | flops 309657600 | bytes 2179072 | tf_op jit(solution)/shard_map/dot_general | solution.py:31
  34.1 0.6 convolution_subtract_fusion.4
  35.2 0.6 convolution_subtract_fusion.3
  36.1 2.8 %collective-permute-start.3 = (f32[2,4,56,448]{3,2,0,1:T(8,128)S(1)}, f32[2,4,56,448]{3,2,0,1:T(8,128)S(1)}, u32[]{:S(2)}, u32[]{:S(2)}) collective-permute-start(f32[2,4,56,448]{3,2,0,1:T(8,128)S(1)} %bitcast.98), channel_id=1, source_target_pairs={{0,8},{1,9},{2,10},{3,11},{4,12},{5,13},{6,14},{7,15},{8,0},{9,1},... | collective-permute-start | bytes 2408456 | tf_op jit(solution)/shard_map/ppermute | solution.py:23
  38.9 7.4 %collective-permute-done.4 = bf16[456,768]{1,0:T(8,128)(2,1)S(1)} collective-permute-done((bf16[456,768]{1,0:T(8,128)(2,1)S(1)}, bf16[456,768]{1,0:T(8,128)(2,1)S(1)}, u32[]{:S(2)}, u32[]{:S(2)}) %collective-permute-start.4) | collective-permute-done | bytes 700448 | tf_op jit(solution)/shard_map/ppermute | solution.py:23
  46.9 3.2 %collective-permute-done.12 = bf16[456,768]{1,0:T(8,128)(2,1)S(1)} collective-permute-done((bf16[456,768]{1,0:T(8,128)(2,1)S(1)}, bf16[456,768]{1,0:T(8,128)(2,1)S(1)}, u32[]{:S(2)}, u32[]{:S(2)}) %collective-permute-start.12) | collective-permute-done | bytes 700448 | tf_op jit(solution)/shard_map/ppermute | solution.py:23
  50.6 0.5 convolution_subtract_fusion
  51.1 0.5 convolution_subtract_fusion.1
  51.9 1.0 copy.21
  52.9 2.6 %collective-permute-start.13 = (f32[2,4,56,448]{3,2,0,1:T(8,128)}, f32[2,4,56,448]{3,2,0,1:T(8,128)}, u32[]{:S(2)}, u32[]{:S(2)}) collective-permute-start(f32[2,4,56,448]{3,2,0,1:T(8,128)} %bitcast.81), channel_id=1, source_target_pairs={{0,8},{1,9},{2,10},{3,11},{4,12},{5,13},{6,14},{7,15},{8,0},{9,1},... | collective-permute-start | bytes 2408456 | tf_op jit(solution)/shard_map/ppermute | solution.py:23
  56.0 0.6 convolution_subtract_fusion.2
  56.7 2.5 %collective-permute-done.3 = f32[2,4,56,448]{3,2,0,1:T(8,128)S(1)} collective-permute-done((f32[2,4,56,448]{3,2,0,1:T(8,128)S(1)}, f32[2,4,56,448]{3,2,0,1:T(8,128)S(1)}, u32[]{:S(2)}, u32[]{:S(2)}) %collective-permute-start.3) | collective-permute-done | bytes 802848 | tf_op jit(solution)/shard_map/ppermute | solution.py:23
  59.4 1.5 pad_maximum_fusion
  60.9 4.2 %all-to-all-start = ((f32[4,224,448]{2,1,0:T(8,128)}), f32[4,224,448]{2,1,0:T(8,128)S(1)}, u32[]{:S(2)}, u32[]{:S(2)}) async-start(f32[4,224,448]{2,1,0:T(8,128)} %pad_maximum_fusion), calls=%async_computation | async-start | bytes 3670016 | tf_op jit(solution)/shard_map/all_to_all | solution.py:74
  65.0 0.7 slice_convert_fusion.4
  65.7 0.6 fusion.71
  68.2 0.7 slice_convert_fusion.3
  68.9 0.6 fusion.72
  71.3 0.7 slice_convert_fusion.1
  72.0 0.7 fusion.74
  74.7 2.7 %collective-permute-start.5 = (bf16[456,768]{1,0:T(8,128)(2,1)S(1)}, bf16[456,768]{1,0:T(8,128)(2,1)}, u32[]{:S(2)}, u32[]{:S(2)}) collective-permute-start(bf16[456,768]{1,0:T(8,128)(2,1)S(1)} %collective-permute-done.4), channel_id=1, source_target_pairs={{0,224},{1,225},{2,226},{3,227},{4,228},{5,229},{6,230},{7,231},{8... | collective-permute-start | bytes 2101256 | tf_op jit(solution)/shard_map/ppermute | solution.py:23
  77.3 1.7 collective-permute-done.13
  79.0 2.3 %bitcast_add_fusion = f32[2,4,56,448]{3,2,0,1:T(8,128)} fusion(f32[2,4,56,448]{3,2,0,1:T(8,128)} %collective-permute-done.13, f32[2,1,4,56,448]{4,3,2,1,0:T(8,128)S(1)} %get-tuple-element.18), kind=kLoop, calls=%fused_computation.28 | loop fusion | flops 200704 | bytes 2408448 | tf_op jit(solution)/shard_map/add | solution.py:70
  81.3 4.9 %all-to-all-done = f32[4,224,448]{2,1,0:T(8,128)S(1)} async-done(((f32[4,224,448]{2,1,0:T(8,128)}), f32[4,224,448]{2,1,0:T(8,128)S(1)}, u32[]{:S(2)}, u32[]{:S(2)}) %all-to-all-start) | async-done | bytes 1605664 | tf_op jit(solution)/shard_map/all_to_all | solution.py:74
  86.2 4.2 %all-to-all-start.2 = ((f32[4,112,448]{2,1,0:T(8,128)}), f32[4,112,448]{2,1,0:T(8,128)}, u32[]{:S(2)}, u32[]{:S(2)}) async-start(f32[4,112,448]{2,1,0:T(8,128)} %bitcast.34), calls=%async_computation.2 | async-start | bytes 1835008 | tf_op jit(solution)/shard_map/all_to_all | solution.py:74
  90.5 0.7 fusion.76
  93.1 0.7 slice_convert_fusion
  93.8 0.7 fusion.73
  96.9 2.4 %collective-permute-start.9 = (f32[56,448]{1,0:T(8,128)S(1)}, f32[56,448]{1,0:T(8,128)S(1)}, u32[]{:S(2)}, u32[]{:S(2)}) collective-permute-start(f32[56,448]{1,0:T(8,128)S(1)} %dynamic-slice_bitcast_fusion), channel_id=1, source_target_pairs={{0,8},{1,9},{2,10},{3,11},{4,12},{5,13},{6,14},{7,15},{8,0},{9,1},... | collective-permute-start | bytes 301064 | tf_op jit(solution)/shard_map/ppermute | solution.py:23
  99.3 1.4 all-to-all-done.2
  100.7 1.3 reduce_sum.19
  102.1 1.4 collective-permute-start.14
  103.5 0.9 collective-permute-start.7
  104.4 3.8 %collective-permute-start.15 = (bf16[56,448]{1,0:T(8,128)(2,1)S(1)}, bf16[56,448]{1,0:T(8,128)(2,1)S(1)}, u32[]{:S(2)}, u32[]{:S(2)}) collective-permute-start(bf16[56,448]{1,0:T(8,128)(2,1)S(1)} %get-tuple-element.30), channel_id=1, source_target_pairs={{0,192},{1,193},{2,194},{3,195},{4,196},{5,197},{6,198},{7,199},{8... | collective-permute-start | bytes 150536 | tf_op jit(solution)/shard_map/ppermute | solution.py:23
  108.3 6.9 %collective-permute-done.7 = bf16[56,448]{1,0:T(8,128)(2,1)S(1)} collective-permute-done((bf16[56,448]{1,0:T(8,128)(2,1)S(1)}, bf16[56,448]{1,0:T(8,128)(2,1)S(1)}, u32[]{:S(2)}, u32[]{:S(2)}) %collective-permute-start.7) | collective-permute-done | bytes 50208 | tf_op jit(solution)/shard_map/ppermute | solution.py:23
  115.2 0.9 broadcast_in_dim.30
  116.1 4.2 %all-to-all-start.1 = ((bf16[4,3,56,448]{3,2,1,0:T(8,128)(2,1)}), bf16[4,3,56,448]{3,2,1,0:T(8,128)(2,1)}, u32[]{:S(2)}, u32[]{:S(2)}) async-start(bf16[4,3,56,448]{3,2,1,0:T(8,128)(2,1)} %broadcast_in_dim.30), calls=%async_computation.1 | async-start | bytes 1376256 | tf_op jit(solution)/shard_map/all_to_all | solution.py:111
  120.3 0.9 collective-permute-done.10
  121.3 6.9 %all-to-all-done.1 = bf16[4,3,56,448]{3,2,1,0:T(8,128)(2,1)} async-done(((bf16[4,3,56,448]{3,2,1,0:T(8,128)(2,1)}), bf16[4,3,56,448]{3,2,1,0:T(8,128)(2,1)}, u32[]{:S(2)}, u32[]{:S(2)}) %all-to-all-start.1) | async-done | bytes 602144 | tf_op jit(solution)/shard_map/all_to_all | solution.py:111
  128.2 2.7 %collective-permute-start.8 = (bf16[4,3,56,448]{3,2,1,0:T(8,128)(2,1)}, bf16[4,3,56,448]{3,2,1,0:T(8,128)(2,1)}, u32[]{:S(2)}, u32[]{:S(2)}) collective-permute-start(bf16[4,3,56,448]{3,2,1,0:T(8,128)(2,1)} %all-to-all-done.1), channel_id=1, source_target_pairs={{0,8},{1,9},{2,10},{3,11},{4,12},{5,13},{6,14},{7,15},{8,0},{9,1},... | collective-permute-start | bytes 1806344 | tf_op jit(solution)/shard_map/ppermute | solution.py:23
  131.3 15.1 %collective-permute-done.17 = bf16[5,56,448]{2,1,0:T(8,128)(2,1)S(1)} collective-permute-done((bf16[5,56,448]{2,1,0:T(8,128)(2,1)S(1)}, bf16[5,56,448]{2,1,0:T(8,128)(2,1)S(1)}, u32[]{:S(2)}, u32[]{:S(2)}) %collective-permute-start.17) | collective-permute-done | bytes 250912 | tf_op jit(solution)/shard_map/ppermute | solution.py:23
  146.5 1.7 broadcast_in_dim.31
  148.2 3.6 %all-to-all-start.3 = ((bf16[4,2,5,56,448]{4,3,1,2,0:T(8,128)(2,1)}), bf16[4,2,5,56,448]{4,3,1,2,0:T(8,128)(2,1)S(1)}, u32[]{:S(2)}, u32[]{:S(2)}) async-start(bf16[4,2,5,56,448]{4,3,1,2,0:T(8,128)(2,1)} %broadcast_in_dim.31), calls=%async_computation.3 | async-start | bytes 4587520 | tf_op jit(solution)/shard_map/all_to_all | solution.py:111
  151.8 2.7 %collective-permute-start.18 = (bf16[456,768]{1,0:T(8,128)(2,1)}, bf16[456,768]{1,0:T(8,128)(2,1)}, u32[]{:S(2)}, u32[]{:S(2)}) collective-permute-start(bf16[456,768]{1,0:T(8,128)(2,1)} %collective-permute-done.5), channel_id=1, source_target_pairs={{0,224},{1,225},{2,226},{3,227},{4,228},{5,229},{6,230},{7,231},{8... | collective-permute-start | bytes 2101256 | tf_op jit(solution)/shard_map/ppermute | solution.py:23
  154.5 2.2 %fusion.1 = bf16[3,2,4,56,448]{4,3,0,2,1:T(8,128)(2,1)S(1)} fusion(bf16[1,4,3,56,448]{4,3,2,1,0:T(8,128)(2,1)} %bitcast.18, bf16[1,4,3,56,448]{4,3,2,1,0:T(8,128)(2,1)} %bitcast.17, pred[]{:T(512)S(6)} %eq.25), kind=kLoop, calls=%fused_computation.18 | loop fusion | flops 1806336 | bytes 2408449 | tf_op jit(solution)/shard_map/transpose | solution.py:117
  156.8 1.0 copy-done.2
  158.8 2.8 %convolution_add_fusion.4 = f32[448,768]{1,0:T(8,128)} fusion(f32[448,768]{1,0:T(8,128)S(1)} %convolution_add_fusion.5, bf16[448,448]{1,0:T(8,128)(2,1)S(1)} %bitcast.96, bf16[456,768]{1,0:T(8,128)(2,1)} %collective-permute-done.6), kind=kOutput, calls=%fused_computation.15 | convolution fusion | flops 308625408 | bytes 3842048 | tf_op jit(solution)/shard_map/dot_general | solution.py:35
  161.6 10.8 %all-to-all-done.3 = bf16[4,2,5,56,448]{4,3,1,2,0:T(8,128)(2,1)S(1)} async-done(((bf16[4,2,5,56,448]{4,3,1,2,0:T(8,128)(2,1)}), bf16[4,2,5,56,448]{4,3,1,2,0:T(8,128)(2,1)S(1)}, u32[]{:S(2)}, u32[]{:S(2)}) %all-to-all-start.3) | async-done | bytes 2007072 | tf_op jit(solution)/shard_map/all_to_all | solution.py:111
  172.9 1.1 copy-done
  174.5 1.6 fusion.8
  176.2 1.6 convolution_add_fusion.2
  177.8 1.6 fusion
  179.4 1.7 convolution_add_fusion
  181.2 8.8 %collective-permute-start.21 = (f32[448,384]{1,0:T(8,128)S(1)}, f32[448,384]{1,0:T(8,128)S(1)}, u32[]{:S(2)}, u32[]{:S(2)}) collective-permute-start(f32[448,384]{1,0:T(8,128)S(1)} %slice.268), channel_id=1, source_target_pairs={{0,1},{1,0},{2,3},{3,2},{4,5},{5,4},{6,7},{7,6},{8,9},{9,8},{10,11... | collective-permute-start | bytes 2064392 | tf_op jit(solution)/shard_map/ppermute | solution.py:23
  190.0 1.8 collective-permute-done.21
  191.8 0.9 fusion.6
  (73 shorter events, 7.0 us)
Async XLA Ops:
  0.0 18.0 %copy-start.10 = (f32[448]{0:T(512)S(1)}, f32[448]{0:T(512)}, u32[]{:S(2)}) copy-start(f32[448]{0:T(512)} %param.5) | copy-start | bytes 5380
  0.0 7.3 %collective-permute-start = (bf16[448,384]{1,0:T(8,128)(2,1)}, bf16[448,384]{1,0:T(8,128)(2,1)S(1)}, u32[]{:S(2)}, u32[]{:S(2)}) collective-permute-start(bf16[448,384]{1,0:T(8,128)(2,1)} %bitcast.105), channel_id=1, source_target_pairs={{0,1},{1,0},{2,3},{3,2},{4,5},{5,4},{6,7},{7,6},{8,9},{9,8},{10,11... | collective-permute-start | bytes 1032200 | tf_op jit(solution)/shard_map/ppermute | solution.py:23
  7.3 10.8 %copy-start.8 = (bf16[448,384]{1,0:T(8,128)(2,1)}, bf16[448,384]{1,0:T(8,128)(2,1)S(1)}, u32[]{:S(2)}) copy-start(bf16[448,384]{1,0:T(8,128)(2,1)S(1)} %collective-permute-done) | copy-start | bytes 1032196
  8.5 19.9 %collective-permute-start.2 = (bf16[456,768]{1,0:T(8,128)(2,1)S(1)}, bf16[456,768]{1,0:T(8,128)(2,1)S(1)}, u32[]{:S(2)}, u32[]{:S(2)}) collective-permute-start(bf16[456,768]{1,0:T(8,128)(2,1)S(1)} %pad_maximum_fusion.1), channel_id=1, source_target_pairs={{0,224},{1,241},{2,226},{3,243},{4,228},{5,245},{6,230},{7,247},{8... | collective-permute-start | bytes 2101256 | tf_op jit(solution)/shard_map/ppermute | solution.py:23
  13.4 18.6 %collective-permute-start.11 = (bf16[456,768]{1,0:T(8,128)(2,1)S(1)}, bf16[456,768]{1,0:T(8,128)(2,1)S(1)}, u32[]{:S(2)}, u32[]{:S(2)}) collective-permute-start(bf16[456,768]{1,0:T(8,128)(2,1)S(1)} %pad_maximum_fusion.1), channel_id=1, source_target_pairs={{0,32},{1,33},{2,34},{3,35},{4,36},{5,37},{6,38},{7,39},{8,40},{9,... | collective-permute-start | bytes 2101256 | tf_op jit(solution)/shard_map/ppermute | solution.py:23
  13.4 18.6 %collective-permute-start.1 = (bf16[456,768]{1,0:T(8,128)(2,1)S(1)}, bf16[456,768]{1,0:T(8,128)(2,1)S(1)}, u32[]{:S(2)}, u32[]{:S(2)}) collective-permute-start(bf16[456,768]{1,0:T(8,128)(2,1)S(1)} %pad_maximum_fusion.1), channel_id=1, source_target_pairs={{0,0},{1,17},{2,2},{3,19},{4,4},{5,21},{6,6},{7,23},{8,8},{9,25},{... | collective-permute-start | bytes 2101256 | tf_op jit(solution)/shard_map/ppermute | solution.py:23
  18.1 16.0 %copy-start.7 = (bf16[1,448,384]{2,1,0:T(8,128)(2,1)S(1)}, bf16[1,448,384]{2,1,0:T(8,128)(2,1)}, u32[]{:S(2)}) copy-start(bf16[1,448,384]{2,1,0:T(8,128)(2,1)} %param.3) | copy-start | bytes 1032196
  28.4 6.8 %copy-start.1 = (bf16[456,768]{1,0:T(8,128)(2,1)}, bf16[456,768]{1,0:T(8,128)(2,1)S(1)}, u32[]{:S(2)}) copy-start(bf16[456,768]{1,0:T(8,128)(2,1)S(1)} %collective-permute-done.2) | copy-start | bytes 2101252
  28.4 5.7 %copy-start.9 = (bf16[448,384]{1,0:T(8,128)(2,1)S(1)}, bf16[448,384]{1,0:T(8,128)(2,1)}, u32[]{:S(2)}) copy-start(bf16[448,384]{1,0:T(8,128)(2,1)} %copy-done.8) | copy-start | bytes 1032196
  28.4 17.9 %collective-permute-start.4 = (bf16[456,768]{1,0:T(8,128)(2,1)S(1)}, bf16[456,768]{1,0:T(8,128)(2,1)S(1)}, u32[]{:S(2)}, u32[]{:S(2)}) collective-permute-start(bf16[456,768]{1,0:T(8,128)(2,1)S(1)} %collective-permute-done.2), channel_id=1, source_target_pairs={{0,224},{1,225},{2,226},{3,227},{4,228},{5,229},{6,230},{7,231},{8... | collective-permute-start | bytes 2101256 | tf_op jit(solution)/shard_map/ppermute | solution.py:23
  31.9 19.2 %copy-start.3 = (bf16[456,768]{1,0:T(8,128)(2,1)}, bf16[456,768]{1,0:T(8,128)(2,1)S(1)}, u32[]{:S(2)}) copy-start(bf16[456,768]{1,0:T(8,128)(2,1)S(1)} %collective-permute-done.11) | copy-start | bytes 2101252
  31.9 18.1 %collective-permute-start.12 = (bf16[456,768]{1,0:T(8,128)(2,1)S(1)}, bf16[456,768]{1,0:T(8,128)(2,1)S(1)}, u32[]{:S(2)}, u32[]{:S(2)}) collective-permute-start(bf16[456,768]{1,0:T(8,128)(2,1)S(1)} %collective-permute-done.11), channel_id=1, source_target_pairs={{0,32},{1,33},{2,34},{3,35},{4,36},{5,37},{6,38},{7,39},{8,40},{9,... | collective-permute-start | bytes 2101256 | tf_op jit(solution)/shard_map/ppermute | solution.py:23
  31.9 2.1 %copy-start.5 = (bf16[456,768]{1,0:T(8,128)(2,1)}, bf16[456,768]{1,0:T(8,128)(2,1)S(1)}, u32[]{:S(2)}) copy-start(bf16[456,768]{1,0:T(8,128)(2,1)S(1)} %collective-permute-done.1) | copy-start | bytes 2101252
  36.1 23.1 %collective-permute-start.3 = (f32[2,4,56,448]{3,2,0,1:T(8,128)S(1)}, f32[2,4,56,448]{3,2,0,1:T(8,128)S(1)}, u32[]{:S(2)}, u32[]{:S(2)}) collective-permute-start(f32[2,4,56,448]{3,2,0,1:T(8,128)S(1)} %bitcast.98), channel_id=1, source_target_pairs={{0,8},{1,9},{2,10},{3,11},{4,12},{5,13},{6,14},{7,15},{8,0},{9,1},... | collective-permute-start | bytes 2408456 | tf_op jit(solution)/shard_map/ppermute | solution.py:23
  50.0 1.1 copy-start.4
  52.9 26.1 %collective-permute-start.13 = (f32[2,4,56,448]{3,2,0,1:T(8,128)}, f32[2,4,56,448]{3,2,0,1:T(8,128)}, u32[]{:S(2)}, u32[]{:S(2)}) collective-permute-start(f32[2,4,56,448]{3,2,0,1:T(8,128)} %bitcast.81), channel_id=1, source_target_pairs={{0,8},{1,9},{2,10},{3,11},{4,12},{5,13},{6,14},{7,15},{8,0},{9,1},... | collective-permute-start | bytes 2408456 | tf_op jit(solution)/shard_map/ppermute | solution.py:23
  60.9 25.4 %all-to-all-start = ((f32[4,224,448]{2,1,0:T(8,128)}), f32[4,224,448]{2,1,0:T(8,128)S(1)}, u32[]{:S(2)}, u32[]{:S(2)}) async-start(f32[4,224,448]{2,1,0:T(8,128)} %pad_maximum_fusion), calls=%async_computation | async-start | bytes 3670016 | tf_op jit(solution)/shard_map/all_to_all | solution.py:74
  74.6 21.8 %collective-permute-start.6 = (bf16[456,768]{1,0:T(8,128)(2,1)}, bf16[456,768]{1,0:T(8,128)(2,1)}, u32[]{:S(2)}, u32[]{:S(2)}) collective-permute-start(bf16[456,768]{1,0:T(8,128)(2,1)} %copy-done.5), channel_id=1, source_target_pairs={{0,32},{1,33},{2,34},{3,35},{4,36},{5,37},{6,38},{7,39},{8,40},{9,... | collective-permute-start | bytes 2101256 | tf_op jit(solution)/shard_map/ppermute | solution.py:23
  74.7 22.2 %collective-permute-start.5 = (bf16[456,768]{1,0:T(8,128)(2,1)S(1)}, bf16[456,768]{1,0:T(8,128)(2,1)}, u32[]{:S(2)}, u32[]{:S(2)}) collective-permute-start(bf16[456,768]{1,0:T(8,128)(2,1)S(1)} %collective-permute-done.4), channel_id=1, source_target_pairs={{0,224},{1,225},{2,226},{3,227},{4,228},{5,229},{6,230},{7,231},{8... | collective-permute-start | bytes 2101256 | tf_op jit(solution)/shard_map/ppermute | solution.py:23
  86.2 14.5 %all-to-all-start.2 = ((f32[4,112,448]{2,1,0:T(8,128)}), f32[4,112,448]{2,1,0:T(8,128)}, u32[]{:S(2)}, u32[]{:S(2)}) async-start(f32[4,112,448]{2,1,0:T(8,128)} %bitcast.34), calls=%async_computation.2 | async-start | bytes 1835008 | tf_op jit(solution)/shard_map/all_to_all | solution.py:74
  96.3 58.1 %collective-permute-start.19 = (bf16[456,768]{1,0:T(8,128)(2,1)}, bf16[456,768]{1,0:T(8,128)(2,1)}, u32[]{:S(2)}, u32[]{:S(2)}) collective-permute-start(bf16[456,768]{1,0:T(8,128)(2,1)} %collective-permute-done.6), channel_id=1, source_target_pairs={{0,32},{1,33},{2,34},{3,35},{4,36},{5,37},{6,38},{7,39},{8,40},{9,... | collective-permute-start | bytes 2101256 | tf_op jit(solution)/shard_map/ppermute | solution.py:23
  96.9 7.4 %collective-permute-start.9 = (f32[56,448]{1,0:T(8,128)S(1)}, f32[56,448]{1,0:T(8,128)S(1)}, u32[]{:S(2)}, u32[]{:S(2)}) collective-permute-start(f32[56,448]{1,0:T(8,128)S(1)} %dynamic-slice_bitcast_fusion), channel_id=1, source_target_pairs={{0,8},{1,9},{2,10},{3,11},{4,12},{5,13},{6,14},{7,15},{8,0},{9,1},... | collective-permute-start | bytes 301064 | tf_op jit(solution)/shard_map/ppermute | solution.py:23
  102.1 19.1 %collective-permute-start.14 = (bf16[56,448]{1,0:T(8,128)(2,1)S(1)}, bf16[56,448]{1,0:T(8,128)(2,1)S(1)}, u32[]{:S(2)}, u32[]{:S(2)}) collective-permute-start(bf16[56,448]{1,0:T(8,128)(2,1)S(1)} %get-tuple-element.29), channel_id=1, source_target_pairs={{0,224},{1,225},{2,226},{3,227},{4,228},{5,229},{6,230},{7,231},{8... | collective-permute-start | bytes 150536 | tf_op jit(solution)/shard_map/ppermute | solution.py:23
  103.5 27.4 %collective-permute-start.16 = (bf16[56,448]{1,0:T(8,128)(2,1)S(1)}, bf16[56,448]{1,0:T(8,128)(2,1)S(1)}, u32[]{:S(2)}, u32[]{:S(2)}) collective-permute-start(bf16[56,448]{1,0:T(8,128)(2,1)S(1)} %get-tuple-element.29), channel_id=1, source_target_pairs={{0,64},{1,81},{2,66},{3,83},{4,68},{5,85},{6,70},{7,87},{8,72},{9,... | collective-permute-start | bytes 150536 | tf_op jit(solution)/shard_map/ppermute | solution.py:23
  103.5 11.7 %collective-permute-start.7 = (bf16[56,448]{1,0:T(8,128)(2,1)S(1)}, bf16[56,448]{1,0:T(8,128)(2,1)S(1)}, u32[]{:S(2)}, u32[]{:S(2)}) collective-permute-start(bf16[56,448]{1,0:T(8,128)(2,1)S(1)} %get-tuple-element.26), channel_id=1, source_target_pairs={{0,32},{1,49},{2,34},{3,51},{4,36},{5,53},{6,38},{7,55},{8,40},{9,... | collective-permute-start | bytes 150536 | tf_op jit(solution)/shard_map/ppermute | solution.py:23
  104.4 16.9 %collective-permute-start.15 = (bf16[56,448]{1,0:T(8,128)(2,1)S(1)}, bf16[56,448]{1,0:T(8,128)(2,1)S(1)}, u32[]{:S(2)}, u32[]{:S(2)}) collective-permute-start(bf16[56,448]{1,0:T(8,128)(2,1)S(1)} %get-tuple-element.30), channel_id=1, source_target_pairs={{0,192},{1,193},{2,194},{3,195},{4,196},{5,197},{6,198},{7,199},{8... | collective-permute-start | bytes 150536 | tf_op jit(solution)/shard_map/ppermute | solution.py:23
  115.2 6.0 %collective-permute-start.10 = (bf16[56,448]{1,0:T(8,128)(2,1)S(1)}, bf16[56,448]{1,0:T(8,128)(2,1)S(1)}, u32[]{:S(2)}, u32[]{:S(2)}) collective-permute-start(bf16[56,448]{1,0:T(8,128)(2,1)S(1)} %get-tuple-element.12), channel_id=1, source_target_pairs={{0,64},{1,81},{2,66},{3,83},{4,68},{5,85},{6,70},{7,87},{8,72},{9,... | collective-permute-start | bytes 150536 | tf_op jit(solution)/shard_map/ppermute | solution.py:23
  116.1 12.1 %all-to-all-start.1 = ((bf16[4,3,56,448]{3,2,1,0:T(8,128)(2,1)}), bf16[4,3,56,448]{3,2,1,0:T(8,128)(2,1)}, u32[]{:S(2)}, u32[]{:S(2)}) async-start(bf16[4,3,56,448]{3,2,1,0:T(8,128)(2,1)} %broadcast_in_dim.30), calls=%async_computation.1 | async-start | bytes 1376256 | tf_op jit(solution)/shard_map/all_to_all | solution.py:111
  128.2 26.3 %collective-permute-start.8 = (bf16[4,3,56,448]{3,2,1,0:T(8,128)(2,1)}, bf16[4,3,56,448]{3,2,1,0:T(8,128)(2,1)}, u32[]{:S(2)}, u32[]{:S(2)}) collective-permute-start(bf16[4,3,56,448]{3,2,1,0:T(8,128)(2,1)} %all-to-all-done.1), channel_id=1, source_target_pairs={{0,8},{1,9},{2,10},{3,11},{4,12},{5,13},{6,14},{7,15},{8,0},{9,1},... | collective-permute-start | bytes 1806344 | tf_op jit(solution)/shard_map/ppermute | solution.py:23
  130.9 15.4 %collective-permute-start.17 = (bf16[5,56,448]{2,1,0:T(8,128)(2,1)S(1)}, bf16[5,56,448]{2,1,0:T(8,128)(2,1)S(1)}, u32[]{:S(2)}, u32[]{:S(2)}) collective-permute-start(bf16[5,56,448]{2,1,0:T(8,128)(2,1)S(1)} %bitcast_dynamic-update-slice_fusion), channel_id=1, source_target_pairs={{0,8},{1,9},{2,10},{3,11},{4,12},{5,13},{6,14},{7,15},{8,0},{9,1},... | collective-permute-start | bytes 752648 | tf_op jit(solution)/shard_map/ppermute | solution.py:23
  148.2 24.2 %all-to-all-start.3 = ((bf16[4,2,5,56,448]{4,3,1,2,0:T(8,128)(2,1)}), bf16[4,2,5,56,448]{4,3,1,2,0:T(8,128)(2,1)S(1)}, u32[]{:S(2)}, u32[]{:S(2)}) async-start(bf16[4,2,5,56,448]{4,3,1,2,0:T(8,128)(2,1)} %broadcast_in_dim.31), calls=%async_computation.3 | async-start | bytes 4587520 | tf_op jit(solution)/shard_map/all_to_all | solution.py:111
  151.8 26.0 %collective-permute-start.18 = (bf16[456,768]{1,0:T(8,128)(2,1)}, bf16[456,768]{1,0:T(8,128)(2,1)}, u32[]{:S(2)}, u32[]{:S(2)}) collective-permute-start(bf16[456,768]{1,0:T(8,128)(2,1)} %collective-permute-done.5), channel_id=1, source_target_pairs={{0,224},{1,225},{2,226},{3,227},{4,228},{5,229},{6,230},{7,231},{8... | collective-permute-start | bytes 2101256 | tf_op jit(solution)/shard_map/ppermute | solution.py:23
  154.5 24.9 %collective-permute-start.20 = (bf16[456,768]{1,0:T(8,128)(2,1)}, bf16[456,768]{1,0:T(8,128)(2,1)}, u32[]{:S(2)}, u32[]{:S(2)}) collective-permute-start(bf16[456,768]{1,0:T(8,128)(2,1)} %collective-permute-done.19), channel_id=1, source_target_pairs={{0,32},{1,33},{2,34},{3,35},{4,36},{5,37},{6,38},{7,39},{8,40},{9,... | collective-permute-start | bytes 2101256 | tf_op jit(solution)/shard_map/ppermute | solution.py:23
  156.7 1.1 copy-start.2
  156.8 1.5 copy-start.6
  172.6 1.3 copy-start
  181.2 10.6 %collective-permute-start.21 = (f32[448,384]{1,0:T(8,128)S(1)}, f32[448,384]{1,0:T(8,128)S(1)}, u32[]{:S(2)}, u32[]{:S(2)}) collective-permute-start(f32[448,384]{1,0:T(8,128)S(1)} %slice.268), channel_id=1, source_target_pairs={{0,1},{1,0},{2,3},{3,2},{4,5},{5,4},{6,7},{7,6},{8,9},{9,8},{10,11... | collective-permute-start | bytes 2064392 | tf_op jit(solution)/shard_map/ppermute | solution.py:23

commit v5 on v1

v5 whole, which is shorter than its diff:
```python
import jax
import jax.numpy as jnp
from jax import lax
from jax.sharding import Mesh, PartitionSpec as P

NZ, NXL, NXH, NY, NC = 8, 2, 2, 4, 2
ALL = ("z", "xl", "xh", "y", "c")


def flat(z, xl, xh, y, c):
    return (((z % NZ * NXL + xl % NXL) * NXH + xh % NXH) * NY + y % NY) * NC + c % NC


def moved(array, where):
    pairs = []
    for z in range(NZ):
        for xl in range(NXL):
            for xh in range(NXH):
                for y in range(NY):
                    for c in range(NC):
                        target = where(z, xl, xh, y, c)
                        if target is not None:
                            pairs.append((flat(z, xl, xh, y, c), flat(*target)))
    return lax.ppermute(array, ALL, pairs)


def other_core(array):
    return moved(array, lambda z, xl, xh, y, c: (z, xl, xh, y, 1 - c))


def across(array):
    return moved(array, lambda z, xl, xh, y, c: (z, xl, 1 - xh, y, c))


def kind(xl, xh):
    return xl if xh == 0 else 1 - xl


def dot_nt(a, b):
    return lax.dot_general(a, b, (((1,), (1,)), ((), ())), preferred_element_type=jnp.float32)


def dot_nn(a, b):
    return lax.dot_general(a, b, (((1,), (0,)), ((), ())), preferred_element_type=jnp.float32)


def dot_tn(a, b):
    return lax.dot_general(a, b, (((0,), (0,)), ((), ())), preferred_element_type=jnp.float32)


def local(three_index, occ_energy, vir_energy):
    own = three_index[0]
    nvir, depth = own.shape
    share = nvir // NY
    c, xh, y = lax.axis_index("c"), lax.axis_index("xh"), lax.axis_index("y")

    high = lax.reduce_precision(occ_energy[0], 8, 7)
    rest = occ_energy[0] - high
    middle = lax.reduce_precision(rest, 8, 7)
    column = lax.broadcasted_iota(jnp.int32, (8, 4 * depth), 1)
    tail = jnp.where(column == 0, high, jnp.where(column == 1, middle, jnp.where(column == 2, rest - middle, 0.0)))
    there = across(own)
    beside = other_core(own)
    there_beside = other_core(there)

    def in_order(first, a, b):
        return jnp.where(first, jnp.concatenate([a, b], axis=1), jnp.concatenate([b, a], axis=1))

    mine = in_order(xh == 0, in_order(c == 0, own, beside), in_order(c == 0, there, there_beside))
    mine = jnp.concatenate([mine, tail.astype(jnp.bfloat16)], axis=0)

    step_one = moved(
        mine,
        lambda z, xl, xh, y, c: (z - 1, kind(xl, xh), xh, y, c) if c == 0 else (z + 1, xl, xh, y, c),
    )
    start, step_one = lax.optimization_barrier((mine, step_one))
    step_zero = moved(start, lambda z, xl, xh, y, c: (z, kind(xl, xh), xh, y, c) if c == 0 else None)
    step_two = moved(step_one, lambda z, xl, xh, y, c: (z - 1 if c == 0 else z + 1, xl, xh, y, c))
    swap_one = other_core(step_one)
    swap_two = moved(step_two, lambda z, xl, xh, y, c: (z, xl, xh, y, 1) if c == 0 else None)

    def numer(a, b):
        a, b = a[:nvir], b[:nvir]
        return dot_nt(a * jnp.bfloat16(2), b) - dot_nt(b, a)

    def packed(*values):
        return jnp.stack([value.reshape(NY, share, nvir) for value in values], axis=1)

    def over_y(parts):
        return jnp.sum(lax.all_to_all(parts, "y", 0, 0, tiled=True), axis=0)

    def energy(block):
        terms = block[nvir, :3].astype(jnp.float32)
        return terms[0] + terms[1] + terms[2]

    vir_rows = lax.dynamic_slice_in_dim(vir_energy, y * share, share)
    virs = vir_rows[:, None] + vir_energy[None, :]

    def amps(value, a, b):
        return (value / (virs - energy(a) - energy(b))).astype(jnp.bfloat16)

    def to_all(*parts):
        parts = jnp.stack(parts)
        whole = lax.all_to_all(jnp.broadcast_to(parts, (NY, *parts.shape)), "y", 0, 0, tiled=True)
        return [whole[:, n].reshape(nvir, nvir) for n in range(parts.shape[0])]

    rows_one = jnp.where(c == 0, mine, step_one)
    cols_one = jnp.where(c == 0, step_one, swap_one)
    parts = packed(numer(rows_one, cols_one))
    parts, swap_one = lax.optimization_barrier((parts, swap_one))
    early = over_y(parts)
    rows_two = jnp.where(c == 0, swap_one, swap_two)
    late = over_y(packed(numer(rows_two, step_two), numer(mine, step_zero)))

    turned_one = moved(step_one, lambda z, xl, xh, y, c: (z, kind(xl, xh), xh, y, 1) if c == 1 else None)
    turned_two = moved(step_two, lambda z, xl, xh, y, c: (z, kind(xl, xh), xh, y, 1) if c == 1 else None)
    step_three = moved(
        step_two,
        lambda z, xl, xh, y, c: (z - 1, xl, xh, y, c) if c == 0 else (z + 1, kind(xl, xh), xh, y, c),
    )
    turned_four = moved(step_three, lambda z, xl, xh, y, c: (z + 1, xl, xh, y, 1) if c == 1 else None)

    amps_one = amps(early[0], rows_one, cols_one)
    first = moved(
        amps_one,
        lambda z, xl, xh, y, c: (z + 1, kind(xl, xh), xh, y, 1) if c == 0 else (z - 1, xl, xh, y, 0),
    )
    second = moved(
        amps_one,
        lambda z, xl, xh, y, c: (z, xl, xh, y, 0) if c == 0 else (z + 1, kind(xl, xh), xh, y, 1),
    )
    first, second = to_all(first, second)

    amps_two = amps(late[0], rows_two, step_two)
    amps_zero = amps(late[1], mine, step_zero)
    third = moved(
        amps_two,
        lambda z, xl, xh, y, c: (z - 1, xl, xh, y, 0) if c == 0 else (z - 2, xl, xh, y, 1),
    )
    fourth = moved(amps_two, lambda z, xl, xh, y, c: (z + 2, kind(xl, xh), xh, y, 1) if c == 0 else None)
    fourth = jnp.where(c == 0, amps_zero, fourth)
    third, fourth, first, second = lax.optimization_barrier((third, fourth, first, second))
    third, fourth = to_all(third, fourth)

    def on_zero(parts, ahead, behind):
        return sum(dot_nn(part, block[:nvir]) for part, block in zip(parts, ahead))

    def on_one(parts, ahead, behind):
        return sum(dot_tn(part, block[:nvir]) for part, block in zip(parts, behind))

    total = lax.cond(c == 0, on_zero, on_one, (first, second), (step_two, step_one), (turned_one, turned_two))
    total = total + lax.cond(
        c == 0, on_zero, on_one, (third, fourth), (step_three, step_zero), (turned_four, step_three)
    )
    chunk = [total[:, n * depth : (n + 1) * depth] for n in range(NXH * NC)]
    sent = jnp.concatenate([jnp.where(c == 0, chunk[n + 1], chunk[n]) for n in (0, NC)], axis=1)
    kept = jnp.concatenate([jnp.where(c == 0, chunk[n], chunk[n + 1]) for n in (0, NC)], axis=1)
    kept = kept + other_core(sent)
    mine_now = jnp.where(xh == 0, kept[:, :depth], kept[:, depth:])
    theirs = jnp.where(xh == 0, kept[:, depth:], kept[:, :depth])
    return (mine_now + across(theirs))[None]


def solution(mesh):
    grid = Mesh(mesh.devices.reshape(NZ, NXL, NXH, NY, NC), ALL)
    return jax.shard_map(
        local,
        mesh=grid,
        in_specs=(P(("z", "xl"), None, ("xh", "y", "c")), P(("z", "xl")), P()),
        out_specs=P(("z", "xl"), None, ("xh", "y", "c")),
        check_vma=False,
    )
```

time: 219 us -> 215 us (0.982); the launches traced: 218 us -> 211 us
  blocking collectives: 65.4 us -> 0 us
  starting transfers between devices: 37.2 us -> 71.5 us
  between operations: 0.98 us -> 14.4 us
  matrix products: 11.9 us -> 22.8 us
  other arithmetic: 10.4 us -> 18 us
  waiting for transfers between devices: 80.8 us -> 76.7 us
  local copies, waits for them, and re-layouts: 11.2 us -> 7.95 us
    unnamed x1 -> x0, blocking collectives: 65.4 us -> none
    ppermute x13 -> x18, starting transfers between devices: 24 us -> 55.4 us  [moved(): return lax.ppermute(array, ALL, pairs)]
    dot_general x10 -> x6, matrix products: 5.43 us -> 12.2 us  [dot_nt(): lax.dot_general(a, b, (((1,), (1,)), ((), ())), preferred_element_type=jn...]
    dot_general x3 -> x4, matrix products: 3.85 us -> 10.6 us  [dot_tn(): lax.dot_general(a, b, (((0,), (0,)), ((), ())), preferred_element_type=jn...]
    ppermute x13 -> x18, waiting for transfers between devices: 69.8 us -> 63.6 us  [moved(): return lax.ppermute(array, ALL, pairs)]
    select_n x0 -> x9, other arithmetic: none -> 5.6 us  [the longest x1 1.93 us: local(): rows_one = jnp.where(c == 0, mine, step_one)]
    unnamed x25 -> x8, local copies, waits for them, and re-layouts: 5.96 us -> 0.72 us
    unnamed x5 -> x0, other arithmetic: 3.58 us -> none
  transfers between devices with their start and end apart: 15 -> 22, of which waited for: 11 -> 11; matrix products, arithmetic and copies ran while one was open for 8% -> 17% of each run, Pallas kernels for 0% -> 0%
where the time goes in v5:
time: 215 us; the launch traced here: 211 us
  waiting for transfers between devices  76.7 us (36%)
  starting transfers between devices  71.5 us (33%)
  matrix products  22.8 us (11%)
  other arithmetic  18 us (8%)
  between operations  14.4 us (7%)
  local copies, waits for them, and re-layouts  7.95 us (4%)
    ppermute x18, waiting for transfers between devices, moved(): return lax.ppermute(array, ALL, pairs)  63.6 us
    ppermute x18, starting transfers between devices, moved(): return lax.ppermute(array, ALL, pairs)  55.4 us
    dot_general x6, matrix products, dot_nt(): lax.dot_general(a, b, (((1,), (1,)), ((), ())), preferred_element_type=jn...  12.2 us
    dot_general x4, matrix products, dot_tn(): lax.dot_general(a, b, (((0,), (0,)), ((), ())), preferred_element_type=jn...  10.6 us
    all_to_all x2, starting transfers between devices, over_y(): return jnp.sum(lax.all_to_all(parts, 'y', 0, 0, tiled=True), axis=0)  8.41 us
    all_to_all x2, starting transfers between devices, to_all(): lax.all_to_all(jnp.broadcast_to(parts, (NY, *parts.shape)), 'y', 0, 0, ti...  7.74 us
    all_to_all x2, waiting for transfers between devices, over_y(): return jnp.sum(lax.all_to_all(parts, 'y', 0, 0, tiled=True), axis=0)  7.56 us
    all_to_all x2, waiting for transfers between devices, to_all(): lax.all_to_all(jnp.broadcast_to(parts, (NY, *parts.shape)), 'y', 0, 0, ti...  5.56 us
  transfers between devices with their start and end apart: 22, of which 11 were waited for; matrix products, arithmetic and copies ran while one was open for 17% of the time, Pallas kernels for 0%

profile of v5, /device:TPU:1, one launch (start us, length us, event | category | flops | bytes accessed | tf_op | source)
XLA Modules:
  0.0 211.4 jit_solution(12463321871686492788)
XLA Ops:
  0.0 3.6 %collective-permute-start.1 = (bf16[448,384]{1,0:T(8,128)(2,1)}, bf16[448,384]{1,0:T(8,128)(2,1)S(1)}, u32[]{:S(2)}, u32[]{:S(2)}) collective-permute-start(bf16[448,384]{1,0:T(8,128)(2,1)} %bitcast.63), channel_id=1, source_target_pairs={{0,8},{1,9},{2,10},{3,11},{4,12},{5,13},{6,14},{7,15},{8,0},{9,1},... | collective-permute-start | bytes 1032200 | tf_op jit(solution)/shard_map/ppermute | solution.py:24
  3.6 1.0 collective-permute-start
  7.5 3.2 %collective-permute-done.1 = bf16[448,384]{1,0:T(8,128)(2,1)S(1)} collective-permute-done((bf16[448,384]{1,0:T(8,128)(2,1)}, bf16[448,384]{1,0:T(8,128)(2,1)S(1)}, u32[]{:S(2)}, u32[]{:S(2)}) %collective-permute-start.1) | collective-permute-done | bytes 344096 | tf_op jit(solution)/shard_map/ppermute | solution.py:24
  10.6 2.2 %collective-permute-start.2 = (bf16[448,384]{1,0:T(8,128)(2,1)S(1)}, bf16[448,384]{1,0:T(8,128)(2,1)S(1)}, u32[]{:S(2)}, u32[]{:S(2)}) collective-permute-start(bf16[448,384]{1,0:T(8,128)(2,1)S(1)} %collective-permute-done.1), channel_id=1, source_target_pairs={{0,1},{1,0},{2,3},{3,2},{4,5},{5,4},{6,7},{7,6},{8,9},{9,8},{10,11... | collective-permute-start | bytes 1032200 | tf_op jit(solution)/shard_map/ppermute | solution.py:24
  12.8 1.2 select_convert_fusion
  14.1 1.3 maximum_select_fusion.1
  15.9 1.2 pad_maximum_fusion.1
  17.1 1.9 collective-permute-start.3
  19.0 20.2 %collective-permute-done.3 = bf16[456,1536]{1,0:T(8,128)(2,1)} collective-permute-done((bf16[456,1536]{1,0:T(8,128)(2,1)}, bf16[456,1536]{1,0:T(8,128)(2,1)}, u32[]{:S(2)}, u32[]{:S(2)}) %collective-permute-start.3) | collective-permute-done | bytes 1400864 | tf_op jit(solution)/shard_map/ppermute | solution.py:24
  39.2 4.1 %collective-permute-start.5 = (bf16[456,1536]{1,0:T(8,128)(2,1)}, bf16[456,1536]{1,0:T(8,128)(2,1)S(1)}, u32[]{:S(2)}, u32[]{:S(2)}) collective-permute-start(bf16[456,1536]{1,0:T(8,128)(2,1)} %collective-permute-done.3), channel_id=1, source_target_pairs={{0,1},{1,0},{2,3},{3,2},{4,5},{5,4},{6,7},{7,6},{8,9},{9,8},{10,11... | collective-permute-start | bytes 4202504 | tf_op jit(solution)/shard_map/ppermute | solution.py:24
  43.3 1.8 collective-permute-start.8
  45.2 13.0 %collective-permute-done.6 = bf16[456,1536]{1,0:T(8,128)(2,1)} collective-permute-done((bf16[456,1536]{1,0:T(8,128)(2,1)}, bf16[456,1536]{1,0:T(8,128)(2,1)}, u32[]{:S(2)}, u32[]{:S(2)}) %collective-permute-start.6) | collective-permute-done | bytes 1400864 | tf_op jit(solution)/shard_map/ppermute | solution.py:24
  58.2 1.3 collective-permute-start.7
  59.5 1.9 broadcast_select_fusion.2
  61.4 0.9 fusion.35
  63.0 1.9 fusion.18
  64.9 4.2 %all-to-all-start.1 = ((f32[4,1,112,448]{3,2,1,0:T(8,128)}), f32[4,1,112,448]{3,2,1,0:T(8,128)}, u32[]{:S(2)}, u32[]{:S(2)}) async-start(f32[4,1,112,448]{3,2,1,0:T(8,128)} %bitcast.61), calls=%async_computation.1 | async-start | bytes 1835008 | tf_op jit(solution)/shard_map/all_to_all | solution.py:90
  69.1 2.2 %fusion.27 = f32[448,448]{1,0:T(8,128)S(1)} fusion(bf16[448,1536]{1,0:T(8,128)(2,1)S(1)} %maximum_select_fusion, bf16[456,1536]{1,0:T(8,128)(2,1)} %collective-permute-done.8), kind=kOutput, calls=%fused_computation.33 | convolution fusion | flops 616562688 | bytes 3555328 | tf_op jit(solution)/shard_map/dot_general | solution.py:40
  71.3 2.2 %fusion.24 = f32[448,448]{1,0:T(8,128)S(1)} fusion(f32[448,448]{1,0:T(8,128)S(1)} %fusion.27, bf16[448,1536]{1,0:T(8,128)(2,1)S(1)} %maximum_select_fusion, bf16[456,1536]{1,0:T(8,128)(2,1)} %collective-permute-done.8), kind=kOutput, calls=%fused_computation.32 | convolution fusion | flops 617451520 | bytes 4358144 | tf_op jit(solution)/shard_map/dot_general | solution.py:40
  73.6 1.5 broadcast_select_fusion
  75.1 2.7 %fusion.30 = f32[448,448]{1,0:T(8,128)S(1)} fusion(bf16[456,1536]{1,0:T(8,128)(2,1)} %collective-permute-done.6, bf16[456,1536]{1,0:T(8,128)(2,1)S(1)} %broadcast_select_fusion), kind=kOutput, calls=%fused_computation.36 | convolution fusion | flops 616562688 | bytes 3555328 | tf_op jit(solution)/shard_map/dot_general | solution.py:40
  77.9 2.2 %fusion.21 = f32[448,448]{1,0:T(8,128)S(1)} fusion(f32[448,448]{1,0:T(8,128)S(1)} %fusion.30, bf16[456,1536]{1,0:T(8,128)(2,1)} %collective-permute-done.6, bf16[456,1536]{1,0:T(8,128)(2,1)S(1)} %broadcast_select_fusion), kind=kOutput, calls=%fused_computation.31 | convolution fusion | flops 617451520 | bytes 4472832 | tf_op jit(solution)/shard_map/dot_general | solution.py:40
  80.1 1.4 pad_maximum_fusion
  81.5 4.2 %all-to-all-start = ((f32[4,2,112,448]{3,2,1,0:T(8,128)}), f32[4,2,112,448]{3,2,1,0:T(8,128)S(1)}, u32[]{:S(2)}, u32[]{:S(2)}) async-start(f32[4,2,112,448]{3,2,1,0:T(8,128)} %pad_maximum_fusion), calls=%async_computation | async-start | bytes 3670016 | tf_op jit(solution)/shard_map/all_to_all | solution.py:90
  85.7 0.7 slice_convert_fusion
  86.4 0.6 fusion.60
  87.1 0.6 slice_convert_fusion.1
  87.7 0.7 fusion.59
  88.4 0.7 slice_convert_fusion.4
  89.0 0.6 fusion.64
  95.1 1.3 reduce_sum.19
  96.4 0.7 slice_convert_fusion.5
  97.1 0.6 fusion.63
  99.6 7.6 %all-to-all-done = f32[4,2,112,448]{3,2,1,0:T(8,128)S(1)} async-done(((f32[4,2,112,448]{3,2,1,0:T(8,128)}), f32[4,2,112,448]{3,2,1,0:T(8,128)S(1)}, u32[]{:S(2)}, u32[]{:S(2)}) %all-to-all-start) | async-done | bytes 1605664 | tf_op jit(solution)/shard_map/all_to_all | solution.py:90
  107.5 1.9 collective-permute-start.12
  109.5 2.6 %collective-permute-start.11 = (bf16[112,448]{1,0:T(8,128)(2,1)S(1)}, bf16[112,448]{1,0:T(8,128)(2,1)S(1)}, u32[]{:S(2)}, u32[]{:S(2)}) collective-permute-start(bf16[112,448]{1,0:T(8,128)(2,1)S(1)} %get-tuple-element.85), channel_id=1, source_target_pairs={{0,33},{1,224},{2,35},{3,226},{4,37},{5,228},{6,39},{7,230},{8,57}... | collective-permute-start | bytes 301064 | tf_op jit(solution)/shard_map/ppermute | solution.py:24
  112.1 2.8 %collective-permute-done.12 = bf16[112,448]{1,0:T(8,128)(2,1)S(1)} collective-permute-done((bf16[112,448]{1,0:T(8,128)(2,1)S(1)}, bf16[112,448]{1,0:T(8,128)(2,1)S(1)}, u32[]{:S(2)}, u32[]{:S(2)}) %collective-permute-start.12) | collective-permute-done | bytes 100384 | tf_op jit(solution)/shard_map/ppermute | solution.py:24
  114.9 0.6 collective-permute-done.11
  115.5 1.0 broadcast_in_dim.30
  116.6 3.5 %all-to-all-start.2 = ((bf16[4,2,112,448]{3,2,1,0:T(8,128)(2,1)}), bf16[4,2,112,448]{3,2,1,0:T(8,128)(2,1)S(1)}, u32[]{:S(2)}, u32[]{:S(2)}) async-start(bf16[4,2,112,448]{3,2,1,0:T(8,128)(2,1)} %broadcast_in_dim.30), calls=%async_computation.2 | async-start | bytes 1835008 | tf_op jit(solution)/shard_map/all_to_all | solution.py:104
  122.5 12.3 %collective-permute-start.4 = (bf16[456,1536]{1,0:T(8,128)(2,1)}, bf16[456,1536]{1,0:T(8,128)(2,1)}, u32[]{:S(2)}, u32[]{:S(2)}) collective-permute-start(bf16[456,1536]{1,0:T(8,128)(2,1)} %collective-permute-done.3), channel_id=1, source_target_pairs={{1,1},{3,3},{5,5},{7,7},{9,25},{11,27},{13,29},{15,31},{17,17},{19... | collective-permute-start | bytes 4202504 | tf_op jit(solution)/shard_map/ppermute | solution.py:24
  134.8 12.3 %collective-permute-start.13 = (bf16[456,1536]{1,0:T(8,128)(2,1)}, bf16[456,1536]{1,0:T(8,128)(2,1)}, u32[]{:S(2)}, u32[]{:S(2)}) collective-permute-start(bf16[456,1536]{1,0:T(8,128)(2,1)} %collective-permute-done.6), channel_id=1, source_target_pairs={{1,1},{3,3},{5,5},{7,7},{9,25},{11,27},{13,29},{15,31},{17,17},{19... | collective-permute-start | bytes 4202504 | tf_op jit(solution)/shard_map/ppermute | solution.py:24
  147.1 0.7 slice_convert_fusion.2
  147.7 1.5 collective-permute-start.10
  149.2 0.7 fusion.62
  151.8 1.9 collective-permute-start.15
  153.7 2.4 %collective-permute-start.9 = (bf16[112,448]{1,0:T(8,128)(2,1)S(1)}, bf16[112,448]{1,0:T(8,128)(2,1)S(1)}, u32[]{:S(2)}, u32[]{:S(2)}) collective-permute-start(bf16[112,448]{1,0:T(8,128)(2,1)S(1)} %get-tuple-element.86), channel_id=1, source_target_pairs={{0,224},{1,193},{2,226},{3,195},{4,228},{5,197},{6,230},{7,199},{8... | collective-permute-start | bytes 301064 | tf_op jit(solution)/shard_map/ppermute | solution.py:24
  156.2 1.0 collective-permute-done.10
  157.4 1.9 collective-permute-done.9
  159.3 1.0 broadcast_in_dim.31
  160.3 4.2 %all-to-all-start.3 = ((bf16[4,2,112,448]{3,2,1,0:T(8,128)(2,1)}), bf16[4,2,112,448]{3,2,1,0:T(8,128)(2,1)}, u32[]{:S(2)}, u32[]{:S(2)}) async-start(bf16[4,2,112,448]{3,2,1,0:T(8,128)(2,1)} %broadcast_in_dim.31), calls=%async_computation.3 | async-start | bytes 1835008 | tf_op jit(solution)/shard_map/all_to_all | solution.py:104
  164.6 4.5 %conditional.2 = (f32[448,1536]{1,0:T(8,128)S(1)}) conditional(s32[]{:T(128)} %convert_element_type.40, (bf16[456,1536]{1,0:T(8,128)(2,1)}, bf16[448,448]{1,0:T(8,128)(2,1)S(1)}, bf16[456,1536]{1,0:T(8,128)(2,1)}, bf16[448,448]{1,0:T(8,128)(2,1)S(1)}) %tuple.55, (bf16[456,1536]{1,0:T(8,128)(2,1)}, bf16[448,448]{1,0:T(8,128)(2,1)S(1)}, ...), branch_computations={%region_2.3_spmd, %region_3.4_spmd} | conditional | flops 1233813504 | bytes 11812872 | solution.py:151
  164.6 2.2 %fusion.1 = f32[448,1536]{1,0:T(8,128)S(1)} fusion(bf16[448,448]{1,0:T(8,128)(2,1)S(1)} %get-tuple-element.42, bf16[456,1536]{1,0:T(8,128)(2,1)} %get-tuple-element.44), kind=kOutput, calls=%fused_computation.2 | convolution fusion | flops 616562688 | bytes 4530176 | tf_op jit(solution)/shard_map/cond/branch_0_fun/dot_general | solution.py:48
  166.9 2.3 %convolution_add_fusion = f32[448,1536]{1,0:T(8,128)S(1)} fusion(f32[448,1536]{1,0:T(8,128)S(1)} %fusion.1, bf16[448,448]{1,0:T(8,128)(2,1)S(1)} %get-tuple-element.45, bf16[456,1536]{1,0:T(8,128)(2,1)} %get-tuple-element.46), kind=kOutput, calls=%fused_computation | convolution fusion | flops 617250816 | bytes 7282688 | tf_op jit(solution)/shard_map/cond/branch_0_fun/dot_general | solution.py:48
  169.1 5.6 %all-to-all-done.3 = bf16[4,2,112,448]{3,2,1,0:T(8,128)(2,1)} async-done(((bf16[4,2,112,448]{3,2,1,0:T(8,128)(2,1)}), bf16[4,2,112,448]{3,2,1,0:T(8,128)(2,1)}, u32[]{:S(2)}, u32[]{:S(2)}) %all-to-all-start.3) | async-done | bytes 802848 | tf_op jit(solution)/shard_map/all_to_all | solution.py:104
  174.7 1.2 fusion.57
  175.9 6.1 %conditional.3 = (f32[448,1536]{1,0:T(8,128)}) conditional(s32[]{:T(128)} %convert_element_type.40, (bf16[456,1536]{1,0:T(8,128)(2,1)}, bf16[448,448]{1,0:T(8,128)(2,1)S(1)}, bf16[456,1536]{1,0:T(8,128)(2,1)}, bf16[448,448]{1,0:T(8,128)(2,1)S(1)}) %tuple.57, (bf16[456,1536]{1,0:T(8,128)(2,1)}, bf16[448,448]{1,0:T(8,128)(2,1)S(1)}, ...), branch_computations={%region_4.5_spmd, %region_5.6_spmd} | conditional | flops 1233813504 | bytes 11812872 | solution.py:152
  176.0 2.2 %fusion.7 = f32[448,1536]{1,0:T(8,128)S(1)} fusion(bf16[448,448]{1,0:T(8,128)(2,1)S(1)} %get-tuple-element.51, bf16[456,1536]{1,0:T(8,128)(2,1)} %get-tuple-element.52), kind=kOutput, calls=%fused_computation.10 | convolution fusion | flops 616562688 | bytes 4530176 | tf_op jit(solution)/shard_map/cond/branch_0_fun/dot_general | solution.py:48
  178.2 3.8 %convolution_add_fusion.2 = f32[448,1536]{1,0:T(8,128)} fusion(f32[448,1536]{1,0:T(8,128)S(1)} %fusion.7, bf16[448,448]{1,0:T(8,128)(2,1)S(1)} %get-tuple-element.53, bf16[456,1536]{1,0:T(8,128)(2,1)} %get-tuple-element.54), kind=kOutput, calls=%fused_computation.8 | convolution fusion | flops 617250816 | bytes 7282688 | tf_op jit(solution)/shard_map/cond/branch_0_fun/dot_general | solution.py:48
  182.0 2.2 %add.125 = f32[448,1536]{1,0:T(8,128)S(1)} add(f32[448,1536]{1,0:T(8,128)S(1)} %get-tuple-element.107, f32[448,1536]{1,0:T(8,128)} %get-tuple-element.108) | non-fusion elementwise | flops 688128 | bytes 8257536 | tf_op jit(solution)/shard_map/add | solution.py:152
  184.6 4.6 %collective-permute-start.16 = (f32[448,768]{1,0:T(8,128)S(1)}, f32[448,768]{1,0:T(8,128)S(1)}, u32[]{:S(2)}, u32[]{:S(2)}) collective-permute-start(f32[448,768]{1,0:T(8,128)S(1)} %pad_maximum_fusion.2), channel_id=1, source_target_pairs={{0,1},{1,0},{2,3},{3,2},{4,5},{5,4},{6,7},{7,6},{8,9},{9,8},{10,11... | collective-permute-start | bytes 4128776 | tf_op jit(solution)/shard_map/ppermute | solution.py:24
  189.2 2.8 %collective-permute-done.16 = f32[448,768]{1,0:T(8,128)S(1)} collective-permute-done((f32[448,768]{1,0:T(8,128)S(1)}, f32[448,768]{1,0:T(8,128)S(1)}, u32[]{:S(2)}, u32[]{:S(2)}) %collective-permute-start.16) | collective-permute-done | bytes 1376288 | tf_op jit(solution)/shard_map/ppermute | solution.py:24
  192.2 18.1 %collective-permute-done.17 = f32[448,384]{1,0:T(8,128)S(1)} collective-permute-done((f32[448,384]{1,0:T(8,128)S(1)}, f32[448,384]{1,0:T(8,128)S(1)}, u32[]{:S(2)}, u32[]{:S(2)}) %collective-permute-start.17) | collective-permute-done | bytes 688160 | tf_op jit(solution)/shard_map/ppermute | solution.py:24
  210.4 1.0 add_bitcast_fusion
  (39 shorter events, 3.1 us)
Async XLA Ops:
  0.0 10.6 %collective-permute-start.1 = (bf16[448,384]{1,0:T(8,128)(2,1)}, bf16[448,384]{1,0:T(8,128)(2,1)S(1)}, u32[]{:S(2)}, u32[]{:S(2)}) collective-permute-start(bf16[448,384]{1,0:T(8,128)(2,1)} %bitcast.63), channel_id=1, source_target_pairs={{0,8},{1,9},{2,10},{3,11},{4,12},{5,13},{6,14},{7,15},{8,0},{9,1},... | collective-permute-start | bytes 1032200 | tf_op jit(solution)/shard_map/ppermute | solution.py:24
  3.6 10.5 %collective-permute-start = (bf16[448,384]{1,0:T(8,128)(2,1)}, bf16[448,384]{1,0:T(8,128)(2,1)S(1)}, u32[]{:S(2)}, u32[]{:S(2)}) collective-permute-start(bf16[448,384]{1,0:T(8,128)(2,1)} %bitcast.64), channel_id=1, source_target_pairs={{0,1},{1,0},{2,3},{3,2},{4,5},{5,4},{6,7},{7,6},{8,9},{9,8},{10,11... | collective-permute-start | bytes 1032200 | tf_op jit(solution)/shard_map/ppermute | solution.py:24
  10.6 4.8 %collective-permute-start.2 = (bf16[448,384]{1,0:T(8,128)(2,1)S(1)}, bf16[448,384]{1,0:T(8,128)(2,1)S(1)}, u32[]{:S(2)}, u32[]{:S(2)}) collective-permute-start(bf16[448,384]{1,0:T(8,128)(2,1)S(1)} %collective-permute-done.1), channel_id=1, source_target_pairs={{0,1},{1,0},{2,3},{3,2},{4,5},{5,4},{6,7},{7,6},{8,9},{9,8},{10,11... | collective-permute-start | bytes 1032200 | tf_op jit(solution)/shard_map/ppermute | solution.py:24
  15.9 29.2 %copy-start.3 = (f32[448]{0:T(512)S(1)}, f32[448]{0:T(512)}, u32[]{:S(2)}) copy-start(f32[448]{0:T(512)} %param.9) | copy-start | bytes 5380
  17.1 22.1 %collective-permute-start.3 = (bf16[456,1536]{1,0:T(8,128)(2,1)}, bf16[456,1536]{1,0:T(8,128)(2,1)}, u32[]{:S(2)}, u32[]{:S(2)}) collective-permute-start(bf16[456,1536]{1,0:T(8,128)(2,1)} %pad_maximum_fusion.1), channel_id=1, source_target_pairs={{0,224},{1,33},{2,226},{3,35},{4,228},{5,37},{6,230},{7,39},{8,248... | collective-permute-start | bytes 4202504 | tf_op jit(solution)/shard_map/ppermute | solution.py:24
  39.2 18.9 %collective-permute-start.6 = (bf16[456,1536]{1,0:T(8,128)(2,1)}, bf16[456,1536]{1,0:T(8,128)(2,1)}, u32[]{:S(2)}, u32[]{:S(2)}) collective-permute-start(bf16[456,1536]{1,0:T(8,128)(2,1)} %collective-permute-done.3), channel_id=1, source_target_pairs={{0,224},{1,33},{2,226},{3,35},{4,228},{5,37},{6,230},{7,39},{8,232... | collective-permute-start | bytes 4202504 | tf_op jit(solution)/shard_map/ppermute | solution.py:24
  39.2 20.2 %collective-permute-start.5 = (bf16[456,1536]{1,0:T(8,128)(2,1)}, bf16[456,1536]{1,0:T(8,128)(2,1)S(1)}, u32[]{:S(2)}, u32[]{:S(2)}) collective-permute-start(bf16[456,1536]{1,0:T(8,128)(2,1)} %collective-permute-done.3), channel_id=1, source_target_pairs={{0,1},{1,0},{2,3},{3,2},{4,5},{5,4},{6,7},{7,6},{8,9},{9,8},{10,11... | collective-permute-start | bytes 4202504 | tf_op jit(solution)/shard_map/ppermute | solution.py:24
  43.3 25.8 %collective-permute-start.8 = (bf16[456,1536]{1,0:T(8,128)(2,1)}, bf16[456,1536]{1,0:T(8,128)(2,1)}, u32[]{:S(2)}, u32[]{:S(2)}) collective-permute-start(bf16[456,1536]{1,0:T(8,128)(2,1)} %pad_maximum_fusion.1), channel_id=1, source_target_pairs={{0,0},{2,2},{4,4},{6,6},{8,24},{10,26},{12,28},{14,30},{16,16},{18... | collective-permute-start | bytes 4202504 | tf_op jit(solution)/shard_map/ppermute | solution.py:24
  58.2 15.4 %collective-permute-start.7 = (bf16[456,1536]{1,0:T(8,128)(2,1)}, bf16[456,1536]{1,0:T(8,128)(2,1)}, u32[]{:S(2)}, u32[]{:S(2)}) collective-permute-start(bf16[456,1536]{1,0:T(8,128)(2,1)} %collective-permute-done.6), channel_id=1, source_target_pairs={{0,1},{2,3},{4,5},{6,7},{8,9},{10,11},{12,13},{14,15},{16,17},{18,... | collective-permute-start | bytes 4202504 | tf_op jit(solution)/shard_map/ppermute | solution.py:24
  61.4 1.1 copy-start
  61.4 1.6 copy-start.1
  64.9 16.7 %all-to-all-start.1 = ((f32[4,1,112,448]{3,2,1,0:T(8,128)}), f32[4,1,112,448]{3,2,1,0:T(8,128)}, u32[]{:S(2)}, u32[]{:S(2)}) async-start(f32[4,1,112,448]{3,2,1,0:T(8,128)} %bitcast.61), calls=%async_computation.1 | async-start | bytes 1835008 | tf_op jit(solution)/shard_map/all_to_all | solution.py:90
  75.1 2.8 %copy-start.2 = (bf16[456,1536]{1,0:T(8,128)(2,1)}, bf16[456,1536]{1,0:T(8,128)(2,1)S(1)}, u32[]{:S(2)}) copy-start(bf16[456,1536]{1,0:T(8,128)(2,1)S(1)} %broadcast_select_fusion) | copy-start | bytes 4202500
  81.5 25.6 %all-to-all-start = ((f32[4,2,112,448]{3,2,1,0:T(8,128)}), f32[4,2,112,448]{3,2,1,0:T(8,128)S(1)}, u32[]{:S(2)}, u32[]{:S(2)}) async-start(f32[4,2,112,448]{3,2,1,0:T(8,128)} %pad_maximum_fusion), calls=%async_computation | async-start | bytes 3670016 | tf_op jit(solution)/shard_map/all_to_all | solution.py:90
  86.4 65.4 %collective-permute-start.14 = (bf16[456,1536]{1,0:T(8,128)(2,1)}, bf16[456,1536]{1,0:T(8,128)(2,1)}, u32[]{:S(2)}, u32[]{:S(2)}) collective-permute-start(bf16[456,1536]{1,0:T(8,128)(2,1)} %collective-permute-done.6), channel_id=1, source_target_pairs={{0,224},{1,33},{2,226},{3,35},{4,228},{5,37},{6,230},{7,39},{8,232... | collective-permute-start | bytes 4202504 | tf_op jit(solution)/shard_map/ppermute | solution.py:24
  107.5 7.3 %collective-permute-start.12 = (bf16[112,448]{1,0:T(8,128)(2,1)S(1)}, bf16[112,448]{1,0:T(8,128)(2,1)S(1)}, u32[]{:S(2)}, u32[]{:S(2)}) collective-permute-start(bf16[112,448]{1,0:T(8,128)(2,1)S(1)} %get-tuple-element.85), channel_id=1, source_target_pairs={{0,0},{1,33},{2,2},{3,35},{4,4},{5,37},{6,6},{7,39},{8,8},{9,57},{... | collective-permute-start | bytes 301064 | tf_op jit(solution)/shard_map/ppermute | solution.py:24
  109.5 6.0 %collective-permute-start.11 = (bf16[112,448]{1,0:T(8,128)(2,1)S(1)}, bf16[112,448]{1,0:T(8,128)(2,1)S(1)}, u32[]{:S(2)}, u32[]{:S(2)}) collective-permute-start(bf16[112,448]{1,0:T(8,128)(2,1)S(1)} %get-tuple-element.85), channel_id=1, source_target_pairs={{0,33},{1,224},{2,35},{3,226},{4,37},{5,228},{6,39},{7,230},{8,57}... | collective-permute-start | bytes 301064 | tf_op jit(solution)/shard_map/ppermute | solution.py:24
  116.6 40.7 %all-to-all-start.2 = ((bf16[4,2,112,448]{3,2,1,0:T(8,128)(2,1)}), bf16[4,2,112,448]{3,2,1,0:T(8,128)(2,1)S(1)}, u32[]{:S(2)}, u32[]{:S(2)}) async-start(bf16[4,2,112,448]{3,2,1,0:T(8,128)(2,1)} %broadcast_in_dim.30), calls=%async_computation.2 | async-start | bytes 1835008 | tf_op jit(solution)/shard_map/all_to_all | solution.py:104
  122.5 42.1 %collective-permute-start.4 = (bf16[456,1536]{1,0:T(8,128)(2,1)}, bf16[456,1536]{1,0:T(8,128)(2,1)}, u32[]{:S(2)}, u32[]{:S(2)}) collective-permute-start(bf16[456,1536]{1,0:T(8,128)(2,1)} %collective-permute-done.3), channel_id=1, source_target_pairs={{1,1},{3,3},{5,5},{7,7},{9,25},{11,27},{13,29},{15,31},{17,17},{19... | collective-permute-start | bytes 4202504 | tf_op jit(solution)/shard_map/ppermute | solution.py:24
  134.8 29.8 %collective-permute-start.13 = (bf16[456,1536]{1,0:T(8,128)(2,1)}, bf16[456,1536]{1,0:T(8,128)(2,1)}, u32[]{:S(2)}, u32[]{:S(2)}) collective-permute-start(bf16[456,1536]{1,0:T(8,128)(2,1)} %collective-permute-done.6), channel_id=1, source_target_pairs={{1,1},{3,3},{5,5},{7,7},{9,25},{11,27},{13,29},{15,31},{17,17},{19... | collective-permute-start | bytes 4202504 | tf_op jit(solution)/shard_map/ppermute | solution.py:24
  147.7 9.4 %collective-permute-start.10 = (bf16[112,448]{1,0:T(8,128)(2,1)S(1)}, bf16[112,448]{1,0:T(8,128)(2,1)S(1)}, u32[]{:S(2)}, u32[]{:S(2)}) collective-permute-start(bf16[112,448]{1,0:T(8,128)(2,1)S(1)} %get-tuple-element.86), channel_id=1, source_target_pairs={{0,65},{2,67},{4,69},{6,71},{8,89},{10,91},{12,93},{14,95},{16,81}... | collective-permute-start | bytes 301064 | tf_op jit(solution)/shard_map/ppermute | solution.py:24
  151.8 24.1 %collective-permute-start.15 = (bf16[456,1536]{1,0:T(8,128)(2,1)}, bf16[456,1536]{1,0:T(8,128)(2,1)}, u32[]{:S(2)}, u32[]{:S(2)}) collective-permute-start(bf16[456,1536]{1,0:T(8,128)(2,1)} %collective-permute-done.14), channel_id=1, source_target_pairs={{1,33},{3,35},{5,37},{7,39},{9,41},{11,43},{13,45},{15,47},{17,49}... | collective-permute-start | bytes 4202504 | tf_op jit(solution)/shard_map/ppermute | solution.py:24
  153.7 5.6 %collective-permute-start.9 = (bf16[112,448]{1,0:T(8,128)(2,1)S(1)}, bf16[112,448]{1,0:T(8,128)(2,1)S(1)}, u32[]{:S(2)}, u32[]{:S(2)}) collective-permute-start(bf16[112,448]{1,0:T(8,128)(2,1)S(1)} %get-tuple-element.86), channel_id=1, source_target_pairs={{0,224},{1,193},{2,226},{3,195},{4,228},{5,197},{6,230},{7,199},{8... | collective-permute-start | bytes 301064 | tf_op jit(solution)/shard_map/ppermute | solution.py:24
  160.3 14.4 %all-to-all-start.3 = ((bf16[4,2,112,448]{3,2,1,0:T(8,128)(2,1)}), bf16[4,2,112,448]{3,2,1,0:T(8,128)(2,1)}, u32[]{:S(2)}, u32[]{:S(2)}) async-start(bf16[4,2,112,448]{3,2,1,0:T(8,128)(2,1)} %broadcast_in_dim.31), calls=%async_computation.3 | async-start | bytes 1835008 | tf_op jit(solution)/shard_map/all_to_all | solution.py:104
  184.6 7.4 %collective-permute-start.16 = (f32[448,768]{1,0:T(8,128)S(1)}, f32[448,768]{1,0:T(8,128)S(1)}, u32[]{:S(2)}, u32[]{:S(2)}) collective-permute-start(f32[448,768]{1,0:T(8,128)S(1)} %pad_maximum_fusion.2), channel_id=1, source_target_pairs={{0,1},{1,0},{2,3},{3,2},{4,5},{5,4},{6,7},{7,6},{8,9},{9,8},{10,11... | collective-permute-start | bytes 4128776 | tf_op jit(solution)/shard_map/ppermute | solution.py:24
  192.1 18.2 %collective-permute-start.17 = (f32[448,384]{1,0:T(8,128)S(1)}, f32[448,384]{1,0:T(8,128)S(1)}, u32[]{:S(2)}, u32[]{:S(2)}) collective-permute-start(f32[448,384]{1,0:T(8,128)S(1)} %slice_select_fusion), channel_id=1, source_target_pairs={{0,8},{1,9},{2,10},{3,11},{4,12},{5,13},{6,14},{7,15},{8,0},{9,1},... | collective-permute-start | bytes 2064392 | tf_op jit(solution)/shard_map/ppermute | solution.py:24

commit v6 on v5

--- a/solution.py
+++ b/solution.py
@@ -74,10 +74,10 @@
         lambda z, xl, xh, y, c: (z - 1, kind(xl, xh), xh, y, c) if c == 0 else (z + 1, xl, xh, y, c),
     )
     start, step_one = lax.optimization_barrier((mine, step_one))
-    step_zero = moved(start, lambda z, xl, xh, y, c: (z, kind(xl, xh), xh, y, c) if c == 0 else None)
+    swap_one = other_core(step_one)
     step_two = moved(step_one, lambda z, xl, xh, y, c: (z - 1 if c == 0 else z + 1, xl, xh, y, c))
-    swap_one = other_core(step_one)
-    swap_two = moved(step_two, lambda z, xl, xh, y, c: (z, xl, xh, y, 1) if c == 0 else None)
+    beyond = moved(start, lambda z, xl, xh, y, c: (z, 1 - xl, xh, y, c) if (xh, c) == (1, 0) else None)
+    turned_one = moved(step_one, lambda z, xl, xh, y, c: (z, 1 - xl, xh, y, c) if (xh, c) == (1, 1) else None)
 
     def numer(a, b):
         a, b = a[:nvir], b[:nvir]
@@ -107,13 +107,16 @@
     rows_one = jnp.where(c == 0, mine, step_one)
     cols_one = jnp.where(c == 0, step_one, swap_one)
     parts = packed(numer(rows_one, cols_one))
-    parts, swap_one = lax.optimization_barrier((parts, swap_one))
     early = over_y(parts)
+    step_two, swap_one, beyond, anchor = lax.optimization_barrier((step_two, swap_one, beyond, parts[0, 0, 0, 0]))
+    swap_two = moved(step_two, lambda z, xl, xh, y, c: (z, xl, xh, y, 1) if c == 0 else None)
+    step_zero = jnp.where(xh == 0, mine, beyond)
     rows_two = jnp.where(c == 0, swap_one, swap_two)
     late = over_y(packed(numer(rows_two, step_two), numer(mine, step_zero)))
 
-    turned_one = moved(step_one, lambda z, xl, xh, y, c: (z, kind(xl, xh), xh, y, 1) if c == 1 else None)
-    turned_two = moved(step_two, lambda z, xl, xh, y, c: (z, kind(xl, xh), xh, y, 1) if c == 1 else None)
+    late = jnp.where(c < NC, late, anchor)
+
+    turned_two = moved(turned_one, lambda z, xl, xh, y, c: (z + 1, xl, xh, y, c) if (xh, c) == (1, 1) else None)
     step_three = moved(
         step_two,
         lambda z, xl, xh, y, c: (z - 1, xl, xh, y, c) if c == 0 else (z + 1, kind(xl, xh), xh, y, c),
@@ -127,8 +130,10 @@
     )
     second = moved(
         amps_one,
-        lambda z, xl, xh, y, c: (z, xl, xh, y, 0) if c == 0 else (z + 1, kind(xl, xh), xh, y, 1),
+        lambda z, xl, xh, y, c: (z + 1, kind(xl, xh), xh, y, 1) if c == 1 else None,
     )
+    second = jnp.where(c == 0, amps_one, second)
+    late, first, second, step_three = lax.optimization_barrier((late, first, second, step_three))
     first, second = to_all(first, second)
 
     amps_two = amps(late[0], rows_two, step_two)
@@ -142,15 +147,29 @@
     third, fourth, first, second = lax.optimization_barrier((third, fourth, first, second))
     third, fourth = to_all(third, fourth)
 
-    def on_zero(parts, ahead, behind):
-        return sum(dot_nn(part, block[:nvir]) for part, block in zip(parts, ahead))
+    def product(dot, *blocks):
+        return lambda parts: sum(dot(part, block[:nvir]) for part, block in zip(parts, blocks))
 
-    def on_one(parts, ahead, behind):
-        return sum(dot_tn(part, block[:nvir]) for part, block in zip(parts, behind))
-
-    total = lax.cond(c == 0, on_zero, on_one, (first, second), (step_two, step_one), (turned_one, turned_two))
-    total = total + lax.cond(
-        c == 0, on_zero, on_one, (third, fourth), (step_three, step_zero), (turned_four, step_three)
+    case = xh * NC + c
+    total = lax.switch(
+        case,
+        [
+            product(dot_nn, step_two, step_one),
+            product(dot_tn, step_one, step_two),
+            product(dot_nn, step_two, step_one),
+            product(dot_tn, turned_one, turned_two),
+        ],
+        (first, second),
+    )
+    total = total + lax.switch(
+        case,
+        [
+            product(dot_nn, step_three, mine),
+            product(dot_tn, turned_four, step_three),
+            product(dot_nn, step_three, beyond),
+            product(dot_tn, turned_four, step_three),
+        ],
+        (third, fourth),
     )
     chunk = [total[:, n * depth : (n + 1) * depth] for n in range(NXH * NC)]
     sent = jnp.concatenate([jnp.where(c == 0, chunk[n + 1], chunk[n]) for n in (0, NC)], axis=1)

time: 215 us -> 215 us (level); the launches traced: 211 us -> 214 us
  starting transfers between devices: 71.5 us -> 83.8 us
  waiting for transfers between devices: 76.7 us -> 65 us
  matrix products: 22.8 us -> 19.3 us
  other arithmetic: 18 us -> 21.2 us
    ppermute x18, starting transfers between devices: 55.4 us -> 66.7 us  [moved(): return lax.ppermute(array, ALL, pairs)]
    ppermute x18, waiting for transfers between devices: 63.6 us -> 55.5 us  [moved(): return lax.ppermute(array, ALL, pairs)]
    all_to_all x2, waiting for transfers between devices: 7.56 us -> 2.97 us  [over_y(): return jnp.sum(lax.all_to_all(parts, 'y', 0, 0, tiled=True), axis=0)]
    dot_general x6, matrix products: 12.2 us -> 8.54 us  [dot_nt(): lax.dot_general(a, b, (((1,), (1,)), ((), ())), preferred_element_type=jn...]
  transfers between devices with their start and end apart: 22 -> 22, of which waited for: 11 -> 9; matrix products, arithmetic and copies ran while one was open for 17% -> 18% of each run, Pallas kernels for 0% -> 0%
where the time goes in v6:
time: 215 us; the launch traced here: 214 us
  starting transfers between devices  83.8 us (39%)
  waiting for transfers between devices  65 us (30%)
  other arithmetic  21.2 us (10%)
  matrix products  19.3 us (9%)
  between operations  14.8 us (7%)
  local copies, waits for them, and re-layouts  10.1 us (5%)
    ppermute x18, starting transfers between devices, moved(): return lax.ppermute(array, ALL, pairs)  66.7 us
    ppermute x18, waiting for transfers between devices, moved(): return lax.ppermute(array, ALL, pairs)  55.5 us
    dot_general x4, matrix products, dot_tn(): lax.dot_general(a, b, (((0,), (0,)), ((), ())), preferred_element_type=jn...  10.7 us
    all_to_all x2, starting transfers between devices, over_y(): return jnp.sum(lax.all_to_all(parts, 'y', 0, 0, tiled=True), axis=0)  8.63 us
    dot_general x6, matrix products, dot_nt(): lax.dot_general(a, b, (((1,), (1,)), ((), ())), preferred_element_type=jn...  8.54 us
    all_to_all x2, starting transfers between devices, to_all(): lax.all_to_all(jnp.broadcast_to(parts, (NY, *parts.shape)), 'y', 0, 0, ti...  8.42 us
    all_to_all x2, waiting for transfers between devices, to_all(): lax.all_to_all(jnp.broadcast_to(parts, (NY, *parts.shape)), 'y', 0, 0, ti...  6.56 us
  transfers between devices with their start and end apart: 22, of which 9 were waited for; matrix products, arithmetic and copies ran while one was open for 18% of the time, Pallas kernels for 0%

profile of v6, /device:TPU:1, one launch (start us, length us, event | category | flops | bytes accessed | tf_op | source)
XLA Modules:
  0.0 214.1 jit_solution(1167288527142739323)
XLA Ops:
  0.0 3.6 %collective-permute-start.1 = (bf16[448,384]{1,0:T(8,128)(2,1)}, bf16[448,384]{1,0:T(8,128)(2,1)S(1)}, u32[]{:S(2)}, u32[]{:S(2)}) collective-permute-start(bf16[448,384]{1,0:T(8,128)(2,1)} %bitcast.80), channel_id=1, source_target_pairs={{0,8},{1,9},{2,10},{3,11},{4,12},{5,13},{6,14},{7,15},{8,0},{9,1},... | collective-permute-start | bytes 1032200 | tf_op jit(solution)/shard_map/ppermute | solution.py:24
  3.6 1.0 collective-permute-start
  7.5 3.1 %collective-permute-done.1 = bf16[448,384]{1,0:T(8,128)(2,1)S(1)} collective-permute-done((bf16[448,384]{1,0:T(8,128)(2,1)}, bf16[448,384]{1,0:T(8,128)(2,1)S(1)}, u32[]{:S(2)}, u32[]{:S(2)}) %collective-permute-start.1) | collective-permute-done | bytes 344096 | tf_op jit(solution)/shard_map/ppermute | solution.py:24
  10.6 2.2 %collective-permute-start.2 = (bf16[448,384]{1,0:T(8,128)(2,1)S(1)}, bf16[448,384]{1,0:T(8,128)(2,1)S(1)}, u32[]{:S(2)}, u32[]{:S(2)}) collective-permute-start(bf16[448,384]{1,0:T(8,128)(2,1)S(1)} %collective-permute-done.1), channel_id=1, source_target_pairs={{0,1},{1,0},{2,3},{3,2},{4,5},{5,4},{6,7},{7,6},{8,9},{9,8},{10,11... | collective-permute-start | bytes 1032200 | tf_op jit(solution)/shard_map/ppermute | solution.py:24
  12.8 1.3 select_convert_fusion
  14.1 1.2 maximum_select_fusion.1
  16.0 1.9 collective-permute-start.3
  17.9 19.9 %collective-permute-done.3 = bf16[456,1536]{1,0:T(8,128)(2,1)S(1)} collective-permute-done((bf16[456,1536]{1,0:T(8,128)(2,1)S(1)}, bf16[456,1536]{1,0:T(8,128)(2,1)S(1)}, u32[]{:S(2)}, u32[]{:S(2)}) %collective-permute-start.3) | collective-permute-done | bytes 1400864 | tf_op jit(solution)/shard_map/ppermute | solution.py:24
  38.3 0.7 fusion.70
  41.0 1.7 collective-permute-start.13
  42.8 1.7 collective-permute-start.6
  44.5 1.9 broadcast_select_fusion.3
  46.5 0.9 fusion.44
  47.4 0.9 fusion.29
  48.8 11.6 %collective-permute-done.4 = bf16[456,1536]{1,0:T(8,128)(2,1)} collective-permute-done((bf16[456,1536]{1,0:T(8,128)(2,1)S(1)}, bf16[456,1536]{1,0:T(8,128)(2,1)}, u32[]{:S(2)}, u32[]{:S(2)}) %collective-permute-start.4) | collective-permute-done | bytes 1400864 | tf_op jit(solution)/shard_map/ppermute | solution.py:24
  60.5 1.3 collective-permute-start.7
  61.9 4.2 %all-to-all-start.1 = ((f32[4,1,112,448]{3,2,1,0:T(8,128)}), f32[4,1,112,448]{3,2,1,0:T(8,128)}, u32[]{:S(2)}, u32[]{:S(2)}) async-start(f32[4,1,112,448]{3,2,1,0:T(8,128)} %bitcast.77), calls=%async_computation.1 | async-start | bytes 1835008 | tf_op jit(solution)/shard_map/all_to_all | solution.py:90
  66.1 0.6 fusion.74
  71.4 0.9 fusion.38
  72.5 0.9 fusion.35
  73.4 1.5 broadcast_select_fusion.1
  74.9 2.7 %fusion.41 = f32[448,448]{1,0:T(8,128)S(1)} fusion(bf16[456,1536]{1,0:T(8,128)(2,1)S(1)} %broadcast_select_fusion.1, bf16[456,1536]{1,0:T(8,128)(2,1)} %collective-permute-done.4), kind=kOutput, calls=%fused_computation.52 | convolution fusion | flops 616562688 | bytes 3555328 | tf_op jit(solution)/shard_map/dot_general | solution.py:40
  77.7 2.2 %fusion.32 = f32[448,448]{1,0:T(8,128)S(1)} fusion(f32[448,448]{1,0:T(8,128)S(1)} %fusion.41, bf16[456,1536]{1,0:T(8,128)(2,1)S(1)} %broadcast_select_fusion.1, bf16[456,1536]{1,0:T(8,128)(2,1)} %collective-permute-done.4), kind=kOutput, calls=%fused_computation.47 | convolution fusion | flops 617451520 | bytes 4472832 | tf_op jit(solution)/shard_map/dot_general | solution.py:40
  79.9 1.5 pad_maximum_fusion
  81.4 4.4 %all-to-all-start = ((f32[4,2,112,448]{3,2,1,0:T(8,128)}), f32[4,2,112,448]{3,2,1,0:T(8,128)}, u32[]{:S(2)}, u32[]{:S(2)}) async-start(f32[4,2,112,448]{3,2,1,0:T(8,128)} %pad_maximum_fusion), calls=%async_computation | async-start | bytes 3670016 | tf_op jit(solution)/shard_map/all_to_all | solution.py:90
  85.8 0.7 slice_convert_fusion
  86.5 0.7 slice_convert_fusion.5
  87.2 1.3 reduce_sum.19
  88.5 0.8 fusion.60
  89.2 1.9 collective-permute-start.9
  91.1 0.7 fusion.73
  93.8 1.8 collective-permute-start.14
  95.5 4.1 %collective-permute-start.8 = (bf16[112,448]{1,0:T(8,128)(2,1)}, bf16[112,448]{1,0:T(8,128)(2,1)S(1)}, u32[]{:S(2)}, u32[]{:S(2)}) collective-permute-start(bf16[112,448]{1,0:T(8,128)(2,1)} %fusion.60), channel_id=1, source_target_pairs={{0,33},{1,224},{2,35},{3,226},{4,37},{5,228},{6,39},{7,230},{8,57}... | collective-permute-start | bytes 301064 | tf_op jit(solution)/shard_map/ppermute | solution.py:24
  99.7 0.7 slice_convert_fusion.2
  100.4 3.0 %all-to-all-done = f32[4,2,112,448]{3,2,1,0:T(8,128)} async-done(((f32[4,2,112,448]{3,2,1,0:T(8,128)}), f32[4,2,112,448]{3,2,1,0:T(8,128)}, u32[]{:S(2)}, u32[]{:S(2)}) %all-to-all-start) | async-done | bytes 1605664 | tf_op jit(solution)/shard_map/all_to_all | solution.py:90
  103.4 1.8 reduce_sum.18
  105.1 1.4 broadcast_select_fusion.4
  106.6 1.0 broadcast_in_dim.35
  107.6 4.2 %all-to-all-start.2 = ((bf16[4,2,112,448]{3,2,1,0:T(8,128)(2,1)}), bf16[4,2,112,448]{3,2,1,0:T(8,128)(2,1)}, u32[]{:S(2)}, u32[]{:S(2)}) async-start(bf16[4,2,112,448]{3,2,1,0:T(8,128)(2,1)} %broadcast_in_dim.35), calls=%async_computation.2 | async-start | bytes 1835008 | tf_op jit(solution)/shard_map/all_to_all | solution.py:104
  111.8 0.7 fusion.72
  114.3 0.8 fusion.62
  115.1 1.3 collective-permute-start.12
  116.3 0.7 fusion.71
  118.9 1.9 collective-permute-start.15
  120.9 7.2 %collective-permute-start.11 = (bf16[112,448]{1,0:T(8,128)(2,1)}, bf16[112,448]{1,0:T(8,128)(2,1)S(1)}, u32[]{:S(2)}, u32[]{:S(2)}) collective-permute-start(bf16[112,448]{1,0:T(8,128)(2,1)} %fusion.62), channel_id=1, source_target_pairs={{0,224},{1,193},{2,226},{3,195},{4,228},{5,197},{6,230},{7,199},{8... | collective-permute-start | bytes 301064 | tf_op jit(solution)/shard_map/ppermute | solution.py:24
  128.0 1.3 collective-permute-done.12
  129.5 2.0 fusion.69
  131.5 1.2 collective-permute-done.11
  132.7 1.0 broadcast_in_dim.36
  133.7 4.2 %all-to-all-start.3 = ((bf16[4,2,112,448]{3,2,1,0:T(8,128)(2,1)}), bf16[4,2,112,448]{3,2,1,0:T(8,128)(2,1)}, u32[]{:S(2)}, u32[]{:S(2)}) async-start(bf16[4,2,112,448]{3,2,1,0:T(8,128)(2,1)} %broadcast_in_dim.36), calls=%async_computation.3 | async-start | bytes 1835008 | tf_op jit(solution)/shard_map/all_to_all | solution.py:104
  138.0 4.8 %conditional.2 = (f32[448,1536]{1,0:T(8,128)}) conditional(s32[]{:T(128)} %clamp.4, (bf16[456,1536]{1,0:T(8,128)(2,1)}, bf16[448,448]{1,0:T(8,128)(2,1)S(1)}, bf16[456,1536]{1,0:T(8,128)(2,1)S(1)}, bf16[448,448]{1,0:T(8,128)(2,1)}) %tuple.82, (bf16[456,1536]{1,0:T(8,128)(2,1)S(1)}, bf16[448,448]{1,0:T(8,128)(2,1)S(1)}, ...), branch_computations={%region_2.3_spmd, %region_3.4_spmd, %region_4.5_spmd, %region_5.6_... | conditional | flops 1233813504 | bytes 13475876 | solution.py:154
  138.0 0.9 fusion.4
  139.0 3.8 %convolution_add_fusion.1 = f32[448,1536]{1,0:T(8,128)} fusion(f32[448,1536]{1,0:T(8,128)S(1)} %fusion.4, bf16[448,448]{1,0:T(8,128)(2,1)S(1)} %copy-done.1, bf16[456,1536]{1,0:T(8,128)(2,1)} %get-tuple-element.86), kind=kOutput, calls=%fused_computation.4 | convolution fusion | flops 617250816 | bytes 7282688 | tf_op jit(solution)/shard_map/cond/branch_1_fun/dot_general | solution.py:48
  142.8 6.6 %all-to-all-done.3 = bf16[4,2,112,448]{3,2,1,0:T(8,128)(2,1)} async-done(((bf16[4,2,112,448]{3,2,1,0:T(8,128)(2,1)}), bf16[4,2,112,448]{3,2,1,0:T(8,128)(2,1)}, u32[]{:S(2)}, u32[]{:S(2)}) %all-to-all-start.3) | async-done | bytes 802848 | tf_op jit(solution)/shard_map/all_to_all | solution.py:104
  149.4 1.2 fusion.68
  150.6 6.1 %conditional.3 = (f32[448,1536]{1,0:T(8,128)}) conditional(s32[]{:T(128)} %clamp.4, (bf16[456,1536]{1,0:T(8,128)(2,1)}, bf16[448,448]{1,0:T(8,128)(2,1)S(1)}, bf16[448,448]{1,0:T(8,128)(2,1)S(1)}, bf16[448,1536]{1,0:T(8,128)(2,1)S(1)}) %tuple.78, (bf16[456,1536]{1,0:T(8,128)(2,1)}, bf16[448,448]{1,0:T(8,128)(2,1)S(1)}, ...), branch_computations={%region_6.7_spmd, %region_7.8_spmd, %region_8.9_spmd, %region_9.10... | conditional | flops 1233813504 | bytes 11812872 | solution.py:164
  150.6 2.2 %fusion.15 = f32[448,1536]{1,0:T(8,128)S(1)} fusion(bf16[448,448]{1,0:T(8,128)(2,1)S(1)} %get-tuple-element.99, bf16[456,1536]{1,0:T(8,128)(2,1)} %get-tuple-element.100), kind=kOutput, calls=%fused_computation.21 | convolution fusion | flops 616562688 | bytes 4530176 | tf_op jit(solution)/shard_map/cond/branch_1_fun/dot_general | solution.py:48
  152.9 3.8 %convolution_add_fusion.5 = f32[448,1536]{1,0:T(8,128)} fusion(f32[448,1536]{1,0:T(8,128)S(1)} %fusion.15, bf16[448,448]{1,0:T(8,128)(2,1)S(1)} %get-tuple-element.101, bf16[456,1536]{1,0:T(8,128)(2,1)} %get-tuple-element.102), kind=kOutput, calls=%fused_computation.19 | convolution fusion | flops 617250816 | bytes 7282688 | tf_op jit(solution)/shard_map/cond/branch_1_fun/dot_general | solution.py:48
  156.7 3.1 %add.141 = f32[448,1536]{1,0:T(8,128)S(1)} add(f32[448,1536]{1,0:T(8,128)} %get-tuple-element.169, f32[448,1536]{1,0:T(8,128)} %get-tuple-element.170) | non-fusion elementwise | flops 688128 | bytes 8257536 | tf_op jit(solution)/shard_map/add | solution.py:164
  160.1 2.0 collective-permute-start.16
  162.1 2.8 %collective-permute-done.16 = f32[448,768]{1,0:T(8,128)S(1)} collective-permute-done((f32[448,768]{1,0:T(8,128)S(1)}, f32[448,768]{1,0:T(8,128)S(1)}, u32[]{:S(2)}, u32[]{:S(2)}) %collective-permute-start.16) | collective-permute-done | bytes 1376288 | tf_op jit(solution)/shard_map/ppermute | solution.py:24
  165.0 32.6 %collective-permute-start.17 = (f32[448,384]{1,0:T(8,128)S(1)}, f32[448,384]{1,0:T(8,128)S(1)}, u32[]{:S(2)}, u32[]{:S(2)}) collective-permute-start(f32[448,384]{1,0:T(8,128)S(1)} %slice_select_fusion), channel_id=1, source_target_pairs={{0,8},{1,9},{2,10},{3,11},{4,12},{5,13},{6,14},{7,15},{8,0},{9,1},... | collective-permute-start | bytes 2064392 | tf_op jit(solution)/shard_map/ppermute | solution.py:24
  197.6 15.5 %collective-permute-done.17 = f32[448,384]{1,0:T(8,128)S(1)} collective-permute-done((f32[448,384]{1,0:T(8,128)S(1)}, f32[448,384]{1,0:T(8,128)S(1)}, u32[]{:S(2)}, u32[]{:S(2)}) %collective-permute-start.17) | collective-permute-done | bytes 688160 | tf_op jit(solution)/shard_map/ppermute | solution.py:24
  213.1 0.9 add_bitcast_fusion
  (50 shorter events, 3.9 us)
Async XLA Ops:
  0.0 10.6 %collective-permute-start.1 = (bf16[448,384]{1,0:T(8,128)(2,1)}, bf16[448,384]{1,0:T(8,128)(2,1)S(1)}, u32[]{:S(2)}, u32[]{:S(2)}) collective-permute-start(bf16[448,384]{1,0:T(8,128)(2,1)} %bitcast.80), channel_id=1, source_target_pairs={{0,8},{1,9},{2,10},{3,11},{4,12},{5,13},{6,14},{7,15},{8,0},{9,1},... | collective-permute-start | bytes 1032200 | tf_op jit(solution)/shard_map/ppermute | solution.py:24
  3.6 10.5 %collective-permute-start = (bf16[448,384]{1,0:T(8,128)(2,1)}, bf16[448,384]{1,0:T(8,128)(2,1)S(1)}, u32[]{:S(2)}, u32[]{:S(2)}) collective-permute-start(bf16[448,384]{1,0:T(8,128)(2,1)} %bitcast.81), channel_id=1, source_target_pairs={{0,1},{1,0},{2,3},{3,2},{4,5},{5,4},{6,7},{7,6},{8,9},{9,8},{10,11... | collective-permute-start | bytes 1032200 | tf_op jit(solution)/shard_map/ppermute | solution.py:24
  10.6 4.8 %collective-permute-start.2 = (bf16[448,384]{1,0:T(8,128)(2,1)S(1)}, bf16[448,384]{1,0:T(8,128)(2,1)S(1)}, u32[]{:S(2)}, u32[]{:S(2)}) collective-permute-start(bf16[448,384]{1,0:T(8,128)(2,1)S(1)} %collective-permute-done.1), channel_id=1, source_target_pairs={{0,1},{1,0},{2,3},{3,2},{4,5},{5,4},{6,7},{7,6},{8,9},{9,8},{10,11... | collective-permute-start | bytes 1032200 | tf_op jit(solution)/shard_map/ppermute | solution.py:24
  15.9 22.4 %copy-start.9 = (f32[448]{0:T(512)S(1)}, f32[448]{0:T(512)}, u32[]{:S(2)}) copy-start(f32[448]{0:T(512)} %param.13) | copy-start | bytes 5380
  16.0 21.9 %copy-start.5 = (bf16[456,1536]{1,0:T(8,128)(2,1)}, bf16[456,1536]{1,0:T(8,128)(2,1)S(1)}, u32[]{:S(2)}) copy-start(bf16[456,1536]{1,0:T(8,128)(2,1)S(1)} %pad_maximum_fusion.1) | copy-start | bytes 4202500
  16.0 21.8 %collective-permute-start.3 = (bf16[456,1536]{1,0:T(8,128)(2,1)S(1)}, bf16[456,1536]{1,0:T(8,128)(2,1)S(1)}, u32[]{:S(2)}, u32[]{:S(2)}) collective-permute-start(bf16[456,1536]{1,0:T(8,128)(2,1)S(1)} %pad_maximum_fusion.1), channel_id=1, source_target_pairs={{0,224},{1,33},{2,226},{3,35},{4,228},{5,37},{6,230},{7,39},{8,248... | collective-permute-start | bytes 4202504 | tf_op jit(solution)/shard_map/ppermute | solution.py:24
  37.8 6.7 %collective-permute-start.5 = (bf16[456,1536]{1,0:T(8,128)(2,1)S(1)}, bf16[456,1536]{1,0:T(8,128)(2,1)}, u32[]{:S(2)}, u32[]{:S(2)}) collective-permute-start(bf16[456,1536]{1,0:T(8,128)(2,1)S(1)} %collective-permute-done.3), channel_id=1, source_target_pairs={{0,1},{1,0},{2,3},{3,2},{4,5},{5,4},{6,7},{7,6},{8,9},{9,8},{10,11... | collective-permute-start | bytes 4202504 | tf_op jit(solution)/shard_map/ppermute | solution.py:24
  40.9 19.6 %collective-permute-start.4 = (bf16[456,1536]{1,0:T(8,128)(2,1)S(1)}, bf16[456,1536]{1,0:T(8,128)(2,1)}, u32[]{:S(2)}, u32[]{:S(2)}) collective-permute-start(bf16[456,1536]{1,0:T(8,128)(2,1)S(1)} %collective-permute-done.3), channel_id=1, source_target_pairs={{0,224},{1,33},{2,226},{3,35},{4,228},{5,37},{6,230},{7,39},{8,232... | collective-permute-start | bytes 4202504 | tf_op jit(solution)/shard_map/ppermute | solution.py:24
  41.0 52.7 %collective-permute-start.13 = (bf16[456,1536]{1,0:T(8,128)(2,1)S(1)}, bf16[456,1536]{1,0:T(8,128)(2,1)}, u32[]{:S(2)}, u32[]{:S(2)}) collective-permute-start(bf16[456,1536]{1,0:T(8,128)(2,1)S(1)} %collective-permute-done.3), channel_id=1, source_target_pairs={{9,25},{11,27},{13,29},{15,31},{25,9},{27,11},{29,13},{31,15},{41,... | collective-permute-start | bytes 4202504 | tf_op jit(solution)/shard_map/ppermute | solution.py:24
  42.8 17.7 %collective-permute-start.6 = (bf16[456,1536]{1,0:T(8,128)(2,1)}, bf16[456,1536]{1,0:T(8,128)(2,1)}, u32[]{:S(2)}, u32[]{:S(2)}) collective-permute-start(bf16[456,1536]{1,0:T(8,128)(2,1)} %copy-done.5), channel_id=1, source_target_pairs={{8,24},{10,26},{12,28},{14,30},{24,8},{26,10},{28,12},{30,14},{40,... | collective-permute-start | bytes 4202504 | tf_op jit(solution)/shard_map/ppermute | solution.py:24
  48.3 13.6 %copy-start.8 = (f32[448,448]{1,0:T(8,128)}, f32[448,448]{1,0:T(8,128)S(1)}, u32[]{:S(2)}) copy-start(f32[448,448]{1,0:T(8,128)S(1)} %fusion.29) | copy-start | bytes 2408452
  60.5 12.9 %collective-permute-start.7 = (bf16[456,1536]{1,0:T(8,128)(2,1)}, bf16[456,1536]{1,0:T(8,128)(2,1)}, u32[]{:S(2)}, u32[]{:S(2)}) collective-permute-start(bf16[456,1536]{1,0:T(8,128)(2,1)} %collective-permute-done.4), channel_id=1, source_target_pairs={{0,1},{2,3},{4,5},{6,7},{8,9},{10,11},{12,13},{14,15},{16,17},{18,... | collective-permute-start | bytes 4202504 | tf_op jit(solution)/shard_map/ppermute | solution.py:24
  61.8 44.7 %collective-permute-start.10 = (bf16[456,1536]{1,0:T(8,128)(2,1)}, bf16[456,1536]{1,0:T(8,128)(2,1)}, u32[]{:S(2)}, u32[]{:S(2)}) collective-permute-start(bf16[456,1536]{1,0:T(8,128)(2,1)} %collective-permute-done.4), channel_id=1, source_target_pairs={{0,224},{1,33},{2,226},{3,35},{4,228},{5,37},{6,230},{7,39},{8,232... | collective-permute-start | bytes 4202504 | tf_op jit(solution)/shard_map/ppermute | solution.py:24
  61.9 19.5 %all-to-all-start.1 = ((f32[4,1,112,448]{3,2,1,0:T(8,128)}), f32[4,1,112,448]{3,2,1,0:T(8,128)}, u32[]{:S(2)}, u32[]{:S(2)}) async-start(f32[4,1,112,448]{3,2,1,0:T(8,128)} %bitcast.77), calls=%async_computation.1 | async-start | bytes 1835008 | tf_op jit(solution)/shard_map/all_to_all | solution.py:90
  71.4 1.1 copy-start.7
  74.9 2.8 %copy-start.6 = (bf16[456,1536]{1,0:T(8,128)(2,1)}, bf16[456,1536]{1,0:T(8,128)(2,1)S(1)}, u32[]{:S(2)}) copy-start(bf16[456,1536]{1,0:T(8,128)(2,1)S(1)} %broadcast_select_fusion.1) | copy-start | bytes 4202500
  81.4 22.0 %all-to-all-start = ((f32[4,2,112,448]{3,2,1,0:T(8,128)}), f32[4,2,112,448]{3,2,1,0:T(8,128)}, u32[]{:S(2)}, u32[]{:S(2)}) async-start(f32[4,2,112,448]{3,2,1,0:T(8,128)} %pad_maximum_fusion), calls=%async_computation | async-start | bytes 3670016 | tf_op jit(solution)/shard_map/all_to_all | solution.py:90
  89.2 10.4 %collective-permute-start.9 = (bf16[112,448]{1,0:T(8,128)(2,1)}, bf16[112,448]{1,0:T(8,128)(2,1)S(1)}, u32[]{:S(2)}, u32[]{:S(2)}) collective-permute-start(bf16[112,448]{1,0:T(8,128)(2,1)} %fusion.60), channel_id=1, source_target_pairs={{1,33},{3,35},{5,37},{7,39},{9,57},{11,59},{13,61},{15,63},{17,49}... | collective-permute-start | bytes 301064 | tf_op jit(solution)/shard_map/ppermute | solution.py:24
  93.8 44.2 %collective-permute-start.14 = (bf16[456,1536]{1,0:T(8,128)(2,1)}, bf16[456,1536]{1,0:T(8,128)(2,1)}, u32[]{:S(2)}, u32[]{:S(2)}) collective-permute-start(bf16[456,1536]{1,0:T(8,128)(2,1)} %collective-permute-done.13), channel_id=1, source_target_pairs={{9,41},{11,43},{13,45},{15,47},{25,57},{27,59},{29,61},{31,63},{41... | collective-permute-start | bytes 4202504 | tf_op jit(solution)/shard_map/ppermute | solution.py:24
  95.5 11.0 %collective-permute-start.8 = (bf16[112,448]{1,0:T(8,128)(2,1)}, bf16[112,448]{1,0:T(8,128)(2,1)S(1)}, u32[]{:S(2)}, u32[]{:S(2)}) collective-permute-start(bf16[112,448]{1,0:T(8,128)(2,1)} %fusion.60), channel_id=1, source_target_pairs={{0,33},{1,224},{2,35},{3,226},{4,37},{5,228},{6,39},{7,230},{8,57}... | collective-permute-start | bytes 301064 | tf_op jit(solution)/shard_map/ppermute | solution.py:24
  106.6 7.7 %copy-start.4 = (f32[2,112,448]{2,1,0:T(8,128)S(1)}, f32[2,112,448]{2,1,0:T(8,128)}, u32[]{:S(2)}) copy-start(f32[2,112,448]{2,1,0:T(8,128)} %broadcast_select_fusion.4) | copy-start | bytes 1204228
  107.6 21.9 %all-to-all-start.2 = ((bf16[4,2,112,448]{3,2,1,0:T(8,128)(2,1)}), bf16[4,2,112,448]{3,2,1,0:T(8,128)(2,1)}, u32[]{:S(2)}, u32[]{:S(2)}) async-start(bf16[4,2,112,448]{3,2,1,0:T(8,128)(2,1)} %broadcast_in_dim.35), calls=%async_computation.2 | async-start | bytes 1835008 | tf_op jit(solution)/shard_map/all_to_all | solution.py:104
  115.1 14.3 %collective-permute-start.12 = (bf16[112,448]{1,0:T(8,128)(2,1)}, bf16[112,448]{1,0:T(8,128)(2,1)S(1)}, u32[]{:S(2)}, u32[]{:S(2)}) collective-permute-start(bf16[112,448]{1,0:T(8,128)(2,1)} %fusion.62), channel_id=1, source_target_pairs={{0,65},{2,67},{4,69},{6,71},{8,89},{10,91},{12,93},{14,95},{16,81}... | collective-permute-start | bytes 301064 | tf_op jit(solution)/shard_map/ppermute | solution.py:24
  118.9 31.7 %collective-permute-start.15 = (bf16[456,1536]{1,0:T(8,128)(2,1)}, bf16[456,1536]{1,0:T(8,128)(2,1)}, u32[]{:S(2)}, u32[]{:S(2)}) collective-permute-start(bf16[456,1536]{1,0:T(8,128)(2,1)} %collective-permute-done.10), channel_id=1, source_target_pairs={{1,33},{3,35},{5,37},{7,39},{9,41},{11,43},{13,45},{15,47},{17,49}... | collective-permute-start | bytes 4202504 | tf_op jit(solution)/shard_map/ppermute | solution.py:24
  120.9 11.8 %collective-permute-start.11 = (bf16[112,448]{1,0:T(8,128)(2,1)}, bf16[112,448]{1,0:T(8,128)(2,1)S(1)}, u32[]{:S(2)}, u32[]{:S(2)}) collective-permute-start(bf16[112,448]{1,0:T(8,128)(2,1)} %fusion.62), channel_id=1, source_target_pairs={{0,224},{1,193},{2,226},{3,195},{4,228},{5,197},{6,230},{7,199},{8... | collective-permute-start | bytes 301064 | tf_op jit(solution)/shard_map/ppermute | solution.py:24
  133.7 15.6 %all-to-all-start.3 = ((bf16[4,2,112,448]{3,2,1,0:T(8,128)(2,1)}), bf16[4,2,112,448]{3,2,1,0:T(8,128)(2,1)}, u32[]{:S(2)}, u32[]{:S(2)}) async-start(bf16[4,2,112,448]{3,2,1,0:T(8,128)(2,1)} %broadcast_in_dim.36), calls=%async_computation.3 | async-start | bytes 1835008 | tf_op jit(solution)/shard_map/all_to_all | solution.py:104
  138.0 1.0 copy-start.1
  160.1 4.8 %collective-permute-start.16 = (f32[448,768]{1,0:T(8,128)S(1)}, f32[448,768]{1,0:T(8,128)S(1)}, u32[]{:S(2)}, u32[]{:S(2)}) collective-permute-start(f32[448,768]{1,0:T(8,128)S(1)} %pad_maximum_fusion.2), channel_id=1, source_target_pairs={{0,1},{1,0},{2,3},{3,2},{4,5},{5,4},{6,7},{7,6},{8,9},{9,8},{10,11... | collective-permute-start | bytes 4128776 | tf_op jit(solution)/shard_map/ppermute | solution.py:24
  165.0 48.1 %collective-permute-start.17 = (f32[448,384]{1,0:T(8,128)S(1)}, f32[448,384]{1,0:T(8,128)S(1)}, u32[]{:S(2)}, u32[]{:S(2)}) collective-permute-start(f32[448,384]{1,0:T(8,128)S(1)} %slice_select_fusion), channel_id=1, source_target_pairs={{0,8},{1,9},{2,10},{3,11},{4,12},{5,13},{6,14},{7,15},{8,0},{9,1},... | collective-permute-start | bytes 2064392 | tf_op jit(solution)/shard_map/ppermute | solution.py:24

commit v7 on v6

--- a/solution.py
+++ b/solution.py
@@ -73,11 +73,10 @@
         mine,
         lambda z, xl, xh, y, c: (z - 1, kind(xl, xh), xh, y, c) if c == 0 else (z + 1, xl, xh, y, c),
     )
-    start, step_one = lax.optimization_barrier((mine, step_one))
+    beyond = moved(mine, lambda z, xl, xh, y, c: (z, 1 - xl, 1, y, c) if (xh, c) == (0, 0) else None)
     swap_one = other_core(step_one)
     step_two = moved(step_one, lambda z, xl, xh, y, c: (z - 1 if c == 0 else z + 1, xl, xh, y, c))
-    beyond = moved(start, lambda z, xl, xh, y, c: (z, 1 - xl, xh, y, c) if (xh, c) == (1, 0) else None)
-    turned_one = moved(step_one, lambda z, xl, xh, y, c: (z, 1 - xl, xh, y, c) if (xh, c) == (1, 1) else None)
+    turned_one = moved(step_one, lambda z, xl, xh, y, c: (z, 1 - xl, 1, y, c) if (xh, c) == (0, 1) else None)
 
     def numer(a, b):
         a, b = a[:nvir], b[:nvir]
@@ -106,14 +105,13 @@
 
     rows_one = jnp.where(c == 0, mine, step_one)
     cols_one = jnp.where(c == 0, step_one, swap_one)
-    parts = packed(numer(rows_one, cols_one))
+    step_zero = jnp.where(xh == 0, mine, beyond)
+    parts = lax.optimization_barrier(packed(numer(rows_one, cols_one), numer(mine, step_zero)))
     early = over_y(parts)
-    step_two, swap_one, beyond, anchor = lax.optimization_barrier((step_two, swap_one, beyond, parts[0, 0, 0, 0]))
+    step_two, swap_one, anchor = lax.optimization_barrier((step_two, swap_one, parts[0, 0, 0, 0]))
     swap_two = moved(step_two, lambda z, xl, xh, y, c: (z, xl, xh, y, 1) if c == 0 else None)
-    step_zero = jnp.where(xh == 0, mine, beyond)
     rows_two = jnp.where(c == 0, swap_one, swap_two)
-    late = over_y(packed(numer(rows_two, step_two), numer(mine, step_zero)))
-
+    late = over_y(packed(numer(rows_two, step_two)))
     late = jnp.where(c < NC, late, anchor)
 
     turned_two = moved(turned_one, lambda z, xl, xh, y, c: (z + 1, xl, xh, y, c) if (xh, c) == (1, 1) else None)
@@ -124,6 +122,7 @@
     turned_four = moved(step_three, lambda z, xl, xh, y, c: (z + 1, xl, xh, y, 1) if c == 1 else None)
 
     amps_one = amps(early[0], rows_one, cols_one)
+    amps_zero = amps(early[1], mine, step_zero)
     first = moved(
         amps_one,
         lambda z, xl, xh, y, c: (z + 1, kind(xl, xh), xh, y, 1) if c == 0 else (z - 1, xl, xh, y, 0),
@@ -133,11 +132,10 @@
         lambda z, xl, xh, y, c: (z + 1, kind(xl, xh), xh, y, 1) if c == 1 else None,
     )
     second = jnp.where(c == 0, amps_one, second)
-    late, first, second, step_three = lax.optimization_barrier((late, first, second, step_three))
+    late, first, second, step_three, amps_zero = lax.optimization_barrier((late, first, second, step_three, amps_zero))
     first, second = to_all(first, second)
 
     amps_two = amps(late[0], rows_two, step_two)
-    amps_zero = amps(late[1], mine, step_zero)
     third = moved(
         amps_two,
         lambda z, xl, xh, y, c: (z - 1, xl, xh, y, 0) if c == 0 else (z - 2, xl, xh, y, 1),

time: 215 us -> 200 us (0.930)
  starting transfers between devices: 83.8 us -> 47.9 us
  waiting for transfers between devices: 65 us -> 84.2 us
    ppermute x18, starting transfers between devices: 66.7 us -> 30.8 us  [moved(): return lax.ppermute(array, ALL, pairs)]
    all_to_all x2, waiting for transfers between devices: 2.97 us -> 16 us  [over_y(): return jnp.sum(lax.all_to_all(parts, 'y', 0, 0, tiled=True), axis=0)]
    all_to_all x2, waiting for transfers between devices: 6.56 us -> 10 us  [to_all(): lax.all_to_all(jnp.broadcast_to(parts, (NY, *parts.shape)), 'y', 0, 0, ti...]
    ppermute x18, waiting for transfers between devices: 55.5 us -> 58.2 us  [moved(): return lax.ppermute(array, ALL, pairs)]
  transfers between devices with their start and end apart: 22 -> 22, of which waited for: 9 -> 11; matrix products, arithmetic and copies ran while one was open for 18% -> 20% of each run, Pallas kernels for 0% -> 0%
where the time goes in v7:
time: 200 us; the launch traced here: 198 us
  waiting for transfers between devices  84.2 us (42%)
  starting transfers between devices  47.9 us (24%)
  other arithmetic  20.7 us (10%)
  matrix products  20.2 us (10%)
  between operations  14.7 us (7%)
  local copies, waits for them, and re-layouts  10.2 us (5%)
    ppermute x18, waiting for transfers between devices, moved(): return lax.ppermute(array, ALL, pairs)  58.2 us
    ppermute x18, starting transfers between devices, moved(): return lax.ppermute(array, ALL, pairs)  30.8 us
    all_to_all x2, waiting for transfers between devices, over_y(): return jnp.sum(lax.all_to_all(parts, 'y', 0, 0, tiled=True), axis=0)  16 us
    dot_general x4, matrix products, dot_tn(): lax.dot_general(a, b, (((0,), (0,)), ((), ())), preferred_element_type=jn...  10.8 us
    all_to_all x2, waiting for transfers between devices, to_all(): lax.all_to_all(jnp.broadcast_to(parts, (NY, *parts.shape)), 'y', 0, 0, ti...  10 us
    dot_general x6, matrix products, dot_nt(): lax.dot_general(a, b, (((1,), (1,)), ((), ())), preferred_element_type=jn...  9.46 us
    all_to_all x2, starting transfers between devices, over_y(): return jnp.sum(lax.all_to_all(parts, 'y', 0, 0, tiled=True), axis=0)  8.65 us
    all_to_all x2, starting transfers between devices, to_all(): lax.all_to_all(jnp.broadcast_to(parts, (NY, *parts.shape)), 'y', 0, 0, ti...  8.44 us
  transfers between devices with their start and end apart: 22, of which 11 were waited for; matrix products, arithmetic and copies ran while one was open for 20% of the time, Pallas kernels for 0%

profile of v7, /device:TPU:1, one launch (start us, length us, event | category | flops | bytes accessed | tf_op | source)
XLA Modules:
  0.0 198.0 jit_solution(2324503342395977388)
XLA Ops:
  0.0 3.6 %collective-permute-start.1 = (bf16[448,384]{1,0:T(8,128)(2,1)}, bf16[448,384]{1,0:T(8,128)(2,1)S(1)}, u32[]{:S(2)}, u32[]{:S(2)}) collective-permute-start(bf16[448,384]{1,0:T(8,128)(2,1)} %bitcast.87), channel_id=1, source_target_pairs={{0,8},{1,9},{2,10},{3,11},{4,12},{5,13},{6,14},{7,15},{8,0},{9,1},... | collective-permute-start | bytes 1032200 | tf_op jit(solution)/shard_map/ppermute | solution.py:24
  3.6 1.0 collective-permute-start
  7.5 3.1 %collective-permute-done.1 = bf16[448,384]{1,0:T(8,128)(2,1)S(1)} collective-permute-done((bf16[448,384]{1,0:T(8,128)(2,1)}, bf16[448,384]{1,0:T(8,128)(2,1)S(1)}, u32[]{:S(2)}, u32[]{:S(2)}) %collective-permute-start.1) | collective-permute-done | bytes 344096 | tf_op jit(solution)/shard_map/ppermute | solution.py:24
  10.6 2.2 %collective-permute-start.2 = (bf16[448,384]{1,0:T(8,128)(2,1)S(1)}, bf16[448,384]{1,0:T(8,128)(2,1)S(1)}, u32[]{:S(2)}, u32[]{:S(2)}) collective-permute-start(bf16[448,384]{1,0:T(8,128)(2,1)S(1)} %collective-permute-done.1), channel_id=1, source_target_pairs={{0,1},{1,0},{2,3},{3,2},{4,5},{5,4},{6,7},{7,6},{8,9},{9,8},{10,11... | collective-permute-start | bytes 1032200 | tf_op jit(solution)/shard_map/ppermute | solution.py:24
  12.8 1.3 select_convert_fusion
  14.1 1.2 maximum_select_fusion.1
  15.9 1.9 collective-permute-start.3
  17.9 0.7 collective-permute-start.6
  18.6 19.2 %collective-permute-done.3 = bf16[456,1536]{1,0:T(8,128)(2,1)S(1)} collective-permute-done((bf16[456,1536]{1,0:T(8,128)(2,1)S(1)}, bf16[456,1536]{1,0:T(8,128)(2,1)S(1)}, u32[]{:S(2)}, u32[]{:S(2)}) %collective-permute-start.3) | collective-permute-done | bytes 1400864 | tf_op jit(solution)/shard_map/ppermute | solution.py:24
  38.2 2.8 %collective-permute-done.5 = bf16[456,1536]{1,0:T(8,128)(2,1)S(1)} collective-permute-done((bf16[456,1536]{1,0:T(8,128)(2,1)S(1)}, bf16[456,1536]{1,0:T(8,128)(2,1)S(1)}, u32[]{:S(2)}, u32[]{:S(2)}) %collective-permute-start.5) | collective-permute-done | bytes 1400864 | tf_op jit(solution)/shard_map/ppermute | solution.py:24
  41.0 0.9 broadcast_select_fusion.3
  42.2 0.9 fusion.41
  43.1 0.9 fusion.44
  44.0 0.9 fusion.32
  44.9 0.9 fusion.29
  46.6 11.1 %collective-permute-done.4 = bf16[456,1536]{1,0:T(8,128)(2,1)} collective-permute-done((bf16[456,1536]{1,0:T(8,128)(2,1)S(1)}, bf16[456,1536]{1,0:T(8,128)(2,1)}, u32[]{:S(2)}, u32[]{:S(2)}) %collective-permute-start.4) | collective-permute-done | bytes 1400864 | tf_op jit(solution)/shard_map/ppermute | solution.py:24
  57.7 1.3 collective-permute-start.7
  61.6 6.4 %collective-permute-start.13 = (bf16[456,1536]{1,0:T(8,128)(2,1)S(1)}, bf16[456,1536]{1,0:T(8,128)(2,1)}, u32[]{:S(2)}, u32[]{:S(2)}) collective-permute-start(bf16[456,1536]{1,0:T(8,128)(2,1)S(1)} %collective-permute-done.3), channel_id=1, source_target_pairs={{1,25},{3,27},{5,29},{7,31},{17,9},{19,11},{21,13},{23,15},{33,57}... | collective-permute-start | bytes 4202504 | tf_op jit(solution)/shard_map/ppermute | solution.py:24
  68.0 4.4 %all-to-all-start.1 = ((f32[4,2,112,448]{3,2,1,0:T(8,128)}), f32[4,2,112,448]{3,2,1,0:T(8,128)}, u32[]{:S(2)}, u32[]{:S(2)}) async-start(f32[4,2,112,448]{3,2,1,0:T(8,128)} %copy-done.4), calls=%async_computation.1 | async-start | bytes 3670016 | tf_op jit(solution)/shard_map/all_to_all | solution.py:89
  72.5 0.7 slice_convert_fusion.4
  73.2 0.6 fusion.73
  76.3 0.7 fusion.74
  78.9 0.7 slice_convert_fusion.1
  79.6 0.7 fusion.72
  82.2 0.7 slice_convert_fusion.5
  82.9 11.6 %all-to-all-done.1 = f32[4,2,112,448]{3,2,1,0:T(8,128)} async-done(((f32[4,2,112,448]{3,2,1,0:T(8,128)}), f32[4,2,112,448]{3,2,1,0:T(8,128)}, u32[]{:S(2)}, u32[]{:S(2)}) %all-to-all-start.1) | async-done | bytes 1605664 | tf_op jit(solution)/shard_map/all_to_all | solution.py:89
  94.5 1.8 reduce_sum.19
  96.2 1.5 broadcast_select_fusion.1
  97.8 2.7 %fusion.38 = f32[448,448]{1,0:T(8,128)S(1)} fusion(bf16[456,1536]{1,0:T(8,128)(2,1)S(1)} %broadcast_select_fusion.1, bf16[456,1536]{1,0:T(8,128)(2,1)} %collective-permute-done.4), kind=kOutput, calls=%fused_computation.49 | convolution fusion | flops 616562688 | bytes 3555328 | tf_op jit(solution)/shard_map/dot_general | solution.py:40
  100.5 3.1 %fusion.35 = f32[448,448]{1,0:T(8,128)} fusion(f32[448,448]{1,0:T(8,128)S(1)} %fusion.38, bf16[456,1536]{1,0:T(8,128)(2,1)S(1)} %broadcast_select_fusion.1, bf16[456,1536]{1,0:T(8,128)(2,1)} %collective-permute-done.4), kind=kOutput, calls=%fused_computation.48 | convolution fusion | flops 617451520 | bytes 4472832 | tf_op jit(solution)/shard_map/dot_general | solution.py:40
  103.7 4.2 %all-to-all-start = ((f32[4,1,112,448]{3,2,1,0:T(8,128)}), f32[4,1,112,448]{3,2,1,0:T(8,128)}, u32[]{:S(2)}, u32[]{:S(2)}) async-start(f32[4,1,112,448]{3,2,1,0:T(8,128)} %bitcast.84), calls=%async_computation | async-start | bytes 1835008 | tf_op jit(solution)/shard_map/all_to_all | solution.py:89
  108.0 1.9 collective-permute-start.9
  112.4 1.8 collective-permute-start.14
  114.2 1.2 collective-permute-start.8
  115.4 0.7 broadcast_select_fusion.5
  116.0 0.7 slice_convert_fusion
  116.7 4.5 %all-to-all-done = f32[4,1,112,448]{3,2,1,0:T(8,128)} async-done(((f32[4,1,112,448]{3,2,1,0:T(8,128)}), f32[4,1,112,448]{3,2,1,0:T(8,128)}, u32[]{:S(2)}, u32[]{:S(2)}) %all-to-all-start) | async-done | bytes 802848 | tf_op jit(solution)/shard_map/all_to_all | solution.py:89
  121.2 1.3 reduce_sum.18
  122.5 0.7 select_bitcast_fusion
  123.2 1.0 pad_maximum_fusion.3
  124.1 1.0 broadcast_in_dim.35
  125.2 4.2 %all-to-all-start.2 = ((bf16[4,2,112,448]{3,2,1,0:T(8,128)(2,1)}), bf16[4,2,112,448]{3,2,1,0:T(8,128)(2,1)}, u32[]{:S(2)}, u32[]{:S(2)}) async-start(bf16[4,2,112,448]{3,2,1,0:T(8,128)(2,1)} %broadcast_in_dim.35), calls=%async_computation.2 | async-start | bytes 1835008 | tf_op jit(solution)/shard_map/all_to_all | solution.py:103
  131.8 0.8 fusion.60
  132.6 1.3 collective-permute-start.12
  133.9 1.9 collective-permute-start.15
  135.8 4.7 %collective-permute-start.11 = (bf16[112,448]{1,0:T(8,128)(2,1)}, bf16[112,448]{1,0:T(8,128)(2,1)}, u32[]{:S(2)}, u32[]{:S(2)}) collective-permute-start(bf16[112,448]{1,0:T(8,128)(2,1)} %fusion.60), channel_id=1, source_target_pairs={{0,224},{1,193},{2,226},{3,195},{4,228},{5,197},{6,230},{7,199},{8... | collective-permute-start | bytes 301064 | tf_op jit(solution)/shard_map/ppermute | solution.py:24
  140.5 1.0 collective-permute-done.12
  141.5 1.8 all-to-all-done.2
  143.3 2.0 %fusion.68 = (bf16[4,1,112,448]{3,2,1,0:T(8,128)(2,1)}, bf16[4,1,112,448]{3,2,1,0:T(8,128)(2,1)S(1)}) fusion(bf16[4,2,112,448]{3,2,1,0:T(8,128)(2,1)} %all-to-all-done.2), kind=kLoop, calls=%fused_computation.107 | loop fusion | bytes 1605632 | tf_op jit(solution)/shard_map/slice | solution.py:104
  145.3 0.9 pad_maximum_fusion.4
  146.2 1.1 broadcast_in_dim.36
  147.3 4.2 %all-to-all-start.3 = ((bf16[4,2,112,448]{3,2,1,0:T(8,128)(2,1)}), bf16[4,2,112,448]{3,2,1,0:T(8,128)(2,1)}, u32[]{:S(2)}, u32[]{:S(2)}) async-start(bf16[4,2,112,448]{3,2,1,0:T(8,128)(2,1)} %broadcast_in_dim.36), calls=%async_computation.3 | async-start | bytes 1835008 | tf_op jit(solution)/shard_map/all_to_all | solution.py:103
  151.5 4.8 %conditional.2 = (f32[448,1536]{1,0:T(8,128)}) conditional(s32[]{:T(128)} %clamp.4, (bf16[456,1536]{1,0:T(8,128)(2,1)}, bf16[448,448]{1,0:T(8,128)(2,1)S(1)}, bf16[456,1536]{1,0:T(8,128)(2,1)S(1)}, bf16[448,448]{1,0:T(8,128)(2,1)}) %tuple.82, (bf16[456,1536]{1,0:T(8,128)(2,1)S(1)}, bf16[448,448]{1,0:T(8,128)(2,1)S(1)}, ...), branch_computations={%region_2.3_spmd, %region_3.4_spmd, %region_4.5_spmd, %region_5.6_... | conditional | flops 1233813504 | bytes 13475876 | solution.py:152
  151.6 0.9 fusion.4
  152.6 3.8 %convolution_add_fusion.1 = f32[448,1536]{1,0:T(8,128)} fusion(f32[448,1536]{1,0:T(8,128)S(1)} %fusion.4, bf16[448,448]{1,0:T(8,128)(2,1)S(1)} %copy-done.1, bf16[456,1536]{1,0:T(8,128)(2,1)} %get-tuple-element.86), kind=kOutput, calls=%fused_computation.4 | convolution fusion | flops 617250816 | bytes 7282688 | tf_op jit(solution)/shard_map/cond/branch_1_fun/dot_general | solution.py:48
  156.4 8.2 %all-to-all-done.3 = bf16[4,2,112,448]{3,2,1,0:T(8,128)(2,1)} async-done(((bf16[4,2,112,448]{3,2,1,0:T(8,128)(2,1)}), bf16[4,2,112,448]{3,2,1,0:T(8,128)(2,1)}, u32[]{:S(2)}, u32[]{:S(2)}) %all-to-all-start.3) | async-done | bytes 802848 | tf_op jit(solution)/shard_map/all_to_all | solution.py:103
  164.6 1.2 fusion.67
  165.8 6.1 %conditional.3 = (f32[448,1536]{1,0:T(8,128)}) conditional(s32[]{:T(128)} %clamp.4, (bf16[456,1536]{1,0:T(8,128)(2,1)}, bf16[448,448]{1,0:T(8,128)(2,1)S(1)}, bf16[448,448]{1,0:T(8,128)(2,1)S(1)}, bf16[448,1536]{1,0:T(8,128)(2,1)S(1)}) %tuple.78, (bf16[456,1536]{1,0:T(8,128)(2,1)}, bf16[448,448]{1,0:T(8,128)(2,1)S(1)}, ...), branch_computations={%region_6.7_spmd, %region_7.8_spmd, %region_8.9_spmd, %region_9.10... | conditional | flops 1233813504 | bytes 17473572 | solution.py:162
  165.8 2.2 %fusion.15 = f32[448,1536]{1,0:T(8,128)S(1)} fusion(bf16[448,448]{1,0:T(8,128)(2,1)S(1)} %get-tuple-element.99, bf16[456,1536]{1,0:T(8,128)(2,1)} %get-tuple-element.100), kind=kOutput, calls=%fused_computation.21 | convolution fusion | flops 616562688 | bytes 4530176 | tf_op jit(solution)/shard_map/cond/branch_1_fun/dot_general | solution.py:48
  168.1 3.8 %convolution_add_fusion.5 = f32[448,1536]{1,0:T(8,128)} fusion(f32[448,1536]{1,0:T(8,128)S(1)} %fusion.15, bf16[448,448]{1,0:T(8,128)(2,1)S(1)} %get-tuple-element.101, bf16[456,1536]{1,0:T(8,128)(2,1)} %get-tuple-element.102), kind=kOutput, calls=%fused_computation.19 | convolution fusion | flops 617250816 | bytes 7282688 | tf_op jit(solution)/shard_map/cond/branch_1_fun/dot_general | solution.py:48
  171.9 3.1 %add.141 = f32[448,1536]{1,0:T(8,128)S(1)} add(f32[448,1536]{1,0:T(8,128)} %get-tuple-element.168, f32[448,1536]{1,0:T(8,128)} %get-tuple-element.169) | non-fusion elementwise | flops 688128 | bytes 8257536 | tf_op jit(solution)/shard_map/add | solution.py:162
  175.7 2.8 %collective-permute-done.16 = f32[448,768]{1,0:T(8,128)S(1)} collective-permute-done((f32[448,768]{1,0:T(8,128)S(1)}, f32[448,768]{1,0:T(8,128)S(1)}, u32[]{:S(2)}, u32[]{:S(2)}) %collective-permute-start.16) | collective-permute-done | bytes 1376288 | tf_op jit(solution)/shard_map/ppermute | solution.py:24
  178.8 18.2 %collective-permute-done.17 = f32[448,384]{1,0:T(8,128)S(1)} collective-permute-done((f32[448,384]{1,0:T(8,128)S(1)}, f32[448,384]{1,0:T(8,128)S(1)}, u32[]{:S(2)}, u32[]{:S(2)}) %collective-permute-start.17) | collective-permute-done | bytes 688160 | tf_op jit(solution)/shard_map/ppermute | solution.py:24
  197.0 0.9 add_bitcast_fusion
  (53 shorter events, 5.9 us)
Async XLA Ops:
  0.0 10.6 %collective-permute-start.1 = (bf16[448,384]{1,0:T(8,128)(2,1)}, bf16[448,384]{1,0:T(8,128)(2,1)S(1)}, u32[]{:S(2)}, u32[]{:S(2)}) collective-permute-start(bf16[448,384]{1,0:T(8,128)(2,1)} %bitcast.87), channel_id=1, source_target_pairs={{0,8},{1,9},{2,10},{3,11},{4,12},{5,13},{6,14},{7,15},{8,0},{9,1},... | collective-permute-start | bytes 1032200 | tf_op jit(solution)/shard_map/ppermute | solution.py:24
  3.6 10.5 %collective-permute-start = (bf16[448,384]{1,0:T(8,128)(2,1)}, bf16[448,384]{1,0:T(8,128)(2,1)S(1)}, u32[]{:S(2)}, u32[]{:S(2)}) collective-permute-start(bf16[448,384]{1,0:T(8,128)(2,1)} %bitcast.88), channel_id=1, source_target_pairs={{0,1},{1,0},{2,3},{3,2},{4,5},{5,4},{6,7},{7,6},{8,9},{9,8},{10,11... | collective-permute-start | bytes 1032200 | tf_op jit(solution)/shard_map/ppermute | solution.py:24
  10.6 4.7 %collective-permute-start.2 = (bf16[448,384]{1,0:T(8,128)(2,1)S(1)}, bf16[448,384]{1,0:T(8,128)(2,1)S(1)}, u32[]{:S(2)}, u32[]{:S(2)}) collective-permute-start(bf16[448,384]{1,0:T(8,128)(2,1)S(1)} %collective-permute-done.1), channel_id=1, source_target_pairs={{0,1},{1,0},{2,3},{3,2},{4,5},{5,4},{6,7},{7,6},{8,9},{9,8},{10,11... | collective-permute-start | bytes 1032200 | tf_op jit(solution)/shard_map/ppermute | solution.py:24
  15.9 21.8 %collective-permute-start.3 = (bf16[456,1536]{1,0:T(8,128)(2,1)S(1)}, bf16[456,1536]{1,0:T(8,128)(2,1)S(1)}, u32[]{:S(2)}, u32[]{:S(2)}) collective-permute-start(bf16[456,1536]{1,0:T(8,128)(2,1)S(1)} %pad_maximum_fusion.1), channel_id=1, source_target_pairs={{0,224},{1,33},{2,226},{3,35},{4,228},{5,37},{6,230},{7,39},{8,248... | collective-permute-start | bytes 4202504 | tf_op jit(solution)/shard_map/ppermute | solution.py:24
  17.9 20.3 %collective-permute-start.6 = (bf16[456,1536]{1,0:T(8,128)(2,1)S(1)}, bf16[456,1536]{1,0:T(8,128)(2,1)S(1)}, u32[]{:S(2)}, u32[]{:S(2)}) collective-permute-start(bf16[456,1536]{1,0:T(8,128)(2,1)S(1)} %pad_maximum_fusion.1), channel_id=1, source_target_pairs={{0,24},{2,26},{4,28},{6,30},{16,8},{18,10},{20,12},{22,14},{32,56}... | collective-permute-start | bytes 4202504 | tf_op jit(solution)/shard_map/ppermute | solution.py:24
  37.8 3.2 %collective-permute-start.5 = (bf16[456,1536]{1,0:T(8,128)(2,1)S(1)}, bf16[456,1536]{1,0:T(8,128)(2,1)S(1)}, u32[]{:S(2)}, u32[]{:S(2)}) collective-permute-start(bf16[456,1536]{1,0:T(8,128)(2,1)S(1)} %collective-permute-done.3), channel_id=1, source_target_pairs={{0,1},{1,0},{2,3},{3,2},{4,5},{5,4},{6,7},{7,6},{8,9},{9,8},{10,11... | collective-permute-start | bytes 4202504 | tf_op jit(solution)/shard_map/ppermute | solution.py:24
  38.2 19.5 %collective-permute-start.4 = (bf16[456,1536]{1,0:T(8,128)(2,1)S(1)}, bf16[456,1536]{1,0:T(8,128)(2,1)}, u32[]{:S(2)}, u32[]{:S(2)}) collective-permute-start(bf16[456,1536]{1,0:T(8,128)(2,1)S(1)} %collective-permute-done.3), channel_id=1, source_target_pairs={{0,224},{1,33},{2,226},{3,35},{4,228},{5,37},{6,230},{7,39},{8,232... | collective-permute-start | bytes 4202504 | tf_op jit(solution)/shard_map/ppermute | solution.py:24
  38.2 3.7 %copy-start.6 = (bf16[456,1536]{1,0:T(8,128)(2,1)}, bf16[456,1536]{1,0:T(8,128)(2,1)S(1)}, u32[]{:S(2)}) copy-start(bf16[456,1536]{1,0:T(8,128)(2,1)S(1)} %collective-permute-done.6) | copy-start | bytes 4202500
  41.0 1.2 copy-start.5
  42.2 1.8 copy-start.9
  42.2 2.7 %copy-start.10 = (bf16[456,1536]{1,0:T(8,128)(2,1)}, bf16[456,1536]{1,0:T(8,128)(2,1)S(1)}, u32[]{:S(2)}) copy-start(bf16[456,1536]{1,0:T(8,128)(2,1)S(1)} %get-tuple-element.141) | copy-start | bytes 4202500
  42.2 2.7 %copy-start.11 = (bf16[456,1536]{1,0:T(8,128)(2,1)}, bf16[456,1536]{1,0:T(8,128)(2,1)S(1)}, u32[]{:S(2)}) copy-start(bf16[456,1536]{1,0:T(8,128)(2,1)S(1)} %get-tuple-element.139) | copy-start | bytes 4202500
  45.8 15.7 %copy-start.12 = (f32[448]{0:T(512)S(1)}, f32[448]{0:T(512)}, u32[]{:S(2)}) copy-start(f32[448]{0:T(512)} %param.13) | copy-start | bytes 5380
  46.0 11.7 %copy-start.4 = (f32[4,2,112,448]{3,2,1,0:T(8,128)}, f32[4,2,112,448]{3,2,1,0:T(8,128)S(1)}, u32[]{:S(2)}) copy-start(f32[4,2,112,448]{3,2,1,0:T(8,128)S(1)} %pad_maximum_fusion) | copy-start | bytes 4816900
  57.7 38.6 %collective-permute-start.7 = (bf16[456,1536]{1,0:T(8,128)(2,1)}, bf16[456,1536]{1,0:T(8,128)(2,1)}, u32[]{:S(2)}, u32[]{:S(2)}) collective-permute-start(bf16[456,1536]{1,0:T(8,128)(2,1)} %collective-permute-done.4), channel_id=1, source_target_pairs={{0,1},{2,3},{4,5},{6,7},{8,9},{10,11},{12,13},{14,15},{16,17},{18,... | collective-permute-start | bytes 4202504 | tf_op jit(solution)/shard_map/ppermute | solution.py:24
  61.6 50.8 %collective-permute-start.13 = (bf16[456,1536]{1,0:T(8,128)(2,1)S(1)}, bf16[456,1536]{1,0:T(8,128)(2,1)}, u32[]{:S(2)}, u32[]{:S(2)}) collective-permute-start(bf16[456,1536]{1,0:T(8,128)(2,1)S(1)} %collective-permute-done.3), channel_id=1, source_target_pairs={{1,25},{3,27},{5,29},{7,31},{17,9},{19,11},{21,13},{23,15},{33,57}... | collective-permute-start | bytes 4202504 | tf_op jit(solution)/shard_map/ppermute | solution.py:24
  68.0 26.5 %all-to-all-start.1 = ((f32[4,2,112,448]{3,2,1,0:T(8,128)}), f32[4,2,112,448]{3,2,1,0:T(8,128)}, u32[]{:S(2)}, u32[]{:S(2)}) async-start(f32[4,2,112,448]{3,2,1,0:T(8,128)} %copy-done.4), calls=%async_computation.1 | async-start | bytes 3670016 | tf_op jit(solution)/shard_map/all_to_all | solution.py:89
  72.4 50.7 %collective-permute-start.10 = (bf16[456,1536]{1,0:T(8,128)(2,1)}, bf16[456,1536]{1,0:T(8,128)(2,1)}, u32[]{:S(2)}, u32[]{:S(2)}) collective-permute-start(bf16[456,1536]{1,0:T(8,128)(2,1)} %collective-permute-done.4), channel_id=1, source_target_pairs={{0,224},{1,33},{2,226},{3,35},{4,228},{5,37},{6,230},{7,39},{8,232... | collective-permute-start | bytes 4202504 | tf_op jit(solution)/shard_map/ppermute | solution.py:24
  97.7 2.8 %copy-start.8 = (bf16[456,1536]{1,0:T(8,128)(2,1)}, bf16[456,1536]{1,0:T(8,128)(2,1)S(1)}, u32[]{:S(2)}) copy-start(bf16[456,1536]{1,0:T(8,128)(2,1)S(1)} %broadcast_select_fusion.1) | copy-start | bytes 4202500
  103.7 17.5 %all-to-all-start = ((f32[4,1,112,448]{3,2,1,0:T(8,128)}), f32[4,1,112,448]{3,2,1,0:T(8,128)}, u32[]{:S(2)}, u32[]{:S(2)}) async-start(f32[4,1,112,448]{3,2,1,0:T(8,128)} %bitcast.84), calls=%async_computation | async-start | bytes 1835008 | tf_op jit(solution)/shard_map/all_to_all | solution.py:89
  108.0 7.3 %collective-permute-start.9 = (bf16[112,448]{1,0:T(8,128)(2,1)S(1)}, bf16[112,448]{1,0:T(8,128)(2,1)S(1)}, u32[]{:S(2)}, u32[]{:S(2)}) collective-permute-start(bf16[112,448]{1,0:T(8,128)(2,1)S(1)} %get-tuple-element.147), channel_id=1, source_target_pairs={{1,33},{3,35},{5,37},{7,39},{9,57},{11,59},{13,61},{15,63},{17,49}... | collective-permute-start | bytes 301064 | tf_op jit(solution)/shard_map/ppermute | solution.py:24
  112.4 39.1 %collective-permute-start.14 = (bf16[456,1536]{1,0:T(8,128)(2,1)}, bf16[456,1536]{1,0:T(8,128)(2,1)}, u32[]{:S(2)}, u32[]{:S(2)}) collective-permute-start(bf16[456,1536]{1,0:T(8,128)(2,1)} %collective-permute-done.13), channel_id=1, source_target_pairs={{9,41},{11,43},{13,45},{15,47},{25,57},{27,59},{29,61},{31,63},{41... | collective-permute-start | bytes 4202504 | tf_op jit(solution)/shard_map/ppermute | solution.py:24
  114.2 8.9 %collective-permute-start.8 = (bf16[112,448]{1,0:T(8,128)(2,1)S(1)}, bf16[112,448]{1,0:T(8,128)(2,1)}, u32[]{:S(2)}, u32[]{:S(2)}) collective-permute-start(bf16[112,448]{1,0:T(8,128)(2,1)S(1)} %get-tuple-element.147), channel_id=1, source_target_pairs={{0,33},{1,224},{2,35},{3,226},{4,37},{5,228},{6,39},{7,230},{8,57}... | collective-permute-start | bytes 301064 | tf_op jit(solution)/shard_map/ppermute | solution.py:24
  125.2 18.1 %all-to-all-start.2 = ((bf16[4,2,112,448]{3,2,1,0:T(8,128)(2,1)}), bf16[4,2,112,448]{3,2,1,0:T(8,128)(2,1)}, u32[]{:S(2)}, u32[]{:S(2)}) async-start(bf16[4,2,112,448]{3,2,1,0:T(8,128)(2,1)} %broadcast_in_dim.35), calls=%async_computation.2 | async-start | bytes 1835008 | tf_op jit(solution)/shard_map/all_to_all | solution.py:103
  132.6 8.9 %collective-permute-start.12 = (bf16[112,448]{1,0:T(8,128)(2,1)}, bf16[112,448]{1,0:T(8,128)(2,1)S(1)}, u32[]{:S(2)}, u32[]{:S(2)}) collective-permute-start(bf16[112,448]{1,0:T(8,128)(2,1)} %fusion.60), channel_id=1, source_target_pairs={{0,65},{2,67},{4,69},{6,71},{8,89},{10,91},{12,93},{14,95},{16,81}... | collective-permute-start | bytes 301064 | tf_op jit(solution)/shard_map/ppermute | solution.py:24
  133.9 31.9 %collective-permute-start.15 = (bf16[456,1536]{1,0:T(8,128)(2,1)}, bf16[456,1536]{1,0:T(8,128)(2,1)}, u32[]{:S(2)}, u32[]{:S(2)}) collective-permute-start(bf16[456,1536]{1,0:T(8,128)(2,1)} %collective-permute-done.10), channel_id=1, source_target_pairs={{1,33},{3,35},{5,37},{7,39},{9,41},{11,43},{13,45},{15,47},{17,49}... | collective-permute-start | bytes 4202504 | tf_op jit(solution)/shard_map/ppermute | solution.py:24
  135.8 9.5 %collective-permute-start.11 = (bf16[112,448]{1,0:T(8,128)(2,1)}, bf16[112,448]{1,0:T(8,128)(2,1)}, u32[]{:S(2)}, u32[]{:S(2)}) collective-permute-start(bf16[112,448]{1,0:T(8,128)(2,1)} %fusion.60), channel_id=1, source_target_pairs={{0,224},{1,193},{2,226},{3,195},{4,228},{5,197},{6,230},{7,199},{8... | collective-permute-start | bytes 301064 | tf_op jit(solution)/shard_map/ppermute | solution.py:24
  147.3 17.3 %all-to-all-start.3 = ((bf16[4,2,112,448]{3,2,1,0:T(8,128)(2,1)}), bf16[4,2,112,448]{3,2,1,0:T(8,128)(2,1)}, u32[]{:S(2)}, u32[]{:S(2)}) async-start(bf16[4,2,112,448]{3,2,1,0:T(8,128)(2,1)} %broadcast_in_dim.36), calls=%async_computation.3 | async-start | bytes 1835008 | tf_op jit(solution)/shard_map/all_to_all | solution.py:103
  151.6 1.0 copy-start.1
  175.3 3.2 %collective-permute-start.16 = (f32[448,768]{1,0:T(8,128)S(1)}, f32[448,768]{1,0:T(8,128)S(1)}, u32[]{:S(2)}, u32[]{:S(2)}) collective-permute-start(f32[448,768]{1,0:T(8,128)S(1)} %pad_maximum_fusion.2), channel_id=1, source_target_pairs={{0,1},{1,0},{2,3},{3,2},{4,5},{5,4},{6,7},{7,6},{8,9},{9,8},{10,11... | collective-permute-start | bytes 4128776 | tf_op jit(solution)/shard_map/ppermute | solution.py:24
  178.7 18.3 %collective-permute-start.17 = (f32[448,384]{1,0:T(8,128)S(1)}, f32[448,384]{1,0:T(8,128)S(1)}, u32[]{:S(2)}, u32[]{:S(2)}) collective-permute-start(f32[448,384]{1,0:T(8,128)S(1)} %slice_select_fusion), channel_id=1, source_target_pairs={{0,8},{1,9},{2,10},{3,11},{4,12},{5,13},{6,14},{7,15},{8,0},{9,1},... | collective-permute-start | bytes 2064392 | tf_op jit(solution)/shard_map/ppermute | solution.py:24

commit v8 on v7

--- a/solution.py
+++ b/solution.py
@@ -106,13 +106,11 @@
     rows_one = jnp.where(c == 0, mine, step_one)
     cols_one = jnp.where(c == 0, step_one, swap_one)
     step_zero = jnp.where(xh == 0, mine, beyond)
-    parts = lax.optimization_barrier(packed(numer(rows_one, cols_one), numer(mine, step_zero)))
-    early = over_y(parts)
-    step_two, swap_one, anchor = lax.optimization_barrier((step_two, swap_one, parts[0, 0, 0, 0]))
+    early = over_y(packed(numer(rows_one, cols_one), numer(mine, step_zero)))
+    step_two, swap_one, early = lax.optimization_barrier((step_two, swap_one, early))
     swap_two = moved(step_two, lambda z, xl, xh, y, c: (z, xl, xh, y, 1) if c == 0 else None)
     rows_two = jnp.where(c == 0, swap_one, swap_two)
     late = over_y(packed(numer(rows_two, step_two)))
-    late = jnp.where(c < NC, late, anchor)
 
     turned_two = moved(turned_one, lambda z, xl, xh, y, c: (z + 1, xl, xh, y, c) if (xh, c) == (1, 1) else None)
     step_three = moved(
@@ -145,37 +143,53 @@
     third, fourth, first, second = lax.optimization_barrier((third, fourth, first, second))
     third, fourth = to_all(third, fourth)
 
-    def product(dot, *blocks):
-        return lambda parts: sum(dot(part, block[:nvir]) for part, block in zip(parts, blocks))
+    width = NC * depth
+
+    def product(h, k, parts, blocks, half):
+        dot = dot_nn if k == 0 else dot_tn
+        at = (1 - h if half == 0 else h) * width
+        return sum(dot(part, block[:nvir, at : at + width]) for part, block in zip(parts, blocks))
+
+    def both_halves(h, k, *blocks):
+        return lambda parts: (product(h, k, parts, blocks, 0), product(h, k, parts, blocks, 1))
+
+    def one_half(h, k, half, *blocks):
+        def branch(parts, total):
+            total = total + product(h, k, parts, blocks, half)
+            cut = [total[:, n * depth : (n + 1) * depth] for n in range(NC)]
+            return cut[1 - k], cut[k]
+
+        return branch
 
     case = xh * NC + c
-    total = lax.switch(
+    halves = lax.switch(
         case,
         [
-            product(dot_nn, step_two, step_one),
-            product(dot_tn, step_one, step_two),
-            product(dot_nn, step_two, step_one),
-            product(dot_tn, turned_one, turned_two),
+            both_halves(0, 0, step_two, step_one),
+            both_halves(0, 1, step_one, step_two),
+            both_halves(1, 0, step_two, step_one),
+            both_halves(1, 1, turned_one, turned_two),
         ],
         (first, second),
     )
-    total = total + lax.switch(
-        case,
-        [
-            product(dot_nn, step_three, mine),
-            product(dot_tn, turned_four, step_three),
-            product(dot_nn, step_three, beyond),
-            product(dot_tn, turned_four, step_three),
-        ],
-        (third, fourth),
-    )
-    chunk = [total[:, n * depth : (n + 1) * depth] for n in range(NXH * NC)]
-    sent = jnp.concatenate([jnp.where(c == 0, chunk[n + 1], chunk[n]) for n in (0, NC)], axis=1)
-    kept = jnp.concatenate([jnp.where(c == 0, chunk[n], chunk[n + 1]) for n in (0, NC)], axis=1)
-    kept = kept + other_core(sent)
-    mine_now = jnp.where(xh == 0, kept[:, :depth], kept[:, depth:])
-    theirs = jnp.where(xh == 0, kept[:, depth:], kept[:, :depth])
-    return (mine_now + across(theirs))[None]
+
+    def finished(half, begun):
+        sent, kept = lax.switch(
+            case,
+            [
+                one_half(0, 0, half, step_three, mine),
+                one_half(0, 1, half, turned_four, step_three),
+                one_half(1, 0, half, step_three, beyond),
+                one_half(1, 1, half, turned_four, step_three),
+            ],
+            (third, fourth),
+            begun,
+        )
+        return kept + other_core(sent)
+
+    theirs, begun = lax.optimization_barrier((finished(0, halves[0]), halves[1]))
+    got = across(theirs)
+    return (finished(1, begun) + got)[None]
 
 
 def solution(mesh):

time: 200 us -> 201 us (level)
  starting transfers between devices: 47.9 us -> 64.8 us
  other arithmetic: 20.7 us -> 13.6 us
  waiting for transfers between devices: 84.2 us -> 77.8 us
    ppermute x18 -> x19, starting transfers between devices: 30.8 us -> 49.3 us  [moved(): return lax.ppermute(array, ALL, pairs)]
    ppermute x18 -> x19, waiting for transfers between devices: 58.2 us -> 46.1 us  [moved(): return lax.ppermute(array, ALL, pairs)]
    all_to_all x2, waiting for transfers between devices: 16 us -> 25.1 us  [over_y(): return jnp.sum(lax.all_to_all(parts, 'y', 0, 0, tiled=True), axis=0)]
    all_to_all x2, waiting for transfers between devices: 10 us -> 6.64 us  [to_all(): lax.all_to_all(jnp.broadcast_to(parts, (NY, *parts.shape)), 'y', 0, 0, ti...]
    dot_general x6, matrix products: 9.46 us -> 6.32 us  [dot_nt(): lax.dot_general(a, b, (((1,), (1,)), ((), ())), preferred_element_type=jn...]
    slice x2, local copies, waits for them, and re-layouts: 3.23 us -> 0.13 us  [to_all(): return [whole[:, n].reshape(nvir, nvir) for n in range(parts.shape[0])]]
    add x2 -> x1, other arithmetic: 3.22 us -> 0.92 us  [finished(): return kept + other_core(sent)]
    unnamed x16 -> x24, local copies, waits for them, and re-layouts: 0.3 us -> 2.38 us
  transfers between devices with their start and end apart: 22 -> 23, of which waited for: 11 -> 9; matrix products, arithmetic and copies ran while one was open for 20% -> 15% of each run, Pallas kernels for 0% -> 0%
where the time goes in v8:
time: 201 us; the launch traced here: 199 us
  waiting for transfers between devices  77.8 us (39%)
  starting transfers between devices  64.8 us (32%)
  matrix products  19 us (9%)
  between operations  14.9 us (7%)
  other arithmetic  13.6 us (7%)
  local copies, waits for them, and re-layouts  8.67 us (4%)
    ppermute x19, starting transfers between devices, moved(): return lax.ppermute(array, ALL, pairs)  49.3 us
    ppermute x19, waiting for transfers between devices, moved(): return lax.ppermute(array, ALL, pairs)  46.1 us
    all_to_all x2, waiting for transfers between devices, over_y(): return jnp.sum(lax.all_to_all(parts, 'y', 0, 0, tiled=True), axis=0)  25.1 us
    dot_general x8, matrix products, dot_tn(): lax.dot_general(a, b, (((0,), (0,)), ((), ())), preferred_element_type=jn...  12.7 us
    all_to_all x2, starting transfers between devices, over_y(): return jnp.sum(lax.all_to_all(parts, 'y', 0, 0, tiled=True), axis=0)  8.09 us
    all_to_all x2, starting transfers between devices, to_all(): lax.all_to_all(jnp.broadcast_to(parts, (NY, *parts.shape)), 'y', 0, 0, ti...  7.41 us
    all_to_all x2, waiting for transfers between devices, to_all(): lax.all_to_all(jnp.broadcast_to(parts, (NY, *parts.shape)), 'y', 0, 0, ti...  6.64 us
    dot_general x6, matrix products, dot_nt(): lax.dot_general(a, b, (((1,), (1,)), ((), ())), preferred_element_type=jn...  6.32 us
  transfers between devices with their start and end apart: 23, of which 9 were waited for; matrix products, arithmetic and copies ran while one was open for 15% of the time, Pallas kernels for 0%

profile of v8, /device:TPU:1, one launch (start us, length us, event | category | flops | bytes accessed | tf_op | source)
XLA Modules:
  0.0 199.1 jit_solution(17916817051878415288)
XLA Ops:
  0.0 3.6 %collective-permute-start.1 = (bf16[448,384]{1,0:T(8,128)(2,1)}, bf16[448,384]{1,0:T(8,128)(2,1)S(1)}, u32[]{:S(2)}, u32[]{:S(2)}) collective-permute-start(bf16[448,384]{1,0:T(8,128)(2,1)} %bitcast.104), channel_id=1, source_target_pairs={{0,8},{1,9},{2,10},{3,11},{4,12},{5,13},{6,14},{7,15},{8,0},{9,1},... | collective-permute-start | bytes 1032200 | tf_op jit(solution)/shard_map/ppermute | solution.py:24
  3.6 1.0 collective-permute-start
  7.5 3.1 %collective-permute-done.1 = bf16[448,384]{1,0:T(8,128)(2,1)S(1)} collective-permute-done((bf16[448,384]{1,0:T(8,128)(2,1)}, bf16[448,384]{1,0:T(8,128)(2,1)S(1)}, u32[]{:S(2)}, u32[]{:S(2)}) %collective-permute-start.1) | collective-permute-done | bytes 344096 | tf_op jit(solution)/shard_map/ppermute | solution.py:24
  10.6 2.2 %collective-permute-start.2 = (bf16[448,384]{1,0:T(8,128)(2,1)S(1)}, bf16[448,384]{1,0:T(8,128)(2,1)S(1)}, u32[]{:S(2)}, u32[]{:S(2)}) collective-permute-start(bf16[448,384]{1,0:T(8,128)(2,1)S(1)} %collective-permute-done.1), channel_id=1, source_target_pairs={{0,1},{1,0},{2,3},{3,2},{4,5},{5,4},{6,7},{7,6},{8,9},{9,8},{10,11... | collective-permute-start | bytes 1032200 | tf_op jit(solution)/shard_map/ppermute | solution.py:24
  12.8 1.3 select_convert_fusion
  14.1 1.2 maximum_select_fusion.1
  16.0 1.9 collective-permute-start.3
  17.9 0.7 collective-permute-start.6
  18.7 19.2 %collective-permute-done.3 = bf16[456,1536]{1,0:T(8,128)(2,1)S(1)} collective-permute-done((bf16[456,1536]{1,0:T(8,128)(2,1)S(1)}, bf16[456,1536]{1,0:T(8,128)(2,1)S(1)}, u32[]{:S(2)}, u32[]{:S(2)}) %collective-permute-start.3) | collective-permute-done | bytes 1400864 | tf_op jit(solution)/shard_map/ppermute | solution.py:24
  38.3 2.8 %collective-permute-done.5 = bf16[456,1536]{1,0:T(8,128)(2,1)S(1)} collective-permute-done((bf16[456,1536]{1,0:T(8,128)(2,1)S(1)}, bf16[456,1536]{1,0:T(8,128)(2,1)S(1)}, u32[]{:S(2)}, u32[]{:S(2)}) %collective-permute-start.5) | collective-permute-done | bytes 1400864 | tf_op jit(solution)/shard_map/ppermute | solution.py:24
  41.0 0.9 broadcast_select_fusion.3
  42.2 0.9 fusion.77
  43.7 0.9 fusion.62
  44.6 0.9 fusion.74
  45.6 0.9 fusion.65
  46.5 1.4 pad_maximum_fusion
  47.9 4.4 %all-to-all-start = ((f32[4,2,112,448]{3,2,1,0:T(8,128)}), f32[4,2,112,448]{3,2,1,0:T(8,128)}, u32[]{:S(2)}, u32[]{:S(2)}) async-start(f32[4,2,112,448]{3,2,1,0:T(8,128)} %pad_maximum_fusion), calls=%async_computation | async-start | bytes 3670016 | tf_op jit(solution)/shard_map/all_to_all | solution.py:89
  52.3 5.8 %collective-permute-start.13 = (bf16[456,1536]{1,0:T(8,128)(2,1)S(1)}, bf16[456,1536]{1,0:T(8,128)(2,1)}, u32[]{:S(2)}, u32[]{:S(2)}) collective-permute-start(bf16[456,1536]{1,0:T(8,128)(2,1)S(1)} %collective-permute-done.3), channel_id=1, source_target_pairs={{1,25},{3,27},{5,29},{7,31},{17,9},{19,11},{21,13},{23,15},{33,57}... | collective-permute-start | bytes 4202504 | tf_op jit(solution)/shard_map/ppermute | solution.py:24
  58.2 15.1 %all-to-all-done = f32[4,2,112,448]{3,2,1,0:T(8,128)} async-done(((f32[4,2,112,448]{3,2,1,0:T(8,128)}), f32[4,2,112,448]{3,2,1,0:T(8,128)}, u32[]{:S(2)}, u32[]{:S(2)}) %all-to-all-start) | async-done | bytes 1605664 | tf_op jit(solution)/shard_map/all_to_all | solution.py:89
  73.2 1.7 reduce_sum.20
  75.0 1.3 collective-permute-start.7
  78.9 0.7 slice_convert_fusion.4
  79.5 0.7 fusion.114
  82.2 0.6 slice_convert_fusion.3
  82.8 0.7 fusion.115
  85.4 0.7 slice_convert_fusion.1
  86.1 0.7 fusion.113
  88.8 1.8 collective-permute-start.14
  90.8 1.9 collective-permute-start.9
  92.7 6.8 %collective-permute-start.8 = (bf16[112,448]{1,0:T(8,128)(2,1)S(1)}, bf16[112,448]{1,0:T(8,128)(2,1)S(1)}, u32[]{:S(2)}, u32[]{:S(2)}) collective-permute-start(bf16[112,448]{1,0:T(8,128)(2,1)S(1)} %get-tuple-element.237), channel_id=1, source_target_pairs={{0,33},{1,224},{2,35},{3,226},{4,37},{5,228},{6,39},{7,230},{8,57}... | collective-permute-start | bytes 301064 | tf_op jit(solution)/shard_map/ppermute | solution.py:24
  99.5 1.5 broadcast_select_fusion.1
  101.0 0.9 fusion.71
  102.1 1.9 fusion.68
  104.0 3.7 %all-to-all-start.1 = ((f32[4,1,112,448]{3,2,1,0:T(8,128)}), f32[4,1,112,448]{3,2,1,0:T(8,128)S(1)}, u32[]{:S(2)}, u32[]{:S(2)}) async-start(f32[4,1,112,448]{3,2,1,0:T(8,128)} %bitcast.7), calls=%async_computation.1 | async-start | bytes 1835008 | tf_op jit(solution)/shard_map/all_to_all | solution.py:89
  107.7 0.6 fusion.111
  110.2 0.6 slice_convert_fusion
  110.8 10.0 %all-to-all-done.1 = f32[4,1,112,448]{3,2,1,0:T(8,128)S(1)} async-done(((f32[4,1,112,448]{3,2,1,0:T(8,128)}), f32[4,1,112,448]{3,2,1,0:T(8,128)S(1)}, u32[]{:S(2)}, u32[]{:S(2)}) %all-to-all-start.1) | async-done | bytes 802848 | tf_op jit(solution)/shard_map/all_to_all | solution.py:89
  120.9 1.0 broadcast_in_dim.30
  121.9 3.5 %all-to-all-start.2 = ((bf16[4,2,112,448]{3,2,1,0:T(8,128)(2,1)}), bf16[4,2,112,448]{3,2,1,0:T(8,128)(2,1)S(1)}, u32[]{:S(2)}, u32[]{:S(2)}) async-start(bf16[4,2,112,448]{3,2,1,0:T(8,128)(2,1)} %broadcast_in_dim.30), calls=%async_computation.2 | async-start | bytes 1835008 | tf_op jit(solution)/shard_map/all_to_all | solution.py:103
  125.5 0.6 fusion.110
  128.0 1.3 collective-permute-start.12
  129.3 1.9 collective-permute-start.15
  131.2 3.4 %collective-permute-start.11 = (bf16[112,448]{1,0:T(8,128)(2,1)S(1)}, bf16[112,448]{1,0:T(8,128)(2,1)S(1)}, u32[]{:S(2)}, u32[]{:S(2)}) collective-permute-start(bf16[112,448]{1,0:T(8,128)(2,1)S(1)} %fusion.93), channel_id=1, source_target_pairs={{0,224},{1,193},{2,226},{3,195},{4,228},{5,197},{6,230},{7,199},{8... | collective-permute-start | bytes 301064 | tf_op jit(solution)/shard_map/ppermute | solution.py:24
  134.6 3.6 %collective-permute-done.12 = bf16[112,448]{1,0:T(8,128)(2,1)S(1)} collective-permute-done((bf16[112,448]{1,0:T(8,128)(2,1)S(1)}, bf16[112,448]{1,0:T(8,128)(2,1)S(1)}, u32[]{:S(2)}, u32[]{:S(2)}) %collective-permute-start.12) | collective-permute-done | bytes 100384 | tf_op jit(solution)/shard_map/ppermute | solution.py:24
  138.4 1.0 broadcast_in_dim.31
  139.4 3.9 %all-to-all-start.3 = ((bf16[4,2,112,448]{3,2,1,0:T(8,128)(2,1)}), bf16[4,2,112,448]{3,2,1,0:T(8,128)(2,1)S(1)}, u32[]{:S(2)}, u32[]{:S(2)}) async-start(bf16[4,2,112,448]{3,2,1,0:T(8,128)(2,1)} %broadcast_in_dim.31), calls=%async_computation.3 | async-start | bytes 1835008 | tf_op jit(solution)/shard_map/all_to_all | solution.py:103
  143.3 5.7 %conditional.3 = (f32[448,768]{1,0:T(8,128)}, f32[448,768]{1,0:T(8,128)S(1)}) conditional(s32[]{:T(128)} %clamp.2, (bf16[456,1536]{1,0:T(8,128)(2,1)}, bf16[448,448]{1,0:T(8,128)(2,1)S(1)}, bf16[456,1536]{1,0:T(8,128)(2,1)}, bf16[448,448]{1,0:T(8,128)(2,1)S(1)}) %tuple.137, (bf16[456,1536]{1,0:T(8,128)(2,1)}, ...), branch_computations={%region_2.3_spmd, %region_3.4_spmd, %region_4.5_spmd, %region_5.6_... | conditional | flops 1233813504 | bytes 18333740 | solution.py:165
  143.3 1.8 fusion.7
  145.6 1.6 fusion.10
  147.3 1.7 convolution_add_fusion.3
  149.0 6.6 %all-to-all-done.3 = bf16[4,2,112,448]{3,2,1,0:T(8,128)(2,1)S(1)} async-done(((bf16[4,2,112,448]{3,2,1,0:T(8,128)(2,1)}), bf16[4,2,112,448]{3,2,1,0:T(8,128)(2,1)S(1)}, u32[]{:S(2)}, u32[]{:S(2)}) %all-to-all-start.3) | async-done | bytes 802848 | tf_op jit(solution)/shard_map/all_to_all | solution.py:103
  155.7 1.3 copy-done.1
  157.0 4.1 %conditional.4 = (f32[448,384]{1,0:T(8,128)S(1)}, f32[448,384]{1,0:T(8,128)S(1)}) conditional(s32[]{:T(128)} %clamp.2, (bf16[456,1536]{1,0:T(8,128)(2,1)}, bf16[448,448]{1,0:T(8,128)(2,1)S(1)}, bf16[448,1536]{1,0:T(8,128)(2,1)S(1)}, bf16[448,448]{1,0:T(8,128)(2,1)S(1)}, f32[448,768]{1,0:T(8,128)}) %tuple.132, ...), branch_computations={%region_6.7_spmd, %region_7.8_spmd, %region_8.9_spmd, %region_9.10... | conditional | flops 617250816 | bytes 10493968 | solution.py:177
  157.0 1.6 fusion.30
  158.6 2.1 %fusion.28 = f32[448,768]{1,0:T(8,128)S(1)} fusion(f32[448,768]{1,0:T(8,128)} %get-tuple-element.138, f32[448,768]{1,0:T(8,128)S(1)} %fusion.30, bf16[448,448]{1,0:T(8,128)(2,1)S(1)} %get-tuple-element.141, bf16[456,1536]{1,0:T(8,128)(2,1)} %get-tuple-element.142), kind=kOutput, calls=%fused_computation.38 | convolution fusion | flops 308969472 | bytes 5218304 | tf_op jit(solution)/shard_map/cond/branch_1_fun/dot_general | solution.py:48
  161.1 2.1 %collective-permute-start.16 = (f32[448,384]{1,0:T(8,128)S(1)}, f32[448,384]{1,0:T(8,128)S(1)}, u32[]{:S(2)}, u32[]{:S(2)}) collective-permute-start(f32[448,384]{1,0:T(8,128)S(1)} %get-tuple-element.207), channel_id=1, source_target_pairs={{0,1},{1,0},{2,3},{3,2},{4,5},{5,4},{6,7},{7,6},{8,9},{9,8},{10,11... | collective-permute-start | bytes 2064392 | tf_op jit(solution)/shard_map/ppermute | solution.py:24
  163.2 1.8 collective-permute-done.16
  165.0 0.9 add.189
  165.9 3.4 %conditional.5 = (f32[448,384]{1,0:T(8,128)S(1)}, f32[448,384]{1,0:T(8,128)S(1)}) conditional(s32[]{:T(128)} %clamp.2, (bf16[456,1536]{1,0:T(8,128)(2,1)}, bf16[448,448]{1,0:T(8,128)(2,1)S(1)}, bf16[448,1536]{1,0:T(8,128)(2,1)S(1)}, bf16[448,448]{1,0:T(8,128)(2,1)S(1)}, f32[448,768]{1,0:T(8,128)S(1)}) %tuple.133, ...), branch_computations={%region_10.11_spmd, %region_11.12_spmd, %region_12.13_spmd, %regio... | conditional | flops 617250816 | bytes 10493968 | solution.py:177
  165.9 1.6 fusion.46
  167.6 1.7 fusion.44
  169.4 13.0 %collective-permute-start.18 = (f32[448,384]{1,0:T(8,128)}, f32[448,384]{1,0:T(8,128)S(1)}, u32[]{:S(2)}, u32[]{:S(2)}) collective-permute-start(f32[448,384]{1,0:T(8,128)} %add.189), channel_id=1, source_target_pairs={{0,8},{1,9},{2,10},{3,11},{4,12},{5,13},{6,14},{7,15},{8,0},{9,1},... | collective-permute-start | bytes 2064392 | tf_op jit(solution)/shard_map/ppermute | solution.py:24
  182.4 15.7 %collective-permute-done.18 = f32[448,384]{1,0:T(8,128)S(1)} collective-permute-done((f32[448,384]{1,0:T(8,128)}, f32[448,384]{1,0:T(8,128)S(1)}, u32[]{:S(2)}, u32[]{:S(2)}) %collective-permute-start.18) | collective-permute-done | bytes 688160 | tf_op jit(solution)/shard_map/ppermute | solution.py:24
  198.1 0.9 add_bitcast_fusion
  (64 shorter events, 4.2 us)
Async XLA Ops:
  0.0 10.6 %collective-permute-start.1 = (bf16[448,384]{1,0:T(8,128)(2,1)}, bf16[448,384]{1,0:T(8,128)(2,1)S(1)}, u32[]{:S(2)}, u32[]{:S(2)}) collective-permute-start(bf16[448,384]{1,0:T(8,128)(2,1)} %bitcast.104), channel_id=1, source_target_pairs={{0,8},{1,9},{2,10},{3,11},{4,12},{5,13},{6,14},{7,15},{8,0},{9,1},... | collective-permute-start | bytes 1032200 | tf_op jit(solution)/shard_map/ppermute | solution.py:24
  3.6 10.5 %collective-permute-start = (bf16[448,384]{1,0:T(8,128)(2,1)}, bf16[448,384]{1,0:T(8,128)(2,1)S(1)}, u32[]{:S(2)}, u32[]{:S(2)}) collective-permute-start(bf16[448,384]{1,0:T(8,128)(2,1)} %bitcast.105), channel_id=1, source_target_pairs={{0,1},{1,0},{2,3},{3,2},{4,5},{5,4},{6,7},{7,6},{8,9},{9,8},{10,11... | collective-permute-start | bytes 1032200 | tf_op jit(solution)/shard_map/ppermute | solution.py:24
  10.6 4.8 %collective-permute-start.2 = (bf16[448,384]{1,0:T(8,128)(2,1)S(1)}, bf16[448,384]{1,0:T(8,128)(2,1)S(1)}, u32[]{:S(2)}, u32[]{:S(2)}) collective-permute-start(bf16[448,384]{1,0:T(8,128)(2,1)S(1)} %collective-permute-done.1), channel_id=1, source_target_pairs={{0,1},{1,0},{2,3},{3,2},{4,5},{5,4},{6,7},{7,6},{8,9},{9,8},{10,11... | collective-permute-start | bytes 1032200 | tf_op jit(solution)/shard_map/ppermute | solution.py:24
  15.9 29.7 %copy-start = (bf16[448,1536]{1,0:T(8,128)(2,1)}, bf16[448,1536]{1,0:T(8,128)(2,1)S(1)}, u32[]{:S(2)}) copy-start(bf16[448,1536]{1,0:T(8,128)(2,1)S(1)} %maximum_select_fusion) | copy-start | bytes 4128772
  16.0 21.8 %collective-permute-start.3 = (bf16[456,1536]{1,0:T(8,128)(2,1)S(1)}, bf16[456,1536]{1,0:T(8,128)(2,1)S(1)}, u32[]{:S(2)}, u32[]{:S(2)}) collective-permute-start(bf16[456,1536]{1,0:T(8,128)(2,1)S(1)} %pad_maximum_fusion.1), channel_id=1, source_target_pairs={{0,224},{1,33},{2,226},{3,35},{4,228},{5,37},{6,230},{7,39},{8,248... | collective-permute-start | bytes 4202504 | tf_op jit(solution)/shard_map/ppermute | solution.py:24
  17.9 20.3 %collective-permute-start.6 = (bf16[456,1536]{1,0:T(8,128)(2,1)S(1)}, bf16[456,1536]{1,0:T(8,128)(2,1)S(1)}, u32[]{:S(2)}, u32[]{:S(2)}) collective-permute-start(bf16[456,1536]{1,0:T(8,128)(2,1)S(1)} %pad_maximum_fusion.1), channel_id=1, source_target_pairs={{0,24},{2,26},{4,28},{6,30},{16,8},{18,10},{20,12},{22,14},{32,56}... | collective-permute-start | bytes 4202504 | tf_op jit(solution)/shard_map/ppermute | solution.py:24
  37.8 14.5 %copy-start.3 = (bf16[456,1536]{1,0:T(8,128)(2,1)}, bf16[456,1536]{1,0:T(8,128)(2,1)S(1)}, u32[]{:S(2)}) copy-start(bf16[456,1536]{1,0:T(8,128)(2,1)S(1)} %collective-permute-done.3) | copy-start | bytes 4202500
  37.8 3.2 %collective-permute-start.5 = (bf16[456,1536]{1,0:T(8,128)(2,1)S(1)}, bf16[456,1536]{1,0:T(8,128)(2,1)S(1)}, u32[]{:S(2)}, u32[]{:S(2)}) collective-permute-start(bf16[456,1536]{1,0:T(8,128)(2,1)S(1)} %collective-permute-done.3), channel_id=1, source_target_pairs={{0,1},{1,0},{2,3},{3,2},{4,5},{5,4},{6,7},{7,6},{8,9},{9,8},{10,11... | collective-permute-start | bytes 4202504 | tf_op jit(solution)/shard_map/ppermute | solution.py:24
  38.2 36.8 %collective-permute-start.4 = (bf16[456,1536]{1,0:T(8,128)(2,1)S(1)}, bf16[456,1536]{1,0:T(8,128)(2,1)S(1)}, u32[]{:S(2)}, u32[]{:S(2)}) collective-permute-start(bf16[456,1536]{1,0:T(8,128)(2,1)S(1)} %collective-permute-done.3), channel_id=1, source_target_pairs={{0,224},{1,33},{2,226},{3,35},{4,228},{5,37},{6,230},{7,39},{8,232... | collective-permute-start | bytes 4202504 | tf_op jit(solution)/shard_map/ppermute | solution.py:24
  38.2 3.7 %copy-start.9 = (bf16[456,1536]{1,0:T(8,128)(2,1)}, bf16[456,1536]{1,0:T(8,128)(2,1)S(1)}, u32[]{:S(2)}) copy-start(bf16[456,1536]{1,0:T(8,128)(2,1)S(1)} %collective-permute-done.6) | copy-start | bytes 4202500
  41.0 1.2 copy-start.8
  42.2 1.1 copy-start.12
  42.2 1.5 copy-start.13
  42.2 3.3 %copy-start.11 = (bf16[456,1536]{1,0:T(8,128)(2,1)}, bf16[456,1536]{1,0:T(8,128)(2,1)S(1)}, u32[]{:S(2)}) copy-start(bf16[456,1536]{1,0:T(8,128)(2,1)S(1)} %get-tuple-element.230) | copy-start | bytes 4202500
  47.9 25.4 %all-to-all-start = ((f32[4,2,112,448]{3,2,1,0:T(8,128)}), f32[4,2,112,448]{3,2,1,0:T(8,128)}, u32[]{:S(2)}, u32[]{:S(2)}) async-start(f32[4,2,112,448]{3,2,1,0:T(8,128)} %pad_maximum_fusion), calls=%async_computation | async-start | bytes 3670016 | tf_op jit(solution)/shard_map/all_to_all | solution.py:89
  52.3 26.5 %copy-start.14 = (f32[448]{0:T(512)S(1)}, f32[448]{0:T(512)}, u32[]{:S(2)}) copy-start(f32[448]{0:T(512)} %param.17) | copy-start | bytes 5380
  52.3 36.5 %collective-permute-start.13 = (bf16[456,1536]{1,0:T(8,128)(2,1)S(1)}, bf16[456,1536]{1,0:T(8,128)(2,1)}, u32[]{:S(2)}, u32[]{:S(2)}) collective-permute-start(bf16[456,1536]{1,0:T(8,128)(2,1)S(1)} %collective-permute-done.3), channel_id=1, source_target_pairs={{1,25},{3,27},{5,29},{7,31},{17,9},{19,11},{21,13},{23,15},{33,57}... | collective-permute-start | bytes 4202504 | tf_op jit(solution)/shard_map/ppermute | solution.py:24
  75.0 32.6 %copy-start.6 = (bf16[456,1536]{1,0:T(8,128)(2,1)}, bf16[456,1536]{1,0:T(8,128)(2,1)S(1)}, u32[]{:S(2)}) copy-start(bf16[456,1536]{1,0:T(8,128)(2,1)S(1)} %collective-permute-done.4) | copy-start | bytes 4202500
  75.0 24.5 %collective-permute-start.7 = (bf16[456,1536]{1,0:T(8,128)(2,1)S(1)}, bf16[456,1536]{1,0:T(8,128)(2,1)}, u32[]{:S(2)}, u32[]{:S(2)}) collective-permute-start(bf16[456,1536]{1,0:T(8,128)(2,1)S(1)} %collective-permute-done.4), channel_id=1, source_target_pairs={{0,1},{2,3},{4,5},{6,7},{8,9},{10,11},{12,13},{14,15},{16,17},{18,... | collective-permute-start | bytes 4202504 | tf_op jit(solution)/shard_map/ppermute | solution.py:24
  88.8 54.5 %collective-permute-start.14 = (bf16[456,1536]{1,0:T(8,128)(2,1)}, bf16[456,1536]{1,0:T(8,128)(2,1)}, u32[]{:S(2)}, u32[]{:S(2)}) collective-permute-start(bf16[456,1536]{1,0:T(8,128)(2,1)} %collective-permute-done.13), channel_id=1, source_target_pairs={{9,41},{11,43},{13,45},{15,47},{25,57},{27,59},{29,61},{31,63},{41... | collective-permute-start | bytes 4202504 | tf_op jit(solution)/shard_map/ppermute | solution.py:24
  90.8 19.4 %collective-permute-start.9 = (bf16[112,448]{1,0:T(8,128)(2,1)S(1)}, bf16[112,448]{1,0:T(8,128)(2,1)S(1)}, u32[]{:S(2)}, u32[]{:S(2)}) collective-permute-start(bf16[112,448]{1,0:T(8,128)(2,1)S(1)} %get-tuple-element.237), channel_id=1, source_target_pairs={{1,33},{3,35},{5,37},{7,39},{9,57},{11,59},{13,61},{15,63},{17,49}... | collective-permute-start | bytes 301064 | tf_op jit(solution)/shard_map/ppermute | solution.py:24
  92.7 28.2 %collective-permute-start.8 = (bf16[112,448]{1,0:T(8,128)(2,1)S(1)}, bf16[112,448]{1,0:T(8,128)(2,1)S(1)}, u32[]{:S(2)}, u32[]{:S(2)}) collective-permute-start(bf16[112,448]{1,0:T(8,128)(2,1)S(1)} %get-tuple-element.237), channel_id=1, source_target_pairs={{0,33},{1,224},{2,35},{3,226},{4,37},{5,228},{6,39},{7,230},{8,57}... | collective-permute-start | bytes 301064 | tf_op jit(solution)/shard_map/ppermute | solution.py:24
  99.5 21.4 %collective-permute-start.10 = (bf16[456,1536]{1,0:T(8,128)(2,1)S(1)}, bf16[456,1536]{1,0:T(8,128)(2,1)}, u32[]{:S(2)}, u32[]{:S(2)}) collective-permute-start(bf16[456,1536]{1,0:T(8,128)(2,1)S(1)} %collective-permute-done.4), channel_id=1, source_target_pairs={{0,224},{1,33},{2,226},{3,35},{4,228},{5,37},{6,230},{7,39},{8,232... | collective-permute-start | bytes 4202504 | tf_op jit(solution)/shard_map/ppermute | solution.py:24
  101.0 1.1 copy-start.10
  104.0 16.8 %all-to-all-start.1 = ((f32[4,1,112,448]{3,2,1,0:T(8,128)}), f32[4,1,112,448]{3,2,1,0:T(8,128)S(1)}, u32[]{:S(2)}, u32[]{:S(2)}) async-start(f32[4,1,112,448]{3,2,1,0:T(8,128)} %bitcast.7), calls=%async_computation.1 | async-start | bytes 1835008 | tf_op jit(solution)/shard_map/all_to_all | solution.py:89
  121.9 16.3 %all-to-all-start.2 = ((bf16[4,2,112,448]{3,2,1,0:T(8,128)(2,1)}), bf16[4,2,112,448]{3,2,1,0:T(8,128)(2,1)S(1)}, u32[]{:S(2)}, u32[]{:S(2)}) async-start(bf16[4,2,112,448]{3,2,1,0:T(8,128)(2,1)} %broadcast_in_dim.30), calls=%async_computation.2 | async-start | bytes 1835008 | tf_op jit(solution)/shard_map/all_to_all | solution.py:103
  128.0 10.2 %collective-permute-start.12 = (bf16[112,448]{1,0:T(8,128)(2,1)S(1)}, bf16[112,448]{1,0:T(8,128)(2,1)S(1)}, u32[]{:S(2)}, u32[]{:S(2)}) collective-permute-start(bf16[112,448]{1,0:T(8,128)(2,1)S(1)} %fusion.93), channel_id=1, source_target_pairs={{0,65},{2,67},{4,69},{6,71},{8,89},{10,91},{12,93},{14,95},{16,81}... | collective-permute-start | bytes 301064 | tf_op jit(solution)/shard_map/ppermute | solution.py:24
  129.3 26.4 %collective-permute-start.15 = (bf16[456,1536]{1,0:T(8,128)(2,1)}, bf16[456,1536]{1,0:T(8,128)(2,1)}, u32[]{:S(2)}, u32[]{:S(2)}) collective-permute-start(bf16[456,1536]{1,0:T(8,128)(2,1)} %collective-permute-done.10), channel_id=1, source_target_pairs={{1,33},{3,35},{5,37},{7,39},{9,41},{11,43},{13,45},{15,47},{17,49}... | collective-permute-start | bytes 4202504 | tf_op jit(solution)/shard_map/ppermute | solution.py:24
  131.2 7.1 %collective-permute-start.11 = (bf16[112,448]{1,0:T(8,128)(2,1)S(1)}, bf16[112,448]{1,0:T(8,128)(2,1)S(1)}, u32[]{:S(2)}, u32[]{:S(2)}) collective-permute-start(bf16[112,448]{1,0:T(8,128)(2,1)S(1)} %fusion.93), channel_id=1, source_target_pairs={{0,224},{1,193},{2,226},{3,195},{4,228},{5,197},{6,230},{7,199},{8... | collective-permute-start | bytes 301064 | tf_op jit(solution)/shard_map/ppermute | solution.py:24
  139.4 16.3 %all-to-all-start.3 = ((bf16[4,2,112,448]{3,2,1,0:T(8,128)(2,1)}), bf16[4,2,112,448]{3,2,1,0:T(8,128)(2,1)S(1)}, u32[]{:S(2)}, u32[]{:S(2)}) async-start(bf16[4,2,112,448]{3,2,1,0:T(8,128)(2,1)} %broadcast_in_dim.31), calls=%async_computation.3 | async-start | bytes 1835008 | tf_op jit(solution)/shard_map/all_to_all | solution.py:103
  143.3 1.8 copy-start.7
  155.6 1.3 copy-start.1
  161.1 4.8 %copy-start.2 = (bf16[448,1536]{1,0:T(8,128)(2,1)S(1)}, bf16[448,1536]{1,0:T(8,128)(2,1)}, u32[]{:S(2)}) copy-start(bf16[448,1536]{1,0:T(8,128)(2,1)} %copy-done) | copy-start | bytes 4128772
  161.1 3.9 %collective-permute-start.16 = (f32[448,384]{1,0:T(8,128)S(1)}, f32[448,384]{1,0:T(8,128)S(1)}, u32[]{:S(2)}, u32[]{:S(2)}) collective-permute-start(f32[448,384]{1,0:T(8,128)S(1)} %get-tuple-element.207), channel_id=1, source_target_pairs={{0,1},{1,0},{2,3},{3,2},{4,5},{5,4},{6,7},{7,6},{8,9},{9,8},{10,11... | collective-permute-start | bytes 2064392 | tf_op jit(solution)/shard_map/ppermute | solution.py:24
  169.3 13.1 %collective-permute-start.17 = (f32[448,384]{1,0:T(8,128)S(1)}, f32[448,384]{1,0:T(8,128)S(1)}, u32[]{:S(2)}, u32[]{:S(2)}) collective-permute-start(f32[448,384]{1,0:T(8,128)S(1)} %get-tuple-element.211), channel_id=1, source_target_pairs={{0,1},{1,0},{2,3},{3,2},{4,5},{5,4},{6,7},{7,6},{8,9},{9,8},{10,11... | collective-permute-start | bytes 2064392 | tf_op jit(solution)/shard_map/ppermute | solution.py:24
  169.4 28.7 %collective-permute-start.18 = (f32[448,384]{1,0:T(8,128)}, f32[448,384]{1,0:T(8,128)S(1)}, u32[]{:S(2)}, u32[]{:S(2)}) collective-permute-start(f32[448,384]{1,0:T(8,128)} %add.189), channel_id=1, source_target_pairs={{0,8},{1,9},{2,10},{3,11},{4,12},{5,13},{6,14},{7,15},{8,0},{9,1},... | collective-permute-start | bytes 2064392 | tf_op jit(solution)/shard_map/ppermute | solution.py:24

commit v9 on v8

--- a/solution.py
+++ b/solution.py
@@ -57,8 +57,8 @@
     high = lax.reduce_precision(occ_energy[0], 8, 7)
     rest = occ_energy[0] - high
     middle = lax.reduce_precision(rest, 8, 7)
-    column = lax.broadcasted_iota(jnp.int32, (8, 4 * depth), 1)
-    tail = jnp.where(column == 0, high, jnp.where(column == 1, middle, jnp.where(column == 2, rest - middle, 0.0)))
+    line = lax.broadcasted_iota(jnp.int32, (8, 4 * depth), 0)
+    tail = jnp.where(line == 0, high, jnp.where(line == 1, middle, jnp.where(line == 2, rest - middle, 0.0)))
     there = across(own)
     beside = other_core(own)
     there_beside = other_core(there)
@@ -76,6 +76,7 @@
     beyond = moved(mine, lambda z, xl, xh, y, c: (z, 1 - xl, 1, y, c) if (xh, c) == (0, 0) else None)
     swap_one = other_core(step_one)
     step_two = moved(step_one, lambda z, xl, xh, y, c: (z - 1 if c == 0 else z + 1, xl, xh, y, c))
+    swap_two = moved(swap_one, lambda z, xl, xh, y, c: (z - 1, xl, xh, y, 1) if c == 1 else None)
     turned_one = moved(step_one, lambda z, xl, xh, y, c: (z, 1 - xl, 1, y, c) if (xh, c) == (0, 1) else None)
 
     def numer(a, b):
@@ -89,8 +90,8 @@
         return jnp.sum(lax.all_to_all(parts, "y", 0, 0, tiled=True), axis=0)
 
     def energy(block):
-        terms = block[nvir, :3].astype(jnp.float32)
-        return terms[0] + terms[1] + terms[2]
+        terms = block[nvir:, :nvir].astype(jnp.float32)
+        return terms[0:1] + terms[1:2] + terms[2:3]
 
     vir_rows = lax.dynamic_slice_in_dim(vir_energy, y * share, share)
     virs = vir_rows[:, None] + vir_energy[None, :]
@@ -107,12 +108,11 @@
     cols_one = jnp.where(c == 0, step_one, swap_one)
     step_zero = jnp.where(xh == 0, mine, beyond)
     early = over_y(packed(numer(rows_one, cols_one), numer(mine, step_zero)))
-    step_two, swap_one, early = lax.optimization_barrier((step_two, swap_one, early))
-    swap_two = moved(step_two, lambda z, xl, xh, y, c: (z, xl, xh, y, 1) if c == 0 else None)
+    step_two, swap_one, swap_two, early = lax.optimization_barrier((step_two, swap_one, swap_two, early))
     rows_two = jnp.where(c == 0, swap_one, swap_two)
     late = over_y(packed(numer(rows_two, step_two)))
 
-    turned_two = moved(turned_one, lambda z, xl, xh, y, c: (z + 1, xl, xh, y, c) if (xh, c) == (1, 1) else None)
+    turned_two = moved(step_two, lambda z, xl, xh, y, c: (z, 1 - xl, 1, y, c) if (xh, c) == (0, 1) else None)
     step_three = moved(
         step_two,
         lambda z, xl, xh, y, c: (z - 1, xl, xh, y, c) if c == 0 else (z + 1, kind(xl, xh), xh, y, c),
@@ -130,7 +130,7 @@
         lambda z, xl, xh, y, c: (z + 1, kind(xl, xh), xh, y, 1) if c == 1 else None,
     )
     second = jnp.where(c == 0, amps_one, second)
-    late, first, second, step_three, amps_zero = lax.optimization_barrier((late, first, second, step_three, amps_zero))
+    late, first, second, amps_zero = lax.optimization_barrier((late, first, second, amps_zero))
     first, second = to_all(first, second)
 
     amps_two = amps(late[0], rows_two, step_two)

time: 201 us -> 186 us (0.925)
  between operations: 14.9 us -> 3.42 us
  starting transfers between devices: 64.8 us -> 55.7 us
  matrix products: 19 us -> 23.8 us
  local copies, waits for them, and re-layouts: 8.67 us -> 4.38 us
  other arithmetic: 13.6 us -> 16.8 us
    ppermute x19, starting transfers between devices: 49.3 us -> 40.8 us  [moved(): return lax.ppermute(array, ALL, pairs)]
    slice x6 -> x0, local copies, waits for them, and re-layouts: 3.85 us -> none  [energy(): return terms[0] + terms[1] + terms[2]]
    all_to_all x2, waiting for transfers between devices: 25.1 us -> 27.9 us  [over_y(): return jnp.sum(lax.all_to_all(parts, 'y', 0, 0, tiled=True), axis=0)]
    dot_general x6, matrix products: 6.32 us -> 9 us  [dot_nt(): lax.dot_general(a, b, (((1,), (1,)), ((), ())), preferred_element_type=jn...]
    ppermute x19, waiting for transfers between devices: 46.1 us -> 43.7 us  [moved(): return lax.ppermute(array, ALL, pairs)]
    dot_general x8, matrix products: 12.7 us -> 14.8 us  [dot_tn(): lax.dot_general(a, b, (((0,), (0,)), ((), ())), preferred_element_type=jn...]
  transfers between devices with their start and end apart: 23 -> 23, of which waited for: 9 -> 9; matrix products, arithmetic and copies ran while one was open for 15% -> 18% of each run, Pallas kernels for 0% -> 0%
where the time goes in v9:
time: 186 us; the launch traced here: 182 us
  waiting for transfers between devices  77.9 us (42%)
  starting transfers between devices  55.7 us (30%)
  matrix products  23.8 us (13%)
  other arithmetic  16.8 us (9%)
  local copies, waits for them, and re-layouts  4.38 us (2%)
  between operations  3.42 us (2%)
    ppermute x19, waiting for transfers between devices, moved(): return lax.ppermute(array, ALL, pairs)  43.7 us
    ppermute x19, starting transfers between devices, moved(): return lax.ppermute(array, ALL, pairs)  40.8 us
    all_to_all x2, waiting for transfers between devices, over_y(): return jnp.sum(lax.all_to_all(parts, 'y', 0, 0, tiled=True), axis=0)  27.9 us
    dot_general x8, matrix products, dot_tn(): lax.dot_general(a, b, (((0,), (0,)), ((), ())), preferred_element_type=jn...  14.8 us
    dot_general x6, matrix products, dot_nt(): lax.dot_general(a, b, (((1,), (1,)), ((), ())), preferred_element_type=jn...  9 us
    all_to_all x2, starting transfers between devices, over_y(): return jnp.sum(lax.all_to_all(parts, 'y', 0, 0, tiled=True), axis=0)  7.69 us
    all_to_all x2, starting transfers between devices, to_all(): lax.all_to_all(jnp.broadcast_to(parts, (NY, *parts.shape)), 'y', 0, 0, ti...  7.19 us
    all_to_all x2, waiting for transfers between devices, to_all(): lax.all_to_all(jnp.broadcast_to(parts, (NY, *parts.shape)), 'y', 0, 0, ti...  6.28 us
  transfers between devices with their start and end apart: 23, of which 9 were waited for; matrix products, arithmetic and copies ran while one was open for 18% of the time, Pallas kernels for 0%

profile of v9, /device:TPU:1, one launch (start us, length us, event | category | flops | bytes accessed | tf_op | source)
XLA Modules:
  0.0 182.3 jit_solution(16955466005029800652)
XLA Ops:
  0.0 3.6 %collective-permute-start.1 = (bf16[448,384]{1,0:T(8,128)(2,1)}, bf16[448,384]{1,0:T(8,128)(2,1)S(1)}, u32[]{:S(2)}, u32[]{:S(2)}) collective-permute-start(bf16[448,384]{1,0:T(8,128)(2,1)} %bitcast.104), channel_id=1, source_target_pairs={{0,8},{1,9},{2,10},{3,11},{4,12},{5,13},{6,14},{7,15},{8,0},{9,1},... | collective-permute-start | bytes 1032200 | tf_op jit(solution)/shard_map/ppermute | solution.py:24
  3.6 1.0 collective-permute-start
  7.6 3.1 %collective-permute-done.1 = bf16[448,384]{1,0:T(8,128)(2,1)S(1)} collective-permute-done((bf16[448,384]{1,0:T(8,128)(2,1)}, bf16[448,384]{1,0:T(8,128)(2,1)S(1)}, u32[]{:S(2)}, u32[]{:S(2)}) %collective-permute-start.1) | collective-permute-done | bytes 344096 | tf_op jit(solution)/shard_map/ppermute | solution.py:24
  10.6 2.2 %collective-permute-start.2 = (bf16[448,384]{1,0:T(8,128)(2,1)S(1)}, bf16[448,384]{1,0:T(8,128)(2,1)S(1)}, u32[]{:S(2)}, u32[]{:S(2)}) collective-permute-start(bf16[448,384]{1,0:T(8,128)(2,1)S(1)} %collective-permute-done.1), channel_id=1, source_target_pairs={{0,1},{1,0},{2,3},{3,2},{4,5},{5,4},{6,7},{7,6},{8,9},{9,8},{10,11... | collective-permute-start | bytes 1032200 | tf_op jit(solution)/shard_map/ppermute | solution.py:24
  12.8 1.3 select_convert_fusion
  14.1 1.2 maximum_select_fusion.1
  15.6 0.3 maximum_select_fusion
  15.9 1.3 pad_maximum_fusion.1
  17.3 1.9 %collective-permute-start.3 = (bf16[456,1536]{1,0:T(8,128)(2,1)}, bf16[456,1536]{1,0:T(8,128)(2,1)}, u32[]{:S(2)}, u32[]{:S(2)}) collective-permute-start(bf16[456,1536]{1,0:T(8,128)(2,1)} %pad_maximum_fusion.1), channel_id=1, source_target_pairs={{0,224},{1,33},{2,226},{3,35},{4,228},{5,37},{6,230},{7,39},{8,248... | collective-permute-start | bytes 4202504 | tf_op jit(solution)/shard_map/ppermute | solution.py:24
  19.1 1.8 collective-permute-start.7
  20.9 18.5 %collective-permute-done.3 = bf16[456,1536]{1,0:T(8,128)(2,1)} collective-permute-done((bf16[456,1536]{1,0:T(8,128)(2,1)}, bf16[456,1536]{1,0:T(8,128)(2,1)}, u32[]{:S(2)}, u32[]{:S(2)}) %collective-permute-start.3) | collective-permute-done | bytes 1400864 | tf_op jit(solution)/shard_map/ppermute | solution.py:24
  39.3 0.4 collective-permute-start.5
  39.9 5.7 %collective-permute-start.13 = (bf16[456,1536]{1,0:T(8,128)(2,1)}, bf16[456,1536]{1,0:T(8,128)(2,1)}, u32[]{:S(2)}, u32[]{:S(2)}) collective-permute-start(bf16[456,1536]{1,0:T(8,128)(2,1)} %collective-permute-done.3), channel_id=1, source_target_pairs={{1,25},{3,27},{5,29},{7,31},{17,9},{19,11},{21,13},{23,15},{33,57}... | collective-permute-start | bytes 4202504 | tf_op jit(solution)/shard_map/ppermute | solution.py:24
  45.7 2.2 %broadcast_select_fusion.3 = (bf16[456,1536]{1,0:T(8,128)(2,1)S(1)}, bf16[456,1536]{1,0:T(8,128)(2,1)S(1)}, bf16[456,1536]{1,0:T(8,128)(2,1)S(1)}) fusion(bf16[456,1536]{1,0:T(8,128)(2,1)} %collective-permute-done.3, pred[]{:T(512)S(6)} %eq.35, bf16[8,1536]{1,0:T(8,128)(2,1)S(1)} %select_convert_fusion, bf16[448,1536]{1,0:T(8,128)(2,1)S(1)} %maximum_select_fusion, ...), kind=kLoop, calls=%fused_computation.77 | loop fusion | flops 4902912 | bytes 9805826 | tf_op jit(solution)/shard_map/jit(_where)/select_n | solution.py:107
  47.9 0.9 fusion.77
  49.0 0.4 copy-done.5
  49.4 0.9 fusion.62
  50.3 0.9 fusion.74
  51.3 0.9 fusion.65
  52.2 6.0 %collective-permute-start.6 = (bf16[456,1536]{1,0:T(8,128)(2,1)S(1)}, bf16[456,1536]{1,0:T(8,128)(2,1)}, u32[]{:S(2)}, u32[]{:S(2)}) collective-permute-start(bf16[456,1536]{1,0:T(8,128)(2,1)S(1)} %collective-permute-done.5), channel_id=1, source_target_pairs={{1,225},{3,227},{5,229},{7,231},{9,233},{11,235},{13,237},{15,239}... | collective-permute-start | bytes 4202504 | tf_op jit(solution)/shard_map/ppermute | solution.py:24
  58.1 1.5 pad_maximum_fusion
  59.6 4.2 %all-to-all-start = ((f32[4,2,112,448]{3,2,1,0:T(8,128)}), f32[4,2,112,448]{3,2,1,0:T(8,128)S(1)}, u32[]{:S(2)}, u32[]{:S(2)}) async-start(f32[4,2,112,448]{3,2,1,0:T(8,128)} %pad_maximum_fusion), calls=%async_computation | async-start | bytes 3670016 | tf_op jit(solution)/shard_map/all_to_all | solution.py:90
  63.8 0.7 slice_convert_fusion.4
  64.5 0.7 slice_convert_fusion.3
  65.2 0.7 slice_convert_fusion.1
  66.0 17.9 %all-to-all-done = f32[4,2,112,448]{3,2,1,0:T(8,128)S(1)} async-done(((f32[4,2,112,448]{3,2,1,0:T(8,128)}), f32[4,2,112,448]{3,2,1,0:T(8,128)S(1)}, u32[]{:S(2)}, u32[]{:S(2)}) %all-to-all-start) | async-done | bytes 1605664 | tf_op jit(solution)/shard_map/all_to_all | solution.py:90
  83.8 1.0 reduce_sum.20
  84.8 1.2 fusion.94
  86.0 1.9 %collective-permute-start.10 = (bf16[112,448]{1,0:T(8,128)(2,1)S(1)}, bf16[112,448]{1,0:T(8,128)(2,1)S(1)}, u32[]{:S(2)}, u32[]{:S(2)}) collective-permute-start(bf16[112,448]{1,0:T(8,128)(2,1)S(1)} %get-tuple-element.237), channel_id=1, source_target_pairs={{1,33},{3,35},{5,37},{7,39},{9,57},{11,59},{13,61},{15,63},{17,49}... | collective-permute-start | bytes 301064 | tf_op jit(solution)/shard_map/ppermute | solution.py:24
  88.0 1.5 broadcast_select_fusion.1
  89.6 2.2 %fusion.71 = f32[448,448]{1,0:T(8,128)S(1)} fusion(bf16[456,1536]{1,0:T(8,128)(2,1)S(1)} %broadcast_select_fusion.1, bf16[456,1536]{1,0:T(8,128)(2,1)} %collective-permute-done.4), kind=kOutput, calls=%fused_computation.88 | convolution fusion | flops 616562688 | bytes 3555328 | tf_op jit(solution)/shard_map/dot_general | solution.py:40
  91.8 6.9 %collective-permute-start.14 = (bf16[456,1536]{1,0:T(8,128)(2,1)}, bf16[456,1536]{1,0:T(8,128)(2,1)}, u32[]{:S(2)}, u32[]{:S(2)}) collective-permute-start(bf16[456,1536]{1,0:T(8,128)(2,1)} %collective-permute-done.4), channel_id=1, source_target_pairs={{1,25},{3,27},{5,29},{7,31},{17,9},{19,11},{21,13},{23,15},{33,57}... | collective-permute-start | bytes 4202504 | tf_op jit(solution)/shard_map/ppermute | solution.py:24
  98.7 0.5 collective-permute-start.8
  99.1 3.2 %fusion.68 = f32[448,448]{1,0:T(8,128)} fusion(f32[448,448]{1,0:T(8,128)S(1)} %fusion.71, bf16[456,1536]{1,0:T(8,128)(2,1)S(1)} %broadcast_select_fusion.1, bf16[456,1536]{1,0:T(8,128)(2,1)} %collective-permute-done.4), kind=kOutput, calls=%fused_computation.87 | convolution fusion | flops 617451520 | bytes 4472832 | tf_op jit(solution)/shard_map/dot_general | solution.py:40
  102.3 3.5 %all-to-all-start.1 = ((f32[4,1,112,448]{3,2,1,0:T(8,128)}), f32[4,1,112,448]{3,2,1,0:T(8,128)S(1)}, u32[]{:S(2)}, u32[]{:S(2)}) async-start(f32[4,1,112,448]{3,2,1,0:T(8,128)} %bitcast.7), calls=%async_computation.1 | async-start | bytes 1835008 | tf_op jit(solution)/shard_map/all_to_all | solution.py:90
  105.8 0.7 slice_convert_fusion.5
  106.6 10.0 %all-to-all-done.1 = f32[4,1,112,448]{3,2,1,0:T(8,128)S(1)} async-done(((f32[4,1,112,448]{3,2,1,0:T(8,128)}), f32[4,1,112,448]{3,2,1,0:T(8,128)S(1)}, u32[]{:S(2)}, u32[]{:S(2)}) %all-to-all-start.1) | async-done | bytes 802848 | tf_op jit(solution)/shard_map/all_to_all | solution.py:90
  116.8 1.0 broadcast_in_dim.30
  117.8 3.7 %all-to-all-start.2 = ((bf16[4,2,112,448]{3,2,1,0:T(8,128)(2,1)}), bf16[4,2,112,448]{3,2,1,0:T(8,128)(2,1)S(1)}, u32[]{:S(2)}, u32[]{:S(2)}) async-start(bf16[4,2,112,448]{3,2,1,0:T(8,128)(2,1)} %broadcast_in_dim.30), calls=%async_computation.2 | async-start | bytes 1835008 | tf_op jit(solution)/shard_map/all_to_all | solution.py:104
  121.6 1.3 collective-permute-start.12
  122.9 1.9 %collective-permute-start.11 = (bf16[112,448]{1,0:T(8,128)(2,1)S(1)}, bf16[112,448]{1,0:T(8,128)(2,1)S(1)}, u32[]{:S(2)}, u32[]{:S(2)}) collective-permute-start(bf16[112,448]{1,0:T(8,128)(2,1)S(1)} %fusion.93), channel_id=1, source_target_pairs={{0,224},{1,193},{2,226},{3,195},{4,228},{5,197},{6,230},{7,199},{8... | collective-permute-start | bytes 301064 | tf_op jit(solution)/shard_map/ppermute | solution.py:24
  124.9 2.7 %collective-permute-start.15 = (bf16[456,1536]{1,0:T(8,128)(2,1)}, bf16[456,1536]{1,0:T(8,128)(2,1)}, u32[]{:S(2)}, u32[]{:S(2)}) collective-permute-start(bf16[456,1536]{1,0:T(8,128)(2,1)} %collective-permute-done.8), channel_id=1, source_target_pairs={{1,33},{3,35},{5,37},{7,39},{9,41},{11,43},{13,45},{15,47},{17,49}... | collective-permute-start | bytes 4202504 | tf_op jit(solution)/shard_map/ppermute | solution.py:24
  127.6 4.7 %collective-permute-done.12 = bf16[112,448]{1,0:T(8,128)(2,1)S(1)} collective-permute-done((bf16[112,448]{1,0:T(8,128)(2,1)S(1)}, bf16[112,448]{1,0:T(8,128)(2,1)S(1)}, u32[]{:S(2)}, u32[]{:S(2)}) %collective-permute-start.12) | collective-permute-done | bytes 100384 | tf_op jit(solution)/shard_map/ppermute | solution.py:24
  132.3 1.1 all-to-all-done.2
  133.5 1.0 broadcast_in_dim.31
  134.5 3.5 %all-to-all-start.3 = ((bf16[4,2,112,448]{3,2,1,0:T(8,128)(2,1)}), bf16[4,2,112,448]{3,2,1,0:T(8,128)(2,1)S(1)}, u32[]{:S(2)}, u32[]{:S(2)}) async-start(bf16[4,2,112,448]{3,2,1,0:T(8,128)(2,1)} %broadcast_in_dim.31), calls=%async_computation.3 | async-start | bytes 1835008 | tf_op jit(solution)/shard_map/all_to_all | solution.py:104
  138.1 7.7 %conditional.3 = (f32[448,768]{1,0:T(8,128)}, f32[448,768]{1,0:T(8,128)S(1)}) conditional(s32[]{:T(128)} %clamp.2, (bf16[456,1536]{1,0:T(8,128)(2,1)}, bf16[448,448]{1,0:T(8,128)(2,1)S(1)}, bf16[456,1536]{1,0:T(8,128)(2,1)}, bf16[448,448]{1,0:T(8,128)(2,1)S(1)}) %tuple.116, (bf16[456,1536]{1,0:T(8,128)(2,1)}, ...), branch_computations={%region_2.3_spmd, %region_3.4_spmd, %region_4.5_spmd, %region_5.6_... | conditional | flops 1233813504 | bytes 12615696 | solution.py:165
  138.1 1.6 fusion.7
  139.7 1.6 convolution_add_fusion.2
  141.4 1.6 fusion.10
  143.1 2.7 %convolution_add_fusion.3 = f32[448,768]{1,0:T(8,128)} fusion(f32[448,768]{1,0:T(8,128)S(1)} %fusion.10, bf16[448,448]{1,0:T(8,128)(2,1)S(1)} %get-tuple-element.123, bf16[456,1536]{1,0:T(8,128)(2,1)} %get-tuple-element.124), kind=kOutput, calls=%fused_computation.9 | convolution fusion | flops 308625408 | bytes 3842048 | tf_op jit(solution)/shard_map/cond/branch_1_fun/dot_general | solution.py:48
  145.8 5.2 %all-to-all-done.3 = bf16[4,2,112,448]{3,2,1,0:T(8,128)(2,1)S(1)} async-done(((bf16[4,2,112,448]{3,2,1,0:T(8,128)(2,1)}), bf16[4,2,112,448]{3,2,1,0:T(8,128)(2,1)S(1)}, u32[]{:S(2)}, u32[]{:S(2)}) %all-to-all-start.3) | async-done | bytes 802848 | tf_op jit(solution)/shard_map/all_to_all | solution.py:104
  151.1 1.3 copy-done.1
  152.3 4.1 %conditional.4 = (f32[448,384]{1,0:T(8,128)S(1)}, f32[448,384]{1,0:T(8,128)S(1)}) conditional(s32[]{:T(128)} %clamp.2, (bf16[456,1536]{1,0:T(8,128)(2,1)}, bf16[448,448]{1,0:T(8,128)(2,1)S(1)}, bf16[448,1536]{1,0:T(8,128)(2,1)S(1)}, bf16[448,448]{1,0:T(8,128)(2,1)S(1)}, f32[448,768]{1,0:T(8,128)}) %tuple.120, ...), branch_computations={%region_6.7_spmd, %region_7.8_spmd, %region_8.9_spmd, %region_9.10... | conditional | flops 617250816 | bytes 10493968 | solution.py:177
  152.3 1.6 fusion.30
  154.0 2.1 %fusion.28 = f32[448,768]{1,0:T(8,128)S(1)} fusion(f32[448,768]{1,0:T(8,128)} %get-tuple-element.138, f32[448,768]{1,0:T(8,128)S(1)} %fusion.30, bf16[448,448]{1,0:T(8,128)(2,1)S(1)} %get-tuple-element.141, bf16[456,1536]{1,0:T(8,128)(2,1)} %get-tuple-element.142), kind=kOutput, calls=%fused_computation.38 | convolution fusion | flops 308969472 | bytes 5218304 | tf_op jit(solution)/shard_map/cond/branch_1_fun/dot_general | solution.py:48
  156.5 2.1 %collective-permute-done.16 = f32[448,384]{1,0:T(8,128)S(1)} collective-permute-done((f32[448,384]{1,0:T(8,128)S(1)}, f32[448,384]{1,0:T(8,128)S(1)}, u32[]{:S(2)}, u32[]{:S(2)}) %collective-permute-start.16) | collective-permute-done | bytes 688160 | tf_op jit(solution)/shard_map/ppermute | solution.py:24
  158.7 0.9 add.153
  159.6 3.5 %conditional.5 = (f32[448,384]{1,0:T(8,128)S(1)}, f32[448,384]{1,0:T(8,128)S(1)}) conditional(s32[]{:T(128)} %clamp.2, (bf16[456,1536]{1,0:T(8,128)(2,1)}, bf16[448,448]{1,0:T(8,128)(2,1)S(1)}, bf16[448,1536]{1,0:T(8,128)(2,1)S(1)}, bf16[448,448]{1,0:T(8,128)(2,1)S(1)}, f32[448,768]{1,0:T(8,128)S(1)}) %tuple.121, ...), branch_computations={%region_10.11_spmd, %region_11.12_spmd, %region_12.13_spmd, %regio... | conditional | flops 617250816 | bytes 10493968 | solution.py:177
  159.6 1.7 fusion.46
  161.3 1.6 fusion.44
  163.2 2.9 %collective-permute-start.18 = (f32[448,384]{1,0:T(8,128)S(1)}, f32[448,384]{1,0:T(8,128)S(1)}, u32[]{:S(2)}, u32[]{:S(2)}) collective-permute-start(f32[448,384]{1,0:T(8,128)S(1)} %copy-done.6), channel_id=1, source_target_pairs={{0,8},{1,9},{2,10},{3,11},{4,12},{5,13},{6,14},{7,15},{8,0},{9,1},... | collective-permute-start | bytes 2064392 | tf_op jit(solution)/shard_map/ppermute | solution.py:24
  166.1 15.3 %collective-permute-done.18 = f32[448,384]{1,0:T(8,128)S(1)} collective-permute-done((f32[448,384]{1,0:T(8,128)S(1)}, f32[448,384]{1,0:T(8,128)S(1)}, u32[]{:S(2)}, u32[]{:S(2)}) %collective-permute-start.18) | collective-permute-done | bytes 688160 | tf_op jit(solution)/shard_map/ppermute | solution.py:24
  181.4 0.9 add_bitcast_fusion
  (54 shorter events, 1.6 us)
Async XLA Ops:
  0.0 10.6 %collective-permute-start.1 = (bf16[448,384]{1,0:T(8,128)(2,1)}, bf16[448,384]{1,0:T(8,128)(2,1)S(1)}, u32[]{:S(2)}, u32[]{:S(2)}) collective-permute-start(bf16[448,384]{1,0:T(8,128)(2,1)} %bitcast.104), channel_id=1, source_target_pairs={{0,8},{1,9},{2,10},{3,11},{4,12},{5,13},{6,14},{7,15},{8,0},{9,1},... | collective-permute-start | bytes 1032200 | tf_op jit(solution)/shard_map/ppermute | solution.py:24
  3.6 10.6 %collective-permute-start = (bf16[448,384]{1,0:T(8,128)(2,1)}, bf16[448,384]{1,0:T(8,128)(2,1)S(1)}, u32[]{:S(2)}, u32[]{:S(2)}) collective-permute-start(bf16[448,384]{1,0:T(8,128)(2,1)} %bitcast.105), channel_id=1, source_target_pairs={{0,1},{1,0},{2,3},{3,2},{4,5},{5,4},{6,7},{7,6},{8,9},{9,8},{10,11... | collective-permute-start | bytes 1032200 | tf_op jit(solution)/shard_map/ppermute | solution.py:24
  10.6 4.8 %collective-permute-start.2 = (bf16[448,384]{1,0:T(8,128)(2,1)S(1)}, bf16[448,384]{1,0:T(8,128)(2,1)S(1)}, u32[]{:S(2)}, u32[]{:S(2)}) collective-permute-start(bf16[448,384]{1,0:T(8,128)(2,1)S(1)} %collective-permute-done.1), channel_id=1, source_target_pairs={{0,1},{1,0},{2,3},{3,2},{4,5},{5,4},{6,7},{7,6},{8,9},{9,8},{10,11... | collective-permute-start | bytes 1032200 | tf_op jit(solution)/shard_map/ppermute | solution.py:24
  15.9 35.3 %copy-start = (bf16[448,1536]{1,0:T(8,128)(2,1)}, bf16[448,1536]{1,0:T(8,128)(2,1)S(1)}, u32[]{:S(2)}) copy-start(bf16[448,1536]{1,0:T(8,128)(2,1)S(1)} %maximum_select_fusion) | copy-start | bytes 4128772
  15.9 23.8 %copy-start.7 = (f32[448]{0:T(512)S(1)}, f32[448]{0:T(512)}, u32[]{:S(2)}) copy-start(f32[448]{0:T(512)} %param.17) | copy-start | bytes 5380
  17.3 22.1 %collective-permute-start.3 = (bf16[456,1536]{1,0:T(8,128)(2,1)}, bf16[456,1536]{1,0:T(8,128)(2,1)}, u32[]{:S(2)}, u32[]{:S(2)}) collective-permute-start(bf16[456,1536]{1,0:T(8,128)(2,1)} %pad_maximum_fusion.1), channel_id=1, source_target_pairs={{0,224},{1,33},{2,226},{3,35},{4,228},{5,37},{6,230},{7,39},{8,248... | collective-permute-start | bytes 4202504 | tf_op jit(solution)/shard_map/ppermute | solution.py:24
  19.1 26.6 %collective-permute-start.7 = (bf16[456,1536]{1,0:T(8,128)(2,1)}, bf16[456,1536]{1,0:T(8,128)(2,1)}, u32[]{:S(2)}, u32[]{:S(2)}) collective-permute-start(bf16[456,1536]{1,0:T(8,128)(2,1)} %pad_maximum_fusion.1), channel_id=1, source_target_pairs={{0,24},{2,26},{4,28},{6,30},{16,8},{18,10},{20,12},{22,14},{32,56}... | collective-permute-start | bytes 4202504 | tf_op jit(solution)/shard_map/ppermute | solution.py:24
  39.3 6.3 %collective-permute-start.5 = (bf16[456,1536]{1,0:T(8,128)(2,1)}, bf16[456,1536]{1,0:T(8,128)(2,1)S(1)}, u32[]{:S(2)}, u32[]{:S(2)}) collective-permute-start(bf16[456,1536]{1,0:T(8,128)(2,1)} %collective-permute-done.3), channel_id=1, source_target_pairs={{0,1},{1,0},{2,3},{3,2},{4,5},{5,4},{6,7},{7,6},{8,9},{9,8},{10,11... | collective-permute-start | bytes 4202504 | tf_op jit(solution)/shard_map/ppermute | solution.py:24
  39.8 45.0 %collective-permute-start.4 = (bf16[456,1536]{1,0:T(8,128)(2,1)}, bf16[456,1536]{1,0:T(8,128)(2,1)}, u32[]{:S(2)}, u32[]{:S(2)}) collective-permute-start(bf16[456,1536]{1,0:T(8,128)(2,1)} %collective-permute-done.3), channel_id=1, source_target_pairs={{0,224},{1,33},{2,226},{3,35},{4,228},{5,37},{6,230},{7,39},{8,232... | collective-permute-start | bytes 4202504 | tf_op jit(solution)/shard_map/ppermute | solution.py:24
  39.9 98.1 %collective-permute-start.13 = (bf16[456,1536]{1,0:T(8,128)(2,1)}, bf16[456,1536]{1,0:T(8,128)(2,1)}, u32[]{:S(2)}, u32[]{:S(2)}) collective-permute-start(bf16[456,1536]{1,0:T(8,128)(2,1)} %collective-permute-done.3), channel_id=1, source_target_pairs={{1,25},{3,27},{5,29},{7,31},{17,9},{19,11},{21,13},{23,15},{33,57}... | collective-permute-start | bytes 4202504 | tf_op jit(solution)/shard_map/ppermute | solution.py:24
  47.9 1.2 copy-start.4
  47.9 1.6 copy-start.5
  47.9 3.4 %copy-start.3 = (bf16[456,1536]{1,0:T(8,128)(2,1)}, bf16[456,1536]{1,0:T(8,128)(2,1)S(1)}, u32[]{:S(2)}) copy-start(bf16[456,1536]{1,0:T(8,128)(2,1)S(1)} %get-tuple-element.230) | copy-start | bytes 4202500
  52.2 32.7 %collective-permute-start.6 = (bf16[456,1536]{1,0:T(8,128)(2,1)S(1)}, bf16[456,1536]{1,0:T(8,128)(2,1)}, u32[]{:S(2)}, u32[]{:S(2)}) collective-permute-start(bf16[456,1536]{1,0:T(8,128)(2,1)S(1)} %collective-permute-done.5), channel_id=1, source_target_pairs={{1,225},{3,227},{5,229},{7,231},{9,233},{11,235},{13,237},{15,239}... | collective-permute-start | bytes 4202504 | tf_op jit(solution)/shard_map/ppermute | solution.py:24
  59.6 24.2 %all-to-all-start = ((f32[4,2,112,448]{3,2,1,0:T(8,128)}), f32[4,2,112,448]{3,2,1,0:T(8,128)S(1)}, u32[]{:S(2)}, u32[]{:S(2)}) async-start(f32[4,2,112,448]{3,2,1,0:T(8,128)} %pad_maximum_fusion), calls=%async_computation | async-start | bytes 3670016 | tf_op jit(solution)/shard_map/all_to_all | solution.py:90
  86.0 20.5 %collective-permute-start.10 = (bf16[112,448]{1,0:T(8,128)(2,1)S(1)}, bf16[112,448]{1,0:T(8,128)(2,1)S(1)}, u32[]{:S(2)}, u32[]{:S(2)}) collective-permute-start(bf16[112,448]{1,0:T(8,128)(2,1)S(1)} %get-tuple-element.237), channel_id=1, source_target_pairs={{1,33},{3,35},{5,37},{7,39},{9,57},{11,59},{13,61},{15,63},{17,49}... | collective-permute-start | bytes 301064 | tf_op jit(solution)/shard_map/ppermute | solution.py:24
  88.0 28.8 %collective-permute-start.9 = (bf16[112,448]{1,0:T(8,128)(2,1)S(1)}, bf16[112,448]{1,0:T(8,128)(2,1)S(1)}, u32[]{:S(2)}, u32[]{:S(2)}) collective-permute-start(bf16[112,448]{1,0:T(8,128)(2,1)S(1)} %get-tuple-element.237), channel_id=1, source_target_pairs={{0,33},{1,224},{2,35},{3,226},{4,37},{5,228},{6,39},{7,230},{8,57}... | collective-permute-start | bytes 301064 | tf_op jit(solution)/shard_map/ppermute | solution.py:24
  91.8 46.3 %collective-permute-start.14 = (bf16[456,1536]{1,0:T(8,128)(2,1)}, bf16[456,1536]{1,0:T(8,128)(2,1)}, u32[]{:S(2)}, u32[]{:S(2)}) collective-permute-start(bf16[456,1536]{1,0:T(8,128)(2,1)} %collective-permute-done.4), channel_id=1, source_target_pairs={{1,25},{3,27},{5,29},{7,31},{17,9},{19,11},{21,13},{23,15},{33,57}... | collective-permute-start | bytes 4202504 | tf_op jit(solution)/shard_map/ppermute | solution.py:24
  98.7 26.2 %collective-permute-start.8 = (bf16[456,1536]{1,0:T(8,128)(2,1)}, bf16[456,1536]{1,0:T(8,128)(2,1)}, u32[]{:S(2)}, u32[]{:S(2)}) collective-permute-start(bf16[456,1536]{1,0:T(8,128)(2,1)} %collective-permute-done.4), channel_id=1, source_target_pairs={{0,224},{1,33},{2,226},{3,35},{4,228},{5,37},{6,230},{7,39},{8,232... | collective-permute-start | bytes 4202504 | tf_op jit(solution)/shard_map/ppermute | solution.py:24
  102.3 14.3 %all-to-all-start.1 = ((f32[4,1,112,448]{3,2,1,0:T(8,128)}), f32[4,1,112,448]{3,2,1,0:T(8,128)S(1)}, u32[]{:S(2)}, u32[]{:S(2)}) async-start(f32[4,1,112,448]{3,2,1,0:T(8,128)} %bitcast.7), calls=%async_computation.1 | async-start | bytes 1835008 | tf_op jit(solution)/shard_map/all_to_all | solution.py:90
  117.8 15.6 %all-to-all-start.2 = ((bf16[4,2,112,448]{3,2,1,0:T(8,128)(2,1)}), bf16[4,2,112,448]{3,2,1,0:T(8,128)(2,1)S(1)}, u32[]{:S(2)}, u32[]{:S(2)}) async-start(bf16[4,2,112,448]{3,2,1,0:T(8,128)(2,1)} %broadcast_in_dim.30), calls=%async_computation.2 | async-start | bytes 1835008 | tf_op jit(solution)/shard_map/all_to_all | solution.py:104
  121.6 10.6 %collective-permute-start.12 = (bf16[112,448]{1,0:T(8,128)(2,1)S(1)}, bf16[112,448]{1,0:T(8,128)(2,1)S(1)}, u32[]{:S(2)}, u32[]{:S(2)}) collective-permute-start(bf16[112,448]{1,0:T(8,128)(2,1)S(1)} %fusion.93), channel_id=1, source_target_pairs={{0,65},{2,67},{4,69},{6,71},{8,89},{10,91},{12,93},{14,95},{16,81}... | collective-permute-start | bytes 301064 | tf_op jit(solution)/shard_map/ppermute | solution.py:24
  122.9 10.5 %collective-permute-start.11 = (bf16[112,448]{1,0:T(8,128)(2,1)S(1)}, bf16[112,448]{1,0:T(8,128)(2,1)S(1)}, u32[]{:S(2)}, u32[]{:S(2)}) collective-permute-start(bf16[112,448]{1,0:T(8,128)(2,1)S(1)} %fusion.93), channel_id=1, source_target_pairs={{0,224},{1,193},{2,226},{3,195},{4,228},{5,197},{6,230},{7,199},{8... | collective-permute-start | bytes 301064 | tf_op jit(solution)/shard_map/ppermute | solution.py:24
  124.9 26.2 %collective-permute-start.15 = (bf16[456,1536]{1,0:T(8,128)(2,1)}, bf16[456,1536]{1,0:T(8,128)(2,1)}, u32[]{:S(2)}, u32[]{:S(2)}) collective-permute-start(bf16[456,1536]{1,0:T(8,128)(2,1)} %collective-permute-done.8), channel_id=1, source_target_pairs={{1,33},{3,35},{5,37},{7,39},{9,41},{11,43},{13,45},{15,47},{17,49}... | collective-permute-start | bytes 4202504 | tf_op jit(solution)/shard_map/ppermute | solution.py:24
  134.5 16.5 %all-to-all-start.3 = ((bf16[4,2,112,448]{3,2,1,0:T(8,128)(2,1)}), bf16[4,2,112,448]{3,2,1,0:T(8,128)(2,1)S(1)}, u32[]{:S(2)}, u32[]{:S(2)}) async-start(bf16[4,2,112,448]{3,2,1,0:T(8,128)(2,1)} %broadcast_in_dim.31), calls=%async_computation.3 | async-start | bytes 1835008 | tf_op jit(solution)/shard_map/all_to_all | solution.py:104
  151.0 1.3 copy-start.1
  156.4 3.2 %copy-start.2 = (bf16[448,1536]{1,0:T(8,128)(2,1)S(1)}, bf16[448,1536]{1,0:T(8,128)(2,1)}, u32[]{:S(2)}) copy-start(bf16[448,1536]{1,0:T(8,128)(2,1)} %copy-done) | copy-start | bytes 4128772
  156.4 2.2 %collective-permute-start.16 = (f32[448,384]{1,0:T(8,128)S(1)}, f32[448,384]{1,0:T(8,128)S(1)}, u32[]{:S(2)}, u32[]{:S(2)}) collective-permute-start(f32[448,384]{1,0:T(8,128)S(1)} %get-tuple-element.207), channel_id=1, source_target_pairs={{0,1},{1,0},{2,3},{3,2},{4,5},{5,4},{6,7},{7,6},{8,9},{9,8},{10,11... | collective-permute-start | bytes 2064392 | tf_op jit(solution)/shard_map/ppermute | solution.py:24
  159.6 3.6 %copy-start.6 = (f32[448,384]{1,0:T(8,128)S(1)}, f32[448,384]{1,0:T(8,128)}, u32[]{:S(2)}) copy-start(f32[448,384]{1,0:T(8,128)} %add.153) | copy-start | bytes 2064388
  163.1 3.0 %collective-permute-start.17 = (f32[448,384]{1,0:T(8,128)S(1)}, f32[448,384]{1,0:T(8,128)S(1)}, u32[]{:S(2)}, u32[]{:S(2)}) collective-permute-start(f32[448,384]{1,0:T(8,128)S(1)} %get-tuple-element.211), channel_id=1, source_target_pairs={{0,1},{1,0},{2,3},{3,2},{4,5},{5,4},{6,7},{7,6},{8,9},{9,8},{10,11... | collective-permute-start | bytes 2064392 | tf_op jit(solution)/shard_map/ppermute | solution.py:24
  163.2 18.2 %collective-permute-start.18 = (f32[448,384]{1,0:T(8,128)S(1)}, f32[448,384]{1,0:T(8,128)S(1)}, u32[]{:S(2)}, u32[]{:S(2)}) collective-permute-start(f32[448,384]{1,0:T(8,128)S(1)} %copy-done.6), channel_id=1, source_target_pairs={{0,8},{1,9},{2,10},{3,11},{4,12},{5,13},{6,14},{7,15},{8,0},{9,1},... | collective-permute-start | bytes 2064392 | tf_op jit(solution)/shard_map/ppermute | solution.py:24

commit v10 on v9

--- a/solution.py
+++ b/solution.py
@@ -61,13 +61,14 @@
     tail = jnp.where(line == 0, high, jnp.where(line == 1, middle, jnp.where(line == 2, rest - middle, 0.0)))
     there = across(own)
     beside = other_core(own)
+    there, tail = lax.optimization_barrier((there, tail.astype(jnp.bfloat16)))
     there_beside = other_core(there)
 
     def in_order(first, a, b):
         return jnp.where(first, jnp.concatenate([a, b], axis=1), jnp.concatenate([b, a], axis=1))
 
     mine = in_order(xh == 0, in_order(c == 0, own, beside), in_order(c == 0, there, there_beside))
-    mine = jnp.concatenate([mine, tail.astype(jnp.bfloat16)], axis=0)
+    mine = jnp.concatenate([mine, tail], axis=0)
 
     step_one = moved(
         mine,
@@ -76,8 +77,6 @@
     beyond = moved(mine, lambda z, xl, xh, y, c: (z, 1 - xl, 1, y, c) if (xh, c) == (0, 0) else None)
     swap_one = other_core(step_one)
     step_two = moved(step_one, lambda z, xl, xh, y, c: (z - 1 if c == 0 else z + 1, xl, xh, y, c))
-    swap_two = moved(swap_one, lambda z, xl, xh, y, c: (z - 1, xl, xh, y, 1) if c == 1 else None)
-    turned_one = moved(step_one, lambda z, xl, xh, y, c: (z, 1 - xl, 1, y, c) if (xh, c) == (0, 1) else None)
 
     def numer(a, b):
         a, b = a[:nvir], b[:nvir]
@@ -107,10 +106,16 @@
     rows_one = jnp.where(c == 0, mine, step_one)
     cols_one = jnp.where(c == 0, step_one, swap_one)
     step_zero = jnp.where(xh == 0, mine, beyond)
-    early = over_y(packed(numer(rows_one, cols_one), numer(mine, step_zero)))
+    parts = packed(numer(rows_one, cols_one), numer(mine, step_zero))
+    parts, swap_one, step_one_after = lax.optimization_barrier((parts, swap_one, step_one))
+    swap_two = moved(swap_one, lambda z, xl, xh, y, c: (z - 1, xl, xh, y, 1) if c == 1 else None)
+    turned_one = moved(step_one_after, lambda z, xl, xh, y, c: (z, 1 - xl, 1, y, c) if (xh, c) == (0, 1) else None)
+    early = over_y(parts)
     step_two, swap_one, swap_two, early = lax.optimization_barrier((step_two, swap_one, swap_two, early))
     rows_two = jnp.where(c == 0, swap_one, swap_two)
-    late = over_y(packed(numer(rows_two, step_two)))
+    parts = packed(numer(rows_two, step_two))
+    parts, early, step_two = lax.optimization_barrier((parts, early, step_two))
+    late = over_y(parts)
 
     turned_two = moved(step_two, lambda z, xl, xh, y, c: (z, 1 - xl, 1, y, c) if (xh, c) == (0, 1) else None)
     step_three = moved(
@@ -130,9 +135,9 @@
         lambda z, xl, xh, y, c: (z + 1, kind(xl, xh), xh, y, 1) if c == 1 else None,
     )
     second = jnp.where(c == 0, amps_one, second)
-    late, first, second, amps_zero = lax.optimization_barrier((late, first, second, amps_zero))
-    first, second = to_all(first, second)
-
+    late, first, second, amps_zero, turned_one, turned_two = lax.optimization_barrier(
+        (late, first, second, amps_zero, turned_one, turned_two)
+    )
     amps_two = amps(late[0], rows_two, step_two)
     third = moved(
         amps_two,
@@ -140,8 +145,7 @@
     )
     fourth = moved(amps_two, lambda z, xl, xh, y, c: (z + 2, kind(xl, xh), xh, y, 1) if c == 0 else None)
     fourth = jnp.where(c == 0, amps_zero, fourth)
-    third, fourth, first, second = lax.optimization_barrier((third, fourth, first, second))
-    third, fourth = to_all(third, fourth)
+    pieces = to_all(first, second, third, fourth)
 
     width = NC * depth
 
@@ -150,46 +154,30 @@
         at = (1 - h if half == 0 else h) * width
         return sum(dot(part, block[:nvir, at : at + width]) for part, block in zip(parts, blocks))
 
-    def both_halves(h, k, *blocks):
-        return lambda parts: (product(h, k, parts, blocks, 0), product(h, k, parts, blocks, 1))
-
     def one_half(h, k, half, *blocks):
-        def branch(parts, total):
-            total = total + product(h, k, parts, blocks, half)
+        def branch(parts):
+            total = product(h, k, parts, blocks, half)
             cut = [total[:, n * depth : (n + 1) * depth] for n in range(NC)]
             return cut[1 - k], cut[k]
 
         return branch
 
-    case = xh * NC + c
-    halves = lax.switch(
-        case,
-        [
-            both_halves(0, 0, step_two, step_one),
-            both_halves(0, 1, step_one, step_two),
-            both_halves(1, 0, step_two, step_one),
-            both_halves(1, 1, turned_one, turned_two),
-        ],
-        (first, second),
-    )
-
-    def finished(half, begun):
+    def finished(half, parts):
         sent, kept = lax.switch(
-            case,
+            xh * NC + c,
             [
-                one_half(0, 0, half, step_three, mine),
-                one_half(0, 1, half, turned_four, step_three),
-                one_half(1, 0, half, step_three, beyond),
-                one_half(1, 1, half, turned_four, step_three),
+                one_half(0, 0, half, step_two, step_one, step_three, mine),
+                one_half(0, 1, half, step_one, step_two, turned_four, step_three),
+                one_half(1, 0, half, step_two, step_one, step_three, beyond),
+                one_half(1, 1, half, turned_one, turned_two, turned_four, step_three),
             ],
-            (third, fourth),
-            begun,
+            parts,
         )
         return kept + other_core(sent)
 
-    theirs, begun = lax.optimization_barrier((finished(0, halves[0]), halves[1]))
+    theirs, pieces = lax.optimization_barrier((finished(0, pieces), pieces))
     got = across(theirs)
-    return (finished(1, begun) + got)[None]
+    return (finished(1, pieces) + got)[None]
 
 
 def solution(mesh):

time: 186 us -> 197 us (1.059)
  waiting for transfers between devices: 77.9 us -> 91.1 us
  matrix products: 23.8 us -> 20.5 us
  other arithmetic: 16.8 us -> 19.2 us
    all_to_all x2 -> x1, waiting for transfers between devices: 6.28 us -> 21.9 us  [to_all(): lax.all_to_all(jnp.broadcast_to(parts, (NY, *parts.shape)), 'y', 0, 0, ti...]
    all_to_all x2, waiting for transfers between devices: 27.9 us -> 21.2 us  [over_y(): return jnp.sum(lax.all_to_all(parts, 'y', 0, 0, tiled=True), axis=0)]
    ppermute x19, waiting for transfers between devices: 43.7 us -> 48 us  [moved(): return lax.ppermute(array, ALL, pairs)]
    dot_general x8, matrix products: 14.8 us -> 11 us  [dot_tn(): lax.dot_general(a, b, (((0,), (0,)), ((), ())), preferred_element_type=jn...]
    ppermute x19, starting transfers between devices: 40.8 us -> 43.7 us  [moved(): return lax.ppermute(array, ALL, pairs)]
    all_to_all x2 -> x1, starting transfers between devices: 7.19 us -> 4.41 us  [to_all(): lax.all_to_all(jnp.broadcast_to(parts, (NY, *parts.shape)), 'y', 0, 0, ti...]
  transfers between devices with their start and end apart: 23 -> 22, of which waited for: 9 -> 10; matrix products, arithmetic and copies ran while one was open for 18% -> 15% of each run, Pallas kernels for 0% -> 0%
where the time goes in v10:
time: 197 us; the launch traced here: 195 us
  waiting for transfers between devices  91.1 us (46%)
  starting transfers between devices  56.9 us (29%)
  matrix products  20.5 us (10%)
  other arithmetic  19.2 us (10%)
  local copies, waits for them, and re-layouts  3.76 us (2%)
  between operations  3.44 us (2%)
    ppermute x19, waiting for transfers between devices, moved(): return lax.ppermute(array, ALL, pairs)  48 us
    ppermute x19, starting transfers between devices, moved(): return lax.ppermute(array, ALL, pairs)  43.7 us
    all_to_all x1, waiting for transfers between devices, to_all(): lax.all_to_all(jnp.broadcast_to(parts, (NY, *parts.shape)), 'y', 0, 0, ti...  21.9 us
    all_to_all x2, waiting for transfers between devices, over_y(): return jnp.sum(lax.all_to_all(parts, 'y', 0, 0, tiled=True), axis=0)  21.2 us
    dot_general x8, matrix products, dot_tn(): lax.dot_general(a, b, (((0,), (0,)), ((), ())), preferred_element_type=jn...  11 us
    dot_general x6, matrix products, dot_nt(): lax.dot_general(a, b, (((1,), (1,)), ((), ())), preferred_element_type=jn...  9.5 us
    all_to_all x2, starting transfers between devices, over_y(): return jnp.sum(lax.all_to_all(parts, 'y', 0, 0, tiled=True), axis=0)  8.84 us
    all_to_all x1, starting transfers between devices, to_all(): lax.all_to_all(jnp.broadcast_to(parts, (NY, *parts.shape)), 'y', 0, 0, ti...  4.41 us
  transfers between devices with their start and end apart: 22, of which 10 were waited for; matrix products, arithmetic and copies ran while one was open for 15% of the time, Pallas kernels for 0%

profile of v10, /device:TPU:1, one launch (start us, length us, event | category | flops | bytes accessed | tf_op | source)
XLA Modules:
  0.0 195.2 jit_solution(16851572089303393521)
XLA Ops:
  0.0 3.6 %collective-permute-start.1 = (bf16[448,384]{1,0:T(8,128)(2,1)}, bf16[448,384]{1,0:T(8,128)(2,1)S(1)}, u32[]{:S(2)}, u32[]{:S(2)}) collective-permute-start(bf16[448,384]{1,0:T(8,128)(2,1)} %bitcast.112), channel_id=1, source_target_pairs={{0,8},{1,9},{2,10},{3,11},{4,12},{5,13},{6,14},{7,15},{8,0},{9,1},... | collective-permute-start | bytes 1032200 | tf_op jit(solution)/shard_map/ppermute | solution.py:24
  3.6 1.0 collective-permute-start
  7.6 1.3 select_convert_fusion
  8.9 1.7 collective-permute-done.1
  10.6 2.2 %collective-permute-start.2 = (bf16[448,384]{1,0:T(8,128)(2,1)S(1)}, bf16[448,384]{1,0:T(8,128)(2,1)S(1)}, u32[]{:S(2)}, u32[]{:S(2)}) collective-permute-start(bf16[448,384]{1,0:T(8,128)(2,1)S(1)} %collective-permute-done.1), channel_id=1, source_target_pairs={{0,1},{1,0},{2,3},{3,2},{4,5},{5,4},{6,7},{7,6},{8,9},{9,8},{10,11... | collective-permute-start | bytes 1032200 | tf_op jit(solution)/shard_map/ppermute | solution.py:24
  12.8 1.2 maximum_select_fusion.1
  14.2 0.3 maximum_select_fusion
  14.6 1.2 pad_maximum_fusion.1
  15.8 1.9 collective-permute-start.3
  17.7 1.8 collective-permute-start.6
  19.5 18.3 %collective-permute-done.3 = bf16[456,1536]{1,0:T(8,128)(2,1)S(1)} collective-permute-done((bf16[456,1536]{1,0:T(8,128)(2,1)}, bf16[456,1536]{1,0:T(8,128)(2,1)S(1)}, u32[]{:S(2)}, u32[]{:S(2)}) %collective-permute-start.3) | collective-permute-done | bytes 1400864 | tf_op jit(solution)/shard_map/ppermute | solution.py:24
  37.8 0.9 collective-permute-start.5
  38.8 2.8 %collective-permute-done.5 = bf16[456,1536]{1,0:T(8,128)(2,1)} collective-permute-done((bf16[456,1536]{1,0:T(8,128)(2,1)S(1)}, bf16[456,1536]{1,0:T(8,128)(2,1)}, u32[]{:S(2)}, u32[]{:S(2)}) %collective-permute-start.5) | collective-permute-done | bytes 1400864 | tf_op jit(solution)/shard_map/ppermute | solution.py:24
  41.6 2.2 %broadcast_select_fusion.3 = (bf16[456,1536]{1,0:T(8,128)(2,1)S(1)}, bf16[456,1536]{1,0:T(8,128)(2,1)S(1)}, bf16[456,1536]{1,0:T(8,128)(2,1)S(1)}) fusion(bf16[456,1536]{1,0:T(8,128)(2,1)S(1)} %collective-permute-done.3, pred[]{:T(512)S(6)} %eq.34, bf16[8,1536]{1,0:T(8,128)(2,1)S(1)} %select_convert_fusion, bf16[448,1536]{1,0:T(8,128)(2,1)S(1)} %maximum_select_fusion, ...), kind=kLoop, calls=%fused_computation.69 | loop fusion | flops 4902912 | bytes 9805826 | tf_op jit(solution)/shard_map/jit(_where)/select_n | solution.py:106
  43.8 0.9 fusion.61
  44.7 0.2 copy-done.6
  44.9 0.9 fusion.46
  45.8 0.9 fusion.58
  46.7 0.9 fusion.49
  47.6 1.5 pad_maximum_fusion
  49.1 5.2 %collective-permute-start.7 = (bf16[456,1536]{1,0:T(8,128)(2,1)}, bf16[456,1536]{1,0:T(8,128)(2,1)}, u32[]{:S(2)}, u32[]{:S(2)}) collective-permute-start(bf16[456,1536]{1,0:T(8,128)(2,1)} %collective-permute-done.5), channel_id=1, source_target_pairs={{1,225},{3,227},{5,229},{7,231},{9,233},{11,235},{13,237},{15,239}... | collective-permute-start | bytes 4202504 | tf_op jit(solution)/shard_map/ppermute | solution.py:24
  54.3 4.4 %all-to-all-start = ((f32[4,2,112,448]{3,2,1,0:T(8,128)}), f32[4,2,112,448]{3,2,1,0:T(8,128)}, u32[]{:S(2)}, u32[]{:S(2)}) async-start(f32[4,2,112,448]{3,2,1,0:T(8,128)} %pad_maximum_fusion), calls=%async_computation | async-start | bytes 3670016 | tf_op jit(solution)/shard_map/all_to_all | solution.py:89
  58.8 6.9 %collective-permute-start.10 = (bf16[456,1536]{1,0:T(8,128)(2,1)S(1)}, bf16[456,1536]{1,0:T(8,128)(2,1)}, u32[]{:S(2)}, u32[]{:S(2)}) collective-permute-start(bf16[456,1536]{1,0:T(8,128)(2,1)S(1)} %collective-permute-done.3), channel_id=1, source_target_pairs={{1,25},{3,27},{5,29},{7,31},{17,9},{19,11},{21,13},{23,15},{33,57}... | collective-permute-start | bytes 4202504 | tf_op jit(solution)/shard_map/ppermute | solution.py:24
  65.6 0.7 slice_convert_fusion.3
  66.3 0.7 slice_convert_fusion.1
  67.1 0.7 slice_convert_fusion.2
  67.8 12.5 %all-to-all-done = f32[4,2,112,448]{3,2,1,0:T(8,128)} async-done(((f32[4,2,112,448]{3,2,1,0:T(8,128)}), f32[4,2,112,448]{3,2,1,0:T(8,128)}, u32[]{:S(2)}, u32[]{:S(2)}) %all-to-all-start) | async-done | bytes 1605664 | tf_op jit(solution)/shard_map/all_to_all | solution.py:89
  80.3 1.8 reduce_sum.20
  82.1 1.5 broadcast_select_fusion.1
  83.6 2.7 %fusion.55 = f32[448,448]{1,0:T(8,128)S(1)} fusion(bf16[456,1536]{1,0:T(8,128)(2,1)S(1)} %broadcast_select_fusion.1, bf16[456,1536]{1,0:T(8,128)(2,1)} %collective-permute-done.4), kind=kOutput, calls=%fused_computation.80 | convolution fusion | flops 616562688 | bytes 3555328 | tf_op jit(solution)/shard_map/dot_general | solution.py:40
  86.3 3.2 %fusion.52 = f32[448,448]{1,0:T(8,128)} fusion(f32[448,448]{1,0:T(8,128)S(1)} %fusion.55, bf16[456,1536]{1,0:T(8,128)(2,1)S(1)} %broadcast_select_fusion.1, bf16[456,1536]{1,0:T(8,128)(2,1)} %collective-permute-done.4), kind=kOutput, calls=%fused_computation.79 | convolution fusion | flops 617451520 | bytes 4472832 | tf_op jit(solution)/shard_map/dot_general | solution.py:40
  89.5 7.8 %collective-permute-start.11 = (bf16[456,1536]{1,0:T(8,128)(2,1)}, bf16[456,1536]{1,0:T(8,128)(2,1)}, u32[]{:S(2)}, u32[]{:S(2)}) collective-permute-start(bf16[456,1536]{1,0:T(8,128)(2,1)} %collective-permute-done.4), channel_id=1, source_target_pairs={{1,25},{3,27},{5,29},{7,31},{17,9},{19,11},{21,13},{23,15},{33,57}... | collective-permute-start | bytes 4202504 | tf_op jit(solution)/shard_map/ppermute | solution.py:24
  97.5 1.9 collective-permute-start.9
  99.6 4.4 %all-to-all-start.1 = ((f32[4,1,112,448]{3,2,1,0:T(8,128)}), f32[4,1,112,448]{3,2,1,0:T(8,128)}, u32[]{:S(2)}, u32[]{:S(2)}) async-start(f32[4,1,112,448]{3,2,1,0:T(8,128)} %bitcast.109), calls=%async_computation.1 | async-start | bytes 1835008 | tf_op jit(solution)/shard_map/all_to_all | solution.py:89
  104.0 0.7 slice_convert_fusion
  104.7 0.7 slice_convert_fusion.4
  105.5 8.6 %all-to-all-done.1 = f32[4,1,112,448]{3,2,1,0:T(8,128)} async-done(((f32[4,1,112,448]{3,2,1,0:T(8,128)}), f32[4,1,112,448]{3,2,1,0:T(8,128)}, u32[]{:S(2)}, u32[]{:S(2)}) %all-to-all-start.1) | async-done | bytes 802848 | tf_op jit(solution)/shard_map/all_to_all | solution.py:89
  114.1 1.3 reduce_sum.21
  115.5 1.3 collective-permute-start.13
  116.8 6.8 %collective-permute-start.12 = (bf16[112,448]{1,0:T(8,128)(2,1)S(1)}, bf16[112,448]{1,0:T(8,128)(2,1)S(1)}, u32[]{:S(2)}, u32[]{:S(2)}) collective-permute-start(bf16[112,448]{1,0:T(8,128)(2,1)S(1)} %fusion.77), channel_id=1, source_target_pairs={{0,224},{1,193},{2,226},{3,195},{4,228},{5,197},{6,230},{7,199},{8... | collective-permute-start | bytes 301064 | tf_op jit(solution)/shard_map/ppermute | solution.py:24
  123.6 4.8 %collective-permute-done.13 = bf16[112,448]{1,0:T(8,128)(2,1)S(1)} collective-permute-done((bf16[112,448]{1,0:T(8,128)(2,1)S(1)}, bf16[112,448]{1,0:T(8,128)(2,1)S(1)}, u32[]{:S(2)}, u32[]{:S(2)}) %collective-permute-start.13) | collective-permute-done | bytes 100384 | tf_op jit(solution)/shard_map/ppermute | solution.py:24
  128.5 1.0 pad_maximum_fusion.2
  129.5 1.4 broadcast_in_dim.27
  130.9 4.4 %all-to-all-start.2 = ((bf16[4,4,112,448]{3,2,1,0:T(8,128)(2,1)}), bf16[4,4,112,448]{3,2,1,0:T(8,128)(2,1)}, u32[]{:S(2)}, u32[]{:S(2)}) async-start(bf16[4,4,112,448]{3,2,1,0:T(8,128)(2,1)} %broadcast_in_dim.27), calls=%async_computation.2 | async-start | bytes 3670016 | tf_op jit(solution)/shard_map/all_to_all | solution.py:103
  135.3 1.9 collective-permute-start.15
  137.3 21.9 %all-to-all-done.2 = bf16[4,4,112,448]{3,2,1,0:T(8,128)(2,1)} async-done(((bf16[4,4,112,448]{3,2,1,0:T(8,128)(2,1)}), bf16[4,4,112,448]{3,2,1,0:T(8,128)(2,1)}, u32[]{:S(2)}, u32[]{:S(2)}) %all-to-all-start.2) | async-done | bytes 1605664 | tf_op jit(solution)/shard_map/all_to_all | solution.py:103
  159.2 1.7 fusion.91
  160.9 0.2 copy-done.1
  161.1 5.6 %conditional.2 = (f32[448,384]{1,0:T(8,128)S(1)}, f32[448,384]{1,0:T(8,128)S(1)}) conditional(s32[]{:T(128)} %clamp.4, (bf16[456,1536]{1,0:T(8,128)(2,1)}, bf16[448,448]{1,0:T(8,128)(2,1)S(1)}, bf16[456,1536]{1,0:T(8,128)(2,1)S(1)}, bf16[448,448]{1,0:T(8,128)(2,1)S(1)}, bf16[456,1536]{1,0:T(8,128)(2,1)}, ...), branch_computations={%region_2.3_spmd, %region_3.4_spmd, %region_4.5_spmd, %region_5.6_... | conditional | flops 1234157568 | bytes 16859152 | solution.py:166
  161.1 0.6 fusion.8
  161.6 1.7 convolution_add_fusion.5
  163.3 1.6 convolution_add_fusion.4
  165.0 1.7 convolution_add_fusion.3
  166.8 2.1 %collective-permute-done.16 = f32[448,384]{1,0:T(8,128)S(1)} collective-permute-done((f32[448,384]{1,0:T(8,128)S(1)}, f32[448,384]{1,0:T(8,128)S(1)}, u32[]{:S(2)}, u32[]{:S(2)}) %collective-permute-start.16) | collective-permute-done | bytes 688160 | tf_op jit(solution)/shard_map/ppermute | solution.py:24
  169.0 0.9 add.154
  169.9 5.8 %conditional.3 = (f32[448,384]{1,0:T(8,128)S(1)}, f32[448,384]{1,0:T(8,128)S(1)}) conditional(s32[]{:T(128)} %clamp.4, (bf16[456,1536]{1,0:T(8,128)(2,1)}, bf16[448,448]{1,0:T(8,128)(2,1)S(1)}, bf16[456,1536]{1,0:T(8,128)(2,1)S(1)}, bf16[448,448]{1,0:T(8,128)(2,1)S(1)}, bf16[456,1536]{1,0:T(8,128)(2,1)}, ...), branch_computations={%region_6.7_spmd, %region_7.8_spmd, %region_8.9_spmd, %region_9.10... | conditional | flops 1234157568 | bytes 16859152 | solution.py:166
  169.9 0.6 fusion.28
  170.5 1.7 convolution_add_fusion.17
  172.1 1.6 convolution_add_fusion.16
  173.8 1.7 convolution_add_fusion.15
  175.9 0.3 collective-permute-start.18
  176.2 1.8 collective-permute-done.17
  178.0 16.3 %collective-permute-done.18 = f32[448,384]{1,0:T(8,128)S(1)} collective-permute-done((f32[448,384]{1,0:T(8,128)}, f32[448,384]{1,0:T(8,128)S(1)}, u32[]{:S(2)}, u32[]{:S(2)}) %collective-permute-start.18) | collective-permute-done | bytes 688160 | tf_op jit(solution)/shard_map/ppermute | solution.py:24
  194.3 0.9 add_bitcast_fusion
  (50 shorter events, 1.2 us)
Async XLA Ops:
  0.0 10.6 %collective-permute-start.1 = (bf16[448,384]{1,0:T(8,128)(2,1)}, bf16[448,384]{1,0:T(8,128)(2,1)S(1)}, u32[]{:S(2)}, u32[]{:S(2)}) collective-permute-start(bf16[448,384]{1,0:T(8,128)(2,1)} %bitcast.112), channel_id=1, source_target_pairs={{0,8},{1,9},{2,10},{3,11},{4,12},{5,13},{6,14},{7,15},{8,0},{9,1},... | collective-permute-start | bytes 1032200 | tf_op jit(solution)/shard_map/ppermute | solution.py:24
  3.6 9.2 %collective-permute-start = (bf16[448,384]{1,0:T(8,128)(2,1)}, bf16[448,384]{1,0:T(8,128)(2,1)S(1)}, u32[]{:S(2)}, u32[]{:S(2)}) collective-permute-start(bf16[448,384]{1,0:T(8,128)(2,1)} %bitcast.113), channel_id=1, source_target_pairs={{0,1},{1,0},{2,3},{3,2},{4,5},{5,4},{6,7},{7,6},{8,9},{9,8},{10,11... | collective-permute-start | bytes 1032200 | tf_op jit(solution)/shard_map/ppermute | solution.py:24
  10.6 3.5 %collective-permute-start.2 = (bf16[448,384]{1,0:T(8,128)(2,1)S(1)}, bf16[448,384]{1,0:T(8,128)(2,1)S(1)}, u32[]{:S(2)}, u32[]{:S(2)}) collective-permute-start(bf16[448,384]{1,0:T(8,128)(2,1)S(1)} %collective-permute-done.1), channel_id=1, source_target_pairs={{0,1},{1,0},{2,3},{3,2},{4,5},{5,4},{6,7},{7,6},{8,9},{9,8},{10,11... | collective-permute-start | bytes 1032200 | tf_op jit(solution)/shard_map/ppermute | solution.py:24
  14.6 24.1 %copy-start.8 = (f32[448]{0:T(512)S(1)}, f32[448]{0:T(512)}, u32[]{:S(2)}) copy-start(f32[448]{0:T(512)} %param.13) | copy-start | bytes 5380
  15.8 22.0 %collective-permute-start.3 = (bf16[456,1536]{1,0:T(8,128)(2,1)}, bf16[456,1536]{1,0:T(8,128)(2,1)S(1)}, u32[]{:S(2)}, u32[]{:S(2)}) collective-permute-start(bf16[456,1536]{1,0:T(8,128)(2,1)} %pad_maximum_fusion.1), channel_id=1, source_target_pairs={{0,224},{1,33},{2,226},{3,35},{4,228},{5,37},{6,230},{7,39},{8,248... | collective-permute-start | bytes 4202504 | tf_op jit(solution)/shard_map/ppermute | solution.py:24
  17.7 21.1 %collective-permute-start.6 = (bf16[456,1536]{1,0:T(8,128)(2,1)}, bf16[456,1536]{1,0:T(8,128)(2,1)}, u32[]{:S(2)}, u32[]{:S(2)}) collective-permute-start(bf16[456,1536]{1,0:T(8,128)(2,1)} %pad_maximum_fusion.1), channel_id=1, source_target_pairs={{0,24},{2,26},{4,28},{6,30},{16,8},{18,10},{20,12},{22,14},{32,56}... | collective-permute-start | bytes 4202504 | tf_op jit(solution)/shard_map/ppermute | solution.py:24
  37.8 21.0 %copy-start = (bf16[456,1536]{1,0:T(8,128)(2,1)}, bf16[456,1536]{1,0:T(8,128)(2,1)S(1)}, u32[]{:S(2)}) copy-start(bf16[456,1536]{1,0:T(8,128)(2,1)S(1)} %collective-permute-done.3) | copy-start | bytes 4202500
  37.8 3.8 %collective-permute-start.5 = (bf16[456,1536]{1,0:T(8,128)(2,1)S(1)}, bf16[456,1536]{1,0:T(8,128)(2,1)}, u32[]{:S(2)}, u32[]{:S(2)}) collective-permute-start(bf16[456,1536]{1,0:T(8,128)(2,1)S(1)} %collective-permute-done.3), channel_id=1, source_target_pairs={{0,1},{1,0},{2,3},{3,2},{4,5},{5,4},{6,7},{7,6},{8,9},{9,8},{10,11... | collective-permute-start | bytes 4202504 | tf_op jit(solution)/shard_map/ppermute | solution.py:24
  38.8 43.3 %collective-permute-start.4 = (bf16[456,1536]{1,0:T(8,128)(2,1)S(1)}, bf16[456,1536]{1,0:T(8,128)(2,1)}, u32[]{:S(2)}, u32[]{:S(2)}) collective-permute-start(bf16[456,1536]{1,0:T(8,128)(2,1)S(1)} %collective-permute-done.3), channel_id=1, source_target_pairs={{0,224},{1,33},{2,226},{3,35},{4,228},{5,37},{6,230},{7,39},{8,232... | collective-permute-start | bytes 4202504 | tf_op jit(solution)/shard_map/ppermute | solution.py:24
  43.8 1.1 copy-start.6
  43.8 2.0 %copy-start.4 = (bf16[456,1536]{1,0:T(8,128)(2,1)}, bf16[456,1536]{1,0:T(8,128)(2,1)S(1)}, u32[]{:S(2)}) copy-start(bf16[456,1536]{1,0:T(8,128)(2,1)S(1)} %get-tuple-element.273) | copy-start | bytes 4202500
  43.8 2.9 %copy-start.5 = (bf16[456,1536]{1,0:T(8,128)(2,1)}, bf16[456,1536]{1,0:T(8,128)(2,1)S(1)}, u32[]{:S(2)}) copy-start(bf16[456,1536]{1,0:T(8,128)(2,1)S(1)} %get-tuple-element.272) | copy-start | bytes 4202500
  49.1 33.0 %collective-permute-start.7 = (bf16[456,1536]{1,0:T(8,128)(2,1)}, bf16[456,1536]{1,0:T(8,128)(2,1)}, u32[]{:S(2)}, u32[]{:S(2)}) collective-permute-start(bf16[456,1536]{1,0:T(8,128)(2,1)} %collective-permute-done.5), channel_id=1, source_target_pairs={{1,225},{3,227},{5,229},{7,231},{9,233},{11,235},{13,237},{15,239}... | collective-permute-start | bytes 4202504 | tf_op jit(solution)/shard_map/ppermute | solution.py:24
  54.3 26.0 %all-to-all-start = ((f32[4,2,112,448]{3,2,1,0:T(8,128)}), f32[4,2,112,448]{3,2,1,0:T(8,128)}, u32[]{:S(2)}, u32[]{:S(2)}) async-start(f32[4,2,112,448]{3,2,1,0:T(8,128)} %pad_maximum_fusion), calls=%async_computation | async-start | bytes 3670016 | tf_op jit(solution)/shard_map/all_to_all | solution.py:89
  58.8 56.6 %collective-permute-start.10 = (bf16[456,1536]{1,0:T(8,128)(2,1)S(1)}, bf16[456,1536]{1,0:T(8,128)(2,1)}, u32[]{:S(2)}, u32[]{:S(2)}) collective-permute-start(bf16[456,1536]{1,0:T(8,128)(2,1)S(1)} %collective-permute-done.3), channel_id=1, source_target_pairs={{1,25},{3,27},{5,29},{7,31},{17,9},{19,11},{21,13},{23,15},{33,57}... | collective-permute-start | bytes 4202504 | tf_op jit(solution)/shard_map/ppermute | solution.py:24
  83.6 5.9 %copy-start.3 = (bf16[456,1536]{1,0:T(8,128)(2,1)}, bf16[456,1536]{1,0:T(8,128)(2,1)S(1)}, u32[]{:S(2)}) copy-start(bf16[456,1536]{1,0:T(8,128)(2,1)S(1)} %broadcast_select_fusion.1) | copy-start | bytes 4202500
  89.5 25.9 %collective-permute-start.11 = (bf16[456,1536]{1,0:T(8,128)(2,1)}, bf16[456,1536]{1,0:T(8,128)(2,1)}, u32[]{:S(2)}, u32[]{:S(2)}) collective-permute-start(bf16[456,1536]{1,0:T(8,128)(2,1)} %collective-permute-done.4), channel_id=1, source_target_pairs={{1,25},{3,27},{5,29},{7,31},{17,9},{19,11},{21,13},{23,15},{33,57}... | collective-permute-start | bytes 4202504 | tf_op jit(solution)/shard_map/ppermute | solution.py:24
  97.5 8.0 %collective-permute-start.9 = (bf16[112,448]{1,0:T(8,128)(2,1)S(1)}, bf16[112,448]{1,0:T(8,128)(2,1)S(1)}, u32[]{:S(2)}, u32[]{:S(2)}) collective-permute-start(bf16[112,448]{1,0:T(8,128)(2,1)S(1)} %get-tuple-element.275), channel_id=1, source_target_pairs={{1,33},{3,35},{5,37},{7,39},{9,57},{11,59},{13,61},{15,63},{17,49}... | collective-permute-start | bytes 301064 | tf_op jit(solution)/shard_map/ppermute | solution.py:24
  99.4 16.0 %collective-permute-start.8 = (bf16[112,448]{1,0:T(8,128)(2,1)S(1)}, bf16[112,448]{1,0:T(8,128)(2,1)S(1)}, u32[]{:S(2)}, u32[]{:S(2)}) collective-permute-start(bf16[112,448]{1,0:T(8,128)(2,1)S(1)} %get-tuple-element.275), channel_id=1, source_target_pairs={{0,33},{1,224},{2,35},{3,226},{4,37},{5,228},{6,39},{7,230},{8,57}... | collective-permute-start | bytes 301064 | tf_op jit(solution)/shard_map/ppermute | solution.py:24
  99.5 35.8 %collective-permute-start.14 = (bf16[456,1536]{1,0:T(8,128)(2,1)}, bf16[456,1536]{1,0:T(8,128)(2,1)}, u32[]{:S(2)}, u32[]{:S(2)}) collective-permute-start(bf16[456,1536]{1,0:T(8,128)(2,1)} %collective-permute-done.4), channel_id=1, source_target_pairs={{0,224},{1,33},{2,226},{3,35},{4,228},{5,37},{6,230},{7,39},{8,232... | collective-permute-start | bytes 4202504 | tf_op jit(solution)/shard_map/ppermute | solution.py:24
  99.6 14.5 %all-to-all-start.1 = ((f32[4,1,112,448]{3,2,1,0:T(8,128)}), f32[4,1,112,448]{3,2,1,0:T(8,128)}, u32[]{:S(2)}, u32[]{:S(2)}) async-start(f32[4,1,112,448]{3,2,1,0:T(8,128)} %bitcast.109), calls=%async_computation.1 | async-start | bytes 1835008 | tf_op jit(solution)/shard_map/all_to_all | solution.py:89
  115.4 8.2 %copy-start.7 = (bf16[112,448]{1,0:T(8,128)(2,1)}, bf16[112,448]{1,0:T(8,128)(2,1)S(1)}, u32[]{:S(2)}) copy-start(bf16[112,448]{1,0:T(8,128)(2,1)S(1)} %collective-permute-done.8) | copy-start | bytes 301060
  115.5 12.9 %collective-permute-start.13 = (bf16[112,448]{1,0:T(8,128)(2,1)S(1)}, bf16[112,448]{1,0:T(8,128)(2,1)S(1)}, u32[]{:S(2)}, u32[]{:S(2)}) collective-permute-start(bf16[112,448]{1,0:T(8,128)(2,1)S(1)} %fusion.77), channel_id=1, source_target_pairs={{0,65},{2,67},{4,69},{6,71},{8,89},{10,91},{12,93},{14,95},{16,81}... | collective-permute-start | bytes 301064 | tf_op jit(solution)/shard_map/ppermute | solution.py:24
  116.8 11.7 %collective-permute-start.12 = (bf16[112,448]{1,0:T(8,128)(2,1)S(1)}, bf16[112,448]{1,0:T(8,128)(2,1)S(1)}, u32[]{:S(2)}, u32[]{:S(2)}) collective-permute-start(bf16[112,448]{1,0:T(8,128)(2,1)S(1)} %fusion.77), channel_id=1, source_target_pairs={{0,224},{1,193},{2,226},{3,195},{4,228},{5,197},{6,230},{7,199},{8... | collective-permute-start | bytes 301064 | tf_op jit(solution)/shard_map/ppermute | solution.py:24
  130.9 28.3 %all-to-all-start.2 = ((bf16[4,4,112,448]{3,2,1,0:T(8,128)(2,1)}), bf16[4,4,112,448]{3,2,1,0:T(8,128)(2,1)}, u32[]{:S(2)}, u32[]{:S(2)}) async-start(bf16[4,4,112,448]{3,2,1,0:T(8,128)(2,1)} %broadcast_in_dim.27), calls=%async_computation.2 | async-start | bytes 3670016 | tf_op jit(solution)/shard_map/all_to_all | solution.py:103
  135.3 25.5 %collective-permute-start.15 = (bf16[456,1536]{1,0:T(8,128)(2,1)}, bf16[456,1536]{1,0:T(8,128)(2,1)}, u32[]{:S(2)}, u32[]{:S(2)}) collective-permute-start(bf16[456,1536]{1,0:T(8,128)(2,1)} %collective-permute-done.14), channel_id=1, source_target_pairs={{1,33},{3,35},{5,37},{7,39},{9,41},{11,43},{13,45},{15,47},{17,49}... | collective-permute-start | bytes 4202504 | tf_op jit(solution)/shard_map/ppermute | solution.py:24
  159.2 1.9 copy-start.1
  166.7 3.2 %copy-start.2 = (bf16[456,1536]{1,0:T(8,128)(2,1)S(1)}, bf16[456,1536]{1,0:T(8,128)(2,1)}, u32[]{:S(2)}) copy-start(bf16[456,1536]{1,0:T(8,128)(2,1)} %copy-done) | copy-start | bytes 4202500
  166.7 2.2 %collective-permute-start.16 = (f32[448,384]{1,0:T(8,128)S(1)}, f32[448,384]{1,0:T(8,128)S(1)}, u32[]{:S(2)}, u32[]{:S(2)}) collective-permute-start(f32[448,384]{1,0:T(8,128)S(1)} %get-tuple-element.243), channel_id=1, source_target_pairs={{0,1},{1,0},{2,3},{3,2},{4,5},{5,4},{6,7},{7,6},{8,9},{9,8},{10,11... | collective-permute-start | bytes 2064392 | tf_op jit(solution)/shard_map/ppermute | solution.py:24
  175.8 2.2 %collective-permute-start.17 = (f32[448,384]{1,0:T(8,128)S(1)}, f32[448,384]{1,0:T(8,128)S(1)}, u32[]{:S(2)}, u32[]{:S(2)}) collective-permute-start(f32[448,384]{1,0:T(8,128)S(1)} %get-tuple-element.249), channel_id=1, source_target_pairs={{0,1},{1,0},{2,3},{3,2},{4,5},{5,4},{6,7},{7,6},{8,9},{9,8},{10,11... | collective-permute-start | bytes 2064392 | tf_op jit(solution)/shard_map/ppermute | solution.py:24
  175.9 18.4 %collective-permute-start.18 = (f32[448,384]{1,0:T(8,128)}, f32[448,384]{1,0:T(8,128)S(1)}, u32[]{:S(2)}, u32[]{:S(2)}) collective-permute-start(f32[448,384]{1,0:T(8,128)} %add.154), channel_id=1, source_target_pairs={{0,8},{1,9},{2,10},{3,11},{4,12},{5,13},{6,14},{7,15},{8,0},{9,1},... | collective-permute-start | bytes 2064392 | tf_op jit(solution)/shard_map/ppermute | solution.py:24

commit v11 on v9

--- a/solution.py
+++ b/solution.py
@@ -61,13 +61,14 @@
     tail = jnp.where(line == 0, high, jnp.where(line == 1, middle, jnp.where(line == 2, rest - middle, 0.0)))
     there = across(own)
     beside = other_core(own)
+    there, tail = lax.optimization_barrier((there, tail.astype(jnp.bfloat16)))
     there_beside = other_core(there)
 
     def in_order(first, a, b):
         return jnp.where(first, jnp.concatenate([a, b], axis=1), jnp.concatenate([b, a], axis=1))
 
     mine = in_order(xh == 0, in_order(c == 0, own, beside), in_order(c == 0, there, there_beside))
-    mine = jnp.concatenate([mine, tail.astype(jnp.bfloat16)], axis=0)
+    mine = jnp.concatenate([mine, tail], axis=0)
 
     step_one = moved(
         mine,
@@ -76,8 +77,6 @@
     beyond = moved(mine, lambda z, xl, xh, y, c: (z, 1 - xl, 1, y, c) if (xh, c) == (0, 0) else None)
     swap_one = other_core(step_one)
     step_two = moved(step_one, lambda z, xl, xh, y, c: (z - 1 if c == 0 else z + 1, xl, xh, y, c))
-    swap_two = moved(swap_one, lambda z, xl, xh, y, c: (z - 1, xl, xh, y, 1) if c == 1 else None)
-    turned_one = moved(step_one, lambda z, xl, xh, y, c: (z, 1 - xl, 1, y, c) if (xh, c) == (0, 1) else None)
 
     def numer(a, b):
         a, b = a[:nvir], b[:nvir]
@@ -107,17 +106,14 @@
     rows_one = jnp.where(c == 0, mine, step_one)
     cols_one = jnp.where(c == 0, step_one, swap_one)
     step_zero = jnp.where(xh == 0, mine, beyond)
-    early = over_y(packed(numer(rows_one, cols_one), numer(mine, step_zero)))
+    parts = packed(numer(rows_one, cols_one), numer(mine, step_zero))
+    parts, swap_one, step_one_after = lax.optimization_barrier((parts, swap_one, step_one))
+    swap_two = moved(swap_one, lambda z, xl, xh, y, c: (z - 1, xl, xh, y, 1) if c == 1 else None)
+    turned_one = moved(step_one_after, lambda z, xl, xh, y, c: (z, 1 - xl, 1, y, c) if (xh, c) == (0, 1) else None)
+    early = over_y(parts)
     step_two, swap_one, swap_two, early = lax.optimization_barrier((step_two, swap_one, swap_two, early))
     rows_two = jnp.where(c == 0, swap_one, swap_two)
     late = over_y(packed(numer(rows_two, step_two)))
-
-    turned_two = moved(step_two, lambda z, xl, xh, y, c: (z, 1 - xl, 1, y, c) if (xh, c) == (0, 1) else None)
-    step_three = moved(
-        step_two,
-        lambda z, xl, xh, y, c: (z - 1, xl, xh, y, c) if c == 0 else (z + 1, kind(xl, xh), xh, y, c),
-    )
-    turned_four = moved(step_three, lambda z, xl, xh, y, c: (z + 1, xl, xh, y, 1) if c == 1 else None)
 
     amps_one = amps(early[0], rows_one, cols_one)
     amps_zero = amps(early[1], mine, step_zero)
@@ -130,7 +126,16 @@
         lambda z, xl, xh, y, c: (z + 1, kind(xl, xh), xh, y, 1) if c == 1 else None,
     )
     second = jnp.where(c == 0, amps_one, second)
-    late, first, second, amps_zero = lax.optimization_barrier((late, first, second, amps_zero))
+    late, first, second, amps_zero, step_two, turned_one = lax.optimization_barrier(
+        (late, first, second, amps_zero, step_two, turned_one)
+    )
+
+    turned_two = moved(step_two, lambda z, xl, xh, y, c: (z, 1 - xl, 1, y, c) if (xh, c) == (0, 1) else None)
+    step_three = moved(
+        step_two,
+        lambda z, xl, xh, y, c: (z - 1, xl, xh, y, c) if c == 0 else (z + 1, kind(xl, xh), xh, y, c),
+    )
+    turned_four = moved(step_three, lambda z, xl, xh, y, c: (z + 1, xl, xh, y, 1) if c == 1 else None)
     first, second = to_all(first, second)
 
     amps_two = amps(late[0], rows_two, step_two)
@@ -140,7 +145,7 @@
     )
     fourth = moved(amps_two, lambda z, xl, xh, y, c: (z + 2, kind(xl, xh), xh, y, 1) if c == 0 else None)
     fourth = jnp.where(c == 0, amps_zero, fourth)
-    third, fourth, first, second = lax.optimization_barrier((third, fourth, first, second))
+    third, fourth, first, second, turned_two = lax.optimization_barrier((third, fourth, first, second, turned_two))
     third, fourth = to_all(third, fourth)
 
     width = NC * depth

time: 186 us -> 186 us (level); the launches traced: 182 us -> 184 us
  starting transfers between devices: 55.7 us -> 61.4 us
    all_to_all x2, waiting for transfers between devices: 27.9 us -> 17.8 us  [over_y(): return jnp.sum(lax.all_to_all(parts, 'y', 0, 0, tiled=True), axis=0)]
    ppermute x19, waiting for transfers between devices: 43.7 us -> 50.9 us  [moved(): return lax.ppermute(array, ALL, pairs)]
    ppermute x19, starting transfers between devices: 40.8 us -> 45 us  [moved(): return lax.ppermute(array, ALL, pairs)]
    slice x2, local copies, waits for them, and re-layouts: 0.13 us -> 2.56 us  [to_all(): return [whole[:, n].reshape(nvir, nvir) for n in range(parts.shape[0])]]
    dot_general x8, matrix products: 14.8 us -> 12.6 us  [dot_tn(): lax.dot_general(a, b, (((0,), (0,)), ((), ())), preferred_element_type=jn...]
  transfers between devices with their start and end apart: 23 -> 23, of which waited for: 9 -> 12; matrix products, arithmetic and copies ran while one was open for 18% -> 18% of each run, Pallas kernels for 0% -> 0%
where the time goes in v11:
time: 186 us; the launch traced here: 184 us
  waiting for transfers between devices  76.1 us (41%)
  starting transfers between devices  61.4 us (33%)
  matrix products  22.1 us (12%)
  other arithmetic  15.5 us (8%)
  local copies, waits for them, and re-layouts  5.81 us (3%)
  between operations  3.25 us (2%)
    ppermute x19, waiting for transfers between devices, moved(): return lax.ppermute(array, ALL, pairs)  50.9 us
    ppermute x19, starting transfers between devices, moved(): return lax.ppermute(array, ALL, pairs)  45 us
    all_to_all x2, waiting for transfers between devices, over_y(): return jnp.sum(lax.all_to_all(parts, 'y', 0, 0, tiled=True), axis=0)  17.8 us
    dot_general x8, matrix products, dot_tn(): lax.dot_general(a, b, (((0,), (0,)), ((), ())), preferred_element_type=jn...  12.6 us
    dot_general x6, matrix products, dot_nt(): lax.dot_general(a, b, (((1,), (1,)), ((), ())), preferred_element_type=jn...  9.5 us
    all_to_all x2, starting transfers between devices, to_all(): lax.all_to_all(jnp.broadcast_to(parts, (NY, *parts.shape)), 'y', 0, 0, ti...  8.62 us
    all_to_all x2, starting transfers between devices, over_y(): return jnp.sum(lax.all_to_all(parts, 'y', 0, 0, tiled=True), axis=0)  7.83 us
    all_to_all x2, waiting for transfers between devices, to_all(): lax.all_to_all(jnp.broadcast_to(parts, (NY, *parts.shape)), 'y', 0, 0, ti...  7.41 us
  transfers between devices with their start and end apart: 23, of which 12 were waited for; matrix products, arithmetic and copies ran while one was open for 18% of the time, Pallas kernels for 0%

profile of v11, /device:TPU:1, one launch (start us, length us, event | category | flops | bytes accessed | tf_op | source)
XLA Modules:
  0.0 184.4 jit_solution(15395329264175411062)
XLA Ops:
  0.0 3.6 %collective-permute-start.1 = (bf16[448,384]{1,0:T(8,128)(2,1)}, bf16[448,384]{1,0:T(8,128)(2,1)S(1)}, u32[]{:S(2)}, u32[]{:S(2)}) collective-permute-start(bf16[448,384]{1,0:T(8,128)(2,1)} %bitcast.105), channel_id=1, source_target_pairs={{0,8},{1,9},{2,10},{3,11},{4,12},{5,13},{6,14},{7,15},{8,0},{9,1},... | collective-permute-start | bytes 1032200 | tf_op jit(solution)/shard_map/ppermute | solution.py:24
  3.6 1.0 collective-permute-start
  7.4 1.3 select_convert_fusion
  8.7 2.0 %collective-permute-done.1 = bf16[448,384]{1,0:T(8,128)(2,1)S(1)} collective-permute-done((bf16[448,384]{1,0:T(8,128)(2,1)}, bf16[448,384]{1,0:T(8,128)(2,1)S(1)}, u32[]{:S(2)}, u32[]{:S(2)}) %collective-permute-start.1) | collective-permute-done | bytes 344096 | tf_op jit(solution)/shard_map/ppermute | solution.py:24
  10.6 2.2 %collective-permute-start.2 = (bf16[448,384]{1,0:T(8,128)(2,1)S(1)}, bf16[448,384]{1,0:T(8,128)(2,1)S(1)}, u32[]{:S(2)}, u32[]{:S(2)}) collective-permute-start(bf16[448,384]{1,0:T(8,128)(2,1)S(1)} %collective-permute-done.1), channel_id=1, source_target_pairs={{0,1},{1,0},{2,3},{3,2},{4,5},{5,4},{6,7},{7,6},{8,9},{9,8},{10,11... | collective-permute-start | bytes 1032200 | tf_op jit(solution)/shard_map/ppermute | solution.py:24
  12.8 1.2 maximum_select_fusion.1
  14.6 1.3 pad_maximum_fusion.1
  15.9 1.9 %collective-permute-start.3 = (bf16[456,1536]{1,0:T(8,128)(2,1)}, bf16[456,1536]{1,0:T(8,128)(2,1)S(1)}, u32[]{:S(2)}, u32[]{:S(2)}) collective-permute-start(bf16[456,1536]{1,0:T(8,128)(2,1)} %pad_maximum_fusion.1), channel_id=1, source_target_pairs={{0,224},{1,33},{2,226},{3,35},{4,228},{5,37},{6,230},{7,39},{8,248... | collective-permute-start | bytes 4202504 | tf_op jit(solution)/shard_map/ppermute | solution.py:24
  17.8 1.8 collective-permute-start.6
  19.6 18.3 %collective-permute-done.3 = bf16[456,1536]{1,0:T(8,128)(2,1)S(1)} collective-permute-done((bf16[456,1536]{1,0:T(8,128)(2,1)}, bf16[456,1536]{1,0:T(8,128)(2,1)S(1)}, u32[]{:S(2)}, u32[]{:S(2)}) %collective-permute-start.3) | collective-permute-done | bytes 1400864 | tf_op jit(solution)/shard_map/ppermute | solution.py:24
  37.9 0.9 collective-permute-start.5
  38.9 2.8 %collective-permute-done.5 = bf16[456,1536]{1,0:T(8,128)(2,1)} collective-permute-done((bf16[456,1536]{1,0:T(8,128)(2,1)S(1)}, bf16[456,1536]{1,0:T(8,128)(2,1)}, u32[]{:S(2)}, u32[]{:S(2)}) %collective-permute-start.5) | collective-permute-done | bytes 1400864 | tf_op jit(solution)/shard_map/ppermute | solution.py:24
  41.7 2.2 %broadcast_select_fusion.3 = (bf16[456,1536]{1,0:T(8,128)(2,1)S(1)}, bf16[456,1536]{1,0:T(8,128)(2,1)S(1)}, bf16[456,1536]{1,0:T(8,128)(2,1)S(1)}) fusion(bf16[456,1536]{1,0:T(8,128)(2,1)S(1)} %collective-permute-done.3, pred[]{:T(512)S(6)} %eq.34, bf16[8,1536]{1,0:T(8,128)(2,1)S(1)} %select_convert_fusion, bf16[448,1536]{1,0:T(8,128)(2,1)S(1)} %maximum_select_fusion, ...), kind=kLoop, calls=%fused_computation.77 | loop fusion | flops 4902912 | bytes 9805826 | tf_op jit(solution)/shard_map/jit(_where)/select_n | solution.py:106
  44.0 0.9 fusion.77
  45.5 0.9 fusion.62
  46.4 0.9 fusion.74
  47.3 0.9 fusion.65
  48.2 1.4 pad_maximum_fusion
  49.6 5.2 %collective-permute-start.7 = (bf16[456,1536]{1,0:T(8,128)(2,1)}, bf16[456,1536]{1,0:T(8,128)(2,1)}, u32[]{:S(2)}, u32[]{:S(2)}) collective-permute-start(bf16[456,1536]{1,0:T(8,128)(2,1)} %collective-permute-done.5), channel_id=1, source_target_pairs={{1,225},{3,227},{5,229},{7,231},{9,233},{11,235},{13,237},{15,239}... | collective-permute-start | bytes 4202504 | tf_op jit(solution)/shard_map/ppermute | solution.py:24
  54.9 4.2 %all-to-all-start = ((f32[4,2,112,448]{3,2,1,0:T(8,128)}), f32[4,2,112,448]{3,2,1,0:T(8,128)S(1)}, u32[]{:S(2)}, u32[]{:S(2)}) async-start(f32[4,2,112,448]{3,2,1,0:T(8,128)} %pad_maximum_fusion), calls=%async_computation | async-start | bytes 3670016 | tf_op jit(solution)/shard_map/all_to_all | solution.py:89
  59.1 6.9 %collective-permute-start.10 = (bf16[456,1536]{1,0:T(8,128)(2,1)S(1)}, bf16[456,1536]{1,0:T(8,128)(2,1)}, u32[]{:S(2)}, u32[]{:S(2)}) collective-permute-start(bf16[456,1536]{1,0:T(8,128)(2,1)S(1)} %collective-permute-done.3), channel_id=1, source_target_pairs={{1,25},{3,27},{5,29},{7,31},{17,9},{19,11},{21,13},{23,15},{33,57}... | collective-permute-start | bytes 4202504 | tf_op jit(solution)/shard_map/ppermute | solution.py:24
  65.9 0.7 slice_convert_fusion.3
  66.7 0.7 slice_convert_fusion.1
  67.4 0.7 slice_convert_fusion.2
  68.1 12.7 %all-to-all-done = f32[4,2,112,448]{3,2,1,0:T(8,128)S(1)} async-done(((f32[4,2,112,448]{3,2,1,0:T(8,128)}), f32[4,2,112,448]{3,2,1,0:T(8,128)S(1)}, u32[]{:S(2)}, u32[]{:S(2)}) %all-to-all-start) | async-done | bytes 1605664 | tf_op jit(solution)/shard_map/all_to_all | solution.py:89
  80.7 1.0 reduce_sum.20
  81.8 1.5 broadcast_select_fusion.1
  83.3 2.7 %fusion.71 = f32[448,448]{1,0:T(8,128)S(1)} fusion(bf16[456,1536]{1,0:T(8,128)(2,1)S(1)} %broadcast_select_fusion.1, bf16[456,1536]{1,0:T(8,128)(2,1)} %collective-permute-done.4), kind=kOutput, calls=%fused_computation.88 | convolution fusion | flops 616562688 | bytes 3555328 | tf_op jit(solution)/shard_map/dot_general | solution.py:40
  86.0 3.2 %fusion.68 = f32[448,448]{1,0:T(8,128)} fusion(f32[448,448]{1,0:T(8,128)S(1)} %fusion.71, bf16[456,1536]{1,0:T(8,128)(2,1)S(1)} %broadcast_select_fusion.1, bf16[456,1536]{1,0:T(8,128)(2,1)} %collective-permute-done.4), kind=kOutput, calls=%fused_computation.87 | convolution fusion | flops 617451520 | bytes 4472832 | tf_op jit(solution)/shard_map/dot_general | solution.py:40
  89.2 3.6 %all-to-all-start.1 = ((f32[4,1,112,448]{3,2,1,0:T(8,128)}), f32[4,1,112,448]{3,2,1,0:T(8,128)S(1)}, u32[]{:S(2)}, u32[]{:S(2)}) async-start(f32[4,1,112,448]{3,2,1,0:T(8,128)} %bitcast.101), calls=%async_computation.1 | async-start | bytes 1835008 | tf_op jit(solution)/shard_map/all_to_all | solution.py:89
  93.0 1.9 %collective-permute-start.9 = (bf16[112,448]{1,0:T(8,128)(2,1)S(1)}, bf16[112,448]{1,0:T(8,128)(2,1)S(1)}, u32[]{:S(2)}, u32[]{:S(2)}) collective-permute-start(bf16[112,448]{1,0:T(8,128)(2,1)S(1)} %get-tuple-element.253), channel_id=1, source_target_pairs={{1,33},{3,35},{5,37},{7,39},{9,57},{11,59},{13,61},{15,63},{17,49}... | collective-permute-start | bytes 301064 | tf_op jit(solution)/shard_map/ppermute | solution.py:24
  95.0 0.7 collective-permute-start.8
  95.7 5.0 %collective-permute-done.9 = bf16[112,448]{1,0:T(8,128)(2,1)S(1)} collective-permute-done((bf16[112,448]{1,0:T(8,128)(2,1)S(1)}, bf16[112,448]{1,0:T(8,128)(2,1)S(1)}, u32[]{:S(2)}, u32[]{:S(2)}) %collective-permute-start.9) | collective-permute-done | bytes 100384 | tf_op jit(solution)/shard_map/ppermute | solution.py:24
  100.7 5.1 %all-to-all-done.1 = f32[4,1,112,448]{3,2,1,0:T(8,128)S(1)} async-done(((f32[4,1,112,448]{3,2,1,0:T(8,128)}), f32[4,1,112,448]{3,2,1,0:T(8,128)S(1)}, u32[]{:S(2)}, u32[]{:S(2)}) %all-to-all-start.1) | async-done | bytes 802848 | tf_op jit(solution)/shard_map/all_to_all | solution.py:89
  106.0 0.7 slice_convert_fusion
  106.7 9.1 %collective-permute-start.14 = (bf16[456,1536]{1,0:T(8,128)(2,1)}, bf16[456,1536]{1,0:T(8,128)(2,1)}, u32[]{:S(2)}, u32[]{:S(2)}) collective-permute-start(bf16[456,1536]{1,0:T(8,128)(2,1)} %collective-permute-done.4), channel_id=1, source_target_pairs={{1,25},{3,27},{5,29},{7,31},{17,9},{19,11},{21,13},{23,15},{33,57}... | collective-permute-start | bytes 4202504 | tf_op jit(solution)/shard_map/ppermute | solution.py:24
  115.8 1.0 broadcast_in_dim.30
  116.8 4.4 %all-to-all-start.2 = ((bf16[4,2,112,448]{3,2,1,0:T(8,128)(2,1)}), bf16[4,2,112,448]{3,2,1,0:T(8,128)(2,1)}, u32[]{:S(2)}, u32[]{:S(2)}) async-start(bf16[4,2,112,448]{3,2,1,0:T(8,128)(2,1)} %broadcast_in_dim.30), calls=%async_computation.2 | async-start | bytes 1835008 | tf_op jit(solution)/shard_map/all_to_all | solution.py:103
  121.2 0.7 slice_convert_fusion.4
  122.0 1.3 collective-permute-start.13
  123.3 1.2 collective-permute-start.12
  124.5 1.1 collective-permute-done.11
  125.6 1.9 %collective-permute-start.15 = (bf16[456,1536]{1,0:T(8,128)(2,1)}, bf16[456,1536]{1,0:T(8,128)(2,1)}, u32[]{:S(2)}, u32[]{:S(2)}) collective-permute-start(bf16[456,1536]{1,0:T(8,128)(2,1)} %collective-permute-done.11), channel_id=1, source_target_pairs={{1,33},{3,35},{5,37},{7,39},{9,41},{11,43},{13,45},{15,47},{17,49}... | collective-permute-start | bytes 4202504 | tf_op jit(solution)/shard_map/ppermute | solution.py:24
  127.5 3.9 %collective-permute-done.13 = bf16[112,448]{1,0:T(8,128)(2,1)S(1)} collective-permute-done((bf16[112,448]{1,0:T(8,128)(2,1)S(1)}, bf16[112,448]{1,0:T(8,128)(2,1)S(1)}, u32[]{:S(2)}, u32[]{:S(2)}) %collective-permute-start.13) | collective-permute-done | bytes 100384 | tf_op jit(solution)/shard_map/ppermute | solution.py:24
  131.4 0.6 all-to-all-done.2
  132.0 1.2 fusion.108
  133.3 1.1 broadcast_in_dim.31
  134.4 4.2 %all-to-all-start.3 = ((bf16[4,2,112,448]{3,2,1,0:T(8,128)(2,1)}), bf16[4,2,112,448]{3,2,1,0:T(8,128)(2,1)}, u32[]{:S(2)}, u32[]{:S(2)}) async-start(bf16[4,2,112,448]{3,2,1,0:T(8,128)(2,1)} %broadcast_in_dim.31), calls=%async_computation.3 | async-start | bytes 1835008 | tf_op jit(solution)/shard_map/all_to_all | solution.py:103
  138.6 5.5 %conditional.3 = (f32[448,768]{1,0:T(8,128)S(1)}, f32[448,768]{1,0:T(8,128)}) conditional(s32[]{:T(128)} %clamp.2, (bf16[456,1536]{1,0:T(8,128)(2,1)}, bf16[448,448]{1,0:T(8,128)(2,1)S(1)}, bf16[456,1536]{1,0:T(8,128)(2,1)S(1)}, bf16[448,448]{1,0:T(8,128)(2,1)S(1)}) %tuple.120, (bf16[456,1536]{1,0:T(8,128)(2,1)S(1)}, ...), branch_computations={%region_2.3_spmd, %region_3.4_spmd, %region_4.5_spmd, %region_5.6_... | conditional | flops 1233813504 | bytes 18219052 | solution.py:170
  139.2 0.6 fusion.10
  139.7 1.7 convolution_add_fusion.3
  141.4 2.7 %convolution_add_fusion.2 = f32[448,768]{1,0:T(8,128)} fusion(f32[448,768]{1,0:T(8,128)S(1)} %fusion.7, bf16[448,448]{1,0:T(8,128)(2,1)S(1)} %get-tuple-element.123, bf16[456,1536]{1,0:T(8,128)(2,1)} %get-tuple-element.124), kind=kOutput, calls=%fused_computation.8 | convolution fusion | flops 308625408 | bytes 3842048 | tf_op jit(solution)/shard_map/cond/branch_1_fun/dot_general | solution.py:48
  144.1 6.8 %all-to-all-done.3 = bf16[4,2,112,448]{3,2,1,0:T(8,128)(2,1)} async-done(((bf16[4,2,112,448]{3,2,1,0:T(8,128)(2,1)}), bf16[4,2,112,448]{3,2,1,0:T(8,128)(2,1)}, u32[]{:S(2)}, u32[]{:S(2)}) %all-to-all-start.3) | async-done | bytes 802848 | tf_op jit(solution)/shard_map/all_to_all | solution.py:103
  150.9 1.3 fusion.107
  152.5 3.6 %conditional.4 = (f32[448,384]{1,0:T(8,128)S(1)}, f32[448,384]{1,0:T(8,128)S(1)}) conditional(s32[]{:T(128)} %clamp.2, (bf16[456,1536]{1,0:T(8,128)(2,1)}, bf16[448,448]{1,0:T(8,128)(2,1)S(1)}, bf16[448,1536]{1,0:T(8,128)(2,1)S(1)}, bf16[448,448]{1,0:T(8,128)(2,1)S(1)}, f32[448,768]{1,0:T(8,128)S(1)}) %tuple.124, ...), branch_computations={%region_6.7_spmd, %region_7.8_spmd, %region_8.9_spmd, %region_9.10... | conditional | flops 617250816 | bytes 10493968 | solution.py:182
  152.5 1.6 fusion.30
  154.2 1.7 fusion.28
  156.3 2.1 %collective-permute-done.16 = f32[448,384]{1,0:T(8,128)S(1)} collective-permute-done((f32[448,384]{1,0:T(8,128)S(1)}, f32[448,384]{1,0:T(8,128)S(1)}, u32[]{:S(2)}, u32[]{:S(2)}) %collective-permute-start.16) | collective-permute-done | bytes 688160 | tf_op jit(solution)/shard_map/ppermute | solution.py:24
  158.5 3.9 %conditional.5 = (f32[448,384]{1,0:T(8,128)S(1)}, f32[448,384]{1,0:T(8,128)S(1)}) conditional(s32[]{:T(128)} %clamp.2, (bf16[456,1536]{1,0:T(8,128)(2,1)}, bf16[448,448]{1,0:T(8,128)(2,1)S(1)}, bf16[448,1536]{1,0:T(8,128)(2,1)S(1)}, bf16[448,448]{1,0:T(8,128)(2,1)S(1)}, f32[448,768]{1,0:T(8,128)}) %tuple.125, ...), branch_computations={%region_10.11_spmd, %region_11.12_spmd, %region_12.13_spmd, %regio... | conditional | flops 617250816 | bytes 10493968 | solution.py:182
  158.5 1.6 fusion.46
  160.2 2.1 %fusion.44 = f32[448,768]{1,0:T(8,128)S(1)} fusion(f32[448,768]{1,0:T(8,128)} %get-tuple-element.158, f32[448,768]{1,0:T(8,128)S(1)} %fusion.46, bf16[448,448]{1,0:T(8,128)(2,1)S(1)} %get-tuple-element.161, bf16[456,1536]{1,0:T(8,128)(2,1)} %get-tuple-element.162), kind=kOutput, calls=%fused_computation.58 | convolution fusion | flops 308969472 | bytes 5218304 | tf_op jit(solution)/shard_map/cond/branch_1_fun/dot_general | solution.py:48
  162.5 5.3 %collective-permute-start.18 = (f32[448,384]{1,0:T(8,128)S(1)}, f32[448,384]{1,0:T(8,128)S(1)}, u32[]{:S(2)}, u32[]{:S(2)}) collective-permute-start(f32[448,384]{1,0:T(8,128)S(1)} %add.153), channel_id=1, source_target_pairs={{0,8},{1,9},{2,10},{3,11},{4,12},{5,13},{6,14},{7,15},{8,0},{9,1},... | collective-permute-start | bytes 2064392 | tf_op jit(solution)/shard_map/ppermute | solution.py:24
  167.8 15.7 %collective-permute-done.18 = f32[448,384]{1,0:T(8,128)S(1)} collective-permute-done((f32[448,384]{1,0:T(8,128)S(1)}, f32[448,384]{1,0:T(8,128)S(1)}, u32[]{:S(2)}, u32[]{:S(2)}) %collective-permute-start.18) | collective-permute-done | bytes 688160 | tf_op jit(solution)/shard_map/ppermute | solution.py:24
  183.5 0.9 add_bitcast_fusion
  (56 shorter events, 3.1 us)
Async XLA Ops:
  0.0 10.6 %collective-permute-start.1 = (bf16[448,384]{1,0:T(8,128)(2,1)}, bf16[448,384]{1,0:T(8,128)(2,1)S(1)}, u32[]{:S(2)}, u32[]{:S(2)}) collective-permute-start(bf16[448,384]{1,0:T(8,128)(2,1)} %bitcast.105), channel_id=1, source_target_pairs={{0,8},{1,9},{2,10},{3,11},{4,12},{5,13},{6,14},{7,15},{8,0},{9,1},... | collective-permute-start | bytes 1032200 | tf_op jit(solution)/shard_map/ppermute | solution.py:24
  3.6 9.2 %collective-permute-start = (bf16[448,384]{1,0:T(8,128)(2,1)}, bf16[448,384]{1,0:T(8,128)(2,1)S(1)}, u32[]{:S(2)}, u32[]{:S(2)}) collective-permute-start(bf16[448,384]{1,0:T(8,128)(2,1)} %bitcast.106), channel_id=1, source_target_pairs={{0,1},{1,0},{2,3},{3,2},{4,5},{5,4},{6,7},{7,6},{8,9},{9,8},{10,11... | collective-permute-start | bytes 1032200 | tf_op jit(solution)/shard_map/ppermute | solution.py:24
  10.6 3.5 %collective-permute-start.2 = (bf16[448,384]{1,0:T(8,128)(2,1)S(1)}, bf16[448,384]{1,0:T(8,128)(2,1)S(1)}, u32[]{:S(2)}, u32[]{:S(2)}) collective-permute-start(bf16[448,384]{1,0:T(8,128)(2,1)S(1)} %collective-permute-done.1), channel_id=1, source_target_pairs={{0,1},{1,0},{2,3},{3,2},{4,5},{5,4},{6,7},{7,6},{8,9},{9,8},{10,11... | collective-permute-start | bytes 1032200 | tf_op jit(solution)/shard_map/ppermute | solution.py:24
  14.6 32.7 %copy-start = (bf16[448,1536]{1,0:T(8,128)(2,1)}, bf16[448,1536]{1,0:T(8,128)(2,1)S(1)}, u32[]{:S(2)}) copy-start(bf16[448,1536]{1,0:T(8,128)(2,1)S(1)} %maximum_select_fusion) | copy-start | bytes 4128772
  14.6 24.2 %copy-start.10 = (f32[448]{0:T(512)S(1)}, f32[448]{0:T(512)}, u32[]{:S(2)}) copy-start(f32[448]{0:T(512)} %param.17) | copy-start | bytes 5380
  15.9 22.0 %collective-permute-start.3 = (bf16[456,1536]{1,0:T(8,128)(2,1)}, bf16[456,1536]{1,0:T(8,128)(2,1)S(1)}, u32[]{:S(2)}, u32[]{:S(2)}) collective-permute-start(bf16[456,1536]{1,0:T(8,128)(2,1)} %pad_maximum_fusion.1), channel_id=1, source_target_pairs={{0,224},{1,33},{2,226},{3,35},{4,228},{5,37},{6,230},{7,39},{8,248... | collective-permute-start | bytes 4202504 | tf_op jit(solution)/shard_map/ppermute | solution.py:24
  17.8 21.1 %collective-permute-start.6 = (bf16[456,1536]{1,0:T(8,128)(2,1)}, bf16[456,1536]{1,0:T(8,128)(2,1)}, u32[]{:S(2)}, u32[]{:S(2)}) collective-permute-start(bf16[456,1536]{1,0:T(8,128)(2,1)} %pad_maximum_fusion.1), channel_id=1, source_target_pairs={{0,24},{2,26},{4,28},{6,30},{16,8},{18,10},{20,12},{22,14},{32,56}... | collective-permute-start | bytes 4202504 | tf_op jit(solution)/shard_map/ppermute | solution.py:24
  37.9 3.8 %collective-permute-start.5 = (bf16[456,1536]{1,0:T(8,128)(2,1)S(1)}, bf16[456,1536]{1,0:T(8,128)(2,1)}, u32[]{:S(2)}, u32[]{:S(2)}) collective-permute-start(bf16[456,1536]{1,0:T(8,128)(2,1)S(1)} %collective-permute-done.3), channel_id=1, source_target_pairs={{0,1},{1,0},{2,3},{3,2},{4,5},{5,4},{6,7},{7,6},{8,9},{9,8},{10,11... | collective-permute-start | bytes 4202504 | tf_op jit(solution)/shard_map/ppermute | solution.py:24
  38.9 42.9 %collective-permute-start.4 = (bf16[456,1536]{1,0:T(8,128)(2,1)S(1)}, bf16[456,1536]{1,0:T(8,128)(2,1)}, u32[]{:S(2)}, u32[]{:S(2)}) collective-permute-start(bf16[456,1536]{1,0:T(8,128)(2,1)S(1)} %collective-permute-done.3), channel_id=1, source_target_pairs={{0,224},{1,33},{2,226},{3,35},{4,228},{5,37},{6,230},{7,39},{8,232... | collective-permute-start | bytes 4202504 | tf_op jit(solution)/shard_map/ppermute | solution.py:24
  43.9 1.2 copy-start.7
  43.9 1.5 copy-start.9
  44.0 3.3 %copy-start.8 = (bf16[456,1536]{1,0:T(8,128)(2,1)}, bf16[456,1536]{1,0:T(8,128)(2,1)S(1)}, u32[]{:S(2)}) copy-start(bf16[456,1536]{1,0:T(8,128)(2,1)S(1)} %get-tuple-element.246) | copy-start | bytes 4202500
  49.6 32.1 %collective-permute-start.7 = (bf16[456,1536]{1,0:T(8,128)(2,1)}, bf16[456,1536]{1,0:T(8,128)(2,1)}, u32[]{:S(2)}, u32[]{:S(2)}) collective-permute-start(bf16[456,1536]{1,0:T(8,128)(2,1)} %collective-permute-done.5), channel_id=1, source_target_pairs={{1,225},{3,227},{5,229},{7,231},{9,233},{11,235},{13,237},{15,239}... | collective-permute-start | bytes 4202504 | tf_op jit(solution)/shard_map/ppermute | solution.py:24
  54.9 25.9 %all-to-all-start = ((f32[4,2,112,448]{3,2,1,0:T(8,128)}), f32[4,2,112,448]{3,2,1,0:T(8,128)S(1)}, u32[]{:S(2)}, u32[]{:S(2)}) async-start(f32[4,2,112,448]{3,2,1,0:T(8,128)} %pad_maximum_fusion), calls=%async_computation | async-start | bytes 3670016 | tf_op jit(solution)/shard_map/all_to_all | solution.py:89
  59.1 46.8 %collective-permute-start.10 = (bf16[456,1536]{1,0:T(8,128)(2,1)S(1)}, bf16[456,1536]{1,0:T(8,128)(2,1)}, u32[]{:S(2)}, u32[]{:S(2)}) collective-permute-start(bf16[456,1536]{1,0:T(8,128)(2,1)S(1)} %collective-permute-done.3), channel_id=1, source_target_pairs={{1,25},{3,27},{5,29},{7,31},{17,9},{19,11},{21,13},{23,15},{33,57}... | collective-permute-start | bytes 4202504 | tf_op jit(solution)/shard_map/ppermute | solution.py:24
  83.2 2.8 %copy-start.6 = (bf16[456,1536]{1,0:T(8,128)(2,1)}, bf16[456,1536]{1,0:T(8,128)(2,1)S(1)}, u32[]{:S(2)}) copy-start(bf16[456,1536]{1,0:T(8,128)(2,1)S(1)} %broadcast_select_fusion.1) | copy-start | bytes 4202500
  89.2 3.7 %copy-start.5 = (f32[2,112,448]{2,1,0:T(8,128)S(1)}, f32[2,112,448]{2,1,0:T(8,128)}, u32[]{:S(2)}) copy-start(f32[2,112,448]{2,1,0:T(8,128)} %reduce_sum.20) | copy-start | bytes 1204228
  89.2 16.5 %all-to-all-start.1 = ((f32[4,1,112,448]{3,2,1,0:T(8,128)}), f32[4,1,112,448]{3,2,1,0:T(8,128)S(1)}, u32[]{:S(2)}, u32[]{:S(2)}) async-start(f32[4,1,112,448]{3,2,1,0:T(8,128)} %bitcast.101), calls=%async_computation.1 | async-start | bytes 1835008 | tf_op jit(solution)/shard_map/all_to_all | solution.py:89
  93.0 7.6 %collective-permute-start.9 = (bf16[112,448]{1,0:T(8,128)(2,1)S(1)}, bf16[112,448]{1,0:T(8,128)(2,1)S(1)}, u32[]{:S(2)}, u32[]{:S(2)}) collective-permute-start(bf16[112,448]{1,0:T(8,128)(2,1)S(1)} %get-tuple-element.253), channel_id=1, source_target_pairs={{1,33},{3,35},{5,37},{7,39},{9,57},{11,59},{13,61},{15,63},{17,49}... | collective-permute-start | bytes 301064 | tf_op jit(solution)/shard_map/ppermute | solution.py:24
  95.0 10.9 %collective-permute-start.8 = (bf16[112,448]{1,0:T(8,128)(2,1)S(1)}, bf16[112,448]{1,0:T(8,128)(2,1)S(1)}, u32[]{:S(2)}, u32[]{:S(2)}) collective-permute-start(bf16[112,448]{1,0:T(8,128)(2,1)S(1)} %get-tuple-element.253), channel_id=1, source_target_pairs={{0,33},{1,224},{2,35},{3,226},{4,37},{5,228},{6,39},{7,230},{8,57}... | collective-permute-start | bytes 301064 | tf_op jit(solution)/shard_map/ppermute | solution.py:24
  105.9 19.7 %collective-permute-start.11 = (bf16[456,1536]{1,0:T(8,128)(2,1)}, bf16[456,1536]{1,0:T(8,128)(2,1)}, u32[]{:S(2)}, u32[]{:S(2)}) collective-permute-start(bf16[456,1536]{1,0:T(8,128)(2,1)} %collective-permute-done.4), channel_id=1, source_target_pairs={{0,224},{1,33},{2,226},{3,35},{4,228},{5,37},{6,230},{7,39},{8,232... | collective-permute-start | bytes 4202504 | tf_op jit(solution)/shard_map/ppermute | solution.py:24
  106.7 26.6 %collective-permute-start.14 = (bf16[456,1536]{1,0:T(8,128)(2,1)}, bf16[456,1536]{1,0:T(8,128)(2,1)}, u32[]{:S(2)}, u32[]{:S(2)}) collective-permute-start(bf16[456,1536]{1,0:T(8,128)(2,1)} %collective-permute-done.4), channel_id=1, source_target_pairs={{1,25},{3,27},{5,29},{7,31},{17,9},{19,11},{21,13},{23,15},{33,57}... | collective-permute-start | bytes 4202504 | tf_op jit(solution)/shard_map/ppermute | solution.py:24
  116.8 15.2 %all-to-all-start.2 = ((bf16[4,2,112,448]{3,2,1,0:T(8,128)(2,1)}), bf16[4,2,112,448]{3,2,1,0:T(8,128)(2,1)}, u32[]{:S(2)}, u32[]{:S(2)}) async-start(bf16[4,2,112,448]{3,2,1,0:T(8,128)(2,1)} %broadcast_in_dim.30), calls=%async_computation.2 | async-start | bytes 1835008 | tf_op jit(solution)/shard_map/all_to_all | solution.py:103
  122.0 9.3 %collective-permute-start.13 = (bf16[112,448]{1,0:T(8,128)(2,1)S(1)}, bf16[112,448]{1,0:T(8,128)(2,1)S(1)}, u32[]{:S(2)}, u32[]{:S(2)}) collective-permute-start(bf16[112,448]{1,0:T(8,128)(2,1)S(1)} %fusion.93), channel_id=1, source_target_pairs={{0,65},{2,67},{4,69},{6,71},{8,89},{10,91},{12,93},{14,95},{16,81}... | collective-permute-start | bytes 301064 | tf_op jit(solution)/shard_map/ppermute | solution.py:24
  123.3 9.9 %collective-permute-start.12 = (bf16[112,448]{1,0:T(8,128)(2,1)S(1)}, bf16[112,448]{1,0:T(8,128)(2,1)S(1)}, u32[]{:S(2)}, u32[]{:S(2)}) collective-permute-start(bf16[112,448]{1,0:T(8,128)(2,1)S(1)} %fusion.93), channel_id=1, source_target_pairs={{0,224},{1,193},{2,226},{3,195},{4,228},{5,197},{6,230},{7,199},{8... | collective-permute-start | bytes 301064 | tf_op jit(solution)/shard_map/ppermute | solution.py:24
  125.6 26.7 %collective-permute-start.15 = (bf16[456,1536]{1,0:T(8,128)(2,1)}, bf16[456,1536]{1,0:T(8,128)(2,1)}, u32[]{:S(2)}, u32[]{:S(2)}) collective-permute-start(bf16[456,1536]{1,0:T(8,128)(2,1)} %collective-permute-done.11), channel_id=1, source_target_pairs={{1,33},{3,35},{5,37},{7,39},{9,41},{11,43},{13,45},{15,47},{17,49}... | collective-permute-start | bytes 4202504 | tf_op jit(solution)/shard_map/ppermute | solution.py:24
  134.4 16.5 %all-to-all-start.3 = ((bf16[4,2,112,448]{3,2,1,0:T(8,128)(2,1)}), bf16[4,2,112,448]{3,2,1,0:T(8,128)(2,1)}, u32[]{:S(2)}, u32[]{:S(2)}) async-start(bf16[4,2,112,448]{3,2,1,0:T(8,128)(2,1)} %broadcast_in_dim.31), calls=%async_computation.3 | async-start | bytes 1835008 | tf_op jit(solution)/shard_map/all_to_all | solution.py:103
  150.9 1.6 copy-start.1
  156.2 2.3 %copy-start.2 = (bf16[448,1536]{1,0:T(8,128)(2,1)S(1)}, bf16[448,1536]{1,0:T(8,128)(2,1)}, u32[]{:S(2)}) copy-start(bf16[448,1536]{1,0:T(8,128)(2,1)} %copy-done) | copy-start | bytes 4128772
  156.2 2.2 %collective-permute-start.16 = (f32[448,384]{1,0:T(8,128)S(1)}, f32[448,384]{1,0:T(8,128)S(1)}, u32[]{:S(2)}, u32[]{:S(2)}) collective-permute-start(f32[448,384]{1,0:T(8,128)S(1)} %get-tuple-element.223), channel_id=1, source_target_pairs={{0,1},{1,0},{2,3},{3,2},{4,5},{5,4},{6,7},{7,6},{8,9},{9,8},{10,11... | collective-permute-start | bytes 2064392 | tf_op jit(solution)/shard_map/ppermute | solution.py:24
  162.4 5.4 %collective-permute-start.17 = (f32[448,384]{1,0:T(8,128)S(1)}, f32[448,384]{1,0:T(8,128)S(1)}, u32[]{:S(2)}, u32[]{:S(2)}) collective-permute-start(f32[448,384]{1,0:T(8,128)S(1)} %get-tuple-element.227), channel_id=1, source_target_pairs={{0,1},{1,0},{2,3},{3,2},{4,5},{5,4},{6,7},{7,6},{8,9},{9,8},{10,11... | collective-permute-start | bytes 2064392 | tf_op jit(solution)/shard_map/ppermute | solution.py:24
  162.5 21.0 %collective-permute-start.18 = (f32[448,384]{1,0:T(8,128)S(1)}, f32[448,384]{1,0:T(8,128)S(1)}, u32[]{:S(2)}, u32[]{:S(2)}) collective-permute-start(f32[448,384]{1,0:T(8,128)S(1)} %add.153), channel_id=1, source_target_pairs={{0,8},{1,9},{2,10},{3,11},{4,12},{5,13},{6,14},{7,15},{8,0},{9,1},... | collective-permute-start | bytes 2064392 | tf_op jit(solution)/shard_map/ppermute | solution.py:24

commit v12 on v11

--- a/solution.py
+++ b/solution.py
@@ -1,6 +1,8 @@
 import jax
 import jax.numpy as jnp
 from jax import lax
+from jax.experimental import pallas as pl
+from jax.experimental.pallas import tpu as pltpu
 from jax.sharding import Mesh, PartitionSpec as P
 
 NZ, NXL, NXH, NY, NC = 8, 2, 2, 4, 2
@@ -48,6 +50,58 @@
     return lax.dot_general(a, b, (((0,), (0,)), ((), ())), preferred_element_type=jnp.float32)
 
 
+def numer_into(a_ref, b_ref, out_ref, slot):
+    nvir = out_ref.shape[3]
+    a, b = a_ref[:nvir, :], b_ref[:nvir, :]
+    value = 2.0 * dot_nt(a, b) - dot_nt(b, a)
+    out_ref[:, slot] = value.reshape(out_ref.shape[0], out_ref.shape[2], nvir)
+
+
+def early_kernel(where_ref, mine_ref, one_ref, swap_ref, beyond_ref, out_ref):
+    @pl.when(where_ref[0] == 0)
+    def _():
+        numer_into(mine_ref, one_ref, out_ref, 0)
+
+    @pl.when(where_ref[0] != 0)
+    def _():
+        numer_into(one_ref, swap_ref, out_ref, 0)
+
+    @pl.when(where_ref[1] == 0)
+    def _():
+        numer_into(mine_ref, mine_ref, out_ref, 1)
+
+    @pl.when(where_ref[1] != 0)
+    def _():
+        numer_into(mine_ref, beyond_ref, out_ref, 1)
+
+
+def late_kernel(where_ref, swap_one_ref, swap_two_ref, two_ref, out_ref):
+    @pl.when(where_ref[0] == 0)
+    def _():
+        numer_into(swap_one_ref, two_ref, out_ref, 0)
+
+    @pl.when(where_ref[0] != 0)
+    def _():
+        numer_into(swap_two_ref, two_ref, out_ref, 0)
+
+
+def numerators(kernel, count, where, nvir, *blocks):
+    share = nvir // NY
+    width = blocks[0].shape[1]
+    return pl.pallas_call(
+        kernel,
+        out_shape=jax.ShapeDtypeStruct((NY, count, share, nvir), jnp.float32),
+        in_specs=[pl.BlockSpec(memory_space=pltpu.SMEM)] + [pl.BlockSpec(memory_space=pltpu.VMEM)] * len(blocks),
+        out_specs=pl.BlockSpec(memory_space=pltpu.VMEM),
+        cost_estimate=pl.CostEstimate(
+            flops=4 * count * nvir * nvir * width,
+            bytes_accessed=2 * len(blocks) * nvir * width + 4 * count * nvir * nvir,
+            transcendentals=0,
+        ),
+        compiler_params=pltpu.CompilerParams(vmem_limit_bytes=24 * 2**20),
+    )(where, *blocks)
+
+
 def local(three_index, occ_energy, vir_energy):
     own = three_index[0]
     nvir, depth = own.shape
@@ -78,13 +132,6 @@
     swap_one = other_core(step_one)
     step_two = moved(step_one, lambda z, xl, xh, y, c: (z - 1 if c == 0 else z + 1, xl, xh, y, c))
 
-    def numer(a, b):
-        a, b = a[:nvir], b[:nvir]
-        return dot_nt(a * jnp.bfloat16(2), b) - dot_nt(b, a)
-
-    def packed(*values):
-        return jnp.stack([value.reshape(NY, share, nvir) for value in values], axis=1)
-
     def over_y(parts):
         return jnp.sum(lax.all_to_all(parts, "y", 0, 0, tiled=True), axis=0)
 
@@ -96,27 +143,27 @@
     virs = vir_rows[:, None] + vir_energy[None, :]
 
     def amps(value, a, b):
-        return (value / (virs - energy(a) - energy(b))).astype(jnp.bfloat16)
+        return (value / (virs - a - b)).astype(jnp.bfloat16)
 
     def to_all(*parts):
         parts = jnp.stack(parts)
         whole = lax.all_to_all(jnp.broadcast_to(parts, (NY, *parts.shape)), "y", 0, 0, tiled=True)
         return [whole[:, n].reshape(nvir, nvir) for n in range(parts.shape[0])]
 
-    rows_one = jnp.where(c == 0, mine, step_one)
-    cols_one = jnp.where(c == 0, step_one, swap_one)
-    step_zero = jnp.where(xh == 0, mine, beyond)
-    parts = packed(numer(rows_one, cols_one), numer(mine, step_zero))
+    where = jnp.stack([c, xh])
+    parts = numerators(early_kernel, 2, where, nvir, mine, step_one, swap_one, beyond)
     parts, swap_one, step_one_after = lax.optimization_barrier((parts, swap_one, step_one))
     swap_two = moved(swap_one, lambda z, xl, xh, y, c: (z - 1, xl, xh, y, 1) if c == 1 else None)
     turned_one = moved(step_one_after, lambda z, xl, xh, y, c: (z, 1 - xl, 1, y, c) if (xh, c) == (0, 1) else None)
     early = over_y(parts)
     step_two, swap_one, swap_two, early = lax.optimization_barrier((step_two, swap_one, swap_two, early))
-    rows_two = jnp.where(c == 0, swap_one, swap_two)
-    late = over_y(packed(numer(rows_two, step_two)))
-
-    amps_one = amps(early[0], rows_one, cols_one)
-    amps_zero = amps(early[1], mine, step_zero)
+    late = over_y(numerators(late_kernel, 1, where, nvir, swap_one, swap_two, step_two))
+
+    mine_energy, one_energy, swap_energy = energy(mine), energy(step_one), energy(swap_one)
+    amps_one = amps(
+        early[0], jnp.where(c == 0, mine_energy, one_energy), jnp.where(c == 0, one_energy, swap_energy)
+    )
+    amps_zero = amps(early[1], mine_energy, jnp.where(xh == 0, mine_energy, energy(beyond)))
     first = moved(
         amps_one,
         lambda z, xl, xh, y, c: (z + 1, kind(xl, xh), xh, y, 1) if c == 0 else (z - 1, xl, xh, y, 0),
@@ -138,7 +185,7 @@
     turned_four = moved(step_three, lambda z, xl, xh, y, c: (z + 1, xl, xh, y, 1) if c == 1 else None)
     first, second = to_all(first, second)
 
-    amps_two = amps(late[0], rows_two, step_two)
+    amps_two = amps(late[0], jnp.where(c == 0, swap_energy, energy(swap_two)), energy(step_two))
     third = moved(
         amps_two,
         lambda z, xl, xh, y, c: (z - 1, xl, xh, y, 0) if c == 0 else (z - 2, xl, xh, y, 1),
@@ -148,53 +195,43 @@
     third, fourth, first, second, turned_two = lax.optimization_barrier((third, fourth, first, second, turned_two))
     third, fourth = to_all(third, fourth)
 
-    width = NC * depth
-
-    def product(h, k, parts, blocks, half):
-        dot = dot_nn if k == 0 else dot_tn
-        at = (1 - h if half == 0 else h) * width
-        return sum(dot(part, block[:nvir, at : at + width]) for part, block in zip(parts, blocks))
-
-    def both_halves(h, k, *blocks):
-        return lambda parts: (product(h, k, parts, blocks, 0), product(h, k, parts, blocks, 1))
-
-    def one_half(h, k, half, *blocks):
-        def branch(parts, total):
-            total = total + product(h, k, parts, blocks, half)
-            cut = [total[:, n * depth : (n + 1) * depth] for n in range(NC)]
-            return cut[1 - k], cut[k]
-
-        return branch
+    def product(dot, *blocks):
+        return lambda parts: sum(dot(part, block[:nvir]) for part, block in zip(parts, blocks))
 
     case = xh * NC + c
-    halves = lax.switch(
+    begun = lax.switch(
         case,
         [
-            both_halves(0, 0, step_two, step_one),
-            both_halves(0, 1, step_one, step_two),
-            both_halves(1, 0, step_two, step_one),
-            both_halves(1, 1, turned_one, turned_two),
+            product(dot_nn, step_two, step_one),
+            product(dot_tn, step_one, step_two),
+            product(dot_nn, step_two, step_one),
+            product(dot_tn, turned_one, turned_two),
         ],
         (first, second),
     )
 
-    def finished(half, begun):
-        sent, kept = lax.switch(
-            case,
-            [
-                one_half(0, 0, half, step_three, mine),
-                one_half(0, 1, half, turned_four, step_three),
-                one_half(1, 0, half, step_three, beyond),
-                one_half(1, 1, half, turned_four, step_three),
-            ],
-            (third, fourth),
-            begun,
-        )
-        return kept + other_core(sent)
-
-    theirs, begun = lax.optimization_barrier((finished(0, halves[0]), halves[1]))
-    got = across(theirs)
-    return (finished(1, begun) + got)[None]
+    def ending(h, k, dot, *blocks):
+        def branch(parts, total):
+            total = total + product(dot, *blocks)(parts)
+            cut = [total[:, n * depth : (n + 1) * depth] for n in range(NXH * NC)]
+            sent = jnp.concatenate([cut[NC * (1 - h) + 1 - k], cut[NC * h + 1 - k]], axis=1)
+            return sent, cut[NC * (1 - h) + k], cut[NC * h + k]
+
+        return branch
+
+    sent, theirs, ours = lax.switch(
+        case,
+        [
+            ending(0, 0, dot_nn, step_three, mine),
+            ending(0, 1, dot_tn, turned_four, step_three),
+            ending(1, 0, dot_nn, step_three, beyond),
+            ending(1, 1, dot_tn, turned_four, step_three),
+        ],
+        (third, fourth),
+        begun,
+    )
+    got = other_core(sent)
+    return (ours + got[:, depth:] + across(theirs + got[:, :depth]))[None]
 
 
 def solution(mesh):

time: 186 us -> 178 us (0.957)
  matrix products: 22.1 us -> 9.08 us
  Pallas kernels: 0 us -> 9.1 us
  other arithmetic: 15.5 us -> 9.84 us
  waiting for transfers between devices: 76.1 us -> 81.5 us
  starting transfers between devices: 61.4 us -> 57.9 us
    dot_general x6 -> x0, matrix products: 9.5 us -> none  [dot_nt(): lax.dot_general(a, b, (((1,), (1,)), ((), ())), preferred_element_type=jn...]
    pallas_call x0 -> x2, Pallas kernels: none -> 9.1 us  [numerators(): pl.pallas_call(kernel, out_shape=jax.ShapeDtypeStruct((NY, count, share,...]
    select_n x2 -> x4, other arithmetic: 3.7 us -> 0.04 us  [the longest x1 0.01 us: local(): jnp.where(c == 0, swap_energy, energy(swap_two))]
    dot_general x8 -> x4, matrix products: 12.6 us -> 9.08 us  [dot_tn(): lax.dot_general(a, b, (((0,), (0,)), ((), ())), preferred_element_type=jn...]
    ppermute x19 -> x18, starting transfers between devices: 45 us -> 41.5 us  [moved(): return lax.ppermute(array, ALL, pairs)]
    all_to_all x2, waiting for transfers between devices: 7.41 us -> 10.8 us  [to_all(): lax.all_to_all(jnp.broadcast_to(parts, (NY, *parts.shape)), 'y', 0, 0, ti...]
    reduce_sum x2, other arithmetic: 1.08 us -> 3.05 us  [over_y(): return jnp.sum(lax.all_to_all(parts, 'y', 0, 0, tiled=True), axis=0)]
    ppermute x19 -> x18, waiting for transfers between devices: 50.9 us -> 51.6 us  [moved(): return lax.ppermute(array, ALL, pairs)]
  transfers between devices with their start and end apart: 23 -> 22, of which waited for: 12 -> 11; matrix products, arithmetic and copies ran while one was open for 18% -> 9% of each run, Pallas kernels for 0% -> 5%
where the time goes in v12:
time: 178 us; the launch traced here: 176 us
  waiting for transfers between devices  81.5 us (46%)
  starting transfers between devices  57.9 us (33%)
  other arithmetic  9.84 us (6%)
  Pallas kernels  9.1 us (5%)
  matrix products  9.08 us (5%)
  local copies, waits for them, and re-layouts  5.06 us (3%)
  between operations  3.21 us (2%)
    ppermute x18, waiting for transfers between devices, moved(): return lax.ppermute(array, ALL, pairs)  51.6 us
    ppermute x18, starting transfers between devices, moved(): return lax.ppermute(array, ALL, pairs)  41.5 us
    all_to_all x2, waiting for transfers between devices, over_y(): return jnp.sum(lax.all_to_all(parts, 'y', 0, 0, tiled=True), axis=0)  19.2 us
    all_to_all x2, waiting for transfers between devices, to_all(): lax.all_to_all(jnp.broadcast_to(parts, (NY, *parts.shape)), 'y', 0, 0, ti...  10.8 us
    pallas_call x2, Pallas kernels, numerators(): pl.pallas_call(kernel, out_shape=jax.ShapeDtypeStruct((NY, count, share,...  9.1 us
    dot_general x4, matrix products, dot_tn(): lax.dot_general(a, b, (((0,), (0,)), ((), ())), preferred_element_type=jn...  9.08 us
    all_to_all x2, starting transfers between devices, over_y(): return jnp.sum(lax.all_to_all(parts, 'y', 0, 0, tiled=True), axis=0)  8.61 us
    all_to_all x2, starting transfers between devices, to_all(): lax.all_to_all(jnp.broadcast_to(parts, (NY, *parts.shape)), 'y', 0, 0, ti...  7.72 us
  transfers between devices with their start and end apart: 22, of which 11 were waited for; matrix products, arithmetic and copies ran while one was open for 9% of the time, Pallas kernels for 5%

profile of v12, /device:TPU:1, one launch (start us, length us, event | category | flops | bytes accessed | tf_op | source)
XLA Modules:
  0.0 175.7 jit_solution(4765980156112158405)
XLA Ops:
  0.0 3.6 %collective-permute-start.1 = (bf16[448,384]{1,0:T(8,128)(2,1)}, bf16[448,384]{1,0:T(8,128)(2,1)S(1)}, u32[]{:S(2)}, u32[]{:S(2)}) collective-permute-start(bf16[448,384]{1,0:T(8,128)(2,1)} %bitcast.71), channel_id=1, source_target_pairs={{0,8},{1,9},{2,10},{3,11},{4,12},{5,13},{6,14},{7,15},{8,0},{9,1},... | collective-permute-start | bytes 1032200 | tf_op jit(solution)/shard_map/ppermute | solution.py:26
  3.6 1.0 collective-permute-start
  7.4 1.3 select_convert_fusion
  8.7 2.0 %collective-permute-done.1 = bf16[448,384]{1,0:T(8,128)(2,1)S(1)} collective-permute-done((bf16[448,384]{1,0:T(8,128)(2,1)}, bf16[448,384]{1,0:T(8,128)(2,1)S(1)}, u32[]{:S(2)}, u32[]{:S(2)}) %collective-permute-start.1) | collective-permute-done | bytes 344096 | tf_op jit(solution)/shard_map/ppermute | solution.py:26
  10.6 2.2 %collective-permute-start.2 = (bf16[448,384]{1,0:T(8,128)(2,1)S(1)}, bf16[448,384]{1,0:T(8,128)(2,1)S(1)}, u32[]{:S(2)}, u32[]{:S(2)}) collective-permute-start(bf16[448,384]{1,0:T(8,128)(2,1)S(1)} %collective-permute-done.1), channel_id=1, source_target_pairs={{0,1},{1,0},{2,3},{3,2},{4,5},{5,4},{6,7},{7,6},{8,9},{9,8},{10,11... | collective-permute-start | bytes 1032200 | tf_op jit(solution)/shard_map/ppermute | solution.py:26
  12.8 1.2 maximum_select_fusion.1
  14.1 0.2 maximum_select_fusion.2
  14.2 0.3 maximum_select_fusion
  14.6 0.1 pad_maximum_fusion.4.mine_ref
  14.7 1.0 copy-done
  15.7 1.9 %collective-permute-start.3 = (bf16[456,1536]{1,0:T(8,128)(2,1)S(1)}, bf16[456,1536]{1,0:T(8,128)(2,1)}, u32[]{:S(2)}, u32[]{:S(2)}) collective-permute-start(bf16[456,1536]{1,0:T(8,128)(2,1)S(1)} %pad_maximum_fusion.4.mine_ref), channel_id=1, source_target_pairs={{0,224},{1,33},{2,226},{3,35},{4,228},{5,37},{6,230},{7,39},{8,248... | collective-permute-start | bytes 4202504 | tf_op jit(solution)/shard_map/ppermute | solution.py:26
  17.5 0.7 collective-permute-start.6
  18.3 19.3 %collective-permute-done.3.one_ref = bf16[456,1536]{1,0:T(8,128)(2,1)} collective-permute-done((bf16[456,1536]{1,0:T(8,128)(2,1)S(1)}, bf16[456,1536]{1,0:T(8,128)(2,1)}, u32[]{:S(2)}, u32[]{:S(2)}) %collective-permute-start.3) | collective-permute-done | bytes 1400864 | tf_op jit(solution)/shard_map/ppermute | solution.py:26
  37.6 0.7 collective-permute-start.5
  38.2 0.1 pad_add_fusion.where_ref
  38.3 2.9 %collective-permute-done.5.swap_ref.swap_one_ref = bf16[456,1536]{1,0:T(8,128)(2,1)S(1)} collective-permute-done((bf16[456,1536]{1,0:T(8,128)(2,1)}, bf16[456,1536]{1,0:T(8,128)(2,1)S(1)}, u32[]{:S(2)}, u32[]{:S(2)}) %collective-permute-start.5) | collective-permute-done | bytes 1400864 | tf_op jit(solution)/shard_map/ppermute | solution.py:26
  41.2 5.1 %shard_map.37 = f32[4,2,112,448]{3,2,1,0:T(8,128)} custom-call(s32[2]{0:T(128)S(1)} %pad_add_fusion.where_ref, bf16[456,1536]{1,0:T(8,128)(2,1)S(1)} %pad_maximum_fusion.4.mine_ref, bf16[456,1536]{1,0:T(8,128)(2,1)} %collective-permute-done.3.one_ref, bf16[456,1536]{1,0:T(8,128)(2,1)S(1)} %collective-permute-done.5.swap_ref.swap_one_ref, ...), custom_call_target="tpu_custom_call" | custom-call | flops 2466250752 | bytes 7110656 | tf_op jit(solution)/shard_map/pallas_call | solution.py:91
  46.3 5.5 %collective-permute-start.7 = (bf16[456,1536]{1,0:T(8,128)(2,1)S(1)}, bf16[456,1536]{1,0:T(8,128)(2,1)S(1)}, u32[]{:S(2)}, u32[]{:S(2)}) collective-permute-start(bf16[456,1536]{1,0:T(8,128)(2,1)S(1)} %collective-permute-done.5.swap_ref.swap_one_ref), channel_id=1, source_target_pairs={{1,225},{3,227},{5,229},{7,231},{9,233},{11,235},{13,237},{15,239}... | collective-permute-start | bytes 4202504 | tf_op jit(solution)/shard_map/ppermute | solution.py:26
  51.9 4.4 %all-to-all-start = ((f32[4,2,112,448]{3,2,1,0:T(8,128)}), f32[4,2,112,448]{3,2,1,0:T(8,128)}, u32[]{:S(2)}, u32[]{:S(2)}) async-start(f32[4,2,112,448]{3,2,1,0:T(8,128)} %shard_map.37), calls=%async_computation | async-start | bytes 3670016 | tf_op jit(solution)/shard_map/all_to_all | solution.py:136
  56.3 0.1 dynamic_slice.3
  56.4 0.7 slice_convert_fusion
  57.1 0.7 slice_convert_fusion.1
  57.8 7.1 %collective-permute-start.10 = (bf16[456,1536]{1,0:T(8,128)(2,1)}, bf16[456,1536]{1,0:T(8,128)(2,1)}, u32[]{:S(2)}, u32[]{:S(2)}) collective-permute-start(bf16[456,1536]{1,0:T(8,128)(2,1)} %collective-permute-done.3.one_ref), channel_id=1, source_target_pairs={{1,25},{3,27},{5,29},{7,31},{17,9},{19,11},{21,13},{23,15},{33,57}... | collective-permute-start | bytes 4202504 | tf_op jit(solution)/shard_map/ppermute | solution.py:26
  64.9 13.5 %all-to-all-done = f32[4,2,112,448]{3,2,1,0:T(8,128)} async-done(((f32[4,2,112,448]{3,2,1,0:T(8,128)}), f32[4,2,112,448]{3,2,1,0:T(8,128)}, u32[]{:S(2)}, u32[]{:S(2)}) %all-to-all-start) | async-done | bytes 1605664 | tf_op jit(solution)/shard_map/all_to_all | solution.py:136
  78.5 1.8 %reduce_sum.20 = f32[2,112,448]{2,1,0:T(8,128)S(1)} reduce(f32[4,2,112,448]{3,2,1,0:T(8,128)} %all-to-all-done, f32[]{:T(128)} %constant.7.clone.1), dimensions={0}, to_apply=%region_0.1 | reduce | flops 301056 | bytes 2007044 | tf_op jit(solution)/shard_map/reduce_sum | solution.py:136
  80.3 4.0 %shard_map.38 = f32[4,1,112,448]{3,2,1,0:T(8,128)} custom-call(s32[2]{0:T(128)S(1)} %pad_add_fusion.where_ref, bf16[456,1536]{1,0:T(8,128)(2,1)S(1)} %collective-permute-done.5.swap_ref.swap_one_ref, bf16[456,1536]{1,0:T(8,128)(2,1)S(1)} %collective-permute-done.7.swap_two_ref, bf16[456,1536]{1,0:T(8,128)(2,1)} %collective-permute-done.4.two_ref), custom_call_target="tpu_custom_call" | custom-call | flops 1233125376 | bytes 4931584 | tf_op jit(solution)/shard_map/pallas_call | solution.py:91
  84.3 4.2 %all-to-all-start.1 = ((f32[4,1,112,448]{3,2,1,0:T(8,128)}), f32[4,1,112,448]{3,2,1,0:T(8,128)}, u32[]{:S(2)}, u32[]{:S(2)}) async-start(f32[4,1,112,448]{3,2,1,0:T(8,128)} %shard_map.38), calls=%async_computation.1 | async-start | bytes 1835008 | tf_op jit(solution)/shard_map/all_to_all | solution.py:136
  88.5 0.1 fusion.36
  88.7 1.9 %collective-permute-start.9 = (bf16[112,448]{1,0:T(8,128)(2,1)S(1)}, bf16[112,448]{1,0:T(8,128)(2,1)S(1)}, u32[]{:S(2)}, u32[]{:S(2)}) collective-permute-start(bf16[112,448]{1,0:T(8,128)(2,1)S(1)} %get-tuple-element.191), channel_id=1, source_target_pairs={{1,33},{3,35},{5,37},{7,39},{9,57},{11,59},{13,61},{15,63},{17,49}... | collective-permute-start | bytes 301064 | tf_op jit(solution)/shard_map/ppermute | solution.py:26
  90.6 0.8 collective-permute-start.8
  91.5 4.8 %collective-permute-done.9 = bf16[112,448]{1,0:T(8,128)(2,1)S(1)} collective-permute-done((bf16[112,448]{1,0:T(8,128)(2,1)S(1)}, bf16[112,448]{1,0:T(8,128)(2,1)S(1)}, u32[]{:S(2)}, u32[]{:S(2)}) %collective-permute-start.9) | collective-permute-done | bytes 100384 | tf_op jit(solution)/shard_map/ppermute | solution.py:26
  96.3 5.6 %all-to-all-done.1 = f32[4,1,112,448]{3,2,1,0:T(8,128)} async-done(((f32[4,1,112,448]{3,2,1,0:T(8,128)}), f32[4,1,112,448]{3,2,1,0:T(8,128)}, u32[]{:S(2)}, u32[]{:S(2)}) %all-to-all-start.1) | async-done | bytes 802848 | tf_op jit(solution)/shard_map/all_to_all | solution.py:136
  101.9 1.3 reduce_sum.21
  103.2 0.1 collective-permute-start.11
  103.3 7.1 %collective-permute-start.14 = (bf16[456,1536]{1,0:T(8,128)(2,1)}, bf16[456,1536]{1,0:T(8,128)(2,1)}, u32[]{:S(2)}, u32[]{:S(2)}) collective-permute-start(bf16[456,1536]{1,0:T(8,128)(2,1)} %collective-permute-done.4.two_ref), channel_id=1, source_target_pairs={{1,25},{3,27},{5,29},{7,31},{17,9},{19,11},{21,13},{23,15},{33,57}... | collective-permute-start | bytes 4202504 | tf_op jit(solution)/shard_map/ppermute | solution.py:26
  110.5 1.0 broadcast_in_dim.30
  111.5 3.5 %all-to-all-start.2 = ((bf16[4,2,112,448]{3,2,1,0:T(8,128)(2,1)}), bf16[4,2,112,448]{3,2,1,0:T(8,128)(2,1)S(1)}, u32[]{:S(2)}, u32[]{:S(2)}) async-start(bf16[4,2,112,448]{3,2,1,0:T(8,128)(2,1)} %broadcast_in_dim.30), calls=%async_computation.2 | async-start | bytes 1835008 | tf_op jit(solution)/shard_map/all_to_all | solution.py:150
  115.0 0.7 slice_convert_fusion.2
  115.7 0.1 fusion.35
  115.8 1.3 collective-permute-start.13
  117.1 3.0 %collective-permute-start.12 = (bf16[112,448]{1,0:T(8,128)(2,1)S(1)}, bf16[112,448]{1,0:T(8,128)(2,1)S(1)}, u32[]{:S(2)}, u32[]{:S(2)}) collective-permute-start(bf16[112,448]{1,0:T(8,128)(2,1)S(1)} %fusion.35), channel_id=1, source_target_pairs={{0,224},{1,193},{2,226},{3,195},{4,228},{5,197},{6,230},{7,199},{8... | collective-permute-start | bytes 301064 | tf_op jit(solution)/shard_map/ppermute | solution.py:26
  120.2 3.6 %collective-permute-done.11 = bf16[456,1536]{1,0:T(8,128)(2,1)} collective-permute-done((bf16[456,1536]{1,0:T(8,128)(2,1)}, bf16[456,1536]{1,0:T(8,128)(2,1)}, u32[]{:S(2)}, u32[]{:S(2)}) %collective-permute-start.11) | collective-permute-done | bytes 1400864 | tf_op jit(solution)/shard_map/ppermute | solution.py:26
  123.8 1.9 %collective-permute-start.15 = (bf16[456,1536]{1,0:T(8,128)(2,1)}, bf16[456,1536]{1,0:T(8,128)(2,1)}, u32[]{:S(2)}, u32[]{:S(2)}) collective-permute-start(bf16[456,1536]{1,0:T(8,128)(2,1)} %collective-permute-done.11), channel_id=1, source_target_pairs={{1,33},{3,35},{5,37},{7,39},{9,41},{11,43},{13,45},{15,47},{17,49}... | collective-permute-start | bytes 4202504 | tf_op jit(solution)/shard_map/ppermute | solution.py:26
  125.7 1.4 all-to-all-done.2
  127.1 0.1 fusion.43
  127.2 1.1 broadcast_in_dim.31
  128.3 4.2 %all-to-all-start.3 = ((bf16[4,2,112,448]{3,2,1,0:T(8,128)(2,1)}), bf16[4,2,112,448]{3,2,1,0:T(8,128)(2,1)}, u32[]{:S(2)}, u32[]{:S(2)}) async-start(bf16[4,2,112,448]{3,2,1,0:T(8,128)(2,1)} %broadcast_in_dim.31), calls=%async_computation.3 | async-start | bytes 1835008 | tf_op jit(solution)/shard_map/all_to_all | solution.py:150
  132.6 4.5 %conditional.2 = (f32[448,1536]{1,0:T(8,128)S(1)}) conditional(s32[]{:T(128)} %clamp.4, (bf16[456,1536]{1,0:T(8,128)(2,1)}, bf16[448,448]{1,0:T(8,128)(2,1)S(1)}, bf16[456,1536]{1,0:T(8,128)(2,1)}, bf16[448,448]{1,0:T(8,128)(2,1)S(1)}) %tuple.85, (bf16[456,1536]{1,0:T(8,128)(2,1)}, bf16[448,448]{1,0:T(8,128)(2,1)S(1)}, ...), branch_computations={%region_2.3_spmd, %region_3.4_spmd, %region_4.5_spmd, %region_5.6_... | conditional | flops 1233813504 | bytes 11812872 | solution.py:202
  132.6 2.2 %fusion.4 = f32[448,1536]{1,0:T(8,128)S(1)} fusion(bf16[448,448]{1,0:T(8,128)(2,1)S(1)} %get-tuple-element.86, bf16[456,1536]{1,0:T(8,128)(2,1)} %get-tuple-element.87), kind=kOutput, calls=%fused_computation.6 | convolution fusion | flops 616562688 | bytes 4530176 | tf_op jit(solution)/shard_map/cond/branch_1_fun/dot_general | solution.py:50
  134.8 2.3 %convolution_add_fusion.1 = f32[448,1536]{1,0:T(8,128)S(1)} fusion(f32[448,1536]{1,0:T(8,128)S(1)} %fusion.4, bf16[448,448]{1,0:T(8,128)(2,1)S(1)} %get-tuple-element.88, bf16[456,1536]{1,0:T(8,128)(2,1)} %get-tuple-element.89), kind=kOutput, calls=%fused_computation.4 | convolution fusion | flops 617250816 | bytes 7282688 | tf_op jit(solution)/shard_map/cond/branch_1_fun/dot_general | solution.py:50
  137.1 9.4 %all-to-all-done.3 = bf16[4,2,112,448]{3,2,1,0:T(8,128)(2,1)} async-done(((bf16[4,2,112,448]{3,2,1,0:T(8,128)(2,1)}), bf16[4,2,112,448]{3,2,1,0:T(8,128)(2,1)}, u32[]{:S(2)}, u32[]{:S(2)}) %all-to-all-start.3) | async-done | bytes 802848 | tf_op jit(solution)/shard_map/all_to_all | solution.py:150
  146.5 1.3 fusion.42
  147.9 0.3 copy-done.1
  148.1 4.9 %conditional.3 = (f32[448,768]{1,0:T(8,128)S(1)}, f32[448,384]{1,0:T(8,128)S(1)}, f32[448,384]{1,0:T(8,128)S(1)}) conditional(s32[]{:T(128)} %clamp.4, (bf16[456,1536]{1,0:T(8,128)(2,1)}, bf16[448,448]{1,0:T(8,128)(2,1)S(1)}, bf16[448,448]{1,0:T(8,128)(2,1)S(1)}, bf16[448,1536]{1,0:T(8,128)(2,1)S(1)}, ...), branch_computations={%region_6.7_spmd, %region_7.8_spmd, %region_8.9_spmd, %region_9.10... | conditional | flops 1234845696 | bytes 28483636 | solution.py:222
  148.1 2.2 %fusion.17 = f32[448,1536]{1,0:T(8,128)S(1)} fusion(bf16[448,448]{1,0:T(8,128)(2,1)S(1)} %get-tuple-element.104, bf16[456,1536]{1,0:T(8,128)(2,1)} %get-tuple-element.105), kind=kOutput, calls=%fused_computation.25 | convolution fusion | flops 616562688 | bytes 4530176 | tf_op jit(solution)/shard_map/cond/branch_1_fun/dot_general | solution.py:50
  150.4 2.3 %fusion.15 = f32[448,1536]{1,0:T(8,128)S(1)} fusion(f32[448,1536]{1,0:T(8,128)S(1)} %get-tuple-element.103, f32[448,1536]{1,0:T(8,128)S(1)} %fusion.17, bf16[448,448]{1,0:T(8,128)(2,1)S(1)} %get-tuple-element.106, bf16[456,1536]{1,0:T(8,128)(2,1)} %get-tuple-element.107), kind=kOutput, calls=%fused_computation.22 | convolution fusion | flops 617938944 | bytes 10035200 | tf_op jit(solution)/shard_map/cond/branch_1_fun/dot_general | solution.py:50
  152.7 0.2 fusion.39
  152.9 0.1 pad_maximum_fusion.1
  153.0 0.1 collective-permute-start.16
  153.1 3.1 %collective-permute-done.16 = f32[448,768]{1,0:T(8,128)S(1)} collective-permute-done((f32[448,768]{1,0:T(8,128)S(1)}, f32[448,768]{1,0:T(8,128)S(1)}, u32[]{:S(2)}, u32[]{:S(2)}) %collective-permute-start.16) | collective-permute-done | bytes 1376288 | tf_op jit(solution)/shard_map/ppermute | solution.py:26
  156.2 0.1 slice_add_fusion
  156.3 2.6 %collective-permute-start.17 = (f32[448,384]{1,0:T(8,128)S(1)}, f32[448,384]{1,0:T(8,128)S(1)}, u32[]{:S(2)}, u32[]{:S(2)}) collective-permute-start(f32[448,384]{1,0:T(8,128)S(1)} %slice_add_fusion), channel_id=1, source_target_pairs={{0,8},{1,9},{2,10},{3,11},{4,12},{5,13},{6,14},{7,15},{8,0},{9,1},... | collective-permute-start | bytes 2064392 | tf_op jit(solution)/shard_map/ppermute | solution.py:26
  158.9 15.9 %collective-permute-done.17 = f32[448,384]{1,0:T(8,128)S(1)} collective-permute-done((f32[448,384]{1,0:T(8,128)S(1)}, f32[448,384]{1,0:T(8,128)S(1)}, u32[]{:S(2)}, u32[]{:S(2)}) %collective-permute-start.17) | collective-permute-done | bytes 688160 | tf_op jit(solution)/shard_map/ppermute | solution.py:26
  174.8 0.9 fusion.28
  (32 shorter events, 0.2 us)
Async XLA Ops:
  0.0 10.6 %collective-permute-start.1 = (bf16[448,384]{1,0:T(8,128)(2,1)}, bf16[448,384]{1,0:T(8,128)(2,1)S(1)}, u32[]{:S(2)}, u32[]{:S(2)}) collective-permute-start(bf16[448,384]{1,0:T(8,128)(2,1)} %bitcast.71), channel_id=1, source_target_pairs={{0,8},{1,9},{2,10},{3,11},{4,12},{5,13},{6,14},{7,15},{8,0},{9,1},... | collective-permute-start | bytes 1032200 | tf_op jit(solution)/shard_map/ppermute | solution.py:26
  3.6 9.2 %collective-permute-start = (bf16[448,384]{1,0:T(8,128)(2,1)}, bf16[448,384]{1,0:T(8,128)(2,1)S(1)}, u32[]{:S(2)}, u32[]{:S(2)}) collective-permute-start(bf16[448,384]{1,0:T(8,128)(2,1)} %bitcast.72), channel_id=1, source_target_pairs={{0,1},{1,0},{2,3},{3,2},{4,5},{5,4},{6,7},{7,6},{8,9},{9,8},{10,11... | collective-permute-start | bytes 1032200 | tf_op jit(solution)/shard_map/ppermute | solution.py:26
  10.6 3.5 %collective-permute-start.2 = (bf16[448,384]{1,0:T(8,128)(2,1)S(1)}, bf16[448,384]{1,0:T(8,128)(2,1)S(1)}, u32[]{:S(2)}, u32[]{:S(2)}) collective-permute-start(bf16[448,384]{1,0:T(8,128)(2,1)S(1)} %collective-permute-done.1), channel_id=1, source_target_pairs={{0,1},{1,0},{2,3},{3,2},{4,5},{5,4},{6,7},{7,6},{8,9},{9,8},{10,11... | collective-permute-start | bytes 1032200 | tf_op jit(solution)/shard_map/ppermute | solution.py:26
  14.6 1.1 copy-start
  15.7 21.9 %collective-permute-start.3 = (bf16[456,1536]{1,0:T(8,128)(2,1)S(1)}, bf16[456,1536]{1,0:T(8,128)(2,1)}, u32[]{:S(2)}, u32[]{:S(2)}) collective-permute-start(bf16[456,1536]{1,0:T(8,128)(2,1)S(1)} %pad_maximum_fusion.4.mine_ref), channel_id=1, source_target_pairs={{0,224},{1,33},{2,226},{3,35},{4,228},{5,37},{6,230},{7,39},{8,248... | collective-permute-start | bytes 4202504 | tf_op jit(solution)/shard_map/ppermute | solution.py:26
  17.5 20.8 %collective-permute-start.6 = (bf16[456,1536]{1,0:T(8,128)(2,1)S(1)}, bf16[456,1536]{1,0:T(8,128)(2,1)S(1)}, u32[]{:S(2)}, u32[]{:S(2)}) collective-permute-start(bf16[456,1536]{1,0:T(8,128)(2,1)S(1)} %pad_maximum_fusion.4.mine_ref), channel_id=1, source_target_pairs={{0,24},{2,26},{4,28},{6,30},{16,8},{18,10},{20,12},{22,14},{32,56}... | collective-permute-start | bytes 4202504 | tf_op jit(solution)/shard_map/ppermute | solution.py:26
  37.6 3.7 %collective-permute-start.5 = (bf16[456,1536]{1,0:T(8,128)(2,1)}, bf16[456,1536]{1,0:T(8,128)(2,1)S(1)}, u32[]{:S(2)}, u32[]{:S(2)}) collective-permute-start(bf16[456,1536]{1,0:T(8,128)(2,1)} %collective-permute-done.3.one_ref), channel_id=1, source_target_pairs={{0,1},{1,0},{2,3},{3,2},{4,5},{5,4},{6,7},{7,6},{8,9},{9,8},{10,11... | collective-permute-start | bytes 4202504 | tf_op jit(solution)/shard_map/ppermute | solution.py:26
  38.3 41.9 %collective-permute-start.4 = (bf16[456,1536]{1,0:T(8,128)(2,1)}, bf16[456,1536]{1,0:T(8,128)(2,1)}, u32[]{:S(2)}, u32[]{:S(2)}) collective-permute-start(bf16[456,1536]{1,0:T(8,128)(2,1)} %collective-permute-done.3.one_ref), channel_id=1, source_target_pairs={{0,224},{1,33},{2,226},{3,35},{4,228},{5,37},{6,230},{7,39},{8,232... | collective-permute-start | bytes 4202504 | tf_op jit(solution)/shard_map/ppermute | solution.py:26
  38.3 8.0 %copy-start.2 = (bf16[456,1536]{1,0:T(8,128)(2,1)}, bf16[456,1536]{1,0:T(8,128)(2,1)S(1)}, u32[]{:S(2)}) copy-start(bf16[456,1536]{1,0:T(8,128)(2,1)S(1)} %collective-permute-done.6.beyond_ref) | copy-start | bytes 4202500
  46.3 10.0 %copy-start.4 = (f32[448]{0:T(512)S(1)}, f32[448]{0:T(512)}, u32[]{:S(2)}) copy-start(f32[448]{0:T(512)} %param.13) | copy-start | bytes 5380
  46.3 33.9 %collective-permute-start.7 = (bf16[456,1536]{1,0:T(8,128)(2,1)S(1)}, bf16[456,1536]{1,0:T(8,128)(2,1)S(1)}, u32[]{:S(2)}, u32[]{:S(2)}) collective-permute-start(bf16[456,1536]{1,0:T(8,128)(2,1)S(1)} %collective-permute-done.5.swap_ref.swap_one_ref), channel_id=1, source_target_pairs={{1,225},{3,227},{5,229},{7,231},{9,233},{11,235},{13,237},{15,239}... | collective-permute-start | bytes 4202504 | tf_op jit(solution)/shard_map/ppermute | solution.py:26
  51.9 26.6 %all-to-all-start = ((f32[4,2,112,448]{3,2,1,0:T(8,128)}), f32[4,2,112,448]{3,2,1,0:T(8,128)}, u32[]{:S(2)}, u32[]{:S(2)}) async-start(f32[4,2,112,448]{3,2,1,0:T(8,128)} %shard_map.37), calls=%async_computation | async-start | bytes 3670016 | tf_op jit(solution)/shard_map/all_to_all | solution.py:136
  57.8 45.4 %collective-permute-start.10 = (bf16[456,1536]{1,0:T(8,128)(2,1)}, bf16[456,1536]{1,0:T(8,128)(2,1)}, u32[]{:S(2)}, u32[]{:S(2)}) collective-permute-start(bf16[456,1536]{1,0:T(8,128)(2,1)} %collective-permute-done.3.one_ref), channel_id=1, source_target_pairs={{1,25},{3,27},{5,29},{7,31},{17,9},{19,11},{21,13},{23,15},{33,57}... | collective-permute-start | bytes 4202504 | tf_op jit(solution)/shard_map/ppermute | solution.py:26
  84.3 17.6 %all-to-all-start.1 = ((f32[4,1,112,448]{3,2,1,0:T(8,128)}), f32[4,1,112,448]{3,2,1,0:T(8,128)}, u32[]{:S(2)}, u32[]{:S(2)}) async-start(f32[4,1,112,448]{3,2,1,0:T(8,128)} %shard_map.38), calls=%async_computation.1 | async-start | bytes 1835008 | tf_op jit(solution)/shard_map/all_to_all | solution.py:136
  88.7 7.5 %collective-permute-start.9 = (bf16[112,448]{1,0:T(8,128)(2,1)S(1)}, bf16[112,448]{1,0:T(8,128)(2,1)S(1)}, u32[]{:S(2)}, u32[]{:S(2)}) collective-permute-start(bf16[112,448]{1,0:T(8,128)(2,1)S(1)} %get-tuple-element.191), channel_id=1, source_target_pairs={{1,33},{3,35},{5,37},{7,39},{9,57},{11,59},{13,61},{15,63},{17,49}... | collective-permute-start | bytes 301064 | tf_op jit(solution)/shard_map/ppermute | solution.py:26
  90.6 12.6 %collective-permute-start.8 = (bf16[112,448]{1,0:T(8,128)(2,1)S(1)}, bf16[112,448]{1,0:T(8,128)(2,1)S(1)}, u32[]{:S(2)}, u32[]{:S(2)}) collective-permute-start(bf16[112,448]{1,0:T(8,128)(2,1)S(1)} %get-tuple-element.191), channel_id=1, source_target_pairs={{0,33},{1,224},{2,35},{3,226},{4,37},{5,228},{6,39},{7,230},{8,57}... | collective-permute-start | bytes 301064 | tf_op jit(solution)/shard_map/ppermute | solution.py:26
  103.2 20.6 %collective-permute-start.11 = (bf16[456,1536]{1,0:T(8,128)(2,1)}, bf16[456,1536]{1,0:T(8,128)(2,1)}, u32[]{:S(2)}, u32[]{:S(2)}) collective-permute-start(bf16[456,1536]{1,0:T(8,128)(2,1)} %collective-permute-done.4.two_ref), channel_id=1, source_target_pairs={{0,224},{1,33},{2,226},{3,35},{4,228},{5,37},{6,230},{7,39},{8,232... | collective-permute-start | bytes 4202504 | tf_op jit(solution)/shard_map/ppermute | solution.py:26
  103.3 23.9 %collective-permute-start.14 = (bf16[456,1536]{1,0:T(8,128)(2,1)}, bf16[456,1536]{1,0:T(8,128)(2,1)}, u32[]{:S(2)}, u32[]{:S(2)}) collective-permute-start(bf16[456,1536]{1,0:T(8,128)(2,1)} %collective-permute-done.4.two_ref), channel_id=1, source_target_pairs={{1,25},{3,27},{5,29},{7,31},{17,9},{19,11},{21,13},{23,15},{33,57}... | collective-permute-start | bytes 4202504 | tf_op jit(solution)/shard_map/ppermute | solution.py:26
  111.5 15.6 %all-to-all-start.2 = ((bf16[4,2,112,448]{3,2,1,0:T(8,128)(2,1)}), bf16[4,2,112,448]{3,2,1,0:T(8,128)(2,1)S(1)}, u32[]{:S(2)}, u32[]{:S(2)}) async-start(bf16[4,2,112,448]{3,2,1,0:T(8,128)(2,1)} %broadcast_in_dim.30), calls=%async_computation.2 | async-start | bytes 1835008 | tf_op jit(solution)/shard_map/all_to_all | solution.py:150
  115.8 9.9 %collective-permute-start.13 = (bf16[112,448]{1,0:T(8,128)(2,1)S(1)}, bf16[112,448]{1,0:T(8,128)(2,1)S(1)}, u32[]{:S(2)}, u32[]{:S(2)}) collective-permute-start(bf16[112,448]{1,0:T(8,128)(2,1)S(1)} %fusion.35), channel_id=1, source_target_pairs={{0,65},{2,67},{4,69},{6,71},{8,89},{10,91},{12,93},{14,95},{16,81}... | collective-permute-start | bytes 301064 | tf_op jit(solution)/shard_map/ppermute | solution.py:26
  117.1 10.1 %collective-permute-start.12 = (bf16[112,448]{1,0:T(8,128)(2,1)S(1)}, bf16[112,448]{1,0:T(8,128)(2,1)S(1)}, u32[]{:S(2)}, u32[]{:S(2)}) collective-permute-start(bf16[112,448]{1,0:T(8,128)(2,1)S(1)} %fusion.35), channel_id=1, source_target_pairs={{0,224},{1,193},{2,226},{3,195},{4,228},{5,197},{6,230},{7,199},{8... | collective-permute-start | bytes 301064 | tf_op jit(solution)/shard_map/ppermute | solution.py:26
  123.8 24.1 %collective-permute-start.15 = (bf16[456,1536]{1,0:T(8,128)(2,1)}, bf16[456,1536]{1,0:T(8,128)(2,1)}, u32[]{:S(2)}, u32[]{:S(2)}) collective-permute-start(bf16[456,1536]{1,0:T(8,128)(2,1)} %collective-permute-done.11), channel_id=1, source_target_pairs={{1,33},{3,35},{5,37},{7,39},{9,41},{11,43},{13,45},{15,47},{17,49}... | collective-permute-start | bytes 4202504 | tf_op jit(solution)/shard_map/ppermute | solution.py:26
  128.3 18.2 %all-to-all-start.3 = ((bf16[4,2,112,448]{3,2,1,0:T(8,128)(2,1)}), bf16[4,2,112,448]{3,2,1,0:T(8,128)(2,1)}, u32[]{:S(2)}, u32[]{:S(2)}) async-start(bf16[4,2,112,448]{3,2,1,0:T(8,128)(2,1)} %broadcast_in_dim.31), calls=%async_computation.3 | async-start | bytes 1835008 | tf_op jit(solution)/shard_map/all_to_all | solution.py:150
  146.5 1.6 copy-start.1
  153.0 3.2 %collective-permute-start.16 = (f32[448,768]{1,0:T(8,128)S(1)}, f32[448,768]{1,0:T(8,128)S(1)}, u32[]{:S(2)}, u32[]{:S(2)}) collective-permute-start(f32[448,768]{1,0:T(8,128)S(1)} %get-tuple-element.162), channel_id=1, source_target_pairs={{0,1},{1,0},{2,3},{3,2},{4,5},{5,4},{6,7},{7,6},{8,9},{9,8},{10,11... | collective-permute-start | bytes 4128776 | tf_op jit(solution)/shard_map/ppermute | solution.py:26
  156.3 18.5 %collective-permute-start.17 = (f32[448,384]{1,0:T(8,128)S(1)}, f32[448,384]{1,0:T(8,128)S(1)}, u32[]{:S(2)}, u32[]{:S(2)}) collective-permute-start(f32[448,384]{1,0:T(8,128)S(1)} %slice_add_fusion), channel_id=1, source_target_pairs={{0,8},{1,9},{2,10},{3,11},{4,12},{5,13},{6,14},{7,15},{8,0},{9,1},... | collective-permute-start | bytes 2064392 | tf_op jit(solution)/shard_map/ppermute | solution.py:26

commit v13 on v12

--- a/solution.py
+++ b/solution.py
@@ -156,6 +156,13 @@
     swap_two = moved(swap_one, lambda z, xl, xh, y, c: (z - 1, xl, xh, y, 1) if c == 1 else None)
     turned_one = moved(step_one_after, lambda z, xl, xh, y, c: (z, 1 - xl, 1, y, c) if (xh, c) == (0, 1) else None)
     early = over_y(parts)
+    turned_two = moved(step_two, lambda z, xl, xh, y, c: (z, 1 - xl, 1, y, c) if (xh, c) == (0, 1) else None)
+    step_three = moved(
+        step_two,
+        lambda z, xl, xh, y, c: (z - 1, xl, xh, y, c) if c == 0 else (z + 1, kind(xl, xh), xh, y, c),
+    )
+    turned_four = moved(step_three, lambda z, xl, xh, y, c: (z + 1, xl, xh, y, 1) if c == 1 else None)
+
     step_two, swap_one, swap_two, early = lax.optimization_barrier((step_two, swap_one, swap_two, early))
     late = over_y(numerators(late_kernel, 1, where, nvir, swap_one, swap_two, step_two))
 
@@ -173,16 +180,10 @@
         lambda z, xl, xh, y, c: (z + 1, kind(xl, xh), xh, y, 1) if c == 1 else None,
     )
     second = jnp.where(c == 0, amps_one, second)
-    late, first, second, amps_zero, step_two, turned_one = lax.optimization_barrier(
-        (late, first, second, amps_zero, step_two, turned_one)
-    )
-
-    turned_two = moved(step_two, lambda z, xl, xh, y, c: (z, 1 - xl, 1, y, c) if (xh, c) == (0, 1) else None)
-    step_three = moved(
-        step_two,
-        lambda z, xl, xh, y, c: (z - 1, xl, xh, y, c) if c == 0 else (z + 1, kind(xl, xh), xh, y, c),
-    )
-    turned_four = moved(step_three, lambda z, xl, xh, y, c: (z + 1, xl, xh, y, 1) if c == 1 else None)
+    late, first, second, amps_zero, turned_one, turned_two, step_three = lax.optimization_barrier(
+        (late, first, second, amps_zero, turned_one, turned_two, step_three)
+    )
+
     first, second = to_all(first, second)
 
     amps_two = amps(late[0], jnp.where(c == 0, swap_energy, energy(swap_two)), energy(step_two))

time: 178 us -> 169 us (0.949)
  starting transfers between devices: 57.9 us -> 53.2 us
  waiting for transfers between devices: 81.5 us -> 79.1 us
    ppermute x18, starting transfers between devices: 41.5 us -> 37.6 us  [moved(): return lax.ppermute(array, ALL, pairs)]
    all_to_all x2, waiting for transfers between devices: 19.2 us -> 16.6 us  [over_y(): return jnp.sum(lax.all_to_all(parts, 'y', 0, 0, tiled=True), axis=0)]
  transfers between devices with their start and end apart: 22 -> 22, of which waited for: 11 -> 11; matrix products, arithmetic and copies ran while one was open for 9% -> 8% of each run, Pallas kernels for 5% -> 5%
where the time goes in v13:
time: 169 us; the launch traced here: 167 us
  waiting for transfers between devices  79.1 us (47%)
  starting transfers between devices  53.2 us (31%)
  Pallas kernels  9.2 us (5%)
  matrix products  9.09 us (5%)
  other arithmetic  8.64 us (5%)
  local copies, waits for them, and re-layouts  4.96 us (3%)
  between operations  3.2 us (2%)
    ppermute x18, waiting for transfers between devices, moved(): return lax.ppermute(array, ALL, pairs)  51.5 us
    ppermute x18, starting transfers between devices, moved(): return lax.ppermute(array, ALL, pairs)  37.6 us
    all_to_all x2, waiting for transfers between devices, over_y(): return jnp.sum(lax.all_to_all(parts, 'y', 0, 0, tiled=True), axis=0)  16.6 us
    all_to_all x2, waiting for transfers between devices, to_all(): lax.all_to_all(jnp.broadcast_to(parts, (NY, *parts.shape)), 'y', 0, 0, ti...  10.9 us
    pallas_call x2, Pallas kernels, numerators(): pl.pallas_call(kernel, out_shape=jax.ShapeDtypeStruct((NY, count, share,...  9.2 us
    dot_general x4, matrix products, dot_tn(): lax.dot_general(a, b, (((0,), (0,)), ((), ())), preferred_element_type=jn...  9.09 us
    all_to_all x2, starting transfers between devices, over_y(): return jnp.sum(lax.all_to_all(parts, 'y', 0, 0, tiled=True), axis=0)  7.89 us
    all_to_all x2, starting transfers between devices, to_all(): lax.all_to_all(jnp.broadcast_to(parts, (NY, *parts.shape)), 'y', 0, 0, ti...  7.72 us
  transfers between devices with their start and end apart: 22, of which 11 were waited for; matrix products, arithmetic and copies ran while one was open for 8% of the time, Pallas kernels for 5%

profile of v13, /device:TPU:1, one launch (start us, length us, event | category | flops | bytes accessed | tf_op | source)
XLA Modules:
  0.0 167.4 jit_solution(13937430238022998182)
XLA Ops:
  0.0 3.6 %collective-permute-start.1 = (bf16[448,384]{1,0:T(8,128)(2,1)}, bf16[448,384]{1,0:T(8,128)(2,1)S(1)}, u32[]{:S(2)}, u32[]{:S(2)}) collective-permute-start(bf16[448,384]{1,0:T(8,128)(2,1)} %bitcast.71), channel_id=1, source_target_pairs={{0,8},{1,9},{2,10},{3,11},{4,12},{5,13},{6,14},{7,15},{8,0},{9,1},... | collective-permute-start | bytes 1032200 | tf_op jit(solution)/shard_map/ppermute | solution.py:26
  3.6 1.0 collective-permute-start
  7.4 1.3 select_convert_fusion
  8.7 2.0 %collective-permute-done.1 = bf16[448,384]{1,0:T(8,128)(2,1)S(1)} collective-permute-done((bf16[448,384]{1,0:T(8,128)(2,1)}, bf16[448,384]{1,0:T(8,128)(2,1)S(1)}, u32[]{:S(2)}, u32[]{:S(2)}) %collective-permute-start.1) | collective-permute-done | bytes 344096 | tf_op jit(solution)/shard_map/ppermute | solution.py:26
  10.6 2.2 %collective-permute-start.2 = (bf16[448,384]{1,0:T(8,128)(2,1)S(1)}, bf16[448,384]{1,0:T(8,128)(2,1)S(1)}, u32[]{:S(2)}, u32[]{:S(2)}) collective-permute-start(bf16[448,384]{1,0:T(8,128)(2,1)S(1)} %collective-permute-done.1), channel_id=1, source_target_pairs={{0,1},{1,0},{2,3},{3,2},{4,5},{5,4},{6,7},{7,6},{8,9},{9,8},{10,11... | collective-permute-start | bytes 1032200 | tf_op jit(solution)/shard_map/ppermute | solution.py:26
  12.8 1.2 maximum_select_fusion.1
  14.0 0.0 collective-permute-done.2
  14.1 0.2 maximum_select_fusion.2
  14.2 0.3 maximum_select_fusion
  14.6 0.1 pad_maximum_fusion.4.mine_ref
  14.7 1.0 copy-done
  15.7 1.9 %collective-permute-start.3 = (bf16[456,1536]{1,0:T(8,128)(2,1)S(1)}, bf16[456,1536]{1,0:T(8,128)(2,1)}, u32[]{:S(2)}, u32[]{:S(2)}) collective-permute-start(bf16[456,1536]{1,0:T(8,128)(2,1)S(1)} %pad_maximum_fusion.4.mine_ref), channel_id=1, source_target_pairs={{0,224},{1,33},{2,226},{3,35},{4,228},{5,37},{6,230},{7,39},{8,248... | collective-permute-start | bytes 4202504 | tf_op jit(solution)/shard_map/ppermute | solution.py:26
  17.5 0.7 collective-permute-start.6
  18.3 19.3 %collective-permute-done.3.one_ref = bf16[456,1536]{1,0:T(8,128)(2,1)} collective-permute-done((bf16[456,1536]{1,0:T(8,128)(2,1)S(1)}, bf16[456,1536]{1,0:T(8,128)(2,1)}, u32[]{:S(2)}, u32[]{:S(2)}) %collective-permute-start.3) | collective-permute-done | bytes 1400864 | tf_op jit(solution)/shard_map/ppermute | solution.py:26
  37.5 0.7 collective-permute-start.5
  38.2 0.1 pad_add_fusion.where_ref
  38.3 2.9 %collective-permute-done.5.swap_ref.swap_one_ref = bf16[456,1536]{1,0:T(8,128)(2,1)S(1)} collective-permute-done((bf16[456,1536]{1,0:T(8,128)(2,1)}, bf16[456,1536]{1,0:T(8,128)(2,1)S(1)}, u32[]{:S(2)}, u32[]{:S(2)}) %collective-permute-start.5) | collective-permute-done | bytes 1400864 | tf_op jit(solution)/shard_map/ppermute | solution.py:26
  41.2 5.1 %shard_map.37 = f32[4,2,112,448]{3,2,1,0:T(8,128)} custom-call(s32[2]{0:T(128)S(1)} %pad_add_fusion.where_ref, bf16[456,1536]{1,0:T(8,128)(2,1)S(1)} %pad_maximum_fusion.4.mine_ref, bf16[456,1536]{1,0:T(8,128)(2,1)} %collective-permute-done.3.one_ref, bf16[456,1536]{1,0:T(8,128)(2,1)S(1)} %collective-permute-done.5.swap_ref.swap_one_ref, ...), custom_call_target="tpu_custom_call" | custom-call | flops 2466250752 | bytes 7110656 | tf_op jit(solution)/shard_map/pallas_call | solution.py:91
  46.4 5.5 %collective-permute-start.7 = (bf16[456,1536]{1,0:T(8,128)(2,1)S(1)}, bf16[456,1536]{1,0:T(8,128)(2,1)S(1)}, u32[]{:S(2)}, u32[]{:S(2)}) collective-permute-start(bf16[456,1536]{1,0:T(8,128)(2,1)S(1)} %collective-permute-done.5.swap_ref.swap_one_ref), channel_id=1, source_target_pairs={{1,225},{3,227},{5,229},{7,231},{9,233},{11,235},{13,237},{15,239}... | collective-permute-start | bytes 4202504 | tf_op jit(solution)/shard_map/ppermute | solution.py:26
  51.9 4.4 %all-to-all-start = ((f32[4,2,112,448]{3,2,1,0:T(8,128)}), f32[4,2,112,448]{3,2,1,0:T(8,128)}, u32[]{:S(2)}, u32[]{:S(2)}) async-start(f32[4,2,112,448]{3,2,1,0:T(8,128)} %shard_map.37), calls=%async_computation | async-start | bytes 3670016 | tf_op jit(solution)/shard_map/all_to_all | solution.py:136
  56.3 0.1 dynamic_slice.3
  56.4 0.7 slice_convert_fusion
  57.1 0.7 slice_convert_fusion.1
  57.8 7.1 %collective-permute-start.10 = (bf16[456,1536]{1,0:T(8,128)(2,1)}, bf16[456,1536]{1,0:T(8,128)(2,1)}, u32[]{:S(2)}, u32[]{:S(2)}) collective-permute-start(bf16[456,1536]{1,0:T(8,128)(2,1)} %collective-permute-done.3.one_ref), channel_id=1, source_target_pairs={{1,25},{3,27},{5,29},{7,31},{17,9},{19,11},{21,13},{23,15},{33,57}... | collective-permute-start | bytes 4202504 | tf_op jit(solution)/shard_map/ppermute | solution.py:26
  64.9 2.4 %collective-permute-start.11 = (bf16[456,1536]{1,0:T(8,128)(2,1)}, bf16[456,1536]{1,0:T(8,128)(2,1)}, u32[]{:S(2)}, u32[]{:S(2)}) collective-permute-start(bf16[456,1536]{1,0:T(8,128)(2,1)} %collective-permute-done.4.two_ref), channel_id=1, source_target_pairs={{1,25},{3,27},{5,29},{7,31},{17,9},{19,11},{21,13},{23,15},{33,57}... | collective-permute-start | bytes 4202504 | tf_op jit(solution)/shard_map/ppermute | solution.py:26
  67.3 11.2 %all-to-all-done = f32[4,2,112,448]{3,2,1,0:T(8,128)} async-done(((f32[4,2,112,448]{3,2,1,0:T(8,128)}), f32[4,2,112,448]{3,2,1,0:T(8,128)}, u32[]{:S(2)}, u32[]{:S(2)}) %all-to-all-start) | async-done | bytes 1605664 | tf_op jit(solution)/shard_map/all_to_all | solution.py:136
  78.5 1.8 %reduce_sum.20 = f32[2,112,448]{2,1,0:T(8,128)S(1)} reduce(f32[4,2,112,448]{3,2,1,0:T(8,128)} %all-to-all-done, f32[]{:T(128)} %constant.7.clone.1), dimensions={0}, to_apply=%region_0.1 | reduce | flops 301056 | bytes 2007044 | tf_op jit(solution)/shard_map/reduce_sum | solution.py:136
  80.3 4.1 %shard_map.38 = f32[4,1,112,448]{3,2,1,0:T(8,128)} custom-call(s32[2]{0:T(128)S(1)} %pad_add_fusion.where_ref, bf16[456,1536]{1,0:T(8,128)(2,1)S(1)} %collective-permute-done.5.swap_ref.swap_one_ref, bf16[456,1536]{1,0:T(8,128)(2,1)S(1)} %collective-permute-done.7.swap_two_ref, bf16[456,1536]{1,0:T(8,128)(2,1)} %collective-permute-done.4.two_ref), custom_call_target="tpu_custom_call" | custom-call | flops 1233125376 | bytes 4931584 | tf_op jit(solution)/shard_map/pallas_call | solution.py:91
  84.4 3.5 %all-to-all-start.1 = ((f32[4,1,112,448]{3,2,1,0:T(8,128)}), f32[4,1,112,448]{3,2,1,0:T(8,128)S(1)}, u32[]{:S(2)}, u32[]{:S(2)}) async-start(f32[4,1,112,448]{3,2,1,0:T(8,128)} %shard_map.38), calls=%async_computation.1 | async-start | bytes 1835008 | tf_op jit(solution)/shard_map/all_to_all | solution.py:136
  87.9 0.1 fusion.36
  88.1 1.9 %collective-permute-start.9 = (bf16[112,448]{1,0:T(8,128)(2,1)S(1)}, bf16[112,448]{1,0:T(8,128)(2,1)S(1)}, u32[]{:S(2)}, u32[]{:S(2)}) collective-permute-start(bf16[112,448]{1,0:T(8,128)(2,1)S(1)} %get-tuple-element.193), channel_id=1, source_target_pairs={{1,33},{3,35},{5,37},{7,39},{9,57},{11,59},{13,61},{15,63},{17,49}... | collective-permute-start | bytes 301064 | tf_op jit(solution)/shard_map/ppermute | solution.py:26
  90.0 0.7 collective-permute-start.8
  90.7 0.7 slice_convert_fusion.2
  91.4 4.3 %collective-permute-done.9 = bf16[112,448]{1,0:T(8,128)(2,1)S(1)} collective-permute-done((bf16[112,448]{1,0:T(8,128)(2,1)S(1)}, bf16[112,448]{1,0:T(8,128)(2,1)S(1)}, u32[]{:S(2)}, u32[]{:S(2)}) %collective-permute-start.9) | collective-permute-done | bytes 100384 | tf_op jit(solution)/shard_map/ppermute | solution.py:26
  95.7 5.5 %all-to-all-done.1 = f32[4,1,112,448]{3,2,1,0:T(8,128)S(1)} async-done(((f32[4,1,112,448]{3,2,1,0:T(8,128)}), f32[4,1,112,448]{3,2,1,0:T(8,128)S(1)}, u32[]{:S(2)}, u32[]{:S(2)}) %all-to-all-start.1) | async-done | bytes 802848 | tf_op jit(solution)/shard_map/all_to_all | solution.py:136
  101.2 0.1 reduce_sum.21
  101.4 1.0 broadcast_in_dim.30
  102.4 3.5 %all-to-all-start.2 = ((bf16[4,2,112,448]{3,2,1,0:T(8,128)(2,1)}), bf16[4,2,112,448]{3,2,1,0:T(8,128)(2,1)S(1)}, u32[]{:S(2)}, u32[]{:S(2)}) async-start(bf16[4,2,112,448]{3,2,1,0:T(8,128)(2,1)} %broadcast_in_dim.30), calls=%async_computation.2 | async-start | bytes 1835008 | tf_op jit(solution)/shard_map/all_to_all | solution.py:150
  105.9 0.1 fusion.35
  106.0 1.3 collective-permute-start.14
  107.3 1.9 %collective-permute-start.15 = (bf16[456,1536]{1,0:T(8,128)(2,1)}, bf16[456,1536]{1,0:T(8,128)(2,1)}, u32[]{:S(2)}, u32[]{:S(2)}) collective-permute-start(bf16[456,1536]{1,0:T(8,128)(2,1)} %collective-permute-done.12), channel_id=1, source_target_pairs={{1,33},{3,35},{5,37},{7,39},{9,41},{11,43},{13,45},{15,47},{17,49}... | collective-permute-start | bytes 4202504 | tf_op jit(solution)/shard_map/ppermute | solution.py:26
  109.3 2.9 %collective-permute-start.13 = (bf16[112,448]{1,0:T(8,128)(2,1)S(1)}, bf16[112,448]{1,0:T(8,128)(2,1)S(1)}, u32[]{:S(2)}, u32[]{:S(2)}) collective-permute-start(bf16[112,448]{1,0:T(8,128)(2,1)S(1)} %fusion.35), channel_id=1, source_target_pairs={{0,224},{1,193},{2,226},{3,195},{4,228},{5,197},{6,230},{7,199},{8... | collective-permute-start | bytes 301064 | tf_op jit(solution)/shard_map/ppermute | solution.py:26
  112.1 4.7 %collective-permute-done.14 = bf16[112,448]{1,0:T(8,128)(2,1)S(1)} collective-permute-done((bf16[112,448]{1,0:T(8,128)(2,1)S(1)}, bf16[112,448]{1,0:T(8,128)(2,1)S(1)}, u32[]{:S(2)}, u32[]{:S(2)}) %collective-permute-start.14) | collective-permute-done | bytes 100384 | tf_op jit(solution)/shard_map/ppermute | solution.py:26
  116.9 2.7 %all-to-all-done.2 = bf16[4,2,112,448]{3,2,1,0:T(8,128)(2,1)S(1)} async-done(((bf16[4,2,112,448]{3,2,1,0:T(8,128)(2,1)}), bf16[4,2,112,448]{3,2,1,0:T(8,128)(2,1)S(1)}, u32[]{:S(2)}, u32[]{:S(2)}) %all-to-all-start.2) | async-done | bytes 802848 | tf_op jit(solution)/shard_map/all_to_all | solution.py:150
  119.5 0.1 fusion.43
  119.6 1.0 broadcast_in_dim.31
  120.7 4.2 %all-to-all-start.3 = ((bf16[4,2,112,448]{3,2,1,0:T(8,128)(2,1)}), bf16[4,2,112,448]{3,2,1,0:T(8,128)(2,1)}, u32[]{:S(2)}, u32[]{:S(2)}) async-start(bf16[4,2,112,448]{3,2,1,0:T(8,128)(2,1)} %broadcast_in_dim.31), calls=%async_computation.3 | async-start | bytes 1835008 | tf_op jit(solution)/shard_map/all_to_all | solution.py:150
  124.9 4.5 %conditional.2 = (f32[448,1536]{1,0:T(8,128)S(1)}) conditional(s32[]{:T(128)} %clamp.4, (bf16[456,1536]{1,0:T(8,128)(2,1)}, bf16[448,448]{1,0:T(8,128)(2,1)S(1)}, bf16[456,1536]{1,0:T(8,128)(2,1)}, bf16[448,448]{1,0:T(8,128)(2,1)S(1)}) %tuple.85, (bf16[456,1536]{1,0:T(8,128)(2,1)}, bf16[448,448]{1,0:T(8,128)(2,1)S(1)}, ...), branch_computations={%region_2.3_spmd, %region_3.4_spmd, %region_4.5_spmd, %region_5.6_... | conditional | flops 1233813504 | bytes 11812872 | solution.py:203
  124.9 2.2 %fusion.4 = f32[448,1536]{1,0:T(8,128)S(1)} fusion(bf16[448,448]{1,0:T(8,128)(2,1)S(1)} %get-tuple-element.86, bf16[456,1536]{1,0:T(8,128)(2,1)} %get-tuple-element.87), kind=kOutput, calls=%fused_computation.6 | convolution fusion | flops 616562688 | bytes 4530176 | tf_op jit(solution)/shard_map/cond/branch_1_fun/dot_general | solution.py:50
  127.2 2.3 %convolution_add_fusion.1 = f32[448,1536]{1,0:T(8,128)S(1)} fusion(f32[448,1536]{1,0:T(8,128)S(1)} %fusion.4, bf16[448,448]{1,0:T(8,128)(2,1)S(1)} %get-tuple-element.88, bf16[456,1536]{1,0:T(8,128)(2,1)} %get-tuple-element.89), kind=kOutput, calls=%fused_computation.4 | convolution fusion | flops 617250816 | bytes 7282688 | tf_op jit(solution)/shard_map/cond/branch_1_fun/dot_general | solution.py:50
  129.5 8.3 %all-to-all-done.3 = bf16[4,2,112,448]{3,2,1,0:T(8,128)(2,1)} async-done(((bf16[4,2,112,448]{3,2,1,0:T(8,128)(2,1)}), bf16[4,2,112,448]{3,2,1,0:T(8,128)(2,1)}, u32[]{:S(2)}, u32[]{:S(2)}) %all-to-all-start.3) | async-done | bytes 802848 | tf_op jit(solution)/shard_map/all_to_all | solution.py:150
  137.7 1.3 fusion.42
  139.1 0.3 copy-done.1
  139.3 4.9 %conditional.3 = (f32[448,768]{1,0:T(8,128)S(1)}, f32[448,384]{1,0:T(8,128)S(1)}, f32[448,384]{1,0:T(8,128)S(1)}) conditional(s32[]{:T(128)} %clamp.4, (bf16[456,1536]{1,0:T(8,128)(2,1)}, bf16[448,448]{1,0:T(8,128)(2,1)S(1)}, bf16[448,448]{1,0:T(8,128)(2,1)S(1)}, bf16[448,1536]{1,0:T(8,128)(2,1)S(1)}, ...), branch_computations={%region_6.7_spmd, %region_7.8_spmd, %region_8.9_spmd, %region_9.10... | conditional | flops 1234845696 | bytes 28483636 | solution.py:223
  139.3 2.2 %fusion.17 = f32[448,1536]{1,0:T(8,128)S(1)} fusion(bf16[448,448]{1,0:T(8,128)(2,1)S(1)} %get-tuple-element.104, bf16[456,1536]{1,0:T(8,128)(2,1)} %get-tuple-element.105), kind=kOutput, calls=%fused_computation.25 | convolution fusion | flops 616562688 | bytes 4530176 | tf_op jit(solution)/shard_map/cond/branch_1_fun/dot_general | solution.py:50
  141.6 2.3 %fusion.15 = f32[448,1536]{1,0:T(8,128)S(1)} fusion(f32[448,1536]{1,0:T(8,128)S(1)} %get-tuple-element.103, f32[448,1536]{1,0:T(8,128)S(1)} %fusion.17, bf16[448,448]{1,0:T(8,128)(2,1)S(1)} %get-tuple-element.106, bf16[456,1536]{1,0:T(8,128)(2,1)} %get-tuple-element.107), kind=kOutput, calls=%fused_computation.22 | convolution fusion | flops 617938944 | bytes 10035200 | tf_op jit(solution)/shard_map/cond/branch_1_fun/dot_general | solution.py:50
  143.9 0.2 fusion.39
  144.1 0.1 pad_maximum_fusion.1
  144.2 0.6 collective-permute-start.16
  144.8 2.8 %collective-permute-done.16 = f32[448,768]{1,0:T(8,128)S(1)} collective-permute-done((f32[448,768]{1,0:T(8,128)S(1)}, f32[448,768]{1,0:T(8,128)S(1)}, u32[]{:S(2)}, u32[]{:S(2)}) %collective-permute-start.16) | collective-permute-done | bytes 1376288 | tf_op jit(solution)/shard_map/ppermute | solution.py:26
  147.5 0.1 slice_add_fusion
  147.6 3.4 %collective-permute-start.17 = (f32[448,384]{1,0:T(8,128)S(1)}, f32[448,384]{1,0:T(8,128)S(1)}, u32[]{:S(2)}, u32[]{:S(2)}) collective-permute-start(f32[448,384]{1,0:T(8,128)S(1)} %slice_add_fusion), channel_id=1, source_target_pairs={{0,8},{1,9},{2,10},{3,11},{4,12},{5,13},{6,14},{7,15},{8,0},{9,1},... | collective-permute-start | bytes 2064392 | tf_op jit(solution)/shard_map/ppermute | solution.py:26
  151.0 15.5 %collective-permute-done.17 = f32[448,384]{1,0:T(8,128)S(1)} collective-permute-done((f32[448,384]{1,0:T(8,128)S(1)}, f32[448,384]{1,0:T(8,128)S(1)}, u32[]{:S(2)}, u32[]{:S(2)}) %collective-permute-start.17) | collective-permute-done | bytes 688160 | tf_op jit(solution)/shard_map/ppermute | solution.py:26
  166.5 0.9 fusion.28
  (32 shorter events, 0.2 us)
Async XLA Ops:
  0.0 10.6 %collective-permute-start.1 = (bf16[448,384]{1,0:T(8,128)(2,1)}, bf16[448,384]{1,0:T(8,128)(2,1)S(1)}, u32[]{:S(2)}, u32[]{:S(2)}) collective-permute-start(bf16[448,384]{1,0:T(8,128)(2,1)} %bitcast.71), channel_id=1, source_target_pairs={{0,8},{1,9},{2,10},{3,11},{4,12},{5,13},{6,14},{7,15},{8,0},{9,1},... | collective-permute-start | bytes 1032200 | tf_op jit(solution)/shard_map/ppermute | solution.py:26
  3.6 9.2 %collective-permute-start = (bf16[448,384]{1,0:T(8,128)(2,1)}, bf16[448,384]{1,0:T(8,128)(2,1)S(1)}, u32[]{:S(2)}, u32[]{:S(2)}) collective-permute-start(bf16[448,384]{1,0:T(8,128)(2,1)} %bitcast.72), channel_id=1, source_target_pairs={{0,1},{1,0},{2,3},{3,2},{4,5},{5,4},{6,7},{7,6},{8,9},{9,8},{10,11... | collective-permute-start | bytes 1032200 | tf_op jit(solution)/shard_map/ppermute | solution.py:26
  10.6 3.5 %collective-permute-start.2 = (bf16[448,384]{1,0:T(8,128)(2,1)S(1)}, bf16[448,384]{1,0:T(8,128)(2,1)S(1)}, u32[]{:S(2)}, u32[]{:S(2)}) collective-permute-start(bf16[448,384]{1,0:T(8,128)(2,1)S(1)} %collective-permute-done.1), channel_id=1, source_target_pairs={{0,1},{1,0},{2,3},{3,2},{4,5},{5,4},{6,7},{7,6},{8,9},{9,8},{10,11... | collective-permute-start | bytes 1032200 | tf_op jit(solution)/shard_map/ppermute | solution.py:26
  14.6 1.1 copy-start
  15.7 21.9 %collective-permute-start.3 = (bf16[456,1536]{1,0:T(8,128)(2,1)S(1)}, bf16[456,1536]{1,0:T(8,128)(2,1)}, u32[]{:S(2)}, u32[]{:S(2)}) collective-permute-start(bf16[456,1536]{1,0:T(8,128)(2,1)S(1)} %pad_maximum_fusion.4.mine_ref), channel_id=1, source_target_pairs={{0,224},{1,33},{2,226},{3,35},{4,228},{5,37},{6,230},{7,39},{8,248... | collective-permute-start | bytes 4202504 | tf_op jit(solution)/shard_map/ppermute | solution.py:26
  17.5 20.8 %collective-permute-start.6 = (bf16[456,1536]{1,0:T(8,128)(2,1)S(1)}, bf16[456,1536]{1,0:T(8,128)(2,1)S(1)}, u32[]{:S(2)}, u32[]{:S(2)}) collective-permute-start(bf16[456,1536]{1,0:T(8,128)(2,1)S(1)} %pad_maximum_fusion.4.mine_ref), channel_id=1, source_target_pairs={{0,24},{2,26},{4,28},{6,30},{16,8},{18,10},{20,12},{22,14},{32,56}... | collective-permute-start | bytes 4202504 | tf_op jit(solution)/shard_map/ppermute | solution.py:26
  37.5 3.7 %collective-permute-start.5 = (bf16[456,1536]{1,0:T(8,128)(2,1)}, bf16[456,1536]{1,0:T(8,128)(2,1)S(1)}, u32[]{:S(2)}, u32[]{:S(2)}) collective-permute-start(bf16[456,1536]{1,0:T(8,128)(2,1)} %collective-permute-done.3.one_ref), channel_id=1, source_target_pairs={{0,1},{1,0},{2,3},{3,2},{4,5},{5,4},{6,7},{7,6},{8,9},{9,8},{10,11... | collective-permute-start | bytes 4202504 | tf_op jit(solution)/shard_map/ppermute | solution.py:26
  38.3 26.6 %collective-permute-start.4 = (bf16[456,1536]{1,0:T(8,128)(2,1)}, bf16[456,1536]{1,0:T(8,128)(2,1)}, u32[]{:S(2)}, u32[]{:S(2)}) collective-permute-start(bf16[456,1536]{1,0:T(8,128)(2,1)} %collective-permute-done.3.one_ref), channel_id=1, source_target_pairs={{0,224},{1,33},{2,226},{3,35},{4,228},{5,37},{6,230},{7,39},{8,232... | collective-permute-start | bytes 4202504 | tf_op jit(solution)/shard_map/ppermute | solution.py:26
  38.3 8.0 %copy-start.2 = (bf16[456,1536]{1,0:T(8,128)(2,1)}, bf16[456,1536]{1,0:T(8,128)(2,1)S(1)}, u32[]{:S(2)}) copy-start(bf16[456,1536]{1,0:T(8,128)(2,1)S(1)} %collective-permute-done.6.beyond_ref) | copy-start | bytes 4202500
  46.4 10.0 %copy-start.4 = (f32[448]{0:T(512)S(1)}, f32[448]{0:T(512)}, u32[]{:S(2)}) copy-start(f32[448]{0:T(512)} %param.13) | copy-start | bytes 5380
  46.4 33.9 %collective-permute-start.7 = (bf16[456,1536]{1,0:T(8,128)(2,1)S(1)}, bf16[456,1536]{1,0:T(8,128)(2,1)S(1)}, u32[]{:S(2)}, u32[]{:S(2)}) collective-permute-start(bf16[456,1536]{1,0:T(8,128)(2,1)S(1)} %collective-permute-done.5.swap_ref.swap_one_ref), channel_id=1, source_target_pairs={{1,225},{3,227},{5,229},{7,231},{9,233},{11,235},{13,237},{15,239}... | collective-permute-start | bytes 4202504 | tf_op jit(solution)/shard_map/ppermute | solution.py:26
  51.9 26.6 %all-to-all-start = ((f32[4,2,112,448]{3,2,1,0:T(8,128)}), f32[4,2,112,448]{3,2,1,0:T(8,128)}, u32[]{:S(2)}, u32[]{:S(2)}) async-start(f32[4,2,112,448]{3,2,1,0:T(8,128)} %shard_map.37), calls=%async_computation | async-start | bytes 3670016 | tf_op jit(solution)/shard_map/all_to_all | solution.py:136
  57.8 43.5 %collective-permute-start.10 = (bf16[456,1536]{1,0:T(8,128)(2,1)}, bf16[456,1536]{1,0:T(8,128)(2,1)}, u32[]{:S(2)}, u32[]{:S(2)}) collective-permute-start(bf16[456,1536]{1,0:T(8,128)(2,1)} %collective-permute-done.3.one_ref), channel_id=1, source_target_pairs={{1,25},{3,27},{5,29},{7,31},{17,9},{19,11},{21,13},{23,15},{33,57}... | collective-permute-start | bytes 4202504 | tf_op jit(solution)/shard_map/ppermute | solution.py:26
  64.9 36.4 %collective-permute-start.12 = (bf16[456,1536]{1,0:T(8,128)(2,1)}, bf16[456,1536]{1,0:T(8,128)(2,1)}, u32[]{:S(2)}, u32[]{:S(2)}) collective-permute-start(bf16[456,1536]{1,0:T(8,128)(2,1)} %collective-permute-done.4.two_ref), channel_id=1, source_target_pairs={{0,224},{1,33},{2,226},{3,35},{4,228},{5,37},{6,230},{7,39},{8,232... | collective-permute-start | bytes 4202504 | tf_op jit(solution)/shard_map/ppermute | solution.py:26
  64.9 36.4 %collective-permute-start.11 = (bf16[456,1536]{1,0:T(8,128)(2,1)}, bf16[456,1536]{1,0:T(8,128)(2,1)}, u32[]{:S(2)}, u32[]{:S(2)}) collective-permute-start(bf16[456,1536]{1,0:T(8,128)(2,1)} %collective-permute-done.4.two_ref), channel_id=1, source_target_pairs={{1,25},{3,27},{5,29},{7,31},{17,9},{19,11},{21,13},{23,15},{33,57}... | collective-permute-start | bytes 4202504 | tf_op jit(solution)/shard_map/ppermute | solution.py:26
  84.4 16.8 %all-to-all-start.1 = ((f32[4,1,112,448]{3,2,1,0:T(8,128)}), f32[4,1,112,448]{3,2,1,0:T(8,128)S(1)}, u32[]{:S(2)}, u32[]{:S(2)}) async-start(f32[4,1,112,448]{3,2,1,0:T(8,128)} %shard_map.38), calls=%async_computation.1 | async-start | bytes 1835008 | tf_op jit(solution)/shard_map/all_to_all | solution.py:136
  88.1 7.6 %collective-permute-start.9 = (bf16[112,448]{1,0:T(8,128)(2,1)S(1)}, bf16[112,448]{1,0:T(8,128)(2,1)S(1)}, u32[]{:S(2)}, u32[]{:S(2)}) collective-permute-start(bf16[112,448]{1,0:T(8,128)(2,1)S(1)} %get-tuple-element.193), channel_id=1, source_target_pairs={{1,33},{3,35},{5,37},{7,39},{9,57},{11,59},{13,61},{15,63},{17,49}... | collective-permute-start | bytes 301064 | tf_op jit(solution)/shard_map/ppermute | solution.py:26
  90.0 11.3 %collective-permute-start.8 = (bf16[112,448]{1,0:T(8,128)(2,1)S(1)}, bf16[112,448]{1,0:T(8,128)(2,1)S(1)}, u32[]{:S(2)}, u32[]{:S(2)}) collective-permute-start(bf16[112,448]{1,0:T(8,128)(2,1)S(1)} %get-tuple-element.193), channel_id=1, source_target_pairs={{0,33},{1,224},{2,35},{3,226},{4,37},{5,228},{6,39},{7,230},{8,57}... | collective-permute-start | bytes 301064 | tf_op jit(solution)/shard_map/ppermute | solution.py:26
  102.4 17.2 %all-to-all-start.2 = ((bf16[4,2,112,448]{3,2,1,0:T(8,128)(2,1)}), bf16[4,2,112,448]{3,2,1,0:T(8,128)(2,1)S(1)}, u32[]{:S(2)}, u32[]{:S(2)}) async-start(bf16[4,2,112,448]{3,2,1,0:T(8,128)(2,1)} %broadcast_in_dim.30), calls=%async_computation.2 | async-start | bytes 1835008 | tf_op jit(solution)/shard_map/all_to_all | solution.py:150
  106.0 10.8 %collective-permute-start.14 = (bf16[112,448]{1,0:T(8,128)(2,1)S(1)}, bf16[112,448]{1,0:T(8,128)(2,1)S(1)}, u32[]{:S(2)}, u32[]{:S(2)}) collective-permute-start(bf16[112,448]{1,0:T(8,128)(2,1)S(1)} %fusion.35), channel_id=1, source_target_pairs={{0,65},{2,67},{4,69},{6,71},{8,89},{10,91},{12,93},{14,95},{16,81}... | collective-permute-start | bytes 301064 | tf_op jit(solution)/shard_map/ppermute | solution.py:26
  107.3 31.7 %collective-permute-start.15 = (bf16[456,1536]{1,0:T(8,128)(2,1)}, bf16[456,1536]{1,0:T(8,128)(2,1)}, u32[]{:S(2)}, u32[]{:S(2)}) collective-permute-start(bf16[456,1536]{1,0:T(8,128)(2,1)} %collective-permute-done.12), channel_id=1, source_target_pairs={{1,33},{3,35},{5,37},{7,39},{9,41},{11,43},{13,45},{15,47},{17,49}... | collective-permute-start | bytes 4202504 | tf_op jit(solution)/shard_map/ppermute | solution.py:26
  109.3 10.3 %collective-permute-start.13 = (bf16[112,448]{1,0:T(8,128)(2,1)S(1)}, bf16[112,448]{1,0:T(8,128)(2,1)S(1)}, u32[]{:S(2)}, u32[]{:S(2)}) collective-permute-start(bf16[112,448]{1,0:T(8,128)(2,1)S(1)} %fusion.35), channel_id=1, source_target_pairs={{0,224},{1,193},{2,226},{3,195},{4,228},{5,197},{6,230},{7,199},{8... | collective-permute-start | bytes 301064 | tf_op jit(solution)/shard_map/ppermute | solution.py:26
  120.7 17.0 %all-to-all-start.3 = ((bf16[4,2,112,448]{3,2,1,0:T(8,128)(2,1)}), bf16[4,2,112,448]{3,2,1,0:T(8,128)(2,1)}, u32[]{:S(2)}, u32[]{:S(2)}) async-start(bf16[4,2,112,448]{3,2,1,0:T(8,128)(2,1)} %broadcast_in_dim.31), calls=%async_computation.3 | async-start | bytes 1835008 | tf_op jit(solution)/shard_map/all_to_all | solution.py:150
  137.7 1.6 copy-start.1
  144.2 3.3 %collective-permute-start.16 = (f32[448,768]{1,0:T(8,128)S(1)}, f32[448,768]{1,0:T(8,128)S(1)}, u32[]{:S(2)}, u32[]{:S(2)}) collective-permute-start(f32[448,768]{1,0:T(8,128)S(1)} %get-tuple-element.164), channel_id=1, source_target_pairs={{0,1},{1,0},{2,3},{3,2},{4,5},{5,4},{6,7},{7,6},{8,9},{9,8},{10,11... | collective-permute-start | bytes 4128776 | tf_op jit(solution)/shard_map/ppermute | solution.py:26
  147.6 18.9 %collective-permute-start.17 = (f32[448,384]{1,0:T(8,128)S(1)}, f32[448,384]{1,0:T(8,128)S(1)}, u32[]{:S(2)}, u32[]{:S(2)}) collective-permute-start(f32[448,384]{1,0:T(8,128)S(1)} %slice_add_fusion), channel_id=1, source_target_pairs={{0,8},{1,9},{2,10},{3,11},{4,12},{5,13},{6,14},{7,15},{8,0},{9,1},... | collective-permute-start | bytes 2064392 | tf_op jit(solution)/shard_map/ppermute | solution.py:26

commit v14 on v13

--- a/solution.py
+++ b/solution.py
@@ -145,6 +145,13 @@
     def amps(value, a, b):
         return (value / (virs - a - b)).astype(jnp.bfloat16)
 
+    def by_hops(*parts):
+        parts = jnp.stack(parts)
+        ahead = [parts] + [moved(parts, lambda z, xl, xh, y, c, n=n: (z, xl, xh, y - n, c)) for n in range(1, NY)]
+        twice = jnp.stack(ahead + ahead)
+        whole = lax.dynamic_slice_in_dim(twice, NY - y, NY, axis=0)
+        return [whole[:, n].reshape(nvir, nvir) for n in range(parts.shape[0])]
+
     def to_all(*parts):
         parts = jnp.stack(parts)
         whole = lax.all_to_all(jnp.broadcast_to(parts, (NY, *parts.shape)), "y", 0, 0, tiled=True)
@@ -180,11 +187,10 @@
         lambda z, xl, xh, y, c: (z + 1, kind(xl, xh), xh, y, 1) if c == 1 else None,
     )
     second = jnp.where(c == 0, amps_one, second)
+    first, second = by_hops(first, second)
     late, first, second, amps_zero, turned_one, turned_two, step_three = lax.optimization_barrier(
         (late, first, second, amps_zero, turned_one, turned_two, step_three)
     )
-
-    first, second = to_all(first, second)
 
     amps_two = amps(late[0], jnp.where(c == 0, swap_energy, energy(swap_two)), energy(step_two))
     third = moved(
@@ -193,7 +199,6 @@
     )
     fourth = moved(amps_two, lambda z, xl, xh, y, c: (z + 2, kind(xl, xh), xh, y, 1) if c == 0 else None)
     fourth = jnp.where(c == 0, amps_zero, fourth)
-    third, fourth, first, second, turned_two = lax.optimization_barrier((third, fourth, first, second, turned_two))
     third, fourth = to_all(third, fourth)
 
     def product(dot, *blocks):

time: 169 us -> 176 us (1.041)
  waiting for transfers between devices: 79.1 us -> 88.3 us
  local copies, waits for them, and re-layouts: 4.96 us -> 3.04 us
    ppermute x18 -> x21, waiting for transfers between devices: 51.5 us -> 69 us  [moved(): return lax.ppermute(array, ALL, pairs)]
    all_to_all x2, waiting for transfers between devices: 16.6 us -> 11.2 us  [over_y(): return jnp.sum(lax.all_to_all(parts, 'y', 0, 0, tiled=True), axis=0)]
    all_to_all x2 -> x1, starting transfers between devices: 7.72 us -> 4.24 us  [to_all(): lax.all_to_all(jnp.broadcast_to(parts, (NY, *parts.shape)), 'y', 0, 0, ti...]
    ppermute x18 -> x21, starting transfers between devices: 37.6 us -> 40.7 us  [moved(): return lax.ppermute(array, ALL, pairs)]
    all_to_all x2 -> x1, waiting for transfers between devices: 10.9 us -> 8.16 us  [to_all(): lax.all_to_all(jnp.broadcast_to(parts, (NY, *parts.shape)), 'y', 0, 0, ti...]
  transfers between devices with their start and end apart: 22 -> 24, of which waited for: 11 -> 10; matrix products, arithmetic and copies ran while one was open for 8% -> 8% of each run, Pallas kernels for 5% -> 5%
where the time goes in v14:
time: 176 us; the launch traced here: 175 us
  waiting for transfers between devices  88.3 us (50%)
  starting transfers between devices  52.9 us (30%)
  Pallas kernels  9.22 us (5%)
  matrix products  9.09 us (5%)
  other arithmetic  8.77 us (5%)
  between operations  3.44 us (2%)
  local copies, waits for them, and re-layouts  3.04 us (2%)
    ppermute x21, waiting for transfers between devices, moved(): return lax.ppermute(array, ALL, pairs)  69 us
    ppermute x21, starting transfers between devices, moved(): return lax.ppermute(array, ALL, pairs)  40.7 us
    all_to_all x2, waiting for transfers between devices, over_y(): return jnp.sum(lax.all_to_all(parts, 'y', 0, 0, tiled=True), axis=0)  11.2 us
    pallas_call x2, Pallas kernels, numerators(): pl.pallas_call(kernel, out_shape=jax.ShapeDtypeStruct((NY, count, share,...  9.22 us
    dot_general x4, matrix products, dot_tn(): lax.dot_general(a, b, (((0,), (0,)), ((), ())), preferred_element_type=jn...  9.09 us
    all_to_all x1, waiting for transfers between devices, to_all(): lax.all_to_all(jnp.broadcast_to(parts, (NY, *parts.shape)), 'y', 0, 0, ti...  8.16 us
    all_to_all x2, starting transfers between devices, over_y(): return jnp.sum(lax.all_to_all(parts, 'y', 0, 0, tiled=True), axis=0)  7.9 us
    all_to_all x1, starting transfers between devices, to_all(): lax.all_to_all(jnp.broadcast_to(parts, (NY, *parts.shape)), 'y', 0, 0, ti...  4.24 us
  transfers between devices with their start and end apart: 24, of which 10 were waited for; matrix products, arithmetic and copies ran while one was open for 8% of the time, Pallas kernels for 5%

profile of v14, /device:TPU:1, one launch (start us, length us, event | category | flops | bytes accessed | tf_op | source)
XLA Modules:
  0.0 175.0 jit_solution(1586913588780750416)
XLA Ops:
  0.0 3.6 %collective-permute-start.1 = (bf16[448,384]{1,0:T(8,128)(2,1)}, bf16[448,384]{1,0:T(8,128)(2,1)S(1)}, u32[]{:S(2)}, u32[]{:S(2)}) collective-permute-start(bf16[448,384]{1,0:T(8,128)(2,1)} %bitcast.86), channel_id=1, source_target_pairs={{0,8},{1,9},{2,10},{3,11},{4,12},{5,13},{6,14},{7,15},{8,0},{9,1},... | collective-permute-start | bytes 1032200 | tf_op jit(solution)/shard_map/ppermute | solution.py:26
  3.6 1.0 collective-permute-start
  7.6 1.4 select_convert_fusion
  8.9 1.7 collective-permute-done.1
  10.6 2.2 %collective-permute-start.2 = (bf16[448,384]{1,0:T(8,128)(2,1)S(1)}, bf16[448,384]{1,0:T(8,128)(2,1)S(1)}, u32[]{:S(2)}, u32[]{:S(2)}) collective-permute-start(bf16[448,384]{1,0:T(8,128)(2,1)S(1)} %collective-permute-done.1), channel_id=1, source_target_pairs={{0,1},{1,0},{2,3},{3,2},{4,5},{5,4},{6,7},{7,6},{8,9},{9,8},{10,11... | collective-permute-start | bytes 1032200 | tf_op jit(solution)/shard_map/ppermute | solution.py:26
  12.8 1.2 maximum_select_fusion.1
  14.0 0.0 collective-permute-done.2
  14.1 0.2 maximum_select_fusion.2
  14.2 0.3 maximum_select_fusion
  14.6 0.1 pad_maximum_fusion.4.mine_ref
  14.7 1.9 %collective-permute-start.3 = (bf16[456,1536]{1,0:T(8,128)(2,1)S(1)}, bf16[456,1536]{1,0:T(8,128)(2,1)}, u32[]{:S(2)}, u32[]{:S(2)}) collective-permute-start(bf16[456,1536]{1,0:T(8,128)(2,1)S(1)} %pad_maximum_fusion.4.mine_ref), channel_id=1, source_target_pairs={{0,224},{1,33},{2,226},{3,35},{4,228},{5,37},{6,230},{7,39},{8,248... | collective-permute-start | bytes 4202504 | tf_op jit(solution)/shard_map/ppermute | solution.py:26
  16.6 0.7 collective-permute-start.6
  17.4 19.3 %collective-permute-done.3.one_ref = bf16[456,1536]{1,0:T(8,128)(2,1)} collective-permute-done((bf16[456,1536]{1,0:T(8,128)(2,1)S(1)}, bf16[456,1536]{1,0:T(8,128)(2,1)}, u32[]{:S(2)}, u32[]{:S(2)}) %collective-permute-start.3) | collective-permute-done | bytes 1400864 | tf_op jit(solution)/shard_map/ppermute | solution.py:26
  36.6 0.7 collective-permute-start.5
  37.3 0.1 pad_add_fusion.where_ref
  37.4 0.0 collective-permute-start.4
  37.4 2.9 %collective-permute-done.5.swap_ref.swap_one_ref = bf16[456,1536]{1,0:T(8,128)(2,1)S(1)} collective-permute-done((bf16[456,1536]{1,0:T(8,128)(2,1)}, bf16[456,1536]{1,0:T(8,128)(2,1)S(1)}, u32[]{:S(2)}, u32[]{:S(2)}) %collective-permute-start.5) | collective-permute-done | bytes 1400864 | tf_op jit(solution)/shard_map/ppermute | solution.py:26
  40.3 5.1 %shard_map.37 = f32[4,2,112,448]{3,2,1,0:T(8,128)} custom-call(s32[2]{0:T(128)S(1)} %pad_add_fusion.where_ref, bf16[456,1536]{1,0:T(8,128)(2,1)S(1)} %pad_maximum_fusion.4.mine_ref, bf16[456,1536]{1,0:T(8,128)(2,1)} %collective-permute-done.3.one_ref, bf16[456,1536]{1,0:T(8,128)(2,1)S(1)} %collective-permute-done.5.swap_ref.swap_one_ref, ...), custom_call_target="tpu_custom_call" | custom-call | flops 2466250752 | bytes 7110656 | tf_op jit(solution)/shard_map/pallas_call | solution.py:91
  45.4 5.5 %collective-permute-start.7 = (bf16[456,1536]{1,0:T(8,128)(2,1)S(1)}, bf16[456,1536]{1,0:T(8,128)(2,1)S(1)}, u32[]{:S(2)}, u32[]{:S(2)}) collective-permute-start(bf16[456,1536]{1,0:T(8,128)(2,1)S(1)} %collective-permute-done.5.swap_ref.swap_one_ref), channel_id=1, source_target_pairs={{1,225},{3,227},{5,229},{7,231},{9,233},{11,235},{13,237},{15,239}... | collective-permute-start | bytes 4202504 | tf_op jit(solution)/shard_map/ppermute | solution.py:26
  51.0 4.4 %all-to-all-start = ((f32[4,2,112,448]{3,2,1,0:T(8,128)}), f32[4,2,112,448]{3,2,1,0:T(8,128)}, u32[]{:S(2)}, u32[]{:S(2)}) async-start(f32[4,2,112,448]{3,2,1,0:T(8,128)} %shard_map.37), calls=%async_computation | async-start | bytes 3670016 | tf_op jit(solution)/shard_map/all_to_all | solution.py:136
  55.4 0.1 dynamic_slice.6
  55.5 0.7 slice_convert_fusion
  56.2 0.7 slice_convert_fusion.1
  56.9 7.1 %collective-permute-start.13 = (bf16[456,1536]{1,0:T(8,128)(2,1)}, bf16[456,1536]{1,0:T(8,128)(2,1)}, u32[]{:S(2)}, u32[]{:S(2)}) collective-permute-start(bf16[456,1536]{1,0:T(8,128)(2,1)} %collective-permute-done.3.one_ref), channel_id=1, source_target_pairs={{1,25},{3,27},{5,29},{7,31},{17,9},{19,11},{21,13},{23,15},{33,57}... | collective-permute-start | bytes 4202504 | tf_op jit(solution)/shard_map/ppermute | solution.py:26
  64.0 2.4 %collective-permute-start.14 = (bf16[456,1536]{1,0:T(8,128)(2,1)}, bf16[456,1536]{1,0:T(8,128)(2,1)}, u32[]{:S(2)}, u32[]{:S(2)}) collective-permute-start(bf16[456,1536]{1,0:T(8,128)(2,1)} %collective-permute-done.4.two_ref), channel_id=1, source_target_pairs={{1,25},{3,27},{5,29},{7,31},{17,9},{19,11},{21,13},{23,15},{33,57}... | collective-permute-start | bytes 4202504 | tf_op jit(solution)/shard_map/ppermute | solution.py:26
  66.4 11.2 %all-to-all-done = f32[4,2,112,448]{3,2,1,0:T(8,128)} async-done(((f32[4,2,112,448]{3,2,1,0:T(8,128)}), f32[4,2,112,448]{3,2,1,0:T(8,128)}, u32[]{:S(2)}, u32[]{:S(2)}) %all-to-all-start) | async-done | bytes 1605664 | tf_op jit(solution)/shard_map/all_to_all | solution.py:136
  77.5 1.8 %reduce_sum.20 = f32[2,112,448]{2,1,0:T(8,128)S(1)} reduce(f32[4,2,112,448]{3,2,1,0:T(8,128)} %all-to-all-done, f32[]{:T(128)} %constant.8.clone.1), dimensions={0}, to_apply=%region_0.1 | reduce | flops 301056 | bytes 2007044 | tf_op jit(solution)/shard_map/reduce_sum | solution.py:136
  79.4 0.1 fusion.36
  79.5 1.9 %collective-permute-start.9 = (bf16[112,448]{1,0:T(8,128)(2,1)S(1)}, bf16[112,448]{1,0:T(8,128)(2,1)S(1)}, u32[]{:S(2)}, u32[]{:S(2)}) collective-permute-start(bf16[112,448]{1,0:T(8,128)(2,1)S(1)} %get-tuple-element.183), channel_id=1, source_target_pairs={{1,33},{3,35},{5,37},{7,39},{9,57},{11,59},{13,61},{15,63},{17,49}... | collective-permute-start | bytes 301064 | tf_op jit(solution)/shard_map/ppermute | solution.py:26
  81.5 0.7 collective-permute-start.8
  82.1 0.7 slice_convert_fusion.2
  82.8 4.1 %shard_map.38 = f32[4,1,112,448]{3,2,1,0:T(8,128)} custom-call(s32[2]{0:T(128)S(1)} %pad_add_fusion.where_ref, bf16[456,1536]{1,0:T(8,128)(2,1)S(1)} %collective-permute-done.5.swap_ref.swap_one_ref, bf16[456,1536]{1,0:T(8,128)(2,1)S(1)} %collective-permute-done.7.swap_two_ref, bf16[456,1536]{1,0:T(8,128)(2,1)} %collective-permute-done.4.two_ref), custom_call_target="tpu_custom_call" | custom-call | flops 1233125376 | bytes 4931584 | tf_op jit(solution)/shard_map/pallas_call | solution.py:91
  86.9 3.5 %all-to-all-start.1 = ((f32[4,1,112,448]{3,2,1,0:T(8,128)}), f32[4,1,112,448]{3,2,1,0:T(8,128)S(1)}, u32[]{:S(2)}, u32[]{:S(2)}) async-start(f32[4,1,112,448]{3,2,1,0:T(8,128)} %shard_map.38), calls=%async_computation.1 | async-start | bytes 1835008 | tf_op jit(solution)/shard_map/all_to_all | solution.py:136
  90.5 2.7 %collective-permute-start.10 = (bf16[2,112,448]{2,1,0:T(8,128)(2,1)S(1)}, bf16[2,112,448]{2,1,0:T(8,128)(2,1)S(1)}, u32[]{:S(2)}, u32[]{:S(2)}) collective-permute-start(bf16[2,112,448]{2,1,0:T(8,128)(2,1)S(1)} %pad_maximum_fusion.5), channel_id=1, source_target_pairs={{0,6},{1,7},{2,0},{3,1},{4,2},{5,3},{6,4},{7,5},{8,14},{9,15},{10,... | collective-permute-start | bytes 602120 | tf_op jit(solution)/shard_map/ppermute | solution.py:26
  93.2 1.9 %collective-permute-start.18 = (bf16[456,1536]{1,0:T(8,128)(2,1)}, bf16[456,1536]{1,0:T(8,128)(2,1)}, u32[]{:S(2)}, u32[]{:S(2)}) collective-permute-start(bf16[456,1536]{1,0:T(8,128)(2,1)} %collective-permute-done.15), channel_id=1, source_target_pairs={{1,33},{3,35},{5,37},{7,39},{9,41},{11,43},{13,45},{15,47},{17,49}... | collective-permute-start | bytes 4202504 | tf_op jit(solution)/shard_map/ppermute | solution.py:26
  95.1 0.7 collective-permute-start.11
  95.8 12.0 %collective-permute-done.10 = bf16[2,112,448]{2,1,0:T(8,128)(2,1)S(1)} collective-permute-done((bf16[2,112,448]{2,1,0:T(8,128)(2,1)S(1)}, bf16[2,112,448]{2,1,0:T(8,128)(2,1)S(1)}, u32[]{:S(2)}, u32[]{:S(2)}) %collective-permute-start.10) | collective-permute-done | bytes 200736 | tf_op jit(solution)/shard_map/ppermute | solution.py:26
  107.8 0.8 collective-permute-start.12
  108.7 5.2 %collective-permute-done.12 = bf16[2,112,448]{2,1,0:T(8,128)(2,1)S(1)} collective-permute-done((bf16[2,112,448]{2,1,0:T(8,128)(2,1)S(1)}, bf16[2,112,448]{2,1,0:T(8,128)(2,1)S(1)}, u32[]{:S(2)}, u32[]{:S(2)}) %collective-permute-start.12) | collective-permute-done | bytes 200736 | tf_op jit(solution)/shard_map/ppermute | solution.py:26
  114.1 0.1 constant_dynamic-slice_fusion.1
  114.2 0.1 reduce_sum.21
  114.3 0.1 fusion.35
  114.4 1.3 collective-permute-start.17
  115.7 0.4 collective-permute-start.16
  116.1 9.1 %collective-permute-done.17 = bf16[112,448]{1,0:T(8,128)(2,1)S(1)} collective-permute-done((bf16[112,448]{1,0:T(8,128)(2,1)S(1)}, bf16[112,448]{1,0:T(8,128)(2,1)S(1)}, u32[]{:S(2)}, u32[]{:S(2)}) %collective-permute-start.17) | collective-permute-done | bytes 100384 | tf_op jit(solution)/shard_map/ppermute | solution.py:26
  125.2 1.0 broadcast_in_dim.27
  126.2 4.2 %all-to-all-start.2 = ((bf16[4,2,112,448]{3,2,1,0:T(8,128)(2,1)}), bf16[4,2,112,448]{3,2,1,0:T(8,128)(2,1)}, u32[]{:S(2)}, u32[]{:S(2)}) async-start(bf16[4,2,112,448]{3,2,1,0:T(8,128)(2,1)} %broadcast_in_dim.27), calls=%async_computation.2 | async-start | bytes 1835008 | tf_op jit(solution)/shard_map/all_to_all | solution.py:157
  130.5 4.5 %conditional.2 = (f32[448,1536]{1,0:T(8,128)S(1)}) conditional(s32[]{:T(128)} %clamp.4, (bf16[456,1536]{1,0:T(8,128)(2,1)}, bf16[448,448]{1,0:T(8,128)(2,1)S(1)}, bf16[456,1536]{1,0:T(8,128)(2,1)}, bf16[448,448]{1,0:T(8,128)(2,1)S(1)}) %tuple.83, (bf16[456,1536]{1,0:T(8,128)(2,1)}, bf16[448,448]{1,0:T(8,128)(2,1)S(1)}, ...), branch_computations={%region_2.3_spmd, %region_3.4_spmd, %region_4.5_spmd, %region_5.6_... | conditional | flops 1233813504 | bytes 11812872 | solution.py:208
  130.5 2.2 %fusion.4 = f32[448,1536]{1,0:T(8,128)S(1)} fusion(bf16[448,448]{1,0:T(8,128)(2,1)S(1)} %get-tuple-element.86, bf16[456,1536]{1,0:T(8,128)(2,1)} %get-tuple-element.87), kind=kOutput, calls=%fused_computation.6 | convolution fusion | flops 616562688 | bytes 4530176 | tf_op jit(solution)/shard_map/cond/branch_1_fun/dot_general | solution.py:50
  132.8 2.3 %convolution_add_fusion.1 = f32[448,1536]{1,0:T(8,128)S(1)} fusion(f32[448,1536]{1,0:T(8,128)S(1)} %fusion.4, bf16[448,448]{1,0:T(8,128)(2,1)S(1)} %get-tuple-element.88, bf16[456,1536]{1,0:T(8,128)(2,1)} %get-tuple-element.89), kind=kOutput, calls=%fused_computation.4 | convolution fusion | flops 617250816 | bytes 7282688 | tf_op jit(solution)/shard_map/cond/branch_1_fun/dot_general | solution.py:50
  135.0 8.2 %all-to-all-done.2 = bf16[4,2,112,448]{3,2,1,0:T(8,128)(2,1)} async-done(((bf16[4,2,112,448]{3,2,1,0:T(8,128)(2,1)}), bf16[4,2,112,448]{3,2,1,0:T(8,128)(2,1)}, u32[]{:S(2)}, u32[]{:S(2)}) %all-to-all-start.2) | async-done | bytes 802848 | tf_op jit(solution)/shard_map/all_to_all | solution.py:157
  143.2 1.3 fusion.42
  144.6 0.3 copy-done.1
  144.8 5.1 %conditional.3 = (f32[448,768]{1,0:T(8,128)S(1)}, f32[448,384]{1,0:T(8,128)S(1)}, f32[448,384]{1,0:T(8,128)S(1)}) conditional(s32[]{:T(128)} %clamp.4, (bf16[456,1536]{1,0:T(8,128)(2,1)}, bf16[448,448]{1,0:T(8,128)(2,1)S(1)}, bf16[448,448]{1,0:T(8,128)(2,1)S(1)}, bf16[448,1536]{1,0:T(8,128)(2,1)S(1)}, ...), branch_computations={%region_6.7_spmd, %region_7.8_spmd, %region_8.9_spmd, %region_9.10... | conditional | flops 1234845696 | bytes 28483636 | solution.py:228
  144.8 2.2 %fusion.17 = f32[448,1536]{1,0:T(8,128)S(1)} fusion(bf16[448,448]{1,0:T(8,128)(2,1)S(1)} %get-tuple-element.104, bf16[456,1536]{1,0:T(8,128)(2,1)} %get-tuple-element.105), kind=kOutput, calls=%fused_computation.25 | convolution fusion | flops 616562688 | bytes 4530176 | tf_op jit(solution)/shard_map/cond/branch_1_fun/dot_general | solution.py:50
  147.1 2.3 %fusion.15 = f32[448,1536]{1,0:T(8,128)S(1)} fusion(f32[448,1536]{1,0:T(8,128)S(1)} %get-tuple-element.103, f32[448,1536]{1,0:T(8,128)S(1)} %fusion.17, bf16[448,448]{1,0:T(8,128)(2,1)S(1)} %get-tuple-element.106, bf16[456,1536]{1,0:T(8,128)(2,1)} %get-tuple-element.107), kind=kOutput, calls=%fused_computation.22 | convolution fusion | flops 617938944 | bytes 10035200 | tf_op jit(solution)/shard_map/cond/branch_1_fun/dot_general | solution.py:50
  149.4 0.2 fusion.39
  149.6 0.1 pad_maximum_fusion.1
  149.9 0.1 collective-permute-start.19
  150.0 3.1 %collective-permute-done.19 = f32[448,768]{1,0:T(8,128)S(1)} collective-permute-done((f32[448,768]{1,0:T(8,128)S(1)}, f32[448,768]{1,0:T(8,128)S(1)}, u32[]{:S(2)}, u32[]{:S(2)}) %collective-permute-start.19) | collective-permute-done | bytes 1376288 | tf_op jit(solution)/shard_map/ppermute | solution.py:26
  153.1 0.1 slice_add_fusion
  153.2 5.2 %collective-permute-start.20 = (f32[448,384]{1,0:T(8,128)S(1)}, f32[448,384]{1,0:T(8,128)S(1)}, u32[]{:S(2)}, u32[]{:S(2)}) collective-permute-start(f32[448,384]{1,0:T(8,128)S(1)} %slice_add_fusion), channel_id=1, source_target_pairs={{0,8},{1,9},{2,10},{3,11},{4,12},{5,13},{6,14},{7,15},{8,0},{9,1},... | collective-permute-start | bytes 2064392 | tf_op jit(solution)/shard_map/ppermute | solution.py:26
  158.4 15.7 %collective-permute-done.20 = f32[448,384]{1,0:T(8,128)S(1)} collective-permute-done((f32[448,384]{1,0:T(8,128)S(1)}, f32[448,384]{1,0:T(8,128)S(1)}, u32[]{:S(2)}, u32[]{:S(2)}) %collective-permute-start.20) | collective-permute-done | bytes 688160 | tf_op jit(solution)/shard_map/ppermute | solution.py:26
  174.1 0.9 fusion.28
  (43 shorter events, 0.4 us)
Async XLA Ops:
  0.0 10.6 %collective-permute-start.1 = (bf16[448,384]{1,0:T(8,128)(2,1)}, bf16[448,384]{1,0:T(8,128)(2,1)S(1)}, u32[]{:S(2)}, u32[]{:S(2)}) collective-permute-start(bf16[448,384]{1,0:T(8,128)(2,1)} %bitcast.86), channel_id=1, source_target_pairs={{0,8},{1,9},{2,10},{3,11},{4,12},{5,13},{6,14},{7,15},{8,0},{9,1},... | collective-permute-start | bytes 1032200 | tf_op jit(solution)/shard_map/ppermute | solution.py:26
  3.6 9.2 %collective-permute-start = (bf16[448,384]{1,0:T(8,128)(2,1)}, bf16[448,384]{1,0:T(8,128)(2,1)S(1)}, u32[]{:S(2)}, u32[]{:S(2)}) collective-permute-start(bf16[448,384]{1,0:T(8,128)(2,1)} %bitcast.87), channel_id=1, source_target_pairs={{0,1},{1,0},{2,3},{3,2},{4,5},{5,4},{6,7},{7,6},{8,9},{9,8},{10,11... | collective-permute-start | bytes 1032200 | tf_op jit(solution)/shard_map/ppermute | solution.py:26
  10.6 3.5 %collective-permute-start.2 = (bf16[448,384]{1,0:T(8,128)(2,1)S(1)}, bf16[448,384]{1,0:T(8,128)(2,1)S(1)}, u32[]{:S(2)}, u32[]{:S(2)}) collective-permute-start(bf16[448,384]{1,0:T(8,128)(2,1)S(1)} %collective-permute-done.1), channel_id=1, source_target_pairs={{0,1},{1,0},{2,3},{3,2},{4,5},{5,4},{6,7},{7,6},{8,9},{9,8},{10,11... | collective-permute-start | bytes 1032200 | tf_op jit(solution)/shard_map/ppermute | solution.py:26
  14.6 22.7 %copy-start = (bf16[448,1536]{1,0:T(8,128)(2,1)}, bf16[448,1536]{1,0:T(8,128)(2,1)S(1)}, u32[]{:S(2)}) copy-start(bf16[448,1536]{1,0:T(8,128)(2,1)S(1)} %maximum_select_fusion) | copy-start | bytes 4128772
  14.7 21.9 %collective-permute-start.3 = (bf16[456,1536]{1,0:T(8,128)(2,1)S(1)}, bf16[456,1536]{1,0:T(8,128)(2,1)}, u32[]{:S(2)}, u32[]{:S(2)}) collective-permute-start(bf16[456,1536]{1,0:T(8,128)(2,1)S(1)} %pad_maximum_fusion.4.mine_ref), channel_id=1, source_target_pairs={{0,224},{1,33},{2,226},{3,35},{4,228},{5,37},{6,230},{7,39},{8,248... | collective-permute-start | bytes 4202504 | tf_op jit(solution)/shard_map/ppermute | solution.py:26
  16.6 20.8 %collective-permute-start.6 = (bf16[456,1536]{1,0:T(8,128)(2,1)S(1)}, bf16[456,1536]{1,0:T(8,128)(2,1)S(1)}, u32[]{:S(2)}, u32[]{:S(2)}) collective-permute-start(bf16[456,1536]{1,0:T(8,128)(2,1)S(1)} %pad_maximum_fusion.4.mine_ref), channel_id=1, source_target_pairs={{0,24},{2,26},{4,28},{6,30},{16,8},{18,10},{20,12},{22,14},{32,56}... | collective-permute-start | bytes 4202504 | tf_op jit(solution)/shard_map/ppermute | solution.py:26
  36.6 3.7 %collective-permute-start.5 = (bf16[456,1536]{1,0:T(8,128)(2,1)}, bf16[456,1536]{1,0:T(8,128)(2,1)S(1)}, u32[]{:S(2)}, u32[]{:S(2)}) collective-permute-start(bf16[456,1536]{1,0:T(8,128)(2,1)} %collective-permute-done.3.one_ref), channel_id=1, source_target_pairs={{0,1},{1,0},{2,3},{3,2},{4,5},{5,4},{6,7},{7,6},{8,9},{9,8},{10,11... | collective-permute-start | bytes 4202504 | tf_op jit(solution)/shard_map/ppermute | solution.py:26
  37.4 26.6 %collective-permute-start.4 = (bf16[456,1536]{1,0:T(8,128)(2,1)}, bf16[456,1536]{1,0:T(8,128)(2,1)}, u32[]{:S(2)}, u32[]{:S(2)}) collective-permute-start(bf16[456,1536]{1,0:T(8,128)(2,1)} %collective-permute-done.3.one_ref), channel_id=1, source_target_pairs={{0,224},{1,33},{2,226},{3,35},{4,228},{5,37},{6,230},{7,39},{8,232... | collective-permute-start | bytes 4202504 | tf_op jit(solution)/shard_map/ppermute | solution.py:26
  37.4 8.0 %copy-start.2 = (bf16[456,1536]{1,0:T(8,128)(2,1)}, bf16[456,1536]{1,0:T(8,128)(2,1)S(1)}, u32[]{:S(2)}) copy-start(bf16[456,1536]{1,0:T(8,128)(2,1)S(1)} %collective-permute-done.6.beyond_ref) | copy-start | bytes 4202500
  45.4 10.0 %copy-start.4 = (f32[448]{0:T(512)S(1)}, f32[448]{0:T(512)}, u32[]{:S(2)}) copy-start(f32[448]{0:T(512)} %param.13) | copy-start | bytes 5380
  45.4 33.9 %collective-permute-start.7 = (bf16[456,1536]{1,0:T(8,128)(2,1)S(1)}, bf16[456,1536]{1,0:T(8,128)(2,1)S(1)}, u32[]{:S(2)}, u32[]{:S(2)}) collective-permute-start(bf16[456,1536]{1,0:T(8,128)(2,1)S(1)} %collective-permute-done.5.swap_ref.swap_one_ref), channel_id=1, source_target_pairs={{1,225},{3,227},{5,229},{7,231},{9,233},{11,235},{13,237},{15,239}... | collective-permute-start | bytes 4202504 | tf_op jit(solution)/shard_map/ppermute | solution.py:26
  51.0 26.6 %all-to-all-start = ((f32[4,2,112,448]{3,2,1,0:T(8,128)}), f32[4,2,112,448]{3,2,1,0:T(8,128)}, u32[]{:S(2)}, u32[]{:S(2)}) async-start(f32[4,2,112,448]{3,2,1,0:T(8,128)} %shard_map.37), calls=%async_computation | async-start | bytes 3670016 | tf_op jit(solution)/shard_map/all_to_all | solution.py:136
  56.9 57.4 %collective-permute-start.13 = (bf16[456,1536]{1,0:T(8,128)(2,1)}, bf16[456,1536]{1,0:T(8,128)(2,1)}, u32[]{:S(2)}, u32[]{:S(2)}) collective-permute-start(bf16[456,1536]{1,0:T(8,128)(2,1)} %collective-permute-done.3.one_ref), channel_id=1, source_target_pairs={{1,25},{3,27},{5,29},{7,31},{17,9},{19,11},{21,13},{23,15},{33,57}... | collective-permute-start | bytes 4202504 | tf_op jit(solution)/shard_map/ppermute | solution.py:26
  64.0 29.2 %collective-permute-start.15 = (bf16[456,1536]{1,0:T(8,128)(2,1)}, bf16[456,1536]{1,0:T(8,128)(2,1)}, u32[]{:S(2)}, u32[]{:S(2)}) collective-permute-start(bf16[456,1536]{1,0:T(8,128)(2,1)} %collective-permute-done.4.two_ref), channel_id=1, source_target_pairs={{0,224},{1,33},{2,226},{3,35},{4,228},{5,37},{6,230},{7,39},{8,232... | collective-permute-start | bytes 4202504 | tf_op jit(solution)/shard_map/ppermute | solution.py:26
  64.0 50.3 %collective-permute-start.14 = (bf16[456,1536]{1,0:T(8,128)(2,1)}, bf16[456,1536]{1,0:T(8,128)(2,1)}, u32[]{:S(2)}, u32[]{:S(2)}) collective-permute-start(bf16[456,1536]{1,0:T(8,128)(2,1)} %collective-permute-done.4.two_ref), channel_id=1, source_target_pairs={{1,25},{3,27},{5,29},{7,31},{17,9},{19,11},{21,13},{23,15},{33,57}... | collective-permute-start | bytes 4202504 | tf_op jit(solution)/shard_map/ppermute | solution.py:26
  79.5 10.9 %collective-permute-start.9 = (bf16[112,448]{1,0:T(8,128)(2,1)S(1)}, bf16[112,448]{1,0:T(8,128)(2,1)S(1)}, u32[]{:S(2)}, u32[]{:S(2)}) collective-permute-start(bf16[112,448]{1,0:T(8,128)(2,1)S(1)} %get-tuple-element.183), channel_id=1, source_target_pairs={{1,33},{3,35},{5,37},{7,39},{9,57},{11,59},{13,61},{15,63},{17,49}... | collective-permute-start | bytes 301064 | tf_op jit(solution)/shard_map/ppermute | solution.py:26
  81.5 9.0 %collective-permute-start.8 = (bf16[112,448]{1,0:T(8,128)(2,1)S(1)}, bf16[112,448]{1,0:T(8,128)(2,1)S(1)}, u32[]{:S(2)}, u32[]{:S(2)}) collective-permute-start(bf16[112,448]{1,0:T(8,128)(2,1)S(1)} %get-tuple-element.183), channel_id=1, source_target_pairs={{0,33},{1,224},{2,35},{3,226},{4,37},{5,228},{6,39},{7,230},{8,57}... | collective-permute-start | bytes 301064 | tf_op jit(solution)/shard_map/ppermute | solution.py:26
  86.9 27.2 %all-to-all-start.1 = ((f32[4,1,112,448]{3,2,1,0:T(8,128)}), f32[4,1,112,448]{3,2,1,0:T(8,128)S(1)}, u32[]{:S(2)}, u32[]{:S(2)}) async-start(f32[4,1,112,448]{3,2,1,0:T(8,128)} %shard_map.38), calls=%async_computation.1 | async-start | bytes 1835008 | tf_op jit(solution)/shard_map/all_to_all | solution.py:136
  90.5 17.4 %collective-permute-start.10 = (bf16[2,112,448]{2,1,0:T(8,128)(2,1)S(1)}, bf16[2,112,448]{2,1,0:T(8,128)(2,1)S(1)}, u32[]{:S(2)}, u32[]{:S(2)}) collective-permute-start(bf16[2,112,448]{2,1,0:T(8,128)(2,1)S(1)} %pad_maximum_fusion.5), channel_id=1, source_target_pairs={{0,6},{1,7},{2,0},{3,1},{4,2},{5,3},{6,4},{7,5},{8,14},{9,15},{10,... | collective-permute-start | bytes 602120 | tf_op jit(solution)/shard_map/ppermute | solution.py:26
  93.2 51.3 %collective-permute-start.18 = (bf16[456,1536]{1,0:T(8,128)(2,1)}, bf16[456,1536]{1,0:T(8,128)(2,1)}, u32[]{:S(2)}, u32[]{:S(2)}) collective-permute-start(bf16[456,1536]{1,0:T(8,128)(2,1)} %collective-permute-done.15), channel_id=1, source_target_pairs={{1,33},{3,35},{5,37},{7,39},{9,41},{11,43},{13,45},{15,47},{17,49}... | collective-permute-start | bytes 4202504 | tf_op jit(solution)/shard_map/ppermute | solution.py:26
  95.1 13.5 %collective-permute-start.11 = (bf16[2,112,448]{2,1,0:T(8,128)(2,1)S(1)}, bf16[2,112,448]{2,1,0:T(8,128)(2,1)S(1)}, u32[]{:S(2)}, u32[]{:S(2)}) collective-permute-start(bf16[2,112,448]{2,1,0:T(8,128)(2,1)S(1)} %pad_maximum_fusion.5), channel_id=1, source_target_pairs={{0,4},{1,5},{2,6},{3,7},{4,0},{5,1},{6,2},{7,3},{8,12},{9,13},{10,... | collective-permute-start | bytes 602120 | tf_op jit(solution)/shard_map/ppermute | solution.py:26
  107.8 6.1 %collective-permute-start.12 = (bf16[2,112,448]{2,1,0:T(8,128)(2,1)S(1)}, bf16[2,112,448]{2,1,0:T(8,128)(2,1)S(1)}, u32[]{:S(2)}, u32[]{:S(2)}) collective-permute-start(bf16[2,112,448]{2,1,0:T(8,128)(2,1)S(1)} %pad_maximum_fusion.5), channel_id=1, source_target_pairs={{0,2},{1,3},{2,4},{3,5},{4,6},{5,7},{6,0},{7,1},{8,10},{9,11},{10,... | collective-permute-start | bytes 602120 | tf_op jit(solution)/shard_map/ppermute | solution.py:26
  114.4 10.8 %collective-permute-start.17 = (bf16[112,448]{1,0:T(8,128)(2,1)S(1)}, bf16[112,448]{1,0:T(8,128)(2,1)S(1)}, u32[]{:S(2)}, u32[]{:S(2)}) collective-permute-start(bf16[112,448]{1,0:T(8,128)(2,1)S(1)} %fusion.35), channel_id=1, source_target_pairs={{0,65},{2,67},{4,69},{6,71},{8,89},{10,91},{12,93},{14,95},{16,81}... | collective-permute-start | bytes 301064 | tf_op jit(solution)/shard_map/ppermute | solution.py:26
  115.7 9.5 %collective-permute-start.16 = (bf16[112,448]{1,0:T(8,128)(2,1)S(1)}, bf16[112,448]{1,0:T(8,128)(2,1)S(1)}, u32[]{:S(2)}, u32[]{:S(2)}) collective-permute-start(bf16[112,448]{1,0:T(8,128)(2,1)S(1)} %fusion.35), channel_id=1, source_target_pairs={{0,224},{1,193},{2,226},{3,195},{4,228},{5,197},{6,230},{7,199},{8... | collective-permute-start | bytes 301064 | tf_op jit(solution)/shard_map/ppermute | solution.py:26
  126.2 17.0 %all-to-all-start.2 = ((bf16[4,2,112,448]{3,2,1,0:T(8,128)(2,1)}), bf16[4,2,112,448]{3,2,1,0:T(8,128)(2,1)}, u32[]{:S(2)}, u32[]{:S(2)}) async-start(bf16[4,2,112,448]{3,2,1,0:T(8,128)(2,1)} %broadcast_in_dim.27), calls=%async_computation.2 | async-start | bytes 1835008 | tf_op jit(solution)/shard_map/all_to_all | solution.py:157
  143.2 1.6 copy-start.1
  149.9 3.2 %collective-permute-start.19 = (f32[448,768]{1,0:T(8,128)S(1)}, f32[448,768]{1,0:T(8,128)S(1)}, u32[]{:S(2)}, u32[]{:S(2)}) collective-permute-start(f32[448,768]{1,0:T(8,128)S(1)} %get-tuple-element.154), channel_id=1, source_target_pairs={{0,1},{1,0},{2,3},{3,2},{4,5},{5,4},{6,7},{7,6},{8,9},{9,8},{10,11... | collective-permute-start | bytes 4128776 | tf_op jit(solution)/shard_map/ppermute | solution.py:26
  153.2 20.9 %collective-permute-start.20 = (f32[448,384]{1,0:T(8,128)S(1)}, f32[448,384]{1,0:T(8,128)S(1)}, u32[]{:S(2)}, u32[]{:S(2)}) collective-permute-start(f32[448,384]{1,0:T(8,128)S(1)} %slice_add_fusion), channel_id=1, source_target_pairs={{0,8},{1,9},{2,10},{3,11},{4,12},{5,13},{6,14},{7,15},{8,0},{9,1},... | collective-permute-start | bytes 2064392 | tf_op jit(solution)/shard_map/ppermute | solution.py:26

commit v15 on v13

--- a/solution.py
+++ b/solution.py
@@ -132,8 +132,8 @@
     swap_one = other_core(step_one)
     step_two = moved(step_one, lambda z, xl, xh, y, c: (z - 1 if c == 0 else z + 1, xl, xh, y, c))
 
-    def over_y(parts):
-        return jnp.sum(lax.all_to_all(parts, "y", 0, 0, tiled=True), axis=0)
+    def exchanged(parts):
+        return lax.all_to_all(parts, "y", 0, 0, tiled=True)
 
     def energy(block):
         terms = block[nvir:, :nvir].astype(jnp.float32)
@@ -155,7 +155,7 @@
     parts, swap_one, step_one_after = lax.optimization_barrier((parts, swap_one, step_one))
     swap_two = moved(swap_one, lambda z, xl, xh, y, c: (z - 1, xl, xh, y, 1) if c == 1 else None)
     turned_one = moved(step_one_after, lambda z, xl, xh, y, c: (z, 1 - xl, 1, y, c) if (xh, c) == (0, 1) else None)
-    early = over_y(parts)
+    early = exchanged(parts)
     turned_two = moved(step_two, lambda z, xl, xh, y, c: (z, 1 - xl, 1, y, c) if (xh, c) == (0, 1) else None)
     step_three = moved(
         step_two,
@@ -163,8 +163,9 @@
     )
     turned_four = moved(step_three, lambda z, xl, xh, y, c: (z + 1, xl, xh, y, 1) if c == 1 else None)
 
-    step_two, swap_one, swap_two, early = lax.optimization_barrier((step_two, swap_one, swap_two, early))
-    late = over_y(numerators(late_kernel, 1, where, nvir, swap_one, swap_two, step_two))
+    parts = numerators(late_kernel, 1, where, nvir, swap_one, swap_two, step_two)
+    early, parts = lax.optimization_barrier((early, parts))
+    early, late = jnp.sum(early, axis=0), jnp.sum(exchanged(parts), axis=0)
 
     mine_energy, one_energy, swap_energy = energy(mine), energy(step_one), energy(swap_one)
     amps_one = amps(

time: 169 us -> 164 us (0.970)
  waiting for transfers between devices: 79.1 us -> 73.4 us
    all_to_all x2, waiting for transfers between devices: 16.6 us -> 0.01 us  [exchanged(): return lax.all_to_all(parts, 'y', 0, 0, tiled=True)]
    ppermute x18, waiting for transfers between devices: 51.5 us -> 63.4 us  [moved(): return lax.ppermute(array, ALL, pairs)]
  transfers between devices with their start and end apart: 22 -> 22, of which waited for: 11 -> 11; matrix products, arithmetic and copies ran while one was open for 8% -> 9% of each run, Pallas kernels for 5% -> 6%
where the time goes in v15:
time: 164 us; the launch traced here: 163 us
  waiting for transfers between devices  73.4 us (45%)
  starting transfers between devices  54.5 us (33%)
  matrix products  9.09 us (6%)
  Pallas kernels  9.03 us (6%)
  other arithmetic  8.62 us (5%)
  local copies, waits for them, and re-layouts  4.96 us (3%)
  between operations  3.17 us (2%)
    ppermute x18, waiting for transfers between devices, moved(): return lax.ppermute(array, ALL, pairs)  63.4 us
    ppermute x18, starting transfers between devices, moved(): return lax.ppermute(array, ALL, pairs)  37.5 us
    all_to_all x2, waiting for transfers between devices, to_all(): lax.all_to_all(jnp.broadcast_to(parts, (NY, *parts.shape)), 'y', 0, 0, ti...  10 us
    dot_general x4, matrix products, dot_tn(): lax.dot_general(a, b, (((0,), (0,)), ((), ())), preferred_element_type=jn...  9.09 us
    pallas_call x2, Pallas kernels, numerators(): pl.pallas_call(kernel, out_shape=jax.ShapeDtypeStruct((NY, count, share,...  9.03 us
    all_to_all x2, starting transfers between devices, exchanged(): return lax.all_to_all(parts, 'y', 0, 0, tiled=True)  8.56 us
    all_to_all x2, starting transfers between devices, to_all(): lax.all_to_all(jnp.broadcast_to(parts, (NY, *parts.shape)), 'y', 0, 0, ti...  8.45 us
  transfers between devices with their start and end apart: 22, of which 11 were waited for; matrix products, arithmetic and copies ran while one was open for 9% of the time, Pallas kernels for 6%

profile of v15, /device:TPU:1, one launch (start us, length us, event | category | flops | bytes accessed | tf_op | source)
XLA Modules:
  0.0 162.8 jit_solution(2886722585919220427)
XLA Ops:
  0.0 3.6 %collective-permute-start.1 = (bf16[448,384]{1,0:T(8,128)(2,1)}, bf16[448,384]{1,0:T(8,128)(2,1)S(1)}, u32[]{:S(2)}, u32[]{:S(2)}) collective-permute-start(bf16[448,384]{1,0:T(8,128)(2,1)} %bitcast.75), channel_id=1, source_target_pairs={{0,8},{1,9},{2,10},{3,11},{4,12},{5,13},{6,14},{7,15},{8,0},{9,1},... | collective-permute-start | bytes 1032200 | tf_op jit(solution)/shard_map/ppermute | solution.py:26
  3.6 1.0 collective-permute-start
  7.4 1.3 select_convert_fusion
  8.7 2.0 %collective-permute-done.1 = bf16[448,384]{1,0:T(8,128)(2,1)S(1)} collective-permute-done((bf16[448,384]{1,0:T(8,128)(2,1)}, bf16[448,384]{1,0:T(8,128)(2,1)S(1)}, u32[]{:S(2)}, u32[]{:S(2)}) %collective-permute-start.1) | collective-permute-done | bytes 344096 | tf_op jit(solution)/shard_map/ppermute | solution.py:26
  10.6 2.2 %collective-permute-start.2 = (bf16[448,384]{1,0:T(8,128)(2,1)S(1)}, bf16[448,384]{1,0:T(8,128)(2,1)S(1)}, u32[]{:S(2)}, u32[]{:S(2)}) collective-permute-start(bf16[448,384]{1,0:T(8,128)(2,1)S(1)} %collective-permute-done.1), channel_id=1, source_target_pairs={{0,1},{1,0},{2,3},{3,2},{4,5},{5,4},{6,7},{7,6},{8,9},{9,8},{10,11... | collective-permute-start | bytes 1032200 | tf_op jit(solution)/shard_map/ppermute | solution.py:26
  12.8 1.2 maximum_select_fusion.1
  14.0 0.0 collective-permute-done.2
  14.1 0.2 maximum_select_fusion.2
  14.2 0.3 maximum_select_fusion
  14.6 0.1 pad_maximum_fusion.4.mine_ref
  14.7 1.0 copy-done
  15.7 1.9 %collective-permute-start.3 = (bf16[456,1536]{1,0:T(8,128)(2,1)S(1)}, bf16[456,1536]{1,0:T(8,128)(2,1)}, u32[]{:S(2)}, u32[]{:S(2)}) collective-permute-start(bf16[456,1536]{1,0:T(8,128)(2,1)S(1)} %pad_maximum_fusion.4.mine_ref), channel_id=1, source_target_pairs={{0,224},{1,33},{2,226},{3,35},{4,228},{5,37},{6,230},{7,39},{8,248... | collective-permute-start | bytes 4202504 | tf_op jit(solution)/shard_map/ppermute | solution.py:26
  17.5 0.7 collective-permute-start.5
  18.3 19.3 %collective-permute-done.3.one_ref = bf16[456,1536]{1,0:T(8,128)(2,1)} collective-permute-done((bf16[456,1536]{1,0:T(8,128)(2,1)S(1)}, bf16[456,1536]{1,0:T(8,128)(2,1)}, u32[]{:S(2)}, u32[]{:S(2)}) %collective-permute-start.3) | collective-permute-done | bytes 1400864 | tf_op jit(solution)/shard_map/ppermute | solution.py:26
  37.5 0.7 collective-permute-start.4
  38.2 0.1 pad_add_fusion.where_ref
  38.3 0.0 collective-permute-start.7
  38.4 2.9 %collective-permute-done.4.swap_ref.swap_one_ref = bf16[456,1536]{1,0:T(8,128)(2,1)S(1)} collective-permute-done((bf16[456,1536]{1,0:T(8,128)(2,1)}, bf16[456,1536]{1,0:T(8,128)(2,1)S(1)}, u32[]{:S(2)}, u32[]{:S(2)}) %collective-permute-start.4) | collective-permute-done | bytes 1400864 | tf_op jit(solution)/shard_map/ppermute | solution.py:26
  41.2 5.1 %shard_map.37 = f32[4,2,112,448]{3,2,1,0:T(8,128)} custom-call(s32[2]{0:T(128)S(1)} %pad_add_fusion.where_ref, bf16[456,1536]{1,0:T(8,128)(2,1)S(1)} %pad_maximum_fusion.4.mine_ref, bf16[456,1536]{1,0:T(8,128)(2,1)} %collective-permute-done.3.one_ref, bf16[456,1536]{1,0:T(8,128)(2,1)S(1)} %collective-permute-done.4.swap_ref.swap_one_ref, ...), custom_call_target="tpu_custom_call" | custom-call | flops 2466250752 | bytes 7110656 | tf_op jit(solution)/shard_map/pallas_call | solution.py:91
  46.4 5.4 %collective-permute-start.6 = (bf16[456,1536]{1,0:T(8,128)(2,1)S(1)}, bf16[456,1536]{1,0:T(8,128)(2,1)S(1)}, u32[]{:S(2)}, u32[]{:S(2)}) collective-permute-start(bf16[456,1536]{1,0:T(8,128)(2,1)S(1)} %collective-permute-done.4.swap_ref.swap_one_ref), channel_id=1, source_target_pairs={{1,225},{3,227},{5,229},{7,231},{9,233},{11,235},{13,237},{15,239}... | collective-permute-start | bytes 4202504 | tf_op jit(solution)/shard_map/ppermute | solution.py:26
  51.8 0.1 dynamic_slice.3
  51.9 4.4 %all-to-all-start = ((f32[4,2,112,448]{3,2,1,0:T(8,128)}), f32[4,2,112,448]{3,2,1,0:T(8,128)}, u32[]{:S(2)}, u32[]{:S(2)}) async-start(f32[4,2,112,448]{3,2,1,0:T(8,128)} %shard_map.37), calls=%async_computation | async-start | bytes 3670016 | tf_op jit(solution)/shard_map/all_to_all | solution.py:136
  56.3 0.7 slice_convert_fusion.2
  57.0 0.7 slice_convert_fusion.3
  57.7 7.1 %collective-permute-start.10 = (bf16[456,1536]{1,0:T(8,128)(2,1)}, bf16[456,1536]{1,0:T(8,128)(2,1)}, u32[]{:S(2)}, u32[]{:S(2)}) collective-permute-start(bf16[456,1536]{1,0:T(8,128)(2,1)} %collective-permute-done.3.one_ref), channel_id=1, source_target_pairs={{1,25},{3,27},{5,29},{7,31},{17,9},{19,11},{21,13},{23,15},{33,57}... | collective-permute-start | bytes 4202504 | tf_op jit(solution)/shard_map/ppermute | solution.py:26
  64.8 2.4 %collective-permute-start.11 = (bf16[456,1536]{1,0:T(8,128)(2,1)}, bf16[456,1536]{1,0:T(8,128)(2,1)}, u32[]{:S(2)}, u32[]{:S(2)}) collective-permute-start(bf16[456,1536]{1,0:T(8,128)(2,1)} %collective-permute-done.7.two_ref), channel_id=1, source_target_pairs={{1,25},{3,27},{5,29},{7,31},{17,9},{19,11},{21,13},{23,15},{33,57}... | collective-permute-start | bytes 4202504 | tf_op jit(solution)/shard_map/ppermute | solution.py:26
  67.2 10.0 %collective-permute-done.6.swap_two_ref = bf16[456,1536]{1,0:T(8,128)(2,1)S(1)} collective-permute-done((bf16[456,1536]{1,0:T(8,128)(2,1)S(1)}, bf16[456,1536]{1,0:T(8,128)(2,1)S(1)}, u32[]{:S(2)}, u32[]{:S(2)}) %collective-permute-start.6) | collective-permute-done | bytes 1400864 | tf_op jit(solution)/shard_map/ppermute | solution.py:26
  77.2 3.9 %shard_map.38 = f32[4,1,112,448]{3,2,1,0:T(8,128)} custom-call(s32[2]{0:T(128)S(1)} %pad_add_fusion.where_ref, bf16[456,1536]{1,0:T(8,128)(2,1)S(1)} %collective-permute-done.4.swap_ref.swap_one_ref, bf16[456,1536]{1,0:T(8,128)(2,1)S(1)} %collective-permute-done.6.swap_two_ref, bf16[456,1536]{1,0:T(8,128)(2,1)} %collective-permute-done.7.two_ref), custom_call_target="tpu_custom_call" | custom-call | flops 1233125376 | bytes 4931584 | tf_op jit(solution)/shard_map/pallas_call | solution.py:91
  81.1 4.2 %all-to-all-start.1 = ((f32[4,1,112,448]{3,2,1,0:T(8,128)}), f32[4,1,112,448]{3,2,1,0:T(8,128)S(1)}, u32[]{:S(2)}, u32[]{:S(2)}) async-start(f32[4,1,112,448]{3,2,1,0:T(8,128)} %shard_map.38), calls=%async_computation.1 | async-start | bytes 1835008 | tf_op jit(solution)/shard_map/all_to_all | solution.py:136
  85.3 1.7 %reduce_sum.22 = f32[2,112,448]{2,1,0:T(8,128)S(1)} reduce(f32[4,2,112,448]{3,2,1,0:T(8,128)} %all-to-all-done, f32[]{:T(128)} %constant.7.clone.1), dimensions={0}, to_apply=%region_1.2 | reduce | flops 301056 | bytes 2007044 | tf_op jit(solution)/shard_map/reduce_sum | solution.py:168
  87.1 0.1 fusion.36
  87.2 1.9 %collective-permute-start.9 = (bf16[112,448]{1,0:T(8,128)(2,1)S(1)}, bf16[112,448]{1,0:T(8,128)(2,1)S(1)}, u32[]{:S(2)}, u32[]{:S(2)}) collective-permute-start(bf16[112,448]{1,0:T(8,128)(2,1)S(1)} %get-tuple-element.189), channel_id=1, source_target_pairs={{1,33},{3,35},{5,37},{7,39},{9,57},{11,59},{13,61},{15,63},{17,49}... | collective-permute-start | bytes 301064 | tf_op jit(solution)/shard_map/ppermute | solution.py:26
  89.2 0.7 slice_convert_fusion
  89.9 5.8 %collective-permute-done.9 = bf16[112,448]{1,0:T(8,128)(2,1)S(1)} collective-permute-done((bf16[112,448]{1,0:T(8,128)(2,1)S(1)}, bf16[112,448]{1,0:T(8,128)(2,1)S(1)}, u32[]{:S(2)}, u32[]{:S(2)}) %collective-permute-start.9) | collective-permute-done | bytes 100384 | tf_op jit(solution)/shard_map/ppermute | solution.py:26
  95.7 0.1 reduce_sum.20
  95.8 0.2 collective-permute-done.8
  96.1 1.0 broadcast_in_dim.30
  97.1 4.2 %all-to-all-start.2 = ((bf16[4,2,112,448]{3,2,1,0:T(8,128)(2,1)}), bf16[4,2,112,448]{3,2,1,0:T(8,128)(2,1)S(1)}, u32[]{:S(2)}, u32[]{:S(2)}) async-start(bf16[4,2,112,448]{3,2,1,0:T(8,128)(2,1)} %broadcast_in_dim.30), calls=%async_computation.2 | async-start | bytes 1835008 | tf_op jit(solution)/shard_map/all_to_all | solution.py:150
  101.4 0.1 fusion.35
  101.5 1.3 collective-permute-start.14
  102.8 1.9 %collective-permute-start.15 = (bf16[456,1536]{1,0:T(8,128)(2,1)}, bf16[456,1536]{1,0:T(8,128)(2,1)}, u32[]{:S(2)}, u32[]{:S(2)}) collective-permute-start(bf16[456,1536]{1,0:T(8,128)(2,1)} %collective-permute-done.12), channel_id=1, source_target_pairs={{1,33},{3,35},{5,37},{7,39},{9,41},{11,43},{13,45},{15,47},{17,49}... | collective-permute-start | bytes 4202504 | tf_op jit(solution)/shard_map/ppermute | solution.py:26
  104.7 2.9 %collective-permute-start.13 = (bf16[112,448]{1,0:T(8,128)(2,1)S(1)}, bf16[112,448]{1,0:T(8,128)(2,1)S(1)}, u32[]{:S(2)}, u32[]{:S(2)}) collective-permute-start(bf16[112,448]{1,0:T(8,128)(2,1)S(1)} %fusion.35), channel_id=1, source_target_pairs={{0,224},{1,193},{2,226},{3,195},{4,228},{5,197},{6,230},{7,199},{8... | collective-permute-start | bytes 301064 | tf_op jit(solution)/shard_map/ppermute | solution.py:26
  107.6 4.4 %collective-permute-done.14 = bf16[112,448]{1,0:T(8,128)(2,1)S(1)} collective-permute-done((bf16[112,448]{1,0:T(8,128)(2,1)S(1)}, bf16[112,448]{1,0:T(8,128)(2,1)S(1)}, u32[]{:S(2)}, u32[]{:S(2)}) %collective-permute-start.14) | collective-permute-done | bytes 100384 | tf_op jit(solution)/shard_map/ppermute | solution.py:26
  112.0 0.6 all-to-all-done.2
  112.6 0.1 fusion.43
  112.7 1.0 broadcast_in_dim.31
  113.7 4.2 %all-to-all-start.3 = ((bf16[4,2,112,448]{3,2,1,0:T(8,128)(2,1)}), bf16[4,2,112,448]{3,2,1,0:T(8,128)(2,1)}, u32[]{:S(2)}, u32[]{:S(2)}) async-start(bf16[4,2,112,448]{3,2,1,0:T(8,128)(2,1)} %broadcast_in_dim.31), calls=%async_computation.3 | async-start | bytes 1835008 | tf_op jit(solution)/shard_map/all_to_all | solution.py:150
  118.0 4.5 %conditional.2 = (f32[448,1536]{1,0:T(8,128)S(1)}) conditional(s32[]{:T(128)} %clamp.4, (bf16[456,1536]{1,0:T(8,128)(2,1)}, bf16[448,448]{1,0:T(8,128)(2,1)S(1)}, bf16[456,1536]{1,0:T(8,128)(2,1)}, bf16[448,448]{1,0:T(8,128)(2,1)S(1)}) %tuple.85, (bf16[456,1536]{1,0:T(8,128)(2,1)}, bf16[448,448]{1,0:T(8,128)(2,1)S(1)}, ...), branch_computations={%region_2.3_spmd, %region_3.4_spmd, %region_4.5_spmd, %region_5.6_... | conditional | flops 1233813504 | bytes 11812872 | solution.py:204
  118.0 2.2 %fusion.4 = f32[448,1536]{1,0:T(8,128)S(1)} fusion(bf16[448,448]{1,0:T(8,128)(2,1)S(1)} %get-tuple-element.86, bf16[456,1536]{1,0:T(8,128)(2,1)} %get-tuple-element.87), kind=kOutput, calls=%fused_computation.6 | convolution fusion | flops 616562688 | bytes 4530176 | tf_op jit(solution)/shard_map/cond/branch_1_fun/dot_general | solution.py:50
  120.2 2.3 %convolution_add_fusion.1 = f32[448,1536]{1,0:T(8,128)S(1)} fusion(f32[448,1536]{1,0:T(8,128)S(1)} %fusion.4, bf16[448,448]{1,0:T(8,128)(2,1)S(1)} %get-tuple-element.88, bf16[456,1536]{1,0:T(8,128)(2,1)} %get-tuple-element.89), kind=kOutput, calls=%fused_computation.4 | convolution fusion | flops 617250816 | bytes 7282688 | tf_op jit(solution)/shard_map/cond/branch_1_fun/dot_general | solution.py:50
  122.5 9.4 %all-to-all-done.3 = bf16[4,2,112,448]{3,2,1,0:T(8,128)(2,1)} async-done(((bf16[4,2,112,448]{3,2,1,0:T(8,128)(2,1)}), bf16[4,2,112,448]{3,2,1,0:T(8,128)(2,1)}, u32[]{:S(2)}, u32[]{:S(2)}) %all-to-all-start.3) | async-done | bytes 802848 | tf_op jit(solution)/shard_map/all_to_all | solution.py:150
  132.0 1.3 fusion.42
  133.3 0.3 copy-done.1
  133.6 4.9 %conditional.3 = (f32[448,768]{1,0:T(8,128)S(1)}, f32[448,384]{1,0:T(8,128)S(1)}, f32[448,384]{1,0:T(8,128)S(1)}) conditional(s32[]{:T(128)} %clamp.4, (bf16[456,1536]{1,0:T(8,128)(2,1)}, bf16[448,448]{1,0:T(8,128)(2,1)S(1)}, bf16[448,448]{1,0:T(8,128)(2,1)S(1)}, bf16[448,1536]{1,0:T(8,128)(2,1)S(1)}, ...), branch_computations={%region_6.7_spmd, %region_7.8_spmd, %region_8.9_spmd, %region_9.10... | conditional | flops 1234845696 | bytes 28483636 | solution.py:224
  133.6 2.2 %fusion.17 = f32[448,1536]{1,0:T(8,128)S(1)} fusion(bf16[448,448]{1,0:T(8,128)(2,1)S(1)} %get-tuple-element.104, bf16[456,1536]{1,0:T(8,128)(2,1)} %get-tuple-element.105), kind=kOutput, calls=%fused_computation.25 | convolution fusion | flops 616562688 | bytes 4530176 | tf_op jit(solution)/shard_map/cond/branch_1_fun/dot_general | solution.py:50
  135.8 2.3 %fusion.15 = f32[448,1536]{1,0:T(8,128)S(1)} fusion(f32[448,1536]{1,0:T(8,128)S(1)} %get-tuple-element.103, f32[448,1536]{1,0:T(8,128)S(1)} %fusion.17, bf16[448,448]{1,0:T(8,128)(2,1)S(1)} %get-tuple-element.106, bf16[456,1536]{1,0:T(8,128)(2,1)} %get-tuple-element.107), kind=kOutput, calls=%fused_computation.22 | convolution fusion | flops 617938944 | bytes 10035200 | tf_op jit(solution)/shard_map/cond/branch_1_fun/dot_general | solution.py:50
  138.1 0.2 fusion.39
  138.3 0.1 pad_maximum_fusion.1
  138.4 0.1 collective-permute-start.16
  138.5 3.1 %collective-permute-done.16 = f32[448,768]{1,0:T(8,128)S(1)} collective-permute-done((f32[448,768]{1,0:T(8,128)S(1)}, f32[448,768]{1,0:T(8,128)S(1)}, u32[]{:S(2)}, u32[]{:S(2)}) %collective-permute-start.16) | collective-permute-done | bytes 1376288 | tf_op jit(solution)/shard_map/ppermute | solution.py:26
  141.7 0.1 slice_add_fusion
  141.7 4.5 %collective-permute-start.17 = (f32[448,384]{1,0:T(8,128)S(1)}, f32[448,384]{1,0:T(8,128)S(1)}, u32[]{:S(2)}, u32[]{:S(2)}) collective-permute-start(f32[448,384]{1,0:T(8,128)S(1)} %slice_add_fusion), channel_id=1, source_target_pairs={{0,8},{1,9},{2,10},{3,11},{4,12},{5,13},{6,14},{7,15},{8,0},{9,1},... | collective-permute-start | bytes 2064392 | tf_op jit(solution)/shard_map/ppermute | solution.py:26
  146.2 15.7 %collective-permute-done.17 = f32[448,384]{1,0:T(8,128)S(1)} collective-permute-done((f32[448,384]{1,0:T(8,128)S(1)}, f32[448,384]{1,0:T(8,128)S(1)}, u32[]{:S(2)}, u32[]{:S(2)}) %collective-permute-start.17) | collective-permute-done | bytes 688160 | tf_op jit(solution)/shard_map/ppermute | solution.py:26
  161.9 0.9 fusion.28
  (32 shorter events, 0.2 us)
Async XLA Ops:
  0.0 10.6 %collective-permute-start.1 = (bf16[448,384]{1,0:T(8,128)(2,1)}, bf16[448,384]{1,0:T(8,128)(2,1)S(1)}, u32[]{:S(2)}, u32[]{:S(2)}) collective-permute-start(bf16[448,384]{1,0:T(8,128)(2,1)} %bitcast.75), channel_id=1, source_target_pairs={{0,8},{1,9},{2,10},{3,11},{4,12},{5,13},{6,14},{7,15},{8,0},{9,1},... | collective-permute-start | bytes 1032200 | tf_op jit(solution)/shard_map/ppermute | solution.py:26
  3.6 9.2 %collective-permute-start = (bf16[448,384]{1,0:T(8,128)(2,1)}, bf16[448,384]{1,0:T(8,128)(2,1)S(1)}, u32[]{:S(2)}, u32[]{:S(2)}) collective-permute-start(bf16[448,384]{1,0:T(8,128)(2,1)} %bitcast.76), channel_id=1, source_target_pairs={{0,1},{1,0},{2,3},{3,2},{4,5},{5,4},{6,7},{7,6},{8,9},{9,8},{10,11... | collective-permute-start | bytes 1032200 | tf_op jit(solution)/shard_map/ppermute | solution.py:26
  10.6 3.5 %collective-permute-start.2 = (bf16[448,384]{1,0:T(8,128)(2,1)S(1)}, bf16[448,384]{1,0:T(8,128)(2,1)S(1)}, u32[]{:S(2)}, u32[]{:S(2)}) collective-permute-start(bf16[448,384]{1,0:T(8,128)(2,1)S(1)} %collective-permute-done.1), channel_id=1, source_target_pairs={{0,1},{1,0},{2,3},{3,2},{4,5},{5,4},{6,7},{7,6},{8,9},{9,8},{10,11... | collective-permute-start | bytes 1032200 | tf_op jit(solution)/shard_map/ppermute | solution.py:26
  14.6 1.1 copy-start
  15.7 21.9 %collective-permute-start.3 = (bf16[456,1536]{1,0:T(8,128)(2,1)S(1)}, bf16[456,1536]{1,0:T(8,128)(2,1)}, u32[]{:S(2)}, u32[]{:S(2)}) collective-permute-start(bf16[456,1536]{1,0:T(8,128)(2,1)S(1)} %pad_maximum_fusion.4.mine_ref), channel_id=1, source_target_pairs={{0,224},{1,33},{2,226},{3,35},{4,228},{5,37},{6,230},{7,39},{8,248... | collective-permute-start | bytes 4202504 | tf_op jit(solution)/shard_map/ppermute | solution.py:26
  17.5 20.8 %collective-permute-start.5 = (bf16[456,1536]{1,0:T(8,128)(2,1)S(1)}, bf16[456,1536]{1,0:T(8,128)(2,1)S(1)}, u32[]{:S(2)}, u32[]{:S(2)}) collective-permute-start(bf16[456,1536]{1,0:T(8,128)(2,1)S(1)} %pad_maximum_fusion.4.mine_ref), channel_id=1, source_target_pairs={{0,24},{2,26},{4,28},{6,30},{16,8},{18,10},{20,12},{22,14},{32,56}... | collective-permute-start | bytes 4202504 | tf_op jit(solution)/shard_map/ppermute | solution.py:26
  37.5 3.7 %collective-permute-start.4 = (bf16[456,1536]{1,0:T(8,128)(2,1)}, bf16[456,1536]{1,0:T(8,128)(2,1)S(1)}, u32[]{:S(2)}, u32[]{:S(2)}) collective-permute-start(bf16[456,1536]{1,0:T(8,128)(2,1)} %collective-permute-done.3.one_ref), channel_id=1, source_target_pairs={{0,1},{1,0},{2,3},{3,2},{4,5},{5,4},{6,7},{7,6},{8,9},{9,8},{10,11... | collective-permute-start | bytes 4202504 | tf_op jit(solution)/shard_map/ppermute | solution.py:26
  38.3 13.5 %copy-start.4 = (f32[448]{0:T(512)S(1)}, f32[448]{0:T(512)}, u32[]{:S(2)}) copy-start(f32[448]{0:T(512)} %param.13) | copy-start | bytes 5380
  38.3 26.5 %collective-permute-start.7 = (bf16[456,1536]{1,0:T(8,128)(2,1)}, bf16[456,1536]{1,0:T(8,128)(2,1)}, u32[]{:S(2)}, u32[]{:S(2)}) collective-permute-start(bf16[456,1536]{1,0:T(8,128)(2,1)} %collective-permute-done.3.one_ref), channel_id=1, source_target_pairs={{0,224},{1,33},{2,226},{3,35},{4,228},{5,37},{6,230},{7,39},{8,232... | collective-permute-start | bytes 4202504 | tf_op jit(solution)/shard_map/ppermute | solution.py:26
  38.3 8.0 %copy-start.2 = (bf16[456,1536]{1,0:T(8,128)(2,1)}, bf16[456,1536]{1,0:T(8,128)(2,1)S(1)}, u32[]{:S(2)}) copy-start(bf16[456,1536]{1,0:T(8,128)(2,1)S(1)} %collective-permute-done.5.beyond_ref) | copy-start | bytes 4202500
  46.4 30.8 %collective-permute-start.6 = (bf16[456,1536]{1,0:T(8,128)(2,1)S(1)}, bf16[456,1536]{1,0:T(8,128)(2,1)S(1)}, u32[]{:S(2)}, u32[]{:S(2)}) collective-permute-start(bf16[456,1536]{1,0:T(8,128)(2,1)S(1)} %collective-permute-done.4.swap_ref.swap_one_ref), channel_id=1, source_target_pairs={{1,225},{3,227},{5,229},{7,231},{9,233},{11,235},{13,237},{15,239}... | collective-permute-start | bytes 4202504 | tf_op jit(solution)/shard_map/ppermute | solution.py:26
  51.9 29.2 %all-to-all-start = ((f32[4,2,112,448]{3,2,1,0:T(8,128)}), f32[4,2,112,448]{3,2,1,0:T(8,128)}, u32[]{:S(2)}, u32[]{:S(2)}) async-start(f32[4,2,112,448]{3,2,1,0:T(8,128)} %shard_map.37), calls=%async_computation | async-start | bytes 3670016 | tf_op jit(solution)/shard_map/all_to_all | solution.py:136
  57.7 38.1 %collective-permute-start.10 = (bf16[456,1536]{1,0:T(8,128)(2,1)}, bf16[456,1536]{1,0:T(8,128)(2,1)}, u32[]{:S(2)}, u32[]{:S(2)}) collective-permute-start(bf16[456,1536]{1,0:T(8,128)(2,1)} %collective-permute-done.3.one_ref), channel_id=1, source_target_pairs={{1,25},{3,27},{5,29},{7,31},{17,9},{19,11},{21,13},{23,15},{33,57}... | collective-permute-start | bytes 4202504 | tf_op jit(solution)/shard_map/ppermute | solution.py:26
  64.8 31.0 %collective-permute-start.12 = (bf16[456,1536]{1,0:T(8,128)(2,1)}, bf16[456,1536]{1,0:T(8,128)(2,1)}, u32[]{:S(2)}, u32[]{:S(2)}) collective-permute-start(bf16[456,1536]{1,0:T(8,128)(2,1)} %collective-permute-done.7.two_ref), channel_id=1, source_target_pairs={{0,224},{1,33},{2,226},{3,35},{4,228},{5,37},{6,230},{7,39},{8,232... | collective-permute-start | bytes 4202504 | tf_op jit(solution)/shard_map/ppermute | solution.py:26
  64.8 31.1 %collective-permute-start.11 = (bf16[456,1536]{1,0:T(8,128)(2,1)}, bf16[456,1536]{1,0:T(8,128)(2,1)}, u32[]{:S(2)}, u32[]{:S(2)}) collective-permute-start(bf16[456,1536]{1,0:T(8,128)(2,1)} %collective-permute-done.7.two_ref), channel_id=1, source_target_pairs={{1,25},{3,27},{5,29},{7,31},{17,9},{19,11},{21,13},{23,15},{33,57}... | collective-permute-start | bytes 4202504 | tf_op jit(solution)/shard_map/ppermute | solution.py:26
  81.1 14.6 %all-to-all-start.1 = ((f32[4,1,112,448]{3,2,1,0:T(8,128)}), f32[4,1,112,448]{3,2,1,0:T(8,128)S(1)}, u32[]{:S(2)}, u32[]{:S(2)}) async-start(f32[4,1,112,448]{3,2,1,0:T(8,128)} %shard_map.38), calls=%async_computation.1 | async-start | bytes 1835008 | tf_op jit(solution)/shard_map/all_to_all | solution.py:136
  87.2 8.4 %collective-permute-start.9 = (bf16[112,448]{1,0:T(8,128)(2,1)S(1)}, bf16[112,448]{1,0:T(8,128)(2,1)S(1)}, u32[]{:S(2)}, u32[]{:S(2)}) collective-permute-start(bf16[112,448]{1,0:T(8,128)(2,1)S(1)} %get-tuple-element.189), channel_id=1, source_target_pairs={{1,33},{3,35},{5,37},{7,39},{9,57},{11,59},{13,61},{15,63},{17,49}... | collective-permute-start | bytes 301064 | tf_op jit(solution)/shard_map/ppermute | solution.py:26
  89.9 6.2 %collective-permute-start.8 = (bf16[112,448]{1,0:T(8,128)(2,1)S(1)}, bf16[112,448]{1,0:T(8,128)(2,1)S(1)}, u32[]{:S(2)}, u32[]{:S(2)}) collective-permute-start(bf16[112,448]{1,0:T(8,128)(2,1)S(1)} %get-tuple-element.189), channel_id=1, source_target_pairs={{0,33},{1,224},{2,35},{3,226},{4,37},{5,228},{6,39},{7,230},{8,57}... | collective-permute-start | bytes 301064 | tf_op jit(solution)/shard_map/ppermute | solution.py:26
  97.1 15.5 %all-to-all-start.2 = ((bf16[4,2,112,448]{3,2,1,0:T(8,128)(2,1)}), bf16[4,2,112,448]{3,2,1,0:T(8,128)(2,1)S(1)}, u32[]{:S(2)}, u32[]{:S(2)}) async-start(bf16[4,2,112,448]{3,2,1,0:T(8,128)(2,1)} %broadcast_in_dim.30), calls=%async_computation.2 | async-start | bytes 1835008 | tf_op jit(solution)/shard_map/all_to_all | solution.py:150
  101.5 10.5 %collective-permute-start.14 = (bf16[112,448]{1,0:T(8,128)(2,1)S(1)}, bf16[112,448]{1,0:T(8,128)(2,1)S(1)}, u32[]{:S(2)}, u32[]{:S(2)}) collective-permute-start(bf16[112,448]{1,0:T(8,128)(2,1)S(1)} %fusion.35), channel_id=1, source_target_pairs={{0,65},{2,67},{4,69},{6,71},{8,89},{10,91},{12,93},{14,95},{16,81}... | collective-permute-start | bytes 301064 | tf_op jit(solution)/shard_map/ppermute | solution.py:26
  102.8 30.5 %collective-permute-start.15 = (bf16[456,1536]{1,0:T(8,128)(2,1)}, bf16[456,1536]{1,0:T(8,128)(2,1)}, u32[]{:S(2)}, u32[]{:S(2)}) collective-permute-start(bf16[456,1536]{1,0:T(8,128)(2,1)} %collective-permute-done.12), channel_id=1, source_target_pairs={{1,33},{3,35},{5,37},{7,39},{9,41},{11,43},{13,45},{15,47},{17,49}... | collective-permute-start | bytes 4202504 | tf_op jit(solution)/shard_map/ppermute | solution.py:26
  104.7 8.0 %collective-permute-start.13 = (bf16[112,448]{1,0:T(8,128)(2,1)S(1)}, bf16[112,448]{1,0:T(8,128)(2,1)S(1)}, u32[]{:S(2)}, u32[]{:S(2)}) collective-permute-start(bf16[112,448]{1,0:T(8,128)(2,1)S(1)} %fusion.35), channel_id=1, source_target_pairs={{0,224},{1,193},{2,226},{3,195},{4,228},{5,197},{6,230},{7,199},{8... | collective-permute-start | bytes 301064 | tf_op jit(solution)/shard_map/ppermute | solution.py:26
  113.7 18.2 %all-to-all-start.3 = ((bf16[4,2,112,448]{3,2,1,0:T(8,128)(2,1)}), bf16[4,2,112,448]{3,2,1,0:T(8,128)(2,1)}, u32[]{:S(2)}, u32[]{:S(2)}) async-start(bf16[4,2,112,448]{3,2,1,0:T(8,128)(2,1)} %broadcast_in_dim.31), calls=%async_computation.3 | async-start | bytes 1835008 | tf_op jit(solution)/shard_map/all_to_all | solution.py:150
  132.0 1.6 copy-start.1
  138.4 3.2 %collective-permute-start.16 = (f32[448,768]{1,0:T(8,128)S(1)}, f32[448,768]{1,0:T(8,128)S(1)}, u32[]{:S(2)}, u32[]{:S(2)}) collective-permute-start(f32[448,768]{1,0:T(8,128)S(1)} %get-tuple-element.160), channel_id=1, source_target_pairs={{0,1},{1,0},{2,3},{3,2},{4,5},{5,4},{6,7},{7,6},{8,9},{9,8},{10,11... | collective-permute-start | bytes 4128776 | tf_op jit(solution)/shard_map/ppermute | solution.py:26
  141.7 20.2 %collective-permute-start.17 = (f32[448,384]{1,0:T(8,128)S(1)}, f32[448,384]{1,0:T(8,128)S(1)}, u32[]{:S(2)}, u32[]{:S(2)}) collective-permute-start(f32[448,384]{1,0:T(8,128)S(1)} %slice_add_fusion), channel_id=1, source_target_pairs={{0,8},{1,9},{2,10},{3,11},{4,12},{5,13},{6,14},{7,15},{8,0},{9,1},... | collective-permute-start | bytes 2064392 | tf_op jit(solution)/shard_map/ppermute | solution.py:26

commit v16 on v15

--- a/solution.py
+++ b/solution.py
@@ -145,6 +145,12 @@
     def amps(value, a, b):
         return (value / (virs - a - b)).astype(jnp.bfloat16)
 
+    def by_hops(*parts):
+        parts = jnp.stack(parts)
+        hops = [parts] + [moved(parts, lambda z, xl, xh, y, c, n=n: (z, xl, xh, y - n, c)) for n in range(1, NY)]
+        whole = lax.dynamic_slice_in_dim(jnp.stack(hops + hops[:-1]), (NY - y) % NY, NY, axis=0)
+        return [whole[:, n].reshape(nvir, nvir) for n in range(parts.shape[0])]
+
     def to_all(*parts):
         parts = jnp.stack(parts)
         whole = lax.all_to_all(jnp.broadcast_to(parts, (NY, *parts.shape)), "y", 0, 0, tiled=True)
@@ -195,7 +201,7 @@
     fourth = moved(amps_two, lambda z, xl, xh, y, c: (z + 2, kind(xl, xh), xh, y, 1) if c == 0 else None)
     fourth = jnp.where(c == 0, amps_zero, fourth)
     third, fourth, first, second, turned_two = lax.optimization_barrier((third, fourth, first, second, turned_two))
-    third, fourth = to_all(third, fourth)
+    third, fourth = by_hops(third, fourth)
 
     def product(dot, *blocks):
         return lambda parts: sum(dot(part, block[:nvir]) for part, block in zip(parts, blocks))

time: 164 us -> 166 us (1.012)
    ppermute x18 -> x21, waiting for transfers between devices: 63.4 us -> 72.7 us  [moved(): return lax.ppermute(array, ALL, pairs)]
    all_to_all x2 -> x1, waiting for transfers between devices: 10 us -> 1.66 us  [to_all(): lax.all_to_all(jnp.broadcast_to(parts, (NY, *parts.shape)), 'y', 0, 0, ti...]
    all_to_all x2 -> x1, starting transfers between devices: 8.45 us -> 4.24 us  [to_all(): lax.all_to_all(jnp.broadcast_to(parts, (NY, *parts.shape)), 'y', 0, 0, ti...]
    ppermute x18 -> x21, starting transfers between devices: 37.5 us -> 40.4 us  [moved(): return lax.ppermute(array, ALL, pairs)]
    unnamed x8 -> x14, local copies, waits for them, and re-layouts: 1.28 us -> 3.99 us
  transfers between devices with their start and end apart: 22 -> 24, of which waited for: 11 -> 14; matrix products, arithmetic and copies ran while one was open for 9% -> 10% of each run, Pallas kernels for 6% -> 5%
where the time goes in v16:
time: 166 us; the launch traced here: 165 us
  waiting for transfers between devices  74.4 us (45%)
  starting transfers between devices  53.2 us (32%)
  other arithmetic  9.44 us (6%)
  matrix products  9.08 us (5%)
  Pallas kernels  9.03 us (5%)
  local copies, waits for them, and re-layouts  6.36 us (4%)
  between operations  3.37 us (2%)
    ppermute x21, waiting for transfers between devices, moved(): return lax.ppermute(array, ALL, pairs)  72.7 us
    ppermute x21, starting transfers between devices, moved(): return lax.ppermute(array, ALL, pairs)  40.4 us
    dot_general x4, matrix products, dot_tn(): lax.dot_general(a, b, (((0,), (0,)), ((), ())), preferred_element_type=jn...  9.08 us
    pallas_call x2, Pallas kernels, numerators(): pl.pallas_call(kernel, out_shape=jax.ShapeDtypeStruct((NY, count, share,...  9.03 us
    all_to_all x2, starting transfers between devices, exchanged(): return lax.all_to_all(parts, 'y', 0, 0, tiled=True)  8.58 us
    all_to_all x1, starting transfers between devices, to_all(): lax.all_to_all(jnp.broadcast_to(parts, (NY, *parts.shape)), 'y', 0, 0, ti...  4.24 us
    unnamed x14, local copies, waits for them, and re-layouts  3.99 us
  transfers between devices with their start and end apart: 24, of which 14 were waited for; matrix products, arithmetic and copies ran while one was open for 10% of the time, Pallas kernels for 5%

profile of v16, /device:TPU:1, one launch (start us, length us, event | category | flops | bytes accessed | tf_op | source)
XLA Modules:
  0.0 165.1 jit_solution(1454220334544889082)
XLA Ops:
  0.0 3.6 %collective-permute-start.1 = (bf16[448,384]{1,0:T(8,128)(2,1)}, bf16[448,384]{1,0:T(8,128)(2,1)S(1)}, u32[]{:S(2)}, u32[]{:S(2)}) collective-permute-start(bf16[448,384]{1,0:T(8,128)(2,1)} %bitcast.91), channel_id=1, source_target_pairs={{0,8},{1,9},{2,10},{3,11},{4,12},{5,13},{6,14},{7,15},{8,0},{9,1},... | collective-permute-start | bytes 1032200 | tf_op jit(solution)/shard_map/ppermute | solution.py:26
  3.6 1.0 collective-permute-start
  7.6 1.4 select_convert_fusion
  8.9 1.7 %collective-permute-done.1 = bf16[448,384]{1,0:T(8,128)(2,1)S(1)} collective-permute-done((bf16[448,384]{1,0:T(8,128)(2,1)}, bf16[448,384]{1,0:T(8,128)(2,1)S(1)}, u32[]{:S(2)}, u32[]{:S(2)}) %collective-permute-start.1) | collective-permute-done | bytes 344096 | tf_op jit(solution)/shard_map/ppermute | solution.py:26
  10.6 2.2 %collective-permute-start.2 = (bf16[448,384]{1,0:T(8,128)(2,1)S(1)}, bf16[448,384]{1,0:T(8,128)(2,1)S(1)}, u32[]{:S(2)}, u32[]{:S(2)}) collective-permute-start(bf16[448,384]{1,0:T(8,128)(2,1)S(1)} %collective-permute-done.1), channel_id=1, source_target_pairs={{0,1},{1,0},{2,3},{3,2},{4,5},{5,4},{6,7},{7,6},{8,9},{9,8},{10,11... | collective-permute-start | bytes 1032200 | tf_op jit(solution)/shard_map/ppermute | solution.py:26
  12.8 1.2 maximum_select_fusion.1
  14.1 0.2 maximum_select_fusion.2
  14.2 0.3 maximum_select_fusion
  14.6 0.1 pad_maximum_fusion.4.mine_ref
  14.7 1.9 %collective-permute-start.3 = (bf16[456,1536]{1,0:T(8,128)(2,1)S(1)}, bf16[456,1536]{1,0:T(8,128)(2,1)}, u32[]{:S(2)}, u32[]{:S(2)}) collective-permute-start(bf16[456,1536]{1,0:T(8,128)(2,1)S(1)} %pad_maximum_fusion.4.mine_ref), channel_id=1, source_target_pairs={{0,224},{1,33},{2,226},{3,35},{4,228},{5,37},{6,230},{7,39},{8,248... | collective-permute-start | bytes 4202504 | tf_op jit(solution)/shard_map/ppermute | solution.py:26
  16.6 0.7 collective-permute-start.5
  17.4 19.3 %collective-permute-done.3.one_ref = bf16[456,1536]{1,0:T(8,128)(2,1)} collective-permute-done((bf16[456,1536]{1,0:T(8,128)(2,1)S(1)}, bf16[456,1536]{1,0:T(8,128)(2,1)}, u32[]{:S(2)}, u32[]{:S(2)}) %collective-permute-start.3) | collective-permute-done | bytes 1400864 | tf_op jit(solution)/shard_map/ppermute | solution.py:26
  36.6 0.7 collective-permute-start.4
  37.4 2.9 %collective-permute-done.4.swap_ref.swap_one_ref = bf16[456,1536]{1,0:T(8,128)(2,1)S(1)} collective-permute-done((bf16[456,1536]{1,0:T(8,128)(2,1)}, bf16[456,1536]{1,0:T(8,128)(2,1)S(1)}, u32[]{:S(2)}, u32[]{:S(2)}) %collective-permute-start.4) | collective-permute-done | bytes 1400864 | tf_op jit(solution)/shard_map/ppermute | solution.py:26
  40.3 5.1 %shard_map.37 = f32[4,2,112,448]{3,2,1,0:T(8,128)} custom-call(s32[2]{0:T(128)S(1)} %pad_add_fusion.where_ref, bf16[456,1536]{1,0:T(8,128)(2,1)S(1)} %pad_maximum_fusion.4.mine_ref, bf16[456,1536]{1,0:T(8,128)(2,1)} %collective-permute-done.3.one_ref, bf16[456,1536]{1,0:T(8,128)(2,1)S(1)} %collective-permute-done.4.swap_ref.swap_one_ref, ...), custom_call_target="tpu_custom_call" | custom-call | flops 2466250752 | bytes 7110656 | tf_op jit(solution)/shard_map/pallas_call | solution.py:91
  45.4 5.4 %collective-permute-start.6 = (bf16[456,1536]{1,0:T(8,128)(2,1)S(1)}, bf16[456,1536]{1,0:T(8,128)(2,1)S(1)}, u32[]{:S(2)}, u32[]{:S(2)}) collective-permute-start(bf16[456,1536]{1,0:T(8,128)(2,1)S(1)} %collective-permute-done.4.swap_ref.swap_one_ref), channel_id=1, source_target_pairs={{1,225},{3,227},{5,229},{7,231},{9,233},{11,235},{13,237},{15,239}... | collective-permute-start | bytes 4202504 | tf_op jit(solution)/shard_map/ppermute | solution.py:26
  50.9 4.4 %all-to-all-start = ((f32[4,2,112,448]{3,2,1,0:T(8,128)}), f32[4,2,112,448]{3,2,1,0:T(8,128)}, u32[]{:S(2)}, u32[]{:S(2)}) async-start(f32[4,2,112,448]{3,2,1,0:T(8,128)} %shard_map.37), calls=%async_computation | async-start | bytes 3670016 | tf_op jit(solution)/shard_map/all_to_all | solution.py:136
  55.3 0.7 slice_convert_fusion.2
  56.0 0.7 slice_convert_fusion.3
  56.8 7.1 %collective-permute-start.10 = (bf16[456,1536]{1,0:T(8,128)(2,1)}, bf16[456,1536]{1,0:T(8,128)(2,1)}, u32[]{:S(2)}, u32[]{:S(2)}) collective-permute-start(bf16[456,1536]{1,0:T(8,128)(2,1)} %collective-permute-done.3.one_ref), channel_id=1, source_target_pairs={{1,25},{3,27},{5,29},{7,31},{17,9},{19,11},{21,13},{23,15},{33,57}... | collective-permute-start | bytes 4202504 | tf_op jit(solution)/shard_map/ppermute | solution.py:26
  63.8 2.4 %collective-permute-start.11 = (bf16[456,1536]{1,0:T(8,128)(2,1)}, bf16[456,1536]{1,0:T(8,128)(2,1)}, u32[]{:S(2)}, u32[]{:S(2)}) collective-permute-start(bf16[456,1536]{1,0:T(8,128)(2,1)} %collective-permute-done.7.two_ref), channel_id=1, source_target_pairs={{1,25},{3,27},{5,29},{7,31},{17,9},{19,11},{21,13},{23,15},{33,57}... | collective-permute-start | bytes 4202504 | tf_op jit(solution)/shard_map/ppermute | solution.py:26
  66.2 10.0 %collective-permute-done.6.swap_two_ref = bf16[456,1536]{1,0:T(8,128)(2,1)S(1)} collective-permute-done((bf16[456,1536]{1,0:T(8,128)(2,1)S(1)}, bf16[456,1536]{1,0:T(8,128)(2,1)S(1)}, u32[]{:S(2)}, u32[]{:S(2)}) %collective-permute-start.6) | collective-permute-done | bytes 1400864 | tf_op jit(solution)/shard_map/ppermute | solution.py:26
  76.2 3.9 %shard_map.38 = f32[4,1,112,448]{3,2,1,0:T(8,128)} custom-call(s32[2]{0:T(128)S(1)} %pad_add_fusion.where_ref, bf16[456,1536]{1,0:T(8,128)(2,1)S(1)} %collective-permute-done.4.swap_ref.swap_one_ref, bf16[456,1536]{1,0:T(8,128)(2,1)S(1)} %collective-permute-done.6.swap_two_ref, bf16[456,1536]{1,0:T(8,128)(2,1)} %collective-permute-done.7.two_ref), custom_call_target="tpu_custom_call" | custom-call | flops 1233125376 | bytes 4931584 | tf_op jit(solution)/shard_map/pallas_call | solution.py:91
  80.2 4.2 %all-to-all-start.1 = ((f32[4,1,112,448]{3,2,1,0:T(8,128)}), f32[4,1,112,448]{3,2,1,0:T(8,128)S(1)}, u32[]{:S(2)}, u32[]{:S(2)}) async-start(f32[4,1,112,448]{3,2,1,0:T(8,128)} %shard_map.38), calls=%async_computation.1 | async-start | bytes 1835008 | tf_op jit(solution)/shard_map/all_to_all | solution.py:136
  84.4 1.7 %reduce_sum.22 = f32[2,112,448]{2,1,0:T(8,128)S(1)} reduce(f32[4,2,112,448]{3,2,1,0:T(8,128)} %all-to-all-done, f32[]{:T(128)} %constant.35.clone.1), dimensions={0}, to_apply=%region_1.2 | reduce | flops 301056 | bytes 2007044 | tf_op jit(solution)/shard_map/reduce_sum | solution.py:174
  86.1 0.1 fusion.36
  86.3 1.9 %collective-permute-start.9 = (bf16[112,448]{1,0:T(8,128)(2,1)S(1)}, bf16[112,448]{1,0:T(8,128)(2,1)S(1)}, u32[]{:S(2)}, u32[]{:S(2)}) collective-permute-start(bf16[112,448]{1,0:T(8,128)(2,1)S(1)} %get-tuple-element.189), channel_id=1, source_target_pairs={{1,33},{3,35},{5,37},{7,39},{9,57},{11,59},{13,61},{15,63},{17,49}... | collective-permute-start | bytes 301064 | tf_op jit(solution)/shard_map/ppermute | solution.py:26
  88.2 0.7 slice_convert_fusion
  88.9 5.8 %collective-permute-done.9 = bf16[112,448]{1,0:T(8,128)(2,1)S(1)} collective-permute-done((bf16[112,448]{1,0:T(8,128)(2,1)S(1)}, bf16[112,448]{1,0:T(8,128)(2,1)S(1)}, u32[]{:S(2)}, u32[]{:S(2)}) %collective-permute-start.9) | collective-permute-done | bytes 100384 | tf_op jit(solution)/shard_map/ppermute | solution.py:26
  94.8 0.1 reduce_sum.20
  94.9 0.2 collective-permute-done.8
  95.2 1.0 broadcast_in_dim.27
  96.2 4.2 %all-to-all-start.2 = ((bf16[4,2,112,448]{3,2,1,0:T(8,128)(2,1)}), bf16[4,2,112,448]{3,2,1,0:T(8,128)(2,1)S(1)}, u32[]{:S(2)}, u32[]{:S(2)}) async-start(bf16[4,2,112,448]{3,2,1,0:T(8,128)(2,1)} %broadcast_in_dim.27), calls=%async_computation.2 | async-start | bytes 1835008 | tf_op jit(solution)/shard_map/all_to_all | solution.py:156
  100.4 0.1 fusion.35
  100.6 1.3 collective-permute-start.14
  101.9 2.8 %collective-permute-start.13 = (bf16[112,448]{1,0:T(8,128)(2,1)S(1)}, bf16[112,448]{1,0:T(8,128)(2,1)S(1)}, u32[]{:S(2)}, u32[]{:S(2)}) collective-permute-start(bf16[112,448]{1,0:T(8,128)(2,1)S(1)} %fusion.35), channel_id=1, source_target_pairs={{0,224},{1,193},{2,226},{3,195},{4,228},{5,197},{6,230},{7,199},{8... | collective-permute-start | bytes 301064 | tf_op jit(solution)/shard_map/ppermute | solution.py:26
  104.6 5.4 %collective-permute-done.14 = bf16[112,448]{1,0:T(8,128)(2,1)S(1)} collective-permute-done((bf16[112,448]{1,0:T(8,128)(2,1)S(1)}, bf16[112,448]{1,0:T(8,128)(2,1)S(1)}, u32[]{:S(2)}, u32[]{:S(2)}) %collective-permute-start.14) | collective-permute-done | bytes 100384 | tf_op jit(solution)/shard_map/ppermute | solution.py:26
  110.0 1.7 %all-to-all-done.2 = bf16[4,2,112,448]{3,2,1,0:T(8,128)(2,1)S(1)} async-done(((bf16[4,2,112,448]{3,2,1,0:T(8,128)(2,1)}), bf16[4,2,112,448]{3,2,1,0:T(8,128)(2,1)S(1)}, u32[]{:S(2)}, u32[]{:S(2)}) %all-to-all-start.2) | async-done | bytes 802848 | tf_op jit(solution)/shard_map/all_to_all | solution.py:156
  111.8 0.7 pad_maximum_fusion.6
  112.5 1.0 collective-permute-start.15
  113.5 1.9 %collective-permute-start.18 = (bf16[456,1536]{1,0:T(8,128)(2,1)}, bf16[456,1536]{1,0:T(8,128)(2,1)}, u32[]{:S(2)}, u32[]{:S(2)}) collective-permute-start(bf16[456,1536]{1,0:T(8,128)(2,1)} %collective-permute-done.12), channel_id=1, source_target_pairs={{1,33},{3,35},{5,37},{7,39},{9,41},{11,43},{13,45},{15,47},{17,49}... | collective-permute-start | bytes 4202504 | tf_op jit(solution)/shard_map/ppermute | solution.py:26
  115.4 1.1 collective-permute-start.16
  116.6 0.1 collective-permute-start.17
  116.7 4.5 %conditional.2 = (f32[448,1536]{1,0:T(8,128)S(1)}) conditional(s32[]{:T(128)} %clamp.4, (bf16[456,1536]{1,0:T(8,128)(2,1)}, bf16[448,448]{1,0:T(8,128)(2,1)S(1)}, bf16[456,1536]{1,0:T(8,128)(2,1)}, bf16[448,448]{1,0:T(8,128)(2,1)S(1)}) %tuple.85, (bf16[456,1536]{1,0:T(8,128)(2,1)}, bf16[448,448]{1,0:T(8,128)(2,1)S(1)}, ...), branch_computations={%region_2.3_spmd, %region_3.4_spmd, %region_4.5_spmd, %region_5.6_... | conditional | flops 1233813504 | bytes 11812872 | solution.py:210
  116.7 2.2 %fusion.4 = f32[448,1536]{1,0:T(8,128)S(1)} fusion(bf16[448,448]{1,0:T(8,128)(2,1)S(1)} %get-tuple-element.86, bf16[456,1536]{1,0:T(8,128)(2,1)} %get-tuple-element.87), kind=kOutput, calls=%fused_computation.6 | convolution fusion | flops 616562688 | bytes 4530176 | tf_op jit(solution)/shard_map/cond/branch_1_fun/dot_general | solution.py:50
  118.9 2.3 %convolution_add_fusion.1 = f32[448,1536]{1,0:T(8,128)S(1)} fusion(f32[448,1536]{1,0:T(8,128)S(1)} %fusion.4, bf16[448,448]{1,0:T(8,128)(2,1)S(1)} %get-tuple-element.88, bf16[456,1536]{1,0:T(8,128)(2,1)} %get-tuple-element.89), kind=kOutput, calls=%fused_computation.4 | convolution fusion | flops 617250816 | bytes 7282688 | tf_op jit(solution)/shard_map/cond/branch_1_fun/dot_general | solution.py:50
  121.2 2.5 %collective-permute-done.15 = bf16[2,112,448]{2,1,0:T(8,128)(2,1)} collective-permute-done((bf16[2,112,448]{2,1,0:T(8,128)(2,1)}, bf16[2,112,448]{2,1,0:T(8,128)(2,1)}, u32[]{:S(2)}, u32[]{:S(2)}) %collective-permute-start.15) | collective-permute-done | bytes 200736 | tf_op jit(solution)/shard_map/ppermute | solution.py:26
  123.7 1.0 bitcast_dynamic-update-slice_fusion.3
  124.7 1.0 bitcast_dynamic-update-slice_fusion.1
  125.7 4.2 %collective-permute-done.17 = bf16[2,112,448]{2,1,0:T(8,128)(2,1)} collective-permute-done((bf16[2,112,448]{2,1,0:T(8,128)(2,1)}, bf16[2,112,448]{2,1,0:T(8,128)(2,1)}, u32[]{:S(2)}, u32[]{:S(2)}) %collective-permute-start.17) | collective-permute-done | bytes 200736 | tf_op jit(solution)/shard_map/ppermute | solution.py:26
  129.9 1.0 bitcast_dynamic-update-slice_fusion
  130.9 1.1 bitcast_dynamic-update-slice_fusion.4
  132.0 1.0 bitcast_dynamic-update-slice_fusion.2
  133.0 1.9 %collective-permute-done.18 = bf16[456,1536]{1,0:T(8,128)(2,1)} collective-permute-done((bf16[456,1536]{1,0:T(8,128)(2,1)}, bf16[456,1536]{1,0:T(8,128)(2,1)}, u32[]{:S(2)}, u32[]{:S(2)}) %collective-permute-start.18) | collective-permute-done | bytes 1400864 | tf_op jit(solution)/shard_map/ppermute | solution.py:26
  134.9 5.1 %conditional.3 = (f32[448,768]{1,0:T(8,128)S(1)}, f32[448,384]{1,0:T(8,128)S(1)}, f32[448,384]{1,0:T(8,128)S(1)}) conditional(s32[]{:T(128)} %clamp.4, (bf16[456,1536]{1,0:T(8,128)(2,1)}, bf16[448,448]{1,0:T(8,128)(2,1)S(1)}, bf16[448,448]{1,0:T(8,128)(2,1)S(1)}, bf16[448,1536]{1,0:T(8,128)(2,1)S(1)}, ...), branch_computations={%region_6.7_spmd, %region_7.8_spmd, %region_8.9_spmd, %region_9.10... | conditional | flops 1234845696 | bytes 22880280 | solution.py:230
  134.9 2.2 %fusion.17 = f32[448,1536]{1,0:T(8,128)S(1)} fusion(bf16[448,448]{1,0:T(8,128)(2,1)S(1)} %get-tuple-element.104, bf16[456,1536]{1,0:T(8,128)(2,1)} %get-tuple-element.105), kind=kOutput, calls=%fused_computation.25 | convolution fusion | flops 616562688 | bytes 4530176 | tf_op jit(solution)/shard_map/cond/branch_1_fun/dot_general | solution.py:50
  137.2 2.3 %fusion.15 = f32[448,1536]{1,0:T(8,128)S(1)} fusion(f32[448,1536]{1,0:T(8,128)S(1)} %get-tuple-element.103, f32[448,1536]{1,0:T(8,128)S(1)} %fusion.17, bf16[448,448]{1,0:T(8,128)(2,1)S(1)} %get-tuple-element.106, bf16[456,1536]{1,0:T(8,128)(2,1)} %get-tuple-element.107), kind=kOutput, calls=%fused_computation.22 | convolution fusion | flops 617938944 | bytes 10035200 | tf_op jit(solution)/shard_map/cond/branch_1_fun/dot_general | solution.py:50
  139.5 0.2 fusion.39
  139.7 0.1 pad_maximum_fusion.1
  140.0 0.1 collective-permute-start.19
  140.1 3.1 %collective-permute-done.19 = f32[448,768]{1,0:T(8,128)S(1)} collective-permute-done((f32[448,768]{1,0:T(8,128)S(1)}, f32[448,768]{1,0:T(8,128)S(1)}, u32[]{:S(2)}, u32[]{:S(2)}) %collective-permute-start.19) | collective-permute-done | bytes 1376288 | tf_op jit(solution)/shard_map/ppermute | solution.py:26
  143.3 5.1 %collective-permute-start.20 = (f32[448,384]{1,0:T(8,128)S(1)}, f32[448,384]{1,0:T(8,128)S(1)}, u32[]{:S(2)}, u32[]{:S(2)}) collective-permute-start(f32[448,384]{1,0:T(8,128)S(1)} %slice_add_fusion), channel_id=1, source_target_pairs={{0,8},{1,9},{2,10},{3,11},{4,12},{5,13},{6,14},{7,15},{8,0},{9,1},... | collective-permute-start | bytes 2064392 | tf_op jit(solution)/shard_map/ppermute | solution.py:26
  148.5 15.7 %collective-permute-done.20 = f32[448,384]{1,0:T(8,128)S(1)} collective-permute-done((f32[448,384]{1,0:T(8,128)S(1)}, f32[448,384]{1,0:T(8,128)S(1)}, u32[]{:S(2)}, u32[]{:S(2)}) %collective-permute-start.20) | collective-permute-done | bytes 688160 | tf_op jit(solution)/shard_map/ppermute | solution.py:26
  164.1 0.9 fusion.28
  (44 shorter events, 0.7 us)
Async XLA Ops:
  0.0 10.6 %collective-permute-start.1 = (bf16[448,384]{1,0:T(8,128)(2,1)}, bf16[448,384]{1,0:T(8,128)(2,1)S(1)}, u32[]{:S(2)}, u32[]{:S(2)}) collective-permute-start(bf16[448,384]{1,0:T(8,128)(2,1)} %bitcast.91), channel_id=1, source_target_pairs={{0,8},{1,9},{2,10},{3,11},{4,12},{5,13},{6,14},{7,15},{8,0},{9,1},... | collective-permute-start | bytes 1032200 | tf_op jit(solution)/shard_map/ppermute | solution.py:26
  3.6 9.2 %collective-permute-start = (bf16[448,384]{1,0:T(8,128)(2,1)}, bf16[448,384]{1,0:T(8,128)(2,1)S(1)}, u32[]{:S(2)}, u32[]{:S(2)}) collective-permute-start(bf16[448,384]{1,0:T(8,128)(2,1)} %bitcast.92), channel_id=1, source_target_pairs={{0,1},{1,0},{2,3},{3,2},{4,5},{5,4},{6,7},{7,6},{8,9},{9,8},{10,11... | collective-permute-start | bytes 1032200 | tf_op jit(solution)/shard_map/ppermute | solution.py:26
  10.6 3.5 %collective-permute-start.2 = (bf16[448,384]{1,0:T(8,128)(2,1)S(1)}, bf16[448,384]{1,0:T(8,128)(2,1)S(1)}, u32[]{:S(2)}, u32[]{:S(2)}) collective-permute-start(bf16[448,384]{1,0:T(8,128)(2,1)S(1)} %collective-permute-done.1), channel_id=1, source_target_pairs={{0,1},{1,0},{2,3},{3,2},{4,5},{5,4},{6,7},{7,6},{8,9},{9,8},{10,11... | collective-permute-start | bytes 1032200 | tf_op jit(solution)/shard_map/ppermute | solution.py:26
  14.6 22.7 %copy-start = (bf16[448,1536]{1,0:T(8,128)(2,1)}, bf16[448,1536]{1,0:T(8,128)(2,1)S(1)}, u32[]{:S(2)}) copy-start(bf16[448,1536]{1,0:T(8,128)(2,1)S(1)} %maximum_select_fusion) | copy-start | bytes 4128772
  14.7 21.9 %collective-permute-start.3 = (bf16[456,1536]{1,0:T(8,128)(2,1)S(1)}, bf16[456,1536]{1,0:T(8,128)(2,1)}, u32[]{:S(2)}, u32[]{:S(2)}) collective-permute-start(bf16[456,1536]{1,0:T(8,128)(2,1)S(1)} %pad_maximum_fusion.4.mine_ref), channel_id=1, source_target_pairs={{0,224},{1,33},{2,226},{3,35},{4,228},{5,37},{6,230},{7,39},{8,248... | collective-permute-start | bytes 4202504 | tf_op jit(solution)/shard_map/ppermute | solution.py:26
  16.6 20.8 %collective-permute-start.5 = (bf16[456,1536]{1,0:T(8,128)(2,1)S(1)}, bf16[456,1536]{1,0:T(8,128)(2,1)S(1)}, u32[]{:S(2)}, u32[]{:S(2)}) collective-permute-start(bf16[456,1536]{1,0:T(8,128)(2,1)S(1)} %pad_maximum_fusion.4.mine_ref), channel_id=1, source_target_pairs={{0,24},{2,26},{4,28},{6,30},{16,8},{18,10},{20,12},{22,14},{32,56}... | collective-permute-start | bytes 4202504 | tf_op jit(solution)/shard_map/ppermute | solution.py:26
  36.6 3.7 %collective-permute-start.4 = (bf16[456,1536]{1,0:T(8,128)(2,1)}, bf16[456,1536]{1,0:T(8,128)(2,1)S(1)}, u32[]{:S(2)}, u32[]{:S(2)}) collective-permute-start(bf16[456,1536]{1,0:T(8,128)(2,1)} %collective-permute-done.3.one_ref), channel_id=1, source_target_pairs={{0,1},{1,0},{2,3},{3,2},{4,5},{5,4},{6,7},{7,6},{8,9},{9,8},{10,11... | collective-permute-start | bytes 4202504 | tf_op jit(solution)/shard_map/ppermute | solution.py:26
  37.4 13.5 %copy-start.4 = (f32[448]{0:T(512)S(1)}, f32[448]{0:T(512)}, u32[]{:S(2)}) copy-start(f32[448]{0:T(512)} %param.13) | copy-start | bytes 5380
  37.4 26.5 %collective-permute-start.7 = (bf16[456,1536]{1,0:T(8,128)(2,1)}, bf16[456,1536]{1,0:T(8,128)(2,1)}, u32[]{:S(2)}, u32[]{:S(2)}) collective-permute-start(bf16[456,1536]{1,0:T(8,128)(2,1)} %collective-permute-done.3.one_ref), channel_id=1, source_target_pairs={{0,224},{1,33},{2,226},{3,35},{4,228},{5,37},{6,230},{7,39},{8,232... | collective-permute-start | bytes 4202504 | tf_op jit(solution)/shard_map/ppermute | solution.py:26
  37.4 8.0 %copy-start.2 = (bf16[456,1536]{1,0:T(8,128)(2,1)}, bf16[456,1536]{1,0:T(8,128)(2,1)S(1)}, u32[]{:S(2)}) copy-start(bf16[456,1536]{1,0:T(8,128)(2,1)S(1)} %collective-permute-done.5.beyond_ref) | copy-start | bytes 4202500
  45.4 30.8 %collective-permute-start.6 = (bf16[456,1536]{1,0:T(8,128)(2,1)S(1)}, bf16[456,1536]{1,0:T(8,128)(2,1)S(1)}, u32[]{:S(2)}, u32[]{:S(2)}) collective-permute-start(bf16[456,1536]{1,0:T(8,128)(2,1)S(1)} %collective-permute-done.4.swap_ref.swap_one_ref), channel_id=1, source_target_pairs={{1,225},{3,227},{5,229},{7,231},{9,233},{11,235},{13,237},{15,239}... | collective-permute-start | bytes 4202504 | tf_op jit(solution)/shard_map/ppermute | solution.py:26
  50.9 29.2 %all-to-all-start = ((f32[4,2,112,448]{3,2,1,0:T(8,128)}), f32[4,2,112,448]{3,2,1,0:T(8,128)}, u32[]{:S(2)}, u32[]{:S(2)}) async-start(f32[4,2,112,448]{3,2,1,0:T(8,128)} %shard_map.37), calls=%async_computation | async-start | bytes 3670016 | tf_op jit(solution)/shard_map/all_to_all | solution.py:136
  56.8 38.1 %collective-permute-start.10 = (bf16[456,1536]{1,0:T(8,128)(2,1)}, bf16[456,1536]{1,0:T(8,128)(2,1)}, u32[]{:S(2)}, u32[]{:S(2)}) collective-permute-start(bf16[456,1536]{1,0:T(8,128)(2,1)} %collective-permute-done.3.one_ref), channel_id=1, source_target_pairs={{1,25},{3,27},{5,29},{7,31},{17,9},{19,11},{21,13},{23,15},{33,57}... | collective-permute-start | bytes 4202504 | tf_op jit(solution)/shard_map/ppermute | solution.py:26
  63.8 31.0 %collective-permute-start.12 = (bf16[456,1536]{1,0:T(8,128)(2,1)}, bf16[456,1536]{1,0:T(8,128)(2,1)}, u32[]{:S(2)}, u32[]{:S(2)}) collective-permute-start(bf16[456,1536]{1,0:T(8,128)(2,1)} %collective-permute-done.7.two_ref), channel_id=1, source_target_pairs={{0,224},{1,33},{2,226},{3,35},{4,228},{5,37},{6,230},{7,39},{8,232... | collective-permute-start | bytes 4202504 | tf_op jit(solution)/shard_map/ppermute | solution.py:26
  63.8 31.0 %collective-permute-start.11 = (bf16[456,1536]{1,0:T(8,128)(2,1)}, bf16[456,1536]{1,0:T(8,128)(2,1)}, u32[]{:S(2)}, u32[]{:S(2)}) collective-permute-start(bf16[456,1536]{1,0:T(8,128)(2,1)} %collective-permute-done.7.two_ref), channel_id=1, source_target_pairs={{1,25},{3,27},{5,29},{7,31},{17,9},{19,11},{21,13},{23,15},{33,57}... | collective-permute-start | bytes 4202504 | tf_op jit(solution)/shard_map/ppermute | solution.py:26
  80.2 14.6 %all-to-all-start.1 = ((f32[4,1,112,448]{3,2,1,0:T(8,128)}), f32[4,1,112,448]{3,2,1,0:T(8,128)S(1)}, u32[]{:S(2)}, u32[]{:S(2)}) async-start(f32[4,1,112,448]{3,2,1,0:T(8,128)} %shard_map.38), calls=%async_computation.1 | async-start | bytes 1835008 | tf_op jit(solution)/shard_map/all_to_all | solution.py:136
  86.3 8.4 %collective-permute-start.9 = (bf16[112,448]{1,0:T(8,128)(2,1)S(1)}, bf16[112,448]{1,0:T(8,128)(2,1)S(1)}, u32[]{:S(2)}, u32[]{:S(2)}) collective-permute-start(bf16[112,448]{1,0:T(8,128)(2,1)S(1)} %get-tuple-element.189), channel_id=1, source_target_pairs={{1,33},{3,35},{5,37},{7,39},{9,57},{11,59},{13,61},{15,63},{17,49}... | collective-permute-start | bytes 301064 | tf_op jit(solution)/shard_map/ppermute | solution.py:26
  88.9 6.2 %collective-permute-start.8 = (bf16[112,448]{1,0:T(8,128)(2,1)S(1)}, bf16[112,448]{1,0:T(8,128)(2,1)S(1)}, u32[]{:S(2)}, u32[]{:S(2)}) collective-permute-start(bf16[112,448]{1,0:T(8,128)(2,1)S(1)} %get-tuple-element.189), channel_id=1, source_target_pairs={{0,33},{1,224},{2,35},{3,226},{4,37},{5,228},{6,39},{7,230},{8,57}... | collective-permute-start | bytes 301064 | tf_op jit(solution)/shard_map/ppermute | solution.py:26
  96.2 15.5 %all-to-all-start.2 = ((bf16[4,2,112,448]{3,2,1,0:T(8,128)(2,1)}), bf16[4,2,112,448]{3,2,1,0:T(8,128)(2,1)S(1)}, u32[]{:S(2)}, u32[]{:S(2)}) async-start(bf16[4,2,112,448]{3,2,1,0:T(8,128)(2,1)} %broadcast_in_dim.27), calls=%async_computation.2 | async-start | bytes 1835008 | tf_op jit(solution)/shard_map/all_to_all | solution.py:156
  100.6 9.4 %collective-permute-start.14 = (bf16[112,448]{1,0:T(8,128)(2,1)S(1)}, bf16[112,448]{1,0:T(8,128)(2,1)S(1)}, u32[]{:S(2)}, u32[]{:S(2)}) collective-permute-start(bf16[112,448]{1,0:T(8,128)(2,1)S(1)} %fusion.35), channel_id=1, source_target_pairs={{0,65},{2,67},{4,69},{6,71},{8,89},{10,91},{12,93},{14,95},{16,81}... | collective-permute-start | bytes 301064 | tf_op jit(solution)/shard_map/ppermute | solution.py:26
  101.9 9.9 %collective-permute-start.13 = (bf16[112,448]{1,0:T(8,128)(2,1)S(1)}, bf16[112,448]{1,0:T(8,128)(2,1)S(1)}, u32[]{:S(2)}, u32[]{:S(2)}) collective-permute-start(bf16[112,448]{1,0:T(8,128)(2,1)S(1)} %fusion.35), channel_id=1, source_target_pairs={{0,224},{1,193},{2,226},{3,195},{4,228},{5,197},{6,230},{7,199},{8... | collective-permute-start | bytes 301064 | tf_op jit(solution)/shard_map/ppermute | solution.py:26
  112.5 11.2 %collective-permute-start.15 = (bf16[2,112,448]{2,1,0:T(8,128)(2,1)}, bf16[2,112,448]{2,1,0:T(8,128)(2,1)}, u32[]{:S(2)}, u32[]{:S(2)}) collective-permute-start(bf16[2,112,448]{2,1,0:T(8,128)(2,1)} %pad_maximum_fusion.6), channel_id=1, source_target_pairs={{0,6},{1,7},{2,0},{3,1},{4,2},{5,3},{6,4},{7,5},{8,14},{9,15},{10,... | collective-permute-start | bytes 602120 | tf_op jit(solution)/shard_map/ppermute | solution.py:26
  113.5 21.4 %collective-permute-start.18 = (bf16[456,1536]{1,0:T(8,128)(2,1)}, bf16[456,1536]{1,0:T(8,128)(2,1)}, u32[]{:S(2)}, u32[]{:S(2)}) collective-permute-start(bf16[456,1536]{1,0:T(8,128)(2,1)} %collective-permute-done.12), channel_id=1, source_target_pairs={{1,33},{3,35},{5,37},{7,39},{9,41},{11,43},{13,45},{15,47},{17,49}... | collective-permute-start | bytes 4202504 | tf_op jit(solution)/shard_map/ppermute | solution.py:26
  115.4 9.3 %collective-permute-start.16 = (bf16[2,112,448]{2,1,0:T(8,128)(2,1)}, bf16[2,112,448]{2,1,0:T(8,128)(2,1)}, u32[]{:S(2)}, u32[]{:S(2)}) collective-permute-start(bf16[2,112,448]{2,1,0:T(8,128)(2,1)} %pad_maximum_fusion.6), channel_id=1, source_target_pairs={{0,4},{1,5},{2,6},{3,7},{4,0},{5,1},{6,2},{7,3},{8,12},{9,13},{10,... | collective-permute-start | bytes 602120 | tf_op jit(solution)/shard_map/ppermute | solution.py:26
  116.6 13.3 %collective-permute-start.17 = (bf16[2,112,448]{2,1,0:T(8,128)(2,1)}, bf16[2,112,448]{2,1,0:T(8,128)(2,1)}, u32[]{:S(2)}, u32[]{:S(2)}) collective-permute-start(bf16[2,112,448]{2,1,0:T(8,128)(2,1)} %pad_maximum_fusion.6), channel_id=1, source_target_pairs={{0,2},{1,3},{2,4},{3,5},{4,6},{5,7},{6,0},{7,1},{8,10},{9,11},{10,... | collective-permute-start | bytes 602120 | tf_op jit(solution)/shard_map/ppermute | solution.py:26
  130.8 4.1 %copy-start.3 = (bf16[456,1536]{1,0:T(8,128)(2,1)S(1)}, bf16[456,1536]{1,0:T(8,128)(2,1)}, u32[]{:S(2)}) copy-start(bf16[456,1536]{1,0:T(8,128)(2,1)} %copy-done.2) | copy-start | bytes 4202500
  130.9 4.1 %copy-start.1 = (bf16[448,1536]{1,0:T(8,128)(2,1)S(1)}, bf16[448,1536]{1,0:T(8,128)(2,1)}, u32[]{:S(2)}) copy-start(bf16[448,1536]{1,0:T(8,128)(2,1)} %copy-done) | copy-start | bytes 4128772
  140.0 3.2 %collective-permute-start.19 = (f32[448,768]{1,0:T(8,128)S(1)}, f32[448,768]{1,0:T(8,128)S(1)}, u32[]{:S(2)}, u32[]{:S(2)}) collective-permute-start(f32[448,768]{1,0:T(8,128)S(1)} %get-tuple-element.160), channel_id=1, source_target_pairs={{0,1},{1,0},{2,3},{3,2},{4,5},{5,4},{6,7},{7,6},{8,9},{9,8},{10,11... | collective-permute-start | bytes 4128776 | tf_op jit(solution)/shard_map/ppermute | solution.py:26
  143.3 20.8 %collective-permute-start.20 = (f32[448,384]{1,0:T(8,128)S(1)}, f32[448,384]{1,0:T(8,128)S(1)}, u32[]{:S(2)}, u32[]{:S(2)}) collective-permute-start(f32[448,384]{1,0:T(8,128)S(1)} %slice_add_fusion), channel_id=1, source_target_pairs={{0,8},{1,9},{2,10},{3,11},{4,12},{5,13},{6,14},{7,15},{8,0},{9,1},... | collective-permute-start | bytes 2064392 | tf_op jit(solution)/shard_map/ppermute | solution.py:26

commit v17 on v16

--- a/solution.py
+++ b/solution.py
@@ -148,8 +148,10 @@
     def by_hops(*parts):
         parts = jnp.stack(parts)
         hops = [parts] + [moved(parts, lambda z, xl, xh, y, c, n=n: (z, xl, xh, y - n, c)) for n in range(1, NY)]
-        whole = lax.dynamic_slice_in_dim(jnp.stack(hops + hops[:-1]), (NY - y) % NY, NY, axis=0)
-        return [whole[:, n].reshape(nvir, nvir) for n in range(parts.shape[0])]
+        return [
+            jnp.concatenate([lax.select_n(y, *(hops[(k - n) % NY][m] for n in range(NY))) for k in range(NY)], axis=0)
+            for m in range(parts.shape[0])
+        ]
 
     def to_all(*parts):
         parts = jnp.stack(parts)

time: 166 us -> 162 us (0.976)
  waiting for transfers between devices: 74.4 us -> 69.1 us
  local copies, waits for them, and re-layouts: 6.36 us -> 2.65 us
  other arithmetic: 9.44 us -> 11.8 us
  starting transfers between devices: 53.2 us -> 55.3 us
    ppermute x21, waiting for transfers between devices: 72.7 us -> 68.5 us  [moved(): return lax.ppermute(array, ALL, pairs)]
    unnamed x14 -> x10, local copies, waits for them, and re-layouts: 3.99 us -> 1.3 us
    select_n x0 -> x2, other arithmetic: none -> 2.33 us  [by_hops(): lax.select_n(y, *(hops[(k - n) % NY][m] for n in range(NY)))]
    ppermute x21, starting transfers between devices: 40.4 us -> 42.5 us  [moved(): return lax.ppermute(array, ALL, pairs)]
  transfers between devices with their start and end apart: 24 -> 24, of which waited for: 14 -> 13; matrix products, arithmetic and copies ran while one was open for 10% -> 9% of each run, Pallas kernels for 5% -> 6%
where the time goes in v17:
time: 162 us; the launch traced here: 161 us
  waiting for transfers between devices  69.1 us (43%)
  starting transfers between devices  55.3 us (34%)
  other arithmetic  11.8 us (7%)
  matrix products  9.08 us (6%)
  Pallas kernels  9.02 us (6%)
  between operations  3.36 us (2%)
  local copies, waits for them, and re-layouts  2.65 us (2%)
    ppermute x21, waiting for transfers between devices, moved(): return lax.ppermute(array, ALL, pairs)  68.5 us
    ppermute x21, starting transfers between devices, moved(): return lax.ppermute(array, ALL, pairs)  42.5 us
    dot_general x4, matrix products, dot_tn(): lax.dot_general(a, b, (((0,), (0,)), ((), ())), preferred_element_type=jn...  9.08 us
    pallas_call x2, Pallas kernels, numerators(): pl.pallas_call(kernel, out_shape=jax.ShapeDtypeStruct((NY, count, share,...  9.02 us
    all_to_all x2, starting transfers between devices, exchanged(): return lax.all_to_all(parts, 'y', 0, 0, tiled=True)  8.58 us
    all_to_all x1, starting transfers between devices, to_all(): lax.all_to_all(jnp.broadcast_to(parts, (NY, *parts.shape)), 'y', 0, 0, ti...  4.24 us
  transfers between devices with their start and end apart: 24, of which 13 were waited for; matrix products, arithmetic and copies ran while one was open for 9% of the time, Pallas kernels for 6%

profile of v17, /device:TPU:1, one launch (start us, length us, event | category | flops | bytes accessed | tf_op | source)
XLA Modules:
  0.0 160.6 jit_solution(9691951109061179772)
XLA Ops:
  0.0 3.6 %collective-permute-start.1 = (bf16[448,384]{1,0:T(8,128)(2,1)}, bf16[448,384]{1,0:T(8,128)(2,1)S(1)}, u32[]{:S(2)}, u32[]{:S(2)}) collective-permute-start(bf16[448,384]{1,0:T(8,128)(2,1)} %bitcast.126), channel_id=1, source_target_pairs={{0,8},{1,9},{2,10},{3,11},{4,12},{5,13},{6,14},{7,15},{8,0},{9,1},... | collective-permute-start | bytes 1032200 | tf_op jit(solution)/shard_map/ppermute | solution.py:26
  3.6 1.0 collective-permute-start
  7.6 1.4 select_convert_fusion
  8.9 1.7 %collective-permute-done.1 = bf16[448,384]{1,0:T(8,128)(2,1)S(1)} collective-permute-done((bf16[448,384]{1,0:T(8,128)(2,1)}, bf16[448,384]{1,0:T(8,128)(2,1)S(1)}, u32[]{:S(2)}, u32[]{:S(2)}) %collective-permute-start.1) | collective-permute-done | bytes 344096 | tf_op jit(solution)/shard_map/ppermute | solution.py:26
  10.6 2.2 %collective-permute-start.2 = (bf16[448,384]{1,0:T(8,128)(2,1)S(1)}, bf16[448,384]{1,0:T(8,128)(2,1)S(1)}, u32[]{:S(2)}, u32[]{:S(2)}) collective-permute-start(bf16[448,384]{1,0:T(8,128)(2,1)S(1)} %collective-permute-done.1), channel_id=1, source_target_pairs={{0,1},{1,0},{2,3},{3,2},{4,5},{5,4},{6,7},{7,6},{8,9},{9,8},{10,11... | collective-permute-start | bytes 1032200 | tf_op jit(solution)/shard_map/ppermute | solution.py:26
  12.8 1.2 maximum_select_fusion.1
  14.1 0.2 maximum_select_fusion.2
  14.2 0.3 maximum_select_fusion
  14.6 0.1 pad_maximum_fusion.4.mine_ref
  14.7 1.0 copy-done
  15.7 1.9 %collective-permute-start.3 = (bf16[456,1536]{1,0:T(8,128)(2,1)S(1)}, bf16[456,1536]{1,0:T(8,128)(2,1)}, u32[]{:S(2)}, u32[]{:S(2)}) collective-permute-start(bf16[456,1536]{1,0:T(8,128)(2,1)S(1)} %pad_maximum_fusion.4.mine_ref), channel_id=1, source_target_pairs={{0,224},{1,33},{2,226},{3,35},{4,228},{5,37},{6,230},{7,39},{8,248... | collective-permute-start | bytes 4202504 | tf_op jit(solution)/shard_map/ppermute | solution.py:26
  17.5 0.7 collective-permute-start.5
  18.3 19.3 %collective-permute-done.3.one_ref = bf16[456,1536]{1,0:T(8,128)(2,1)} collective-permute-done((bf16[456,1536]{1,0:T(8,128)(2,1)S(1)}, bf16[456,1536]{1,0:T(8,128)(2,1)}, u32[]{:S(2)}, u32[]{:S(2)}) %collective-permute-start.3) | collective-permute-done | bytes 1400864 | tf_op jit(solution)/shard_map/ppermute | solution.py:26
  37.5 0.7 collective-permute-start.4
  38.4 2.9 %collective-permute-done.4.swap_ref.swap_one_ref = bf16[456,1536]{1,0:T(8,128)(2,1)S(1)} collective-permute-done((bf16[456,1536]{1,0:T(8,128)(2,1)}, bf16[456,1536]{1,0:T(8,128)(2,1)S(1)}, u32[]{:S(2)}, u32[]{:S(2)}) %collective-permute-start.4) | collective-permute-done | bytes 1400864 | tf_op jit(solution)/shard_map/ppermute | solution.py:26
  41.2 5.1 %shard_map.37 = f32[4,2,112,448]{3,2,1,0:T(8,128)} custom-call(s32[2]{0:T(128)S(1)} %pad_add_fusion.where_ref, bf16[456,1536]{1,0:T(8,128)(2,1)S(1)} %pad_maximum_fusion.4.mine_ref, bf16[456,1536]{1,0:T(8,128)(2,1)} %collective-permute-done.3.one_ref, bf16[456,1536]{1,0:T(8,128)(2,1)S(1)} %collective-permute-done.4.swap_ref.swap_one_ref, ...), custom_call_target="tpu_custom_call" | custom-call | flops 2466250752 | bytes 7110656 | tf_op jit(solution)/shard_map/pallas_call | solution.py:91
  46.3 5.4 %collective-permute-start.6 = (bf16[456,1536]{1,0:T(8,128)(2,1)S(1)}, bf16[456,1536]{1,0:T(8,128)(2,1)S(1)}, u32[]{:S(2)}, u32[]{:S(2)}) collective-permute-start(bf16[456,1536]{1,0:T(8,128)(2,1)S(1)} %collective-permute-done.4.swap_ref.swap_one_ref), channel_id=1, source_target_pairs={{1,225},{3,227},{5,229},{7,231},{9,233},{11,235},{13,237},{15,239}... | collective-permute-start | bytes 4202504 | tf_op jit(solution)/shard_map/ppermute | solution.py:26
  51.8 0.1 dynamic_slice.3
  51.9 4.4 %all-to-all-start = ((f32[4,2,112,448]{3,2,1,0:T(8,128)}), f32[4,2,112,448]{3,2,1,0:T(8,128)}, u32[]{:S(2)}, u32[]{:S(2)}) async-start(f32[4,2,112,448]{3,2,1,0:T(8,128)} %shard_map.37), calls=%async_computation | async-start | bytes 3670016 | tf_op jit(solution)/shard_map/all_to_all | solution.py:136
  56.3 0.7 slice_convert_fusion.2
  57.0 0.7 slice_convert_fusion.3
  57.7 7.1 %collective-permute-start.10 = (bf16[456,1536]{1,0:T(8,128)(2,1)}, bf16[456,1536]{1,0:T(8,128)(2,1)}, u32[]{:S(2)}, u32[]{:S(2)}) collective-permute-start(bf16[456,1536]{1,0:T(8,128)(2,1)} %collective-permute-done.3.one_ref), channel_id=1, source_target_pairs={{1,25},{3,27},{5,29},{7,31},{17,9},{19,11},{21,13},{23,15},{33,57}... | collective-permute-start | bytes 4202504 | tf_op jit(solution)/shard_map/ppermute | solution.py:26
  64.8 2.4 %collective-permute-start.11 = (bf16[456,1536]{1,0:T(8,128)(2,1)}, bf16[456,1536]{1,0:T(8,128)(2,1)}, u32[]{:S(2)}, u32[]{:S(2)}) collective-permute-start(bf16[456,1536]{1,0:T(8,128)(2,1)} %collective-permute-done.7.two_ref), channel_id=1, source_target_pairs={{1,25},{3,27},{5,29},{7,31},{17,9},{19,11},{21,13},{23,15},{33,57}... | collective-permute-start | bytes 4202504 | tf_op jit(solution)/shard_map/ppermute | solution.py:26
  67.2 10.0 %collective-permute-done.6.swap_two_ref = bf16[456,1536]{1,0:T(8,128)(2,1)S(1)} collective-permute-done((bf16[456,1536]{1,0:T(8,128)(2,1)S(1)}, bf16[456,1536]{1,0:T(8,128)(2,1)S(1)}, u32[]{:S(2)}, u32[]{:S(2)}) %collective-permute-start.6) | collective-permute-done | bytes 1400864 | tf_op jit(solution)/shard_map/ppermute | solution.py:26
  77.2 3.9 %shard_map.38 = f32[4,1,112,448]{3,2,1,0:T(8,128)} custom-call(s32[2]{0:T(128)S(1)} %pad_add_fusion.where_ref, bf16[456,1536]{1,0:T(8,128)(2,1)S(1)} %collective-permute-done.4.swap_ref.swap_one_ref, bf16[456,1536]{1,0:T(8,128)(2,1)S(1)} %collective-permute-done.6.swap_two_ref, bf16[456,1536]{1,0:T(8,128)(2,1)} %collective-permute-done.7.two_ref), custom_call_target="tpu_custom_call" | custom-call | flops 1233125376 | bytes 4931584 | tf_op jit(solution)/shard_map/pallas_call | solution.py:91
  81.1 4.2 %all-to-all-start.1 = ((f32[4,1,112,448]{3,2,1,0:T(8,128)}), f32[4,1,112,448]{3,2,1,0:T(8,128)S(1)}, u32[]{:S(2)}, u32[]{:S(2)}) async-start(f32[4,1,112,448]{3,2,1,0:T(8,128)} %shard_map.38), calls=%async_computation.1 | async-start | bytes 1835008 | tf_op jit(solution)/shard_map/all_to_all | solution.py:136
  85.3 1.7 %reduce_sum.22 = f32[2,112,448]{2,1,0:T(8,128)S(1)} reduce(f32[4,2,112,448]{3,2,1,0:T(8,128)} %all-to-all-done, f32[]{:T(128)} %constant.6.clone.1), dimensions={0}, to_apply=%region_1.2 | reduce | flops 301056 | bytes 2007044 | tf_op jit(solution)/shard_map/reduce_sum | solution.py:176
  87.1 0.1 fusion.36
  87.2 1.9 %collective-permute-start.9 = (bf16[112,448]{1,0:T(8,128)(2,1)S(1)}, bf16[112,448]{1,0:T(8,128)(2,1)S(1)}, u32[]{:S(2)}, u32[]{:S(2)}) collective-permute-start(bf16[112,448]{1,0:T(8,128)(2,1)S(1)} %get-tuple-element.195), channel_id=1, source_target_pairs={{1,33},{3,35},{5,37},{7,39},{9,57},{11,59},{13,61},{15,63},{17,49}... | collective-permute-start | bytes 301064 | tf_op jit(solution)/shard_map/ppermute | solution.py:26
  89.2 0.7 slice_convert_fusion
  89.9 5.8 %collective-permute-done.9 = bf16[112,448]{1,0:T(8,128)(2,1)S(1)} collective-permute-done((bf16[112,448]{1,0:T(8,128)(2,1)S(1)}, bf16[112,448]{1,0:T(8,128)(2,1)S(1)}, u32[]{:S(2)}, u32[]{:S(2)}) %collective-permute-start.9) | collective-permute-done | bytes 100384 | tf_op jit(solution)/shard_map/ppermute | solution.py:26
  95.7 0.1 reduce_sum.20
  95.8 0.2 collective-permute-done.8
  96.1 1.0 broadcast_in_dim.27
  97.1 4.2 %all-to-all-start.2 = ((bf16[4,2,112,448]{3,2,1,0:T(8,128)(2,1)}), bf16[4,2,112,448]{3,2,1,0:T(8,128)(2,1)S(1)}, u32[]{:S(2)}, u32[]{:S(2)}) async-start(bf16[4,2,112,448]{3,2,1,0:T(8,128)(2,1)} %broadcast_in_dim.27), calls=%async_computation.2 | async-start | bytes 1835008 | tf_op jit(solution)/shard_map/all_to_all | solution.py:158
  101.4 0.1 fusion.35
  101.5 1.3 collective-permute-start.14
  102.8 1.9 %collective-permute-start.18 = (bf16[456,1536]{1,0:T(8,128)(2,1)}, bf16[456,1536]{1,0:T(8,128)(2,1)}, u32[]{:S(2)}, u32[]{:S(2)}) collective-permute-start(bf16[456,1536]{1,0:T(8,128)(2,1)} %collective-permute-done.12), channel_id=1, source_target_pairs={{1,33},{3,35},{5,37},{7,39},{9,41},{11,43},{13,45},{15,47},{17,49}... | collective-permute-start | bytes 4202504 | tf_op jit(solution)/shard_map/ppermute | solution.py:26
  104.7 2.9 %collective-permute-start.13 = (bf16[112,448]{1,0:T(8,128)(2,1)S(1)}, bf16[112,448]{1,0:T(8,128)(2,1)S(1)}, u32[]{:S(2)}, u32[]{:S(2)}) collective-permute-start(bf16[112,448]{1,0:T(8,128)(2,1)S(1)} %fusion.35), channel_id=1, source_target_pairs={{0,224},{1,193},{2,226},{3,195},{4,228},{5,197},{6,230},{7,199},{8... | collective-permute-start | bytes 301064 | tf_op jit(solution)/shard_map/ppermute | solution.py:26
  107.6 4.5 %collective-permute-done.14 = bf16[112,448]{1,0:T(8,128)(2,1)S(1)} collective-permute-done((bf16[112,448]{1,0:T(8,128)(2,1)S(1)}, bf16[112,448]{1,0:T(8,128)(2,1)S(1)}, u32[]{:S(2)}, u32[]{:S(2)}) %collective-permute-start.14) | collective-permute-done | bytes 100384 | tf_op jit(solution)/shard_map/ppermute | solution.py:26
  112.0 0.6 all-to-all-done.2
  112.7 0.7 pad_maximum_fusion.8
  113.4 0.9 collective-permute-start.15
  114.4 2.4 %collective-permute-start.16 = (bf16[2,112,448]{2,1,0:T(8,128)(2,1)}, bf16[2,112,448]{2,1,0:T(8,128)(2,1)}, u32[]{:S(2)}, u32[]{:S(2)}) collective-permute-start(bf16[2,112,448]{2,1,0:T(8,128)(2,1)} %pad_maximum_fusion.8), channel_id=1, source_target_pairs={{0,4},{1,5},{2,6},{3,7},{4,0},{5,1},{6,2},{7,3},{8,12},{9,13},{10,... | collective-permute-start | bytes 602120 | tf_op jit(solution)/shard_map/ppermute | solution.py:26
  116.8 1.2 collective-permute-start.17
  117.9 4.5 %conditional.2 = (f32[448,1536]{1,0:T(8,128)S(1)}) conditional(s32[]{:T(128)} %clamp.4, (bf16[456,1536]{1,0:T(8,128)(2,1)}, bf16[448,448]{1,0:T(8,128)(2,1)S(1)}, bf16[456,1536]{1,0:T(8,128)(2,1)}, bf16[448,448]{1,0:T(8,128)(2,1)S(1)}) %tuple.86, (bf16[456,1536]{1,0:T(8,128)(2,1)}, bf16[448,448]{1,0:T(8,128)(2,1)S(1)}, ...), branch_computations={%region_2.3_spmd, %region_3.4_spmd, %region_4.5_spmd, %region_5.6_... | conditional | flops 1233813504 | bytes 11812872 | solution.py:212
  117.9 2.2 %fusion.4 = f32[448,1536]{1,0:T(8,128)S(1)} fusion(bf16[448,448]{1,0:T(8,128)(2,1)S(1)} %get-tuple-element.86, bf16[456,1536]{1,0:T(8,128)(2,1)} %get-tuple-element.87), kind=kOutput, calls=%fused_computation.6 | convolution fusion | flops 616562688 | bytes 4530176 | tf_op jit(solution)/shard_map/cond/branch_1_fun/dot_general | solution.py:50
  120.2 2.3 %convolution_add_fusion.1 = f32[448,1536]{1,0:T(8,128)S(1)} fusion(f32[448,1536]{1,0:T(8,128)S(1)} %fusion.4, bf16[448,448]{1,0:T(8,128)(2,1)S(1)} %get-tuple-element.88, bf16[456,1536]{1,0:T(8,128)(2,1)} %get-tuple-element.89), kind=kOutput, calls=%fused_computation.4 | convolution fusion | flops 617250816 | bytes 7282688 | tf_op jit(solution)/shard_map/cond/branch_1_fun/dot_general | solution.py:50
  122.5 0.1 collective-permute-done.15
  122.5 5.1 %collective-permute-done.16 = bf16[2,112,448]{2,1,0:T(8,128)(2,1)} collective-permute-done((bf16[2,112,448]{2,1,0:T(8,128)(2,1)}, bf16[2,112,448]{2,1,0:T(8,128)(2,1)}, u32[]{:S(2)}, u32[]{:S(2)}) %collective-permute-start.16) | collective-permute-done | bytes 200736 | tf_op jit(solution)/shard_map/ppermute | solution.py:26
  127.7 0.1 collective-permute-done.17
  127.8 1.2 select_select_fusion.3
  129.1 1.2 select_select_fusion.7
  130.3 0.3 copy-done.1
  130.6 5.1 %conditional.3 = (f32[448,768]{1,0:T(8,128)S(1)}, f32[448,384]{1,0:T(8,128)S(1)}, f32[448,384]{1,0:T(8,128)S(1)}) conditional(s32[]{:T(128)} %clamp.4, (bf16[456,1536]{1,0:T(8,128)(2,1)}, bf16[448,448]{1,0:T(8,128)(2,1)S(1)}, bf16[448,448]{1,0:T(8,128)(2,1)S(1)}, bf16[448,1536]{1,0:T(8,128)(2,1)S(1)}, ...), branch_computations={%region_6.7_spmd, %region_7.8_spmd, %region_8.9_spmd, %region_9.10... | conditional | flops 1234845696 | bytes 22880280 | solution.py:232
  130.6 2.2 %fusion.17 = f32[448,1536]{1,0:T(8,128)S(1)} fusion(bf16[448,448]{1,0:T(8,128)(2,1)S(1)} %get-tuple-element.104, bf16[456,1536]{1,0:T(8,128)(2,1)} %get-tuple-element.105), kind=kOutput, calls=%fused_computation.25 | convolution fusion | flops 616562688 | bytes 4530176 | tf_op jit(solution)/shard_map/cond/branch_1_fun/dot_general | solution.py:50
  132.8 2.3 %fusion.15 = f32[448,1536]{1,0:T(8,128)S(1)} fusion(f32[448,1536]{1,0:T(8,128)S(1)} %get-tuple-element.103, f32[448,1536]{1,0:T(8,128)S(1)} %fusion.17, bf16[448,448]{1,0:T(8,128)(2,1)S(1)} %get-tuple-element.106, bf16[456,1536]{1,0:T(8,128)(2,1)} %get-tuple-element.107), kind=kOutput, calls=%fused_computation.22 | convolution fusion | flops 617938944 | bytes 10035200 | tf_op jit(solution)/shard_map/cond/branch_1_fun/dot_general | solution.py:50
  135.2 0.2 fusion.39
  135.4 0.1 pad_maximum_fusion.1
  135.7 0.1 collective-permute-start.19
  135.8 3.1 %collective-permute-done.19 = f32[448,768]{1,0:T(8,128)S(1)} collective-permute-done((f32[448,768]{1,0:T(8,128)S(1)}, f32[448,768]{1,0:T(8,128)S(1)}, u32[]{:S(2)}, u32[]{:S(2)}) %collective-permute-start.19) | collective-permute-done | bytes 1376288 | tf_op jit(solution)/shard_map/ppermute | solution.py:26
  139.0 5.0 %collective-permute-start.20 = (f32[448,384]{1,0:T(8,128)S(1)}, f32[448,384]{1,0:T(8,128)S(1)}, u32[]{:S(2)}, u32[]{:S(2)}) collective-permute-start(f32[448,384]{1,0:T(8,128)S(1)} %slice_add_fusion), channel_id=1, source_target_pairs={{0,8},{1,9},{2,10},{3,11},{4,12},{5,13},{6,14},{7,15},{8,0},{9,1},... | collective-permute-start | bytes 2064392 | tf_op jit(solution)/shard_map/ppermute | solution.py:26
  144.0 15.7 %collective-permute-done.20 = f32[448,384]{1,0:T(8,128)S(1)} collective-permute-done((f32[448,384]{1,0:T(8,128)S(1)}, f32[448,384]{1,0:T(8,128)S(1)}, u32[]{:S(2)}, u32[]{:S(2)}) %collective-permute-start.20) | collective-permute-done | bytes 688160 | tf_op jit(solution)/shard_map/ppermute | solution.py:26
  159.7 0.9 fusion.28
  (40 shorter events, 0.5 us)
Async XLA Ops:
  0.0 10.6 %collective-permute-start.1 = (bf16[448,384]{1,0:T(8,128)(2,1)}, bf16[448,384]{1,0:T(8,128)(2,1)S(1)}, u32[]{:S(2)}, u32[]{:S(2)}) collective-permute-start(bf16[448,384]{1,0:T(8,128)(2,1)} %bitcast.126), channel_id=1, source_target_pairs={{0,8},{1,9},{2,10},{3,11},{4,12},{5,13},{6,14},{7,15},{8,0},{9,1},... | collective-permute-start | bytes 1032200 | tf_op jit(solution)/shard_map/ppermute | solution.py:26
  3.6 9.2 %collective-permute-start = (bf16[448,384]{1,0:T(8,128)(2,1)}, bf16[448,384]{1,0:T(8,128)(2,1)S(1)}, u32[]{:S(2)}, u32[]{:S(2)}) collective-permute-start(bf16[448,384]{1,0:T(8,128)(2,1)} %bitcast.127), channel_id=1, source_target_pairs={{0,1},{1,0},{2,3},{3,2},{4,5},{5,4},{6,7},{7,6},{8,9},{9,8},{10,11... | collective-permute-start | bytes 1032200 | tf_op jit(solution)/shard_map/ppermute | solution.py:26
  10.6 3.5 %collective-permute-start.2 = (bf16[448,384]{1,0:T(8,128)(2,1)S(1)}, bf16[448,384]{1,0:T(8,128)(2,1)S(1)}, u32[]{:S(2)}, u32[]{:S(2)}) collective-permute-start(bf16[448,384]{1,0:T(8,128)(2,1)S(1)} %collective-permute-done.1), channel_id=1, source_target_pairs={{0,1},{1,0},{2,3},{3,2},{4,5},{5,4},{6,7},{7,6},{8,9},{9,8},{10,11... | collective-permute-start | bytes 1032200 | tf_op jit(solution)/shard_map/ppermute | solution.py:26
  14.6 1.1 copy-start
  15.7 21.9 %collective-permute-start.3 = (bf16[456,1536]{1,0:T(8,128)(2,1)S(1)}, bf16[456,1536]{1,0:T(8,128)(2,1)}, u32[]{:S(2)}, u32[]{:S(2)}) collective-permute-start(bf16[456,1536]{1,0:T(8,128)(2,1)S(1)} %pad_maximum_fusion.4.mine_ref), channel_id=1, source_target_pairs={{0,224},{1,33},{2,226},{3,35},{4,228},{5,37},{6,230},{7,39},{8,248... | collective-permute-start | bytes 4202504 | tf_op jit(solution)/shard_map/ppermute | solution.py:26
  17.5 20.8 %collective-permute-start.5 = (bf16[456,1536]{1,0:T(8,128)(2,1)S(1)}, bf16[456,1536]{1,0:T(8,128)(2,1)S(1)}, u32[]{:S(2)}, u32[]{:S(2)}) collective-permute-start(bf16[456,1536]{1,0:T(8,128)(2,1)S(1)} %pad_maximum_fusion.4.mine_ref), channel_id=1, source_target_pairs={{0,24},{2,26},{4,28},{6,30},{16,8},{18,10},{20,12},{22,14},{32,56}... | collective-permute-start | bytes 4202504 | tf_op jit(solution)/shard_map/ppermute | solution.py:26
  37.5 3.7 %collective-permute-start.4 = (bf16[456,1536]{1,0:T(8,128)(2,1)}, bf16[456,1536]{1,0:T(8,128)(2,1)S(1)}, u32[]{:S(2)}, u32[]{:S(2)}) collective-permute-start(bf16[456,1536]{1,0:T(8,128)(2,1)} %collective-permute-done.3.one_ref), channel_id=1, source_target_pairs={{0,1},{1,0},{2,3},{3,2},{4,5},{5,4},{6,7},{7,6},{8,9},{9,8},{10,11... | collective-permute-start | bytes 4202504 | tf_op jit(solution)/shard_map/ppermute | solution.py:26
  38.3 13.5 %copy-start.4 = (f32[448]{0:T(512)S(1)}, f32[448]{0:T(512)}, u32[]{:S(2)}) copy-start(f32[448]{0:T(512)} %param.13) | copy-start | bytes 5380
  38.3 26.5 %collective-permute-start.7 = (bf16[456,1536]{1,0:T(8,128)(2,1)}, bf16[456,1536]{1,0:T(8,128)(2,1)}, u32[]{:S(2)}, u32[]{:S(2)}) collective-permute-start(bf16[456,1536]{1,0:T(8,128)(2,1)} %collective-permute-done.3.one_ref), channel_id=1, source_target_pairs={{0,224},{1,33},{2,226},{3,35},{4,228},{5,37},{6,230},{7,39},{8,232... | collective-permute-start | bytes 4202504 | tf_op jit(solution)/shard_map/ppermute | solution.py:26
  38.3 8.0 %copy-start.2 = (bf16[456,1536]{1,0:T(8,128)(2,1)}, bf16[456,1536]{1,0:T(8,128)(2,1)S(1)}, u32[]{:S(2)}) copy-start(bf16[456,1536]{1,0:T(8,128)(2,1)S(1)} %collective-permute-done.5.beyond_ref) | copy-start | bytes 4202500
  46.3 30.8 %collective-permute-start.6 = (bf16[456,1536]{1,0:T(8,128)(2,1)S(1)}, bf16[456,1536]{1,0:T(8,128)(2,1)S(1)}, u32[]{:S(2)}, u32[]{:S(2)}) collective-permute-start(bf16[456,1536]{1,0:T(8,128)(2,1)S(1)} %collective-permute-done.4.swap_ref.swap_one_ref), channel_id=1, source_target_pairs={{1,225},{3,227},{5,229},{7,231},{9,233},{11,235},{13,237},{15,239}... | collective-permute-start | bytes 4202504 | tf_op jit(solution)/shard_map/ppermute | solution.py:26
  51.9 29.2 %all-to-all-start = ((f32[4,2,112,448]{3,2,1,0:T(8,128)}), f32[4,2,112,448]{3,2,1,0:T(8,128)}, u32[]{:S(2)}, u32[]{:S(2)}) async-start(f32[4,2,112,448]{3,2,1,0:T(8,128)} %shard_map.37), calls=%async_computation | async-start | bytes 3670016 | tf_op jit(solution)/shard_map/all_to_all | solution.py:136
  57.7 38.1 %collective-permute-start.10 = (bf16[456,1536]{1,0:T(8,128)(2,1)}, bf16[456,1536]{1,0:T(8,128)(2,1)}, u32[]{:S(2)}, u32[]{:S(2)}) collective-permute-start(bf16[456,1536]{1,0:T(8,128)(2,1)} %collective-permute-done.3.one_ref), channel_id=1, source_target_pairs={{1,25},{3,27},{5,29},{7,31},{17,9},{19,11},{21,13},{23,15},{33,57}... | collective-permute-start | bytes 4202504 | tf_op jit(solution)/shard_map/ppermute | solution.py:26
  64.8 31.0 %collective-permute-start.12 = (bf16[456,1536]{1,0:T(8,128)(2,1)}, bf16[456,1536]{1,0:T(8,128)(2,1)}, u32[]{:S(2)}, u32[]{:S(2)}) collective-permute-start(bf16[456,1536]{1,0:T(8,128)(2,1)} %collective-permute-done.7.two_ref), channel_id=1, source_target_pairs={{0,224},{1,33},{2,226},{3,35},{4,228},{5,37},{6,230},{7,39},{8,232... | collective-permute-start | bytes 4202504 | tf_op jit(solution)/shard_map/ppermute | solution.py:26
  64.8 31.0 %collective-permute-start.11 = (bf16[456,1536]{1,0:T(8,128)(2,1)}, bf16[456,1536]{1,0:T(8,128)(2,1)}, u32[]{:S(2)}, u32[]{:S(2)}) collective-permute-start(bf16[456,1536]{1,0:T(8,128)(2,1)} %collective-permute-done.7.two_ref), channel_id=1, source_target_pairs={{1,25},{3,27},{5,29},{7,31},{17,9},{19,11},{21,13},{23,15},{33,57}... | collective-permute-start | bytes 4202504 | tf_op jit(solution)/shard_map/ppermute | solution.py:26
  81.1 14.6 %all-to-all-start.1 = ((f32[4,1,112,448]{3,2,1,0:T(8,128)}), f32[4,1,112,448]{3,2,1,0:T(8,128)S(1)}, u32[]{:S(2)}, u32[]{:S(2)}) async-start(f32[4,1,112,448]{3,2,1,0:T(8,128)} %shard_map.38), calls=%async_computation.1 | async-start | bytes 1835008 | tf_op jit(solution)/shard_map/all_to_all | solution.py:136
  87.2 8.4 %collective-permute-start.9 = (bf16[112,448]{1,0:T(8,128)(2,1)S(1)}, bf16[112,448]{1,0:T(8,128)(2,1)S(1)}, u32[]{:S(2)}, u32[]{:S(2)}) collective-permute-start(bf16[112,448]{1,0:T(8,128)(2,1)S(1)} %get-tuple-element.195), channel_id=1, source_target_pairs={{1,33},{3,35},{5,37},{7,39},{9,57},{11,59},{13,61},{15,63},{17,49}... | collective-permute-start | bytes 301064 | tf_op jit(solution)/shard_map/ppermute | solution.py:26
  89.9 6.2 %collective-permute-start.8 = (bf16[112,448]{1,0:T(8,128)(2,1)S(1)}, bf16[112,448]{1,0:T(8,128)(2,1)S(1)}, u32[]{:S(2)}, u32[]{:S(2)}) collective-permute-start(bf16[112,448]{1,0:T(8,128)(2,1)S(1)} %get-tuple-element.195), channel_id=1, source_target_pairs={{0,33},{1,224},{2,35},{3,226},{4,37},{5,228},{6,39},{7,230},{8,57}... | collective-permute-start | bytes 301064 | tf_op jit(solution)/shard_map/ppermute | solution.py:26
  97.1 15.5 %all-to-all-start.2 = ((bf16[4,2,112,448]{3,2,1,0:T(8,128)(2,1)}), bf16[4,2,112,448]{3,2,1,0:T(8,128)(2,1)S(1)}, u32[]{:S(2)}, u32[]{:S(2)}) async-start(bf16[4,2,112,448]{3,2,1,0:T(8,128)(2,1)} %broadcast_in_dim.27), calls=%async_computation.2 | async-start | bytes 1835008 | tf_op jit(solution)/shard_map/all_to_all | solution.py:158
  101.5 10.5 %collective-permute-start.14 = (bf16[112,448]{1,0:T(8,128)(2,1)S(1)}, bf16[112,448]{1,0:T(8,128)(2,1)S(1)}, u32[]{:S(2)}, u32[]{:S(2)}) collective-permute-start(bf16[112,448]{1,0:T(8,128)(2,1)S(1)} %fusion.35), channel_id=1, source_target_pairs={{0,65},{2,67},{4,69},{6,71},{8,89},{10,91},{12,93},{14,95},{16,81}... | collective-permute-start | bytes 301064 | tf_op jit(solution)/shard_map/ppermute | solution.py:26
  102.8 27.5 %collective-permute-start.18 = (bf16[456,1536]{1,0:T(8,128)(2,1)}, bf16[456,1536]{1,0:T(8,128)(2,1)}, u32[]{:S(2)}, u32[]{:S(2)}) collective-permute-start(bf16[456,1536]{1,0:T(8,128)(2,1)} %collective-permute-done.12), channel_id=1, source_target_pairs={{1,33},{3,35},{5,37},{7,39},{9,41},{11,43},{13,45},{15,47},{17,49}... | collective-permute-start | bytes 4202504 | tf_op jit(solution)/shard_map/ppermute | solution.py:26
  104.7 8.0 %collective-permute-start.13 = (bf16[112,448]{1,0:T(8,128)(2,1)S(1)}, bf16[112,448]{1,0:T(8,128)(2,1)S(1)}, u32[]{:S(2)}, u32[]{:S(2)}) collective-permute-start(bf16[112,448]{1,0:T(8,128)(2,1)S(1)} %fusion.35), channel_id=1, source_target_pairs={{0,224},{1,193},{2,226},{3,195},{4,228},{5,197},{6,230},{7,199},{8... | collective-permute-start | bytes 301064 | tf_op jit(solution)/shard_map/ppermute | solution.py:26
  113.4 9.1 %collective-permute-start.15 = (bf16[2,112,448]{2,1,0:T(8,128)(2,1)}, bf16[2,112,448]{2,1,0:T(8,128)(2,1)}, u32[]{:S(2)}, u32[]{:S(2)}) collective-permute-start(bf16[2,112,448]{2,1,0:T(8,128)(2,1)} %pad_maximum_fusion.8), channel_id=1, source_target_pairs={{0,2},{1,3},{2,4},{3,5},{4,6},{5,7},{6,0},{7,1},{8,10},{9,11},{10,... | collective-permute-start | bytes 602120 | tf_op jit(solution)/shard_map/ppermute | solution.py:26
  114.4 13.3 %collective-permute-start.16 = (bf16[2,112,448]{2,1,0:T(8,128)(2,1)}, bf16[2,112,448]{2,1,0:T(8,128)(2,1)}, u32[]{:S(2)}, u32[]{:S(2)}) collective-permute-start(bf16[2,112,448]{2,1,0:T(8,128)(2,1)} %pad_maximum_fusion.8), channel_id=1, source_target_pairs={{0,4},{1,5},{2,6},{3,7},{4,0},{5,1},{6,2},{7,3},{8,12},{9,13},{10,... | collective-permute-start | bytes 602120 | tf_op jit(solution)/shard_map/ppermute | solution.py:26
  116.8 11.1 %collective-permute-start.17 = (bf16[2,112,448]{2,1,0:T(8,128)(2,1)}, bf16[2,112,448]{2,1,0:T(8,128)(2,1)}, u32[]{:S(2)}, u32[]{:S(2)}) collective-permute-start(bf16[2,112,448]{2,1,0:T(8,128)(2,1)} %pad_maximum_fusion.8), channel_id=1, source_target_pairs={{0,6},{1,7},{2,0},{3,1},{4,2},{5,3},{6,4},{7,5},{8,14},{9,15},{10,... | collective-permute-start | bytes 602120 | tf_op jit(solution)/shard_map/ppermute | solution.py:26
  127.8 2.5 %copy-start.3 = (bf16[456,1536]{1,0:T(8,128)(2,1)S(1)}, bf16[456,1536]{1,0:T(8,128)(2,1)}, u32[]{:S(2)}) copy-start(bf16[456,1536]{1,0:T(8,128)(2,1)} %copy-done.2) | copy-start | bytes 4202500
  129.0 1.6 copy-start.1
  135.7 3.2 %collective-permute-start.19 = (f32[448,768]{1,0:T(8,128)S(1)}, f32[448,768]{1,0:T(8,128)S(1)}, u32[]{:S(2)}, u32[]{:S(2)}) collective-permute-start(f32[448,768]{1,0:T(8,128)S(1)} %get-tuple-element.160), channel_id=1, source_target_pairs={{0,1},{1,0},{2,3},{3,2},{4,5},{5,4},{6,7},{7,6},{8,9},{9,8},{10,11... | collective-permute-start | bytes 4128776 | tf_op jit(solution)/shard_map/ppermute | solution.py:26
  139.0 20.7 %collective-permute-start.20 = (f32[448,384]{1,0:T(8,128)S(1)}, f32[448,384]{1,0:T(8,128)S(1)}, u32[]{:S(2)}, u32[]{:S(2)}) collective-permute-start(f32[448,384]{1,0:T(8,128)S(1)} %slice_add_fusion), channel_id=1, source_target_pairs={{0,8},{1,9},{2,10},{3,11},{4,12},{5,13},{6,14},{7,15},{8,0},{9,1},... | collective-permute-start | bytes 2064392 | tf_op jit(solution)/shard_map/ppermute | solution.py:26

commit v18 on v17

--- a/solution.py
+++ b/solution.py
@@ -153,11 +153,6 @@
             for m in range(parts.shape[0])
         ]
 
-    def to_all(*parts):
-        parts = jnp.stack(parts)
-        whole = lax.all_to_all(jnp.broadcast_to(parts, (NY, *parts.shape)), "y", 0, 0, tiled=True)
-        return [whole[:, n].reshape(nvir, nvir) for n in range(parts.shape[0])]
-
     where = jnp.stack([c, xh])
     parts = numerators(early_kernel, 2, where, nvir, mine, step_one, swap_one, beyond)
     parts, swap_one, step_one_after = lax.optimization_barrier((parts, swap_one, step_one))
@@ -193,7 +188,7 @@
         (late, first, second, amps_zero, turned_one, turned_two, step_three)
     )
 
-    first, second = to_all(first, second)
+    first, second = by_hops(first, second)
 
     amps_two = amps(late[0], jnp.where(c == 0, swap_energy, energy(swap_two)), energy(step_two))
     third = moved(

time: 162 us -> 163 us (level)
  starting transfers between devices: 55.3 us -> 58 us
    ppermute x21 -> x24, starting transfers between devices: 42.5 us -> 49.4 us  [moved(): return lax.ppermute(array, ALL, pairs)]
    all_to_all x1 -> x0, starting transfers between devices: 4.24 us -> none  [to_all(): lax.all_to_all(jnp.broadcast_to(parts, (NY, *parts.shape)), 'y', 0, 0, ti...]
    ppermute x21 -> x24, waiting for transfers between devices: 68.5 us -> 68.5 us  [moved(): return lax.ppermute(array, ALL, pairs)]
  transfers between devices with their start and end apart: 24 -> 26, of which waited for: 13 -> 11; matrix products, arithmetic and copies ran while one was open for 9% -> 9% of each run, Pallas kernels for 6% -> 6%
where the time goes in v18:
time: 163 us; the launch traced here: 162 us
  waiting for transfers between devices  68.5 us (42%)
  starting transfers between devices  58 us (36%)
  other arithmetic  11.9 us (7%)
  Pallas kernels  9.45 us (6%)
  matrix products  9.08 us (6%)
  between operations  3.2 us (2%)
    ppermute x24, waiting for transfers between devices, moved(): return lax.ppermute(array, ALL, pairs)  68.5 us
    ppermute x24, starting transfers between devices, moved(): return lax.ppermute(array, ALL, pairs)  49.4 us
    pallas_call x2, Pallas kernels, numerators(): pl.pallas_call(kernel, out_shape=jax.ShapeDtypeStruct((NY, count, share,...  9.45 us
    dot_general x4, matrix products, dot_tn(): lax.dot_general(a, b, (((0,), (0,)), ((), ())), preferred_element_type=jn...  9.08 us
    all_to_all x2, starting transfers between devices, exchanged(): return lax.all_to_all(parts, 'y', 0, 0, tiled=True)  8.57 us
  transfers between devices with their start and end apart: 26, of which 11 were waited for; matrix products, arithmetic and copies ran while one was open for 9% of the time, Pallas kernels for 6%

profile of v18, /device:TPU:1, one launch (start us, length us, event | category | flops | bytes accessed | tf_op | source)
XLA Modules:
  0.0 161.9 jit_solution(5098627404557669333)
XLA Ops:
  0.0 3.6 %collective-permute-start.1 = (bf16[448,384]{1,0:T(8,128)(2,1)}, bf16[448,384]{1,0:T(8,128)(2,1)S(1)}, u32[]{:S(2)}, u32[]{:S(2)}) collective-permute-start(bf16[448,384]{1,0:T(8,128)(2,1)} %bitcast.177), channel_id=1, source_target_pairs={{0,8},{1,9},{2,10},{3,11},{4,12},{5,13},{6,14},{7,15},{8,0},{9,1},... | collective-permute-start | bytes 1032200 | tf_op jit(solution)/shard_map/ppermute | solution.py:26
  3.6 1.0 collective-permute-start
  7.4 1.3 select_convert_fusion
  8.7 2.0 %collective-permute-done.1 = bf16[448,384]{1,0:T(8,128)(2,1)S(1)} collective-permute-done((bf16[448,384]{1,0:T(8,128)(2,1)}, bf16[448,384]{1,0:T(8,128)(2,1)S(1)}, u32[]{:S(2)}, u32[]{:S(2)}) %collective-permute-start.1) | collective-permute-done | bytes 344096 | tf_op jit(solution)/shard_map/ppermute | solution.py:26
  10.6 2.2 %collective-permute-start.2 = (bf16[448,384]{1,0:T(8,128)(2,1)S(1)}, bf16[448,384]{1,0:T(8,128)(2,1)S(1)}, u32[]{:S(2)}, u32[]{:S(2)}) collective-permute-start(bf16[448,384]{1,0:T(8,128)(2,1)S(1)} %collective-permute-done.1), channel_id=1, source_target_pairs={{0,1},{1,0},{2,3},{3,2},{4,5},{5,4},{6,7},{7,6},{8,9},{9,8},{10,11... | collective-permute-start | bytes 1032200 | tf_op jit(solution)/shard_map/ppermute | solution.py:26
  12.8 1.2 maximum_select_fusion.1
  14.1 0.2 maximum_select_fusion.2
  14.2 0.3 maximum_select_fusion
  14.6 0.1 pad_maximum_fusion.4.mine_ref
  14.7 1.0 copy-done
  15.7 1.9 %collective-permute-start.3 = (bf16[456,1536]{1,0:T(8,128)(2,1)S(1)}, bf16[456,1536]{1,0:T(8,128)(2,1)}, u32[]{:S(2)}, u32[]{:S(2)}) collective-permute-start(bf16[456,1536]{1,0:T(8,128)(2,1)S(1)} %pad_maximum_fusion.4.mine_ref), channel_id=1, source_target_pairs={{0,224},{1,33},{2,226},{3,35},{4,228},{5,37},{6,230},{7,39},{8,248... | collective-permute-start | bytes 4202504 | tf_op jit(solution)/shard_map/ppermute | solution.py:26
  17.5 1.8 %collective-permute-start.5 = (bf16[456,1536]{1,0:T(8,128)(2,1)S(1)}, bf16[456,1536]{1,0:T(8,128)(2,1)}, u32[]{:S(2)}, u32[]{:S(2)}) collective-permute-start(bf16[456,1536]{1,0:T(8,128)(2,1)S(1)} %pad_maximum_fusion.4.mine_ref), channel_id=1, source_target_pairs={{0,24},{2,26},{4,28},{6,30},{16,8},{18,10},{20,12},{22,14},{32,56}... | collective-permute-start | bytes 4202504 | tf_op jit(solution)/shard_map/ppermute | solution.py:26
  19.3 18.2 %collective-permute-done.3.one_ref = bf16[456,1536]{1,0:T(8,128)(2,1)} collective-permute-done((bf16[456,1536]{1,0:T(8,128)(2,1)S(1)}, bf16[456,1536]{1,0:T(8,128)(2,1)}, u32[]{:S(2)}, u32[]{:S(2)}) %collective-permute-start.3) | collective-permute-done | bytes 1400864 | tf_op jit(solution)/shard_map/ppermute | solution.py:26
  37.5 0.7 collective-permute-start.4
  38.4 2.8 %collective-permute-done.4.swap_ref.swap_one_ref = bf16[456,1536]{1,0:T(8,128)(2,1)S(1)} collective-permute-done((bf16[456,1536]{1,0:T(8,128)(2,1)}, bf16[456,1536]{1,0:T(8,128)(2,1)S(1)}, u32[]{:S(2)}, u32[]{:S(2)}) %collective-permute-start.4) | collective-permute-done | bytes 1400864 | tf_op jit(solution)/shard_map/ppermute | solution.py:26
  41.2 5.5 %shard_map.37 = f32[4,2,112,448]{3,2,1,0:T(8,128)} custom-call(s32[2]{0:T(128)S(1)} %pad_add_fusion.where_ref, bf16[456,1536]{1,0:T(8,128)(2,1)S(1)} %pad_maximum_fusion.4.mine_ref, bf16[456,1536]{1,0:T(8,128)(2,1)} %collective-permute-done.3.one_ref, bf16[456,1536]{1,0:T(8,128)(2,1)S(1)} %collective-permute-done.4.swap_ref.swap_one_ref, ...), custom_call_target="tpu_custom_call" | custom-call | flops 2466250752 | bytes 7110656 | tf_op jit(solution)/shard_map/pallas_call | solution.py:91
  46.8 5.4 %collective-permute-start.6 = (bf16[456,1536]{1,0:T(8,128)(2,1)S(1)}, bf16[456,1536]{1,0:T(8,128)(2,1)S(1)}, u32[]{:S(2)}, u32[]{:S(2)}) collective-permute-start(bf16[456,1536]{1,0:T(8,128)(2,1)S(1)} %collective-permute-done.4.swap_ref.swap_one_ref), channel_id=1, source_target_pairs={{1,225},{3,227},{5,229},{7,231},{9,233},{11,235},{13,237},{15,239}... | collective-permute-start | bytes 4202504 | tf_op jit(solution)/shard_map/ppermute | solution.py:26
  52.2 0.7 slice_convert_fusion.2
  52.9 4.4 %all-to-all-start = ((f32[4,2,112,448]{3,2,1,0:T(8,128)}), f32[4,2,112,448]{3,2,1,0:T(8,128)}, u32[]{:S(2)}, u32[]{:S(2)}) async-start(f32[4,2,112,448]{3,2,1,0:T(8,128)} %shard_map.37), calls=%async_computation | async-start | bytes 3670016 | tf_op jit(solution)/shard_map/all_to_all | solution.py:136
  57.3 0.7 slice_convert_fusion.3
  58.0 7.1 %collective-permute-start.10 = (bf16[456,1536]{1,0:T(8,128)(2,1)}, bf16[456,1536]{1,0:T(8,128)(2,1)}, u32[]{:S(2)}, u32[]{:S(2)}) collective-permute-start(bf16[456,1536]{1,0:T(8,128)(2,1)} %collective-permute-done.3.one_ref), channel_id=1, source_target_pairs={{1,25},{3,27},{5,29},{7,31},{17,9},{19,11},{21,13},{23,15},{33,57}... | collective-permute-start | bytes 4202504 | tf_op jit(solution)/shard_map/ppermute | solution.py:26
  65.1 2.4 %collective-permute-start.11 = (bf16[456,1536]{1,0:T(8,128)(2,1)}, bf16[456,1536]{1,0:T(8,128)(2,1)}, u32[]{:S(2)}, u32[]{:S(2)}) collective-permute-start(bf16[456,1536]{1,0:T(8,128)(2,1)} %collective-permute-done.7.two_ref), channel_id=1, source_target_pairs={{1,25},{3,27},{5,29},{7,31},{17,9},{19,11},{21,13},{23,15},{33,57}... | collective-permute-start | bytes 4202504 | tf_op jit(solution)/shard_map/ppermute | solution.py:26
  67.5 0.7 slice_convert_fusion
  68.2 9.4 %collective-permute-done.6.swap_two_ref = bf16[456,1536]{1,0:T(8,128)(2,1)S(1)} collective-permute-done((bf16[456,1536]{1,0:T(8,128)(2,1)S(1)}, bf16[456,1536]{1,0:T(8,128)(2,1)S(1)}, u32[]{:S(2)}, u32[]{:S(2)}) %collective-permute-start.6) | collective-permute-done | bytes 1400864 | tf_op jit(solution)/shard_map/ppermute | solution.py:26
  77.6 3.9 %shard_map.38 = f32[4,1,112,448]{3,2,1,0:T(8,128)} custom-call(s32[2]{0:T(128)S(1)} %pad_add_fusion.where_ref, bf16[456,1536]{1,0:T(8,128)(2,1)S(1)} %collective-permute-done.4.swap_ref.swap_one_ref, bf16[456,1536]{1,0:T(8,128)(2,1)S(1)} %collective-permute-done.6.swap_two_ref, bf16[456,1536]{1,0:T(8,128)(2,1)} %collective-permute-done.7.two_ref), custom_call_target="tpu_custom_call" | custom-call | flops 1233125376 | bytes 4931584 | tf_op jit(solution)/shard_map/pallas_call | solution.py:91
  81.5 4.2 %all-to-all-start.1 = ((f32[4,1,112,448]{3,2,1,0:T(8,128)}), f32[4,1,112,448]{3,2,1,0:T(8,128)S(1)}, u32[]{:S(2)}, u32[]{:S(2)}) async-start(f32[4,1,112,448]{3,2,1,0:T(8,128)} %shard_map.38), calls=%async_computation.1 | async-start | bytes 1835008 | tf_op jit(solution)/shard_map/all_to_all | solution.py:136
  85.7 1.7 %reduce_sum.22 = f32[2,112,448]{2,1,0:T(8,128)S(1)} reduce(f32[4,2,112,448]{3,2,1,0:T(8,128)} %all-to-all-done, f32[]{:T(128)} %constant.6.clone.1), dimensions={0}, to_apply=%region_1.2 | reduce | flops 301056 | bytes 2007044 | tf_op jit(solution)/shard_map/reduce_sum | solution.py:171
  87.5 0.1 fusion.36
  87.7 1.9 %collective-permute-start.9 = (bf16[112,448]{1,0:T(8,128)(2,1)S(1)}, bf16[112,448]{1,0:T(8,128)(2,1)S(1)}, u32[]{:S(2)}, u32[]{:S(2)}) collective-permute-start(bf16[112,448]{1,0:T(8,128)(2,1)S(1)} %get-tuple-element.201), channel_id=1, source_target_pairs={{1,33},{3,35},{5,37},{7,39},{9,57},{11,59},{13,61},{15,63},{17,49}... | collective-permute-start | bytes 301064 | tf_op jit(solution)/shard_map/ppermute | solution.py:26
  89.6 0.1 collective-permute-start.8
  89.7 1.9 %collective-permute-start.21 = (bf16[456,1536]{1,0:T(8,128)(2,1)}, bf16[456,1536]{1,0:T(8,128)(2,1)}, u32[]{:S(2)}, u32[]{:S(2)}) collective-permute-start(bf16[456,1536]{1,0:T(8,128)(2,1)} %collective-permute-done.12), channel_id=1, source_target_pairs={{1,33},{3,35},{5,37},{7,39},{9,41},{11,43},{13,45},{15,47},{17,49}... | collective-permute-start | bytes 4202504 | tf_op jit(solution)/shard_map/ppermute | solution.py:26
  91.6 4.7 %collective-permute-done.9 = bf16[112,448]{1,0:T(8,128)(2,1)S(1)} collective-permute-done((bf16[112,448]{1,0:T(8,128)(2,1)S(1)}, bf16[112,448]{1,0:T(8,128)(2,1)S(1)}, u32[]{:S(2)}, u32[]{:S(2)}) %collective-permute-start.9) | collective-permute-done | bytes 100384 | tf_op jit(solution)/shard_map/ppermute | solution.py:26
  96.4 0.1 reduce_sum.20
  96.5 0.1 fusion.35
  96.6 1.3 collective-permute-start.14
  98.0 1.5 collective-permute-start.15
  99.5 2.4 %collective-permute-start.16 = (bf16[2,112,448]{2,1,0:T(8,128)(2,1)S(1)}, bf16[2,112,448]{2,1,0:T(8,128)(2,1)S(1)}, u32[]{:S(2)}, u32[]{:S(2)}) collective-permute-start(bf16[2,112,448]{2,1,0:T(8,128)(2,1)S(1)} %pad_maximum_fusion.9), channel_id=1, source_target_pairs={{0,4},{1,5},{2,6},{3,7},{4,0},{5,1},{6,2},{7,3},{8,12},{9,13},{10,... | collective-permute-start | bytes 602120 | tf_op jit(solution)/shard_map/ppermute | solution.py:26
  101.9 1.2 collective-permute-start.17
  103.1 3.6 %collective-permute-done.14 = bf16[112,448]{1,0:T(8,128)(2,1)S(1)} collective-permute-done((bf16[112,448]{1,0:T(8,128)(2,1)S(1)}, bf16[112,448]{1,0:T(8,128)(2,1)S(1)}, u32[]{:S(2)}, u32[]{:S(2)}) %collective-permute-start.14) | collective-permute-done | bytes 100384 | tf_op jit(solution)/shard_map/ppermute | solution.py:26
  106.7 1.7 %collective-permute-start.13 = (bf16[112,448]{1,0:T(8,128)(2,1)S(1)}, bf16[112,448]{1,0:T(8,128)(2,1)S(1)}, u32[]{:S(2)}, u32[]{:S(2)}) collective-permute-start(bf16[112,448]{1,0:T(8,128)(2,1)S(1)} %fusion.35), channel_id=1, source_target_pairs={{0,224},{1,193},{2,226},{3,195},{4,228},{5,197},{6,230},{7,199},{8... | collective-permute-start | bytes 301064 | tf_op jit(solution)/shard_map/ppermute | solution.py:26
  108.4 3.1 %collective-permute-done.16 = bf16[2,112,448]{2,1,0:T(8,128)(2,1)S(1)} collective-permute-done((bf16[2,112,448]{2,1,0:T(8,128)(2,1)S(1)}, bf16[2,112,448]{2,1,0:T(8,128)(2,1)S(1)}, u32[]{:S(2)}, u32[]{:S(2)}) %collective-permute-start.16) | collective-permute-done | bytes 200736 | tf_op jit(solution)/shard_map/ppermute | solution.py:26
  111.7 1.1 collective-permute-done.13
  112.8 0.7 pad_maximum_fusion.10
  113.5 0.7 collective-permute-start.18
  114.1 2.7 %collective-permute-start.19 = (bf16[2,112,448]{2,1,0:T(8,128)(2,1)}, bf16[2,112,448]{2,1,0:T(8,128)(2,1)}, u32[]{:S(2)}, u32[]{:S(2)}) collective-permute-start(bf16[2,112,448]{2,1,0:T(8,128)(2,1)} %pad_maximum_fusion.10), channel_id=1, source_target_pairs={{0,4},{1,5},{2,6},{3,7},{4,0},{5,1},{6,2},{7,3},{8,12},{9,13},{10,... | collective-permute-start | bytes 602120 | tf_op jit(solution)/shard_map/ppermute | solution.py:26
  116.9 0.9 collective-permute-start.20
  117.8 4.5 %conditional.2 = (f32[448,1536]{1,0:T(8,128)S(1)}) conditional(s32[]{:T(128)} %clamp.4, (bf16[456,1536]{1,0:T(8,128)(2,1)}, bf16[448,448]{1,0:T(8,128)(2,1)S(1)}, bf16[456,1536]{1,0:T(8,128)(2,1)}, bf16[448,448]{1,0:T(8,128)(2,1)S(1)}) %tuple.43, (bf16[456,1536]{1,0:T(8,128)(2,1)}, bf16[448,448]{1,0:T(8,128)(2,1)S(1)}, ...), branch_computations={%region_2.3_spmd, %region_3.4_spmd, %region_4.5_spmd, %region_5.6_... | conditional | flops 1233813504 | bytes 11812872 | solution.py:207
  117.8 2.2 %fusion.4 = f32[448,1536]{1,0:T(8,128)S(1)} fusion(bf16[448,448]{1,0:T(8,128)(2,1)S(1)} %get-tuple-element.86, bf16[456,1536]{1,0:T(8,128)(2,1)} %get-tuple-element.87), kind=kOutput, calls=%fused_computation.6 | convolution fusion | flops 616562688 | bytes 4530176 | tf_op jit(solution)/shard_map/cond/branch_1_fun/dot_general | solution.py:50
  120.0 2.3 %convolution_add_fusion.1 = f32[448,1536]{1,0:T(8,128)S(1)} fusion(f32[448,1536]{1,0:T(8,128)S(1)} %fusion.4, bf16[448,448]{1,0:T(8,128)(2,1)S(1)} %get-tuple-element.88, bf16[456,1536]{1,0:T(8,128)(2,1)} %get-tuple-element.89), kind=kOutput, calls=%fused_computation.4 | convolution fusion | flops 617250816 | bytes 7282688 | tf_op jit(solution)/shard_map/cond/branch_1_fun/dot_general | solution.py:50
  122.3 5.0 %collective-permute-done.19 = bf16[2,112,448]{2,1,0:T(8,128)(2,1)} collective-permute-done((bf16[2,112,448]{2,1,0:T(8,128)(2,1)}, bf16[2,112,448]{2,1,0:T(8,128)(2,1)}, u32[]{:S(2)}, u32[]{:S(2)}) %collective-permute-start.19) | collective-permute-done | bytes 200736 | tf_op jit(solution)/shard_map/ppermute | solution.py:26
  127.3 1.1 select_select_fusion.3
  128.4 1.2 select_select_fusion.7
  129.6 0.2 copy-done.1
  129.9 5.1 %conditional.3 = (f32[448,768]{1,0:T(8,128)S(1)}, f32[448,384]{1,0:T(8,128)S(1)}, f32[448,384]{1,0:T(8,128)S(1)}) conditional(s32[]{:T(128)} %clamp.4, (bf16[456,1536]{1,0:T(8,128)(2,1)}, bf16[448,448]{1,0:T(8,128)(2,1)S(1)}, bf16[448,448]{1,0:T(8,128)(2,1)S(1)}, bf16[448,1536]{1,0:T(8,128)(2,1)S(1)}, ...), branch_computations={%region_6.7_spmd, %region_7.8_spmd, %region_8.9_spmd, %region_9.10... | conditional | flops 1234845696 | bytes 22822936 | solution.py:227
  129.9 2.2 %fusion.17 = f32[448,1536]{1,0:T(8,128)S(1)} fusion(bf16[448,448]{1,0:T(8,128)(2,1)S(1)} %get-tuple-element.104, bf16[456,1536]{1,0:T(8,128)(2,1)} %get-tuple-element.105), kind=kOutput, calls=%fused_computation.25 | convolution fusion | flops 616562688 | bytes 4530176 | tf_op jit(solution)/shard_map/cond/branch_1_fun/dot_general | solution.py:50
  132.1 2.3 %fusion.15 = f32[448,1536]{1,0:T(8,128)S(1)} fusion(f32[448,1536]{1,0:T(8,128)S(1)} %get-tuple-element.103, f32[448,1536]{1,0:T(8,128)S(1)} %fusion.17, bf16[448,448]{1,0:T(8,128)(2,1)S(1)} %get-tuple-element.106, bf16[456,1536]{1,0:T(8,128)(2,1)} %get-tuple-element.107), kind=kOutput, calls=%fused_computation.22 | convolution fusion | flops 617938944 | bytes 10035200 | tf_op jit(solution)/shard_map/cond/branch_1_fun/dot_general | solution.py:50
  134.4 0.2 fusion.39
  134.6 0.1 pad_maximum_fusion.1
  135.0 0.1 collective-permute-start.22
  135.1 3.1 %collective-permute-done.22 = f32[448,768]{1,0:T(8,128)S(1)} collective-permute-done((f32[448,768]{1,0:T(8,128)S(1)}, f32[448,768]{1,0:T(8,128)S(1)}, u32[]{:S(2)}, u32[]{:S(2)}) %collective-permute-start.22) | collective-permute-done | bytes 1376288 | tf_op jit(solution)/shard_map/ppermute | solution.py:26
  138.2 0.1 slice_add_fusion
  138.3 7.1 %collective-permute-start.23 = (f32[448,384]{1,0:T(8,128)S(1)}, f32[448,384]{1,0:T(8,128)S(1)}, u32[]{:S(2)}, u32[]{:S(2)}) collective-permute-start(f32[448,384]{1,0:T(8,128)S(1)} %slice_add_fusion), channel_id=1, source_target_pairs={{0,8},{1,9},{2,10},{3,11},{4,12},{5,13},{6,14},{7,15},{8,0},{9,1},... | collective-permute-start | bytes 2064392 | tf_op jit(solution)/shard_map/ppermute | solution.py:26
  145.4 15.5 %collective-permute-done.23 = f32[448,384]{1,0:T(8,128)S(1)} collective-permute-done((f32[448,384]{1,0:T(8,128)S(1)}, f32[448,384]{1,0:T(8,128)S(1)}, u32[]{:S(2)}, u32[]{:S(2)}) %collective-permute-start.23) | collective-permute-done | bytes 688160 | tf_op jit(solution)/shard_map/ppermute | solution.py:26
  160.9 1.0 fusion.28
  (42 shorter events, 0.7 us)
Async XLA Ops:
  0.0 10.6 %collective-permute-start.1 = (bf16[448,384]{1,0:T(8,128)(2,1)}, bf16[448,384]{1,0:T(8,128)(2,1)S(1)}, u32[]{:S(2)}, u32[]{:S(2)}) collective-permute-start(bf16[448,384]{1,0:T(8,128)(2,1)} %bitcast.177), channel_id=1, source_target_pairs={{0,8},{1,9},{2,10},{3,11},{4,12},{5,13},{6,14},{7,15},{8,0},{9,1},... | collective-permute-start | bytes 1032200 | tf_op jit(solution)/shard_map/ppermute | solution.py:26
  3.6 9.2 %collective-permute-start = (bf16[448,384]{1,0:T(8,128)(2,1)}, bf16[448,384]{1,0:T(8,128)(2,1)S(1)}, u32[]{:S(2)}, u32[]{:S(2)}) collective-permute-start(bf16[448,384]{1,0:T(8,128)(2,1)} %bitcast.178), channel_id=1, source_target_pairs={{0,1},{1,0},{2,3},{3,2},{4,5},{5,4},{6,7},{7,6},{8,9},{9,8},{10,11... | collective-permute-start | bytes 1032200 | tf_op jit(solution)/shard_map/ppermute | solution.py:26
  10.6 3.5 %collective-permute-start.2 = (bf16[448,384]{1,0:T(8,128)(2,1)S(1)}, bf16[448,384]{1,0:T(8,128)(2,1)S(1)}, u32[]{:S(2)}, u32[]{:S(2)}) collective-permute-start(bf16[448,384]{1,0:T(8,128)(2,1)S(1)} %collective-permute-done.1), channel_id=1, source_target_pairs={{0,1},{1,0},{2,3},{3,2},{4,5},{5,4},{6,7},{7,6},{8,9},{9,8},{10,11... | collective-permute-start | bytes 1032200 | tf_op jit(solution)/shard_map/ppermute | solution.py:26
  14.6 1.1 copy-start
  14.6 23.7 %copy-start.2 = (f32[448]{0:T(512)S(1)}, f32[448]{0:T(512)}, u32[]{:S(2)}) copy-start(f32[448]{0:T(512)} %param.13) | copy-start | bytes 5380
  15.7 21.9 %collective-permute-start.3 = (bf16[456,1536]{1,0:T(8,128)(2,1)S(1)}, bf16[456,1536]{1,0:T(8,128)(2,1)}, u32[]{:S(2)}, u32[]{:S(2)}) collective-permute-start(bf16[456,1536]{1,0:T(8,128)(2,1)S(1)} %pad_maximum_fusion.4.mine_ref), channel_id=1, source_target_pairs={{0,224},{1,33},{2,226},{3,35},{4,228},{5,37},{6,230},{7,39},{8,248... | collective-permute-start | bytes 4202504 | tf_op jit(solution)/shard_map/ppermute | solution.py:26
  17.5 20.8 %collective-permute-start.5 = (bf16[456,1536]{1,0:T(8,128)(2,1)S(1)}, bf16[456,1536]{1,0:T(8,128)(2,1)}, u32[]{:S(2)}, u32[]{:S(2)}) collective-permute-start(bf16[456,1536]{1,0:T(8,128)(2,1)S(1)} %pad_maximum_fusion.4.mine_ref), channel_id=1, source_target_pairs={{0,24},{2,26},{4,28},{6,30},{16,8},{18,10},{20,12},{22,14},{32,56}... | collective-permute-start | bytes 4202504 | tf_op jit(solution)/shard_map/ppermute | solution.py:26
  37.5 3.7 %collective-permute-start.4 = (bf16[456,1536]{1,0:T(8,128)(2,1)}, bf16[456,1536]{1,0:T(8,128)(2,1)S(1)}, u32[]{:S(2)}, u32[]{:S(2)}) collective-permute-start(bf16[456,1536]{1,0:T(8,128)(2,1)} %collective-permute-done.3.one_ref), channel_id=1, source_target_pairs={{0,1},{1,0},{2,3},{3,2},{4,5},{5,4},{6,7},{7,6},{8,9},{9,8},{10,11... | collective-permute-start | bytes 4202504 | tf_op jit(solution)/shard_map/ppermute | solution.py:26
  38.2 26.9 %collective-permute-start.7 = (bf16[456,1536]{1,0:T(8,128)(2,1)}, bf16[456,1536]{1,0:T(8,128)(2,1)}, u32[]{:S(2)}, u32[]{:S(2)}) collective-permute-start(bf16[456,1536]{1,0:T(8,128)(2,1)} %collective-permute-done.3.one_ref), channel_id=1, source_target_pairs={{0,224},{1,33},{2,226},{3,35},{4,228},{5,37},{6,230},{7,39},{8,232... | collective-permute-start | bytes 4202504 | tf_op jit(solution)/shard_map/ppermute | solution.py:26
  46.8 30.8 %collective-permute-start.6 = (bf16[456,1536]{1,0:T(8,128)(2,1)S(1)}, bf16[456,1536]{1,0:T(8,128)(2,1)S(1)}, u32[]{:S(2)}, u32[]{:S(2)}) collective-permute-start(bf16[456,1536]{1,0:T(8,128)(2,1)S(1)} %collective-permute-done.4.swap_ref.swap_one_ref), channel_id=1, source_target_pairs={{1,225},{3,227},{5,229},{7,231},{9,233},{11,235},{13,237},{15,239}... | collective-permute-start | bytes 4202504 | tf_op jit(solution)/shard_map/ppermute | solution.py:26
  52.9 28.6 %all-to-all-start = ((f32[4,2,112,448]{3,2,1,0:T(8,128)}), f32[4,2,112,448]{3,2,1,0:T(8,128)}, u32[]{:S(2)}, u32[]{:S(2)}) async-start(f32[4,2,112,448]{3,2,1,0:T(8,128)} %shard_map.37), calls=%async_computation | async-start | bytes 3670016 | tf_op jit(solution)/shard_map/all_to_all | solution.py:136
  58.0 38.4 %collective-permute-start.10 = (bf16[456,1536]{1,0:T(8,128)(2,1)}, bf16[456,1536]{1,0:T(8,128)(2,1)}, u32[]{:S(2)}, u32[]{:S(2)}) collective-permute-start(bf16[456,1536]{1,0:T(8,128)(2,1)} %collective-permute-done.3.one_ref), channel_id=1, source_target_pairs={{1,25},{3,27},{5,29},{7,31},{17,9},{19,11},{21,13},{23,15},{33,57}... | collective-permute-start | bytes 4202504 | tf_op jit(solution)/shard_map/ppermute | solution.py:26
  65.1 24.6 %collective-permute-start.12 = (bf16[456,1536]{1,0:T(8,128)(2,1)}, bf16[456,1536]{1,0:T(8,128)(2,1)}, u32[]{:S(2)}, u32[]{:S(2)}) collective-permute-start(bf16[456,1536]{1,0:T(8,128)(2,1)} %collective-permute-done.7.two_ref), channel_id=1, source_target_pairs={{0,224},{1,33},{2,226},{3,35},{4,228},{5,37},{6,230},{7,39},{8,232... | collective-permute-start | bytes 4202504 | tf_op jit(solution)/shard_map/ppermute | solution.py:26
  65.1 31.4 %collective-permute-start.11 = (bf16[456,1536]{1,0:T(8,128)(2,1)}, bf16[456,1536]{1,0:T(8,128)(2,1)}, u32[]{:S(2)}, u32[]{:S(2)}) collective-permute-start(bf16[456,1536]{1,0:T(8,128)(2,1)} %collective-permute-done.7.two_ref), channel_id=1, source_target_pairs={{1,25},{3,27},{5,29},{7,31},{17,9},{19,11},{21,13},{23,15},{33,57}... | collective-permute-start | bytes 4202504 | tf_op jit(solution)/shard_map/ppermute | solution.py:26
  81.5 14.8 %all-to-all-start.1 = ((f32[4,1,112,448]{3,2,1,0:T(8,128)}), f32[4,1,112,448]{3,2,1,0:T(8,128)S(1)}, u32[]{:S(2)}, u32[]{:S(2)}) async-start(f32[4,1,112,448]{3,2,1,0:T(8,128)} %shard_map.38), calls=%async_computation.1 | async-start | bytes 1835008 | tf_op jit(solution)/shard_map/all_to_all | solution.py:136
  87.7 8.7 %collective-permute-start.9 = (bf16[112,448]{1,0:T(8,128)(2,1)S(1)}, bf16[112,448]{1,0:T(8,128)(2,1)S(1)}, u32[]{:S(2)}, u32[]{:S(2)}) collective-permute-start(bf16[112,448]{1,0:T(8,128)(2,1)S(1)} %get-tuple-element.201), channel_id=1, source_target_pairs={{1,33},{3,35},{5,37},{7,39},{9,57},{11,59},{13,61},{15,63},{17,49}... | collective-permute-start | bytes 301064 | tf_op jit(solution)/shard_map/ppermute | solution.py:26
  89.6 6.9 %collective-permute-start.8 = (bf16[112,448]{1,0:T(8,128)(2,1)S(1)}, bf16[112,448]{1,0:T(8,128)(2,1)S(1)}, u32[]{:S(2)}, u32[]{:S(2)}) collective-permute-start(bf16[112,448]{1,0:T(8,128)(2,1)S(1)} %get-tuple-element.201), channel_id=1, source_target_pairs={{0,33},{1,224},{2,35},{3,226},{4,37},{5,228},{6,39},{7,230},{8,57}... | collective-permute-start | bytes 301064 | tf_op jit(solution)/shard_map/ppermute | solution.py:26
  89.7 39.9 %collective-permute-start.21 = (bf16[456,1536]{1,0:T(8,128)(2,1)}, bf16[456,1536]{1,0:T(8,128)(2,1)}, u32[]{:S(2)}, u32[]{:S(2)}) collective-permute-start(bf16[456,1536]{1,0:T(8,128)(2,1)} %collective-permute-done.12), channel_id=1, source_target_pairs={{1,33},{3,35},{5,37},{7,39},{9,41},{11,43},{13,45},{15,47},{17,49}... | collective-permute-start | bytes 4202504 | tf_op jit(solution)/shard_map/ppermute | solution.py:26
  96.6 10.1 %collective-permute-start.14 = (bf16[112,448]{1,0:T(8,128)(2,1)S(1)}, bf16[112,448]{1,0:T(8,128)(2,1)S(1)}, u32[]{:S(2)}, u32[]{:S(2)}) collective-permute-start(bf16[112,448]{1,0:T(8,128)(2,1)S(1)} %fusion.35), channel_id=1, source_target_pairs={{0,65},{2,67},{4,69},{6,71},{8,89},{10,91},{12,93},{14,95},{16,81}... | collective-permute-start | bytes 301064 | tf_op jit(solution)/shard_map/ppermute | solution.py:26
  98.0 10.4 %collective-permute-start.15 = (bf16[2,112,448]{2,1,0:T(8,128)(2,1)S(1)}, bf16[2,112,448]{2,1,0:T(8,128)(2,1)S(1)}, u32[]{:S(2)}, u32[]{:S(2)}) collective-permute-start(bf16[2,112,448]{2,1,0:T(8,128)(2,1)S(1)} %pad_maximum_fusion.9), channel_id=1, source_target_pairs={{0,2},{1,3},{2,4},{3,5},{4,6},{5,7},{6,0},{7,1},{8,10},{9,11},{10,... | collective-permute-start | bytes 602120 | tf_op jit(solution)/shard_map/ppermute | solution.py:26
  99.5 12.0 %collective-permute-start.16 = (bf16[2,112,448]{2,1,0:T(8,128)(2,1)S(1)}, bf16[2,112,448]{2,1,0:T(8,128)(2,1)S(1)}, u32[]{:S(2)}, u32[]{:S(2)}) collective-permute-start(bf16[2,112,448]{2,1,0:T(8,128)(2,1)S(1)} %pad_maximum_fusion.9), channel_id=1, source_target_pairs={{0,4},{1,5},{2,6},{3,7},{4,0},{5,1},{6,2},{7,3},{8,12},{9,13},{10,... | collective-permute-start | bytes 602120 | tf_op jit(solution)/shard_map/ppermute | solution.py:26
  101.9 9.6 %collective-permute-start.17 = (bf16[2,112,448]{2,1,0:T(8,128)(2,1)S(1)}, bf16[2,112,448]{2,1,0:T(8,128)(2,1)S(1)}, u32[]{:S(2)}, u32[]{:S(2)}) collective-permute-start(bf16[2,112,448]{2,1,0:T(8,128)(2,1)S(1)} %pad_maximum_fusion.9), channel_id=1, source_target_pairs={{0,6},{1,7},{2,0},{3,1},{4,2},{5,3},{6,4},{7,5},{8,14},{9,15},{10,... | collective-permute-start | bytes 602120 | tf_op jit(solution)/shard_map/ppermute | solution.py:26
  106.7 6.1 %collective-permute-start.13 = (bf16[112,448]{1,0:T(8,128)(2,1)S(1)}, bf16[112,448]{1,0:T(8,128)(2,1)S(1)}, u32[]{:S(2)}, u32[]{:S(2)}) collective-permute-start(bf16[112,448]{1,0:T(8,128)(2,1)S(1)} %fusion.35), channel_id=1, source_target_pairs={{0,224},{1,193},{2,226},{3,195},{4,228},{5,197},{6,230},{7,199},{8... | collective-permute-start | bytes 301064 | tf_op jit(solution)/shard_map/ppermute | solution.py:26
  113.5 8.8 %collective-permute-start.18 = (bf16[2,112,448]{2,1,0:T(8,128)(2,1)}, bf16[2,112,448]{2,1,0:T(8,128)(2,1)}, u32[]{:S(2)}, u32[]{:S(2)}) collective-permute-start(bf16[2,112,448]{2,1,0:T(8,128)(2,1)} %pad_maximum_fusion.10), channel_id=1, source_target_pairs={{0,2},{1,3},{2,4},{3,5},{4,6},{5,7},{6,0},{7,1},{8,10},{9,11},{10,... | collective-permute-start | bytes 602120 | tf_op jit(solution)/shard_map/ppermute | solution.py:26
  114.1 13.1 %collective-permute-start.19 = (bf16[2,112,448]{2,1,0:T(8,128)(2,1)}, bf16[2,112,448]{2,1,0:T(8,128)(2,1)}, u32[]{:S(2)}, u32[]{:S(2)}) collective-permute-start(bf16[2,112,448]{2,1,0:T(8,128)(2,1)} %pad_maximum_fusion.10), channel_id=1, source_target_pairs={{0,4},{1,5},{2,6},{3,7},{4,0},{5,1},{6,2},{7,3},{8,12},{9,13},{10,... | collective-permute-start | bytes 602120 | tf_op jit(solution)/shard_map/ppermute | solution.py:26
  116.9 10.4 %collective-permute-start.20 = (bf16[2,112,448]{2,1,0:T(8,128)(2,1)}, bf16[2,112,448]{2,1,0:T(8,128)(2,1)}, u32[]{:S(2)}, u32[]{:S(2)}) collective-permute-start(bf16[2,112,448]{2,1,0:T(8,128)(2,1)} %pad_maximum_fusion.10), channel_id=1, source_target_pairs={{0,6},{1,7},{2,0},{3,1},{4,2},{5,3},{6,4},{7,5},{8,14},{9,15},{10,... | collective-permute-start | bytes 602120 | tf_op jit(solution)/shard_map/ppermute | solution.py:26
  128.3 1.5 copy-start.1
  135.0 3.2 %collective-permute-start.22 = (f32[448,768]{1,0:T(8,128)S(1)}, f32[448,768]{1,0:T(8,128)S(1)}, u32[]{:S(2)}, u32[]{:S(2)}) collective-permute-start(f32[448,768]{1,0:T(8,128)S(1)} %get-tuple-element.160), channel_id=1, source_target_pairs={{0,1},{1,0},{2,3},{3,2},{4,5},{5,4},{6,7},{7,6},{8,9},{9,8},{10,11... | collective-permute-start | bytes 4128776 | tf_op jit(solution)/shard_map/ppermute | solution.py:26
  138.3 22.6 %collective-permute-start.23 = (f32[448,384]{1,0:T(8,128)S(1)}, f32[448,384]{1,0:T(8,128)S(1)}, u32[]{:S(2)}, u32[]{:S(2)}) collective-permute-start(f32[448,384]{1,0:T(8,128)S(1)} %slice_add_fusion), channel_id=1, source_target_pairs={{0,8},{1,9},{2,10},{3,11},{4,12},{5,13},{6,14},{7,15},{8,0},{9,1},... | collective-permute-start | bytes 2064392 | tf_op jit(solution)/shard_map/ppermute | solution.py:26

commit v19 on v18

--- a/solution.py
+++ b/solution.py
@@ -188,7 +188,6 @@
         (late, first, second, amps_zero, turned_one, turned_two, step_three)
     )
 
-    first, second = by_hops(first, second)
 
     amps_two = amps(late[0], jnp.where(c == 0, swap_energy, energy(swap_two)), energy(step_two))
     third = moved(
@@ -198,7 +197,7 @@
     fourth = moved(amps_two, lambda z, xl, xh, y, c: (z + 2, kind(xl, xh), xh, y, 1) if c == 0 else None)
     fourth = jnp.where(c == 0, amps_zero, fourth)
     third, fourth, first, second, turned_two = lax.optimization_barrier((third, fourth, first, second, turned_two))
-    third, fourth = by_hops(third, fourth)
+    first, second, third, fourth = by_hops(first, second, third, fourth)
 
     def product(dot, *blocks):
         return lambda parts: sum(dot(part, block[:nvir]) for part, block in zip(parts, blocks))

time: 163 us -> 169 us (1.037)
  waiting for transfers between devices: 68.5 us -> 75.9 us
  starting transfers between devices: 58 us -> 56.3 us
    ppermute x24 -> x21, waiting for transfers between devices: 68.5 us -> 75.2 us  [moved(): return lax.ppermute(array, ALL, pairs)]
    ppermute x24 -> x21, starting transfers between devices: 49.4 us -> 47.8 us  [moved(): return lax.ppermute(array, ALL, pairs)]
  transfers between devices with their start and end apart: 26 -> 23, of which waited for: 11 -> 11; matrix products, arithmetic and copies ran while one was open for 9% -> 8% of each run, Pallas kernels for 6% -> 6%
where the time goes in v19:
time: 169 us; the launch traced here: 168 us
  waiting for transfers between devices  75.9 us (45%)
  starting transfers between devices  56.3 us (33%)
  other arithmetic  11.2 us (7%)
  Pallas kernels  9.44 us (6%)
  matrix products  9.1 us (5%)
  between operations  3.39 us (2%)
  local copies, waits for them, and re-layouts  2.14 us (1%)
    ppermute x21, waiting for transfers between devices, moved(): return lax.ppermute(array, ALL, pairs)  75.2 us
    ppermute x21, starting transfers between devices, moved(): return lax.ppermute(array, ALL, pairs)  47.8 us
    pallas_call x2, Pallas kernels, numerators(): pl.pallas_call(kernel, out_shape=jax.ShapeDtypeStruct((NY, count, share,...  9.44 us
    dot_general x4, matrix products, dot_tn(): lax.dot_general(a, b, (((0,), (0,)), ((), ())), preferred_element_type=jn...  9.1 us
    all_to_all x2, starting transfers between devices, exchanged(): return lax.all_to_all(parts, 'y', 0, 0, tiled=True)  8.56 us
  transfers between devices with their start and end apart: 23, of which 11 were waited for; matrix products, arithmetic and copies ran while one was open for 8% of the time, Pallas kernels for 6%

profile of v19, /device:TPU:1, one launch (start us, length us, event | category | flops | bytes accessed | tf_op | source)
XLA Modules:
  0.0 167.7 jit_solution(14579905951413668191)
XLA Ops:
  0.0 3.6 %collective-permute-start.1 = (bf16[448,384]{1,0:T(8,128)(2,1)}, bf16[448,384]{1,0:T(8,128)(2,1)S(1)}, u32[]{:S(2)}, u32[]{:S(2)}) collective-permute-start(bf16[448,384]{1,0:T(8,128)(2,1)} %bitcast.177), channel_id=1, source_target_pairs={{0,8},{1,9},{2,10},{3,11},{4,12},{5,13},{6,14},{7,15},{8,0},{9,1},... | collective-permute-start | bytes 1032200 | tf_op jit(solution)/shard_map/ppermute | solution.py:26
  3.6 1.0 collective-permute-start
  7.6 1.4 select_convert_fusion
  9.0 1.6 collective-permute-done.1
  10.6 2.2 %collective-permute-start.2 = (bf16[448,384]{1,0:T(8,128)(2,1)S(1)}, bf16[448,384]{1,0:T(8,128)(2,1)S(1)}, u32[]{:S(2)}, u32[]{:S(2)}) collective-permute-start(bf16[448,384]{1,0:T(8,128)(2,1)S(1)} %collective-permute-done.1), channel_id=1, source_target_pairs={{0,1},{1,0},{2,3},{3,2},{4,5},{5,4},{6,7},{7,6},{8,9},{9,8},{10,11... | collective-permute-start | bytes 1032200 | tf_op jit(solution)/shard_map/ppermute | solution.py:26
  12.8 1.2 maximum_select_fusion.1
  14.1 0.2 maximum_select_fusion.2
  14.2 0.3 maximum_select_fusion
  14.6 0.1 pad_maximum_fusion.4.mine_ref
  14.7 1.0 copy-done
  15.7 1.9 %collective-permute-start.3 = (bf16[456,1536]{1,0:T(8,128)(2,1)S(1)}, bf16[456,1536]{1,0:T(8,128)(2,1)}, u32[]{:S(2)}, u32[]{:S(2)}) collective-permute-start(bf16[456,1536]{1,0:T(8,128)(2,1)S(1)} %pad_maximum_fusion.4.mine_ref), channel_id=1, source_target_pairs={{0,224},{1,33},{2,226},{3,35},{4,228},{5,37},{6,230},{7,39},{8,248... | collective-permute-start | bytes 4202504 | tf_op jit(solution)/shard_map/ppermute | solution.py:26
  17.6 1.8 %collective-permute-start.5 = (bf16[456,1536]{1,0:T(8,128)(2,1)S(1)}, bf16[456,1536]{1,0:T(8,128)(2,1)}, u32[]{:S(2)}, u32[]{:S(2)}) collective-permute-start(bf16[456,1536]{1,0:T(8,128)(2,1)S(1)} %pad_maximum_fusion.4.mine_ref), channel_id=1, source_target_pairs={{0,24},{2,26},{4,28},{6,30},{16,8},{18,10},{20,12},{22,14},{32,56}... | collective-permute-start | bytes 4202504 | tf_op jit(solution)/shard_map/ppermute | solution.py:26
  19.4 18.2 %collective-permute-done.3.one_ref = bf16[456,1536]{1,0:T(8,128)(2,1)} collective-permute-done((bf16[456,1536]{1,0:T(8,128)(2,1)S(1)}, bf16[456,1536]{1,0:T(8,128)(2,1)}, u32[]{:S(2)}, u32[]{:S(2)}) %collective-permute-start.3) | collective-permute-done | bytes 1400864 | tf_op jit(solution)/shard_map/ppermute | solution.py:26
  37.6 0.7 collective-permute-start.4
  38.2 0.1 pad_add_fusion.where_ref
  38.3 0.1 dynamic_slice.3
  38.4 2.8 %collective-permute-done.4.swap_ref.swap_one_ref = bf16[456,1536]{1,0:T(8,128)(2,1)S(1)} collective-permute-done((bf16[456,1536]{1,0:T(8,128)(2,1)}, bf16[456,1536]{1,0:T(8,128)(2,1)S(1)}, u32[]{:S(2)}, u32[]{:S(2)}) %collective-permute-start.4) | collective-permute-done | bytes 1400864 | tf_op jit(solution)/shard_map/ppermute | solution.py:26
  41.2 5.5 %shard_map.37 = f32[4,2,112,448]{3,2,1,0:T(8,128)} custom-call(s32[2]{0:T(128)S(1)} %pad_add_fusion.where_ref, bf16[456,1536]{1,0:T(8,128)(2,1)S(1)} %pad_maximum_fusion.4.mine_ref, bf16[456,1536]{1,0:T(8,128)(2,1)} %collective-permute-done.3.one_ref, bf16[456,1536]{1,0:T(8,128)(2,1)S(1)} %collective-permute-done.4.swap_ref.swap_one_ref, ...), custom_call_target="tpu_custom_call" | custom-call | flops 2466250752 | bytes 7110656 | tf_op jit(solution)/shard_map/pallas_call | solution.py:91
  46.8 5.4 %collective-permute-start.6 = (bf16[456,1536]{1,0:T(8,128)(2,1)S(1)}, bf16[456,1536]{1,0:T(8,128)(2,1)S(1)}, u32[]{:S(2)}, u32[]{:S(2)}) collective-permute-start(bf16[456,1536]{1,0:T(8,128)(2,1)S(1)} %collective-permute-done.4.swap_ref.swap_one_ref), channel_id=1, source_target_pairs={{1,225},{3,227},{5,229},{7,231},{9,233},{11,235},{13,237},{15,239}... | collective-permute-start | bytes 4202504 | tf_op jit(solution)/shard_map/ppermute | solution.py:26
  52.2 0.7 slice_convert_fusion.2
  52.9 4.4 %all-to-all-start = ((f32[4,2,112,448]{3,2,1,0:T(8,128)}), f32[4,2,112,448]{3,2,1,0:T(8,128)}, u32[]{:S(2)}, u32[]{:S(2)}) async-start(f32[4,2,112,448]{3,2,1,0:T(8,128)} %shard_map.37), calls=%async_computation | async-start | bytes 3670016 | tf_op jit(solution)/shard_map/all_to_all | solution.py:136
  57.3 0.7 slice_convert_fusion.3
  58.0 7.1 %collective-permute-start.10 = (bf16[456,1536]{1,0:T(8,128)(2,1)}, bf16[456,1536]{1,0:T(8,128)(2,1)}, u32[]{:S(2)}, u32[]{:S(2)}) collective-permute-start(bf16[456,1536]{1,0:T(8,128)(2,1)} %collective-permute-done.3.one_ref), channel_id=1, source_target_pairs={{1,25},{3,27},{5,29},{7,31},{17,9},{19,11},{21,13},{23,15},{33,57}... | collective-permute-start | bytes 4202504 | tf_op jit(solution)/shard_map/ppermute | solution.py:26
  65.1 2.4 %collective-permute-start.11 = (bf16[456,1536]{1,0:T(8,128)(2,1)}, bf16[456,1536]{1,0:T(8,128)(2,1)}, u32[]{:S(2)}, u32[]{:S(2)}) collective-permute-start(bf16[456,1536]{1,0:T(8,128)(2,1)} %collective-permute-done.7.two_ref), channel_id=1, source_target_pairs={{1,25},{3,27},{5,29},{7,31},{17,9},{19,11},{21,13},{23,15},{33,57}... | collective-permute-start | bytes 4202504 | tf_op jit(solution)/shard_map/ppermute | solution.py:26
  67.5 0.7 slice_convert_fusion
  68.3 7.6 %collective-permute-done.6.swap_two_ref = bf16[456,1536]{1,0:T(8,128)(2,1)S(1)} collective-permute-done((bf16[456,1536]{1,0:T(8,128)(2,1)S(1)}, bf16[456,1536]{1,0:T(8,128)(2,1)S(1)}, u32[]{:S(2)}, u32[]{:S(2)}) %collective-permute-start.6) | collective-permute-done | bytes 1400864 | tf_op jit(solution)/shard_map/ppermute | solution.py:26
  75.8 3.9 %shard_map.38 = f32[4,1,112,448]{3,2,1,0:T(8,128)} custom-call(s32[2]{0:T(128)S(1)} %pad_add_fusion.where_ref, bf16[456,1536]{1,0:T(8,128)(2,1)S(1)} %collective-permute-done.4.swap_ref.swap_one_ref, bf16[456,1536]{1,0:T(8,128)(2,1)S(1)} %collective-permute-done.6.swap_two_ref, bf16[456,1536]{1,0:T(8,128)(2,1)} %collective-permute-done.7.two_ref), custom_call_target="tpu_custom_call" | custom-call | flops 1233125376 | bytes 4931584 | tf_op jit(solution)/shard_map/pallas_call | solution.py:91
  79.7 4.2 %all-to-all-start.1 = ((f32[4,1,112,448]{3,2,1,0:T(8,128)}), f32[4,1,112,448]{3,2,1,0:T(8,128)S(1)}, u32[]{:S(2)}, u32[]{:S(2)}) async-start(f32[4,1,112,448]{3,2,1,0:T(8,128)} %shard_map.38), calls=%async_computation.1 | async-start | bytes 1835008 | tf_op jit(solution)/shard_map/all_to_all | solution.py:136
  83.9 1.8 %reduce_sum.22 = f32[2,112,448]{2,1,0:T(8,128)S(1)} reduce(f32[4,2,112,448]{3,2,1,0:T(8,128)} %all-to-all-done, f32[]{:T(128)} %constant.6.clone.1), dimensions={0}, to_apply=%region_1.2 | reduce | flops 301056 | bytes 2007044 | tf_op jit(solution)/shard_map/reduce_sum | solution.py:171
  85.7 0.1 fusion.36
  85.9 1.9 %collective-permute-start.9 = (bf16[112,448]{1,0:T(8,128)(2,1)S(1)}, bf16[112,448]{1,0:T(8,128)(2,1)S(1)}, u32[]{:S(2)}, u32[]{:S(2)}) collective-permute-start(bf16[112,448]{1,0:T(8,128)(2,1)S(1)} %get-tuple-element.201), channel_id=1, source_target_pairs={{1,33},{3,35},{5,37},{7,39},{9,57},{11,59},{13,61},{15,63},{17,49}... | collective-permute-start | bytes 301064 | tf_op jit(solution)/shard_map/ppermute | solution.py:26
  87.8 0.1 collective-permute-start.8
  87.9 6.6 %collective-permute-done.9 = bf16[112,448]{1,0:T(8,128)(2,1)S(1)} collective-permute-done((bf16[112,448]{1,0:T(8,128)(2,1)S(1)}, bf16[112,448]{1,0:T(8,128)(2,1)S(1)}, u32[]{:S(2)}, u32[]{:S(2)}) %collective-permute-start.9) | collective-permute-done | bytes 100384 | tf_op jit(solution)/shard_map/ppermute | solution.py:26
  94.6 0.7 all-to-all-done.1
  95.3 0.1 reduce_sum.20
  95.4 0.1 fusion.35
  95.5 1.3 collective-permute-start.14
  96.8 2.6 %collective-permute-start.13 = (bf16[112,448]{1,0:T(8,128)(2,1)S(1)}, bf16[112,448]{1,0:T(8,128)(2,1)S(1)}, u32[]{:S(2)}, u32[]{:S(2)}) collective-permute-start(bf16[112,448]{1,0:T(8,128)(2,1)S(1)} %fusion.35), channel_id=1, source_target_pairs={{0,224},{1,193},{2,226},{3,195},{4,228},{5,197},{6,230},{7,199},{8... | collective-permute-start | bytes 301064 | tf_op jit(solution)/shard_map/ppermute | solution.py:26
  99.5 4.3 %collective-permute-done.14 = bf16[112,448]{1,0:T(8,128)(2,1)S(1)} collective-permute-done((bf16[112,448]{1,0:T(8,128)(2,1)S(1)}, bf16[112,448]{1,0:T(8,128)(2,1)S(1)}, u32[]{:S(2)}, u32[]{:S(2)}) %collective-permute-start.14) | collective-permute-done | bytes 100384 | tf_op jit(solution)/shard_map/ppermute | solution.py:26
  103.8 0.1 pad_maximum_fusion.5
  103.9 0.9 collective-permute-start.15
  104.8 2.8 %collective-permute-start.16 = (bf16[4,112,448]{2,1,0:T(8,128)(2,1)S(1)}, bf16[4,112,448]{2,1,0:T(8,128)(2,1)S(1)}, u32[]{:S(2)}, u32[]{:S(2)}) collective-permute-start(bf16[4,112,448]{2,1,0:T(8,128)(2,1)S(1)} %pad_maximum_fusion.5), channel_id=1, source_target_pairs={{0,4},{1,5},{2,6},{3,7},{4,0},{5,1},{6,2},{7,3},{8,12},{9,13},{10,... | collective-permute-start | bytes 1204232 | tf_op jit(solution)/shard_map/ppermute | solution.py:26
  107.6 2.0 %collective-permute-start.17 = (bf16[4,112,448]{2,1,0:T(8,128)(2,1)S(1)}, bf16[4,112,448]{2,1,0:T(8,128)(2,1)S(1)}, u32[]{:S(2)}, u32[]{:S(2)}) collective-permute-start(bf16[4,112,448]{2,1,0:T(8,128)(2,1)S(1)} %pad_maximum_fusion.5), channel_id=1, source_target_pairs={{0,6},{1,7},{2,0},{3,1},{4,2},{5,3},{6,4},{7,5},{8,14},{9,15},{10,... | collective-permute-start | bytes 1204232 | tf_op jit(solution)/shard_map/ppermute | solution.py:26
  109.6 1.9 %collective-permute-start.18 = (bf16[456,1536]{1,0:T(8,128)(2,1)}, bf16[456,1536]{1,0:T(8,128)(2,1)}, u32[]{:S(2)}, u32[]{:S(2)}) collective-permute-start(bf16[456,1536]{1,0:T(8,128)(2,1)} %collective-permute-done.12), channel_id=1, source_target_pairs={{1,33},{3,35},{5,37},{7,39},{9,41},{11,43},{13,45},{15,47},{17,49}... | collective-permute-start | bytes 4202504 | tf_op jit(solution)/shard_map/ppermute | solution.py:26
  111.5 4.9 %collective-permute-done.15 = bf16[4,112,448]{2,1,0:T(8,128)(2,1)S(1)} collective-permute-done((bf16[4,112,448]{2,1,0:T(8,128)(2,1)S(1)}, bf16[4,112,448]{2,1,0:T(8,128)(2,1)S(1)}, u32[]{:S(2)}, u32[]{:S(2)}) %collective-permute-start.15) | collective-permute-done | bytes 401440 | tf_op jit(solution)/shard_map/ppermute | solution.py:26
  116.4 10.7 %collective-permute-done.16 = bf16[4,112,448]{2,1,0:T(8,128)(2,1)S(1)} collective-permute-done((bf16[4,112,448]{2,1,0:T(8,128)(2,1)S(1)}, bf16[4,112,448]{2,1,0:T(8,128)(2,1)S(1)}, u32[]{:S(2)}, u32[]{:S(2)}) %collective-permute-start.16) | collective-permute-done | bytes 401440 | tf_op jit(solution)/shard_map/ppermute | solution.py:26
  127.3 0.5 copy-done.2
  127.8 0.1 copy-done.3
  128.0 4.5 %conditional.2 = (f32[448,1536]{1,0:T(8,128)S(1)}) conditional(s32[]{:T(128)} %clamp.4, (bf16[456,1536]{1,0:T(8,128)(2,1)}, bf16[448,448]{1,0:T(8,128)(2,1)S(1)}, bf16[456,1536]{1,0:T(8,128)(2,1)}, bf16[448,448]{1,0:T(8,128)(2,1)S(1)}) %tuple.43, (bf16[456,1536]{1,0:T(8,128)(2,1)}, bf16[448,448]{1,0:T(8,128)(2,1)S(1)}, ...), branch_computations={%region_2.3_spmd, %region_3.4_spmd, %region_4.5_spmd, %region_5.6_... | conditional | flops 1233813504 | bytes 11812872 | solution.py:206
  128.0 2.2 %fusion.4 = f32[448,1536]{1,0:T(8,128)S(1)} fusion(bf16[448,448]{1,0:T(8,128)(2,1)S(1)} %get-tuple-element.86, bf16[456,1536]{1,0:T(8,128)(2,1)} %get-tuple-element.87), kind=kOutput, calls=%fused_computation.6 | convolution fusion | flops 616562688 | bytes 4530176 | tf_op jit(solution)/shard_map/cond/branch_1_fun/dot_general | solution.py:50
  130.2 2.3 %convolution_add_fusion.1 = f32[448,1536]{1,0:T(8,128)S(1)} fusion(f32[448,1536]{1,0:T(8,128)S(1)} %fusion.4, bf16[448,448]{1,0:T(8,128)(2,1)S(1)} %get-tuple-element.88, bf16[456,1536]{1,0:T(8,128)(2,1)} %get-tuple-element.89), kind=kOutput, calls=%fused_computation.4 | convolution fusion | flops 617250816 | bytes 7282688 | tf_op jit(solution)/shard_map/cond/branch_1_fun/dot_general | solution.py:50
  132.5 1.0 select_select_fusion.15
  133.6 1.1 select_select_fusion.11
  134.8 0.2 copy-done.1
  135.0 5.1 %conditional.3 = (f32[448,768]{1,0:T(8,128)S(1)}, f32[448,384]{1,0:T(8,128)S(1)}, f32[448,384]{1,0:T(8,128)S(1)}) conditional(s32[]{:T(128)} %clamp.4, (bf16[456,1536]{1,0:T(8,128)(2,1)}, bf16[448,448]{1,0:T(8,128)(2,1)S(1)}, bf16[448,448]{1,0:T(8,128)(2,1)S(1)}, bf16[448,1536]{1,0:T(8,128)(2,1)S(1)}, ...), branch_computations={%region_6.7_spmd, %region_7.8_spmd, %region_8.9_spmd, %region_9.10... | conditional | flops 1234845696 | bytes 22822936 | solution.py:226
  135.0 2.2 %fusion.17 = f32[448,1536]{1,0:T(8,128)S(1)} fusion(bf16[448,448]{1,0:T(8,128)(2,1)S(1)} %get-tuple-element.104, bf16[456,1536]{1,0:T(8,128)(2,1)} %get-tuple-element.105), kind=kOutput, calls=%fused_computation.25 | convolution fusion | flops 616562688 | bytes 4530176 | tf_op jit(solution)/shard_map/cond/branch_1_fun/dot_general | solution.py:50
  137.2 2.3 %fusion.15 = f32[448,1536]{1,0:T(8,128)S(1)} fusion(f32[448,1536]{1,0:T(8,128)S(1)} %get-tuple-element.103, f32[448,1536]{1,0:T(8,128)S(1)} %fusion.17, bf16[448,448]{1,0:T(8,128)(2,1)S(1)} %get-tuple-element.106, bf16[456,1536]{1,0:T(8,128)(2,1)} %get-tuple-element.107), kind=kOutput, calls=%fused_computation.22 | convolution fusion | flops 617938944 | bytes 10035200 | tf_op jit(solution)/shard_map/cond/branch_1_fun/dot_general | solution.py:50
  139.6 0.2 fusion.39
  139.8 0.1 pad_maximum_fusion.1
  140.1 0.4 collective-permute-start.19
  140.5 2.9 %collective-permute-done.19 = f32[448,768]{1,0:T(8,128)S(1)} collective-permute-done((f32[448,768]{1,0:T(8,128)S(1)}, f32[448,768]{1,0:T(8,128)S(1)}, u32[]{:S(2)}, u32[]{:S(2)}) %collective-permute-start.19) | collective-permute-done | bytes 1376288 | tf_op jit(solution)/shard_map/ppermute | solution.py:26
  143.4 7.9 %collective-permute-start.20 = (f32[448,384]{1,0:T(8,128)S(1)}, f32[448,384]{1,0:T(8,128)S(1)}, u32[]{:S(2)}, u32[]{:S(2)}) collective-permute-start(f32[448,384]{1,0:T(8,128)S(1)} %slice_add_fusion), channel_id=1, source_target_pairs={{0,8},{1,9},{2,10},{3,11},{4,12},{5,13},{6,14},{7,15},{8,0},{9,1},... | collective-permute-start | bytes 2064392 | tf_op jit(solution)/shard_map/ppermute | solution.py:26
  151.3 15.5 %collective-permute-done.20 = f32[448,384]{1,0:T(8,128)S(1)} collective-permute-done((f32[448,384]{1,0:T(8,128)S(1)}, f32[448,384]{1,0:T(8,128)S(1)}, u32[]{:S(2)}, u32[]{:S(2)}) %collective-permute-start.20) | collective-permute-done | bytes 688160 | tf_op jit(solution)/shard_map/ppermute | solution.py:26
  166.8 0.9 fusion.28
  (39 shorter events, 0.6 us)
Async XLA Ops:
  0.0 10.6 %collective-permute-start.1 = (bf16[448,384]{1,0:T(8,128)(2,1)}, bf16[448,384]{1,0:T(8,128)(2,1)S(1)}, u32[]{:S(2)}, u32[]{:S(2)}) collective-permute-start(bf16[448,384]{1,0:T(8,128)(2,1)} %bitcast.177), channel_id=1, source_target_pairs={{0,8},{1,9},{2,10},{3,11},{4,12},{5,13},{6,14},{7,15},{8,0},{9,1},... | collective-permute-start | bytes 1032200 | tf_op jit(solution)/shard_map/ppermute | solution.py:26
  3.6 9.2 %collective-permute-start = (bf16[448,384]{1,0:T(8,128)(2,1)}, bf16[448,384]{1,0:T(8,128)(2,1)S(1)}, u32[]{:S(2)}, u32[]{:S(2)}) collective-permute-start(bf16[448,384]{1,0:T(8,128)(2,1)} %bitcast.178), channel_id=1, source_target_pairs={{0,1},{1,0},{2,3},{3,2},{4,5},{5,4},{6,7},{7,6},{8,9},{9,8},{10,11... | collective-permute-start | bytes 1032200 | tf_op jit(solution)/shard_map/ppermute | solution.py:26
  10.6 3.5 %collective-permute-start.2 = (bf16[448,384]{1,0:T(8,128)(2,1)S(1)}, bf16[448,384]{1,0:T(8,128)(2,1)S(1)}, u32[]{:S(2)}, u32[]{:S(2)}) collective-permute-start(bf16[448,384]{1,0:T(8,128)(2,1)S(1)} %collective-permute-done.1), channel_id=1, source_target_pairs={{0,1},{1,0},{2,3},{3,2},{4,5},{5,4},{6,7},{7,6},{8,9},{9,8},{10,11... | collective-permute-start | bytes 1032200 | tf_op jit(solution)/shard_map/ppermute | solution.py:26
  14.6 1.1 copy-start
  14.6 23.7 %copy-start.4 = (f32[448]{0:T(512)S(1)}, f32[448]{0:T(512)}, u32[]{:S(2)}) copy-start(f32[448]{0:T(512)} %param.13) | copy-start | bytes 5380
  15.7 21.9 %collective-permute-start.3 = (bf16[456,1536]{1,0:T(8,128)(2,1)S(1)}, bf16[456,1536]{1,0:T(8,128)(2,1)}, u32[]{:S(2)}, u32[]{:S(2)}) collective-permute-start(bf16[456,1536]{1,0:T(8,128)(2,1)S(1)} %pad_maximum_fusion.4.mine_ref), channel_id=1, source_target_pairs={{0,224},{1,33},{2,226},{3,35},{4,228},{5,37},{6,230},{7,39},{8,248... | collective-permute-start | bytes 4202504 | tf_op jit(solution)/shard_map/ppermute | solution.py:26
  17.6 20.8 %collective-permute-start.5 = (bf16[456,1536]{1,0:T(8,128)(2,1)S(1)}, bf16[456,1536]{1,0:T(8,128)(2,1)}, u32[]{:S(2)}, u32[]{:S(2)}) collective-permute-start(bf16[456,1536]{1,0:T(8,128)(2,1)S(1)} %pad_maximum_fusion.4.mine_ref), channel_id=1, source_target_pairs={{0,24},{2,26},{4,28},{6,30},{16,8},{18,10},{20,12},{22,14},{32,56}... | collective-permute-start | bytes 4202504 | tf_op jit(solution)/shard_map/ppermute | solution.py:26
  37.6 3.7 %collective-permute-start.4 = (bf16[456,1536]{1,0:T(8,128)(2,1)}, bf16[456,1536]{1,0:T(8,128)(2,1)S(1)}, u32[]{:S(2)}, u32[]{:S(2)}) collective-permute-start(bf16[456,1536]{1,0:T(8,128)(2,1)} %collective-permute-done.3.one_ref), channel_id=1, source_target_pairs={{0,1},{1,0},{2,3},{3,2},{4,5},{5,4},{6,7},{7,6},{8,9},{9,8},{10,11... | collective-permute-start | bytes 4202504 | tf_op jit(solution)/shard_map/ppermute | solution.py:26
  38.2 26.9 %collective-permute-start.7 = (bf16[456,1536]{1,0:T(8,128)(2,1)}, bf16[456,1536]{1,0:T(8,128)(2,1)}, u32[]{:S(2)}, u32[]{:S(2)}) collective-permute-start(bf16[456,1536]{1,0:T(8,128)(2,1)} %collective-permute-done.3.one_ref), channel_id=1, source_target_pairs={{0,224},{1,33},{2,226},{3,35},{4,228},{5,37},{6,230},{7,39},{8,232... | collective-permute-start | bytes 4202504 | tf_op jit(solution)/shard_map/ppermute | solution.py:26
  46.8 29.1 %collective-permute-start.6 = (bf16[456,1536]{1,0:T(8,128)(2,1)S(1)}, bf16[456,1536]{1,0:T(8,128)(2,1)S(1)}, u32[]{:S(2)}, u32[]{:S(2)}) collective-permute-start(bf16[456,1536]{1,0:T(8,128)(2,1)S(1)} %collective-permute-done.4.swap_ref.swap_one_ref), channel_id=1, source_target_pairs={{1,225},{3,227},{5,229},{7,231},{9,233},{11,235},{13,237},{15,239}... | collective-permute-start | bytes 4202504 | tf_op jit(solution)/shard_map/ppermute | solution.py:26
  52.9 26.8 %all-to-all-start = ((f32[4,2,112,448]{3,2,1,0:T(8,128)}), f32[4,2,112,448]{3,2,1,0:T(8,128)}, u32[]{:S(2)}, u32[]{:S(2)}) async-start(f32[4,2,112,448]{3,2,1,0:T(8,128)} %shard_map.37), calls=%async_computation | async-start | bytes 3670016 | tf_op jit(solution)/shard_map/all_to_all | solution.py:136
  58.0 37.4 %collective-permute-start.10 = (bf16[456,1536]{1,0:T(8,128)(2,1)}, bf16[456,1536]{1,0:T(8,128)(2,1)}, u32[]{:S(2)}, u32[]{:S(2)}) collective-permute-start(bf16[456,1536]{1,0:T(8,128)(2,1)} %collective-permute-done.3.one_ref), channel_id=1, source_target_pairs={{1,25},{3,27},{5,29},{7,31},{17,9},{19,11},{21,13},{23,15},{33,57}... | collective-permute-start | bytes 4202504 | tf_op jit(solution)/shard_map/ppermute | solution.py:26
  65.1 30.3 %collective-permute-start.11 = (bf16[456,1536]{1,0:T(8,128)(2,1)}, bf16[456,1536]{1,0:T(8,128)(2,1)}, u32[]{:S(2)}, u32[]{:S(2)}) collective-permute-start(bf16[456,1536]{1,0:T(8,128)(2,1)} %collective-permute-done.7.two_ref), channel_id=1, source_target_pairs={{1,25},{3,27},{5,29},{7,31},{17,9},{19,11},{21,13},{23,15},{33,57}... | collective-permute-start | bytes 4202504 | tf_op jit(solution)/shard_map/ppermute | solution.py:26
  67.5 27.9 %collective-permute-start.12 = (bf16[456,1536]{1,0:T(8,128)(2,1)}, bf16[456,1536]{1,0:T(8,128)(2,1)}, u32[]{:S(2)}, u32[]{:S(2)}) collective-permute-start(bf16[456,1536]{1,0:T(8,128)(2,1)} %collective-permute-done.7.two_ref), channel_id=1, source_target_pairs={{0,224},{1,33},{2,226},{3,35},{4,228},{5,37},{6,230},{7,39},{8,232... | collective-permute-start | bytes 4202504 | tf_op jit(solution)/shard_map/ppermute | solution.py:26
  79.7 15.5 %all-to-all-start.1 = ((f32[4,1,112,448]{3,2,1,0:T(8,128)}), f32[4,1,112,448]{3,2,1,0:T(8,128)S(1)}, u32[]{:S(2)}, u32[]{:S(2)}) async-start(f32[4,1,112,448]{3,2,1,0:T(8,128)} %shard_map.38), calls=%async_computation.1 | async-start | bytes 1835008 | tf_op jit(solution)/shard_map/all_to_all | solution.py:136
  85.9 8.7 %collective-permute-start.9 = (bf16[112,448]{1,0:T(8,128)(2,1)S(1)}, bf16[112,448]{1,0:T(8,128)(2,1)S(1)}, u32[]{:S(2)}, u32[]{:S(2)}) collective-permute-start(bf16[112,448]{1,0:T(8,128)(2,1)S(1)} %get-tuple-element.201), channel_id=1, source_target_pairs={{1,33},{3,35},{5,37},{7,39},{9,57},{11,59},{13,61},{15,63},{17,49}... | collective-permute-start | bytes 301064 | tf_op jit(solution)/shard_map/ppermute | solution.py:26
  87.8 7.6 %collective-permute-start.8 = (bf16[112,448]{1,0:T(8,128)(2,1)S(1)}, bf16[112,448]{1,0:T(8,128)(2,1)S(1)}, u32[]{:S(2)}, u32[]{:S(2)}) collective-permute-start(bf16[112,448]{1,0:T(8,128)(2,1)S(1)} %get-tuple-element.201), channel_id=1, source_target_pairs={{0,33},{1,224},{2,35},{3,226},{4,37},{5,228},{6,39},{7,230},{8,57}... | collective-permute-start | bytes 301064 | tf_op jit(solution)/shard_map/ppermute | solution.py:26
  95.5 8.2 %collective-permute-start.14 = (bf16[112,448]{1,0:T(8,128)(2,1)S(1)}, bf16[112,448]{1,0:T(8,128)(2,1)S(1)}, u32[]{:S(2)}, u32[]{:S(2)}) collective-permute-start(bf16[112,448]{1,0:T(8,128)(2,1)S(1)} %fusion.35), channel_id=1, source_target_pairs={{0,65},{2,67},{4,69},{6,71},{8,89},{10,91},{12,93},{14,95},{16,81}... | collective-permute-start | bytes 301064 | tf_op jit(solution)/shard_map/ppermute | solution.py:26
  96.8 6.9 %collective-permute-start.13 = (bf16[112,448]{1,0:T(8,128)(2,1)S(1)}, bf16[112,448]{1,0:T(8,128)(2,1)S(1)}, u32[]{:S(2)}, u32[]{:S(2)}) collective-permute-start(bf16[112,448]{1,0:T(8,128)(2,1)S(1)} %fusion.35), channel_id=1, source_target_pairs={{0,224},{1,193},{2,226},{3,195},{4,228},{5,197},{6,230},{7,199},{8... | collective-permute-start | bytes 301064 | tf_op jit(solution)/shard_map/ppermute | solution.py:26
  103.9 12.5 %collective-permute-start.15 = (bf16[4,112,448]{2,1,0:T(8,128)(2,1)S(1)}, bf16[4,112,448]{2,1,0:T(8,128)(2,1)S(1)}, u32[]{:S(2)}, u32[]{:S(2)}) collective-permute-start(bf16[4,112,448]{2,1,0:T(8,128)(2,1)S(1)} %pad_maximum_fusion.5), channel_id=1, source_target_pairs={{0,2},{1,3},{2,4},{3,5},{4,6},{5,7},{6,0},{7,1},{8,10},{9,11},{10,... | collective-permute-start | bytes 1204232 | tf_op jit(solution)/shard_map/ppermute | solution.py:26
  104.8 22.3 %collective-permute-start.16 = (bf16[4,112,448]{2,1,0:T(8,128)(2,1)S(1)}, bf16[4,112,448]{2,1,0:T(8,128)(2,1)S(1)}, u32[]{:S(2)}, u32[]{:S(2)}) collective-permute-start(bf16[4,112,448]{2,1,0:T(8,128)(2,1)S(1)} %pad_maximum_fusion.5), channel_id=1, source_target_pairs={{0,4},{1,5},{2,6},{3,7},{4,0},{5,1},{6,2},{7,3},{8,12},{9,13},{10,... | collective-permute-start | bytes 1204232 | tf_op jit(solution)/shard_map/ppermute | solution.py:26
  107.6 19.4 %collective-permute-start.17 = (bf16[4,112,448]{2,1,0:T(8,128)(2,1)S(1)}, bf16[4,112,448]{2,1,0:T(8,128)(2,1)S(1)}, u32[]{:S(2)}, u32[]{:S(2)}) collective-permute-start(bf16[4,112,448]{2,1,0:T(8,128)(2,1)S(1)} %pad_maximum_fusion.5), channel_id=1, source_target_pairs={{0,6},{1,7},{2,0},{3,1},{4,2},{5,3},{6,4},{7,5},{8,14},{9,15},{10,... | collective-permute-start | bytes 1204232 | tf_op jit(solution)/shard_map/ppermute | solution.py:26
  109.6 25.2 %collective-permute-start.18 = (bf16[456,1536]{1,0:T(8,128)(2,1)}, bf16[456,1536]{1,0:T(8,128)(2,1)}, u32[]{:S(2)}, u32[]{:S(2)}) collective-permute-start(bf16[456,1536]{1,0:T(8,128)(2,1)} %collective-permute-done.12), channel_id=1, source_target_pairs={{1,33},{3,35},{5,37},{7,39},{9,41},{11,43},{13,45},{15,47},{17,49}... | collective-permute-start | bytes 4202504 | tf_op jit(solution)/shard_map/ppermute | solution.py:26
  127.1 0.8 copy-start.2
  127.1 0.9 copy-start.3
  133.5 1.4 copy-start.1
  140.1 3.2 %collective-permute-start.19 = (f32[448,768]{1,0:T(8,128)S(1)}, f32[448,768]{1,0:T(8,128)S(1)}, u32[]{:S(2)}, u32[]{:S(2)}) collective-permute-start(f32[448,768]{1,0:T(8,128)S(1)} %get-tuple-element.160), channel_id=1, source_target_pairs={{0,1},{1,0},{2,3},{3,2},{4,5},{5,4},{6,7},{7,6},{8,9},{9,8},{10,11... | collective-permute-start | bytes 4128776 | tf_op jit(solution)/shard_map/ppermute | solution.py:26
  143.4 23.4 %collective-permute-start.20 = (f32[448,384]{1,0:T(8,128)S(1)}, f32[448,384]{1,0:T(8,128)S(1)}, u32[]{:S(2)}, u32[]{:S(2)}) collective-permute-start(f32[448,384]{1,0:T(8,128)S(1)} %slice_add_fusion), channel_id=1, source_target_pairs={{0,8},{1,9},{2,10},{3,11},{4,12},{5,13},{6,14},{7,15},{8,0},{9,1},... | collective-permute-start | bytes 2064392 | tf_op jit(solution)/shard_map/ppermute | solution.py:26

commit v20 on v18

--- a/solution.py
+++ b/solution.py
@@ -184,9 +184,7 @@
         lambda z, xl, xh, y, c: (z + 1, kind(xl, xh), xh, y, 1) if c == 1 else None,
     )
     second = jnp.where(c == 0, amps_one, second)
-    late, first, second, amps_zero, turned_one, turned_two, step_three = lax.optimization_barrier(
-        (late, first, second, amps_zero, turned_one, turned_two, step_three)
-    )
+    late, first, second, amps_zero = lax.optimization_barrier((late, first, second, amps_zero))
 
     first, second = by_hops(first, second)
 

time: 163 us -> 173 us (1.061)
  waiting for transfers between devices: 68.5 us -> 78.2 us
    ppermute x24, waiting for transfers between devices: 68.5 us -> 78.2 us  [moved(): return lax.ppermute(array, ALL, pairs)]
where the time goes in v20:
time: 173 us
  waiting for transfers between devices  78.2 us (45%)
  starting transfers between devices  58.7 us (34%)
  other arithmetic  12 us (7%)
  Pallas kernels  9.51 us (5%)
  matrix products  9.09 us (5%)
  between operations  3.37 us (2%)
    ppermute x24, waiting for transfers between devices, moved(): return lax.ppermute(array, ALL, pairs)  78.2 us
    ppermute x24, starting transfers between devices, moved(): return lax.ppermute(array, ALL, pairs)  50.1 us
    pallas_call x2, Pallas kernels, numerators(): pl.pallas_call(kernel, out_shape=jax.ShapeDtypeStruct((NY, count, share,...  9.51 us
    dot_general x4, matrix products, dot_tn(): lax.dot_general(a, b, (((0,), (0,)), ((), ())), preferred_element_type=jn...  9.09 us
    all_to_all x2, starting transfers between devices, exchanged(): return lax.all_to_all(parts, 'y', 0, 0, tiled=True)  8.58 us
  transfers between devices with their start and end apart: 26, of which 11 were waited for; matrix products, arithmetic and copies ran while one was open for 9% of the time, Pallas kernels for 6%

profile of v20, /device:TPU:1, one launch (start us, length us, event | category | flops | bytes accessed | tf_op | source)
XLA Modules:
  0.0 172.6 jit_solution(7414155575810515971)
XLA Ops:
  0.0 3.6 %collective-permute-start.1 = (bf16[448,384]{1,0:T(8,128)(2,1)}, bf16[448,384]{1,0:T(8,128)(2,1)S(1)}, u32[]{:S(2)}, u32[]{:S(2)}) collective-permute-start(bf16[448,384]{1,0:T(8,128)(2,1)} %bitcast.177), channel_id=1, source_target_pairs={{0,8},{1,9},{2,10},{3,11},{4,12},{5,13},{6,14},{7,15},{8,0},{9,1},... | collective-permute-start | bytes 1032200 | tf_op jit(solution)/shard_map/ppermute | solution.py:26
  3.6 1.0 collective-permute-start
  7.6 1.4 select_convert_fusion
  8.9 1.7 collective-permute-done.1
  10.6 2.2 %collective-permute-start.2 = (bf16[448,384]{1,0:T(8,128)(2,1)S(1)}, bf16[448,384]{1,0:T(8,128)(2,1)S(1)}, u32[]{:S(2)}, u32[]{:S(2)}) collective-permute-start(bf16[448,384]{1,0:T(8,128)(2,1)S(1)} %collective-permute-done.1), channel_id=1, source_target_pairs={{0,1},{1,0},{2,3},{3,2},{4,5},{5,4},{6,7},{7,6},{8,9},{9,8},{10,11... | collective-permute-start | bytes 1032200 | tf_op jit(solution)/shard_map/ppermute | solution.py:26
  12.8 1.2 maximum_select_fusion.1
  14.1 0.2 maximum_select_fusion.2
  14.2 0.3 maximum_select_fusion
  14.6 0.1 pad_maximum_fusion.4.mine_ref
  14.7 1.0 copy-done
  15.7 1.9 %collective-permute-start.3 = (bf16[456,1536]{1,0:T(8,128)(2,1)S(1)}, bf16[456,1536]{1,0:T(8,128)(2,1)}, u32[]{:S(2)}, u32[]{:S(2)}) collective-permute-start(bf16[456,1536]{1,0:T(8,128)(2,1)S(1)} %pad_maximum_fusion.4.mine_ref), channel_id=1, source_target_pairs={{0,224},{1,33},{2,226},{3,35},{4,228},{5,37},{6,230},{7,39},{8,248... | collective-permute-start | bytes 4202504 | tf_op jit(solution)/shard_map/ppermute | solution.py:26
  17.5 1.8 %collective-permute-start.7 = (bf16[456,1536]{1,0:T(8,128)(2,1)S(1)}, bf16[456,1536]{1,0:T(8,128)(2,1)}, u32[]{:S(2)}, u32[]{:S(2)}) collective-permute-start(bf16[456,1536]{1,0:T(8,128)(2,1)S(1)} %pad_maximum_fusion.4.mine_ref), channel_id=1, source_target_pairs={{0,24},{2,26},{4,28},{6,30},{16,8},{18,10},{20,12},{22,14},{32,56}... | collective-permute-start | bytes 4202504 | tf_op jit(solution)/shard_map/ppermute | solution.py:26
  19.3 18.2 %collective-permute-done.3.one_ref = bf16[456,1536]{1,0:T(8,128)(2,1)} collective-permute-done((bf16[456,1536]{1,0:T(8,128)(2,1)S(1)}, bf16[456,1536]{1,0:T(8,128)(2,1)}, u32[]{:S(2)}, u32[]{:S(2)}) %collective-permute-start.3) | collective-permute-done | bytes 1400864 | tf_op jit(solution)/shard_map/ppermute | solution.py:26
  37.5 0.7 collective-permute-start.6
  38.2 0.1 pad_add_fusion.where_ref
  38.3 0.1 dynamic_slice.3
  38.4 2.8 %collective-permute-done.6.swap_ref.swap_one_ref = bf16[456,1536]{1,0:T(8,128)(2,1)S(1)} collective-permute-done((bf16[456,1536]{1,0:T(8,128)(2,1)}, bf16[456,1536]{1,0:T(8,128)(2,1)S(1)}, u32[]{:S(2)}, u32[]{:S(2)}) %collective-permute-start.6) | collective-permute-done | bytes 1400864 | tf_op jit(solution)/shard_map/ppermute | solution.py:26
  41.2 5.5 %shard_map.37 = f32[4,2,112,448]{3,2,1,0:T(8,128)} custom-call(s32[2]{0:T(128)S(1)} %pad_add_fusion.where_ref, bf16[456,1536]{1,0:T(8,128)(2,1)S(1)} %pad_maximum_fusion.4.mine_ref, bf16[456,1536]{1,0:T(8,128)(2,1)} %collective-permute-done.3.one_ref, bf16[456,1536]{1,0:T(8,128)(2,1)S(1)} %collective-permute-done.6.swap_ref.swap_one_ref, ...), custom_call_target="tpu_custom_call" | custom-call | flops 2466250752 | bytes 7110656 | tf_op jit(solution)/shard_map/pallas_call | solution.py:91
  46.8 5.4 %collective-permute-start.8 = (bf16[456,1536]{1,0:T(8,128)(2,1)S(1)}, bf16[456,1536]{1,0:T(8,128)(2,1)S(1)}, u32[]{:S(2)}, u32[]{:S(2)}) collective-permute-start(bf16[456,1536]{1,0:T(8,128)(2,1)S(1)} %collective-permute-done.6.swap_ref.swap_one_ref), channel_id=1, source_target_pairs={{1,225},{3,227},{5,229},{7,231},{9,233},{11,235},{13,237},{15,239}... | collective-permute-start | bytes 4202504 | tf_op jit(solution)/shard_map/ppermute | solution.py:26
  52.2 0.7 slice_convert_fusion.2
  52.9 4.4 %all-to-all-start = ((f32[4,2,112,448]{3,2,1,0:T(8,128)}), f32[4,2,112,448]{3,2,1,0:T(8,128)}, u32[]{:S(2)}, u32[]{:S(2)}) async-start(f32[4,2,112,448]{3,2,1,0:T(8,128)} %shard_map.37), calls=%async_computation | async-start | bytes 3670016 | tf_op jit(solution)/shard_map/all_to_all | solution.py:136
  57.3 0.7 slice_convert_fusion.3
  58.0 7.1 %collective-permute-start.20 = (bf16[456,1536]{1,0:T(8,128)(2,1)}, bf16[456,1536]{1,0:T(8,128)(2,1)}, u32[]{:S(2)}, u32[]{:S(2)}) collective-permute-start(bf16[456,1536]{1,0:T(8,128)(2,1)} %collective-permute-done.3.one_ref), channel_id=1, source_target_pairs={{1,25},{3,27},{5,29},{7,31},{17,9},{19,11},{21,13},{23,15},{33,57}... | collective-permute-start | bytes 4202504 | tf_op jit(solution)/shard_map/ppermute | solution.py:26
  65.1 0.7 slice_convert_fusion
  65.8 11.7 %collective-permute-done.8.swap_two_ref = bf16[456,1536]{1,0:T(8,128)(2,1)S(1)} collective-permute-done((bf16[456,1536]{1,0:T(8,128)(2,1)S(1)}, bf16[456,1536]{1,0:T(8,128)(2,1)S(1)}, u32[]{:S(2)}, u32[]{:S(2)}) %collective-permute-start.8) | collective-permute-done | bytes 1400864 | tf_op jit(solution)/shard_map/ppermute | solution.py:26
  77.6 4.0 %shard_map.38 = f32[4,1,112,448]{3,2,1,0:T(8,128)} custom-call(s32[2]{0:T(128)S(1)} %pad_add_fusion.where_ref, bf16[456,1536]{1,0:T(8,128)(2,1)S(1)} %collective-permute-done.6.swap_ref.swap_one_ref, bf16[456,1536]{1,0:T(8,128)(2,1)S(1)} %collective-permute-done.8.swap_two_ref, bf16[456,1536]{1,0:T(8,128)(2,1)} %collective-permute-done.4.two_ref), custom_call_target="tpu_custom_call" | custom-call | flops 1233125376 | bytes 4931584 | tf_op jit(solution)/shard_map/pallas_call | solution.py:91
  81.6 4.2 %all-to-all-start.1 = ((f32[4,1,112,448]{3,2,1,0:T(8,128)}), f32[4,1,112,448]{3,2,1,0:T(8,128)S(1)}, u32[]{:S(2)}, u32[]{:S(2)}) async-start(f32[4,1,112,448]{3,2,1,0:T(8,128)} %shard_map.38), calls=%async_computation.1 | async-start | bytes 1835008 | tf_op jit(solution)/shard_map/all_to_all | solution.py:136
  85.8 1.7 %reduce_sum.22 = f32[2,112,448]{2,1,0:T(8,128)S(1)} reduce(f32[4,2,112,448]{3,2,1,0:T(8,128)} %all-to-all-done, f32[]{:T(128)} %constant.6.clone.1), dimensions={0}, to_apply=%region_1.2 | reduce | flops 301056 | bytes 2007044 | tf_op jit(solution)/shard_map/reduce_sum | solution.py:171
  87.5 0.1 fusion.36
  87.7 1.9 %collective-permute-start.10 = (bf16[112,448]{1,0:T(8,128)(2,1)S(1)}, bf16[112,448]{1,0:T(8,128)(2,1)S(1)}, u32[]{:S(2)}, u32[]{:S(2)}) collective-permute-start(bf16[112,448]{1,0:T(8,128)(2,1)S(1)} %get-tuple-element.195), channel_id=1, source_target_pairs={{1,33},{3,35},{5,37},{7,39},{9,57},{11,59},{13,61},{15,63},{17,49}... | collective-permute-start | bytes 301064 | tf_op jit(solution)/shard_map/ppermute | solution.py:26
  89.6 6.1 %collective-permute-start.16 = (bf16[456,1536]{1,0:T(8,128)(2,1)}, bf16[456,1536]{1,0:T(8,128)(2,1)S(1)}, u32[]{:S(2)}, u32[]{:S(2)}) collective-permute-start(bf16[456,1536]{1,0:T(8,128)(2,1)} %collective-permute-done.4.two_ref), channel_id=1, source_target_pairs={{1,25},{3,27},{5,29},{7,31},{17,9},{19,11},{21,13},{23,15},{33,57}... | collective-permute-start | bytes 4202504 | tf_op jit(solution)/shard_map/ppermute | solution.py:26
  95.7 0.1 collective-permute-start.9
  95.9 0.1 reduce_sum.20
  96.0 5.3 %collective-permute-done.9 = bf16[112,448]{1,0:T(8,128)(2,1)S(1)} collective-permute-done((bf16[112,448]{1,0:T(8,128)(2,1)S(1)}, bf16[112,448]{1,0:T(8,128)(2,1)S(1)}, u32[]{:S(2)}, u32[]{:S(2)}) %collective-permute-start.9) | collective-permute-done | bytes 100384 | tf_op jit(solution)/shard_map/ppermute | solution.py:26
  101.2 0.1 fusion.35
  101.4 1.3 collective-permute-start.12
  102.7 2.8 %collective-permute-start.15 = (bf16[2,112,448]{2,1,0:T(8,128)(2,1)S(1)}, bf16[2,112,448]{2,1,0:T(8,128)(2,1)S(1)}, u32[]{:S(2)}, u32[]{:S(2)}) collective-permute-start(bf16[2,112,448]{2,1,0:T(8,128)(2,1)S(1)} %pad_maximum_fusion.9), channel_id=1, source_target_pairs={{0,6},{1,7},{2,0},{3,1},{4,2},{5,3},{6,4},{7,5},{8,14},{9,15},{10,... | collective-permute-start | bytes 602120 | tf_op jit(solution)/shard_map/ppermute | solution.py:26
  105.4 0.6 collective-permute-start.14
  106.0 4.8 %collective-permute-done.12 = bf16[112,448]{1,0:T(8,128)(2,1)S(1)} collective-permute-done((bf16[112,448]{1,0:T(8,128)(2,1)S(1)}, bf16[112,448]{1,0:T(8,128)(2,1)S(1)}, u32[]{:S(2)}, u32[]{:S(2)}) %collective-permute-start.12) | collective-permute-done | bytes 100384 | tf_op jit(solution)/shard_map/ppermute | solution.py:26
  110.8 1.5 collective-permute-start.13
  112.3 1.9 %collective-permute-start.21 = (bf16[456,1536]{1,0:T(8,128)(2,1)}, bf16[456,1536]{1,0:T(8,128)(2,1)}, u32[]{:S(2)}, u32[]{:S(2)}) collective-permute-start(bf16[456,1536]{1,0:T(8,128)(2,1)} %collective-permute-done.5), channel_id=1, source_target_pairs={{1,33},{3,35},{5,37},{7,39},{9,41},{11,43},{13,45},{15,47},{17,49}... | collective-permute-start | bytes 4202504 | tf_op jit(solution)/shard_map/ppermute | solution.py:26
  114.2 6.1 %collective-permute-start.11 = (bf16[112,448]{1,0:T(8,128)(2,1)S(1)}, bf16[112,448]{1,0:T(8,128)(2,1)S(1)}, u32[]{:S(2)}, u32[]{:S(2)}) collective-permute-start(bf16[112,448]{1,0:T(8,128)(2,1)S(1)} %fusion.35), channel_id=1, source_target_pairs={{0,224},{1,193},{2,226},{3,195},{4,228},{5,197},{6,230},{7,199},{8... | collective-permute-start | bytes 301064 | tf_op jit(solution)/shard_map/ppermute | solution.py:26
  120.6 3.6 %collective-permute-done.11 = bf16[112,448]{1,0:T(8,128)(2,1)S(1)} collective-permute-done((bf16[112,448]{1,0:T(8,128)(2,1)S(1)}, bf16[112,448]{1,0:T(8,128)(2,1)S(1)}, u32[]{:S(2)}, u32[]{:S(2)}) %collective-permute-start.11) | collective-permute-done | bytes 100384 | tf_op jit(solution)/shard_map/ppermute | solution.py:26
  124.2 0.7 pad_maximum_fusion.10
  124.9 3.6 %collective-permute-start.19 = (bf16[2,112,448]{2,1,0:T(8,128)(2,1)}, bf16[2,112,448]{2,1,0:T(8,128)(2,1)}, u32[]{:S(2)}, u32[]{:S(2)}) collective-permute-start(bf16[2,112,448]{2,1,0:T(8,128)(2,1)} %pad_maximum_fusion.10), channel_id=1, source_target_pairs={{0,6},{1,7},{2,0},{3,1},{4,2},{5,3},{6,4},{7,5},{8,14},{9,15},{10,... | collective-permute-start | bytes 602120 | tf_op jit(solution)/shard_map/ppermute | solution.py:26
  128.5 0.6 collective-permute-start.17
  129.1 4.5 %conditional.2 = (f32[448,1536]{1,0:T(8,128)S(1)}) conditional(s32[]{:T(128)} %clamp.4, (bf16[456,1536]{1,0:T(8,128)(2,1)}, bf16[448,448]{1,0:T(8,128)(2,1)S(1)}, bf16[456,1536]{1,0:T(8,128)(2,1)}, bf16[448,448]{1,0:T(8,128)(2,1)S(1)}) %tuple.43, (bf16[456,1536]{1,0:T(8,128)(2,1)}, bf16[448,448]{1,0:T(8,128)(2,1)S(1)}, ...), branch_computations={%region_2.3_spmd, %region_3.4_spmd, %region_4.5_spmd, %region_5.6_... | conditional | flops 1233813504 | bytes 17416228 | solution.py:205
  129.1 2.2 %fusion.4 = f32[448,1536]{1,0:T(8,128)S(1)} fusion(bf16[448,448]{1,0:T(8,128)(2,1)S(1)} %get-tuple-element.86, bf16[456,1536]{1,0:T(8,128)(2,1)} %get-tuple-element.87), kind=kOutput, calls=%fused_computation.6 | convolution fusion | flops 616562688 | bytes 4530176 | tf_op jit(solution)/shard_map/cond/branch_1_fun/dot_general | solution.py:50
  131.4 2.3 %convolution_add_fusion.1 = f32[448,1536]{1,0:T(8,128)S(1)} fusion(f32[448,1536]{1,0:T(8,128)S(1)} %fusion.4, bf16[448,448]{1,0:T(8,128)(2,1)S(1)} %get-tuple-element.88, bf16[456,1536]{1,0:T(8,128)(2,1)} %get-tuple-element.89), kind=kOutput, calls=%fused_computation.4 | convolution fusion | flops 617250816 | bytes 7282688 | tf_op jit(solution)/shard_map/cond/branch_1_fun/dot_general | solution.py:50
  133.7 4.4 %collective-permute-done.19 = bf16[2,112,448]{2,1,0:T(8,128)(2,1)} collective-permute-done((bf16[2,112,448]{2,1,0:T(8,128)(2,1)}, bf16[2,112,448]{2,1,0:T(8,128)(2,1)}, u32[]{:S(2)}, u32[]{:S(2)}) %collective-permute-start.19) | collective-permute-done | bytes 200736 | tf_op jit(solution)/shard_map/ppermute | solution.py:26
  138.1 4.1 %collective-permute-done.17 = bf16[2,112,448]{2,1,0:T(8,128)(2,1)} collective-permute-done((bf16[2,112,448]{2,1,0:T(8,128)(2,1)}, bf16[2,112,448]{2,1,0:T(8,128)(2,1)}, u32[]{:S(2)}, u32[]{:S(2)}) %collective-permute-start.17) | collective-permute-done | bytes 200736 | tf_op jit(solution)/shard_map/ppermute | solution.py:26
  142.2 1.1 select_select_fusion.7
  143.3 1.2 select_select_fusion.3
  144.5 0.2 copy-done.1
  144.8 5.1 %conditional.3 = (f32[448,768]{1,0:T(8,128)S(1)}, f32[448,384]{1,0:T(8,128)S(1)}, f32[448,384]{1,0:T(8,128)S(1)}) conditional(s32[]{:T(128)} %clamp.4, (bf16[456,1536]{1,0:T(8,128)(2,1)}, bf16[448,448]{1,0:T(8,128)(2,1)S(1)}, bf16[448,448]{1,0:T(8,128)(2,1)S(1)}, bf16[448,1536]{1,0:T(8,128)(2,1)S(1)}, ...), branch_computations={%region_6.7_spmd, %region_7.8_spmd, %region_8.9_spmd, %region_9.10... | conditional | flops 1234845696 | bytes 22822936 | solution.py:225
  144.8 2.2 %fusion.17 = f32[448,1536]{1,0:T(8,128)S(1)} fusion(bf16[448,448]{1,0:T(8,128)(2,1)S(1)} %get-tuple-element.104, bf16[456,1536]{1,0:T(8,128)(2,1)} %get-tuple-element.105), kind=kOutput, calls=%fused_computation.25 | convolution fusion | flops 616562688 | bytes 4530176 | tf_op jit(solution)/shard_map/cond/branch_1_fun/dot_general | solution.py:50
  147.0 2.3 %fusion.15 = f32[448,1536]{1,0:T(8,128)S(1)} fusion(f32[448,1536]{1,0:T(8,128)S(1)} %get-tuple-element.103, f32[448,1536]{1,0:T(8,128)S(1)} %fusion.17, bf16[448,448]{1,0:T(8,128)(2,1)S(1)} %get-tuple-element.106, bf16[456,1536]{1,0:T(8,128)(2,1)} %get-tuple-element.107), kind=kOutput, calls=%fused_computation.22 | convolution fusion | flops 617938944 | bytes 10035200 | tf_op jit(solution)/shard_map/cond/branch_1_fun/dot_general | solution.py:50
  149.3 0.2 fusion.39
  149.5 0.1 pad_maximum_fusion.1
  149.8 0.1 collective-permute-start.22
  149.9 3.1 %collective-permute-done.22 = f32[448,768]{1,0:T(8,128)S(1)} collective-permute-done((f32[448,768]{1,0:T(8,128)S(1)}, f32[448,768]{1,0:T(8,128)S(1)}, u32[]{:S(2)}, u32[]{:S(2)}) %collective-permute-start.22) | collective-permute-done | bytes 1376288 | tf_op jit(solution)/shard_map/ppermute | solution.py:26
  153.1 0.1 collective-permute-start.23
  153.2 18.4 %collective-permute-done.23 = f32[448,384]{1,0:T(8,128)S(1)} collective-permute-done((f32[448,384]{1,0:T(8,128)S(1)}, f32[448,384]{1,0:T(8,128)S(1)}, u32[]{:S(2)}, u32[]{:S(2)}) %collective-permute-start.23) | collective-permute-done | bytes 688160 | tf_op jit(solution)/shard_map/ppermute | solution.py:26
  171.6 0.9 fusion.28
  (42 shorter events, 0.6 us)
Async XLA Ops:
  0.0 10.6 %collective-permute-start.1 = (bf16[448,384]{1,0:T(8,128)(2,1)}, bf16[448,384]{1,0:T(8,128)(2,1)S(1)}, u32[]{:S(2)}, u32[]{:S(2)}) collective-permute-start(bf16[448,384]{1,0:T(8,128)(2,1)} %bitcast.177), channel_id=1, source_target_pairs={{0,8},{1,9},{2,10},{3,11},{4,12},{5,13},{6,14},{7,15},{8,0},{9,1},... | collective-permute-start | bytes 1032200 | tf_op jit(solution)/shard_map/ppermute | solution.py:26
  3.6 9.2 %collective-permute-start = (bf16[448,384]{1,0:T(8,128)(2,1)}, bf16[448,384]{1,0:T(8,128)(2,1)S(1)}, u32[]{:S(2)}, u32[]{:S(2)}) collective-permute-start(bf16[448,384]{1,0:T(8,128)(2,1)} %bitcast.178), channel_id=1, source_target_pairs={{0,1},{1,0},{2,3},{3,2},{4,5},{5,4},{6,7},{7,6},{8,9},{9,8},{10,11... | collective-permute-start | bytes 1032200 | tf_op jit(solution)/shard_map/ppermute | solution.py:26
  10.6 3.5 %collective-permute-start.2 = (bf16[448,384]{1,0:T(8,128)(2,1)S(1)}, bf16[448,384]{1,0:T(8,128)(2,1)S(1)}, u32[]{:S(2)}, u32[]{:S(2)}) collective-permute-start(bf16[448,384]{1,0:T(8,128)(2,1)S(1)} %collective-permute-done.1), channel_id=1, source_target_pairs={{0,1},{1,0},{2,3},{3,2},{4,5},{5,4},{6,7},{7,6},{8,9},{9,8},{10,11... | collective-permute-start | bytes 1032200 | tf_op jit(solution)/shard_map/ppermute | solution.py:26
  14.6 1.1 copy-start
  14.6 23.7 %copy-start.3 = (f32[448]{0:T(512)S(1)}, f32[448]{0:T(512)}, u32[]{:S(2)}) copy-start(f32[448]{0:T(512)} %param.13) | copy-start | bytes 5380
  15.7 21.9 %collective-permute-start.3 = (bf16[456,1536]{1,0:T(8,128)(2,1)S(1)}, bf16[456,1536]{1,0:T(8,128)(2,1)}, u32[]{:S(2)}, u32[]{:S(2)}) collective-permute-start(bf16[456,1536]{1,0:T(8,128)(2,1)S(1)} %pad_maximum_fusion.4.mine_ref), channel_id=1, source_target_pairs={{0,224},{1,33},{2,226},{3,35},{4,228},{5,37},{6,230},{7,39},{8,248... | collective-permute-start | bytes 4202504 | tf_op jit(solution)/shard_map/ppermute | solution.py:26
  17.5 20.8 %collective-permute-start.7 = (bf16[456,1536]{1,0:T(8,128)(2,1)S(1)}, bf16[456,1536]{1,0:T(8,128)(2,1)}, u32[]{:S(2)}, u32[]{:S(2)}) collective-permute-start(bf16[456,1536]{1,0:T(8,128)(2,1)S(1)} %pad_maximum_fusion.4.mine_ref), channel_id=1, source_target_pairs={{0,24},{2,26},{4,28},{6,30},{16,8},{18,10},{20,12},{22,14},{32,56}... | collective-permute-start | bytes 4202504 | tf_op jit(solution)/shard_map/ppermute | solution.py:26
  37.5 3.7 %collective-permute-start.6 = (bf16[456,1536]{1,0:T(8,128)(2,1)}, bf16[456,1536]{1,0:T(8,128)(2,1)S(1)}, u32[]{:S(2)}, u32[]{:S(2)}) collective-permute-start(bf16[456,1536]{1,0:T(8,128)(2,1)} %collective-permute-done.3.one_ref), channel_id=1, source_target_pairs={{0,1},{1,0},{2,3},{3,2},{4,5},{5,4},{6,7},{7,6},{8,9},{9,8},{10,11... | collective-permute-start | bytes 4202504 | tf_op jit(solution)/shard_map/ppermute | solution.py:26
  38.2 26.9 %collective-permute-start.4 = (bf16[456,1536]{1,0:T(8,128)(2,1)}, bf16[456,1536]{1,0:T(8,128)(2,1)}, u32[]{:S(2)}, u32[]{:S(2)}) collective-permute-start(bf16[456,1536]{1,0:T(8,128)(2,1)} %collective-permute-done.3.one_ref), channel_id=1, source_target_pairs={{0,224},{1,33},{2,226},{3,35},{4,228},{5,37},{6,230},{7,39},{8,232... | collective-permute-start | bytes 4202504 | tf_op jit(solution)/shard_map/ppermute | solution.py:26
  46.8 30.8 %collective-permute-start.8 = (bf16[456,1536]{1,0:T(8,128)(2,1)S(1)}, bf16[456,1536]{1,0:T(8,128)(2,1)S(1)}, u32[]{:S(2)}, u32[]{:S(2)}) collective-permute-start(bf16[456,1536]{1,0:T(8,128)(2,1)S(1)} %collective-permute-done.6.swap_ref.swap_one_ref), channel_id=1, source_target_pairs={{1,225},{3,227},{5,229},{7,231},{9,233},{11,235},{13,237},{15,239}... | collective-permute-start | bytes 4202504 | tf_op jit(solution)/shard_map/ppermute | solution.py:26
  52.9 28.7 %all-to-all-start = ((f32[4,2,112,448]{3,2,1,0:T(8,128)}), f32[4,2,112,448]{3,2,1,0:T(8,128)}, u32[]{:S(2)}, u32[]{:S(2)}) async-start(f32[4,2,112,448]{3,2,1,0:T(8,128)} %shard_map.37), calls=%async_computation | async-start | bytes 3670016 | tf_op jit(solution)/shard_map/all_to_all | solution.py:136
  58.0 71.1 %collective-permute-start.20 = (bf16[456,1536]{1,0:T(8,128)(2,1)}, bf16[456,1536]{1,0:T(8,128)(2,1)}, u32[]{:S(2)}, u32[]{:S(2)}) collective-permute-start(bf16[456,1536]{1,0:T(8,128)(2,1)} %collective-permute-done.3.one_ref), channel_id=1, source_target_pairs={{1,25},{3,27},{5,29},{7,31},{17,9},{19,11},{21,13},{23,15},{33,57}... | collective-permute-start | bytes 4202504 | tf_op jit(solution)/shard_map/ppermute | solution.py:26
  65.1 40.3 %collective-permute-start.5 = (bf16[456,1536]{1,0:T(8,128)(2,1)}, bf16[456,1536]{1,0:T(8,128)(2,1)}, u32[]{:S(2)}, u32[]{:S(2)}) collective-permute-start(bf16[456,1536]{1,0:T(8,128)(2,1)} %collective-permute-done.4.two_ref), channel_id=1, source_target_pairs={{0,224},{1,33},{2,226},{3,35},{4,228},{5,37},{6,230},{7,39},{8,232... | collective-permute-start | bytes 4202504 | tf_op jit(solution)/shard_map/ppermute | solution.py:26
  81.6 14.3 %all-to-all-start.1 = ((f32[4,1,112,448]{3,2,1,0:T(8,128)}), f32[4,1,112,448]{3,2,1,0:T(8,128)S(1)}, u32[]{:S(2)}, u32[]{:S(2)}) async-start(f32[4,1,112,448]{3,2,1,0:T(8,128)} %shard_map.38), calls=%async_computation.1 | async-start | bytes 1835008 | tf_op jit(solution)/shard_map/all_to_all | solution.py:136
  87.7 8.1 %collective-permute-start.10 = (bf16[112,448]{1,0:T(8,128)(2,1)S(1)}, bf16[112,448]{1,0:T(8,128)(2,1)S(1)}, u32[]{:S(2)}, u32[]{:S(2)}) collective-permute-start(bf16[112,448]{1,0:T(8,128)(2,1)S(1)} %get-tuple-element.195), channel_id=1, source_target_pairs={{1,33},{3,35},{5,37},{7,39},{9,57},{11,59},{13,61},{15,63},{17,49}... | collective-permute-start | bytes 301064 | tf_op jit(solution)/shard_map/ppermute | solution.py:26
  89.6 30.9 %collective-permute-start.16 = (bf16[456,1536]{1,0:T(8,128)(2,1)}, bf16[456,1536]{1,0:T(8,128)(2,1)S(1)}, u32[]{:S(2)}, u32[]{:S(2)}) collective-permute-start(bf16[456,1536]{1,0:T(8,128)(2,1)} %collective-permute-done.4.two_ref), channel_id=1, source_target_pairs={{1,25},{3,27},{5,29},{7,31},{17,9},{19,11},{21,13},{23,15},{33,57}... | collective-permute-start | bytes 4202504 | tf_op jit(solution)/shard_map/ppermute | solution.py:26
  95.7 5.5 %collective-permute-start.9 = (bf16[112,448]{1,0:T(8,128)(2,1)S(1)}, bf16[112,448]{1,0:T(8,128)(2,1)S(1)}, u32[]{:S(2)}, u32[]{:S(2)}) collective-permute-start(bf16[112,448]{1,0:T(8,128)(2,1)S(1)} %get-tuple-element.195), channel_id=1, source_target_pairs={{0,33},{1,224},{2,35},{3,226},{4,37},{5,228},{6,39},{7,230},{8,57}... | collective-permute-start | bytes 301064 | tf_op jit(solution)/shard_map/ppermute | solution.py:26
  101.4 9.4 %collective-permute-start.12 = (bf16[112,448]{1,0:T(8,128)(2,1)S(1)}, bf16[112,448]{1,0:T(8,128)(2,1)S(1)}, u32[]{:S(2)}, u32[]{:S(2)}) collective-permute-start(bf16[112,448]{1,0:T(8,128)(2,1)S(1)} %fusion.35), channel_id=1, source_target_pairs={{0,65},{2,67},{4,69},{6,71},{8,89},{10,91},{12,93},{14,95},{16,81}... | collective-permute-start | bytes 301064 | tf_op jit(solution)/shard_map/ppermute | solution.py:26
  102.7 9.6 %collective-permute-start.15 = (bf16[2,112,448]{2,1,0:T(8,128)(2,1)S(1)}, bf16[2,112,448]{2,1,0:T(8,128)(2,1)S(1)}, u32[]{:S(2)}, u32[]{:S(2)}) collective-permute-start(bf16[2,112,448]{2,1,0:T(8,128)(2,1)S(1)} %pad_maximum_fusion.9), channel_id=1, source_target_pairs={{0,6},{1,7},{2,0},{3,1},{4,2},{5,3},{6,4},{7,5},{8,14},{9,15},{10,... | collective-permute-start | bytes 602120 | tf_op jit(solution)/shard_map/ppermute | solution.py:26
  105.4 8.8 %collective-permute-start.14 = (bf16[2,112,448]{2,1,0:T(8,128)(2,1)S(1)}, bf16[2,112,448]{2,1,0:T(8,128)(2,1)S(1)}, u32[]{:S(2)}, u32[]{:S(2)}) collective-permute-start(bf16[2,112,448]{2,1,0:T(8,128)(2,1)S(1)} %pad_maximum_fusion.9), channel_id=1, source_target_pairs={{0,4},{1,5},{2,6},{3,7},{4,0},{5,1},{6,2},{7,3},{8,12},{9,13},{10,... | collective-permute-start | bytes 602120 | tf_op jit(solution)/shard_map/ppermute | solution.py:26
  110.8 9.6 %collective-permute-start.13 = (bf16[2,112,448]{2,1,0:T(8,128)(2,1)S(1)}, bf16[2,112,448]{2,1,0:T(8,128)(2,1)S(1)}, u32[]{:S(2)}, u32[]{:S(2)}) collective-permute-start(bf16[2,112,448]{2,1,0:T(8,128)(2,1)S(1)} %pad_maximum_fusion.9), channel_id=1, source_target_pairs={{0,2},{1,3},{2,4},{3,5},{4,6},{5,7},{6,0},{7,1},{8,10},{9,11},{10,... | collective-permute-start | bytes 602120 | tf_op jit(solution)/shard_map/ppermute | solution.py:26
  112.3 32.2 %collective-permute-start.21 = (bf16[456,1536]{1,0:T(8,128)(2,1)}, bf16[456,1536]{1,0:T(8,128)(2,1)}, u32[]{:S(2)}, u32[]{:S(2)}) collective-permute-start(bf16[456,1536]{1,0:T(8,128)(2,1)} %collective-permute-done.5), channel_id=1, source_target_pairs={{1,33},{3,35},{5,37},{7,39},{9,41},{11,43},{13,45},{15,47},{17,49}... | collective-permute-start | bytes 4202504 | tf_op jit(solution)/shard_map/ppermute | solution.py:26
  114.2 9.9 %collective-permute-start.11 = (bf16[112,448]{1,0:T(8,128)(2,1)S(1)}, bf16[112,448]{1,0:T(8,128)(2,1)S(1)}, u32[]{:S(2)}, u32[]{:S(2)}) collective-permute-start(bf16[112,448]{1,0:T(8,128)(2,1)S(1)} %fusion.35), channel_id=1, source_target_pairs={{0,224},{1,193},{2,226},{3,195},{4,228},{5,197},{6,230},{7,199},{8... | collective-permute-start | bytes 301064 | tf_op jit(solution)/shard_map/ppermute | solution.py:26
  124.9 13.2 %collective-permute-start.19 = (bf16[2,112,448]{2,1,0:T(8,128)(2,1)}, bf16[2,112,448]{2,1,0:T(8,128)(2,1)}, u32[]{:S(2)}, u32[]{:S(2)}) collective-permute-start(bf16[2,112,448]{2,1,0:T(8,128)(2,1)} %pad_maximum_fusion.10), channel_id=1, source_target_pairs={{0,6},{1,7},{2,0},{3,1},{4,2},{5,3},{6,4},{7,5},{8,14},{9,15},{10,... | collective-permute-start | bytes 602120 | tf_op jit(solution)/shard_map/ppermute | solution.py:26
  128.5 9.6 %collective-permute-start.18 = (bf16[2,112,448]{2,1,0:T(8,128)(2,1)}, bf16[2,112,448]{2,1,0:T(8,128)(2,1)}, u32[]{:S(2)}, u32[]{:S(2)}) collective-permute-start(bf16[2,112,448]{2,1,0:T(8,128)(2,1)} %pad_maximum_fusion.10), channel_id=1, source_target_pairs={{0,4},{1,5},{2,6},{3,7},{4,0},{5,1},{6,2},{7,3},{8,12},{9,13},{10,... | collective-permute-start | bytes 602120 | tf_op jit(solution)/shard_map/ppermute | solution.py:26
  128.5 13.6 %collective-permute-start.17 = (bf16[2,112,448]{2,1,0:T(8,128)(2,1)}, bf16[2,112,448]{2,1,0:T(8,128)(2,1)}, u32[]{:S(2)}, u32[]{:S(2)}) collective-permute-start(bf16[2,112,448]{2,1,0:T(8,128)(2,1)} %pad_maximum_fusion.10), channel_id=1, source_target_pairs={{0,2},{1,3},{2,4},{3,5},{4,6},{5,7},{6,0},{7,1},{8,10},{9,11},{10,... | collective-permute-start | bytes 602120 | tf_op jit(solution)/shard_map/ppermute | solution.py:26
  143.2 1.5 copy-start.1
  149.8 3.2 %collective-permute-start.22 = (f32[448,768]{1,0:T(8,128)S(1)}, f32[448,768]{1,0:T(8,128)S(1)}, u32[]{:S(2)}, u32[]{:S(2)}) collective-permute-start(f32[448,768]{1,0:T(8,128)S(1)} %get-tuple-element.154), channel_id=1, source_target_pairs={{0,1},{1,0},{2,3},{3,2},{4,5},{5,4},{6,7},{7,6},{8,9},{9,8},{10,11... | collective-permute-start | bytes 4128776 | tf_op jit(solution)/shard_map/ppermute | solution.py:26
  153.1 18.5 %collective-permute-start.23 = (f32[448,384]{1,0:T(8,128)S(1)}, f32[448,384]{1,0:T(8,128)S(1)}, u32[]{:S(2)}, u32[]{:S(2)}) collective-permute-start(f32[448,384]{1,0:T(8,128)S(1)} %slice_add_fusion), channel_id=1, source_target_pairs={{0,8},{1,9},{2,10},{3,11},{4,12},{5,13},{6,14},{7,15},{8,0},{9,1},... | collective-permute-start | bytes 2064392 | tf_op jit(solution)/shard_map/ppermute | solution.py:26
